TPU v7x, 32 devices: a whole 2x2x4 slice. The times are simulated.
32 devices in a mesh: seq: 4 (over z), head: 4 (over y, x), rep: 2 (over core).
Axes of the slice: x: 2, y: 2, z: 4, core: 2. Of those that a mesh axis runs over, the one named last changes fastest.
Arguments:
- hidden: bfloat16 [8192, 8192], P(('seq', 'rep')), may hold values from -6 to 6
- key_weight: bfloat16 [8192, 1024], P(('seq', 'rep'), 'head'), may hold values from -0.0625 to 0.0625
- value_weight: bfloat16 [8192, 1024], P(('seq', 'rep'), 'head'), may hold values from -0.0625 to 0.0625
- group_scale: float32 [2, 1024], P(None, 'head'), may hold values from 0.05 to 0.4
- new_kv: bfloat16 [4, 32, 2, 1024], P(None, 'seq', None, 'head'), may hold values from -6 to 6
- decode_query: bfloat16 [4, 32, 8192], P(None, 'seq', 'head'), may hold values from -400 to 400
- page_table: int32 [32, 32], replicated, may hold values from 0 to 255, as said below
- lengths: int32 [32], replicated, may hold values from 1 to 1024
Outputs:
- kv_cache: bfloat16 [8192, 2, 1024], P(('seq', 'rep'), None, 'head')
- smoothing: float32 [1024], P('head')
- attention: bfloat16 [4, 32, 8192], P(None, 'seq', 'head')
Inputs may be any that keep to these rules, and one draw needn't show every extreme that they name: `page_table`: page p holds prefilled tokens p * 32 to p * 32 + 31. Slot j of request r is live when j * 32 < lengths[r]. Over the live slots of one parity of j of the 8 requests r with one value of r // 8, at most 16 pages lie in any one block of 32 consecutive pages; this bound is reached.
All inputs are finite; a program needn't handle non-finite values.
Results may differ from a plain program's by a relative error of at most 0.007.
The roundings to bfloat16 on the way count: a program that leaves them out, or rounds other values in their place, can miss the bound.
Values may be sent and summed in bfloat16 or wider, within the bound.
No kernel may reach another device: no remote copies, remote signals or barrier semaphores. Data moves between devices by JAX's collectives and lax.ppermute only.
A program may use at most 128 MiB of HBM per device.

v0:
```python
import jax
import jax.numpy as jnp
from jax import lax
from jax.sharding import PartitionSpec as P

KVH = 8
HD = 128
QH = 64
PAGE = 32


EPSILON = 1e-05
NEGATIVE = -1e30


def combined_all(shard, axis, combine):
    everything = jax.tree.map(lambda part: lax.all_gather(part, axis), shard)
    first = jax.tree.map(lambda part: part[0], everything)

    def turn(k, so_far):
        return combine(so_far, jax.tree.map(lambda part: part[k], everything))

    return lax.fori_loop(1, lax.axis_size(axis), turn, first)


def clipped(raw_keys, raw_values, smooth, group_scale):
    keys_out = jnp.clip(raw_keys / smooth, -8.0 * group_scale[0], 7.0 * group_scale[0])
    values_out = jnp.clip(raw_values, -8.0 * group_scale[1], 7.0 * group_scale[1])
    return (keys_out, values_out)


def combine(earlier, latter):
    highest = jnp.maximum(earlier[0], latter[0])
    left_scale = jnp.exp(earlier[0] - highest)
    right_scale = jnp.exp(latter[0] - highest)
    return (
        highest,
        earlier[1] * left_scale + latter[1] * right_scale,
        earlier[2] * left_scale[..., None] + latter[2] * right_scale[..., None],
    )


def on_device(
    hidden, key_weight, value_weight, group_scale, new_kv, decode_query, page_table, lengths
):
    tokens = hidden.shape[0]
    columns = key_weight.shape[1]
    heads_kv = columns // HD
    group_size = QH // KVH
    raw_keys = jnp.dot(
        hidden,
        lax.all_gather(key_weight, ("seq", "rep"), axis=0, tiled=True),
        preferred_element_type=jnp.float32,
    )
    raw_values = jnp.dot(
        hidden,
        lax.all_gather(value_weight, ("seq", "rep"), axis=0, tiled=True),
        preferred_element_type=jnp.float32,
    )
    local_max = jnp.max(jnp.abs(raw_keys), axis=0)
    smoothing = jnp.sqrt(lax.pmax(local_max, ("seq", "rep")) + EPSILON)
    keys_clip, values_clip = clipped(raw_keys, raw_values, smoothing, group_scale)
    kv_cache = jnp.stack([keys_clip, values_clip], axis=1).astype(jnp.bfloat16)
    groups = lax.axis_size("seq")
    owners = lax.axis_size("rep")
    sources = groups * owners
    pages_dev = tokens // PAGE
    requests = page_table.shape[0]
    slot_count = page_table.shape[1]
    per_group = requests // groups
    entries = per_group * slot_count
    capacity = entries // (owners * sources)
    page_pool = kv_cache.reshape(pages_dev, PAGE, 2, columns)
    slot_ids = jnp.arange(slot_count, dtype=jnp.int32)
    live_slots = (slot_ids[None, :] * PAGE < lengths[:, None]).reshape(groups, entries)
    owner_of = jnp.broadcast_to(slot_ids % owners, (requests, slot_count)).reshape(groups, entries)
    source_of = (page_table // pages_dev).reshape(groups, entries)
    local_of = (page_table % pages_dev).reshape(groups, entries)
    my_index = lax.axis_index(("seq", "rep"))
    owner_hot = owner_of[:, None, :] == jnp.arange(owners, dtype=jnp.int32)[None, :, None]
    sending = live_slots[:, None, :] & owner_hot & (source_of == my_index)[:, None, :]
    send_rank = jnp.cumsum(sending.astype(jnp.int32), axis=2) - 1
    chosen = sending[:, :, None, :] & (
        send_rank[:, :, None, :] == jnp.arange(capacity, dtype=jnp.int32)[None, None, :, None]
    )
    send_page = jnp.sum(jnp.where(chosen, local_of[:, None, None, :], 0), axis=3)
    send_live = jnp.any(chosen, axis=3)
    outgoing = jnp.where(
        send_live[..., None, None, None], page_pool[send_page], jnp.zeros((), jnp.bfloat16)
    )
    incoming = lax.all_to_all(
        outgoing.reshape((sources,) + outgoing.shape[2:]),
        ("seq", "rep"),
        split_axis=0,
        concat_axis=0,
        tiled=True,
    )
    received = incoming.reshape((sources * capacity,) + incoming.shape[-3:])
    my_group = lax.axis_index("seq")
    my_owner = lax.axis_index("rep")
    mine_table = lax.dynamic_slice_in_dim(page_table, my_group * per_group, per_group, 0)
    mine_length = lax.dynamic_slice_in_dim(lengths, my_group * per_group, per_group, 0)
    half_slots = slot_count // owners
    owned_table = lax.dynamic_index_in_dim(
        mine_table.reshape(per_group, half_slots, owners), my_owner, 2, keepdims=False
    )
    owned_slot = jnp.arange(half_slots, dtype=jnp.int32) * owners + my_owner
    owned_live = owned_slot[None, :] * PAGE < mine_length[:, None]
    owned_source = (owned_table // pages_dev).reshape(-1)
    flat_live = owned_live.reshape(-1)
    source_hot = (
        owned_source[:, None] == jnp.arange(sources, dtype=jnp.int32)[None, :]
    ) & flat_live[:, None]
    running = jnp.cumsum(source_hot.astype(jnp.int32), axis=0)
    arrival = jnp.sum(jnp.where(source_hot, running, 0), axis=1) - 1
    slot_index = jnp.where(flat_live, owned_source * capacity + arrival, 0)
    owned_pages = received[slot_index].reshape(per_group, half_slots * PAGE, 2, columns)
    position = (owned_slot[:, None] * PAGE + jnp.arange(PAGE, dtype=jnp.int32)[None, :]).reshape(-1)
    valid_keys = position[None, :] < mine_length[:, None]
    score_scale = HD ** (-0.5)
    smooth_query = jnp.repeat(smoothing.reshape(heads_kv, HD), group_size, axis=0).reshape(-1)
    queries = (decode_query.astype(jnp.float32) * smooth_query).astype(jnp.bfloat16)
    step_count = queries.shape[0]
    queries = queries.reshape(step_count, per_group, heads_kv, group_size, HD)
    cache_keys = owned_pages[:, :, 0].reshape(per_group, -1, heads_kv, HD)
    cache_values = owned_pages[:, :, 1].reshape(per_group, -1, heads_kv, HD)
    scores = (
        jnp.einsum("trkgd,rnkd->rktgn", queries, cache_keys, preferred_element_type=jnp.float32)
        * score_scale
    )
    key_mask = valid_keys[:, None, None, None, :]
    scores = jnp.where(key_mask, scores, NEGATIVE)
    row_max = jnp.max(scores, axis=-1)
    weights = jnp.where(key_mask, jnp.exp(scores - row_max[..., None]), 0.0)
    row_total = jnp.sum(weights, axis=-1)
    summed = jnp.einsum(
        "rktgn,rnkd->rktgd",
        weights.astype(jnp.bfloat16),
        cache_values,
        preferred_element_type=jnp.float32,
    )
    merged = combined_all((row_max, row_total, summed), "rep", combine)
    fresh_keys, fresh_values = clipped(
        new_kv[:, :, 0].astype(jnp.float32),
        new_kv[:, :, 1].astype(jnp.float32),
        smoothing,
        group_scale,
    )
    fresh_keys = fresh_keys.astype(jnp.bfloat16).reshape(step_count, per_group, heads_kv, HD)
    fresh_values = fresh_values.astype(jnp.bfloat16).reshape(step_count, per_group, heads_kv, HD)
    fresh_scores = (
        jnp.einsum("trkgd,urkd->rktgu", queries, fresh_keys, preferred_element_type=jnp.float32)
        * score_scale
    )
    causal = jnp.arange(step_count)[None, :] <= jnp.arange(step_count)[:, None]
    causal_mask = causal[None, None, :, None, :]
    fresh_scores = jnp.where(causal_mask, fresh_scores, NEGATIVE)
    fresh_max = jnp.max(fresh_scores, axis=-1)
    fresh_weights = jnp.where(causal_mask, jnp.exp(fresh_scores - fresh_max[..., None]), 0.0)
    fresh_total = jnp.sum(fresh_weights, axis=-1)
    fresh_summed = jnp.einsum(
        "rktgu,urkd->rktgd",
        fresh_weights.astype(jnp.bfloat16),
        fresh_values,
        preferred_element_type=jnp.float32,
    )
    final_max, final_total, final_summed = combine(merged, (fresh_max, fresh_total, fresh_summed))
    attention = (final_summed / final_total[..., None]).astype(jnp.bfloat16)
    attention = attention.transpose(2, 0, 1, 3, 4).reshape(
        step_count, per_group, heads_kv * group_size * HD
    )
    return (kv_cache, smoothing, attention)


def solution(mesh):
    placed = (
        P(("seq", "rep"), None),
        P(("seq", "rep"), "head"),
        P(("seq", "rep"), "head"),
        P(None, "head"),
        P(None, "seq", None, "head"),
        P(None, "seq", "head"),
        P(),
        P(),
    )
    return jax.shard_map(
        on_device,
        mesh=mesh,
        in_specs=placed,
        out_specs=(P(("seq", "rep"), None, "head"), P("head"), P(None, "seq", "head")),
        check_vma=False,
    )
```

profile of v0, /device:TPU:0, one launch (start us, length us, event | category | flops | bytes accessed | tf_op | source)
XLA Modules:
  0.0 254.8 jit_solution(7717836365928281233)
XLA Ops:
  7.2 0.7 all-gather.6.cloned.1.call-update
  7.9 0.7 all-gather.8.cloned.1.call-update
  8.7 0.7 fusion.39
  9.4 0.1 eq.80
  9.5 0.1 eq.76
  9.6 0.7 lt.141
  10.4 0.1 lt.149
  10.5 0.1 lt.143
  10.5 0.7 add_select_fusion
  11.3 0.1 broadcast_in_dim.135
  11.4 0.1 lt.147
  11.5 0.1 broadcast_in_dim.132
  11.6 2.4 reduce-window.6
  14.0 0.1 slice.63
  14.1 0.1 copy.65
  14.2 0.1 copy.66
  14.3 0.1 add_add_fusion
  14.5 0.1 lt.139
  14.5 0.1 broadcast_in_dim.130
  14.6 0.2 select_reduce_fusion
  14.9 0.1 reshape.468
  15.0 0.2 fusion.18
  15.2 0.8 slice_multiply_fusion.7
  16.0 43.2 %all-gather.6.cloned.1.call-done = bf16[8192,256]{1,0:T(8,128)(2,1)} async-done(((bf16[1024,256]{1,0:T(8,128)(2,1)}), bf16[8192,256]{1,0:T(8,128)(2,1)}) %all-gather.6.cloned.1.call-update) | async-done | bytes 4194320 | tf_op jit(solution)/shard_map/all_gather | solution.py:52
  59.2 9.3 %abs_reduce_fusion = (f32[256]{0:T(256)S(1)}, f32[1024,256]{1,0:T(8,128)S(1)}) fusion(bf16[1024,8192]{1,0:T(8,128)(2,1)} %param.8, bf16[8192,256]{1,0:T(8,128)(2,1)} %all-gather.6.cloned.1.call-done), kind=kOutput, calls=%fused_computation.19 | convolution fusion | flops 4295491584 | bytes 22021120 | tf_op jit(solution)/shard_map/dot_general | solution.py:50
  68.6 16.0 %pmax.7 = f32[256]{0:T(256)S(1)} all-reduce(f32[256]{0:T(256)S(1)} %get-tuple-element.55), channel_id=1, replica_groups=mesh['seq'=4,'head'=4,'rep'=2] {'seq','rep'}, use_global_device_ids=true, to_apply=%region_1.0 | all-reduce | flops 256 | bytes 2048 | tf_op jit(solution)/shard_map/pmax | solution.py:61
  84.6 0.1 minimum_convert_fusion
  84.7 22.1 %all-gather.8.cloned.1.call-done = bf16[8192,256]{1,0:T(8,128)(2,1)} async-done(((bf16[1024,256]{1,0:T(8,128)(2,1)}), bf16[8192,256]{1,0:T(8,128)(2,1)}) %all-gather.8.cloned.1.call-update) | async-done | bytes 4194320 | tf_op jit(solution)/shard_map/all_gather | solution.py:57
  106.8 11.4 %fusion.2 = bf16[1024,256]{1,0:T(8,128)(2,1)S(1)} fusion(bf16[1024,8192]{1,0:T(8,128)(2,1)} %param.8, bf16[8192,256]{1,0:T(8,128)(2,1)} %all-gather.8.cloned.1.call-done, f32[256]{0:T(256)S(1)} %bitcast.92, f32[256]{0:T(256)S(1)} %bitcast.94), kind=kOutput, calls=%fused_computation.7 | convolution fusion | flops 4296278016 | bytes 21497856 | tf_op jit(solution)/shard_map/dot_general | solution.py:55
  118.3 0.1 pad_maximum_fusion.1
  118.4 2.7 %gather_fusion = bf16[128,32,2,256]{3,1,2,0:T(8,128)(2,1)} fusion(bf16[32,32,2,256]{3,1,0,2:T(8,128)(2,1)S(1)} %pad_maximum_fusion.1, s32[1024]{0:T(1024)S(1)} %pad_clamp_fusion.1), kind=kCustom, calls=%fused_computation | custom fusion | bytes 8389120 | tf_op jit(solution)/shard_map/gather | solution.py:89
  121.1 4.5 %broadcast_select_fusion = bf16[8,16,32,2,256]{4,2,3,1,0:T(8,128)(2,1)} fusion(bf16[8,16,32,2,256]{4,2,3,1,0:T(8,128)(2,1)} %bitcast.74, pred[8,16]{1,0:T(8,128)(4,1)S(1)} %broadcast_in_dim.133), kind=kLoop, calls=%fused_computation.2 | loop fusion | flops 2097152 | bytes 8388736 | tf_op jit(solution)/shard_map/jit(_where)/select_n | solution.py:88
  125.6 4.9 %all-to-all-start = ((bf16[8,16,32,2,256]{4,2,3,1,0:T(8,128)(2,1)}), bf16[8,16,32,2,256]{4,2,3,1,0:T(8,128)(2,1)}, u32[]{:S(2)}, u32[]{:S(2)}) async-start(bf16[8,16,32,2,256]{4,2,3,1,0:T(8,128)(2,1)} %broadcast_select_fusion), calls=%async_computation | async-start | bytes 8388608 | tf_op jit(solution)/shard_map/all_to_all | solution.py:91
  130.5 0.1 dynamic_slice.22
  130.6 0.1 broadcast_compare_fusion.1
  130.7 0.1 lt.157
  130.8 0.1 lt.159
  130.9 0.7 constant_dynamic-slice_fusion.1
  131.5 0.1 copy.67
  131.7 0.1 squeeze.38
  131.8 0.1 squeeze.37
  131.9 0.1 fusion.27
  132.0 0.2 reduce_window_sum.29
  132.2 0.1 add.166
  132.3 0.2 select_reduce_fusion.1
  132.7 0.1 fusion.66
  132.8 0.1 pad_maximum_fusion
  132.9 2.0 copy.80
  135.0 0.7 fusion.58
  135.7 0.2 fusion.21
  135.9 88.4 %all-to-all-done = bf16[8,16,32,2,256]{4,2,3,1,0:T(8,128)(2,1)} async-done(((bf16[8,16,32,2,256]{4,2,3,1,0:T(8,128)(2,1)}), bf16[8,16,32,2,256]{4,2,3,1,0:T(8,128)(2,1)}, u32[]{:S(2)}, u32[]{:S(2)}) %all-to-all-start) | async-done | bytes 4194336 | tf_op jit(solution)/shard_map/all_to_all | solution.py:91
  224.3 5.0 %gather_fusion.1 = bf16[128,32,2,256]{3,1,2,0:T(8,128)(2,1)} fusion(bf16[128,32,2,256]{3,1,2,0:T(8,128)(2,1)} %bitcast.14, s32[1024]{0:T(1024)S(1)} %pad_clamp_fusion), kind=kCustom, calls=%fused_computation.1 | custom fusion | bytes 8389120 | tf_op jit(solution)/shard_map/gather | solution.py:117
  229.3 2.6 %copy.70 = bf16[128,32,2,256]{3,1,0,2:T(8,128)(2,1)S(1)} copy(bf16[128,32,2,256]{3,1,2,0:T(8,128)(2,1)} %gather_fusion.1) | data formatting | bytes 8388608 | tf_op jit(solution)/shard_map/gather | solution.py:117
  231.9 1.7 fusion.56
  233.5 2.4 copy.74
  236.0 2.9 %copy.71 = bf16[8,512,1,256]{1,3,0,2:T(8,128)(2,1)S(1)} copy(bf16[8,512,1,256]{3,1,0,2:T(8,128)(2,1)} %get-tuple-element.47) | data formatting | bytes 4194304 | tf_op jit(solution)/shard_map/slice | solution.py:125
  238.8 0.5 fusion.57
  239.4 2.0 all-gather.1
  241.3 0.4 fusion.8
  241.7 0.8 fusion.10
  242.5 2.2 all-gather
  244.7 1.8 all-gather.2
  246.6 0.6 fusion.6
  247.2 0.7 reshape.463
  (45 shorter events, 0.8 us)
Async XLA Ops:
  7.2 52.0 %all-gather.6.cloned.1.call-start = ((), (), s32[]{:S(2)}) async-start(), calls=%async_computation.1 | async-start | bytes 4718592 | tf_op jit(solution)/shard_map/all_gather | solution.py:52
  7.9 98.9 %all-gather.8.cloned.1.call-start = ((), (), s32[]{:S(2)}) async-start(), calls=%async_computation.2 | async-start | bytes 4718592 | tf_op jit(solution)/shard_map/all_gather | solution.py:57
  84.6 48.1 %copy-start.3 = (f32[256]{0:T(256)}, f32[256]{0:T(256)S(1)}, u32[]{:S(2)}) copy-start(f32[256]{0:T(256)S(1)} %add_sqrt_fusion) | copy-start | bytes 3076
  125.6 4.9 %copy-start.4 = (s32[32]{0:T(128)S(1)}, s32[32]{0:T(128)}, u32[]{:S(2)}) copy-start(s32[32]{0:T(128)} %param.15) | copy-start | bytes 388
  125.6 7.0 %copy-start.2 = (bf16[4,8,2,256]{3,2,1,0:T(2,128)(2,1)S(1)}, bf16[4,8,2,256]{3,2,1,0:T(2,128)(2,1)}, u32[]{:S(2)}) copy-start(bf16[4,8,2,256]{3,2,1,0:T(2,128)(2,1)} %param.12) | copy-start | bytes 98308
  125.6 98.7 %all-to-all-start = ((bf16[8,16,32,2,256]{4,2,3,1,0:T(8,128)(2,1)}), bf16[8,16,32,2,256]{4,2,3,1,0:T(8,128)(2,1)}, u32[]{:S(2)}, u32[]{:S(2)}) async-start(bf16[8,16,32,2,256]{4,2,3,1,0:T(8,128)(2,1)} %broadcast_select_fusion), calls=%async_computation | async-start | bytes 8388608 | tf_op jit(solution)/shard_map/all_to_all | solution.py:91
  130.5 4.5 %copy-start.1 = (bf16[4,8,2048]{2,1,0:T(8,128)(2,1)S(1)}, bf16[4,8,2048]{2,1,0:T(8,128)(2,1)}, u32[]{:S(2)}) copy-start(bf16[4,8,2048]{2,1,0:T(8,128)(2,1)} %param.13) | copy-start | bytes 393220
  238.8 2.9 %copy-start = (bf16[8,512,1,256]{1,3,0,2:T(8,128)(2,1)S(1)}, bf16[8,512,1,256]{1,3,0,2:T(8,128)(2,1)}, u32[]{:S(2)}) copy-start(bf16[8,512,1,256]{1,3,0,2:T(8,128)(2,1)} %copy.74) | copy-start | bytes 6291460
Sparse Core Ops, SparseCore 0:
  9.6 49.5 all-gather.5
  60.8 45.9 all-gather.7
where the time goes:
time: 255 us
  waiting for transfers between devices  155 us (61%)
  local copies, waits for them, and re-layouts  23.4 us (9%)
  matrix products  23.4 us (9%)
  blocking collectives  22 us (9%)
  between operations  14.3 us (6%)
  other arithmetic  11.7 us (5%)
  starting transfers between devices  4.93 us (2%)
    all_to_all x1, waiting for transfers between devices, on_device(): lax.all_to_all(outgoing.reshape((sources,) + outgoing.shape[2:]), ('seq',...  88.4 us
    all_gather x1, waiting for transfers between devices, on_device(): lax.all_gather(key_weight, ('seq', 'rep'), axis=0, tiled=True)  43.2 us
    all_gather x1, waiting for transfers between devices, on_device(): lax.all_gather(value_weight, ('seq', 'rep'), axis=0, tiled=True)  22.1 us
    pmax x1, blocking collectives, on_device(): smoothing = jnp.sqrt(lax.pmax(local_max, ('seq', 'rep')) + EPSILON)  16 us
    dot_general x1, matrix products, on_device(): jnp.dot(hidden, lax.all_gather(value_weight, ('seq', 'rep'), axis=0, tile...  11.4 us
    dot_general x1, matrix products, on_device(): jnp.dot(hidden, lax.all_gather(key_weight, ('seq', 'rep'), axis=0, tiled=...  9.35 us
    gather x2, local copies, waits for them, and re-layouts, on_device(): received[slot_index].reshape(per_group, half_slots * PAGE, 2, columns)  7.6 us
    all_gather x3, blocking collectives, combined_all(): everything = jax.tree.map(lambda part: lax.all_gather(part, axis), shard)  6 us
  transfers between devices with their start and end apart: 3, of which 3 were waited for; matrix products, arithmetic and copies ran while one was open for 9% of the time, Pallas kernels for 0%

commit v1 on v0

v1 whole, which is shorter than its diff:
```python
import functools

import jax
import jax.numpy as jnp
from jax import lax
from jax.experimental import pallas as pl
from jax.experimental.pallas import tpu as pltpu
from jax.sharding import PartitionSpec as P

KVH = 8
HD = 128
QH = 64
PAGE = 32


EPSILON = 1e-05
NEGATIVE = -1e30
SHORT = 8


def shifted(x, axis, k):
    n = lax.axis_size(axis)
    return lax.ppermute(x, axis, [(i, (i + k) % n) for i in range(n)])


def from_all(x, axis):
    n = lax.axis_size(axis)
    if n > SHORT:
        order = (lax.axis_index(axis) - jnp.arange(n)) % n
        return list(lax.all_gather(x, axis)[order])
    return [x] + [shifted(x, axis, k) for k in range(1, n)]


def to_groups(x):
    n = lax.axis_size("seq")
    if n > SHORT:
        me, k = lax.axis_index("seq"), jnp.arange(n)
        back = lax.all_to_all(x[(me - k) % n], "seq", split_axis=0, concat_axis=0)
        return list(back[(me + k) % n])
    return [x[0]] + [shifted(x[k], "seq", -k) for k in range(1, n)]


def project_kernel(count, has_total, info, *refs):
    lefts, weights = refs[:count], refs[count : 2 * count]
    out = refs[-1]
    out[...] = refs[2 * count][...] if has_total else jnp.zeros_like(out)
    for j in range(count):

        @pl.when(info[count + j] == 1)
        def _(j=j):
            out[...] += jnp.dot(
                lefts[j][...], weights[j][...], preferred_element_type=jnp.float32
            )


def project(hidden, total, weights, where, live):
    tokens = hidden.shape[0]
    depth, columns = weights[0].shape
    count = len(weights)
    tile = min(tokens, 256)
    info = jnp.stack([jnp.asarray(v, jnp.int32) for v in list(where) + list(live)])

    def left_spec(j):
        return pl.BlockSpec((tile, depth), lambda i, info: (i * info[count + j], info[j]))

    total_spec = pl.BlockSpec((tile, columns), lambda i, info: (i, 0))
    has_total = total is not None
    return pl.pallas_call(
        functools.partial(project_kernel, count, has_total),
        out_shape=jax.ShapeDtypeStruct((tokens, columns), jnp.float32),
        grid_spec=pltpu.PrefetchScalarGridSpec(
            num_scalar_prefetch=1,
            grid=(tokens // tile,),
            in_specs=[left_spec(j) for j in range(count)]
            + [pl.BlockSpec((depth, columns), lambda i, info: (0, 0))] * count
            + [total_spec] * has_total,
            out_specs=total_spec,
        ),
        cost_estimate=pl.CostEstimate(
            flops=2 * tokens * depth * columns * count,
            bytes_accessed=2 * count * depth * (tokens + columns) + 8 * tokens * columns,
            transcendentals=0,
        ),
        input_output_aliases={1 + 2 * count: 0} if has_total else {},
        name="project",
    )(info, *([hidden] * count), *weights, *([total] if has_total else []))


def score_kernel(parts, steps, scale, group, query, smooth, count, *refs):
    keys, (probs, highest, total), scores = refs[:parts], refs[parts:-1], refs[-1]
    tokens = keys[0].shape[0]
    scaled = (query[0].astype(jnp.float32) * smooth[...]).astype(jnp.bfloat16)
    for p in range(parts):
        scores[:, p * tokens : (p + 1) * tokens] = lax.dot_general(
            scaled, keys[p][...], (((1,), (1,)), ((), ())), preferred_element_type=jnp.float32
        )
    requests = count.shape[1]
    rows = scores.shape[0]
    group_rows = rows // (steps * requests)
    pair = 2 if requests % 2 == 0 else 1
    for first in range(0, requests, pair):
        times = jnp.concatenate(
            [
                jnp.broadcast_to(count[0, first + a : first + a + 1, :], (group_rows, parts * tokens))
                for a in range(pair)
            ],
            axis=0,
        )
        for step in range(steps):
            start = (step * requests + first) * group_rows
            at = pl.ds(start, pair * group_rows)
            raw = jnp.where(times > 0.0, scores[at, :] * scale, NEGATIVE)
            top = jnp.max(raw, axis=1, keepdims=True)
            expd = jnp.exp(raw - top)
            highest[0, at, :] = top
            total[0, at, :] = jnp.sum(expd * times, axis=1, keepdims=True)
            probs[0, at, :] = (expd.astype(jnp.bfloat16).astype(jnp.float32) * times).astype(
                jnp.bfloat16
            )


def score(groups, query, smooth, count, keys, steps, scale):
    slots, rows, width = query.shape
    tokens = keys[0].shape[0]
    parts = len(keys)
    requests = count.shape[1]
    slot_spec = pl.BlockSpec((1, rows, 1), lambda k, group: (k, 0, 0))
    return pl.pallas_call(
        functools.partial(score_kernel, parts, steps, scale),
        out_shape=(
            jax.ShapeDtypeStruct((slots, rows, parts * tokens), jnp.bfloat16),
            jax.ShapeDtypeStruct((slots, rows, 1), jnp.float32),
            jax.ShapeDtypeStruct((slots, rows, 1), jnp.float32),
        ),
        grid_spec=pltpu.PrefetchScalarGridSpec(
            num_scalar_prefetch=1,
            grid=(slots,),
            in_specs=[
                pl.BlockSpec((1, rows, width), lambda k, group: (k, 0, 0)),
                pl.BlockSpec((1, width), lambda k, group: (0, 0)),
                pl.BlockSpec((1, requests, parts * tokens), lambda k, group: (group[k], 0, 0)),
            ]
            + [pl.BlockSpec((tokens, width), lambda k, group: (0, 0))] * parts,
            out_specs=(
                pl.BlockSpec((1, rows, parts * tokens), lambda k, group: (k, 0, 0)),
                slot_spec,
                slot_spec,
            ),
            scratch_shapes=[pltpu.VMEM((rows, parts * tokens), jnp.float32)],
        ),
        cost_estimate=pl.CostEstimate(
            flops=2 * slots * rows * width * parts * tokens,
            bytes_accessed=2 * slots * rows * parts * tokens,
            transcendentals=slots * rows * parts * tokens,
        ),
        name="score",
    )(groups, query, smooth, count, *keys)


def weigh_kernel(parts, probs, *refs):
    values, out = refs[:parts], refs[-1]
    tokens = values[0].shape[0]
    out[0] = sum(
        jnp.dot(
            probs[0, :, p * tokens : (p + 1) * tokens],
            values[p][...],
            preferred_element_type=jnp.float32,
        )
        for p in range(parts)
    ).astype(jnp.bfloat16)


def weigh(probs, values):
    slots, rows, _ = probs.shape
    tokens, width = values[0].shape
    parts = len(values)
    return pl.pallas_call(
        functools.partial(weigh_kernel, parts),
        out_shape=jax.ShapeDtypeStruct((slots, rows, width), jnp.bfloat16),
        grid=(slots,),
        in_specs=[pl.BlockSpec((1, rows, parts * tokens), lambda k: (k, 0, 0))]
        + [pl.BlockSpec((tokens, width), lambda k: (0, 0))] * parts,
        out_specs=pl.BlockSpec((1, rows, width), lambda k: (k, 0, 0)),
        cost_estimate=pl.CostEstimate(
            flops=2 * slots * rows * width * parts * tokens,
            bytes_accessed=2 * slots * rows * parts * tokens,
            transcendentals=0,
        ),
        name="weigh",
    )(probs, *values)


def token_counts(page_table, lengths, first_pages, pages_dev):
    slots = page_table.shape[1]
    slot_ids = jnp.arange(slots, dtype=jnp.int32)
    whole_slots, rest = lengths // PAGE, lengths % PAGE
    pages = jnp.concatenate(
        [first + jnp.arange(pages_dev, dtype=jnp.int32) for first in first_pages]
    )
    same = page_table[:, :, None] == pages[None, None, :]
    whole = jnp.sum(same & (slot_ids[None, :] < whole_slots[:, None])[:, :, None], axis=1)
    last = jnp.sum(same & (slot_ids[None, :] == whole_slots[:, None])[:, :, None], axis=1)
    token = jnp.arange(pages.shape[0] * PAGE, dtype=jnp.int32)
    spread = token[None, :] // PAGE == jnp.arange(pages.shape[0], dtype=jnp.int32)[:, None]
    spread = spread.astype(jnp.bfloat16)
    whole = jnp.dot(whole.astype(jnp.bfloat16), spread, preferred_element_type=jnp.float32)
    last = jnp.dot(last.astype(jnp.bfloat16), spread, preferred_element_type=jnp.float32)
    return whole + jnp.where((token % PAGE)[None, :] < rest[:, None], last, 0.0)


def clip_keys(raw, smooth, scale):
    return jnp.clip(raw / smooth, -8.0 * scale[0], 7.0 * scale[0]).astype(jnp.bfloat16)


def clip_values(raw, scale):
    return jnp.clip(raw, -8.0 * scale[1], 7.0 * scale[1]).astype(jnp.bfloat16)


def my_part(x, parts, index, axis):
    size = x.shape[axis] // parts
    pieces = [lax.slice_in_dim(x, p * size, (p + 1) * size, axis=axis) for p in range(parts)]
    out = pieces[0]
    for p in range(1, parts):
        out = jnp.where(index == p, pieces[p], out)
    return out


def line_project(hidden, key_weight, value_weight):
    groups, owners = lax.axis_size("seq"), lax.axis_size("rep")
    my_group, my_owner = lax.axis_index("seq"), lax.axis_index("rep")

    def block_of(group):
        group = jnp.clip(group, 0, groups - 1)
        return [group * owners + (my_owner - k) % owners for k in range(owners)]

    weights = (key_weight, value_weight)
    moving = [(weight, weight) for weight in weights]
    totals = [
        project(hidden, None, from_all(w, "rep"), block_of(my_group), [jnp.int32(1)] * owners)
        for w in weights
    ]
    for hop in range(1, groups):
        here_left = (my_group - hop >= 0).astype(jnp.int32)
        here_right = (my_group + hop < groups).astype(jnp.int32)
        for j in range(len(weights)):
            left, right = moving[j]
            left = lax.ppermute(left, "seq", [(i, i + 1) for i in range(hop - 1, groups - 1)])
            right = lax.ppermute(right, "seq", [(i, i - 1) for i in range(1, groups - hop + 1)])
            moving[j] = (left, right)
            totals[j] = project(
                hidden,
                totals[j],
                from_all(left, "rep") + from_all(right, "rep"),
                block_of(my_group - hop) + block_of(my_group + hop),
                [here_left] * owners + [here_right] * owners,
            )
    return totals


def on_device(
    hidden, key_weight, value_weight, group_scale, new_kv, decode_query, page_table, lengths
):
    tokens = hidden.shape[0]
    columns = key_weight.shape[1]
    group_size = QH // KVH
    groups, owners = lax.axis_size("seq"), lax.axis_size("rep")
    my_group, my_owner = lax.axis_index("seq"), lax.axis_index("rep")
    assert columns // HD == owners
    pages_dev = tokens // PAGE
    step_count, per_group = decode_query.shape[:2]

    raw_query = my_part(decode_query, owners, my_owner, 2).reshape(-1, HD)

    owner_at = [(my_owner - k) % owners for k in range(owners)]
    yes = jnp.int32(1)

    if groups > SHORT:
        raw_keys, raw_values = (
            project(
                hidden,
                None,
                [lax.all_gather(weight, ("seq", "rep"), axis=0, tiled=True)],
                [0],
                [yes],
            )
            for weight in (key_weight, value_weight)
        )
    else:
        raw_keys, raw_values = line_project(hidden, key_weight, value_weight)
    queries = jnp.stack(from_all(raw_query, "seq"))

    local_max = jnp.max(jnp.abs(raw_keys), axis=0, keepdims=True)
    local_max = functools.reduce(jnp.maximum, from_all(local_max, "rep"))
    local_max = functools.reduce(jnp.maximum, from_all(local_max, "seq"))
    smooth = jnp.sqrt(local_max + EPSILON)
    smoothing = smooth.reshape(-1)
    keys = clip_keys(raw_keys, smooth, group_scale)
    values = clip_values(raw_values, group_scale)
    kv_cache = jnp.stack([keys, values], axis=1)

    def by_head(x):
        return [my_part(x, owners, my_owner, 1)] + [
            shifted(my_part(x, owners, (my_owner + k) % owners, 1), "rep", k)
            for k in range(1, owners)
        ]

    my_smooth = my_part(smooth, owners, my_owner, 1)
    first_pages = [(my_group * owners + owner) * pages_dev for owner in owner_at]
    counts = token_counts(page_table, lengths, first_pages, pages_dev)
    counts = counts.reshape(groups, per_group, -1)
    group_at = jnp.stack([(my_group - k) % groups for k in range(groups)])
    score_scale = HD ** (-0.5)
    probs, highest, total = score(
        group_at, queries, my_smooth, counts, by_head(keys), step_count, score_scale
    )
    summed = weigh(probs, by_head(values))
    stats = jnp.stack([highest[..., 0], total[..., 0]], axis=1)

    stats = jnp.stack(to_groups(stats))
    highest, total = stats[:, 0], stats[:, 1]

    shape = (step_count, per_group, group_size, HD)
    query = (raw_query.astype(jnp.float32) * my_smooth).astype(jnp.bfloat16).reshape(shape)
    my_kv = my_part(new_kv, owners, my_owner, 3).astype(jnp.float32)
    my_scale = my_part(group_scale, owners, my_owner, 1)
    fresh_keys = clip_keys(my_kv[:, :, 0], my_smooth, my_scale)
    fresh_values = clip_values(my_kv[:, :, 1], my_scale)
    fresh_scores = (
        jnp.einsum("trgd,urd->trgu", query, fresh_keys, preferred_element_type=jnp.float32)
        * score_scale
    )
    causal = jnp.arange(step_count)[None, :] <= jnp.arange(step_count)[:, None]
    causal = causal[:, None, None, :]
    fresh_scores = jnp.where(causal, fresh_scores, NEGATIVE)
    fresh_max = jnp.max(fresh_scores, axis=-1)
    fresh_weights = jnp.where(causal, jnp.exp(fresh_scores - fresh_max[..., None]), 0.0)
    fresh_total = jnp.sum(fresh_weights, axis=-1)
    fresh_summed = jnp.einsum(
        "trgu,urd->trgd",
        fresh_weights.astype(jnp.bfloat16),
        fresh_values,
        preferred_element_type=jnp.float32,
    )

    fresh_max, fresh_total = fresh_max.reshape(-1), fresh_total.reshape(-1)
    top = jnp.maximum(jnp.max(highest, axis=0), fresh_max)
    share = jnp.exp(highest - top[None])
    fresh_share = jnp.exp(fresh_max - top)
    norm = 1.0 / (jnp.sum(total * share, axis=0) + fresh_total * fresh_share)
    share, fresh_share = share * norm, fresh_share * norm
    attention = fresh_summed.reshape(-1, HD) * fresh_share[:, None]
    for k, part in enumerate(to_groups(summed)):
        attention = attention + part.astype(jnp.float32) * share[k][:, None]
    attention = attention.astype(jnp.bfloat16).reshape(step_count, per_group, group_size * HD)
    by_owner = from_all(attention, "rep")
    attention = jnp.concatenate(
        [
            functools.reduce(
                lambda out, k: jnp.where((my_owner - k) % owners == head, by_owner[k], out),
                range(1, owners),
                by_owner[0],
            )
            for head in range(owners)
        ],
        axis=2,
    )
    return (kv_cache, smoothing, attention)


def solution(mesh):
    placed = (
        P(("seq", "rep"), None),
        P(("seq", "rep"), "head"),
        P(("seq", "rep"), "head"),
        P(None, "head"),
        P(None, "seq", None, "head"),
        P(None, "seq", "head"),
        P(),
        P(),
    )
    return jax.shard_map(
        on_device,
        mesh=mesh,
        in_specs=placed,
        out_specs=(P(("seq", "rep"), None, "head"), P("head"), P(None, "seq", "head")),
        check_vma=False,
    )
```

time: 255 us -> 193 us (0.76)
  waiting for transfers between devices: 155 us -> 49.8 us
  Pallas kernels: 0 us -> 68.8 us
  starting transfers between devices: 4.93 us -> 40 us
  blocking collectives: 22 us -> 0 us
  matrix products: 23.4 us -> 1.82 us
  local copies, waits for them, and re-layouts: 23.4 us -> 9.92 us
  between operations: 14.3 us -> 1.33 us
  other arithmetic: 11.7 us -> 19.6 us
    all_to_all x1 -> x0, waiting for transfers between devices: 88.4 us -> none  [on_device(): lax.all_to_all(outgoing.reshape((sources,) + outgoing.shape[2:]), ('seq',...]
    pallas_call x0 -> x10, Pallas kernels: none -> 68.8 us  [the longest x8 56.4 us: project(): pl.pallas_call(functools.partial(project_kernel, count, has_total), out_s...]
    all_gather x2 -> x0, waiting for transfers between devices: 65.3 us -> none  [the longest x1 43.2 us: on_device(): lax.all_gather(key_weight, ('seq', 'rep'), axis=0, tiled=True)]
    ppermute x0 -> x42, waiting for transfers between devices: none -> 49.8 us  [the longest x30 28.2 us: shifted(): return lax.ppermute(x, axis, [(i, (i + k) % n) for i in range(n)])]
    ppermute x0 -> x42, starting transfers between devices: none -> 40 us  [the longest x30 21.1 us: shifted(): return lax.ppermute(x, axis, [(i, (i + k) % n) for i in range(n)])]
    dot_general x6 -> x4, matrix products: 23.4 us -> 1.82 us  [the longest x1 0.91 us: token_counts(): jnp.dot(last.astype(jnp.bfloat16), spread, preferred_element_type=jnp.flo...]
    pmax x1 -> x0, blocking collectives: 16 us -> none  [on_device(): smoothing = jnp.sqrt(lax.pmax(local_max, ('seq', 'rep')) + EPSILON)]
    gather x3 -> x0, local copies, waits for them, and re-layouts: 10.3 us -> none  [the longest x2 7.6 us: on_device(): received[slot_index].reshape(per_group, half_slots * PAGE, 2, columns)]
  transfers between devices with their start and end apart: 3 -> 42, of which waited for: 3 -> 10; matrix products, arithmetic and copies ran while one was open for 9% -> 13% of each run, Pallas kernels for 0% -> 36%
where the time goes in v1:
time: 193 us; the launch traced here: 191 us
  Pallas kernels  68.8 us (36%)
  waiting for transfers between devices  49.8 us (26%)
  starting transfers between devices  40 us (21%)
  other arithmetic  19.6 us (10%)
  local copies, waits for them, and re-layouts  9.92 us (5%)
    pallas_call x8, Pallas kernels, project(): pl.pallas_call(functools.partial(project_kernel, count, has_total), out_s...  56.4 us
    ppermute x30, waiting for transfers between devices, shifted(): return lax.ppermute(x, axis, [(i, (i + k) % n) for i in range(n)])  28.2 us
    ppermute x30, starting transfers between devices, shifted(): return lax.ppermute(x, axis, [(i, (i + k) % n) for i in range(n)])  21.1 us
    ppermute x6, waiting for transfers between devices, line_project(): lax.ppermute(right, 'seq', [(i, i - 1) for i in range(1, groups - hop + 1)])  19 us
    ppermute x6, starting transfers between devices, line_project(): lax.ppermute(left, 'seq', [(i, i + 1) for i in range(hop - 1, groups - 1)])  11.2 us
    ppermute x6, starting transfers between devices, line_project(): lax.ppermute(right, 'seq', [(i, i - 1) for i in range(1, groups - hop + 1)])  7.72 us
    pallas_call x1, Pallas kernels, score(): pl.pallas_call(functools.partial(score_kernel, parts, steps, scale), out_...  7.68 us
    unnamed x51, local copies, waits for them, and re-layouts  6.7 us
  transfers between devices with their start and end apart: 42, of which 10 were waited for; matrix products, arithmetic and copies ran while one was open for 13% of the time, Pallas kernels for 36%

profile of v1, /device:TPU:0, one launch (start us, length us, event | category | flops | bytes accessed | tf_op | source)
XLA Modules:
  0.0 191.4 jit_solution(18189045218102321723)
XLA Ops:
  1.2 4.5 %collective-permute-start = (bf16[1024,256]{1,0:T(8,128)(2,1)}, bf16[1024,256]{1,0:T(8,128)(2,1)S(1)}, u32[]{:S(2)}, u32[]{:S(2)}) collective-permute-start(bf16[1024,256]{1,0:T(8,128)(2,1)} %refs_2_.8), channel_id=1, source_target_pairs={{0,8},{8,16},{16,24},{1,9},{9,17},{17,25},{2,10},{10,18},{18,26},{... | collective-permute-start | bytes 1572872 | tf_op jit(solution)/shard_map/ppermute | solution.py:247
  5.7 1.3 collective-permute-start.4
  7.0 1.5 bitcast_convert_fusion
  8.6 2.7 %collective-permute-start.30 = (bf16[256,128]{1,0:T(8,128)(2,1)S(1)}, bf16[256,128]{1,0:T(8,128)(2,1)S(1)}, u32[]{:S(2)}, u32[]{:S(2)}) collective-permute-start(bf16[256,128]{1,0:T(8,128)(2,1)S(1)} %reshape.220), channel_id=1, source_target_pairs={{0,8},{8,16},{16,24},{24,0},{1,9},{9,17},{17,25},{25,1},{2,10},{10... | collective-permute-start | bytes 196616 | tf_op jit(solution)/shard_map/ppermute | solution.py:23
  12.1 1.3 convert_reduce_fusion
  13.7 11.8 %collective-permute-done.30 = bf16[256,128]{1,0:T(8,128)(2,1)S(1)} collective-permute-done((bf16[256,128]{1,0:T(8,128)(2,1)S(1)}, bf16[256,128]{1,0:T(8,128)(2,1)S(1)}, u32[]{:S(2)}, u32[]{:S(2)}) %collective-permute-start.30) | collective-permute-done | bytes 65568 | tf_op jit(solution)/shard_map/ppermute | solution.py:23
  25.5 0.9 fusion.1.count
  26.4 4.7 %collective-permute-done.31 = bf16[256,128]{1,0:T(8,128)(2,1)} collective-permute-done((bf16[256,128]{1,0:T(8,128)(2,1)S(1)}, bf16[256,128]{1,0:T(8,128)(2,1)}, u32[]{:S(2)}, u32[]{:S(2)}) %collective-permute-start.31) | collective-permute-done | bytes 65568 | tf_op jit(solution)/shard_map/ppermute | solution.py:23
  31.1 4.2 %collective-permute-done.32 = bf16[256,128]{1,0:T(8,128)(2,1)S(1)} collective-permute-done((bf16[256,128]{1,0:T(8,128)(2,1)S(1)}, bf16[256,128]{1,0:T(8,128)(2,1)S(1)}, u32[]{:S(2)}, u32[]{:S(2)}) %collective-permute-start.32) | collective-permute-done | bytes 65568 | tf_op jit(solution)/shard_map/ppermute | solution.py:23
  35.4 1.6 collective-permute-start.17
  37.0 1.3 collective-permute-start.21
  38.4 0.8 slice_multiply_fusion.3
  39.2 1.5 collective-permute-start.1
  41.7 0.8 fusion.21
  42.4 2.6 %collective-permute-done.17.refs_4_ = bf16[1024,256]{1,0:T(8,128)(2,1)S(1)} collective-permute-done((bf16[1024,256]{1,0:T(8,128)(2,1)}, bf16[1024,256]{1,0:T(8,128)(2,1)S(1)}, u32[]{:S(2)}, u32[]{:S(2)}) %collective-permute-start.17) | collective-permute-done | bytes 524320 | tf_op jit(solution)/shard_map/ppermute | solution.py:247
  45.1 1.3 collective-permute-start.5
  46.3 2.8 %collective-permute-done.21.refs_6_ = bf16[1024,256]{1,0:T(8,128)(2,1)S(1)} collective-permute-done((bf16[1024,256]{1,0:T(8,128)(2,1)}, bf16[1024,256]{1,0:T(8,128)(2,1)S(1)}, u32[]{:S(2)}, u32[]{:S(2)}) %collective-permute-start.21) | collective-permute-done | bytes 524320 | tf_op jit(solution)/shard_map/ppermute | solution.py:248
  49.6 0.7 slice_select_fusion.1
  50.3 1.5 collective-permute-start.18
  51.8 1.3 collective-permute-start.22
  53.8 8.4 %collective-permute-done.5.refs_6_ = bf16[1024,256]{1,0:T(8,128)(2,1)} collective-permute-done((bf16[1024,256]{1,0:T(8,128)(2,1)S(1)}, bf16[1024,256]{1,0:T(8,128)(2,1)}, u32[]{:S(2)}, u32[]{:S(2)}) %collective-permute-start.5) | collective-permute-done | bytes 524320 | tf_op jit(solution)/shard_map/ppermute | solution.py:248
  62.2 1.5 collective-permute-start.2
  64.2 1.3 collective-permute-start.6
  65.5 7.8 %collective-permute-done.22.refs_6_ = bf16[1024,256]{1,0:T(8,128)(2,1)S(1)} collective-permute-done((bf16[1024,256]{1,0:T(8,128)(2,1)S(1)}, bf16[1024,256]{1,0:T(8,128)(2,1)S(1)}, u32[]{:S(2)}, u32[]{:S(2)}) %collective-permute-start.22) | collective-permute-done | bytes 524320 | tf_op jit(solution)/shard_map/ppermute | solution.py:248
  73.3 0.8 copy-done.8
  74.2 0.7 stack.203.info
  74.9 0.7 stack.194.info
  76.2 1.6 pad_maximum_fusion.1.query
  77.8 6.2 %project.8.refs_8_ = f32[1024,256]{1,0:T(8,128)} custom-call(s32[4]{0:T(128)} %pad_add_fusion.info, bf16[1024,8192]{1,0:T(8,128)(2,1)} %refs_3_.11, bf16[1024,8192]{1,0:T(8,128)(2,1)} %refs_3_.11, bf16[1024,256]{1,0:T(8,128)(2,1)} %refs_2_.8, bf16[1024,256]{1,0:T(8,128)(2,1)} %copy-done.3), custom_call_target="tpu_custom_call" | custom-call | flops 1073741824 | bytes 7340032 | tf_op jit(solution)/shard_map/project/pallas_call | solution.py:68
  84.0 6.3 %project.12.refs_8_ = f32[1024,256]{1,0:T(8,128)} custom-call(s32[4]{0:T(128)} %pad_add_fusion.info, bf16[1024,8192]{1,0:T(8,128)(2,1)} %refs_3_.11, bf16[1024,8192]{1,0:T(8,128)(2,1)} %refs_3_.11, bf16[1024,256]{1,0:T(8,128)(2,1)} %refs_2_.12, bf16[1024,256]{1,0:T(8,128)(2,1)} %copy-done.4), custom_call_target="tpu_custom_call" | custom-call | flops 1073741824 | bytes 7340032 | tf_op jit(solution)/shard_map/project/pallas_call | solution.py:68
  90.4 0.7 collective-permute-start.19
  91.7 1.3 collective-permute-start.23
  93.0 7.3 %project.9.refs_8_ = f32[1024,256]{1,0:T(8,128)} custom-call(s32[8]{0:T(128)} %stack.203.info, bf16[1024,8192]{1,0:T(8,128)(2,1)} %refs_3_.11, bf16[1024,8192]{1,0:T(8,128)(2,1)} %refs_3_.11, bf16[1024,8192]{1,0:T(8,128)(2,1)} %refs_3_.11, bf16[1024,8192]{1,0:T(8,128)(2,1)} %refs_3_.11, bf16[1024,256]{1,0:T(8,128)(2,1)} %copy-done.1, ...), custom_call_target="tpu_custom_call", output_to_operand_aliasing={{}: (9, {})} | custom-call | flops 2147483648 | bytes 12582912 | tf_op jit(solution)/shard_map/project/pallas_call | solution.py:68
  100.8 7.3 %project.13.refs_8_ = f32[1024,256]{1,0:T(8,128)} custom-call(s32[8]{0:T(128)} %stack.203.info, bf16[1024,8192]{1,0:T(8,128)(2,1)} %refs_3_.11, bf16[1024,8192]{1,0:T(8,128)(2,1)} %refs_3_.11, bf16[1024,8192]{1,0:T(8,128)(2,1)} %refs_3_.11, bf16[1024,8192]{1,0:T(8,128)(2,1)} %refs_3_.11, ...), custom_call_target="tpu_custom_call", output_to_operand_aliasing={{}: (9, {})} | custom-call | flops 2147483648 | bytes 12582912 | tf_op jit(solution)/shard_map/project/pallas_call | solution.py:68
  108.1 7.3 %project.10.refs_8_ = f32[1024,256]{1,0:T(8,128)} custom-call(s32[8]{0:T(128)} %stack.194.info, bf16[1024,8192]{1,0:T(8,128)(2,1)} %refs_3_.11, bf16[1024,8192]{1,0:T(8,128)(2,1)} %refs_3_.11, bf16[1024,8192]{1,0:T(8,128)(2,1)} %refs_3_.11, bf16[1024,8192]{1,0:T(8,128)(2,1)} %refs_3_.11, ...), custom_call_target="tpu_custom_call", output_to_operand_aliasing={{}: (9, {})} | custom-call | flops 2147483648 | bytes 12582912 | tf_op jit(solution)/shard_map/project/pallas_call | solution.py:68
  116.0 0.8 copy-done.15
  116.8 7.3 %project.14.refs_8_ = f32[1024,256]{1,0:T(8,128)} custom-call(s32[8]{0:T(128)} %stack.194.info, bf16[1024,8192]{1,0:T(8,128)(2,1)} %refs_3_.11, bf16[1024,8192]{1,0:T(8,128)(2,1)} %refs_3_.11, bf16[1024,8192]{1,0:T(8,128)(2,1)} %refs_3_.11, bf16[1024,8192]{1,0:T(8,128)(2,1)} %refs_3_.11, ...), custom_call_target="tpu_custom_call", output_to_operand_aliasing={{}: (9, {})} | custom-call | flops 2147483648 | bytes 12582912 | tf_op jit(solution)/shard_map/project/pallas_call | solution.py:68
  124.2 0.8 copy-done.16
  124.9 0.8 copy-done.17
  125.7 7.3 %project.11 = f32[1024,256]{1,0:T(8,128)} custom-call(s32[8]{0:T(128)} %stack.185.info, bf16[1024,8192]{1,0:T(8,128)(2,1)} %refs_3_.11, bf16[1024,8192]{1,0:T(8,128)(2,1)} %refs_3_.11, bf16[1024,8192]{1,0:T(8,128)(2,1)} %refs_3_.11, bf16[1024,8192]{1,0:T(8,128)(2,1)} %refs_3_.11, ...), custom_call_target="tpu_custom_call", output_to_operand_aliasing={{}: (9, {})} | custom-call | flops 2147483648 | bytes 12582912 | tf_op jit(solution)/shard_map/project/pallas_call | solution.py:68
  133.0 1.3 abs_reduce_fusion
  134.6 7.4 %project.15 = f32[1024,256]{1,0:T(8,128)} custom-call(s32[8]{0:T(128)} %stack.185.info, bf16[1024,8192]{1,0:T(8,128)(2,1)} %refs_3_.11, bf16[1024,8192]{1,0:T(8,128)(2,1)} %refs_3_.11, bf16[1024,8192]{1,0:T(8,128)(2,1)} %refs_3_.11, bf16[1024,8192]{1,0:T(8,128)(2,1)} %refs_3_.11, bf16[1024,256]{1,0:T(8,128)(2,1)} %copy-done.13, ...), custom_call_target="tpu_custom_call", output_to_operand_aliasing={{}: (9, {})} | custom-call | flops 2147483648 | bytes 12582912 | tf_op jit(solution)/shard_map/project/pallas_call | solution.py:68
  142.0 1.3 minimum_convert_fusion
  143.3 1.3 fusion.50
  144.7 3.4 %collective-permute-start.14 = (f32[1,256]{1,0:T(1,128)S(1)}, f32[1,256]{1,0:T(1,128)S(1)}, u32[]{:S(2)}, u32[]{:S(2)}) collective-permute-start(f32[1,256]{1,0:T(1,128)S(1)} %max.108), channel_id=1, source_target_pairs={{0,8},{8,16},{16,24},{24,0},{1,9},{9,17},{17,25},{25,1},{2,10},{10... | collective-permute-start | bytes 3080 | tf_op jit(solution)/shard_map/ppermute | solution.py:23
  148.1 2.4 %collective-permute-start.16 = (f32[1,256]{1,0:T(1,128)S(1)}, f32[1,256]{1,0:T(1,128)S(1)}, u32[]{:S(2)}, u32[]{:S(2)}) collective-permute-start(f32[1,256]{1,0:T(1,128)S(1)} %max.108), channel_id=1, source_target_pairs={{0,24},{8,0},{16,8},{24,16},{1,25},{9,1},{17,9},{25,17},{2,26},{10... | collective-permute-start | bytes 3080 | tf_op jit(solution)/shard_map/ppermute | solution.py:23
  150.6 0.8 broadcast_select_fusion
  151.3 1.3 collective-permute-done.15
  153.0 0.8 broadcast_select_fusion.1
  155.3 0.7 copy-done.22
  156.0 7.7 %score.1 = (bf16[4,256,2048]{2,1,0:T(8,128)(2,1)}, f32[4,256,1]{2,1,0:T(8,128)}, f32[4,256,1]{2,1,0:T(8,128)}) custom-call(s32[4]{0:T(128)} %pad_add_fusion.1.group, bf16[4,256,128]{2,1,0:T(8,128)(2,1)} %pad_maximum_fusion.1.query, f32[1,128]{1,0:T(1,128)} %broadcast_select_fusion.7.smooth, f32[4,8,2048]{2,1,0:T(8,128)} %fusion.1.count, ...), custom_call_target="tpu_custom_call" | custom-call | flops 536870912 | bytes 4194304 | tf_op jit(solution)/shard_map/score/pallas_call | solution.py:128
  163.7 1.2 reduce.1
  164.9 1.3 reduce.2
  166.2 3.4 %collective-permute-start.34 = (f32[2,256]{1,0:T(2,128)S(1)}, f32[2,256]{1,0:T(2,128)S(1)}, u32[]{:S(2)}, u32[]{:S(2)}) collective-permute-start(f32[2,256]{1,0:T(2,128)S(1)} %bitcast.136), channel_id=1, source_target_pairs={{0,24},{8,0},{16,8},{24,16},{1,25},{9,1},{17,9},{25,17},{2,26},{10... | collective-permute-start | bytes 6152 | tf_op jit(solution)/shard_map/ppermute | solution.py:23
  169.6 0.7 collective-permute-start.36
  170.4 0.7 copy-done.18
  171.1 4.8 %weigh.1 = bf16[4,256,128]{2,1,0:T(8,128)(2,1)} custom-call(bf16[4,256,2048]{2,1,0:T(8,128)(2,1)} %get-tuple-element.8.probs, bf16[1024,128]{1,0:T(8,128)(2,1)} %get-tuple-element.31.refs_0_, bf16[1024,128]{1,0:T(8,128)(2,1)} %copy-done.18), custom_call_target="tpu_custom_call" | custom-call | flops 536870912 | bytes 4194304 | tf_op jit(solution)/shard_map/weigh/pallas_call | solution.py:177
  175.8 0.9 slice_bitcast_fusion.2
  176.7 3.2 %collective-permute-start.38 = (bf16[256,128]{1,0:T(8,128)(2,1)S(1)}, bf16[256,128]{1,0:T(8,128)(2,1)S(1)}, u32[]{:S(2)}, u32[]{:S(2)}) collective-permute-start(bf16[256,128]{1,0:T(8,128)(2,1)S(1)} %get-tuple-element.34), channel_id=1, source_target_pairs={{0,24},{8,0},{16,8},{24,16},{1,25},{9,1},{17,9},{25,17},{2,26},{10... | collective-permute-start | bytes 196616 | tf_op jit(solution)/shard_map/ppermute | solution.py:23
  179.9 1.1 collective-permute-start.39
  181.2 1.2 collective-permute-done.38
  182.4 4.9 %collective-permute-done.39 = bf16[256,128]{1,0:T(8,128)(2,1)S(1)} collective-permute-done((bf16[256,128]{1,0:T(8,128)(2,1)S(1)}, bf16[256,128]{1,0:T(8,128)(2,1)S(1)}, u32[]{:S(2)}, u32[]{:S(2)}) %collective-permute-start.39) | collective-permute-done | bytes 65568 | tf_op jit(solution)/shard_map/ppermute | solution.py:23
  187.3 1.1 fusion.11
  188.6 2.0 %copy.67 = bf16[1024,2,256]{2,1,0:T(2,128)(2,1)} copy(bf16[1024,2,256]{2,0,1:T(8,128)(2,1)S(1)} %pad_maximum_fusion) | data formatting | bytes 2097152
  (141 shorter events, 10.1 us)
Async XLA Ops:
  0.6 36.3 %collective-permute-start.12 = (bf16[1024,256]{1,0:T(8,128)(2,1)}, bf16[1024,256]{1,0:T(8,128)(2,1)S(1)}, u32[]{:S(2)}, u32[]{:S(2)}) collective-permute-start(bf16[1024,256]{1,0:T(8,128)(2,1)} %refs_2_.8), channel_id=1, source_target_pairs={{0,1},{1,0},{2,3},{3,2},{4,5},{5,4},{6,7},{7,6},{8,9},{9,8},{10,11... | collective-permute-start | bytes 1572872 | tf_op jit(solution)/shard_map/ppermute | solution.py:23
  1.2 37.1 %collective-permute-start = (bf16[1024,256]{1,0:T(8,128)(2,1)}, bf16[1024,256]{1,0:T(8,128)(2,1)S(1)}, u32[]{:S(2)}, u32[]{:S(2)}) collective-permute-start(bf16[1024,256]{1,0:T(8,128)(2,1)} %refs_2_.8), channel_id=1, source_target_pairs={{0,8},{8,16},{16,24},{1,9},{9,17},{17,25},{2,10},{10,18},{18,26},{... | collective-permute-start | bytes 1572872 | tf_op jit(solution)/shard_map/ppermute | solution.py:247
  5.7 33.5 %collective-permute-start.4 = (bf16[1024,256]{1,0:T(8,128)(2,1)}, bf16[1024,256]{1,0:T(8,128)(2,1)S(1)}, u32[]{:S(2)}, u32[]{:S(2)}) collective-permute-start(bf16[1024,256]{1,0:T(8,128)(2,1)} %refs_2_.8), channel_id=1, source_target_pairs={{8,0},{16,8},{24,16},{9,1},{17,9},{25,17},{10,2},{18,10},{26,18},{... | collective-permute-start | bytes 1572872 | tf_op jit(solution)/shard_map/ppermute | solution.py:248
  8.6 16.9 %collective-permute-start.30 = (bf16[256,128]{1,0:T(8,128)(2,1)S(1)}, bf16[256,128]{1,0:T(8,128)(2,1)S(1)}, u32[]{:S(2)}, u32[]{:S(2)}) collective-permute-start(bf16[256,128]{1,0:T(8,128)(2,1)S(1)} %reshape.220), channel_id=1, source_target_pairs={{0,8},{8,16},{16,24},{24,0},{1,9},{9,17},{17,25},{25,1},{2,10},{10... | collective-permute-start | bytes 196616 | tf_op jit(solution)/shard_map/ppermute | solution.py:23
  11.3 29.4 %collective-permute-start.29 = (bf16[1024,256]{1,0:T(8,128)(2,1)}, bf16[1024,256]{1,0:T(8,128)(2,1)S(1)}, u32[]{:S(2)}, u32[]{:S(2)}) collective-permute-start(bf16[1024,256]{1,0:T(8,128)(2,1)} %refs_2_.12), channel_id=1, source_target_pairs={{0,1},{1,0},{2,3},{3,2},{4,5},{5,4},{6,7},{7,6},{8,9},{9,8},{10,11... | collective-permute-start | bytes 1572872 | tf_op jit(solution)/shard_map/ppermute | solution.py:23
  25.5 5.6 %copy-start.20 = (bf16[256,128]{1,0:T(8,128)(2,1)}, bf16[256,128]{1,0:T(8,128)(2,1)S(1)}, u32[]{:S(2)}) copy-start(bf16[256,128]{1,0:T(8,128)(2,1)S(1)} %collective-permute-done.30) | copy-start | bytes 196612
  25.5 5.6 %collective-permute-start.31 = (bf16[256,128]{1,0:T(8,128)(2,1)S(1)}, bf16[256,128]{1,0:T(8,128)(2,1)}, u32[]{:S(2)}, u32[]{:S(2)}) collective-permute-start(bf16[256,128]{1,0:T(8,128)(2,1)S(1)} %reshape.220), channel_id=1, source_target_pairs={{0,16},{8,24},{16,0},{24,8},{1,17},{9,25},{17,1},{25,9},{2,18},{10... | collective-permute-start | bytes 196616 | tf_op jit(solution)/shard_map/ppermute | solution.py:23
  31.1 4.3 %collective-permute-start.32 = (bf16[256,128]{1,0:T(8,128)(2,1)S(1)}, bf16[256,128]{1,0:T(8,128)(2,1)S(1)}, u32[]{:S(2)}, u32[]{:S(2)}) collective-permute-start(bf16[256,128]{1,0:T(8,128)(2,1)S(1)} %reshape.220), channel_id=1, source_target_pairs={{0,24},{8,0},{16,8},{24,16},{1,25},{9,1},{17,9},{25,17},{2,26},{10... | collective-permute-start | bytes 196616 | tf_op jit(solution)/shard_map/ppermute | solution.py:23
  35.4 9.7 %collective-permute-start.17 = (bf16[1024,256]{1,0:T(8,128)(2,1)}, bf16[1024,256]{1,0:T(8,128)(2,1)S(1)}, u32[]{:S(2)}, u32[]{:S(2)}) collective-permute-start(bf16[1024,256]{1,0:T(8,128)(2,1)} %refs_2_.12), channel_id=1, source_target_pairs={{0,8},{8,16},{16,24},{1,9},{9,17},{17,25},{2,10},{10,18},{18,26},{... | collective-permute-start | bytes 1572872 | tf_op jit(solution)/shard_map/ppermute | solution.py:247
  37.0 40.8 %copy-start.3 = (bf16[1024,256]{1,0:T(8,128)(2,1)}, bf16[1024,256]{1,0:T(8,128)(2,1)S(1)}, u32[]{:S(2)}) copy-start(bf16[1024,256]{1,0:T(8,128)(2,1)S(1)} %collective-permute-done.12.refs_3_) | copy-start | bytes 1572868
  37.0 12.1 %collective-permute-start.21 = (bf16[1024,256]{1,0:T(8,128)(2,1)}, bf16[1024,256]{1,0:T(8,128)(2,1)S(1)}, u32[]{:S(2)}, u32[]{:S(2)}) collective-permute-start(bf16[1024,256]{1,0:T(8,128)(2,1)} %refs_2_.12), channel_id=1, source_target_pairs={{8,0},{16,8},{24,16},{9,1},{17,9},{25,17},{10,2},{18,10},{26,18},{... | collective-permute-start | bytes 1572872 | tf_op jit(solution)/shard_map/ppermute | solution.py:248
  38.3 45.7 %copy-start.1 = (bf16[1024,256]{1,0:T(8,128)(2,1)}, bf16[1024,256]{1,0:T(8,128)(2,1)S(1)}, u32[]{:S(2)}) copy-start(bf16[1024,256]{1,0:T(8,128)(2,1)S(1)} %collective-permute-done.refs_4_) | copy-start | bytes 1572868
  38.3 10.8 %collective-permute-start.10 = (bf16[1024,256]{1,0:T(8,128)(2,1)S(1)}, bf16[1024,256]{1,0:T(8,128)(2,1)S(1)}, u32[]{:S(2)}, u32[]{:S(2)}) collective-permute-start(bf16[1024,256]{1,0:T(8,128)(2,1)S(1)} %collective-permute-done.refs_4_), channel_id=1, source_target_pairs={{0,1},{1,0},{2,3},{3,2},{4,5},{5,4},{6,7},{7,6},{8,9},{9,8},{10,11... | collective-permute-start | bytes 1572872 | tf_op jit(solution)/shard_map/ppermute | solution.py:23
  39.2 44.8 %copy-start.2 = (bf16[1024,256]{1,0:T(8,128)(2,1)}, bf16[1024,256]{1,0:T(8,128)(2,1)S(1)}, u32[]{:S(2)}) copy-start(bf16[1024,256]{1,0:T(8,128)(2,1)S(1)} %collective-permute-done.4.refs_6_) | copy-start | bytes 1572868
  39.2 12.6 %collective-permute-start.1 = (bf16[1024,256]{1,0:T(8,128)(2,1)S(1)}, bf16[1024,256]{1,0:T(8,128)(2,1)}, u32[]{:S(2)}, u32[]{:S(2)}) collective-permute-start(bf16[1024,256]{1,0:T(8,128)(2,1)S(1)} %collective-permute-done.refs_4_), channel_id=1, source_target_pairs={{8,16},{16,24},{9,17},{17,25},{10,18},{18,26},{11,19},{19,27},{12,... | collective-permute-start | bytes 1572872 | tf_op jit(solution)/shard_map/ppermute | solution.py:247
  40.7 43.3 %copy-start.4 = (bf16[1024,256]{1,0:T(8,128)(2,1)}, bf16[1024,256]{1,0:T(8,128)(2,1)S(1)}, u32[]{:S(2)}) copy-start(bf16[1024,256]{1,0:T(8,128)(2,1)S(1)} %collective-permute-done.29.refs_3_) | copy-start | bytes 1572868
  40.7 9.7 %collective-permute-start.11 = (bf16[1024,256]{1,0:T(8,128)(2,1)S(1)}, bf16[1024,256]{1,0:T(8,128)(2,1)S(1)}, u32[]{:S(2)}, u32[]{:S(2)}) collective-permute-start(bf16[1024,256]{1,0:T(8,128)(2,1)S(1)} %collective-permute-done.4.refs_6_), channel_id=1, source_target_pairs={{0,1},{1,0},{2,3},{3,2},{4,5},{5,4},{6,7},{7,6},{8,9},{9,8},{10,11... | collective-permute-start | bytes 1572872 | tf_op jit(solution)/shard_map/ppermute | solution.py:23
  45.1 39.0 %copy-start.5 = (bf16[1024,256]{1,0:T(8,128)(2,1)}, bf16[1024,256]{1,0:T(8,128)(2,1)S(1)}, u32[]{:S(2)}) copy-start(bf16[1024,256]{1,0:T(8,128)(2,1)S(1)} %collective-permute-done.17.refs_4_) | copy-start | bytes 1572868
  45.1 17.1 %collective-permute-start.5 = (bf16[1024,256]{1,0:T(8,128)(2,1)S(1)}, bf16[1024,256]{1,0:T(8,128)(2,1)}, u32[]{:S(2)}, u32[]{:S(2)}) collective-permute-start(bf16[1024,256]{1,0:T(8,128)(2,1)S(1)} %collective-permute-done.4.refs_6_), channel_id=1, source_target_pairs={{8,0},{16,8},{9,1},{17,9},{10,2},{18,10},{11,3},{19,11},{12,4},{20... | collective-permute-start | bytes 1572872 | tf_op jit(solution)/shard_map/ppermute | solution.py:248
  49.1 34.9 %copy-start.6 = (bf16[1024,256]{1,0:T(8,128)(2,1)}, bf16[1024,256]{1,0:T(8,128)(2,1)S(1)}, u32[]{:S(2)}) copy-start(bf16[1024,256]{1,0:T(8,128)(2,1)S(1)} %collective-permute-done.21.refs_6_) | copy-start | bytes 1572868
  49.1 13.1 %collective-permute-start.27 = (bf16[1024,256]{1,0:T(8,128)(2,1)S(1)}, bf16[1024,256]{1,0:T(8,128)(2,1)S(1)}, u32[]{:S(2)}, u32[]{:S(2)}) collective-permute-start(bf16[1024,256]{1,0:T(8,128)(2,1)S(1)} %collective-permute-done.17.refs_4_), channel_id=1, source_target_pairs={{0,1},{1,0},{2,3},{3,2},{4,5},{5,4},{6,7},{7,6},{8,9},{9,8},{10,11... | collective-permute-start | bytes 1572872 | tf_op jit(solution)/shard_map/ppermute | solution.py:23
  49.1 24.2 %copy-start.7 = (bf16[1024,256]{1,0:T(8,128)(2,1)}, bf16[1024,256]{1,0:T(8,128)(2,1)S(1)}, u32[]{:S(2)}) copy-start(bf16[1024,256]{1,0:T(8,128)(2,1)S(1)} %collective-permute-done.10.refs_5_) | copy-start | bytes 1572868
  49.1 14.5 %collective-permute-start.28 = (bf16[1024,256]{1,0:T(8,128)(2,1)S(1)}, bf16[1024,256]{1,0:T(8,128)(2,1)S(1)}, u32[]{:S(2)}, u32[]{:S(2)}) collective-permute-start(bf16[1024,256]{1,0:T(8,128)(2,1)S(1)} %collective-permute-done.21.refs_6_), channel_id=1, source_target_pairs={{0,1},{1,0},{2,3},{3,2},{4,5},{5,4},{6,7},{7,6},{8,9},{9,8},{10,11... | collective-permute-start | bytes 1572872 | tf_op jit(solution)/shard_map/ppermute | solution.py:23
  50.3 1.5 copy-start.10
  50.3 13.8 %collective-permute-start.18 = (bf16[1024,256]{1,0:T(8,128)(2,1)S(1)}, bf16[1024,256]{1,0:T(8,128)(2,1)}, u32[]{:S(2)}, u32[]{:S(2)}) collective-permute-start(bf16[1024,256]{1,0:T(8,128)(2,1)S(1)} %collective-permute-done.17.refs_4_), channel_id=1, source_target_pairs={{8,16},{16,24},{9,17},{17,25},{10,18},{18,26},{11,19},{19,27},{12,... | collective-permute-start | bytes 1572872 | tf_op jit(solution)/shard_map/ppermute | solution.py:247
  51.8 21.5 %collective-permute-start.22 = (bf16[1024,256]{1,0:T(8,128)(2,1)S(1)}, bf16[1024,256]{1,0:T(8,128)(2,1)S(1)}, u32[]{:S(2)}, u32[]{:S(2)}) collective-permute-start(bf16[1024,256]{1,0:T(8,128)(2,1)S(1)} %collective-permute-done.21.refs_6_), channel_id=1, source_target_pairs={{8,0},{16,8},{9,1},{17,9},{10,2},{18,10},{11,3},{19,11},{12,4},{20... | collective-permute-start | bytes 1572872 | tf_op jit(solution)/shard_map/ppermute | solution.py:248
  62.2 28.2 %collective-permute-start.8 = (bf16[1024,256]{1,0:T(8,128)(2,1)}, bf16[1024,256]{1,0:T(8,128)(2,1)}, u32[]{:S(2)}, u32[]{:S(2)}) collective-permute-start(bf16[1024,256]{1,0:T(8,128)(2,1)} %collective-permute-done.1.refs_4_), channel_id=1, source_target_pairs={{0,1},{1,0},{2,3},{3,2},{4,5},{5,4},{6,7},{7,6},{8,9},{9,8},{10,11... | collective-permute-start | bytes 1572872 | tf_op jit(solution)/shard_map/ppermute | solution.py:23
  62.2 11.1 %copy-start.11 = (bf16[1024,256]{1,0:T(8,128)(2,1)}, bf16[1024,256]{1,0:T(8,128)(2,1)S(1)}, u32[]{:S(2)}) copy-start(bf16[1024,256]{1,0:T(8,128)(2,1)S(1)} %collective-permute-done.27.refs_5_) | copy-start | bytes 1572868
  62.2 29.5 %collective-permute-start.2 = (bf16[1024,256]{1,0:T(8,128)(2,1)}, bf16[1024,256]{1,0:T(8,128)(2,1)}, u32[]{:S(2)}, u32[]{:S(2)}) collective-permute-start(bf16[1024,256]{1,0:T(8,128)(2,1)} %collective-permute-done.1.refs_4_), channel_id=1, source_target_pairs={{16,24},{17,25},{18,26},{19,27},{20,28},{21,29},{22,30},{23,31}} | collective-permute-start | bytes 1572872 | tf_op jit(solution)/shard_map/ppermute | solution.py:247
  63.7 9.7 %copy-start.12 = (bf16[1024,256]{1,0:T(8,128)(2,1)}, bf16[1024,256]{1,0:T(8,128)(2,1)S(1)}, u32[]{:S(2)}) copy-start(bf16[1024,256]{1,0:T(8,128)(2,1)S(1)} %collective-permute-done.28.refs_7_) | copy-start | bytes 1572868
  63.7 27.4 %collective-permute-start.9 = (bf16[1024,256]{1,0:T(8,128)(2,1)}, bf16[1024,256]{1,0:T(8,128)(2,1)}, u32[]{:S(2)}, u32[]{:S(2)}) collective-permute-start(bf16[1024,256]{1,0:T(8,128)(2,1)} %collective-permute-done.5.refs_6_), channel_id=1, source_target_pairs={{0,1},{1,0},{2,3},{3,2},{4,5},{5,4},{6,7},{7,6},{8,9},{9,8},{10,11... | collective-permute-start | bytes 1572872 | tf_op jit(solution)/shard_map/ppermute | solution.py:23
  64.2 36.1 %collective-permute-start.6 = (bf16[1024,256]{1,0:T(8,128)(2,1)}, bf16[1024,256]{1,0:T(8,128)(2,1)}, u32[]{:S(2)}, u32[]{:S(2)}) collective-permute-start(bf16[1024,256]{1,0:T(8,128)(2,1)} %collective-permute-done.5.refs_6_), channel_id=1, source_target_pairs={{8,0},{9,1},{10,2},{11,3},{12,4},{13,5},{14,6},{15,7}} | collective-permute-start | bytes 1572872 | tf_op jit(solution)/shard_map/ppermute | solution.py:248
  73.3 0.8 copy-start.8
  74.1 26.2 %collective-permute-start.25 = (bf16[1024,256]{1,0:T(8,128)(2,1)}, bf16[1024,256]{1,0:T(8,128)(2,1)}, u32[]{:S(2)}, u32[]{:S(2)}) collective-permute-start(bf16[1024,256]{1,0:T(8,128)(2,1)} %collective-permute-done.18.refs_4_), channel_id=1, source_target_pairs={{0,1},{1,0},{2,3},{3,2},{4,5},{5,4},{6,7},{7,6},{8,9},{9,8},{10,11... | collective-permute-start | bytes 1572872 | tf_op jit(solution)/shard_map/ppermute | solution.py:23
  84.0 7.0 %copy-start.9 = (bf16[1024,256]{1,0:T(8,128)(2,1)S(1)}, bf16[1024,256]{1,0:T(8,128)(2,1)}, u32[]{:S(2)}) copy-start(bf16[1024,256]{1,0:T(8,128)(2,1)} %copy-done.8) | copy-start | bytes 1572868
  90.4 25.1 %collective-permute-start.19 = (bf16[1024,256]{1,0:T(8,128)(2,1)}, bf16[1024,256]{1,0:T(8,128)(2,1)S(1)}, u32[]{:S(2)}, u32[]{:S(2)}) collective-permute-start(bf16[1024,256]{1,0:T(8,128)(2,1)} %collective-permute-done.18.refs_4_), channel_id=1, source_target_pairs={{16,24},{17,25},{18,26},{19,27},{20,28},{21,29},{22,30},{23,31}} | collective-permute-start | bytes 1572872 | tf_op jit(solution)/shard_map/ppermute | solution.py:247
  91.1 24.9 %collective-permute-start.26 = (bf16[1024,256]{1,0:T(8,128)(2,1)S(1)}, bf16[1024,256]{1,0:T(8,128)(2,1)S(1)}, u32[]{:S(2)}, u32[]{:S(2)}) collective-permute-start(bf16[1024,256]{1,0:T(8,128)(2,1)S(1)} %copy-done.9), channel_id=1, source_target_pairs={{0,1},{1,0},{2,3},{3,2},{4,5},{5,4},{6,7},{7,6},{8,9},{9,8},{10,11... | collective-permute-start | bytes 1572872 | tf_op jit(solution)/shard_map/ppermute | solution.py:23
  91.7 23.9 %collective-permute-start.23 = (bf16[1024,256]{1,0:T(8,128)(2,1)S(1)}, bf16[1024,256]{1,0:T(8,128)(2,1)S(1)}, u32[]{:S(2)}, u32[]{:S(2)}) collective-permute-start(bf16[1024,256]{1,0:T(8,128)(2,1)S(1)} %copy-done.9), channel_id=1, source_target_pairs={{8,0},{9,1},{10,2},{11,3},{12,4},{13,5},{14,6},{15,7}} | collective-permute-start | bytes 1572872 | tf_op jit(solution)/shard_map/ppermute | solution.py:248
  100.3 23.9 %collective-permute-start.3 = (bf16[1024,256]{1,0:T(8,128)(2,1)}, bf16[1024,256]{1,0:T(8,128)(2,1)S(1)}, u32[]{:S(2)}, u32[]{:S(2)}) collective-permute-start(bf16[1024,256]{1,0:T(8,128)(2,1)} %collective-permute-done.2.refs_4_), channel_id=1, source_target_pairs={{0,1},{1,0},{2,3},{3,2},{4,5},{5,4},{6,7},{7,6},{8,9},{9,8},{10,11... | collective-permute-start | bytes 1572872 | tf_op jit(solution)/shard_map/ppermute | solution.py:23
  100.4 23.8 %collective-permute-start.7 = (bf16[1024,256]{1,0:T(8,128)(2,1)}, bf16[1024,256]{1,0:T(8,128)(2,1)S(1)}, u32[]{:S(2)}, u32[]{:S(2)}) collective-permute-start(bf16[1024,256]{1,0:T(8,128)(2,1)} %collective-permute-done.6.refs_6_), channel_id=1, source_target_pairs={{0,1},{1,0},{2,3},{3,2},{4,5},{5,4},{6,7},{7,6},{8,9},{9,8},{10,11... | collective-permute-start | bytes 1572872 | tf_op jit(solution)/shard_map/ppermute | solution.py:23
  115.4 8.7 %copy-start.13 = (bf16[1024,256]{1,0:T(8,128)(2,1)}, bf16[1024,256]{1,0:T(8,128)(2,1)S(1)}, u32[]{:S(2)}) copy-start(bf16[1024,256]{1,0:T(8,128)(2,1)S(1)} %collective-permute-done.19.refs_4_) | copy-start | bytes 1572868
  115.4 19.1 %collective-permute-start.20 = (bf16[1024,256]{1,0:T(8,128)(2,1)S(1)}, bf16[1024,256]{1,0:T(8,128)(2,1)}, u32[]{:S(2)}, u32[]{:S(2)}) collective-permute-start(bf16[1024,256]{1,0:T(8,128)(2,1)S(1)} %collective-permute-done.19.refs_4_), channel_id=1, source_target_pairs={{0,1},{1,0},{2,3},{3,2},{4,5},{5,4},{6,7},{7,6},{8,9},{9,8},{10,11... | collective-permute-start | bytes 1572872 | tf_op jit(solution)/shard_map/ppermute | solution.py:23
  115.6 8.5 %copy-start.14 = (bf16[1024,256]{1,0:T(8,128)(2,1)}, bf16[1024,256]{1,0:T(8,128)(2,1)S(1)}, u32[]{:S(2)}) copy-start(bf16[1024,256]{1,0:T(8,128)(2,1)S(1)} %collective-permute-done.23.refs_6_) | copy-start | bytes 1572868
  115.6 19.0 %collective-permute-start.24 = (bf16[1024,256]{1,0:T(8,128)(2,1)S(1)}, bf16[1024,256]{1,0:T(8,128)(2,1)}, u32[]{:S(2)}, u32[]{:S(2)}) collective-permute-start(bf16[1024,256]{1,0:T(8,128)(2,1)S(1)} %collective-permute-done.23.refs_6_), channel_id=1, source_target_pairs={{0,1},{1,0},{2,3},{3,2},{4,5},{5,4},{6,7},{7,6},{8,9},{9,8},{10,11... | collective-permute-start | bytes 1572872 | tf_op jit(solution)/shard_map/ppermute | solution.py:23
  116.0 0.8 copy-start.15
  124.1 0.8 copy-start.16
  124.9 0.8 copy-start.17
  134.3 18.3 %copy-start = (f32[1024,256]{1,0:T(8,128)S(1)}, f32[1024,256]{1,0:T(8,128)}, u32[]{:S(2)}) copy-start(f32[1024,256]{1,0:T(8,128)} %project.11) | copy-start | bytes 3145732
  134.3 19.4 %copy-start.19 = (f32[4,8,8,128]{3,1,2,0:T(8,128)S(1)}, f32[4,8,8,128]{3,1,2,0:T(8,128)}, u32[]{:S(2)}) copy-start(f32[4,8,8,128]{3,1,2,0:T(8,128)} %get-tuple-element.28) | copy-start | bytes 393220
  134.3 10.3 %collective-permute-start.13 = (f32[1,256]{1,0:T(1,128)S(1)}, f32[1,256]{1,0:T(1,128)S(1)}, u32[]{:S(2)}, u32[]{:S(2)}) collective-permute-start(f32[1,256]{1,0:T(1,128)S(1)} %bitcast.128), channel_id=1, source_target_pairs={{0,1},{1,0},{2,3},{3,2},{4,5},{5,4},{6,7},{7,6},{8,9},{9,8},{10,11... | collective-permute-start | bytes 3080 | tf_op jit(solution)/shard_map/ppermute | solution.py:23
  144.7 6.6 %collective-permute-start.14 = (f32[1,256]{1,0:T(1,128)S(1)}, f32[1,256]{1,0:T(1,128)S(1)}, u32[]{:S(2)}, u32[]{:S(2)}) collective-permute-start(f32[1,256]{1,0:T(1,128)S(1)} %max.108), channel_id=1, source_target_pairs={{0,8},{8,16},{16,24},{24,0},{1,9},{9,17},{17,25},{25,1},{2,10},{10... | collective-permute-start | bytes 3080 | tf_op jit(solution)/shard_map/ppermute | solution.py:23
  148.1 4.5 %collective-permute-start.15 = (f32[1,256]{1,0:T(1,128)S(1)}, f32[1,256]{1,0:T(1,128)S(1)}, u32[]{:S(2)}, u32[]{:S(2)}) collective-permute-start(f32[1,256]{1,0:T(1,128)S(1)} %max.108), channel_id=1, source_target_pairs={{0,16},{8,24},{16,0},{24,8},{1,17},{9,25},{17,1},{25,9},{2,18},{10... | collective-permute-start | bytes 3080 | tf_op jit(solution)/shard_map/ppermute | solution.py:23
  148.1 4.5 %collective-permute-start.16 = (f32[1,256]{1,0:T(1,128)S(1)}, f32[1,256]{1,0:T(1,128)S(1)}, u32[]{:S(2)}, u32[]{:S(2)}) collective-permute-start(f32[1,256]{1,0:T(1,128)S(1)} %max.108), channel_id=1, source_target_pairs={{0,24},{8,0},{16,8},{24,16},{1,25},{9,1},{17,9},{25,17},{2,26},{10... | collective-permute-start | bytes 3080 | tf_op jit(solution)/shard_map/ppermute | solution.py:23
  151.3 19.0 %collective-permute-start.37 = (bf16[1024,128]{1,0:T(8,128)(2,1)S(1)}, bf16[1024,128]{1,0:T(8,128)(2,1)S(1)}, u32[]{:S(2)}, u32[]{:S(2)}) collective-permute-start(bf16[1024,128]{1,0:T(8,128)(2,1)S(1)} %get-tuple-element.30), channel_id=1, source_target_pairs={{0,1},{1,0},{2,3},{3,2},{4,5},{5,4},{6,7},{7,6},{8,9},{9,8},{10,11... | collective-permute-start | bytes 786440 | tf_op jit(solution)/shard_map/ppermute | solution.py:23
  152.6 38.8 %copy-start.21 = (f32[1,256]{1,0:T(1,128)}, f32[1,256]{1,0:T(1,128)S(1)}, u32[]{:S(2)}) copy-start(f32[1,256]{1,0:T(1,128)S(1)} %add_sqrt_fusion) | copy-start | bytes 3076
  153.7 1.6 collective-permute-start.33
  166.2 14.8 %collective-permute-start.34 = (f32[2,256]{1,0:T(2,128)S(1)}, f32[2,256]{1,0:T(2,128)S(1)}, u32[]{:S(2)}, u32[]{:S(2)}) collective-permute-start(f32[2,256]{1,0:T(2,128)S(1)} %bitcast.136), channel_id=1, source_target_pairs={{0,24},{8,0},{16,8},{24,16},{1,25},{9,1},{17,9},{25,17},{2,26},{10... | collective-permute-start | bytes 6152 | tf_op jit(solution)/shard_map/ppermute | solution.py:23
  169.6 11.4 %collective-permute-start.35 = (f32[2,256]{1,0:T(2,128)S(1)}, f32[2,256]{1,0:T(2,128)S(1)}, u32[]{:S(2)}, u32[]{:S(2)}) collective-permute-start(f32[2,256]{1,0:T(2,128)S(1)} %bitcast.134), channel_id=1, source_target_pairs={{0,16},{8,24},{16,0},{24,8},{1,17},{9,25},{17,1},{25,9},{2,18},{10... | collective-permute-start | bytes 6152 | tf_op jit(solution)/shard_map/ppermute | solution.py:23
  169.6 11.4 %collective-permute-start.36 = (f32[2,256]{1,0:T(2,128)S(1)}, f32[2,256]{1,0:T(2,128)S(1)}, u32[]{:S(2)}, u32[]{:S(2)}) collective-permute-start(f32[2,256]{1,0:T(2,128)S(1)} %bitcast.135), channel_id=1, source_target_pairs={{0,8},{8,16},{16,24},{24,0},{1,9},{9,17},{17,25},{25,1},{2,10},{10... | collective-permute-start | bytes 6152 | tf_op jit(solution)/shard_map/ppermute | solution.py:23
  170.4 0.7 copy-start.18
  176.7 5.7 %collective-permute-start.38 = (bf16[256,128]{1,0:T(8,128)(2,1)S(1)}, bf16[256,128]{1,0:T(8,128)(2,1)S(1)}, u32[]{:S(2)}, u32[]{:S(2)}) collective-permute-start(bf16[256,128]{1,0:T(8,128)(2,1)S(1)} %get-tuple-element.34), channel_id=1, source_target_pairs={{0,24},{8,0},{16,8},{24,16},{1,25},{9,1},{17,9},{25,17},{2,26},{10... | collective-permute-start | bytes 196616 | tf_op jit(solution)/shard_map/ppermute | solution.py:23
  179.9 7.4 %collective-permute-start.39 = (bf16[256,128]{1,0:T(8,128)(2,1)S(1)}, bf16[256,128]{1,0:T(8,128)(2,1)S(1)}, u32[]{:S(2)}, u32[]{:S(2)}) collective-permute-start(bf16[256,128]{1,0:T(8,128)(2,1)S(1)} %get-tuple-element.36), channel_id=1, source_target_pairs={{0,16},{8,24},{16,0},{24,8},{1,17},{9,25},{17,1},{25,9},{2,18},{10... | collective-permute-start | bytes 196616 | tf_op jit(solution)/shard_map/ppermute | solution.py:23
  181.0 6.3 %collective-permute-start.40 = (bf16[256,128]{1,0:T(8,128)(2,1)S(1)}, bf16[256,128]{1,0:T(8,128)(2,1)S(1)}, u32[]{:S(2)}, u32[]{:S(2)}) collective-permute-start(bf16[256,128]{1,0:T(8,128)(2,1)S(1)} %get-tuple-element.35), channel_id=1, source_target_pairs={{0,8},{8,16},{16,24},{24,0},{1,9},{9,17},{17,25},{25,1},{2,10},{10... | collective-permute-start | bytes 196616 | tf_op jit(solution)/shard_map/ppermute | solution.py:23
  188.4 2.2 %collective-permute-start.41 = (bf16[4,8,1024]{2,1,0:T(8,128)(2,1)S(1)}, bf16[4,8,1024]{2,1,0:T(8,128)(2,1)S(1)}, u32[]{:S(2)}, u32[]{:S(2)}) collective-permute-start(bf16[4,8,1024]{2,1,0:T(8,128)(2,1)S(1)} %reshape.223), channel_id=1, source_target_pairs={{0,1},{1,0},{2,3},{3,2},{4,5},{5,4},{6,7},{7,6},{8,9},{9,8},{10,11... | collective-permute-start | bytes 196616 | tf_op jit(solution)/shard_map/ppermute | solution.py:23
  (1 other events, 0.7 us)

commit v2 on v1

--- a/solution.py
+++ b/solution.py
@@ -6,6 +6,7 @@
 from jax.experimental import pallas as pl
 from jax.experimental.pallas import tpu as pltpu
 from jax.sharding import PartitionSpec as P
+
 
 KVH = 8
 HD = 128
@@ -40,50 +41,50 @@
     return [x[0]] + [shifted(x[k], "seq", -k) for k in range(1, n)]
 
 
-def project_kernel(count, has_total, info, *refs):
-    lefts, weights = refs[:count], refs[count : 2 * count]
-    out = refs[-1]
-    out[...] = refs[2 * count][...] if has_total else jnp.zeros_like(out)
-    for j in range(count):
+def project_kernel(count, has_total, info, left, *refs):
+    weights, total = refs[:count], refs[count] if has_total else None
+    out, held, arrived = refs[-3:]
+    depth = held.shape[1]
+    copies = [pltpu.make_async_copy(weights[j], held.at[j], arrived.at[j]) for j in range(count)]
+    for copy in copies:
+        copy.start()
+    out[...] = total[...] if has_total else jnp.zeros_like(out)
+    for j, copy in enumerate(copies):
+        copy.wait()
 
         @pl.when(info[count + j] == 1)
         def _(j=j):
-            out[...] += jnp.dot(
-                lefts[j][...], weights[j][...], preferred_element_type=jnp.float32
-            )
+            block = pl.ds(pl.multiple_of(info[j] * depth, depth), depth)
+            out[...] += jnp.dot(left[:, block], held[j], preferred_element_type=jnp.float32)
 
 
 def project(hidden, total, weights, where, live):
     tokens = hidden.shape[0]
     depth, columns = weights[0].shape
     count = len(weights)
-    tile = min(tokens, 256)
     info = jnp.stack([jnp.asarray(v, jnp.int32) for v in list(where) + list(live)])
-
-    def left_spec(j):
-        return pl.BlockSpec((tile, depth), lambda i, info: (i * info[count + j], info[j]))
-
-    total_spec = pl.BlockSpec((tile, columns), lambda i, info: (i, 0))
     has_total = total is not None
+    whole = pl.BlockSpec(memory_space=pltpu.VMEM)
     return pl.pallas_call(
         functools.partial(project_kernel, count, has_total),
         out_shape=jax.ShapeDtypeStruct((tokens, columns), jnp.float32),
-        grid_spec=pltpu.PrefetchScalarGridSpec(
-            num_scalar_prefetch=1,
-            grid=(tokens // tile,),
-            in_specs=[left_spec(j) for j in range(count)]
-            + [pl.BlockSpec((depth, columns), lambda i, info: (0, 0))] * count
-            + [total_spec] * has_total,
-            out_specs=total_spec,
-        ),
+        in_specs=[pl.BlockSpec(memory_space=pltpu.SMEM), whole]
+        + [pl.BlockSpec(memory_space=pl.ANY)] * count
+        + [whole] * has_total,
+        out_specs=whole,
+        scratch_shapes=[
+            pltpu.VMEM((count, depth, columns), weights[0].dtype),
+            pltpu.SemaphoreType.DMA((count,)),
+        ],
+        compiler_params=pltpu.CompilerParams(vmem_limit_bytes=12 * 2**20),
         cost_estimate=pl.CostEstimate(
             flops=2 * tokens * depth * columns * count,
             bytes_accessed=2 * count * depth * (tokens + columns) + 8 * tokens * columns,
             transcendentals=0,
         ),
-        input_output_aliases={1 + 2 * count: 0} if has_total else {},
+        input_output_aliases={2 + count: 0} if has_total else {},
         name="project",
-    )(info, *([hidden] * count), *weights, *([total] if has_total else []))
+    )(info, hidden, *weights, *([total] if has_total else []))
 
 
 def score_kernel(parts, steps, scale, group, query, smooth, count, *refs):
@@ -225,36 +226,64 @@
     return out
 
 
-def line_project(hidden, key_weight, value_weight):
+def line_project(hidden, key_weight, value_weight, raw_query):
     groups, owners = lax.axis_size("seq"), lax.axis_size("rep")
     my_group, my_owner = lax.axis_index("seq"), lax.axis_index("rep")
 
-    def block_of(group):
-        group = jnp.clip(group, 0, groups - 1)
-        return [group * owners + (my_owner - k) % owners for k in range(owners)]
-
-    weights = (key_weight, value_weight)
-    moving = [(weight, weight) for weight in weights]
-    totals = [
-        project(hidden, None, from_all(w, "rep"), block_of(my_group), [jnp.int32(1)] * owners)
-        for w in weights
-    ]
+    def block_of(group, k):
+        return jnp.clip(group, 0, groups - 1) * owners + (my_owner - k) % owners
+
+    yes = jnp.int32(1)
+    names = ("k", "v")
+    moving, arrived, totals = {}, {}, {}
+
+    def send(name, hop):
+        left, right = moving[name]
+        left = lax.ppermute(left, "seq", [(i, i + 1) for i in range(hop - 1, groups - 1)])
+        right = lax.ppermute(right, "seq", [(i, i - 1) for i in range(1, groups - hop + 1)])
+        arrived[name] = (left, right)
+
+    def absorb(name, hop):
+        left, right = moving[name]
+        here = [(my_group - hop, (my_group >= hop).astype(jnp.int32), left)]
+        here.append((my_group + hop, (my_group + hop < groups).astype(jnp.int32), right))
+        if hop == 0:
+            here = [(my_group, yes, left)]
+        elif 2 * hop >= groups:
+            is_left = my_group >= hop
+            here = [
+                (
+                    jnp.where(is_left, my_group - hop, my_group + hop),
+                    here[0][1] + here[1][1],
+                    jnp.where(is_left, left, right),
+                )
+            ]
+        passed = [[shifted(block, "rep", k) for _, _, block in here] for k in range(1, owners)]
+        for k, blocks in enumerate([[block for _, _, block in here]] + passed):
+            totals[name] = project(
+                hidden,
+                totals.get(name),
+                blocks,
+                [block_of(group, k) for group, _, _ in here],
+                [live for _, live, _ in here],
+            )
+
+    moving["k"], moving["v"] = (key_weight,) * 2, (value_weight,) * 2
+    for name in names:
+        send(name, 1)
+        absorb(name, 0)
+    queries = None
     for hop in range(1, groups):
-        here_left = (my_group - hop >= 0).astype(jnp.int32)
-        here_right = (my_group + hop < groups).astype(jnp.int32)
-        for j in range(len(weights)):
-            left, right = moving[j]
-            left = lax.ppermute(left, "seq", [(i, i + 1) for i in range(hop - 1, groups - 1)])
-            right = lax.ppermute(right, "seq", [(i, i - 1) for i in range(1, groups - hop + 1)])
-            moving[j] = (left, right)
-            totals[j] = project(
-                hidden,
-                totals[j],
-                from_all(left, "rep") + from_all(right, "rep"),
-                block_of(my_group - hop) + block_of(my_group + hop),
-                [here_left] * owners + [here_right] * owners,
-            )
-    return totals
+        for name in names:
+            other = names[1 - names.index(name)]
+            moving[name], totals[other] = lax.optimization_barrier((arrived[name], totals[other]))
+            if hop < groups - 1:
+                send(name, hop + 1)
+            if name == "k" and hop == max(1, groups - 2):
+                raw_query, moving[name] = lax.optimization_barrier((raw_query, moving[name]))
+                queries = jnp.stack(from_all(raw_query, "seq"))
+            absorb(name, hop)
+    return totals["k"], totals["v"], queries
 
 
 def on_device(
@@ -272,22 +301,18 @@
     raw_query = my_part(decode_query, owners, my_owner, 2).reshape(-1, HD)
 
     owner_at = [(my_owner - k) % owners for k in range(owners)]
-    yes = jnp.int32(1)
-
     if groups > SHORT:
         raw_keys, raw_values = (
-            project(
+            jnp.dot(
                 hidden,
-                None,
-                [lax.all_gather(weight, ("seq", "rep"), axis=0, tiled=True)],
-                [0],
-                [yes],
+                lax.all_gather(weight, ("seq", "rep"), axis=0, tiled=True),
+                preferred_element_type=jnp.float32,
             )
             for weight in (key_weight, value_weight)
         )
+        queries = jnp.stack(from_all(raw_query, "seq"))
     else:
-        raw_keys, raw_values = line_project(hidden, key_weight, value_weight)
-    queries = jnp.stack(from_all(raw_query, "seq"))
+        raw_keys, raw_values, queries = line_project(hidden, key_weight, value_weight, raw_query)
 
     local_max = jnp.max(jnp.abs(raw_keys), axis=0, keepdims=True)
     local_max = functools.reduce(jnp.maximum, from_all(local_max, "rep"))
@@ -378,6 +403,7 @@
         P(),
         P(),
     )
+
     return jax.shard_map(
         on_device,
         mesh=mesh,

time: 193 us -> 203 us (1.052)
  Pallas kernels: 68.8 us -> 38.6 us
  local copies, waits for them, and re-layouts: 9.92 us -> 39 us
  waiting for transfers between devices: 49.8 us -> 66.5 us
  other arithmetic: 19.6 us -> 13.6 us
    unnamed x51 -> x43, local copies, waits for them, and re-layouts: 6.7 us -> 37.8 us
    pallas_call x8 -> x16, Pallas kernels: 56.4 us -> 26 us  [project(): pl.pallas_call(functools.partial(project_kernel, count, has_total), out_s...]
    ppermute x12, waiting for transfers between devices: 21.7 us -> 34.5 us  [the longest x6 34.5 us: send(): lax.ppermute(right, 'seq', [(i, i - 1) for i in range(1, groups - hop + 1)])]
    ppermute x12, starting transfers between devices: 18.9 us -> 22.7 us  [the longest x6 15 us: send(): lax.ppermute(left, 'seq', [(i, i + 1) for i in range(hop - 1, groups - 1)])]
    ppermute x30 -> x26, waiting for transfers between devices: 28.2 us -> 32 us  [shifted(): return lax.ppermute(x, axis, [(i, (i + k) % n) for i in range(n)])]
    ppermute x30 -> x26, starting transfers between devices: 21.1 us -> 17.5 us  [shifted(): return lax.ppermute(x, axis, [(i, (i + k) % n) for i in range(n)])]
  transfers between devices with their start and end apart: 42 -> 38, of which waited for: 10 -> 15; matrix products, arithmetic and copies ran while one was open for 13% -> 7% of each run, Pallas kernels for 36% -> 16%
where the time goes in v2:
time: 203 us; the launch traced here: 201 us
  waiting for transfers between devices  66.5 us (33%)
  starting transfers between devices  40.2 us (20%)
  local copies, waits for them, and re-layouts  39 us (19%)
  Pallas kernels  38.6 us (19%)
  other arithmetic  13.6 us (7%)
    unnamed x43, local copies, waits for them, and re-layouts  37.8 us
    ppermute x6, waiting for transfers between devices, send(): lax.ppermute(right, 'seq', [(i, i - 1) for i in range(1, groups - hop + 1)])  34.5 us
    ppermute x26, waiting for transfers between devices, shifted(): return lax.ppermute(x, axis, [(i, (i + k) % n) for i in range(n)])  32 us
    pallas_call x16, Pallas kernels, project(): pl.pallas_call(functools.partial(project_kernel, count, has_total), out_s...  26 us
    ppermute x26, starting transfers between devices, shifted(): return lax.ppermute(x, axis, [(i, (i + k) % n) for i in range(n)])  17.5 us
    ppermute x6, starting transfers between devices, send(): lax.ppermute(left, 'seq', [(i, i + 1) for i in range(hop - 1, groups - 1)])  15 us
    pallas_call x1, Pallas kernels, score(): pl.pallas_call(functools.partial(score_kernel, parts, steps, scale), out_...  7.82 us
    ppermute x6, starting transfers between devices, send(): lax.ppermute(right, 'seq', [(i, i - 1) for i in range(1, groups - hop + 1)])  7.72 us
  transfers between devices with their start and end apart: 38, of which 15 were waited for; matrix products, arithmetic and copies ran while one was open for 7% of the time, Pallas kernels for 16%

profile of v2, /device:TPU:0, one launch (start us, length us, event | category | flops | bytes accessed | tf_op | source)
XLA Modules:
  0.0 201.3 jit_solution(10572682802738860730)
XLA Ops:
  0.6 1.3 collective-permute-start.3
  1.9 6.4 %collective-permute-start.2 = (bf16[1024,256]{1,0:T(8,128)(2,1)}, bf16[1024,256]{1,0:T(8,128)(2,1)}, u32[]{:S(2)}, u32[]{:S(2)}) collective-permute-start(bf16[1024,256]{1,0:T(8,128)(2,1)} %refs_0_.3), channel_id=1, source_target_pairs={{0,8},{8,16},{16,24},{1,9},{9,17},{17,25},{2,10},{10,18},{18,26},{... | collective-permute-start | bytes 1572872 | tf_op jit(solution)/shard_map/ppermute | solution.py:242
  8.3 1.3 collective-permute-start.1
  11.0 0.9 bitcast_convert_fusion
  12.0 5.8 %copy-done = bf16[1024,8192]{1,0:T(8,128)(2,1)S(1)} copy-done((bf16[1024,8192]{1,0:T(8,128)(2,1)S(1)}, bf16[1024,8192]{1,0:T(8,128)(2,1)}, u32[]{:S(2)}) %copy-start) | copy-done | bytes 16777240
  17.8 2.3 %project.16.refs_1_ = f32[1024,256]{1,0:T(8,128)S(1)} custom-call(s32[2]{0:T(128)S(1)} %pad_add_fusion.info, bf16[1024,8192]{1,0:T(8,128)(2,1)S(1)} %copy-done, bf16[1024,256]{1,0:T(8,128)(2,1)} %refs_0_.2), custom_call_target="tpu_custom_call" | custom-call | flops 536870912 | bytes 4718592 | tf_op jit(solution)/shard_map/project/pallas_call | solution.py:68
  20.9 4.3 %collective-permute-start = (bf16[1024,256]{1,0:T(8,128)(2,1)}, bf16[1024,256]{1,0:T(8,128)(2,1)S(1)}, u32[]{:S(2)}, u32[]{:S(2)}) collective-permute-start(bf16[1024,256]{1,0:T(8,128)(2,1)} %refs_0_.2), channel_id=1, source_target_pairs={{0,8},{8,16},{16,24},{1,9},{9,17},{17,25},{2,10},{10,18},{18,26},{... | collective-permute-start | bytes 1572872 | tf_op jit(solution)/shard_map/ppermute | solution.py:242
  25.3 5.8 %copy-done.1 = bf16[1024,8192]{1,0:T(8,128)(2,1)S(1)} copy-done((bf16[1024,8192]{1,0:T(8,128)(2,1)S(1)}, bf16[1024,8192]{1,0:T(8,128)(2,1)}, u32[]{:S(2)}) %copy-start.1) | copy-done | bytes 16777240
  31.0 1.4 project.17.refs_2_
  33.1 3.7 %copy-done.2 = bf16[1024,8192]{1,0:T(8,128)(2,1)S(1)} copy-done((bf16[1024,8192]{1,0:T(8,128)(2,1)S(1)}, bf16[1024,8192]{1,0:T(8,128)(2,1)}, u32[]{:S(2)}) %copy-start.2) | copy-done | bytes 16777240
  36.8 1.0 copy-done.6
  37.8 1.4 project.18.refs_1_
  39.3 2.3 %project.19.refs_2_ = f32[1024,256]{1,0:T(8,128)S(1)} custom-call(s32[2]{0:T(128)S(1)} %pad_add_fusion.1.info, bf16[1024,8192]{1,0:T(8,128)(2,1)S(1)} %copy-done.2, bf16[1024,256]{1,0:T(8,128)(2,1)} %collective-permute-done.7.refs_0_, f32[1024,256]{1,0:T(8,128)S(1)} %project.18.refs_1_), custom_call_target="tpu_custom_call", output_to_operand_aliasing={{}: (3, {})} | custom-call | flops 536870912 | bytes 4718592 | tf_op jit(solution)/shard_map/project/pallas_call | solution.py:68
  41.6 2.3 %project.20.refs_2_ = f32[1024,256]{1,0:T(8,128)S(1)} custom-call(s32[4]{0:T(128)S(1)} %add_add_fusion.1.info, bf16[1024,8192]{1,0:T(8,128)(2,1)S(1)} %copy-done.2, bf16[1024,256]{1,0:T(8,128)(2,1)} %collective-permute-done.2.refs_0_, bf16[1024,256]{1,0:T(8,128)(2,1)S(1)} %collective-permute-done.3.refs_1_, ...), custom_call_target="tpu_custom_call", output_to_operand_aliasing={{}: (4, {})} | custom-call | flops 1073741824 | bytes 7340032 | tf_op jit(solution)/shard_map/project/pallas_call | solution.py:68
  44.0 1.5 project.21.refs_1_
  46.1 1.5 collective-permute-start.10
  47.5 1.3 collective-permute-start.11
  48.9 1.5 project.22.refs_2_
  50.5 1.5 project.23.refs_1_
  52.0 14.9 %collective-permute-done.11 = bf16[1024,256]{1,0:T(8,128)(2,1)S(1)} collective-permute-done((bf16[1024,256]{1,0:T(8,128)(2,1)S(1)}, bf16[1024,256]{1,0:T(8,128)(2,1)S(1)}, u32[]{:S(2)}, u32[]{:S(2)}) %collective-permute-start.11) | collective-permute-done | bytes 524320 | tf_op jit(solution)/shard_map/ppermute | solution.py:243
  66.9 0.8 copy-done.8
  67.9 1.5 collective-permute-start.8
  69.4 1.3 collective-permute-start.9
  70.9 1.5 project.24.refs_1_
  72.3 1.5 project.25.refs_1_
  73.8 13.4 %collective-permute-done.9 = bf16[1024,256]{1,0:T(8,128)(2,1)} collective-permute-done((bf16[1024,256]{1,0:T(8,128)(2,1)S(1)}, bf16[1024,256]{1,0:T(8,128)(2,1)}, u32[]{:S(2)}, u32[]{:S(2)}) %collective-permute-start.9) | collective-permute-done | bytes 524320 | tf_op jit(solution)/shard_map/ppermute | solution.py:243
  87.2 1.1 broadcast_select_fusion.2.refs_0_
  88.4 0.9 fusion.1.count
  90.0 1.3 collective-permute-start.18
  91.4 5.8 %copy-done.3 = bf16[1024,8192]{1,0:T(8,128)(2,1)S(1)} copy-done((bf16[1024,8192]{1,0:T(8,128)(2,1)S(1)}, bf16[1024,8192]{1,0:T(8,128)(2,1)}, u32[]{:S(2)}) %copy-start.3) | copy-done | bytes 16777240
  97.1 1.6 project.26.refs_1_
  98.7 1.4 project.27.refs_1_
  100.2 6.2 %collective-permute-done.18 = bf16[1024,256]{1,0:T(8,128)(2,1)S(1)} collective-permute-done((bf16[1024,256]{1,0:T(8,128)(2,1)}, bf16[1024,256]{1,0:T(8,128)(2,1)S(1)}, u32[]{:S(2)}, u32[]{:S(2)}) %collective-permute-start.18) | collective-permute-done | bytes 524320 | tf_op jit(solution)/shard_map/ppermute | solution.py:243
  107.4 1.3 collective-permute-start.16
  108.8 4.1 %collective-permute-start.27 = (bf16[256,128]{1,0:T(8,128)(2,1)S(1)}, bf16[256,128]{1,0:T(8,128)(2,1)S(1)}, u32[]{:S(2)}, u32[]{:S(2)}) collective-permute-start(bf16[256,128]{1,0:T(8,128)(2,1)S(1)} %reshape.218), channel_id=1, source_target_pairs={{0,16},{8,24},{16,0},{24,8},{1,17},{9,25},{17,1},{25,9},{2,18},{10... | collective-permute-start | bytes 196616 | tf_op jit(solution)/shard_map/ppermute | solution.py:24
  113.0 13.5 %collective-permute-done.28 = bf16[256,128]{1,0:T(8,128)(2,1)S(1)} collective-permute-done((bf16[256,128]{1,0:T(8,128)(2,1)S(1)}, bf16[256,128]{1,0:T(8,128)(2,1)S(1)}, u32[]{:S(2)}, u32[]{:S(2)}) %collective-permute-start.28) | collective-permute-done | bytes 65568 | tf_op jit(solution)/shard_map/ppermute | solution.py:24
  127.1 5.5 %collective-permute-done.26 = bf16[256,128]{1,0:T(8,128)(2,1)S(1)} collective-permute-done((bf16[256,128]{1,0:T(8,128)(2,1)S(1)}, bf16[256,128]{1,0:T(8,128)(2,1)S(1)}, u32[]{:S(2)}, u32[]{:S(2)}) %collective-permute-start.26) | collective-permute-done | bytes 65568 | tf_op jit(solution)/shard_map/ppermute | solution.py:24
  133.3 5.8 %copy-done.4 = bf16[1024,8192]{1,0:T(8,128)(2,1)S(1)} copy-done((bf16[1024,8192]{1,0:T(8,128)(2,1)S(1)}, bf16[1024,8192]{1,0:T(8,128)(2,1)}, u32[]{:S(2)}) %copy-start.4) | copy-done | bytes 16777240
  139.1 1.4 project.28.refs_1_
  140.5 1.4 project.29
  143.3 2.0 %collective-permute-start.22 = (f32[1,256]{1,0:T(1,128)S(1)}, f32[1,256]{1,0:T(1,128)S(1)}, u32[]{:S(2)}, u32[]{:S(2)}) collective-permute-start(f32[1,256]{1,0:T(1,128)S(1)} %max.108), channel_id=1, source_target_pairs={{0,8},{8,16},{16,24},{24,0},{1,9},{9,17},{17,25},{25,1},{2,10},{10... | collective-permute-start | bytes 3080 | tf_op jit(solution)/shard_map/ppermute | solution.py:24
  145.4 1.5 project.30.refs_1_
  146.9 0.9 collective-permute-done.23
  147.8 1.5 collective-permute-done.22
  150.0 0.8 broadcast_select_fusion.5
  151.5 0.9 fusion.49
  153.1 7.8 %score.1 = (bf16[4,256,2048]{2,1,0:T(8,128)(2,1)}, f32[4,256,1]{2,1,0:T(8,128)}, f32[4,256,1]{2,1,0:T(8,128)}) custom-call(s32[4]{0:T(128)} %pad_add_fusion.6.group, bf16[4,256,128]{2,1,0:T(8,128)(2,1)} %pad_maximum_fusion.1.query, f32[1,128]{1,0:T(1,128)} %broadcast_select_fusion.11.smooth, f32[4,8,2048]{2,1,0:T(8,128)} %fusion.1.count, ...), custom_call_target="tpu_custom_call" | custom-call | flops 536870912 | bytes 4194304 | tf_op jit(solution)/shard_map/score/pallas_call | solution.py:129
  161.0 1.2 reduce.1
  162.2 1.3 reduce.2
  164.1 2.0 %collective-permute-start.32 = (f32[2,256]{1,0:T(2,128)S(1)}, f32[2,256]{1,0:T(2,128)S(1)}, u32[]{:S(2)}, u32[]{:S(2)}) collective-permute-start(f32[2,256]{1,0:T(2,128)S(1)} %bitcast.134), channel_id=1, source_target_pairs={{0,8},{8,16},{16,24},{24,0},{1,9},{9,17},{17,25},{25,1},{2,10},{10... | collective-permute-start | bytes 6152 | tf_op jit(solution)/shard_map/ppermute | solution.py:24
  166.2 1.8 collective-permute-start.30
  168.3 1.2 collective-permute-done.32
  169.9 5.8 %copy-done.5 = bf16[1024,8192]{1,0:T(8,128)(2,1)S(1)} copy-done((bf16[1024,8192]{1,0:T(8,128)(2,1)S(1)}, bf16[1024,8192]{1,0:T(8,128)(2,1)}, u32[]{:S(2)}) %copy-start.5) | copy-done | bytes 16777240
  175.6 1.4 project.31
  177.2 0.8 broadcast_select_fusion.4
  178.0 1.5 collective-permute-done.33.refs_1_
  180.2 4.8 %weigh.1 = bf16[4,256,128]{2,1,0:T(8,128)(2,1)} custom-call(bf16[4,256,2048]{2,1,0:T(8,128)(2,1)} %get-tuple-element.50.probs, bf16[1024,128]{1,0:T(8,128)(2,1)} %get-tuple-element.73.refs_0_, bf16[1024,128]{1,0:T(8,128)(2,1)} %copy-done.9), custom_call_target="tpu_custom_call" | custom-call | flops 536870912 | bytes 4194304 | tf_op jit(solution)/shard_map/weigh/pallas_call | solution.py:178
  184.9 0.9 slice_bitcast_fusion.2
  185.9 3.6 %collective-permute-start.34 = (bf16[256,128]{1,0:T(8,128)(2,1)S(1)}, bf16[256,128]{1,0:T(8,128)(2,1)S(1)}, u32[]{:S(2)}, u32[]{:S(2)}) collective-permute-start(bf16[256,128]{1,0:T(8,128)(2,1)S(1)} %get-tuple-element.76), channel_id=1, source_target_pairs={{0,24},{8,0},{16,8},{24,16},{1,25},{9,1},{17,9},{25,17},{2,26},{10... | collective-permute-start | bytes 196616 | tf_op jit(solution)/shard_map/ppermute | solution.py:24
  190.2 1.8 collective-permute-done.34
  192.0 4.0 %collective-permute-done.36 = bf16[256,128]{1,0:T(8,128)(2,1)S(1)} collective-permute-done((bf16[256,128]{1,0:T(8,128)(2,1)S(1)}, bf16[256,128]{1,0:T(8,128)(2,1)S(1)}, u32[]{:S(2)}, u32[]{:S(2)}) %collective-permute-start.36) | collective-permute-done | bytes 65568 | tf_op jit(solution)/shard_map/ppermute | solution.py:24
  196.0 1.3 collective-permute-done.35
  197.3 1.1 fusion.11
  198.6 2.0 %copy.75 = bf16[1024,2,256]{2,1,0:T(2,128)(2,1)} copy(bf16[1024,2,256]{2,0,1:T(8,128)(2,1)S(1)} %pad_maximum_fusion) | data formatting | bytes 2097152
  (140 shorter events, 14.4 us)
Async XLA Ops:
  0.6 19.6 %copy-start.12 = (s32[32,32]{1,0:T(8,128)S(1)}, s32[32,32]{1,0:T(8,128)}, u32[]{:S(2)}) copy-start(s32[32,32]{1,0:T(8,128)} %param.14) | copy-start | bytes 12292
  0.6 31.8 %collective-permute-start.3 = (bf16[1024,256]{1,0:T(8,128)(2,1)}, bf16[1024,256]{1,0:T(8,128)(2,1)S(1)}, u32[]{:S(2)}, u32[]{:S(2)}) collective-permute-start(bf16[1024,256]{1,0:T(8,128)(2,1)} %refs_0_.3), channel_id=1, source_target_pairs={{8,0},{16,8},{24,16},{9,1},{17,9},{25,17},{10,2},{18,10},{26,18},{... | collective-permute-start | bytes 1572872 | tf_op jit(solution)/shard_map/ppermute | solution.py:243
  1.9 30.5 %collective-permute-start.2 = (bf16[1024,256]{1,0:T(8,128)(2,1)}, bf16[1024,256]{1,0:T(8,128)(2,1)}, u32[]{:S(2)}, u32[]{:S(2)}) collective-permute-start(bf16[1024,256]{1,0:T(8,128)(2,1)} %refs_0_.3), channel_id=1, source_target_pairs={{0,8},{8,16},{16,24},{1,9},{9,17},{17,25},{2,10},{10,18},{18,26},{... | collective-permute-start | bytes 1572872 | tf_op jit(solution)/shard_map/ppermute | solution.py:242
  8.3 30.9 %collective-permute-start.7 = (bf16[1024,256]{1,0:T(8,128)(2,1)}, bf16[1024,256]{1,0:T(8,128)(2,1)}, u32[]{:S(2)}, u32[]{:S(2)}) collective-permute-start(bf16[1024,256]{1,0:T(8,128)(2,1)} %refs_0_.3), channel_id=1, source_target_pairs={{0,1},{1,0},{2,3},{3,2},{4,5},{5,4},{6,7},{7,6},{8,9},{9,8},{10,11... | collective-permute-start | bytes 1572872 | tf_op jit(solution)/shard_map/ppermute | solution.py:24
  8.3 37.1 %collective-permute-start.1 = (bf16[1024,256]{1,0:T(8,128)(2,1)}, bf16[1024,256]{1,0:T(8,128)(2,1)S(1)}, u32[]{:S(2)}, u32[]{:S(2)}) collective-permute-start(bf16[1024,256]{1,0:T(8,128)(2,1)} %refs_0_.2), channel_id=1, source_target_pairs={{8,0},{16,8},{24,16},{9,1},{17,9},{25,17},{10,2},{18,10},{26,18},{... | collective-permute-start | bytes 1572872 | tf_op jit(solution)/shard_map/ppermute | solution.py:243
  9.6 11.3 %collective-permute-start.4 = (bf16[1024,256]{1,0:T(8,128)(2,1)}, bf16[1024,256]{1,0:T(8,128)(2,1)S(1)}, u32[]{:S(2)}, u32[]{:S(2)}) collective-permute-start(bf16[1024,256]{1,0:T(8,128)(2,1)} %refs_0_.2), channel_id=1, source_target_pairs={{0,1},{1,0},{2,3},{3,2},{4,5},{5,4},{6,7},{7,6},{8,9},{9,8},{10,11... | collective-permute-start | bytes 1572872 | tf_op jit(solution)/shard_map/ppermute | solution.py:24
  12.0 5.8 %copy-start = (bf16[1024,8192]{1,0:T(8,128)(2,1)S(1)}, bf16[1024,8192]{1,0:T(8,128)(2,1)}, u32[]{:S(2)}) copy-start(bf16[1024,8192]{1,0:T(8,128)(2,1)} %left.31) | copy-start | bytes 50331652
  20.8 18.4 %copy-start.13 = (f32[2,256]{1,0:T(2,128)S(1)}, f32[2,256]{1,0:T(2,128)}, u32[]{:S(2)}) copy-start(f32[2,256]{1,0:T(2,128)} %param.11) | copy-start | bytes 6148
  20.9 24.5 %collective-permute-start = (bf16[1024,256]{1,0:T(8,128)(2,1)}, bf16[1024,256]{1,0:T(8,128)(2,1)S(1)}, u32[]{:S(2)}, u32[]{:S(2)}) collective-permute-start(bf16[1024,256]{1,0:T(8,128)(2,1)} %refs_0_.2), channel_id=1, source_target_pairs={{0,8},{8,16},{16,24},{1,9},{9,17},{17,25},{2,10},{10,18},{18,26},{... | collective-permute-start | bytes 1572872 | tf_op jit(solution)/shard_map/ppermute | solution.py:242
  25.2 5.8 %copy-start.1 = (bf16[1024,8192]{1,0:T(8,128)(2,1)S(1)}, bf16[1024,8192]{1,0:T(8,128)(2,1)}, u32[]{:S(2)}) copy-start(bf16[1024,8192]{1,0:T(8,128)(2,1)} %left.31) | copy-start | bytes 50331652
  31.0 5.8 %copy-start.2 = (bf16[1024,8192]{1,0:T(8,128)(2,1)S(1)}, bf16[1024,8192]{1,0:T(8,128)(2,1)}, u32[]{:S(2)}) copy-start(bf16[1024,8192]{1,0:T(8,128)(2,1)} %left.31) | copy-start | bytes 50331652
  32.5 11.4 %collective-permute-start.5 = (bf16[1024,256]{1,0:T(8,128)(2,1)}, bf16[1024,256]{1,0:T(8,128)(2,1)S(1)}, u32[]{:S(2)}, u32[]{:S(2)}) collective-permute-start(bf16[1024,256]{1,0:T(8,128)(2,1)} %collective-permute-done.2.refs_0_), channel_id=1, source_target_pairs={{0,1},{1,0},{2,3},{3,2},{4,5},{5,4},{6,7},{7,6},{8,9},{9,8},{10,11... | collective-permute-start | bytes 1572872 | tf_op jit(solution)/shard_map/ppermute | solution.py:24
  32.6 11.4 %collective-permute-start.6 = (bf16[1024,256]{1,0:T(8,128)(2,1)S(1)}, bf16[1024,256]{1,0:T(8,128)(2,1)S(1)}, u32[]{:S(2)}, u32[]{:S(2)}) collective-permute-start(bf16[1024,256]{1,0:T(8,128)(2,1)S(1)} %collective-permute-done.3.refs_1_), channel_id=1, source_target_pairs={{0,1},{1,0},{2,3},{3,2},{4,5},{5,4},{6,7},{7,6},{8,9},{9,8},{10,11... | collective-permute-start | bytes 1572872 | tf_op jit(solution)/shard_map/ppermute | solution.py:24
  36.8 1.0 copy-start.6
  41.6 7.3 %copy-start.10 = (bf16[4,8,2,256]{3,2,1,0:T(2,128)(2,1)S(1)}, bf16[4,8,2,256]{3,2,1,0:T(2,128)(2,1)}, u32[]{:S(2)}) copy-start(bf16[4,8,2,256]{3,2,1,0:T(2,128)(2,1)} %param.12) | copy-start | bytes 98308
  45.5 5.0 %collective-permute-start.12 = (bf16[1024,256]{1,0:T(8,128)(2,1)S(1)}, bf16[1024,256]{1,0:T(8,128)(2,1)S(1)}, u32[]{:S(2)}, u32[]{:S(2)}) collective-permute-start(bf16[1024,256]{1,0:T(8,128)(2,1)S(1)} %collective-permute-done.refs_0_), channel_id=1, source_target_pairs={{0,1},{1,0},{2,3},{3,2},{4,5},{5,4},{6,7},{7,6},{8,9},{9,8},{10,11... | collective-permute-start | bytes 1572872 | tf_op jit(solution)/shard_map/ppermute | solution.py:24
  45.6 4.9 %collective-permute-start.13 = (bf16[1024,256]{1,0:T(8,128)(2,1)S(1)}, bf16[1024,256]{1,0:T(8,128)(2,1)S(1)}, u32[]{:S(2)}, u32[]{:S(2)}) collective-permute-start(bf16[1024,256]{1,0:T(8,128)(2,1)S(1)} %collective-permute-done.1.refs_1_), channel_id=1, source_target_pairs={{0,1},{1,0},{2,3},{3,2},{4,5},{5,4},{6,7},{7,6},{8,9},{9,8},{10,11... | collective-permute-start | bytes 1572872 | tf_op jit(solution)/shard_map/ppermute | solution.py:24
  46.1 5.9 %collective-permute-start.10 = (bf16[1024,256]{1,0:T(8,128)(2,1)}, bf16[1024,256]{1,0:T(8,128)(2,1)}, u32[]{:S(2)}, u32[]{:S(2)}) collective-permute-start(bf16[1024,256]{1,0:T(8,128)(2,1)} %collective-permute-done.2.refs_0_), channel_id=1, source_target_pairs={{8,16},{16,24},{9,17},{17,25},{10,18},{18,26},{11,19},{19,27},{12,... | collective-permute-start | bytes 1572872 | tf_op jit(solution)/shard_map/ppermute | solution.py:242
  47.5 19.3 %collective-permute-start.11 = (bf16[1024,256]{1,0:T(8,128)(2,1)S(1)}, bf16[1024,256]{1,0:T(8,128)(2,1)S(1)}, u32[]{:S(2)}, u32[]{:S(2)}) collective-permute-start(bf16[1024,256]{1,0:T(8,128)(2,1)S(1)} %collective-permute-done.3.refs_1_), channel_id=1, source_target_pairs={{8,0},{16,8},{9,1},{17,9},{10,2},{18,10},{11,3},{19,11},{12,4},{20... | collective-permute-start | bytes 1572872 | tf_op jit(solution)/shard_map/ppermute | solution.py:243
  66.9 0.8 copy-start.8
  67.7 4.6 %collective-permute-start.14 = (bf16[1024,256]{1,0:T(8,128)(2,1)S(1)}, bf16[1024,256]{1,0:T(8,128)(2,1)S(1)}, u32[]{:S(2)}, u32[]{:S(2)}) collective-permute-start(bf16[1024,256]{1,0:T(8,128)(2,1)S(1)} %broadcast_select_fusion.3.refs_0_), channel_id=1, source_target_pairs={{0,1},{1,0},{2,3},{3,2},{4,5},{5,4},{6,7},{7,6},{8,9},{9,8},{10,11... | collective-permute-start | bytes 1572872 | tf_op jit(solution)/shard_map/ppermute | solution.py:24
  67.9 5.9 %collective-permute-start.8 = (bf16[1024,256]{1,0:T(8,128)(2,1)S(1)}, bf16[1024,256]{1,0:T(8,128)(2,1)}, u32[]{:S(2)}, u32[]{:S(2)}) collective-permute-start(bf16[1024,256]{1,0:T(8,128)(2,1)S(1)} %collective-permute-done.refs_0_), channel_id=1, source_target_pairs={{8,16},{16,24},{9,17},{17,25},{10,18},{18,26},{11,19},{19,27},{12,... | collective-permute-start | bytes 1572872 | tf_op jit(solution)/shard_map/ppermute | solution.py:242
  69.4 17.9 %collective-permute-start.9 = (bf16[1024,256]{1,0:T(8,128)(2,1)S(1)}, bf16[1024,256]{1,0:T(8,128)(2,1)}, u32[]{:S(2)}, u32[]{:S(2)}) collective-permute-start(bf16[1024,256]{1,0:T(8,128)(2,1)S(1)} %collective-permute-done.1.refs_1_), channel_id=1, source_target_pairs={{8,0},{16,8},{9,1},{17,9},{10,2},{18,10},{11,3},{19,11},{12,4},{20... | collective-permute-start | bytes 1572872 | tf_op jit(solution)/shard_map/ppermute | solution.py:243
  88.3 10.4 %collective-permute-start.19 = (bf16[1024,256]{1,0:T(8,128)(2,1)S(1)}, bf16[1024,256]{1,0:T(8,128)(2,1)S(1)}, u32[]{:S(2)}, u32[]{:S(2)}) collective-permute-start(bf16[1024,256]{1,0:T(8,128)(2,1)S(1)} %broadcast_select_fusion.2.refs_0_), channel_id=1, source_target_pairs={{0,1},{1,0},{2,3},{3,2},{4,5},{5,4},{6,7},{7,6},{8,9},{9,8},{10,11... | collective-permute-start | bytes 1572872 | tf_op jit(solution)/shard_map/ppermute | solution.py:24
  89.3 10.9 %collective-permute-start.17 = (bf16[1024,256]{1,0:T(8,128)(2,1)}, bf16[1024,256]{1,0:T(8,128)(2,1)S(1)}, u32[]{:S(2)}, u32[]{:S(2)}) collective-permute-start(bf16[1024,256]{1,0:T(8,128)(2,1)} %collective-permute-done.10), channel_id=1, source_target_pairs={{16,24},{17,25},{18,26},{19,27},{20,28},{21,29},{22,30},{23,31}} | collective-permute-start | bytes 1572872 | tf_op jit(solution)/shard_map/ppermute | solution.py:242
  90.0 16.4 %collective-permute-start.18 = (bf16[1024,256]{1,0:T(8,128)(2,1)}, bf16[1024,256]{1,0:T(8,128)(2,1)S(1)}, u32[]{:S(2)}, u32[]{:S(2)}) collective-permute-start(bf16[1024,256]{1,0:T(8,128)(2,1)} %copy-done.8), channel_id=1, source_target_pairs={{8,0},{9,1},{10,2},{11,3},{12,4},{13,5},{14,6},{15,7}} | collective-permute-start | bytes 1572872 | tf_op jit(solution)/shard_map/ppermute | solution.py:243
  91.3 5.8 %copy-start.3 = (bf16[1024,8192]{1,0:T(8,128)(2,1)S(1)}, bf16[1024,8192]{1,0:T(8,128)(2,1)}, u32[]{:S(2)}) copy-start(bf16[1024,8192]{1,0:T(8,128)(2,1)} %left.31) | copy-start | bytes 50331652
  106.5 34.0 %collective-permute-start.20 = (bf16[1024,256]{1,0:T(8,128)(2,1)S(1)}, bf16[1024,256]{1,0:T(8,128)(2,1)S(1)}, u32[]{:S(2)}, u32[]{:S(2)}) collective-permute-start(bf16[1024,256]{1,0:T(8,128)(2,1)S(1)} %broadcast_select_fusion.1.refs_0_), channel_id=1, source_target_pairs={{0,1},{1,0},{2,3},{3,2},{4,5},{5,4},{6,7},{7,6},{8,9},{9,8},{10,11... | collective-permute-start | bytes 1572872 | tf_op jit(solution)/shard_map/ppermute | solution.py:24
  106.7 35.3 %collective-permute-start.15 = (bf16[1024,256]{1,0:T(8,128)(2,1)}, bf16[1024,256]{1,0:T(8,128)(2,1)S(1)}, u32[]{:S(2)}, u32[]{:S(2)}) collective-permute-start(bf16[1024,256]{1,0:T(8,128)(2,1)} %collective-permute-done.8), channel_id=1, source_target_pairs={{16,24},{17,25},{18,26},{19,27},{20,28},{21,29},{22,30},{23,31}} | collective-permute-start | bytes 1572872 | tf_op jit(solution)/shard_map/ppermute | solution.py:242
  107.4 34.6 %collective-permute-start.16 = (bf16[1024,256]{1,0:T(8,128)(2,1)}, bf16[1024,256]{1,0:T(8,128)(2,1)S(1)}, u32[]{:S(2)}, u32[]{:S(2)}) collective-permute-start(bf16[1024,256]{1,0:T(8,128)(2,1)} %collective-permute-done.9), channel_id=1, source_target_pairs={{8,0},{9,1},{10,2},{11,3},{12,4},{13,5},{14,6},{15,7}} | collective-permute-start | bytes 1572872 | tf_op jit(solution)/shard_map/ppermute | solution.py:243
  108.8 17.7 %collective-permute-start.28 = (bf16[256,128]{1,0:T(8,128)(2,1)S(1)}, bf16[256,128]{1,0:T(8,128)(2,1)S(1)}, u32[]{:S(2)}, u32[]{:S(2)}) collective-permute-start(bf16[256,128]{1,0:T(8,128)(2,1)S(1)} %reshape.218), channel_id=1, source_target_pairs={{0,24},{8,0},{16,8},{24,16},{1,25},{9,1},{17,9},{25,17},{2,26},{10... | collective-permute-start | bytes 196616 | tf_op jit(solution)/shard_map/ppermute | solution.py:24
  108.8 18.3 %collective-permute-start.27 = (bf16[256,128]{1,0:T(8,128)(2,1)S(1)}, bf16[256,128]{1,0:T(8,128)(2,1)S(1)}, u32[]{:S(2)}, u32[]{:S(2)}) collective-permute-start(bf16[256,128]{1,0:T(8,128)(2,1)S(1)} %reshape.218), channel_id=1, source_target_pairs={{0,16},{8,24},{16,0},{24,8},{1,17},{9,25},{17,1},{25,9},{2,18},{10... | collective-permute-start | bytes 196616 | tf_op jit(solution)/shard_map/ppermute | solution.py:24
  126.5 6.1 %collective-permute-start.26 = (bf16[256,128]{1,0:T(8,128)(2,1)S(1)}, bf16[256,128]{1,0:T(8,128)(2,1)S(1)}, u32[]{:S(2)}, u32[]{:S(2)}) collective-permute-start(bf16[256,128]{1,0:T(8,128)(2,1)S(1)} %reshape.218), channel_id=1, source_target_pairs={{0,8},{8,16},{16,24},{24,0},{1,9},{9,17},{17,25},{25,1},{2,10},{10... | collective-permute-start | bytes 196616 | tf_op jit(solution)/shard_map/ppermute | solution.py:24
  133.3 5.8 %copy-start.4 = (bf16[1024,8192]{1,0:T(8,128)(2,1)S(1)}, bf16[1024,8192]{1,0:T(8,128)(2,1)}, u32[]{:S(2)}) copy-start(bf16[1024,8192]{1,0:T(8,128)(2,1)} %left.31) | copy-start | bytes 50331652
  139.1 6.3 %slice-start = ((s8[16777216]{0:T(1024)(128)(4,1)}), s8[4194304]{0:T(1024)(128)(4,1)S(1)}, s32[]{:S(2)}) async-start(s8[16777216]{0:T(1024)(128)(4,1)} %bitcast.106), calls=%async_computation | async-start | bytes 8388608
  139.1 6.3 %slice-start.1 = ((s8[16777216]{0:T(1024)(128)(4,1)}), s8[4194304]{0:T(1024)(128)(4,1)S(1)}, s32[]{:S(2)}) async-start(s8[16777216]{0:T(1024)(128)(4,1)} %bitcast.106), calls=%async_computation.1 | async-start | bytes 8388608
  140.5 4.8 %slice-start.2 = ((s8[16777216]{0:T(1024)(128)(4,1)}), s8[4194304]{0:T(1024)(128)(4,1)S(1)}, s32[]{:S(2)}) async-start(s8[16777216]{0:T(1024)(128)(4,1)} %bitcast.106), calls=%async_computation.2 | async-start | bytes 8388608
  140.5 4.8 %slice-start.3 = ((s8[16777216]{0:T(1024)(128)(4,1)}), s8[4194304]{0:T(1024)(128)(4,1)S(1)}, s32[]{:S(2)}) async-start(s8[16777216]{0:T(1024)(128)(4,1)} %bitcast.106), calls=%async_computation.3 | async-start | bytes 8388608
  142.1 1.2 collective-permute-start.21
  142.2 27.6 %collective-permute-start.25 = (bf16[1024,256]{1,0:T(8,128)(2,1)S(1)}, bf16[1024,256]{1,0:T(8,128)(2,1)S(1)}, u32[]{:S(2)}, u32[]{:S(2)}) collective-permute-start(bf16[1024,256]{1,0:T(8,128)(2,1)S(1)} %broadcast_select_fusion.refs_0_), channel_id=1, source_target_pairs={{0,1},{1,0},{2,3},{3,2},{4,5},{5,4},{6,7},{7,6},{8,9},{9,8},{10,11... | collective-permute-start | bytes 1572872 | tf_op jit(solution)/shard_map/ppermute | solution.py:24
  143.3 3.6 %collective-permute-start.24 = (f32[1,256]{1,0:T(1,128)S(1)}, f32[1,256]{1,0:T(1,128)S(1)}, u32[]{:S(2)}, u32[]{:S(2)}) collective-permute-start(f32[1,256]{1,0:T(1,128)S(1)} %max.108), channel_id=1, source_target_pairs={{0,24},{8,0},{16,8},{24,16},{1,25},{9,1},{17,9},{25,17},{2,26},{10... | collective-permute-start | bytes 3080 | tf_op jit(solution)/shard_map/ppermute | solution.py:24
  143.3 4.5 %collective-permute-start.23 = (f32[1,256]{1,0:T(1,128)S(1)}, f32[1,256]{1,0:T(1,128)S(1)}, u32[]{:S(2)}, u32[]{:S(2)}) collective-permute-start(f32[1,256]{1,0:T(1,128)S(1)} %max.108), channel_id=1, source_target_pairs={{0,16},{8,24},{16,0},{24,8},{1,17},{9,25},{17,1},{25,9},{2,18},{10... | collective-permute-start | bytes 3080 | tf_op jit(solution)/shard_map/ppermute | solution.py:24
  143.3 5.9 %collective-permute-start.22 = (f32[1,256]{1,0:T(1,128)S(1)}, f32[1,256]{1,0:T(1,128)S(1)}, u32[]{:S(2)}, u32[]{:S(2)}) collective-permute-start(f32[1,256]{1,0:T(1,128)S(1)} %max.108), channel_id=1, source_target_pairs={{0,8},{8,16},{16,24},{24,0},{1,9},{9,17},{17,25},{25,1},{2,10},{10... | collective-permute-start | bytes 3080 | tf_op jit(solution)/shard_map/ppermute | solution.py:24
  149.3 35.7 %copy-start.11 = (f32[1,256]{1,0:T(1,128)}, f32[1,256]{1,0:T(1,128)S(1)}, u32[]{:S(2)}) copy-start(f32[1,256]{1,0:T(1,128)S(1)} %add_sqrt_fusion) | copy-start | bytes 3076
  150.8 1.7 collective-permute-start.29
  152.4 0.7 copy-start.14
  153.1 45.3 %copy-start.7 = (bf16[1024,1,256]{2,0,1:T(8,128)(2,1)S(1)}, bf16[1024,1,256]{2,0,1:T(8,128)(2,1)}, u32[]{:S(2)}) copy-start(bf16[1024,1,256]{2,0,1:T(8,128)(2,1)} %fusion.49) | copy-start | bytes 1572868
  163.5 4.8 %collective-permute-start.31 = (f32[2,256]{1,0:T(2,128)S(1)}, f32[2,256]{1,0:T(2,128)S(1)}, u32[]{:S(2)}, u32[]{:S(2)}) collective-permute-start(f32[2,256]{1,0:T(2,128)S(1)} %bitcast.135), channel_id=1, source_target_pairs={{0,16},{8,24},{16,0},{24,8},{1,17},{9,25},{17,1},{25,9},{2,18},{10... | collective-permute-start | bytes 6152 | tf_op jit(solution)/shard_map/ppermute | solution.py:24
  164.1 5.4 %collective-permute-start.32 = (f32[2,256]{1,0:T(2,128)S(1)}, f32[2,256]{1,0:T(2,128)S(1)}, u32[]{:S(2)}, u32[]{:S(2)}) collective-permute-start(f32[2,256]{1,0:T(2,128)S(1)} %bitcast.134), channel_id=1, source_target_pairs={{0,8},{8,16},{16,24},{24,0},{1,9},{9,17},{17,25},{25,1},{2,10},{10... | collective-permute-start | bytes 6152 | tf_op jit(solution)/shard_map/ppermute | solution.py:24
  166.2 3.6 %collective-permute-start.30 = (f32[2,256]{1,0:T(2,128)S(1)}, f32[2,256]{1,0:T(2,128)S(1)}, u32[]{:S(2)}, u32[]{:S(2)}) collective-permute-start(f32[2,256]{1,0:T(2,128)S(1)} %bitcast.133), channel_id=1, source_target_pairs={{0,24},{8,0},{16,8},{24,16},{1,25},{9,1},{17,9},{25,17},{2,26},{10... | collective-permute-start | bytes 6152 | tf_op jit(solution)/shard_map/ppermute | solution.py:24
  169.9 5.8 %copy-start.5 = (bf16[1024,8192]{1,0:T(8,128)(2,1)S(1)}, bf16[1024,8192]{1,0:T(8,128)(2,1)}, u32[]{:S(2)}) copy-start(bf16[1024,8192]{1,0:T(8,128)(2,1)} %left.31) | copy-start | bytes 50331652
  177.9 1.5 collective-permute-start.33
  179.5 0.7 copy-start.9
  185.9 6.1 %collective-permute-start.34 = (bf16[256,128]{1,0:T(8,128)(2,1)S(1)}, bf16[256,128]{1,0:T(8,128)(2,1)S(1)}, u32[]{:S(2)}, u32[]{:S(2)}) collective-permute-start(bf16[256,128]{1,0:T(8,128)(2,1)S(1)} %get-tuple-element.76), channel_id=1, source_target_pairs={{0,24},{8,0},{16,8},{24,16},{1,25},{9,1},{17,9},{25,17},{2,26},{10... | collective-permute-start | bytes 196616 | tf_op jit(solution)/shard_map/ppermute | solution.py:24
  189.5 6.5 %collective-permute-start.36 = (bf16[256,128]{1,0:T(8,128)(2,1)S(1)}, bf16[256,128]{1,0:T(8,128)(2,1)S(1)}, u32[]{:S(2)}, u32[]{:S(2)}) collective-permute-start(bf16[256,128]{1,0:T(8,128)(2,1)S(1)} %get-tuple-element.77), channel_id=1, source_target_pairs={{0,8},{8,16},{16,24},{24,0},{1,9},{9,17},{17,25},{25,1},{2,10},{10... | collective-permute-start | bytes 196616 | tf_op jit(solution)/shard_map/ppermute | solution.py:24
  189.5 7.8 %collective-permute-start.35 = (bf16[256,128]{1,0:T(8,128)(2,1)S(1)}, bf16[256,128]{1,0:T(8,128)(2,1)S(1)}, u32[]{:S(2)}, u32[]{:S(2)}) collective-permute-start(bf16[256,128]{1,0:T(8,128)(2,1)S(1)} %get-tuple-element.78), channel_id=1, source_target_pairs={{0,16},{8,24},{16,0},{24,8},{1,17},{9,25},{17,1},{25,9},{2,18},{10... | collective-permute-start | bytes 196616 | tf_op jit(solution)/shard_map/ppermute | solution.py:24
  198.4 2.2 %collective-permute-start.37 = (bf16[4,8,1024]{2,1,0:T(8,128)(2,1)S(1)}, bf16[4,8,1024]{2,1,0:T(8,128)(2,1)S(1)}, u32[]{:S(2)}, u32[]{:S(2)}) collective-permute-start(bf16[4,8,1024]{2,1,0:T(8,128)(2,1)S(1)} %reshape.223), channel_id=1, source_target_pairs={{0,1},{1,0},{2,3},{3,2},{4,5},{5,4},{6,7},{7,6},{8,9},{9,8},{10,11... | collective-permute-start | bytes 196616 | tf_op jit(solution)/shard_map/ppermute | solution.py:24

commit v3 on v2

--- a/solution.py
+++ b/solution.py
@@ -36,47 +36,72 @@
     n = lax.axis_size("seq")
     if n > SHORT:
         me, k = lax.axis_index("seq"), jnp.arange(n)
-        back = lax.all_to_all(x[(me - k) % n], "seq", split_axis=0, concat_axis=0)
+        back = lax.all_to_all(jnp.stack(x)[(me - k) % n], "seq", split_axis=0, concat_axis=0)
         return list(back[(me + k) % n])
     return [x[0]] + [shifted(x[k], "seq", -k) for k in range(1, n)]
 
 
-def project_kernel(count, has_total, info, left, *refs):
+def project_kernel(count, pieces, has_total, info, hidden, *refs):
     weights, total = refs[:count], refs[count] if has_total else None
-    out, held, arrived = refs[-3:]
-    depth = held.shape[1]
-    copies = [pltpu.make_async_copy(weights[j], held.at[j], arrived.at[j]) for j in range(count)]
-    for copy in copies:
-        copy.start()
-    out[...] = total[...] if has_total else jnp.zeros_like(out)
-    for j, copy in enumerate(copies):
-        copy.wait()
+    out, lefts, rights, left_here, right_here = refs[-5:]
+    tokens, depth = lefts.shape[1:]
+    tile = tokens // pieces
+
+    def right_copy(j):
+        return pltpu.make_async_copy(weights[j], rights.at[j], right_here.at[j])
+
+    def left_copy(j, p):
+        rows = pl.ds(p * tile, tile)
+        block = pl.ds(pl.multiple_of(info[j] * depth, depth), depth)
+        return pltpu.make_async_copy(
+            hidden.at[rows, block], lefts.at[j, rows, :], left_here.at[j, p]
+        )
+
+    for j in range(count):
 
         @pl.when(info[count + j] == 1)
         def _(j=j):
-            block = pl.ds(pl.multiple_of(info[j] * depth, depth), depth)
-            out[...] += jnp.dot(left[:, block], held[j], preferred_element_type=jnp.float32)
+            right_copy(j).start()
+            for p in range(pieces):
+                left_copy(j, p).start()
+
+    out[...] = total[...] if has_total else jnp.zeros_like(out)
+    for j in range(count):
+
+        @pl.when(info[count + j] == 1)
+        def _(j=j):
+            right_copy(j).wait()
+            for p in range(pieces):
+                rows = pl.ds(p * tile, tile)
+                left_copy(j, p).wait()
+                out[rows, :] += jnp.dot(
+                    lefts[j, rows, :], rights[j], preferred_element_type=jnp.float32
+                )
 
 
 def project(hidden, total, weights, where, live):
     tokens = hidden.shape[0]
     depth, columns = weights[0].shape
     count = len(weights)
+    pieces = 4 if tokens % 64 == 0 else 1
     info = jnp.stack([jnp.asarray(v, jnp.int32) for v in list(where) + list(live)])
     has_total = total is not None
     whole = pl.BlockSpec(memory_space=pltpu.VMEM)
     return pl.pallas_call(
-        functools.partial(project_kernel, count, has_total),
+        functools.partial(project_kernel, count, pieces, has_total),
         out_shape=jax.ShapeDtypeStruct((tokens, columns), jnp.float32),
-        in_specs=[pl.BlockSpec(memory_space=pltpu.SMEM), whole]
+        in_specs=[pl.BlockSpec(memory_space=pltpu.SMEM)]
+        + [pl.BlockSpec(memory_space=pltpu.HBM)]
         + [pl.BlockSpec(memory_space=pl.ANY)] * count
         + [whole] * has_total,
         out_specs=whole,
         scratch_shapes=[
+            pltpu.VMEM((count, tokens, depth), hidden.dtype),
             pltpu.VMEM((count, depth, columns), weights[0].dtype),
+            pltpu.SemaphoreType.DMA((count, pieces)),
             pltpu.SemaphoreType.DMA((count,)),
         ],
-        compiler_params=pltpu.CompilerParams(vmem_limit_bytes=12 * 2**20),
+        compiler_params=pltpu.CompilerParams(vmem_limit_bytes=50 * 2**20),
         cost_estimate=pl.CostEstimate(
             flops=2 * tokens * depth * columns * count,
             bytes_accessed=2 * count * depth * (tokens + columns) + 8 * tokens * columns,
@@ -87,8 +112,9 @@
     )(info, hidden, *weights, *([total] if has_total else []))
 
 
-def score_kernel(parts, steps, scale, group, query, smooth, count, *refs):
-    keys, (probs, highest, total), scores = refs[:parts], refs[parts:-1], refs[-1]
+def score_kernel(slots, parts, steps, scale, group, query, smooth, count, *refs):
+    keys, probs, stats = refs[:parts], refs[parts], refs[parts + 1 : parts + 1 + slots]
+    scores, tops, sums = refs[-3:]
     tokens = keys[0].shape[0]
     scaled = (query[0].astype(jnp.float32) * smooth[...]).astype(jnp.bfloat16)
     for p in range(parts):
@@ -107,17 +133,24 @@
             ],
             axis=0,
         )
+        bias = jnp.where(times > 0.0, 0.0, NEGATIVE)
         for step in range(steps):
             start = (step * requests + first) * group_rows
             at = pl.ds(start, pair * group_rows)
-            raw = jnp.where(times > 0.0, scores[at, :] * scale, NEGATIVE)
+            raw = scores[at, :] * scale + bias
             top = jnp.max(raw, axis=1, keepdims=True)
-            expd = jnp.exp(raw - top)
-            highest[0, at, :] = top
-            total[0, at, :] = jnp.sum(expd * times, axis=1, keepdims=True)
-            probs[0, at, :] = (expd.astype(jnp.bfloat16).astype(jnp.float32) * times).astype(
-                jnp.bfloat16
+            counted = jnp.exp(raw - top) * times
+            probs[0, at, :] = counted.astype(jnp.bfloat16)
+            tops[at, :] = jnp.broadcast_to(top, (pair * group_rows, 128))
+            sums[at, :] = jnp.broadcast_to(
+                jnp.sum(counted, axis=1, keepdims=True), (pair * group_rows, 128)
             )
+    for slot in range(slots):
+
+        @pl.when(pl.program_id(0) == slot)
+        def _(slot=slot):
+            stats[slot][0:1, :] = jnp.transpose(tops[...])[0:1, :]
+            stats[slot][1:2, :] = jnp.transpose(sums[...])[0:1, :]
 
 
 def score(groups, query, smooth, count, keys, steps, scale):
@@ -125,14 +158,10 @@
     tokens = keys[0].shape[0]
     parts = len(keys)
     requests = count.shape[1]
-    slot_spec = pl.BlockSpec((1, rows, 1), lambda k, group: (k, 0, 0))
-    return pl.pallas_call(
-        functools.partial(score_kernel, parts, steps, scale),
-        out_shape=(
-            jax.ShapeDtypeStruct((slots, rows, parts * tokens), jnp.bfloat16),
-            jax.ShapeDtypeStruct((slots, rows, 1), jnp.float32),
-            jax.ShapeDtypeStruct((slots, rows, 1), jnp.float32),
-        ),
+    probs, *stats = pl.pallas_call(
+        functools.partial(score_kernel, slots, parts, steps, scale),
+        out_shape=[jax.ShapeDtypeStruct((slots, rows, parts * tokens), jnp.bfloat16)]
+        + [jax.ShapeDtypeStruct((2, rows), jnp.float32)] * slots,
         grid_spec=pltpu.PrefetchScalarGridSpec(
             num_scalar_prefetch=1,
             grid=(slots,),
@@ -142,13 +171,15 @@
                 pl.BlockSpec((1, requests, parts * tokens), lambda k, group: (group[k], 0, 0)),
             ]
             + [pl.BlockSpec((tokens, width), lambda k, group: (0, 0))] * parts,
-            out_specs=(
-                pl.BlockSpec((1, rows, parts * tokens), lambda k, group: (k, 0, 0)),
-                slot_spec,
-                slot_spec,
-            ),
-            scratch_shapes=[pltpu.VMEM((rows, parts * tokens), jnp.float32)],
+            out_specs=[pl.BlockSpec((1, rows, parts * tokens), lambda k, group: (k, 0, 0))]
+            + [pl.BlockSpec((2, rows), lambda k, group: (0, 0))] * slots,
+            scratch_shapes=[
+                pltpu.VMEM((rows, parts * tokens), jnp.float32),
+                pltpu.VMEM((rows, 128), jnp.float32),
+                pltpu.VMEM((rows, 128), jnp.float32),
+            ],
         ),
+        compiler_params=pltpu.CompilerParams(vmem_limit_bytes=16 * 2**20),
         cost_estimate=pl.CostEstimate(
             flops=2 * slots * rows * width * parts * tokens,
             bytes_accessed=2 * slots * rows * parts * tokens,
@@ -156,12 +187,13 @@
         ),
         name="score",
     )(groups, query, smooth, count, *keys)
-
-
-def weigh_kernel(parts, probs, *refs):
-    values, out = refs[:parts], refs[-1]
+    return probs, stats
+
+
+def weigh_kernel(slots, parts, probs, *refs):
+    values, outs = refs[:parts], refs[parts:]
     tokens = values[0].shape[0]
-    out[0] = sum(
+    summed = sum(
         jnp.dot(
             probs[0, :, p * tokens : (p + 1) * tokens],
             values[p][...],
@@ -169,6 +201,11 @@
         )
         for p in range(parts)
     ).astype(jnp.bfloat16)
+    for slot in range(slots):
+
+        @pl.when(pl.program_id(0) == slot)
+        def _(slot=slot):
+            outs[slot][...] = summed
 
 
 def weigh(probs, values):
@@ -176,12 +213,13 @@
     tokens, width = values[0].shape
     parts = len(values)
     return pl.pallas_call(
-        functools.partial(weigh_kernel, parts),
-        out_shape=jax.ShapeDtypeStruct((slots, rows, width), jnp.bfloat16),
+        functools.partial(weigh_kernel, slots, parts),
+        out_shape=[jax.ShapeDtypeStruct((rows, width), jnp.bfloat16)] * slots,
         grid=(slots,),
         in_specs=[pl.BlockSpec((1, rows, parts * tokens), lambda k: (k, 0, 0))]
         + [pl.BlockSpec((tokens, width), lambda k: (0, 0))] * parts,
-        out_specs=pl.BlockSpec((1, rows, width), lambda k: (k, 0, 0)),
+        out_specs=[pl.BlockSpec((rows, width), lambda k: (0, 0))] * slots,
+        compiler_params=pltpu.CompilerParams(vmem_limit_bytes=16 * 2**20),
         cost_estimate=pl.CostEstimate(
             flops=2 * slots * rows * width * parts * tokens,
             bytes_accessed=2 * slots * rows * parts * tokens,
@@ -224,6 +262,13 @@
     for p in range(1, parts):
         out = jnp.where(index == p, pieces[p], out)
     return out
+
+
+def smooth_of(raw_keys):
+    top = jnp.max(jnp.abs(raw_keys), axis=0, keepdims=True)
+    top = functools.reduce(jnp.maximum, from_all(top, "rep"))
+    top = functools.reduce(jnp.maximum, from_all(top, "seq"))
+    return jnp.sqrt(top + EPSILON)
 
 
 def line_project(hidden, key_weight, value_weight, raw_query):
@@ -271,19 +316,20 @@
     moving["k"], moving["v"] = (key_weight,) * 2, (value_weight,) * 2
     for name in names:
         send(name, 1)
+    queries = from_all(raw_query, "seq")
+    for name in names:
         absorb(name, 0)
-    queries = None
     for hop in range(1, groups):
         for name in names:
-            other = names[1 - names.index(name)]
-            moving[name], totals[other] = lax.optimization_barrier((arrived[name], totals[other]))
+            if name == names[-1] and hop == groups - 1:
+                smooth = smooth_of(totals["k"])
+                moving[name], smooth = lax.optimization_barrier((arrived[name], smooth))
+            else:
+                moving[name], totals = lax.optimization_barrier((arrived[name], totals))
             if hop < groups - 1:
                 send(name, hop + 1)
-            if name == "k" and hop == max(1, groups - 2):
-                raw_query, moving[name] = lax.optimization_barrier((raw_query, moving[name]))
-                queries = jnp.stack(from_all(raw_query, "seq"))
             absorb(name, hop)
-    return totals["k"], totals["v"], queries
+    return totals["k"], totals["v"], smooth, jnp.stack(queries)
 
 
 def on_device(
@@ -311,23 +357,22 @@
             for weight in (key_weight, value_weight)
         )
         queries = jnp.stack(from_all(raw_query, "seq"))
+        smooth = smooth_of(raw_keys)
     else:
-        raw_keys, raw_values, queries = line_project(hidden, key_weight, value_weight, raw_query)
-
-    local_max = jnp.max(jnp.abs(raw_keys), axis=0, keepdims=True)
-    local_max = functools.reduce(jnp.maximum, from_all(local_max, "rep"))
-    local_max = functools.reduce(jnp.maximum, from_all(local_max, "seq"))
-    smooth = jnp.sqrt(local_max + EPSILON)
-    smoothing = smooth.reshape(-1)
-    keys = clip_keys(raw_keys, smooth, group_scale)
-    values = clip_values(raw_values, group_scale)
-    kv_cache = jnp.stack([keys, values], axis=1)
+        raw_keys, raw_values, smooth, queries = line_project(hidden, key_weight, value_weight, raw_query)
 
     def by_head(x):
         return [my_part(x, owners, my_owner, 1)] + [
             shifted(my_part(x, owners, (my_owner + k) % owners, 1), "rep", k)
             for k in range(1, owners)
         ]
+
+    smoothing = smooth.reshape(-1)
+    keys = clip_keys(raw_keys, smooth, group_scale)
+    head_keys = by_head(keys)
+    head_keys, raw_values = lax.optimization_barrier((head_keys, raw_values))
+    values = clip_values(raw_values, group_scale)
+    kv_cache = jnp.stack([keys, values], axis=1)
 
     my_smooth = my_part(smooth, owners, my_owner, 1)
     first_pages = [(my_group * owners + owner) * pages_dev for owner in owner_at]
@@ -335,12 +380,10 @@
     counts = counts.reshape(groups, per_group, -1)
     group_at = jnp.stack([(my_group - k) % groups for k in range(groups)])
     score_scale = HD ** (-0.5)
-    probs, highest, total = score(
-        group_at, queries, my_smooth, counts, by_head(keys), step_count, score_scale
+    probs, stats = score(
+        group_at, queries, my_smooth, counts, head_keys, step_count, score_scale
     )
     summed = weigh(probs, by_head(values))
-    stats = jnp.stack([highest[..., 0], total[..., 0]], axis=1)
-
     stats = jnp.stack(to_groups(stats))
     highest, total = stats[:, 0], stats[:, 1]
 
@@ -374,7 +417,8 @@
     norm = 1.0 / (jnp.sum(total * share, axis=0) + fresh_total * fresh_share)
     share, fresh_share = share * norm, fresh_share * norm
     attention = fresh_summed.reshape(-1, HD) * fresh_share[:, None]
-    for k, part in enumerate(to_groups(summed)):
+    summed, kv_cache = lax.optimization_barrier((to_groups(summed), kv_cache))
+    for k, part in enumerate(summed):
         attention = attention + part.astype(jnp.float32) * share[k][:, None]
     attention = attention.astype(jnp.bfloat16).reshape(step_count, per_group, group_size * HD)
     by_owner = from_all(attention, "rep")

time: 203 us -> 166 us (0.82)
  local copies, waits for them, and re-layouts: 39 us -> 4.68 us
  waiting for transfers between devices: 66.5 us -> 35.9 us
  Pallas kernels: 38.6 us -> 63.3 us
  starting transfers between devices: 40.2 us -> 46 us
  other arithmetic: 13.6 us -> 10.9 us
    unnamed x43 -> x41, local copies, waits for them, and re-layouts: 37.8 us -> 3.82 us
    pallas_call x18, Pallas kernels: 38.6 us -> 63.3 us  [the longest x16 55.6 us: project(): pl.pallas_call(functools.partial(project_kernel, count, pieces, has_total...]
    ppermute x6, waiting for transfers between devices: 34.5 us -> 17.7 us  [send(): lax.ppermute(right, 'seq', [(i, i - 1) for i in range(1, groups - hop + 1)])]
    ppermute x26, waiting for transfers between devices: 32 us -> 18.2 us  [shifted(): return lax.ppermute(x, axis, [(i, (i + k) % n) for i in range(n)])]
    ppermute x26, starting transfers between devices: 17.5 us -> 25.9 us  [shifted(): return lax.ppermute(x, axis, [(i, (i + k) % n) for i in range(n)])]
    ppermute x6, starting transfers between devices: 15 us -> 12.4 us  [send(): lax.ppermute(left, 'seq', [(i, i + 1) for i in range(hop - 1, groups - 1)])]
    pallas_call x2 -> x0, other arithmetic: 2.51 us -> none  [score(): pl.pallas_call(functools.partial(score_kernel, parts, steps, scale), out_...]
  transfers between devices with their start and end apart: 38 -> 38, of which waited for: 15 -> 11; matrix products, arithmetic and copies ran while one was open for 7% -> 8% of each run, Pallas kernels for 16% -> 34%
where the time goes in v3:
time: 166 us; the launch traced here: 165 us
  Pallas kernels  63.3 us (38%)
  starting transfers between devices  46 us (28%)
  waiting for transfers between devices  35.9 us (22%)
  other arithmetic  10.9 us (7%)
  local copies, waits for them, and re-layouts  4.68 us (3%)
  matrix products  2.45 us (1%)
  between operations  1.67 us (1%)
    pallas_call x16, Pallas kernels, project(): pl.pallas_call(functools.partial(project_kernel, count, pieces, has_total...  55.6 us
    ppermute x26, starting transfers between devices, shifted(): return lax.ppermute(x, axis, [(i, (i + k) % n) for i in range(n)])  25.9 us
    ppermute x26, waiting for transfers between devices, shifted(): return lax.ppermute(x, axis, [(i, (i + k) % n) for i in range(n)])  18.2 us
    ppermute x6, waiting for transfers between devices, send(): lax.ppermute(right, 'seq', [(i, i - 1) for i in range(1, groups - hop + 1)])  17.7 us
    ppermute x6, starting transfers between devices, send(): lax.ppermute(left, 'seq', [(i, i + 1) for i in range(hop - 1, groups - 1)])  12.4 us
    ppermute x6, starting transfers between devices, send(): lax.ppermute(right, 'seq', [(i, i - 1) for i in range(1, groups - hop + 1)])  7.74 us
    pallas_call x1, Pallas kernels, score(): pl.pallas_call(functools.partial(score_kernel, slots, parts, steps, scale...  5.88 us
    unnamed x41, local copies, waits for them, and re-layouts  3.82 us
  transfers between devices with their start and end apart: 38, of which 11 were waited for; matrix products, arithmetic and copies ran while one was open for 8% of the time, Pallas kernels for 34%

profile of v3, /device:TPU:0, one launch (start us, length us, event | category | flops | bytes accessed | tf_op | source)
XLA Modules:
  0.0 164.9 jit_solution(15456624132315340210)
XLA Ops:
  1.2 4.5 %collective-permute-start.5 = (bf16[1024,256]{1,0:T(8,128)(2,1)}, bf16[1024,256]{1,0:T(8,128)(2,1)S(1)}, u32[]{:S(2)}, u32[]{:S(2)}) collective-permute-start(bf16[1024,256]{1,0:T(8,128)(2,1)} %refs_0_.2), channel_id=1, source_target_pairs={{0,8},{8,16},{16,24},{1,9},{9,17},{17,25},{2,10},{10,18},{18,26},{... | collective-permute-start | bytes 1572872 | tf_op jit(solution)/shard_map/ppermute | solution.py:287
  5.7 1.3 collective-permute-start.6
  7.3 4.4 %collective-permute-start.3 = (bf16[1024,256]{1,0:T(8,128)(2,1)}, bf16[1024,256]{1,0:T(8,128)(2,1)S(1)}, u32[]{:S(2)}, u32[]{:S(2)}) collective-permute-start(bf16[1024,256]{1,0:T(8,128)(2,1)} %refs_0_.3), channel_id=1, source_target_pairs={{0,8},{8,16},{16,24},{1,9},{9,17},{17,25},{2,10},{10,18},{18,26},{... | collective-permute-start | bytes 1572872 | tf_op jit(solution)/shard_map/ppermute | solution.py:287
  11.9 0.9 bitcast_convert_fusion
  12.9 1.0 copy-done.1
  13.9 3.4 %project.16.refs_1_ = f32[1024,256]{1,0:T(8,128)S(1)} custom-call(s32[2]{0:T(128)S(1)} %pad_add_fusion.info, bf16[1024,8192]{1,0:T(8,128)(2,1)} %hidden.31, bf16[1024,256]{1,0:T(8,128)(2,1)S(1)} %copy-done.1), custom_call_target="tpu_custom_call" | custom-call | flops 536870912 | bytes 4718592 | tf_op jit(solution)/shard_map/project/pallas_call | solution.py:90
  17.3 3.4 %project.18.refs_1_ = f32[1024,256]{1,0:T(8,128)S(1)} custom-call(s32[2]{0:T(128)S(1)} %pad_add_fusion.info, bf16[1024,8192]{1,0:T(8,128)(2,1)} %hidden.31, bf16[1024,256]{1,0:T(8,128)(2,1)S(1)} %copy-done.2), custom_call_target="tpu_custom_call" | custom-call | flops 536870912 | bytes 4718592 | tf_op jit(solution)/shard_map/project/pallas_call | solution.py:90
  20.8 1.3 collective-permute-start.4
  22.1 3.8 %project.17.refs_2_ = f32[1024,256]{1,0:T(8,128)S(1)} custom-call(s32[2]{0:T(128)S(1)} %pad_add_fusion.1.info, bf16[1024,8192]{1,0:T(8,128)(2,1)} %hidden.31, bf16[1024,256]{1,0:T(8,128)(2,1)} %collective-permute-done.7.refs_0_, f32[1024,256]{1,0:T(8,128)S(1)} %project.16.refs_1_), custom_call_target="tpu_custom_call", output_to_operand_aliasing={{}: (3, {})} | custom-call | flops 536870912 | bytes 4718592 | tf_op jit(solution)/shard_map/project/pallas_call | solution.py:90
  26.0 2.7 %collective-permute-start = (bf16[256,128]{1,0:T(8,128)(2,1)S(1)}, bf16[256,128]{1,0:T(8,128)(2,1)S(1)}, u32[]{:S(2)}, u32[]{:S(2)}) collective-permute-start(bf16[256,128]{1,0:T(8,128)(2,1)S(1)} %reshape.216), channel_id=1, source_target_pairs={{0,8},{8,16},{16,24},{24,0},{1,9},{9,17},{17,25},{25,1},{2,10},{10... | collective-permute-start | bytes 196616 | tf_op jit(solution)/shard_map/ppermute | solution.py:24
  28.7 3.8 %project.19.refs_2_ = f32[1024,256]{1,0:T(8,128)S(1)} custom-call(s32[2]{0:T(128)S(1)} %pad_add_fusion.1.info, bf16[1024,8192]{1,0:T(8,128)(2,1)} %hidden.31, bf16[1024,256]{1,0:T(8,128)(2,1)} %collective-permute-done.8.refs_0_, f32[1024,256]{1,0:T(8,128)S(1)} %project.18.refs_1_), custom_call_target="tpu_custom_call", output_to_operand_aliasing={{}: (3, {})} | custom-call | flops 536870912 | bytes 4718592 | tf_op jit(solution)/shard_map/project/pallas_call | solution.py:90
  33.2 0.6 convert_reduce_fusion
  33.8 3.8 %project.20.refs_2_ = f32[1024,256]{1,0:T(8,128)S(1)} custom-call(s32[4]{0:T(128)S(1)} %add_add_fusion.1.info, bf16[1024,8192]{1,0:T(8,128)(2,1)} %hidden.31, bf16[1024,256]{1,0:T(8,128)(2,1)S(1)} %collective-permute-done.5.refs_0_, bf16[1024,256]{1,0:T(8,128)(2,1)} %collective-permute-done.6.refs_1_, ...), custom_call_target="tpu_custom_call", output_to_operand_aliasing={{}: (4, {})} | custom-call | flops 1073741824 | bytes 7340032 | tf_op jit(solution)/shard_map/project/pallas_call | solution.py:90
  37.7 3.4 %project.21.refs_1_ = f32[1024,256]{1,0:T(8,128)S(1)} custom-call(s32[4]{0:T(128)S(1)} %add_add_fusion.info, bf16[1024,8192]{1,0:T(8,128)(2,1)} %hidden.31, bf16[1024,256]{1,0:T(8,128)(2,1)S(1)} %collective-permute-done.9.refs_0_, bf16[1024,256]{1,0:T(8,128)(2,1)S(1)} %collective-permute-done.10.refs_1_, ...), custom_call_target="tpu_custom_call", output_to_operand_aliasing={{}: (4, {})} | custom-call | flops 1073741824 | bytes 7340032 | tf_op jit(solution)/shard_map/project/pallas_call | solution.py:90
  41.8 0.7 collective-permute-start.13
  42.5 1.3 collective-permute-start.14
  44.0 0.9 fusion.1.count
  44.9 3.4 %project.22.refs_2_ = f32[1024,256]{1,0:T(8,128)S(1)} custom-call(s32[4]{0:T(128)S(1)} %add_add_fusion.1.info, bf16[1024,8192]{1,0:T(8,128)(2,1)} %hidden.31, bf16[1024,256]{1,0:T(8,128)(2,1)S(1)} %collective-permute-done.3.refs_0_, bf16[1024,256]{1,0:T(8,128)(2,1)S(1)} %collective-permute-done.4.refs_1_, ...), custom_call_target="tpu_custom_call", output_to_operand_aliasing={{}: (4, {})} | custom-call | flops 1073741824 | bytes 7340032 | tf_op jit(solution)/shard_map/project/pallas_call | solution.py:90
  48.3 12.0 %collective-permute-start.1 = (bf16[256,128]{1,0:T(8,128)(2,1)S(1)}, bf16[256,128]{1,0:T(8,128)(2,1)}, u32[]{:S(2)}, u32[]{:S(2)}) collective-permute-start(bf16[256,128]{1,0:T(8,128)(2,1)S(1)} %reshape.216), channel_id=1, source_target_pairs={{0,16},{8,24},{16,0},{24,8},{1,17},{9,25},{17,1},{25,9},{2,18},{10... | collective-permute-start | bytes 196616 | tf_op jit(solution)/shard_map/ppermute | solution.py:24
  60.4 3.4 %project.23.refs_1_ = f32[1024,256]{1,0:T(8,128)S(1)} custom-call(s32[4]{0:T(128)S(1)} %add_add_fusion.info, bf16[1024,8192]{1,0:T(8,128)(2,1)} %hidden.31, bf16[1024,256]{1,0:T(8,128)(2,1)S(1)} %collective-permute-done.15.refs_0_, bf16[1024,256]{1,0:T(8,128)(2,1)S(1)} %collective-permute-done.16.refs_1_, ...), custom_call_target="tpu_custom_call", output_to_operand_aliasing={{}: (4, {})} | custom-call | flops 1073741824 | bytes 7340032 | tf_op jit(solution)/shard_map/project/pallas_call | solution.py:90
  63.8 0.7 collective-permute-done.14
  64.6 0.6 copy-done.9
  65.3 0.7 collective-permute-start.11
  66.0 1.3 collective-permute-start.12
  67.3 0.6 slice_multiply_fusion.1
  67.9 3.4 %project.24.refs_1_ = f32[1024,256]{1,0:T(8,128)S(1)} custom-call(s32[2]{0:T(128)S(1)} %pad_add_fusion.4.info, bf16[1024,8192]{1,0:T(8,128)(2,1)} %hidden.31, bf16[1024,256]{1,0:T(8,128)(2,1)S(1)} %broadcast_select_fusion.3.refs_0_, f32[1024,256]{1,0:T(8,128)S(1)} %project.21.refs_1_), custom_call_target="tpu_custom_call", output_to_operand_aliasing={{}: (3, {})} | custom-call | flops 536870912 | bytes 4718592 | tf_op jit(solution)/shard_map/project/pallas_call | solution.py:90
  71.3 3.8 %project.25.refs_1_ = f32[1024,256]{1,0:T(8,128)S(1)} custom-call(s32[2]{0:T(128)S(1)} %pad_add_fusion.3.info, bf16[1024,8192]{1,0:T(8,128)(2,1)} %hidden.31, bf16[1024,256]{1,0:T(8,128)(2,1)} %collective-permute-done.17.refs_0_, f32[1024,256]{1,0:T(8,128)S(1)} %project.24.refs_1_), custom_call_target="tpu_custom_call", output_to_operand_aliasing={{}: (3, {})} | custom-call | flops 536870912 | bytes 4718592 | tf_op jit(solution)/shard_map/project/pallas_call | solution.py:90
  75.1 9.4 %collective-permute-done.12 = bf16[1024,256]{1,0:T(8,128)(2,1)S(1)} collective-permute-done((bf16[1024,256]{1,0:T(8,128)(2,1)}, bf16[1024,256]{1,0:T(8,128)(2,1)S(1)}, u32[]{:S(2)}, u32[]{:S(2)}) %collective-permute-start.12) | collective-permute-done | bytes 524320 | tf_op jit(solution)/shard_map/ppermute | solution.py:288
  84.8 0.7 collective-permute-start.20
  85.5 1.3 collective-permute-start.21
  87.3 3.4 %project.26.refs_1_ = f32[1024,256]{1,0:T(8,128)S(1)} custom-call(s32[2]{0:T(128)S(1)} %pad_add_fusion.4.info, bf16[1024,8192]{1,0:T(8,128)(2,1)} %hidden.31, bf16[1024,256]{1,0:T(8,128)(2,1)S(1)} %broadcast_select_fusion.2.refs_0_, f32[1024,256]{1,0:T(8,128)S(1)} %project.23.refs_1_), custom_call_target="tpu_custom_call", output_to_operand_aliasing={{}: (3, {})} | custom-call | flops 536870912 | bytes 4718592 | tf_op jit(solution)/shard_map/project/pallas_call | solution.py:90
  90.7 3.4 %project.27.refs_1_ = f32[1024,256]{1,0:T(8,128)S(1)} custom-call(s32[2]{0:T(128)S(1)} %pad_add_fusion.3.info, bf16[1024,8192]{1,0:T(8,128)(2,1)} %hidden.31, bf16[1024,256]{1,0:T(8,128)(2,1)S(1)} %collective-permute-done.22.refs_0_, f32[1024,256]{1,0:T(8,128)S(1)} %project.26.refs_1_), custom_call_target="tpu_custom_call", output_to_operand_aliasing={{}: (3, {})} | custom-call | flops 536870912 | bytes 4718592 | tf_op jit(solution)/shard_map/project/pallas_call | solution.py:90
  94.0 7.6 %collective-permute-done.21 = bf16[1024,256]{1,0:T(8,128)(2,1)S(1)} collective-permute-done((bf16[1024,256]{1,0:T(8,128)(2,1)S(1)}, bf16[1024,256]{1,0:T(8,128)(2,1)S(1)}, u32[]{:S(2)}, u32[]{:S(2)}) %collective-permute-start.21) | collective-permute-done | bytes 524320 | tf_op jit(solution)/shard_map/ppermute | solution.py:288
  101.9 0.7 fusion.29
  102.6 1.4 collective-permute-start.18
  104.0 1.3 collective-permute-start.19
  105.3 3.4 %project.28.refs_1_ = f32[1024,256]{1,0:T(8,128)S(1)} custom-call(s32[2]{0:T(128)S(1)} %get-tuple-element.134.info, bf16[1024,8192]{1,0:T(8,128)(2,1)} %hidden.31, bf16[1024,256]{1,0:T(8,128)(2,1)S(1)} %broadcast_select_fusion.1.refs_0_, f32[1024,256]{1,0:T(8,128)S(1)} %project.25.refs_1_), custom_call_target="tpu_custom_call", output_to_operand_aliasing={{}: (3, {})} | custom-call | flops 536870912 | bytes 4718592 | tf_op jit(solution)/shard_map/project/pallas_call | solution.py:90
  108.7 3.4 %project.29 = f32[1024,256]{1,0:T(8,128)S(1)} custom-call(s32[2]{0:T(128)S(1)} %get-tuple-element.133.info, bf16[1024,8192]{1,0:T(8,128)(2,1)} %hidden.31, bf16[1024,256]{1,0:T(8,128)(2,1)S(1)} %collective-permute-done.23.refs_0_, f32[1024,256]{1,0:T(8,128)S(1)} %project.28.refs_1_), custom_call_target="tpu_custom_call", output_to_operand_aliasing={{}: (3, {})} | custom-call | flops 536870912 | bytes 4718592 | tf_op jit(solution)/shard_map/project/pallas_call | solution.py:90
  112.7 0.7 collective-permute-done.24
  113.5 2.1 %collective-permute-start.25 = (f32[1,256]{1,0:T(1,128)S(1)}, f32[1,256]{1,0:T(1,128)S(1)}, u32[]{:S(2)}, u32[]{:S(2)}) collective-permute-start(f32[1,256]{1,0:T(1,128)S(1)} %max.106), channel_id=1, source_target_pairs={{0,8},{8,16},{16,24},{24,0},{1,9},{9,17},{17,25},{25,1},{2,10},{10... | collective-permute-start | bytes 3080 | tf_op jit(solution)/shard_map/ppermute | solution.py:24
  115.6 6.2 %collective-permute-done.2 = bf16[256,128]{1,0:T(8,128)(2,1)S(1)} collective-permute-done((bf16[256,128]{1,0:T(8,128)(2,1)S(1)}, bf16[256,128]{1,0:T(8,128)(2,1)S(1)}, u32[]{:S(2)}, u32[]{:S(2)}) %collective-permute-start.2) | collective-permute-done | bytes 65568 | tf_op jit(solution)/shard_map/ppermute | solution.py:24
  121.8 1.6 pad_maximum_fusion.1.query
  123.4 2.0 %collective-permute-done.27 = f32[1,256]{1,0:T(1,128)S(1)} collective-permute-done((f32[1,256]{1,0:T(1,128)S(1)}, f32[1,256]{1,0:T(1,128)S(1)}, u32[]{:S(2)}, u32[]{:S(2)}) %collective-permute-start.27) | collective-permute-done | bytes 1056 | tf_op jit(solution)/shard_map/ppermute | solution.py:24
  126.1 0.6 reshape.220
  126.7 1.1 broadcast_select_fusion.refs_0_
  127.9 0.8 minimum_convert_fusion.1
  128.7 0.7 broadcast_select_fusion.5
  130.0 0.9 convolution_bitcast_fusion
  130.9 3.4 %project.30.refs_1_ = f32[1024,256]{1,0:T(8,128)S(1)} custom-call(s32[2]{0:T(128)S(1)} %get-tuple-element.134.info, bf16[1024,8192]{1,0:T(8,128)(2,1)} %hidden.31, bf16[1024,256]{1,0:T(8,128)(2,1)S(1)} %broadcast_select_fusion.refs_0_, f32[1024,256]{1,0:T(8,128)S(1)} %project.27.refs_1_), custom_call_target="tpu_custom_call", output_to_operand_aliasing={{}: (3, {})} | custom-call | flops 536870912 | bytes 4718592 | tf_op jit(solution)/shard_map/project/pallas_call | solution.py:90
  134.3 0.9 fusion.46
  135.2 3.4 %project.31 = f32[1024,256]{1,0:T(8,128)S(1)} custom-call(s32[2]{0:T(128)S(1)} %get-tuple-element.133.info, bf16[1024,8192]{1,0:T(8,128)(2,1)} %hidden.31, bf16[1024,256]{1,0:T(8,128)(2,1)S(1)} %collective-permute-done.29.refs_0_, f32[1024,256]{1,0:T(8,128)S(1)} %project.30.refs_1_), custom_call_target="tpu_custom_call", output_to_operand_aliasing={{}: (3, {})} | custom-call | flops 536870912 | bytes 4718592 | tf_op jit(solution)/shard_map/project/pallas_call | solution.py:90
  138.8 5.9 %score.1 = (bf16[4,256,2048]{2,1,0:T(8,128)(2,1)S(1)}, f32[2,256]{1,0:T(2,128)S(1)}, f32[2,256]{1,0:T(2,128)S(1)}, f32[2,256]{1,0:T(2,128)S(1)}, f32[2,256]{1,0:T(2,128)S(1)}) custom-call(s32[4]{0:T(128)S(1)} %pad_add_fusion.2.group, bf16[4,256,128]{2,1,0:T(8,128)(2,1)S(1)} %copy-done.4, f32[1,128]{1,0:T(1,128)S(1)} %broadcast_select_fusion.11.smooth, ...), custom_call_target="tpu_custom_call" | custom-call | flops 536870912 | bytes 4194304 | tf_op jit(solution)/shard_map/score/pallas_call | solution.py:161
  144.7 1.8 %collective-permute-start.34 = (f32[2,256]{1,0:T(2,128)S(1)}, f32[2,256]{1,0:T(2,128)S(1)}, u32[]{:S(2)}, u32[]{:S(2)}) collective-permute-start(f32[2,256]{1,0:T(2,128)S(1)} %get-tuple-element.76), channel_id=1, source_target_pairs={{0,24},{8,0},{16,8},{24,16},{1,25},{9,1},{17,9},{25,17},{2,26},{10... | collective-permute-start | bytes 6152 | tf_op jit(solution)/shard_map/ppermute | solution.py:24
  146.6 0.6 collective-permute-start.36
  147.4 0.9 collective-permute-done.34
  148.4 2.7 %collective-permute-done.35 = f32[2,256]{1,0:T(2,128)S(1)} collective-permute-done((f32[2,256]{1,0:T(2,128)S(1)}, f32[2,256]{1,0:T(2,128)S(1)}, u32[]{:S(2)}, u32[]{:S(2)}) %collective-permute-start.35) | collective-permute-done | bytes 2080 | tf_op jit(solution)/shard_map/ppermute | solution.py:24
  151.1 0.9 collective-permute-done.36
  152.1 1.8 %weigh.1 = (bf16[256,128]{1,0:T(8,128)(2,1)S(1)}, bf16[256,128]{1,0:T(8,128)(2,1)S(1)}, bf16[256,128]{1,0:T(8,128)(2,1)S(1)}, bf16[256,128]{1,0:T(8,128)(2,1)S(1)}) custom-call(bf16[4,256,2048]{2,1,0:T(8,128)(2,1)S(1)} %get-tuple-element.68.probs, bf16[1024,128]{1,0:T(8,128)(2,1)S(1)} %get-tuple-element.105.refs_0_, ...), custom_call_target="tpu_custom_call" | custom-call | flops 536870912 | bytes 4194304 | tf_op jit(solution)/shard_map/weigh/pallas_call | solution.py:215
  153.9 0.8 collective-permute-start.31
  155.1 1.9 %collective-permute-start.33 = (bf16[256,128]{1,0:T(8,128)(2,1)S(1)}, bf16[256,128]{1,0:T(8,128)(2,1)S(1)}, u32[]{:S(2)}, u32[]{:S(2)}) collective-permute-start(bf16[256,128]{1,0:T(8,128)(2,1)S(1)} %get-tuple-element.73), channel_id=1, source_target_pairs={{0,8},{8,16},{16,24},{24,0},{1,9},{9,17},{17,25},{25,1},{2,10},{10... | collective-permute-start | bytes 196616 | tf_op jit(solution)/shard_map/ppermute | solution.py:24
  157.1 1.8 %collective-permute-done.31 = bf16[256,128]{1,0:T(8,128)(2,1)S(1)} collective-permute-done((bf16[256,128]{1,0:T(8,128)(2,1)S(1)}, bf16[256,128]{1,0:T(8,128)(2,1)S(1)}, u32[]{:S(2)}, u32[]{:S(2)}) %collective-permute-start.31) | collective-permute-done | bytes 65568 | tf_op jit(solution)/shard_map/ppermute | solution.py:24
  158.8 2.9 %collective-permute-done.32 = bf16[256,128]{1,0:T(8,128)(2,1)S(1)} collective-permute-done((bf16[256,128]{1,0:T(8,128)(2,1)S(1)}, bf16[256,128]{1,0:T(8,128)(2,1)S(1)}, u32[]{:S(2)}, u32[]{:S(2)}) %collective-permute-start.32) | collective-permute-done | bytes 65568 | tf_op jit(solution)/shard_map/ppermute | solution.py:24
  162.1 2.0 %copy.60 = bf16[1024,2,256]{2,1,0:T(2,128)(2,1)} copy(bf16[1024,2,256]{2,0,1:T(8,128)(2,1)S(1)} %pad_maximum_fusion) | data formatting | bytes 2097152
  164.2 0.7 pad_maximum_fusion.2
  (134 shorter events, 7.2 us)
Async XLA Ops:
  0.6 20.2 %collective-permute-start.7 = (bf16[1024,256]{1,0:T(8,128)(2,1)}, bf16[1024,256]{1,0:T(8,128)(2,1)}, u32[]{:S(2)}, u32[]{:S(2)}) collective-permute-start(bf16[1024,256]{1,0:T(8,128)(2,1)} %refs_0_.2), channel_id=1, source_target_pairs={{0,1},{1,0},{2,3},{3,2},{4,5},{5,4},{6,7},{7,6},{8,9},{9,8},{10,11... | collective-permute-start | bytes 1572872 | tf_op jit(solution)/shard_map/ppermute | solution.py:24
  1.2 31.3 %collective-permute-start.5 = (bf16[1024,256]{1,0:T(8,128)(2,1)}, bf16[1024,256]{1,0:T(8,128)(2,1)S(1)}, u32[]{:S(2)}, u32[]{:S(2)}) collective-permute-start(bf16[1024,256]{1,0:T(8,128)(2,1)} %refs_0_.2), channel_id=1, source_target_pairs={{0,8},{8,16},{16,24},{1,9},{9,17},{17,25},{2,10},{10,18},{18,26},{... | collective-permute-start | bytes 1572872 | tf_op jit(solution)/shard_map/ppermute | solution.py:287
  5.7 26.8 %collective-permute-start.6 = (bf16[1024,256]{1,0:T(8,128)(2,1)}, bf16[1024,256]{1,0:T(8,128)(2,1)}, u32[]{:S(2)}, u32[]{:S(2)}) collective-permute-start(bf16[1024,256]{1,0:T(8,128)(2,1)} %refs_0_.2), channel_id=1, source_target_pairs={{8,0},{16,8},{24,16},{9,1},{17,9},{25,17},{10,2},{18,10},{26,18},{... | collective-permute-start | bytes 1572872 | tf_op jit(solution)/shard_map/ppermute | solution.py:288
  7.0 18.9 %collective-permute-start.8 = (bf16[1024,256]{1,0:T(8,128)(2,1)}, bf16[1024,256]{1,0:T(8,128)(2,1)}, u32[]{:S(2)}, u32[]{:S(2)}) collective-permute-start(bf16[1024,256]{1,0:T(8,128)(2,1)} %refs_0_.3), channel_id=1, source_target_pairs={{0,1},{1,0},{2,3},{3,2},{4,5},{5,4},{6,7},{7,6},{8,9},{9,8},{10,11... | collective-permute-start | bytes 1572872 | tf_op jit(solution)/shard_map/ppermute | solution.py:24
  7.3 33.8 %collective-permute-start.3 = (bf16[1024,256]{1,0:T(8,128)(2,1)}, bf16[1024,256]{1,0:T(8,128)(2,1)S(1)}, u32[]{:S(2)}, u32[]{:S(2)}) collective-permute-start(bf16[1024,256]{1,0:T(8,128)(2,1)} %refs_0_.3), channel_id=1, source_target_pairs={{0,8},{8,16},{16,24},{1,9},{9,17},{17,25},{2,10},{10,18},{18,26},{... | collective-permute-start | bytes 1572872 | tf_op jit(solution)/shard_map/ppermute | solution.py:287
  12.9 1.0 copy-start.1
  13.9 3.4 %copy-start.2 = (bf16[1024,256]{1,0:T(8,128)(2,1)S(1)}, bf16[1024,256]{1,0:T(8,128)(2,1)}, u32[]{:S(2)}) copy-start(bf16[1024,256]{1,0:T(8,128)(2,1)} %refs_0_.3) | copy-start | bytes 1572868
  13.9 6.9 %copy-start.19 = (s32[32]{0:T(128)S(1)}, s32[32]{0:T(128)}, u32[]{:S(2)}) copy-start(s32[32]{0:T(128)} %param.15) | copy-start | bytes 388
  20.8 12.4 %copy-start.13 = (s32[32,32]{1,0:T(8,128)S(1)}, s32[32,32]{1,0:T(8,128)}, u32[]{:S(2)}) copy-start(s32[32,32]{1,0:T(8,128)} %param.14) | copy-start | bytes 12292
  20.8 20.3 %collective-permute-start.4 = (bf16[1024,256]{1,0:T(8,128)(2,1)}, bf16[1024,256]{1,0:T(8,128)(2,1)S(1)}, u32[]{:S(2)}, u32[]{:S(2)}) collective-permute-start(bf16[1024,256]{1,0:T(8,128)(2,1)} %refs_0_.3), channel_id=1, source_target_pairs={{8,0},{16,8},{24,16},{9,1},{17,9},{25,17},{10,2},{18,10},{26,18},{... | collective-permute-start | bytes 1572872 | tf_op jit(solution)/shard_map/ppermute | solution.py:288
  26.0 87.6 %collective-permute-start = (bf16[256,128]{1,0:T(8,128)(2,1)S(1)}, bf16[256,128]{1,0:T(8,128)(2,1)S(1)}, u32[]{:S(2)}, u32[]{:S(2)}) collective-permute-start(bf16[256,128]{1,0:T(8,128)(2,1)S(1)} %reshape.216), channel_id=1, source_target_pairs={{0,8},{8,16},{16,24},{24,0},{1,9},{9,17},{17,25},{25,1},{2,10},{10... | collective-permute-start | bytes 196616 | tf_op jit(solution)/shard_map/ppermute | solution.py:24
  32.5 5.2 %collective-permute-start.10 = (bf16[1024,256]{1,0:T(8,128)(2,1)}, bf16[1024,256]{1,0:T(8,128)(2,1)S(1)}, u32[]{:S(2)}, u32[]{:S(2)}) collective-permute-start(bf16[1024,256]{1,0:T(8,128)(2,1)} %collective-permute-done.6.refs_1_), channel_id=1, source_target_pairs={{0,1},{1,0},{2,3},{3,2},{4,5},{5,4},{6,7},{7,6},{8,9},{9,8},{10,11... | collective-permute-start | bytes 1572872 | tf_op jit(solution)/shard_map/ppermute | solution.py:24
  32.6 5.1 %collective-permute-start.9 = (bf16[1024,256]{1,0:T(8,128)(2,1)S(1)}, bf16[1024,256]{1,0:T(8,128)(2,1)S(1)}, u32[]{:S(2)}, u32[]{:S(2)}) collective-permute-start(bf16[1024,256]{1,0:T(8,128)(2,1)S(1)} %collective-permute-done.5.refs_0_), channel_id=1, source_target_pairs={{0,1},{1,0},{2,3},{3,2},{4,5},{5,4},{6,7},{7,6},{8,9},{9,8},{10,11... | collective-permute-start | bytes 1572872 | tf_op jit(solution)/shard_map/ppermute | solution.py:24
  41.1 22.7 %copy-start = (bf16[1024,256]{1,0:T(8,128)(2,1)}, bf16[1024,256]{1,0:T(8,128)(2,1)S(1)}, u32[]{:S(2)}) copy-start(bf16[1024,256]{1,0:T(8,128)(2,1)S(1)} %collective-permute-done.4.refs_1_) | copy-start | bytes 1572868
  41.1 7.2 %collective-permute-start.15 = (bf16[1024,256]{1,0:T(8,128)(2,1)S(1)}, bf16[1024,256]{1,0:T(8,128)(2,1)S(1)}, u32[]{:S(2)}, u32[]{:S(2)}) collective-permute-start(bf16[1024,256]{1,0:T(8,128)(2,1)S(1)} %collective-permute-done.3.refs_0_), channel_id=1, source_target_pairs={{0,1},{1,0},{2,3},{3,2},{4,5},{5,4},{6,7},{7,6},{8,9},{9,8},{10,11... | collective-permute-start | bytes 1572872 | tf_op jit(solution)/shard_map/ppermute | solution.py:24
  41.3 19.1 %collective-permute-start.16 = (bf16[1024,256]{1,0:T(8,128)(2,1)S(1)}, bf16[1024,256]{1,0:T(8,128)(2,1)S(1)}, u32[]{:S(2)}, u32[]{:S(2)}) collective-permute-start(bf16[1024,256]{1,0:T(8,128)(2,1)S(1)} %collective-permute-done.4.refs_1_), channel_id=1, source_target_pairs={{0,1},{1,0},{2,3},{3,2},{4,5},{5,4},{6,7},{7,6},{8,9},{9,8},{10,11... | collective-permute-start | bytes 1572872 | tf_op jit(solution)/shard_map/ppermute | solution.py:24
  41.8 22.0 %collective-permute-start.13 = (bf16[1024,256]{1,0:T(8,128)(2,1)S(1)}, bf16[1024,256]{1,0:T(8,128)(2,1)S(1)}, u32[]{:S(2)}, u32[]{:S(2)}) collective-permute-start(bf16[1024,256]{1,0:T(8,128)(2,1)S(1)} %collective-permute-done.5.refs_0_), channel_id=1, source_target_pairs={{8,16},{16,24},{9,17},{17,25},{10,18},{18,26},{11,19},{19,27},{12,... | collective-permute-start | bytes 1572872 | tf_op jit(solution)/shard_map/ppermute | solution.py:287
  42.5 22.0 %collective-permute-start.14 = (bf16[1024,256]{1,0:T(8,128)(2,1)}, bf16[1024,256]{1,0:T(8,128)(2,1)S(1)}, u32[]{:S(2)}, u32[]{:S(2)}) collective-permute-start(bf16[1024,256]{1,0:T(8,128)(2,1)} %collective-permute-done.6.refs_1_), channel_id=1, source_target_pairs={{8,0},{16,8},{9,1},{17,9},{10,2},{18,10},{11,3},{19,11},{12,4},{20... | collective-permute-start | bytes 1572872 | tf_op jit(solution)/shard_map/ppermute | solution.py:288
  44.9 22.4 %copy-start.16 = (f32[2,256]{1,0:T(2,128)S(1)}, f32[2,256]{1,0:T(2,128)}, u32[]{:S(2)}) copy-start(f32[2,256]{1,0:T(2,128)} %param.11) | copy-start | bytes 6148
  48.3 67.3 %collective-permute-start.1 = (bf16[256,128]{1,0:T(8,128)(2,1)S(1)}, bf16[256,128]{1,0:T(8,128)(2,1)}, u32[]{:S(2)}, u32[]{:S(2)}) collective-permute-start(bf16[256,128]{1,0:T(8,128)(2,1)S(1)} %reshape.216), channel_id=1, source_target_pairs={{0,16},{8,24},{16,0},{24,8},{1,17},{9,25},{17,1},{25,9},{2,18},{10... | collective-permute-start | bytes 196616 | tf_op jit(solution)/shard_map/ppermute | solution.py:24
  63.8 0.8 copy-start.7
  64.5 0.8 copy-start.9
  64.5 6.8 %collective-permute-start.17 = (bf16[1024,256]{1,0:T(8,128)(2,1)S(1)}, bf16[1024,256]{1,0:T(8,128)(2,1)}, u32[]{:S(2)}, u32[]{:S(2)}) collective-permute-start(bf16[1024,256]{1,0:T(8,128)(2,1)S(1)} %broadcast_select_fusion.3.refs_0_), channel_id=1, source_target_pairs={{0,1},{1,0},{2,3},{3,2},{4,5},{5,4},{6,7},{7,6},{8,9},{9,8},{10,11... | collective-permute-start | bytes 1572872 | tf_op jit(solution)/shard_map/ppermute | solution.py:24
  65.3 9.8 %collective-permute-start.11 = (bf16[1024,256]{1,0:T(8,128)(2,1)S(1)}, bf16[1024,256]{1,0:T(8,128)(2,1)S(1)}, u32[]{:S(2)}, u32[]{:S(2)}) collective-permute-start(bf16[1024,256]{1,0:T(8,128)(2,1)S(1)} %collective-permute-done.3.refs_0_), channel_id=1, source_target_pairs={{8,16},{16,24},{9,17},{17,25},{10,18},{18,26},{11,19},{19,27},{12,... | collective-permute-start | bytes 1572872 | tf_op jit(solution)/shard_map/ppermute | solution.py:287
  66.0 18.5 %collective-permute-start.12 = (bf16[1024,256]{1,0:T(8,128)(2,1)}, bf16[1024,256]{1,0:T(8,128)(2,1)S(1)}, u32[]{:S(2)}, u32[]{:S(2)}) collective-permute-start(bf16[1024,256]{1,0:T(8,128)(2,1)} %copy-done), channel_id=1, source_target_pairs={{8,0},{16,8},{9,1},{17,9},{10,2},{18,10},{11,3},{19,11},{12,4},{20... | collective-permute-start | bytes 1572872 | tf_op jit(solution)/shard_map/ppermute | solution.py:288
  67.9 16.8 %copy-start.8 = (bf16[1024,256]{1,0:T(8,128)(2,1)S(1)}, bf16[1024,256]{1,0:T(8,128)(2,1)}, u32[]{:S(2)}) copy-start(bf16[1024,256]{1,0:T(8,128)(2,1)} %copy-done.7) | copy-start | bytes 1572868
  67.9 17.5 %copy-start.10 = (bf16[1024,256]{1,0:T(8,128)(2,1)S(1)}, bf16[1024,256]{1,0:T(8,128)(2,1)}, u32[]{:S(2)}) copy-start(bf16[1024,256]{1,0:T(8,128)(2,1)} %copy-done.9) | copy-start | bytes 1572868
  67.9 19.3 %copy-start.11 = (bf16[4,8,2,256]{3,2,1,0:T(2,128)(2,1)S(1)}, bf16[4,8,2,256]{3,2,1,0:T(2,128)(2,1)}, u32[]{:S(2)}) copy-start(bf16[4,8,2,256]{3,2,1,0:T(2,128)(2,1)} %param.12) | copy-start | bytes 98308
  75.1 9.4 %copy-start.5 = (bf16[1024,256]{1,0:T(8,128)(2,1)}, bf16[1024,256]{1,0:T(8,128)(2,1)S(1)}, u32[]{:S(2)}) copy-start(bf16[1024,256]{1,0:T(8,128)(2,1)S(1)} %collective-permute-done.11) | copy-start | bytes 1572868
  84.5 9.5 %copy-start.6 = (bf16[1024,256]{1,0:T(8,128)(2,1)}, bf16[1024,256]{1,0:T(8,128)(2,1)S(1)}, u32[]{:S(2)}) copy-start(bf16[1024,256]{1,0:T(8,128)(2,1)S(1)} %collective-permute-done.12) | copy-start | bytes 1572868
  84.6 6.1 %collective-permute-start.22 = (bf16[1024,256]{1,0:T(8,128)(2,1)S(1)}, bf16[1024,256]{1,0:T(8,128)(2,1)S(1)}, u32[]{:S(2)}, u32[]{:S(2)}) collective-permute-start(bf16[1024,256]{1,0:T(8,128)(2,1)S(1)} %broadcast_select_fusion.2.refs_0_), channel_id=1, source_target_pairs={{0,1},{1,0},{2,3},{3,2},{4,5},{5,4},{6,7},{7,6},{8,9},{9,8},{10,11... | collective-permute-start | bytes 1572872 | tf_op jit(solution)/shard_map/ppermute | solution.py:24
  84.8 9.3 %collective-permute-start.20 = (bf16[1024,256]{1,0:T(8,128)(2,1)S(1)}, bf16[1024,256]{1,0:T(8,128)(2,1)S(1)}, u32[]{:S(2)}, u32[]{:S(2)}) collective-permute-start(bf16[1024,256]{1,0:T(8,128)(2,1)S(1)} %copy-done.8), channel_id=1, source_target_pairs={{16,24},{17,25},{18,26},{19,27},{20,28},{21,29},{22,30},{23,31}} | collective-permute-start | bytes 1572872 | tf_op jit(solution)/shard_map/ppermute | solution.py:287
  85.5 16.2 %collective-permute-start.21 = (bf16[1024,256]{1,0:T(8,128)(2,1)S(1)}, bf16[1024,256]{1,0:T(8,128)(2,1)S(1)}, u32[]{:S(2)}, u32[]{:S(2)}) collective-permute-start(bf16[1024,256]{1,0:T(8,128)(2,1)S(1)} %copy-done.10), channel_id=1, source_target_pairs={{8,0},{9,1},{10,2},{11,3},{12,4},{13,5},{14,6},{15,7}} | collective-permute-start | bytes 1572872 | tf_op jit(solution)/shard_map/ppermute | solution.py:288
  101.7 7.0 %collective-permute-start.23 = (bf16[1024,256]{1,0:T(8,128)(2,1)S(1)}, bf16[1024,256]{1,0:T(8,128)(2,1)S(1)}, u32[]{:S(2)}, u32[]{:S(2)}) collective-permute-start(bf16[1024,256]{1,0:T(8,128)(2,1)S(1)} %broadcast_select_fusion.1.refs_0_), channel_id=1, source_target_pairs={{0,1},{1,0},{2,3},{3,2},{4,5},{5,4},{6,7},{7,6},{8,9},{9,8},{10,11... | collective-permute-start | bytes 1572872 | tf_op jit(solution)/shard_map/ppermute | solution.py:24
  101.8 24.1 %copy-start.18 = (pred[4,4]{1,0:T(4,128)(4,1)}, pred[4,4]{1,0:T(4,128)(4,1)S(1)}, u32[]{:S(2)}) copy-start(pred[4,4]{1,0:T(4,128)(4,1)S(1)} %iota_compare_fusion.5) | copy-start | bytes 52
  102.6 22.8 %collective-permute-start.18 = (bf16[1024,256]{1,0:T(8,128)(2,1)}, bf16[1024,256]{1,0:T(8,128)(2,1)}, u32[]{:S(2)}, u32[]{:S(2)}) collective-permute-start(bf16[1024,256]{1,0:T(8,128)(2,1)} %copy-done.5), channel_id=1, source_target_pairs={{16,24},{17,25},{18,26},{19,27},{20,28},{21,29},{22,30},{23,31}} | collective-permute-start | bytes 1572872 | tf_op jit(solution)/shard_map/ppermute | solution.py:287
  104.0 21.4 %collective-permute-start.19 = (bf16[1024,256]{1,0:T(8,128)(2,1)}, bf16[1024,256]{1,0:T(8,128)(2,1)}, u32[]{:S(2)}, u32[]{:S(2)}) collective-permute-start(bf16[1024,256]{1,0:T(8,128)(2,1)} %copy-done.6), channel_id=1, source_target_pairs={{8,0},{9,1},{10,2},{11,3},{12,4},{13,5},{14,6},{15,7}} | collective-permute-start | bytes 1572872 | tf_op jit(solution)/shard_map/ppermute | solution.py:288
  112.1 1.3 collective-permute-start.24
  113.4 8.4 %collective-permute-start.2 = (bf16[256,128]{1,0:T(8,128)(2,1)S(1)}, bf16[256,128]{1,0:T(8,128)(2,1)S(1)}, u32[]{:S(2)}, u32[]{:S(2)}) collective-permute-start(bf16[256,128]{1,0:T(8,128)(2,1)S(1)} %reshape.216), channel_id=1, source_target_pairs={{0,24},{8,0},{16,8},{24,16},{1,25},{9,1},{17,9},{25,17},{2,26},{10... | collective-permute-start | bytes 196616 | tf_op jit(solution)/shard_map/ppermute | solution.py:24
  113.5 9.9 %collective-permute-start.25 = (f32[1,256]{1,0:T(1,128)S(1)}, f32[1,256]{1,0:T(1,128)S(1)}, u32[]{:S(2)}, u32[]{:S(2)}) collective-permute-start(f32[1,256]{1,0:T(1,128)S(1)} %max.106), channel_id=1, source_target_pairs={{0,8},{8,16},{16,24},{24,0},{1,9},{9,17},{17,25},{25,1},{2,10},{10... | collective-permute-start | bytes 3080 | tf_op jit(solution)/shard_map/ppermute | solution.py:24
  115.6 7.8 %collective-permute-start.26 = (f32[1,256]{1,0:T(1,128)S(1)}, f32[1,256]{1,0:T(1,128)S(1)}, u32[]{:S(2)}, u32[]{:S(2)}) collective-permute-start(f32[1,256]{1,0:T(1,128)S(1)} %max.106), channel_id=1, source_target_pairs={{0,16},{8,24},{16,0},{24,8},{1,17},{9,25},{17,1},{25,9},{2,18},{10... | collective-permute-start | bytes 3080 | tf_op jit(solution)/shard_map/ppermute | solution.py:24
  121.8 3.6 %collective-permute-start.27 = (f32[1,256]{1,0:T(1,128)S(1)}, f32[1,256]{1,0:T(1,128)S(1)}, u32[]{:S(2)}, u32[]{:S(2)}) collective-permute-start(f32[1,256]{1,0:T(1,128)S(1)} %max.106), channel_id=1, source_target_pairs={{0,24},{8,0},{16,8},{24,16},{1,25},{9,1},{17,9},{25,17},{2,26},{10... | collective-permute-start | bytes 3080 | tf_op jit(solution)/shard_map/ppermute | solution.py:24
  125.4 13.1 %copy-start.12 = (f32[1,256]{1,0:T(1,128)}, f32[1,256]{1,0:T(1,128)S(1)}, u32[]{:S(2)}) copy-start(f32[1,256]{1,0:T(1,128)S(1)} %add_sqrt_fusion) | copy-start | bytes 3076
  127.8 7.4 %collective-permute-start.29 = (bf16[1024,256]{1,0:T(8,128)(2,1)S(1)}, bf16[1024,256]{1,0:T(8,128)(2,1)S(1)}, u32[]{:S(2)}, u32[]{:S(2)}) collective-permute-start(bf16[1024,256]{1,0:T(8,128)(2,1)S(1)} %broadcast_select_fusion.refs_0_), channel_id=1, source_target_pairs={{0,1},{1,0},{2,3},{3,2},{4,5},{5,4},{6,7},{7,6},{8,9},{9,8},{10,11... | collective-permute-start | bytes 1572872 | tf_op jit(solution)/shard_map/ppermute | solution.py:24
  129.4 9.2 %collective-permute-start.28 = (bf16[1024,128]{1,0:T(8,128)(2,1)}, bf16[1024,128]{1,0:T(8,128)(2,1)}, u32[]{:S(2)}, u32[]{:S(2)}) collective-permute-start(bf16[1024,128]{1,0:T(8,128)(2,1)} %get-tuple-element.106), channel_id=1, source_target_pairs={{0,1},{1,0},{2,3},{3,2},{4,5},{5,4},{6,7},{7,6},{8,9},{9,8},{10,11... | collective-permute-start | bytes 786440 | tf_op jit(solution)/shard_map/ppermute | solution.py:24
  130.9 7.7 %copy-start.14 = (f32[1,256]{1,0:T(1,128)S(1)}, f32[1,256]{1,0:T(1,128)}, u32[]{:S(2)}) copy-start(f32[1,256]{1,0:T(1,128)} %get-tuple-element.119) | copy-start | bytes 3076
  130.9 7.7 %copy-start.15 = (f32[1,256]{1,0:T(1,128)S(1)}, f32[1,256]{1,0:T(1,128)}, u32[]{:S(2)}) copy-start(f32[1,256]{1,0:T(1,128)} %get-tuple-element.121) | copy-start | bytes 3076
  134.3 4.5 %copy-start.3 = (f32[4,8,2048]{2,1,0:T(8,128)S(1)}, f32[4,8,2048]{2,1,0:T(8,128)}, u32[]{:S(2)}) copy-start(f32[4,8,2048]{2,1,0:T(8,128)} %fusion.1.count) | copy-start | bytes 786436
  134.3 4.5 %copy-start.4 = (bf16[4,256,128]{2,1,0:T(8,128)(2,1)S(1)}, bf16[4,256,128]{2,1,0:T(8,128)(2,1)}, u32[]{:S(2)}) copy-start(bf16[4,256,128]{2,1,0:T(8,128)(2,1)} %pad_maximum_fusion.1.query) | copy-start | bytes 786436
  134.3 17.7 %copy-start.17 = (f32[256]{0:T(256)S(1)}, f32[256]{0:T(256)}, u32[]{:S(2)}) copy-start(f32[256]{0:T(256)} %reshape.220) | copy-start | bytes 3076
  144.7 3.6 %collective-permute-start.34 = (f32[2,256]{1,0:T(2,128)S(1)}, f32[2,256]{1,0:T(2,128)S(1)}, u32[]{:S(2)}, u32[]{:S(2)}) collective-permute-start(f32[2,256]{1,0:T(2,128)S(1)} %get-tuple-element.76), channel_id=1, source_target_pairs={{0,24},{8,0},{16,8},{24,16},{1,25},{9,1},{17,9},{25,17},{2,26},{10... | collective-permute-start | bytes 6152 | tf_op jit(solution)/shard_map/ppermute | solution.py:24
  146.6 4.5 %collective-permute-start.35 = (f32[2,256]{1,0:T(2,128)S(1)}, f32[2,256]{1,0:T(2,128)S(1)}, u32[]{:S(2)}, u32[]{:S(2)}) collective-permute-start(f32[2,256]{1,0:T(2,128)S(1)} %get-tuple-element.77), channel_id=1, source_target_pairs={{0,16},{8,24},{16,0},{24,8},{1,17},{9,25},{17,1},{25,9},{2,18},{10... | collective-permute-start | bytes 6152 | tf_op jit(solution)/shard_map/ppermute | solution.py:24
  146.6 5.4 %collective-permute-start.36 = (f32[2,256]{1,0:T(2,128)S(1)}, f32[2,256]{1,0:T(2,128)S(1)}, u32[]{:S(2)}, u32[]{:S(2)}) collective-permute-start(f32[2,256]{1,0:T(2,128)S(1)} %get-tuple-element.78), channel_id=1, source_target_pairs={{0,8},{8,16},{16,24},{24,0},{1,9},{9,17},{17,25},{25,1},{2,10},{10... | collective-permute-start | bytes 6152 | tf_op jit(solution)/shard_map/ppermute | solution.py:24
  147.3 4.8 %collective-permute-start.30 = (bf16[1024,128]{1,0:T(8,128)(2,1)S(1)}, bf16[1024,128]{1,0:T(8,128)(2,1)S(1)}, u32[]{:S(2)}, u32[]{:S(2)}) collective-permute-start(bf16[1024,128]{1,0:T(8,128)(2,1)S(1)} %get-tuple-element.104), channel_id=1, source_target_pairs={{0,1},{1,0},{2,3},{3,2},{4,5},{5,4},{6,7},{7,6},{8,9},{9,8},{10,11... | collective-permute-start | bytes 786440 | tf_op jit(solution)/shard_map/ppermute | solution.py:24
  153.9 5.0 %collective-permute-start.31 = (bf16[256,128]{1,0:T(8,128)(2,1)S(1)}, bf16[256,128]{1,0:T(8,128)(2,1)S(1)}, u32[]{:S(2)}, u32[]{:S(2)}) collective-permute-start(bf16[256,128]{1,0:T(8,128)(2,1)S(1)} %get-tuple-element.71), channel_id=1, source_target_pairs={{0,24},{8,0},{16,8},{24,16},{1,25},{9,1},{17,9},{25,17},{2,26},{10... | collective-permute-start | bytes 196616 | tf_op jit(solution)/shard_map/ppermute | solution.py:24
  154.7 7.1 %collective-permute-start.32 = (bf16[256,128]{1,0:T(8,128)(2,1)S(1)}, bf16[256,128]{1,0:T(8,128)(2,1)S(1)}, u32[]{:S(2)}, u32[]{:S(2)}) collective-permute-start(bf16[256,128]{1,0:T(8,128)(2,1)S(1)} %get-tuple-element.72), channel_id=1, source_target_pairs={{0,16},{8,24},{16,0},{24,8},{1,17},{9,25},{17,1},{25,9},{2,18},{10... | collective-permute-start | bytes 196616 | tf_op jit(solution)/shard_map/ppermute | solution.py:24
  155.1 6.6 %collective-permute-start.33 = (bf16[256,128]{1,0:T(8,128)(2,1)S(1)}, bf16[256,128]{1,0:T(8,128)(2,1)S(1)}, u32[]{:S(2)}, u32[]{:S(2)}) collective-permute-start(bf16[256,128]{1,0:T(8,128)(2,1)S(1)} %get-tuple-element.73), channel_id=1, source_target_pairs={{0,8},{8,16},{16,24},{24,0},{1,9},{9,17},{17,25},{25,1},{2,10},{10... | collective-permute-start | bytes 196616 | tf_op jit(solution)/shard_map/ppermute | solution.py:24
  162.1 2.1 %collective-permute-start.37 = (bf16[4,8,1024]{2,1,0:T(8,128)(2,1)S(1)}, bf16[4,8,1024]{2,1,0:T(8,128)(2,1)S(1)}, u32[]{:S(2)}, u32[]{:S(2)}) collective-permute-start(bf16[4,8,1024]{2,1,0:T(8,128)(2,1)S(1)} %reshape.221), channel_id=1, source_target_pairs={{0,1},{1,0},{2,3},{3,2},{4,5},{5,4},{6,7},{7,6},{8,9},{9,8},{10,11... | collective-permute-start | bytes 196616 | tf_op jit(solution)/shard_map/ppermute | solution.py:24

commit v4 on v3

v4 whole, which is shorter than its diff:
```python
import functools

import jax
import jax.numpy as jnp
from jax import lax
from jax.experimental import pallas as pl
from jax.experimental.pallas import tpu as pltpu
from jax.sharding import PartitionSpec as P


KVH = 8
HD = 128
QH = 64
PAGE = 32


EPSILON = 1e-05
NEGATIVE = -1e30
SHORT = 8


def shifted(x, axis, k):
    n = lax.axis_size(axis)
    return lax.ppermute(x, axis, [(i, (i + k) % n) for i in range(n)])


def from_all(x, axis):
    n = lax.axis_size(axis)
    if n > SHORT:
        order = (lax.axis_index(axis) - jnp.arange(n)) % n
        return list(lax.all_gather(x, axis)[order])
    return [x] + [shifted(x, axis, k) for k in range(1, n)]


def to_groups(x):
    n = lax.axis_size("seq")
    if n > SHORT:
        me, k = lax.axis_index("seq"), jnp.arange(n)
        back = lax.all_to_all(jnp.stack(x)[(me - k) % n], "seq", split_axis=0, concat_axis=0)
        return list(back[(me + k) % n])
    return [x[0]] + [shifted(x[k], "seq", -k) for k in range(1, n)]


def load_kernel(owners, place, hidden, key_weight, value_weight, held, keys, values, arrived):
    depth = key_weight.shape[0]
    blocks = held.shape[1] // depth

    def block(j):
        index = lax.rem(place[0] * owners + place[1] + j, blocks)
        return pl.ds(pl.multiple_of(index * depth, depth), depth)

    def copy(j):
        return pltpu.make_async_copy(hidden.at[:, block(j)], held.at[:, block(j)], arrived.at[j])

    for j in range(blocks):
        copy(j).start()
    copy(0).wait()
    for weight, out in ((key_weight, keys), (value_weight, values)):
        out[...] = jnp.dot(held[:, block(0)], weight[...], preferred_element_type=jnp.float32)
    for j in range(1, blocks):
        copy(j).wait()


def load(hidden, key_weight, value_weight, place, owners):
    tokens, width = hidden.shape
    depth, columns = key_weight.shape
    whole = pl.BlockSpec(memory_space=pltpu.VMEM)
    total = jax.ShapeDtypeStruct((tokens, columns), jnp.float32)
    return pl.pallas_call(
        functools.partial(load_kernel, owners),
        out_shape=(jax.ShapeDtypeStruct(hidden.shape, hidden.dtype), total, total),
        in_specs=[
            pl.BlockSpec(memory_space=pltpu.SMEM),
            pl.BlockSpec(memory_space=pltpu.HBM),
            whole,
            whole,
        ],
        out_specs=(whole,) * 3,
        scratch_shapes=[pltpu.SemaphoreType.DMA((width // depth,))],
        compiler_params=pltpu.CompilerParams(vmem_limit_bytes=36 * 2**20),
        cost_estimate=pl.CostEstimate(
            flops=4 * tokens * depth * columns,
            bytes_accessed=2 * tokens * width,
            transcendentals=0,
        ),
        name="load",
    )(place, hidden, key_weight, value_weight)


def project_kernel(hops, back, groups, owners, place, left, *refs):
    count = len(hops)
    weights, total = refs[:count], refs[count]
    out, held, arrived = refs[-3:]
    depth = held.shape[1]
    copies = [pltpu.make_async_copy(weights[j], held.at[j], arrived.at[j]) for j in range(count)]
    for copy in copies:
        copy.start()
    out[...] = total[...]
    owner = lax.rem(place[1] + owners - back, owners)
    for j, copy in enumerate(copies):
        copy.wait()
        group = place[0] + hops[j][0]
        for hop in hops[j][1:]:
            group = jnp.where((group >= 0) & (group < groups), group, place[0] + hop)

        @pl.when((group >= 0) & (group < groups))
        def _(j=j, group=group):
            block = pl.ds(pl.multiple_of((group * owners + owner) * depth, depth), depth)
            out[...] += jnp.dot(left[:, block], held[j], preferred_element_type=jnp.float32)


def project(hidden, total, weights, place, hops, back, groups, owners):
    tokens = hidden.shape[0]
    depth, columns = weights[0].shape
    count = len(weights)
    whole = pl.BlockSpec(memory_space=pltpu.VMEM)
    return pl.pallas_call(
        functools.partial(project_kernel, hops, back, groups, owners),
        out_shape=jax.ShapeDtypeStruct((tokens, columns), jnp.float32),
        in_specs=[pl.BlockSpec(memory_space=pltpu.SMEM), whole]
        + [pl.BlockSpec(memory_space=pl.ANY)] * count
        + [whole],
        out_specs=whole,
        scratch_shapes=[
            pltpu.VMEM((count, depth, columns), weights[0].dtype),
            pltpu.SemaphoreType.DMA((count,)),
        ],
        compiler_params=pltpu.CompilerParams(vmem_limit_bytes=12 * 2**20),
        cost_estimate=pl.CostEstimate(
            flops=2 * tokens * depth * columns * count,
            bytes_accessed=2 * count * depth * (tokens + columns) + 8 * tokens * columns,
            transcendentals=0,
        ),
        input_output_aliases={2 + count: 0},
        name="project",
    )(place, hidden, *weights, total)


def score_kernel(slots, parts, steps, scale, group, query, smooth, count, *refs):
    keys, probs, stats = refs[:parts], refs[parts], refs[parts + 1 : parts + 1 + slots]
    scores, tops, sums = refs[-3:]
    tokens = keys[0].shape[0]
    scaled = (query[0].astype(jnp.float32) * smooth[...]).astype(jnp.bfloat16)
    for p in range(parts):
        scores[:, p * tokens : (p + 1) * tokens] = lax.dot_general(
            scaled, keys[p][...], (((1,), (1,)), ((), ())), preferred_element_type=jnp.float32
        )
    requests = count.shape[1]
    rows = scores.shape[0]
    group_rows = rows // (steps * requests)
    pair = 2 if requests % 2 == 0 else 1
    for first in range(0, requests, pair):
        times = jnp.concatenate(
            [
                jnp.broadcast_to(count[0, first + a : first + a + 1, :], (group_rows, parts * tokens))
                for a in range(pair)
            ],
            axis=0,
        )
        bias = jnp.where(times > 0.0, 0.0, NEGATIVE)
        for step in range(steps):
            start = (step * requests + first) * group_rows
            at = pl.ds(start, pair * group_rows)
            raw = scores[at, :] * scale + bias
            top = jnp.max(raw, axis=1, keepdims=True)
            counted = jnp.exp(raw - top) * times
            probs[0, at, :] = counted.astype(jnp.bfloat16)
            tops[at, :] = jnp.broadcast_to(top, (pair * group_rows, 128))
            sums[at, :] = jnp.broadcast_to(
                jnp.sum(counted, axis=1, keepdims=True), (pair * group_rows, 128)
            )
    for slot in range(slots):

        @pl.when(pl.program_id(0) == slot)
        def _(slot=slot):
            stats[slot][0:1, :] = jnp.transpose(tops[...])[0:1, :]
            stats[slot][1:2, :] = jnp.transpose(sums[...])[0:1, :]


def score(groups, query, smooth, count, keys, steps, scale):
    slots, rows, width = query.shape
    tokens = keys[0].shape[0]
    parts = len(keys)
    requests = count.shape[1]
    probs, *stats = pl.pallas_call(
        functools.partial(score_kernel, slots, parts, steps, scale),
        out_shape=[jax.ShapeDtypeStruct((slots, rows, parts * tokens), jnp.bfloat16)]
        + [jax.ShapeDtypeStruct((2, rows), jnp.float32)] * slots,
        grid_spec=pltpu.PrefetchScalarGridSpec(
            num_scalar_prefetch=1,
            grid=(slots,),
            in_specs=[
                pl.BlockSpec((1, rows, width), lambda k, group: (k, 0, 0)),
                pl.BlockSpec((1, width), lambda k, group: (0, 0)),
                pl.BlockSpec((1, requests, parts * tokens), lambda k, group: (group[k], 0, 0)),
            ]
            + [pl.BlockSpec((tokens, width), lambda k, group: (0, 0))] * parts,
            out_specs=[pl.BlockSpec((1, rows, parts * tokens), lambda k, group: (k, 0, 0))]
            + [pl.BlockSpec((2, rows), lambda k, group: (0, 0))] * slots,
            scratch_shapes=[
                pltpu.VMEM((rows, parts * tokens), jnp.float32),
                pltpu.VMEM((rows, 128), jnp.float32),
                pltpu.VMEM((rows, 128), jnp.float32),
            ],
        ),
        compiler_params=pltpu.CompilerParams(vmem_limit_bytes=16 * 2**20),
        cost_estimate=pl.CostEstimate(
            flops=2 * slots * rows * width * parts * tokens,
            bytes_accessed=2 * slots * rows * parts * tokens,
            transcendentals=slots * rows * parts * tokens,
        ),
        name="score",
    )(groups, query, smooth, count, *keys)
    return probs, stats


def thirds(x):
    out = []
    for _ in range(3):
        out.append(x.astype(jnp.bfloat16))
        x = x - out[-1].astype(jnp.float32)
    return out


def weigh_kernel(slots, parts, probs, *refs):
    values, stats, outs = refs[:parts], refs[parts : parts + slots], refs[parts + slots :]
    tokens, width = values[0].shape
    rows = probs.shape[1]
    summed = sum(
        jnp.dot(
            probs[0, :, p * tokens : (p + 1) * tokens],
            values[p][...],
            preferred_element_type=jnp.float32,
        )
        for p in range(parts)
    ).astype(jnp.bfloat16)
    for slot in range(slots):

        @pl.when(pl.program_id(0) == slot)
        def _(slot=slot):
            outs[slot][0:rows, :] = summed
            lines = []
            for third in thirds(stats[slot][...]):
                third = third.astype(jnp.float32)
                lines += [third[:, c : c + width] for c in range(0, rows, width)]
            tail = outs[slot].shape[0] - rows
            lines.append(jnp.zeros((tail - 2 * len(lines), width), jnp.float32))
            outs[slot][rows:, :] = jnp.concatenate(lines, axis=0).astype(jnp.bfloat16)


def packed_rows(rows, width):
    return rows + (6 * (rows // width) // 16 + 1) * 16


def weigh(probs, values, stats):
    slots, rows, _ = probs.shape
    tokens, width = values[0].shape
    parts = len(values)
    total_rows = packed_rows(rows, width)
    return pl.pallas_call(
        functools.partial(weigh_kernel, slots, parts),
        out_shape=[jax.ShapeDtypeStruct((total_rows, width), jnp.bfloat16)] * slots,
        grid=(slots,),
        in_specs=[pl.BlockSpec((1, rows, parts * tokens), lambda k: (k, 0, 0))]
        + [pl.BlockSpec((tokens, width), lambda k: (0, 0))] * parts
        + [pl.BlockSpec((2, rows), lambda k: (0, 0))] * slots,
        out_specs=[pl.BlockSpec((total_rows, width), lambda k: (0, 0))] * slots,
        compiler_params=pltpu.CompilerParams(vmem_limit_bytes=16 * 2**20),
        cost_estimate=pl.CostEstimate(
            flops=2 * slots * rows * width * parts * tokens,
            bytes_accessed=2 * slots * rows * parts * tokens,
            transcendentals=0,
        ),
        name="weigh",
    )(probs, *values, *stats)


def fresh_kernel(scale, query, smooth, new_keys, new_values, group_scale, summed, highest, total):
    steps, requests, width = new_keys.shape
    group_rows = query.shape[0] // (steps * requests)
    rows = requests * group_rows
    scaled = (query[...].astype(jnp.float32) * smooth[...]).astype(jnp.bfloat16)
    scaled = scaled.astype(jnp.float32)

    def by_row(x):
        x = x.astype(jnp.bfloat16).astype(jnp.float32)
        spread = [jnp.broadcast_to(x[r : r + 1], (group_rows, width)) for r in range(requests)]
        return jnp.concatenate(spread, axis=0)

    def clip(x, row):
        limit = group_scale[row : row + 1, :]
        return jnp.clip(x, -8.0 * limit, 7.0 * limit)

    keys = [by_row(clip(new_keys[u] / smooth[...], 0)) for u in range(steps)]
    values = [by_row(clip(new_values[u], 1)) for u in range(steps)]
    for step in range(steps):
        at = pl.ds(step * rows, rows)
        mine = scaled[step * rows : (step + 1) * rows]
        scores = [
            jnp.sum(mine * keys[u], axis=1, keepdims=True) * scale for u in range(step + 1)
        ]
        top = functools.reduce(jnp.maximum, scores)
        expd = [jnp.exp(score - top) for score in scores]
        highest[at, :] = jnp.broadcast_to(top, (rows, width))
        total[at, :] = jnp.broadcast_to(sum(expd), (rows, width))
        summed[at, :] = sum(
            e.astype(jnp.bfloat16).astype(jnp.float32) * value for e, value in zip(expd, values)
        )


def fresh(query, smooth, new_keys, new_values, group_scale, scale):
    return pl.pallas_call(
        functools.partial(fresh_kernel, scale),
        out_shape=(jax.ShapeDtypeStruct(query.shape, jnp.float32),) * 3,
        compiler_params=pltpu.CompilerParams(vmem_limit_bytes=16 * 2**20),
        name="fresh",
    )(query, smooth, new_keys, new_values, group_scale)


def finish_kernel(slots, *refs):
    messages, (summed, highest, total, out) = refs[:slots], refs[slots:]
    rows, width = out.shape
    pieces = rows // width
    tails = [message[rows:, :].astype(jnp.float32) for message in messages]

    def column(slot, piece, which):
        lines = [tails[slot][2 * (j * pieces + piece) + which :][:1] for j in range(3)]
        return jnp.transpose(jnp.broadcast_to(lines[0] + lines[1] + lines[2], (width, width)))

    for piece in range(pieces):
        at = pl.ds(piece * width, width)
        parts = [
            (messages[k][at, :].astype(jnp.float32), column(k, piece, 0), column(k, piece, 1))
            for k in range(slots)
        ]
        parts.append((summed[at, :], highest[at, :], total[at, :]))
        top = functools.reduce(jnp.maximum, [part[1] for part in parts])
        shares = [jnp.exp(part[1] - top) for part in parts]
        norm = sum(share * part[2] for share, part in zip(shares, parts))
        out[at, :] = (sum(share * part[0] for share, part in zip(shares, parts)) / norm).astype(
            out.dtype
        )


def finish(messages, own):
    return pl.pallas_call(
        functools.partial(finish_kernel, len(messages)),
        out_shape=jax.ShapeDtypeStruct(own[0].shape, jnp.bfloat16),
        compiler_params=pltpu.CompilerParams(vmem_limit_bytes=16 * 2**20),
        name="finish",
    )(*messages, *own)


def token_counts(page_table, lengths, first_pages, pages_dev):
    slots = page_table.shape[1]
    slot_ids = jnp.arange(slots, dtype=jnp.int32)
    whole_slots, rest = lengths // PAGE, lengths % PAGE
    pages = jnp.concatenate(
        [first + jnp.arange(pages_dev, dtype=jnp.int32) for first in first_pages]
    )
    same = page_table[:, :, None] == pages[None, None, :]
    whole = jnp.sum(same & (slot_ids[None, :] < whole_slots[:, None])[:, :, None], axis=1)
    last = jnp.sum(same & (slot_ids[None, :] == whole_slots[:, None])[:, :, None], axis=1)
    token = jnp.arange(pages.shape[0] * PAGE, dtype=jnp.int32)
    spread = token[None, :] // PAGE == jnp.arange(pages.shape[0], dtype=jnp.int32)[:, None]
    spread = spread.astype(jnp.bfloat16)
    whole = jnp.dot(whole.astype(jnp.bfloat16), spread, preferred_element_type=jnp.float32)
    last = jnp.dot(last.astype(jnp.bfloat16), spread, preferred_element_type=jnp.float32)
    return whole + jnp.where((token % PAGE)[None, :] < rest[:, None], last, 0.0)


def clip_keys(raw, smooth, scale):
    return jnp.clip(raw / smooth, -8.0 * scale[0], 7.0 * scale[0]).astype(jnp.bfloat16)


def clip_values(raw, scale):
    return jnp.clip(raw, -8.0 * scale[1], 7.0 * scale[1]).astype(jnp.bfloat16)


def my_part(x, axis, owner_is, ahead=0):
    owners = len(owner_is)
    size = x.shape[axis] // owners
    pieces = [lax.slice_in_dim(x, p * size, (p + 1) * size, axis=axis) for p in range(owners)]
    out = pieces[0]
    for p in range(1, owners):
        out = jnp.where(owner_is[(p - ahead) % owners], pieces[p], out)
    return out


def smooth_of(raw_keys):
    top = jnp.max(jnp.abs(raw_keys), axis=0, keepdims=True)
    top = functools.reduce(jnp.maximum, from_all(top, "rep"))
    top = functools.reduce(jnp.maximum, from_all(top, "seq"))
    return jnp.sqrt(top + EPSILON)


def line_project(hidden, key_weight, value_weight, raw_query, early):
    groups, owners = lax.axis_size("seq"), lax.axis_size("rep")
    names = ("k", "v")
    moving, arrived, totals = {}, {}, {}

    def send(name, hop):
        left, right = moving[name]
        left = lax.ppermute(left, "seq", [(i, i + 1) for i in range(hop - 1, groups - 1)])
        right = lax.ppermute(right, "seq", [(i, i - 1) for i in range(1, groups - hop + 1)])
        arrived[name] = (left, right)

    def absorb(name, hop):
        left, right = moving[name]
        if hop == 0:
            here = [((0,), left)]
        elif 2 * hop >= groups:
            here = [((-hop, hop), left + right)]
        else:
            here = [((-hop,), left), ((hop,), right)]
        blocks = [block for _, block in here]
        passed = [[shifted(block, "rep", k) for block in blocks] for k in range(1, owners)]
        for k, ready in enumerate([blocks] + passed):
            if hop == 0 and k == 0:
                continue
            totals[name] = project(
                hidden,
                totals[name],
                ready,
                early[0],
                tuple(hops for hops, _ in here),
                k,
                groups,
                owners,
            )

    moving["k"], moving["v"] = (key_weight,) * 2, (value_weight,) * 2
    for name in names:
        send(name, 1)
    queries = from_all(raw_query, "seq")
    early, first = lax.optimization_barrier((early, (key_weight, value_weight)))
    hidden, totals["k"], totals["v"] = load(hidden, *first, early[0], owners)
    for name in names:
        absorb(name, 0)
    for hop in range(1, groups):
        for name in names:
            if name == names[-1] and hop == groups - 1:
                smooth = smooth_of(totals["k"])
                moving[name], smooth = lax.optimization_barrier((arrived[name], smooth))
            else:
                moving[name], totals = lax.optimization_barrier((arrived[name], totals))
            if hop < groups - 1:
                send(name, hop + 1)
            absorb(name, hop)
    return totals["k"], totals["v"], smooth, queries, early


def on_device(
    hidden, key_weight, value_weight, group_scale, new_kv, decode_query, page_table, lengths
):
    tokens = hidden.shape[0]
    columns = key_weight.shape[1]
    group_size = QH // KVH
    groups, owners = lax.axis_size("seq"), lax.axis_size("rep")
    my_group, my_owner = lax.axis_index("seq"), lax.axis_index("rep")
    assert columns // HD == owners
    pages_dev = tokens // PAGE
    step_count, per_group = decode_query.shape[:2]

    owner_is = [my_owner == owner for owner in range(owners)]
    raw_query = my_part(decode_query, 2, owner_is).reshape(1, -1, HD)

    first_pages = [
        (my_group * owners + (my_owner - k) % owners) * pages_dev for k in range(owners)
    ]
    counts = token_counts(page_table, lengths, first_pages, pages_dev)
    my_kv = my_part(new_kv, 3, owner_is).astype(jnp.float32)
    early = (
        jnp.stack([my_group, my_owner]),
        owner_is,
        counts.reshape(groups, per_group, -1),
        (my_group - jnp.arange(groups, dtype=jnp.int32)) % groups,
        (my_kv[:, :, 0], my_kv[:, :, 1], my_part(group_scale, 1, owner_is)),
    )
    if groups > SHORT:
        raw_keys, raw_values = (
            jnp.dot(
                hidden,
                lax.all_gather(weight, ("seq", "rep"), axis=0, tiled=True),
                preferred_element_type=jnp.float32,
            )
            for weight in (key_weight, value_weight)
        )
        queries = from_all(raw_query, "seq")
        smooth = smooth_of(raw_keys)
    else:
        raw_keys, raw_values, smooth, queries, early = line_project(
            hidden, key_weight, value_weight, raw_query, early
        )
    _, owner_is, counts, group_at, my_new = early

    def by_head(x):
        return [my_part(x, 1, owner_is)] + [
            shifted(my_part(x, 1, owner_is, k), "rep", k) for k in range(1, owners)
        ]

    smoothing = smooth.reshape(-1)
    my_smooth = my_part(smooth, 1, owner_is)
    keys = clip_keys(raw_keys, smooth, group_scale)
    head_keys, raw_values = lax.optimization_barrier((by_head(keys), raw_values))
    values = clip_values(raw_values, group_scale)
    score_scale = HD ** (-0.5)
    probs, stats = score(
        group_at,
        jnp.concatenate(queries),
        my_smooth,
        counts,
        head_keys,
        step_count,
        score_scale,
    )
    messages = weigh(probs, by_head(values), stats)

    messages, keys, values, late = lax.optimization_barrier(
        (messages, keys, values, (raw_query, my_smooth))
    )
    messages = to_groups(messages)
    kv_cache = jnp.stack([keys, values], axis=1)
    own = fresh(late[0].reshape(-1, HD), late[1], *my_new, score_scale)
    messages, kv_cache, own = lax.optimization_barrier((messages, kv_cache, own))
    attention = finish(messages, own).reshape(step_count, per_group, group_size * HD)
    by_owner = from_all(attention, "rep")
    attention = jnp.concatenate(
        [
            functools.reduce(
                lambda out, k: jnp.where(owner_is[(head + k) % owners], by_owner[k], out),
                range(1, owners),
                by_owner[0],
            )
            for head in range(owners)
        ],
        axis=2,
    )
    return (kv_cache, smoothing, attention)


def solution(mesh):
    placed = (
        P(("seq", "rep"), None),
        P(("seq", "rep"), "head"),
        P(("seq", "rep"), "head"),
        P(None, "head"),
        P(None, "seq", None, "head"),
        P(None, "seq", "head"),
        P(),
        P(),
    )

    return jax.shard_map(
        on_device,
        mesh=mesh,
        in_specs=placed,
        out_specs=(P(("seq", "rep"), None, "head"), P("head"), P(None, "seq", "head")),
        check_vma=False,
    )
```

time: 166 us -> 167 us (level)
  waiting for transfers between devices: 35.9 us -> 66.5 us
  Pallas kernels: 63.3 us -> 42.7 us
  starting transfers between devices: 46 us -> 32.9 us
  local copies, waits for them, and re-layouts: 4.68 us -> 15.5 us
  other arithmetic: 10.9 us -> 6.91 us
  matrix products: 2.45 us -> 0.42 us
    ppermute x6, waiting for transfers between devices: 17.7 us -> 42.2 us  [send(): lax.ppermute(right, 'seq', [(i, i - 1) for i in range(1, groups - hop + 1)])]
    pallas_call x16 -> x17, Pallas kernels: 55.6 us -> 36 us  [the longest x14 22.5 us: project(): pl.pallas_call(functools.partial(project_kernel, hops, back, groups, owne...]
    ppermute x26 -> x23, starting transfers between devices: 25.9 us -> 12.7 us  [shifted(): return lax.ppermute(x, axis, [(i, (i + k) % n) for i in range(n)])]
    unnamed x41 -> x21, local copies, waits for them, and re-layouts: 3.82 us -> 14.7 us
    ppermute x6, waiting for transfers between devices: 0.02 us -> 7.68 us  [send(): lax.ppermute(left, 'seq', [(i, i + 1) for i in range(hop - 1, groups - 1)])]
    add x0 -> x4, other arithmetic: none -> 2.78 us  [absorb(): here = [((-hop, hop), left + right)]]
    another operation x10 -> x1, other arithmetic: 2.19 us -> 0.08 us  [on_device(): jnp.stack([my_group, my_owner])]
    ppermute x26 -> x23, waiting for transfers between devices: 18.2 us -> 16.7 us  [shifted(): return lax.ppermute(x, axis, [(i, (i + k) % n) for i in range(n)])]
  transfers between devices with their start and end apart: 38 -> 35, of which waited for: 11 -> 12; matrix products, arithmetic and copies ran while one was open for 8% -> 5% of each run, Pallas kernels for 34% -> 24%
where the time goes in v4:
time: 167 us; the launch traced here: 166 us
  waiting for transfers between devices  66.5 us (40%)
  Pallas kernels  42.7 us (26%)
  starting transfers between devices  32.9 us (20%)
  local copies, waits for them, and re-layouts  15.5 us (9%)
  other arithmetic  6.91 us (4%)
    ppermute x6, waiting for transfers between devices, send(): lax.ppermute(right, 'seq', [(i, i - 1) for i in range(1, groups - hop + 1)])  42.2 us
    pallas_call x14, Pallas kernels, project(): pl.pallas_call(functools.partial(project_kernel, hops, back, groups, owne...  22.5 us
    ppermute x23, waiting for transfers between devices, shifted(): return lax.ppermute(x, axis, [(i, (i + k) % n) for i in range(n)])  16.7 us
    unnamed x21, local copies, waits for them, and re-layouts  14.7 us
    pallas_call x1, Pallas kernels, load(): pl.pallas_call(functools.partial(load_kernel, owners), out_shape=(jax.Sha...  12.8 us
    ppermute x23, starting transfers between devices, shifted(): return lax.ppermute(x, axis, [(i, (i + k) % n) for i in range(n)])  12.7 us
    ppermute x6, starting transfers between devices, send(): lax.ppermute(left, 'seq', [(i, i + 1) for i in range(hop - 1, groups - 1)])  12.5 us
    ppermute x6, starting transfers between devices, send(): lax.ppermute(right, 'seq', [(i, i - 1) for i in range(1, groups - hop + 1)])  7.74 us
  transfers between devices with their start and end apart: 35, of which 12 were waited for; matrix products, arithmetic and copies ran while one was open for 5% of the time, Pallas kernels for 24%

profile of v4, /device:TPU:0, one launch (start us, length us, event | category | flops | bytes accessed | tf_op | source)
XLA Modules:
  0.0 166.3 jit_solution(3695348083674376335)
XLA Ops:
  0.6 0.6 collective-permute-start.7
  1.2 4.5 %collective-permute-start.5 = (bf16[1024,256]{1,0:T(8,128)(2,1)}, bf16[1024,256]{1,0:T(8,128)(2,1)S(1)}, u32[]{:S(2)}, u32[]{:S(2)}) collective-permute-start(bf16[1024,256]{1,0:T(8,128)(2,1)} %key_weight), channel_id=1, source_target_pairs={{0,8},{8,16},{16,24},{1,9},{9,17},{17,25},{2,10},{10,18},{18,26},{... | collective-permute-start | bytes 1572872 | tf_op jit(solution)/shard_map/ppermute | solution.py:404
  5.7 1.3 collective-permute-start.6
  7.0 0.3 collective-permute-start.8
  7.3 0.7 and_select_fusion.1
  8.0 0.8 fusion.16
  8.9 1.3 convert_reduce_fusion
  10.4 0.7 slice_select_fusion.1.group_scale
  11.4 1.0 copy-done.2
  12.4 12.8 %load.1 = (bf16[1024,8192]{1,0:T(8,128)(2,1)}, f32[1024,256]{1,0:T(8,128)S(1)}, f32[1024,256]{1,0:T(8,128)S(1)}) custom-call(s32[2]{0:T(128)S(1)} %pad_add_fusion.place, bf16[1024,8192]{1,0:T(8,128)(2,1)} %hidden.1, bf16[1024,256]{1,0:T(8,128)(2,1)S(1)} %copy-done.2, bf16[1024,256]{1,0:T(8,128)(2,1)} %value_weight), custom_call_target="tpu_custom_call" | custom-call | flops 1073741824 | bytes 16777216 | tf_op jit(solution)/shard_map/load/pallas_call | solution.py:69
  25.3 5.8 %copy-done = bf16[1024,8192]{1,0:T(8,128)(2,1)S(1)} copy-done((bf16[1024,8192]{1,0:T(8,128)(2,1)S(1)}, bf16[1024,8192]{1,0:T(8,128)(2,1)}, u32[]{:S(2)}) %copy-start) | copy-done | bytes 16777240
  31.1 2.3 %project.15.refs_2_ = f32[1024,256]{1,0:T(8,128)S(1)} custom-call(s32[2]{0:T(128)S(1)} %pad_add_fusion.place, bf16[1024,8192]{1,0:T(8,128)(2,1)S(1)} %copy-done, bf16[1024,256]{1,0:T(8,128)(2,1)} %collective-permute-done.8.refs_0_, f32[1024,256]{1,0:T(8,128)S(1)} %get-tuple-element.77.refs_1_), custom_call_target="tpu_custom_call", output_to_operand_aliasing={{}: (3, {})} | custom-call | flops 536870912 | bytes 4718592 | tf_op jit(solution)/shard_map/project/pallas_call | solution.py:117
  33.4 2.3 %project.14.refs_2_ = f32[1024,256]{1,0:T(8,128)S(1)} custom-call(s32[2]{0:T(128)S(1)} %pad_add_fusion.place, bf16[1024,8192]{1,0:T(8,128)(2,1)S(1)} %copy-done, bf16[1024,256]{1,0:T(8,128)(2,1)} %collective-permute-done.7.refs_0_, f32[1024,256]{1,0:T(8,128)S(1)} %get-tuple-element.76.refs_1_), custom_call_target="tpu_custom_call", output_to_operand_aliasing={{}: (3, {})} | custom-call | flops 536870912 | bytes 4718592 | tf_op jit(solution)/shard_map/project/pallas_call | solution.py:117
  35.7 0.4 collective-permute-start.10
  36.3 4.4 %collective-permute-start.3 = (bf16[1024,256]{1,0:T(8,128)(2,1)}, bf16[1024,256]{1,0:T(8,128)(2,1)S(1)}, u32[]{:S(2)}, u32[]{:S(2)}) collective-permute-start(bf16[1024,256]{1,0:T(8,128)(2,1)} %value_weight), channel_id=1, source_target_pairs={{0,8},{8,16},{16,24},{1,9},{9,17},{17,25},{2,10},{10,18},{18,26},{... | collective-permute-start | bytes 1572872 | tf_op jit(solution)/shard_map/ppermute | solution.py:404
  40.8 1.3 collective-permute-start.4
  42.1 1.5 project.16.refs_2_
  43.6 1.5 project.17.refs_1_
  45.1 7.7 %collective-permute-done.3.refs_0_ = bf16[1024,256]{1,0:T(8,128)(2,1)S(1)} collective-permute-done((bf16[1024,256]{1,0:T(8,128)(2,1)}, bf16[1024,256]{1,0:T(8,128)(2,1)S(1)}, u32[]{:S(2)}, u32[]{:S(2)}) %collective-permute-start.3) | collective-permute-done | bytes 524320 | tf_op jit(solution)/shard_map/ppermute | solution.py:404
  52.8 4.0 %collective-permute-done.4.refs_1_ = bf16[1024,256]{1,0:T(8,128)(2,1)S(1)} collective-permute-done((bf16[1024,256]{1,0:T(8,128)(2,1)}, bf16[1024,256]{1,0:T(8,128)(2,1)S(1)}, u32[]{:S(2)}, u32[]{:S(2)}) %collective-permute-start.4) | collective-permute-done | bytes 524320 | tf_op jit(solution)/shard_map/ppermute | solution.py:405
  56.9 0.5 collective-permute-start.16
  57.4 0.7 collective-permute-start.13
  58.0 1.3 collective-permute-start.14
  59.3 1.5 project.18.refs_2_
  60.9 1.5 project.19.refs_1_
  62.4 13.7 %collective-permute-done.14 = bf16[1024,256]{1,0:T(8,128)(2,1)S(1)} collective-permute-done((bf16[1024,256]{1,0:T(8,128)(2,1)S(1)}, bf16[1024,256]{1,0:T(8,128)(2,1)S(1)}, u32[]{:S(2)}, u32[]{:S(2)}) %collective-permute-start.14) | collective-permute-done | bytes 524320 | tf_op jit(solution)/shard_map/ppermute | solution.py:405
  76.4 0.7 collective-permute-start.11
  77.1 1.3 collective-permute-start.12
  78.4 1.5 project.20.refs_1_
  79.9 1.5 project.21.refs_1_
  81.4 12.6 %collective-permute-done.12 = bf16[1024,256]{1,0:T(8,128)(2,1)} collective-permute-done((bf16[1024,256]{1,0:T(8,128)(2,1)S(1)}, bf16[1024,256]{1,0:T(8,128)(2,1)}, u32[]{:S(2)}, u32[]{:S(2)}) %collective-permute-start.12) | collective-permute-done | bytes 524320 | tf_op jit(solution)/shard_map/ppermute | solution.py:405
  94.0 1.2 add.89.refs_0_
  95.2 0.7 collective-permute-start.20
  96.0 1.3 collective-permute-start.21
  97.3 1.6 project.22.refs_1_
  98.9 1.5 project.23.refs_1_
  100.4 11.8 %collective-permute-done.21 = bf16[1024,256]{1,0:T(8,128)(2,1)S(1)} collective-permute-done((bf16[1024,256]{1,0:T(8,128)(2,1)S(1)}, bf16[1024,256]{1,0:T(8,128)(2,1)S(1)}, u32[]{:S(2)}, u32[]{:S(2)}) %collective-permute-start.21) | collective-permute-done | bytes 524320 | tf_op jit(solution)/shard_map/ppermute | solution.py:405
  112.4 1.5 collective-permute-start.18
  113.9 1.3 collective-permute-start.19
  115.2 1.5 project.24.refs_1_
  116.6 1.5 project.25
  118.2 0.6 collective-permute-start.24
  118.7 0.8 collective-permute-done.24
  119.5 1.8 %collective-permute-start.25 = (f32[1,256]{1,0:T(1,128)S(1)}, f32[1,256]{1,0:T(1,128)S(1)}, u32[]{:S(2)}, u32[]{:S(2)}) collective-permute-start(f32[1,256]{1,0:T(1,128)S(1)} %max.36), channel_id=1, source_target_pairs={{0,8},{8,16},{16,24},{24,0},{1,9},{9,17},{17,25},{25,1},{2,10},{10... | collective-permute-start | bytes 3080 | tf_op jit(solution)/shard_map/ppermute | solution.py:24
  121.4 2.4 %collective-permute-start.27 = (f32[1,256]{1,0:T(1,128)S(1)}, f32[1,256]{1,0:T(1,128)S(1)}, u32[]{:S(2)}, u32[]{:S(2)}) collective-permute-start(f32[1,256]{1,0:T(1,128)S(1)} %max.36), channel_id=1, source_target_pairs={{0,24},{8,0},{16,8},{24,16},{1,25},{9,1},{17,9},{25,17},{2,26},{10... | collective-permute-start | bytes 3080 | tf_op jit(solution)/shard_map/ppermute | solution.py:24
  123.8 1.1 collective-permute-done.25
  125.0 0.9 collective-permute-done.26
  125.9 2.5 %collective-permute-start.1 = (bf16[1,256,128]{2,1,0:T(8,128)(2,1)S(1)}, bf16[1,256,128]{2,1,0:T(8,128)(2,1)S(1)}, u32[]{:S(2)}, u32[]{:S(2)}) collective-permute-start(bf16[1,256,128]{2,1,0:T(8,128)(2,1)S(1)} %reshape.109), channel_id=1, source_target_pairs={{0,16},{8,24},{16,0},{24,8},{1,17},{9,25},{17,1},{25,9},{2,18},{10... | collective-permute-start | bytes 196616 | tf_op jit(solution)/shard_map/ppermute | solution.py:24
  128.3 4.9 %collective-permute-done.27 = f32[1,256]{1,0:T(1,128)S(1)} collective-permute-done((f32[1,256]{1,0:T(1,128)S(1)}, f32[1,256]{1,0:T(1,128)S(1)}, u32[]{:S(2)}, u32[]{:S(2)}) %collective-permute-start.27) | collective-permute-done | bytes 1056 | tf_op jit(solution)/shard_map/ppermute | solution.py:24
  133.3 1.3 add.93.refs_0_
  134.9 0.6 collective-permute-start.28
  135.5 2.0 %collective-permute-done.2 = bf16[1,256,128]{2,1,0:T(8,128)(2,1)S(1)} collective-permute-done((bf16[1,256,128]{2,1,0:T(8,128)(2,1)S(1)}, bf16[1,256,128]{2,1,0:T(8,128)(2,1)S(1)}, u32[]{:S(2)}, u32[]{:S(2)}) %collective-permute-start.2) | collective-permute-done | bytes 65568 | tf_op jit(solution)/shard_map/ppermute | solution.py:24
  137.6 5.8 %copy-done.1 = bf16[1024,8192]{1,0:T(8,128)(2,1)S(1)} copy-done((bf16[1024,8192]{1,0:T(8,128)(2,1)S(1)}, bf16[1024,8192]{1,0:T(8,128)(2,1)}, u32[]{:S(2)}) %copy-start.1) | copy-done | bytes 16777240
  143.3 1.5 project.26.refs_1_
  144.8 1.5 project.27
  146.5 4.9 %score.1 = (bf16[4,256,2048]{2,1,0:T(8,128)(2,1)S(1)}, f32[2,256]{1,0:T(2,128)S(1)}, f32[2,256]{1,0:T(2,128)S(1)}, f32[2,256]{1,0:T(2,128)S(1)}, f32[2,256]{1,0:T(2,128)S(1)}) custom-call(s32[4]{0:T(128)S(1)} %and_select_fusion.group, bf16[4,256,128]{2,1,0:T(8,128)(2,1)S(1)} %pad_maximum_fusion.1.query, f32[1,128]{1,0:T(1,128)S(1)} %broadcast_select_fusion.6.smooth, ...), custom_call_target="tpu_custom_call" | custom-call | flops 536870912 | bytes 4194304 | tf_op jit(solution)/shard_map/score/pallas_call | solution.py:185
  151.4 1.8 %weigh.1 = (bf16[272,128]{1,0:T(8,128)(2,1)S(1)}, bf16[272,128]{1,0:T(8,128)(2,1)S(1)}, bf16[272,128]{1,0:T(8,128)(2,1)S(1)}, bf16[272,128]{1,0:T(8,128)(2,1)S(1)}) custom-call(bf16[4,256,2048]{2,1,0:T(8,128)(2,1)S(1)} %get-tuple-element.105.probs, bf16[1024,128]{1,0:T(8,128)(2,1)S(1)} %get-tuple-element.146.refs_0_, ...), custom_call_target="tpu_custom_call" | custom-call | flops 536870912 | bytes 4194304 | tf_op jit(solution)/shard_map/weigh/pallas_call | solution.py:260
  153.3 1.9 %collective-permute-start.31 = (bf16[272,128]{1,0:T(8,128)(2,1)S(1)}, bf16[272,128]{1,0:T(8,128)(2,1)S(1)}, u32[]{:S(2)}, u32[]{:S(2)}) collective-permute-start(bf16[272,128]{1,0:T(8,128)(2,1)S(1)} %get-tuple-element.116), channel_id=1, source_target_pairs={{0,24},{8,0},{16,8},{24,16},{1,25},{9,1},{17,9},{25,17},{2,26},{10... | collective-permute-start | bytes 208904 | tf_op jit(solution)/shard_map/ppermute | solution.py:24
  155.1 0.6 collective-permute-start.33
  156.1 1.8 %collective-permute-done.31.refs_1_ = bf16[272,128]{1,0:T(8,128)(2,1)S(1)} collective-permute-done((bf16[272,128]{1,0:T(8,128)(2,1)S(1)}, bf16[272,128]{1,0:T(8,128)(2,1)S(1)}, u32[]{:S(2)}, u32[]{:S(2)}) %collective-permute-start.31) | collective-permute-done | bytes 69664 | tf_op jit(solution)/shard_map/ppermute | solution.py:24
  157.9 5.1 %collective-permute-done.32.refs_2_ = bf16[272,128]{1,0:T(8,128)(2,1)S(1)} collective-permute-done((bf16[272,128]{1,0:T(8,128)(2,1)S(1)}, bf16[272,128]{1,0:T(8,128)(2,1)S(1)}, u32[]{:S(2)}, u32[]{:S(2)}) %collective-permute-start.32) | collective-permute-done | bytes 69664 | tf_op jit(solution)/shard_map/ppermute | solution.py:24
  163.0 0.4 finish.1
  163.5 2.0 %copy.30 = bf16[1024,2,256]{2,1,0:T(2,128)(2,1)} copy(bf16[1024,2,256]{2,0,1:T(8,128)(2,1)S(1)} %pad_maximum_fusion) | data formatting | bytes 2097152
  165.6 0.7 pad_maximum_fusion.2
  (81 shorter events, 2.6 us)
Async XLA Ops:
  0.6 32.7 %collective-permute-start.7 = (bf16[1024,256]{1,0:T(8,128)(2,1)}, bf16[1024,256]{1,0:T(8,128)(2,1)}, u32[]{:S(2)}, u32[]{:S(2)}) collective-permute-start(bf16[1024,256]{1,0:T(8,128)(2,1)} %key_weight), channel_id=1, source_target_pairs={{0,1},{1,0},{2,3},{3,2},{4,5},{5,4},{6,7},{7,6},{8,9},{9,8},{10,11... | collective-permute-start | bytes 1572872 | tf_op jit(solution)/shard_map/ppermute | solution.py:24
  1.2 34.5 %collective-permute-start.5 = (bf16[1024,256]{1,0:T(8,128)(2,1)}, bf16[1024,256]{1,0:T(8,128)(2,1)S(1)}, u32[]{:S(2)}, u32[]{:S(2)}) collective-permute-start(bf16[1024,256]{1,0:T(8,128)(2,1)} %key_weight), channel_id=1, source_target_pairs={{0,8},{8,16},{16,24},{1,9},{9,17},{17,25},{2,10},{10,18},{18,26},{... | collective-permute-start | bytes 1572872 | tf_op jit(solution)/shard_map/ppermute | solution.py:404
  5.7 30.0 %collective-permute-start.6 = (bf16[1024,256]{1,0:T(8,128)(2,1)}, bf16[1024,256]{1,0:T(8,128)(2,1)S(1)}, u32[]{:S(2)}, u32[]{:S(2)}) collective-permute-start(bf16[1024,256]{1,0:T(8,128)(2,1)} %key_weight), channel_id=1, source_target_pairs={{8,0},{16,8},{24,16},{9,1},{17,9},{25,17},{10,2},{18,10},{26,18},{... | collective-permute-start | bytes 1572872 | tf_op jit(solution)/shard_map/ppermute | solution.py:405
  7.0 18.3 %collective-permute-start.8 = (bf16[1024,256]{1,0:T(8,128)(2,1)}, bf16[1024,256]{1,0:T(8,128)(2,1)}, u32[]{:S(2)}, u32[]{:S(2)}) collective-permute-start(bf16[1024,256]{1,0:T(8,128)(2,1)} %value_weight), channel_id=1, source_target_pairs={{0,1},{1,0},{2,3},{3,2},{4,5},{5,4},{6,7},{7,6},{8,9},{9,8},{10,11... | collective-permute-start | bytes 1572872 | tf_op jit(solution)/shard_map/ppermute | solution.py:24
  11.4 1.0 copy-start.2
  25.3 5.8 %copy-start = (bf16[1024,8192]{1,0:T(8,128)(2,1)S(1)}, bf16[1024,8192]{1,0:T(8,128)(2,1)}, u32[]{:S(2)}) copy-start(bf16[1024,8192]{1,0:T(8,128)(2,1)} %get-tuple-element.75.left) | copy-start | bytes 50331652
  35.7 7.9 %collective-permute-start.10 = (bf16[1024,256]{1,0:T(8,128)(2,1)S(1)}, bf16[1024,256]{1,0:T(8,128)(2,1)S(1)}, u32[]{:S(2)}, u32[]{:S(2)}) collective-permute-start(bf16[1024,256]{1,0:T(8,128)(2,1)S(1)} %collective-permute-done.6.refs_1_), channel_id=1, source_target_pairs={{0,1},{1,0},{2,3},{3,2},{4,5},{5,4},{6,7},{7,6},{8,9},{9,8},{10,11... | collective-permute-start | bytes 1572872 | tf_op jit(solution)/shard_map/ppermute | solution.py:24
  36.1 7.5 %collective-permute-start.9 = (bf16[1024,256]{1,0:T(8,128)(2,1)S(1)}, bf16[1024,256]{1,0:T(8,128)(2,1)S(1)}, u32[]{:S(2)}, u32[]{:S(2)}) collective-permute-start(bf16[1024,256]{1,0:T(8,128)(2,1)S(1)} %collective-permute-done.5.refs_0_), channel_id=1, source_target_pairs={{0,1},{1,0},{2,3},{3,2},{4,5},{5,4},{6,7},{7,6},{8,9},{9,8},{10,11... | collective-permute-start | bytes 1572872 | tf_op jit(solution)/shard_map/ppermute | solution.py:24
  36.3 16.5 %collective-permute-start.3 = (bf16[1024,256]{1,0:T(8,128)(2,1)}, bf16[1024,256]{1,0:T(8,128)(2,1)S(1)}, u32[]{:S(2)}, u32[]{:S(2)}) collective-permute-start(bf16[1024,256]{1,0:T(8,128)(2,1)} %value_weight), channel_id=1, source_target_pairs={{0,8},{8,16},{16,24},{1,9},{9,17},{17,25},{2,10},{10,18},{18,26},{... | collective-permute-start | bytes 1572872 | tf_op jit(solution)/shard_map/ppermute | solution.py:404
  40.8 16.1 %collective-permute-start.4 = (bf16[1024,256]{1,0:T(8,128)(2,1)}, bf16[1024,256]{1,0:T(8,128)(2,1)S(1)}, u32[]{:S(2)}, u32[]{:S(2)}) collective-permute-start(bf16[1024,256]{1,0:T(8,128)(2,1)} %value_weight), channel_id=1, source_target_pairs={{8,0},{16,8},{24,16},{9,1},{17,9},{25,17},{10,2},{18,10},{26,18},{... | collective-permute-start | bytes 1572872 | tf_op jit(solution)/shard_map/ppermute | solution.py:405
  45.1 33.2 %slice-start = ((s8[16777216]{0:T(1024)(128)(4,1)}), s8[4194304]{0:T(1024)(128)(4,1)S(1)}, s32[]{:S(2)}) async-start(s8[16777216]{0:T(1024)(128)(4,1)} %bitcast.17), calls=%async_computation | async-start | bytes 8388608
  45.1 33.2 %slice-start.1 = ((s8[16777216]{0:T(1024)(128)(4,1)}), s8[4194304]{0:T(1024)(128)(4,1)S(1)}, s32[]{:S(2)}) async-start(s8[16777216]{0:T(1024)(128)(4,1)} %bitcast.17), calls=%async_computation.1 | async-start | bytes 8388608
  56.8 4.0 %collective-permute-start.15 = (bf16[1024,256]{1,0:T(8,128)(2,1)S(1)}, bf16[1024,256]{1,0:T(8,128)(2,1)S(1)}, u32[]{:S(2)}, u32[]{:S(2)}) collective-permute-start(bf16[1024,256]{1,0:T(8,128)(2,1)S(1)} %collective-permute-done.3.refs_0_), channel_id=1, source_target_pairs={{0,1},{1,0},{2,3},{3,2},{4,5},{5,4},{6,7},{7,6},{8,9},{9,8},{10,11... | collective-permute-start | bytes 1572872 | tf_op jit(solution)/shard_map/ppermute | solution.py:24
  56.9 4.0 %collective-permute-start.16 = (bf16[1024,256]{1,0:T(8,128)(2,1)S(1)}, bf16[1024,256]{1,0:T(8,128)(2,1)S(1)}, u32[]{:S(2)}, u32[]{:S(2)}) collective-permute-start(bf16[1024,256]{1,0:T(8,128)(2,1)S(1)} %collective-permute-done.4.refs_1_), channel_id=1, source_target_pairs={{0,1},{1,0},{2,3},{3,2},{4,5},{5,4},{6,7},{7,6},{8,9},{9,8},{10,11... | collective-permute-start | bytes 1572872 | tf_op jit(solution)/shard_map/ppermute | solution.py:24
  57.4 5.1 %collective-permute-start.13 = (bf16[1024,256]{1,0:T(8,128)(2,1)S(1)}, bf16[1024,256]{1,0:T(8,128)(2,1)S(1)}, u32[]{:S(2)}, u32[]{:S(2)}) collective-permute-start(bf16[1024,256]{1,0:T(8,128)(2,1)S(1)} %collective-permute-done.5.refs_0_), channel_id=1, source_target_pairs={{8,16},{16,24},{9,17},{17,25},{10,18},{18,26},{11,19},{19,27},{12,... | collective-permute-start | bytes 1572872 | tf_op jit(solution)/shard_map/ppermute | solution.py:404
  58.0 18.1 %collective-permute-start.14 = (bf16[1024,256]{1,0:T(8,128)(2,1)S(1)}, bf16[1024,256]{1,0:T(8,128)(2,1)S(1)}, u32[]{:S(2)}, u32[]{:S(2)}) collective-permute-start(bf16[1024,256]{1,0:T(8,128)(2,1)S(1)} %collective-permute-done.6.refs_1_), channel_id=1, source_target_pairs={{8,0},{16,8},{9,1},{17,9},{10,2},{18,10},{11,3},{19,11},{12,4},{20... | collective-permute-start | bytes 1572872 | tf_op jit(solution)/shard_map/ppermute | solution.py:405
  60.9 17.5 %slice-start.2 = ((s8[16777216]{0:T(1024)(128)(4,1)}), s8[4194304]{0:T(1024)(128)(4,1)S(1)}, s32[]{:S(2)}) async-start(s8[16777216]{0:T(1024)(128)(4,1)} %bitcast.17), calls=%async_computation.2 | async-start | bytes 8388608
  60.9 17.5 %slice-start.3 = ((s8[16777216]{0:T(1024)(128)(4,1)}), s8[4194304]{0:T(1024)(128)(4,1)S(1)}, s32[]{:S(2)}) async-start(s8[16777216]{0:T(1024)(128)(4,1)} %bitcast.17), calls=%async_computation.3 | async-start | bytes 8388608
  76.3 3.6 %collective-permute-start.17 = (bf16[1024,256]{1,0:T(8,128)(2,1)S(1)}, bf16[1024,256]{1,0:T(8,128)(2,1)S(1)}, u32[]{:S(2)}, u32[]{:S(2)}) collective-permute-start(bf16[1024,256]{1,0:T(8,128)(2,1)S(1)} %add.88.refs_0_), channel_id=1, source_target_pairs={{0,1},{1,0},{2,3},{3,2},{4,5},{5,4},{6,7},{7,6},{8,9},{9,8},{10,11... | collective-permute-start | bytes 1572872 | tf_op jit(solution)/shard_map/ppermute | solution.py:24
  76.4 5.0 %collective-permute-start.11 = (bf16[1024,256]{1,0:T(8,128)(2,1)S(1)}, bf16[1024,256]{1,0:T(8,128)(2,1)S(1)}, u32[]{:S(2)}, u32[]{:S(2)}) collective-permute-start(bf16[1024,256]{1,0:T(8,128)(2,1)S(1)} %collective-permute-done.3.refs_0_), channel_id=1, source_target_pairs={{8,16},{16,24},{9,17},{17,25},{10,18},{18,26},{11,19},{19,27},{12,... | collective-permute-start | bytes 1572872 | tf_op jit(solution)/shard_map/ppermute | solution.py:404
  77.1 16.9 %collective-permute-start.12 = (bf16[1024,256]{1,0:T(8,128)(2,1)S(1)}, bf16[1024,256]{1,0:T(8,128)(2,1)}, u32[]{:S(2)}, u32[]{:S(2)}) collective-permute-start(bf16[1024,256]{1,0:T(8,128)(2,1)S(1)} %collective-permute-done.4.refs_1_), channel_id=1, source_target_pairs={{8,0},{16,8},{9,1},{17,9},{10,2},{18,10},{11,3},{19,11},{12,4},{20... | collective-permute-start | bytes 1572872 | tf_op jit(solution)/shard_map/ppermute | solution.py:405
  95.2 3.7 %collective-permute-start.22 = (bf16[1024,256]{1,0:T(8,128)(2,1)S(1)}, bf16[1024,256]{1,0:T(8,128)(2,1)S(1)}, u32[]{:S(2)}, u32[]{:S(2)}) collective-permute-start(bf16[1024,256]{1,0:T(8,128)(2,1)S(1)} %add.89.refs_0_), channel_id=1, source_target_pairs={{0,1},{1,0},{2,3},{3,2},{4,5},{5,4},{6,7},{7,6},{8,9},{9,8},{10,11... | collective-permute-start | bytes 1572872 | tf_op jit(solution)/shard_map/ppermute | solution.py:24
  95.2 5.1 %collective-permute-start.20 = (bf16[1024,256]{1,0:T(8,128)(2,1)S(1)}, bf16[1024,256]{1,0:T(8,128)(2,1)S(1)}, u32[]{:S(2)}, u32[]{:S(2)}) collective-permute-start(bf16[1024,256]{1,0:T(8,128)(2,1)S(1)} %collective-permute-done.13), channel_id=1, source_target_pairs={{16,24},{17,25},{18,26},{19,27},{20,28},{21,29},{22,30},{23,31}} | collective-permute-start | bytes 1572872 | tf_op jit(solution)/shard_map/ppermute | solution.py:404
  96.0 16.2 %collective-permute-start.21 = (bf16[1024,256]{1,0:T(8,128)(2,1)S(1)}, bf16[1024,256]{1,0:T(8,128)(2,1)S(1)}, u32[]{:S(2)}, u32[]{:S(2)}) collective-permute-start(bf16[1024,256]{1,0:T(8,128)(2,1)S(1)} %collective-permute-done.14), channel_id=1, source_target_pairs={{8,0},{9,1},{10,2},{11,3},{12,4},{13,5},{14,6},{15,7}} | collective-permute-start | bytes 1572872 | tf_op jit(solution)/shard_map/ppermute | solution.py:405
  112.3 6.4 %copy-start.3 = (bf16[4,8,2048]{2,1,0:T(8,128)(2,1)S(1)}, bf16[4,8,2048]{2,1,0:T(8,128)(2,1)}, u32[]{:S(2)}) copy-start(bf16[4,8,2048]{2,1,0:T(8,128)(2,1)} %param.13) | copy-start | bytes 393220
  112.3 11.4 %copy-start.5 = (f32[2,256]{1,0:T(2,128)S(1)}, f32[2,256]{1,0:T(2,128)}, u32[]{:S(2)}) copy-start(f32[2,256]{1,0:T(2,128)} %param.11) | copy-start | bytes 6148
  112.3 4.3 %collective-permute-start.23 = (bf16[1024,256]{1,0:T(8,128)(2,1)S(1)}, bf16[1024,256]{1,0:T(8,128)(2,1)S(1)}, u32[]{:S(2)}, u32[]{:S(2)}) collective-permute-start(bf16[1024,256]{1,0:T(8,128)(2,1)S(1)} %add.90.refs_0_), channel_id=1, source_target_pairs={{0,1},{1,0},{2,3},{3,2},{4,5},{5,4},{6,7},{7,6},{8,9},{9,8},{10,11... | collective-permute-start | bytes 1572872 | tf_op jit(solution)/shard_map/ppermute | solution.py:24
  112.4 20.9 %collective-permute-start.18 = (bf16[1024,256]{1,0:T(8,128)(2,1)S(1)}, bf16[1024,256]{1,0:T(8,128)(2,1)}, u32[]{:S(2)}, u32[]{:S(2)}) collective-permute-start(bf16[1024,256]{1,0:T(8,128)(2,1)S(1)} %collective-permute-done.11), channel_id=1, source_target_pairs={{16,24},{17,25},{18,26},{19,27},{20,28},{21,29},{22,30},{23,31}} | collective-permute-start | bytes 1572872 | tf_op jit(solution)/shard_map/ppermute | solution.py:404
  113.9 19.4 %collective-permute-start.19 = (bf16[1024,256]{1,0:T(8,128)(2,1)}, bf16[1024,256]{1,0:T(8,128)(2,1)}, u32[]{:S(2)}, u32[]{:S(2)}) collective-permute-start(bf16[1024,256]{1,0:T(8,128)(2,1)} %collective-permute-done.12), channel_id=1, source_target_pairs={{8,0},{9,1},{10,2},{11,3},{12,4},{13,5},{14,6},{15,7}} | collective-permute-start | bytes 1572872 | tf_op jit(solution)/shard_map/ppermute | solution.py:405
  118.2 1.4 collective-permute-start.24
  119.5 5.4 %collective-permute-start.25 = (f32[1,256]{1,0:T(1,128)S(1)}, f32[1,256]{1,0:T(1,128)S(1)}, u32[]{:S(2)}, u32[]{:S(2)}) collective-permute-start(f32[1,256]{1,0:T(1,128)S(1)} %max.36), channel_id=1, source_target_pairs={{0,8},{8,16},{16,24},{24,0},{1,9},{9,17},{17,25},{25,1},{2,10},{10... | collective-permute-start | bytes 3080 | tf_op jit(solution)/shard_map/ppermute | solution.py:24
  121.4 4.5 %collective-permute-start.26 = (f32[1,256]{1,0:T(1,128)S(1)}, f32[1,256]{1,0:T(1,128)S(1)}, u32[]{:S(2)}, u32[]{:S(2)}) collective-permute-start(f32[1,256]{1,0:T(1,128)S(1)} %max.36), channel_id=1, source_target_pairs={{0,16},{8,24},{16,0},{24,8},{1,17},{9,25},{17,1},{25,9},{2,18},{10... | collective-permute-start | bytes 3080 | tf_op jit(solution)/shard_map/ppermute | solution.py:24
  121.4 11.9 %collective-permute-start.27 = (f32[1,256]{1,0:T(1,128)S(1)}, f32[1,256]{1,0:T(1,128)S(1)}, u32[]{:S(2)}, u32[]{:S(2)}) collective-permute-start(f32[1,256]{1,0:T(1,128)S(1)} %max.36), channel_id=1, source_target_pairs={{0,24},{8,0},{16,8},{24,16},{1,25},{9,1},{17,9},{25,17},{2,26},{10... | collective-permute-start | bytes 3080 | tf_op jit(solution)/shard_map/ppermute | solution.py:24
  124.9 10.5 %collective-permute-start = (bf16[1,256,128]{2,1,0:T(8,128)(2,1)S(1)}, bf16[1,256,128]{2,1,0:T(8,128)(2,1)S(1)}, u32[]{:S(2)}, u32[]{:S(2)}) collective-permute-start(bf16[1,256,128]{2,1,0:T(8,128)(2,1)S(1)} %reshape.109), channel_id=1, source_target_pairs={{0,8},{8,16},{16,24},{24,0},{1,9},{9,17},{17,25},{25,1},{2,10},{10... | collective-permute-start | bytes 196616 | tf_op jit(solution)/shard_map/ppermute | solution.py:24
  125.9 9.6 %collective-permute-start.1 = (bf16[1,256,128]{2,1,0:T(8,128)(2,1)S(1)}, bf16[1,256,128]{2,1,0:T(8,128)(2,1)S(1)}, u32[]{:S(2)}, u32[]{:S(2)}) collective-permute-start(bf16[1,256,128]{2,1,0:T(8,128)(2,1)S(1)} %reshape.109), channel_id=1, source_target_pairs={{0,16},{8,24},{16,0},{24,8},{1,17},{9,25},{17,1},{25,9},{2,18},{10... | collective-permute-start | bytes 196616 | tf_op jit(solution)/shard_map/ppermute | solution.py:24
  133.2 4.3 %collective-permute-start.2 = (bf16[1,256,128]{2,1,0:T(8,128)(2,1)S(1)}, bf16[1,256,128]{2,1,0:T(8,128)(2,1)S(1)}, u32[]{:S(2)}, u32[]{:S(2)}) collective-permute-start(bf16[1,256,128]{2,1,0:T(8,128)(2,1)S(1)} %reshape.109), channel_id=1, source_target_pairs={{0,24},{8,0},{16,8},{24,16},{1,25},{9,1},{17,9},{25,17},{2,26},{10... | collective-permute-start | bytes 196616 | tf_op jit(solution)/shard_map/ppermute | solution.py:24
  133.3 13.2 %copy-start.4 = (f32[1,256]{1,0:T(1,128)}, f32[1,256]{1,0:T(1,128)S(1)}, u32[]{:S(2)}) copy-start(f32[1,256]{1,0:T(1,128)S(1)} %add_sqrt_fusion) | copy-start | bytes 3076
  134.6 10.2 %collective-permute-start.29 = (bf16[1024,256]{1,0:T(8,128)(2,1)S(1)}, bf16[1024,256]{1,0:T(8,128)(2,1)S(1)}, u32[]{:S(2)}, u32[]{:S(2)}) collective-permute-start(bf16[1024,256]{1,0:T(8,128)(2,1)S(1)} %add.93.refs_0_), channel_id=1, source_target_pairs={{0,1},{1,0},{2,3},{3,2},{4,5},{5,4},{6,7},{7,6},{8,9},{9,8},{10,11... | collective-permute-start | bytes 1572872 | tf_op jit(solution)/shard_map/ppermute | solution.py:24
  134.9 11.4 %collective-permute-start.28 = (bf16[1024,128]{1,0:T(8,128)(2,1)S(1)}, bf16[1024,128]{1,0:T(8,128)(2,1)S(1)}, u32[]{:S(2)}, u32[]{:S(2)}) collective-permute-start(bf16[1024,128]{1,0:T(8,128)(2,1)S(1)} %get-tuple-element.147), channel_id=1, source_target_pairs={{0,1},{1,0},{2,3},{3,2},{4,5},{5,4},{6,7},{7,6},{8,9},{9,8},{10,11... | collective-permute-start | bytes 786440 | tf_op jit(solution)/shard_map/ppermute | solution.py:24
  137.5 5.8 %copy-start.1 = (bf16[1024,8192]{1,0:T(8,128)(2,1)S(1)}, bf16[1024,8192]{1,0:T(8,128)(2,1)}, u32[]{:S(2)}) copy-start(bf16[1024,8192]{1,0:T(8,128)(2,1)} %get-tuple-element.75.left) | copy-start | bytes 50331652
  146.4 5.0 %collective-permute-start.30 = (bf16[1024,128]{1,0:T(8,128)(2,1)S(1)}, bf16[1024,128]{1,0:T(8,128)(2,1)S(1)}, u32[]{:S(2)}, u32[]{:S(2)}) collective-permute-start(bf16[1024,128]{1,0:T(8,128)(2,1)S(1)} %get-tuple-element.145), channel_id=1, source_target_pairs={{0,1},{1,0},{2,3},{3,2},{4,5},{5,4},{6,7},{7,6},{8,9},{9,8},{10,11... | collective-permute-start | bytes 786440 | tf_op jit(solution)/shard_map/ppermute | solution.py:24
  153.3 4.6 %collective-permute-start.31 = (bf16[272,128]{1,0:T(8,128)(2,1)S(1)}, bf16[272,128]{1,0:T(8,128)(2,1)S(1)}, u32[]{:S(2)}, u32[]{:S(2)}) collective-permute-start(bf16[272,128]{1,0:T(8,128)(2,1)S(1)} %get-tuple-element.116), channel_id=1, source_target_pairs={{0,24},{8,0},{16,8},{24,16},{1,25},{9,1},{17,9},{25,17},{2,26},{10... | collective-permute-start | bytes 208904 | tf_op jit(solution)/shard_map/ppermute | solution.py:24
  155.1 7.8 %collective-permute-start.32 = (bf16[272,128]{1,0:T(8,128)(2,1)S(1)}, bf16[272,128]{1,0:T(8,128)(2,1)S(1)}, u32[]{:S(2)}, u32[]{:S(2)}) collective-permute-start(bf16[272,128]{1,0:T(8,128)(2,1)S(1)} %get-tuple-element.117), channel_id=1, source_target_pairs={{0,16},{8,24},{16,0},{24,8},{1,17},{9,25},{17,1},{25,9},{2,18},{10... | collective-permute-start | bytes 208904 | tf_op jit(solution)/shard_map/ppermute | solution.py:24
  155.1 7.8 %collective-permute-start.33 = (bf16[272,128]{1,0:T(8,128)(2,1)S(1)}, bf16[272,128]{1,0:T(8,128)(2,1)S(1)}, u32[]{:S(2)}, u32[]{:S(2)}) collective-permute-start(bf16[272,128]{1,0:T(8,128)(2,1)S(1)} %get-tuple-element.118), channel_id=1, source_target_pairs={{0,8},{8,16},{16,24},{24,0},{1,9},{9,17},{17,25},{25,1},{2,10},{10... | collective-permute-start | bytes 208904 | tf_op jit(solution)/shard_map/ppermute | solution.py:24
  163.4 2.2 %collective-permute-start.34 = (bf16[4,8,1024]{2,1,0:T(8,128)(2,1)S(1)}, bf16[4,8,1024]{2,1,0:T(8,128)(2,1)S(1)}, u32[]{:S(2)}, u32[]{:S(2)}) collective-permute-start(bf16[4,8,1024]{2,1,0:T(8,128)(2,1)S(1)} %reshape.111), channel_id=1, source_target_pairs={{0,1},{1,0},{2,3},{3,2},{4,5},{5,4},{6,7},{7,6},{8,9},{9,8},{10,11... | collective-permute-start | bytes 196616 | tf_op jit(solution)/shard_map/ppermute | solution.py:24

commit v5 on v4

--- a/solution.py
+++ b/solution.py
@@ -4,13 +4,12 @@
 import jax.numpy as jnp
 from jax import lax
 from jax.experimental import pallas as pl
+from jax.experimental.layout import Layout, with_layout_constraint
 from jax.experimental.pallas import tpu as pltpu
 from jax.sharding import PartitionSpec as P
 
 
-KVH = 8
 HD = 128
-QH = 64
 PAGE = 32
 
 
@@ -41,9 +40,14 @@
     return [x[0]] + [shifted(x[k], "seq", -k) for k in range(1, n)]
 
 
-def load_kernel(owners, place, hidden, key_weight, value_weight, held, keys, values, arrived):
-    depth = key_weight.shape[0]
+def load_kernel(owners, place, hidden, *refs):
+    weights, (held, keys, values, taken, arrived, taken_arrived) = refs[:2], refs[2:]
+    depth = taken.shape[1]
     blocks = held.shape[1] // depth
+    takes = [
+        pltpu.make_async_copy(weight, taken.at[j], taken_arrived.at[j])
+        for j, weight in enumerate(weights)
+    ]
 
     def block(j):
         index = lax.rem(place[0] * owners + place[1] + j, blocks)
@@ -52,11 +56,15 @@
     def copy(j):
         return pltpu.make_async_copy(hidden.at[:, block(j)], held.at[:, block(j)], arrived.at[j])
 
-    for j in range(blocks):
+    copy(0).start()
+    for take in takes:
+        take.start()
+    for j in range(1, blocks):
         copy(j).start()
     copy(0).wait()
-    for weight, out in ((key_weight, keys), (value_weight, values)):
-        out[...] = jnp.dot(held[:, block(0)], weight[...], preferred_element_type=jnp.float32)
+    for j, out in enumerate((keys, values)):
+        takes[j].wait()
+        out[...] = jnp.dot(held[:, block(0)], taken[j], preferred_element_type=jnp.float32)
     for j in range(1, blocks):
         copy(j).wait()
 
@@ -72,12 +80,16 @@
         in_specs=[
             pl.BlockSpec(memory_space=pltpu.SMEM),
             pl.BlockSpec(memory_space=pltpu.HBM),
-            whole,
-            whole,
+            pl.BlockSpec(memory_space=pl.ANY),
+            pl.BlockSpec(memory_space=pl.ANY),
         ],
         out_specs=(whole,) * 3,
-        scratch_shapes=[pltpu.SemaphoreType.DMA((width // depth,))],
-        compiler_params=pltpu.CompilerParams(vmem_limit_bytes=36 * 2**20),
+        scratch_shapes=[
+            pltpu.VMEM((2, depth, columns), key_weight.dtype),
+            pltpu.SemaphoreType.DMA((width // depth,)),
+            pltpu.SemaphoreType.DMA((2,)),
+        ],
+        compiler_params=pltpu.CompilerParams(vmem_limit_bytes=30 * 2**20),
         cost_estimate=pl.CostEstimate(
             flops=4 * tokens * depth * columns,
             bytes_accessed=2 * tokens * width,
@@ -92,7 +104,10 @@
     weights, total = refs[:count], refs[count]
     out, held, arrived = refs[-3:]
     depth = held.shape[1]
-    copies = [pltpu.make_async_copy(weights[j], held.at[j], arrived.at[j]) for j in range(count)]
+    copies = [
+        pltpu.make_async_copy(weights[j].at[pl.ds(0, depth)], held.at[j], arrived.at[j])
+        for j in range(count)
+    ]
     for copy in copies:
         copy.start()
     out[...] = total[...]
@@ -109,9 +124,9 @@
             out[...] += jnp.dot(left[:, block], held[j], preferred_element_type=jnp.float32)
 
 
-def project(hidden, total, weights, place, hops, back, groups, owners):
+def project(hidden, total, weights, depth, place, hops, back, groups, owners):
     tokens = hidden.shape[0]
-    depth, columns = weights[0].shape
+    columns = weights[0].shape[1]
     count = len(weights)
     whole = pl.BlockSpec(memory_space=pltpu.VMEM)
     return pl.pallas_call(
@@ -140,35 +155,37 @@
     keys, probs, stats = refs[:parts], refs[parts], refs[parts + 1 : parts + 1 + slots]
     scores, tops, sums = refs[-3:]
     tokens = keys[0].shape[0]
-    scaled = (query[0].astype(jnp.float32) * smooth[...]).astype(jnp.bfloat16)
+    width = keys[0].shape[1]
+    requests = count.shape[1]
+    rows = scores.shape[0]
+    heads = query.shape[1] * query.shape[2] // (steps * requests * width)
+    per_line = query.shape[2] // width
+    raw = [
+        query[0][
+            (head // per_line) * steps * requests : (head // per_line + 1) * steps * requests,
+            (head % per_line) * width : (head % per_line + 1) * width,
+        ]
+        for head in range(heads)
+    ]
+    raw = jnp.concatenate(raw, axis=0)
+    scaled = (raw.astype(jnp.float32) * smooth[...]).astype(jnp.bfloat16)
     for p in range(parts):
         scores[:, p * tokens : (p + 1) * tokens] = lax.dot_general(
             scaled, keys[p][...], (((1,), (1,)), ((), ())), preferred_element_type=jnp.float32
         )
-    requests = count.shape[1]
-    rows = scores.shape[0]
-    group_rows = rows // (steps * requests)
-    pair = 2 if requests % 2 == 0 else 1
-    for first in range(0, requests, pair):
-        times = jnp.concatenate(
-            [
-                jnp.broadcast_to(count[0, first + a : first + a + 1, :], (group_rows, parts * tokens))
-                for a in range(pair)
-            ],
-            axis=0,
+    again = 2 if (rows // requests) % 2 == 0 else 1
+    times = jnp.concatenate([count[0]] * again, axis=0)
+    bias = jnp.where(times > 0.0, 0.0, NEGATIVE)
+    for start in range(0, rows, again * requests):
+        at = pl.ds(start, again * requests)
+        raw = scores[at, :] * scale + bias
+        top = jnp.max(raw, axis=1, keepdims=True)
+        counted = jnp.exp(raw - top) * times
+        probs[0, at, :] = counted.astype(jnp.bfloat16)
+        tops[at, :] = jnp.broadcast_to(top, (again * requests, 128))
+        sums[at, :] = jnp.broadcast_to(
+            jnp.sum(counted, axis=1, keepdims=True), (again * requests, 128)
         )
-        bias = jnp.where(times > 0.0, 0.0, NEGATIVE)
-        for step in range(steps):
-            start = (step * requests + first) * group_rows
-            at = pl.ds(start, pair * group_rows)
-            raw = scores[at, :] * scale + bias
-            top = jnp.max(raw, axis=1, keepdims=True)
-            counted = jnp.exp(raw - top) * times
-            probs[0, at, :] = counted.astype(jnp.bfloat16)
-            tops[at, :] = jnp.broadcast_to(top, (pair * group_rows, 128))
-            sums[at, :] = jnp.broadcast_to(
-                jnp.sum(counted, axis=1, keepdims=True), (pair * group_rows, 128)
-            )
     for slot in range(slots):
 
         @pl.when(pl.program_id(0) == slot)
@@ -178,8 +195,9 @@
 
 
 def score(groups, query, smooth, count, keys, steps, scale):
-    slots, rows, width = query.shape
-    tokens = keys[0].shape[0]
+    slots, packed, columns = query.shape
+    tokens, width = keys[0].shape
+    rows = packed * columns // width
     parts = len(keys)
     requests = count.shape[1]
     probs, *stats = pl.pallas_call(
@@ -190,7 +208,7 @@
             num_scalar_prefetch=1,
             grid=(slots,),
             in_specs=[
-                pl.BlockSpec((1, rows, width), lambda k, group: (k, 0, 0)),
+                pl.BlockSpec((1, packed, columns), lambda k, group: (k, 0, 0)),
                 pl.BlockSpec((1, width), lambda k, group: (0, 0)),
                 pl.BlockSpec((1, requests, parts * tokens), lambda k, group: (group[k], 0, 0)),
             ]
@@ -277,41 +295,44 @@
 
 def fresh_kernel(scale, query, smooth, new_keys, new_values, group_scale, summed, highest, total):
     steps, requests, width = new_keys.shape
-    group_rows = query.shape[0] // (steps * requests)
-    rows = requests * group_rows
-    scaled = (query[...].astype(jnp.float32) * smooth[...]).astype(jnp.bfloat16)
-    scaled = scaled.astype(jnp.float32)
-
-    def by_row(x):
+    lines = steps * requests
+
+    def by_line(x):
         x = x.astype(jnp.bfloat16).astype(jnp.float32)
-        spread = [jnp.broadcast_to(x[r : r + 1], (group_rows, width)) for r in range(requests)]
-        return jnp.concatenate(spread, axis=0)
+        return jnp.concatenate([x] * steps, axis=0)
 
     def clip(x, row):
         limit = group_scale[row : row + 1, :]
         return jnp.clip(x, -8.0 * limit, 7.0 * limit)
 
-    keys = [by_row(clip(new_keys[u] / smooth[...], 0)) for u in range(steps)]
-    values = [by_row(clip(new_values[u], 1)) for u in range(steps)]
-    for step in range(steps):
-        at = pl.ds(step * rows, rows)
-        mine = scaled[step * rows : (step + 1) * rows]
+    keys = [by_line(clip(new_keys[u] / smooth[...], 0)) for u in range(steps)]
+    values = [by_line(clip(new_values[u], 1)) for u in range(steps)]
+    line = lax.broadcasted_iota(jnp.int32, (lines, 1), 0)
+    seen = [line >= u * requests for u in range(steps)]
+    for head in range(query.shape[1] // width):
+        at = pl.ds(head * lines, lines)
+        mine = query[:, head * width : (head + 1) * width].astype(jnp.float32) * smooth[...]
+        mine = mine.astype(jnp.bfloat16).astype(jnp.float32)
         scores = [
-            jnp.sum(mine * keys[u], axis=1, keepdims=True) * scale for u in range(step + 1)
+            jnp.where(seen[u], jnp.sum(mine * keys[u], axis=1, keepdims=True) * scale, NEGATIVE)
+            for u in range(steps)
         ]
         top = functools.reduce(jnp.maximum, scores)
-        expd = [jnp.exp(score - top) for score in scores]
-        highest[at, :] = jnp.broadcast_to(top, (rows, width))
-        total[at, :] = jnp.broadcast_to(sum(expd), (rows, width))
+        expd = [jnp.where(seen[u], jnp.exp(scores[u] - top), 0.0) for u in range(steps)]
+        highest[at, :] = jnp.broadcast_to(top, (lines, width))
+        total[at, :] = jnp.broadcast_to(sum(expd), (lines, width))
         summed[at, :] = sum(
             e.astype(jnp.bfloat16).astype(jnp.float32) * value for e, value in zip(expd, values)
         )
 
 
 def fresh(query, smooth, new_keys, new_values, group_scale, scale):
+    lines, columns = query.shape
+    width = smooth.shape[1]
+    part = jax.ShapeDtypeStruct((lines * columns // width, width), jnp.float32)
     return pl.pallas_call(
         functools.partial(fresh_kernel, scale),
-        out_shape=(jax.ShapeDtypeStruct(query.shape, jnp.float32),) * 3,
+        out_shape=(part,) * 3,
         compiler_params=pltpu.CompilerParams(vmem_limit_bytes=16 * 2**20),
         name="fresh",
     )(query, smooth, new_keys, new_values, group_scale)
@@ -319,13 +340,14 @@
 
 def finish_kernel(slots, *refs):
     messages, (summed, highest, total, out) = refs[:slots], refs[slots:]
-    rows, width = out.shape
+    rows, width = summed.shape
+    lines = out.shape[0]
+    tails = [message[rows:, :].astype(jnp.float32) for message in messages]
     pieces = rows // width
-    tails = [message[rows:, :].astype(jnp.float32) for message in messages]
 
     def column(slot, piece, which):
-        lines = [tails[slot][2 * (j * pieces + piece) + which :][:1] for j in range(3)]
-        return jnp.transpose(jnp.broadcast_to(lines[0] + lines[1] + lines[2], (width, width)))
+        row = [tails[slot][2 * (j * pieces + piece) + which :][:1] for j in range(3)]
+        return jnp.transpose(jnp.broadcast_to(row[0] + row[1] + row[2], (width, width)))
 
     for piece in range(pieces):
         at = pl.ds(piece * width, width)
@@ -337,15 +359,18 @@
         top = functools.reduce(jnp.maximum, [part[1] for part in parts])
         shares = [jnp.exp(part[1] - top) for part in parts]
         norm = sum(share * part[2] for share, part in zip(shares, parts))
-        out[at, :] = (sum(share * part[0] for share, part in zip(shares, parts)) / norm).astype(
-            out.dtype
-        )
-
-
-def finish(messages, own):
+        merged = sum(share * part[0] for share, part in zip(shares, parts)) / norm
+        merged = merged.astype(out.dtype)
+        for first in range(0, width, lines):
+            head = (piece * width + first) // lines
+            out[:, head * width : (head + 1) * width] = merged[first : first + lines]
+
+
+def finish(messages, own, lines):
+    rows, width = own[0].shape
     return pl.pallas_call(
         functools.partial(finish_kernel, len(messages)),
-        out_shape=jax.ShapeDtypeStruct(own[0].shape, jnp.bfloat16),
+        out_shape=jax.ShapeDtypeStruct((lines, rows * width // lines), jnp.bfloat16),
         compiler_params=pltpu.CompilerParams(vmem_limit_bytes=16 * 2**20),
         name="finish",
     )(*messages, *own)
@@ -422,6 +447,7 @@
                 hidden,
                 totals[name],
                 ready,
+                depth,
                 early[0],
                 tuple(hops for hops, _ in here),
                 k,
@@ -429,12 +455,14 @@
                 owners,
             )
 
-    moving["k"], moving["v"] = (key_weight,) * 2, (value_weight,) * 2
+    depth = key_weight.shape[0]
+    moving["k"], moving["v"] = (key_weight,) * 2, (jnp.concatenate([value_weight, raw_query]),) * 2
+    lefts, rights = [None] * groups, [None] * groups
     for name in names:
         send(name, 1)
-    queries = from_all(raw_query, "seq")
     early, first = lax.optimization_barrier((early, (key_weight, value_weight)))
     hidden, totals["k"], totals["v"] = load(hidden, *first, early[0], owners)
+    moving["v"] = (value_weight,) * 2
     for name in names:
         absorb(name, 0)
     for hop in range(1, groups):
@@ -447,6 +475,8 @@
             if hop < groups - 1:
                 send(name, hop + 1)
             absorb(name, hop)
+        lefts[hop], rights[groups - hop] = (block[depth:] for block in moving["v"])
+    queries = [raw_query] + [lefts[k] + rights[k] for k in range(1, groups)]
     return totals["k"], totals["v"], smooth, queries, early
 
 
@@ -455,7 +485,6 @@
 ):
     tokens = hidden.shape[0]
     columns = key_weight.shape[1]
-    group_size = QH // KVH
     groups, owners = lax.axis_size("seq"), lax.axis_size("rep")
     my_group, my_owner = lax.axis_index("seq"), lax.axis_index("rep")
     assert columns // HD == owners
@@ -463,19 +492,18 @@
     step_count, per_group = decode_query.shape[:2]
 
     owner_is = [my_owner == owner for owner in range(owners)]
-    raw_query = my_part(decode_query, 2, owner_is).reshape(1, -1, HD)
+    own_query = my_part(decode_query, 2, owner_is).reshape(step_count * per_group, -1)
+    raw_query = jnp.concatenate(jnp.split(own_query, own_query.shape[1] // columns, axis=1))
 
     first_pages = [
         (my_group * owners + (my_owner - k) % owners) * pages_dev for k in range(owners)
     ]
-    counts = token_counts(page_table, lengths, first_pages, pages_dev)
-    my_kv = my_part(new_kv, 3, owner_is).astype(jnp.float32)
     early = (
         jnp.stack([my_group, my_owner]),
         owner_is,
-        counts.reshape(groups, per_group, -1),
+        first_pages,
         (my_group - jnp.arange(groups, dtype=jnp.int32)) % groups,
-        (my_kv[:, :, 0], my_kv[:, :, 1], my_part(group_scale, 1, owner_is)),
+        own_query,
     )
     if groups > SHORT:
         raw_keys, raw_values = (
@@ -492,7 +520,11 @@
         raw_keys, raw_values, smooth, queries, early = line_project(
             hidden, key_weight, value_weight, raw_query, early
         )
-    _, owner_is, counts, group_at, my_new = early
+    _, owner_is, first_pages, group_at, own_query = early
+    counts = token_counts(page_table, lengths, first_pages, pages_dev)
+    counts = counts.reshape(groups, per_group, -1)
+    my_kv = my_part(new_kv, 3, owner_is).astype(jnp.float32)
+    my_new = (my_kv[:, :, 0], my_kv[:, :, 1], my_part(group_scale, 1, owner_is))
 
     def by_head(x):
         return [my_part(x, 1, owner_is)] + [
@@ -507,7 +539,7 @@
     score_scale = HD ** (-0.5)
     probs, stats = score(
         group_at,
-        jnp.concatenate(queries),
+        jnp.stack(queries),
         my_smooth,
         counts,
         head_keys,
@@ -517,13 +549,13 @@
     messages = weigh(probs, by_head(values), stats)
 
     messages, keys, values, late = lax.optimization_barrier(
-        (messages, keys, values, (raw_query, my_smooth))
+        (messages, keys, values, (own_query, my_smooth))
     )
     messages = to_groups(messages)
-    kv_cache = jnp.stack([keys, values], axis=1)
-    own = fresh(late[0].reshape(-1, HD), late[1], *my_new, score_scale)
+    kv_cache = with_layout_constraint(jnp.stack([keys, values], axis=1), Layout((0, 1, 2)))
+    own = fresh(late[0], late[1], *my_new, score_scale)
     messages, kv_cache, own = lax.optimization_barrier((messages, kv_cache, own))
-    attention = finish(messages, own).reshape(step_count, per_group, group_size * HD)
+    attention = finish(messages, own, step_count * per_group)
     by_owner = from_all(attention, "rep")
     attention = jnp.concatenate(
         [
@@ -534,8 +566,8 @@
             )
             for head in range(owners)
         ],
-        axis=2,
-    )
+        axis=1,
+    ).reshape(decode_query.shape)
     return (kv_cache, smoothing, attention)
 
 

time: 167 us -> 135 us (0.81)
  local copies, waits for them, and re-layouts: 15.5 us -> 4.86 us
  Pallas kernels: 42.7 us -> 34.2 us
  waiting for transfers between devices: 66.5 us -> 59.2 us
  starting transfers between devices: 32.9 us -> 28.2 us
    unnamed x21 -> x17, local copies, waits for them, and re-layouts: 14.7 us -> 3.2 us
    pallas_call x1, Pallas kernels: 12.8 us -> 6.57 us  [load(): pl.pallas_call(functools.partial(load_kernel, owners), out_shape=(jax.Sha...]
    ppermute x6, waiting for transfers between devices: 42.2 us -> 37 us  [send(): lax.ppermute(right, 'seq', [(i, i - 1) for i in range(1, groups - hop + 1)])]
    ppermute x23 -> x20, starting transfers between devices: 12.7 us -> 9.3 us  [shifted(): return lax.ppermute(x, axis, [(i, (i + k) % n) for i in range(n)])]
    ppermute x23 -> x20, waiting for transfers between devices: 16.7 us -> 13.5 us  [shifted(): return lax.ppermute(x, axis, [(i, (i + k) % n) for i in range(n)])]
    another operation x1 -> x5, other arithmetic: 0.1 us -> 3.26 us  [the longest x1 3.19 us: on_device(): jnp.stack([keys, values], axis=1)]
    add x4, other arithmetic: 2.78 us -> 0.57 us  [absorb(): here = [((-hop, hop), left + right)]]
    pallas_call x14, Pallas kernels: 22.5 us -> 20.4 us  [project(): pl.pallas_call(functools.partial(project_kernel, hops, back, groups, owne...]
  transfers between devices with their start and end apart: 35 -> 32, of which waited for: 12 -> 13; matrix products, arithmetic and copies ran while one was open for 5% -> 5% of each run, Pallas kernels for 24% -> 24%
where the time goes in v5:
time: 135 us
  waiting for transfers between devices  59.2 us (44%)
  Pallas kernels  34.2 us (25%)
  starting transfers between devices  28.2 us (21%)
  other arithmetic  6.68 us (5%)
  local copies, waits for them, and re-layouts  4.86 us (4%)
    ppermute x6, waiting for transfers between devices, send(): lax.ppermute(right, 'seq', [(i, i - 1) for i in range(1, groups - hop + 1)])  37 us
    pallas_call x14, Pallas kernels, project(): pl.pallas_call(functools.partial(project_kernel, hops, back, groups, owne...  20.4 us
    ppermute x20, waiting for transfers between devices, shifted(): return lax.ppermute(x, axis, [(i, (i + k) % n) for i in range(n)])  13.5 us
    ppermute x6, starting transfers between devices, send(): lax.ppermute(left, 'seq', [(i, i + 1) for i in range(hop - 1, groups - 1)])  10.9 us
    ppermute x20, starting transfers between devices, shifted(): return lax.ppermute(x, axis, [(i, (i + k) % n) for i in range(n)])  9.3 us
    ppermute x6, waiting for transfers between devices, send(): lax.ppermute(left, 'seq', [(i, i + 1) for i in range(hop - 1, groups - 1)])  8.8 us
    ppermute x6, starting transfers between devices, send(): lax.ppermute(right, 'seq', [(i, i - 1) for i in range(1, groups - hop + 1)])  7.93 us
    pallas_call x1, Pallas kernels, load(): pl.pallas_call(functools.partial(load_kernel, owners), out_shape=(jax.Sha...  6.57 us
  transfers between devices with their start and end apart: 32, of which 13 were waited for; matrix products, arithmetic and copies ran while one was open for 5% of the time, Pallas kernels for 24%

profile of v5, /device:TPU:0, one launch (start us, length us, event | category | flops | bytes accessed | tf_op | source)
XLA Modules:
  0.0 134.9 jit_solution(13893684958427988380)
XLA Ops:
  0.6 0.6 collective-permute-start.4
  1.2 4.5 %collective-permute-start.2 = (bf16[1024,256]{1,0:T(8,128)(2,1)}, bf16[1024,256]{1,0:T(8,128)(2,1)S(1)}, u32[]{:S(2)}, u32[]{:S(2)}) collective-permute-start(bf16[1024,256]{1,0:T(8,128)(2,1)} %refs_0_), channel_id=1, source_target_pairs={{0,8},{8,16},{16,24},{1,9},{9,17},{17,25},{2,10},{10,18},{18,26},{... | collective-permute-start | bytes 1572872 | tf_op jit(solution)/shard_map/ppermute | solution.py:429
  5.7 1.3 collective-permute-start.3
  7.0 0.3 collective-permute-start.5
  7.3 1.1 constant_dynamic-update-slice_fusion.4
  8.4 0.9 select_bitcast_fusion.query
  9.4 1.0 copy-done
  10.4 1.0 copy-done.1
  11.4 6.6 %load.1 = (bf16[1024,8192]{1,0:T(8,128)(2,1)S(1)}, f32[1024,256]{1,0:T(8,128)S(1)}, f32[1024,256]{1,0:T(8,128)S(1)}) custom-call(s32[2]{0:T(128)S(1)} %pad_add_fusion.place, bf16[1024,8192]{1,0:T(8,128)(2,1)} %hidden.1, bf16[1024,256]{1,0:T(8,128)(2,1)S(1)} %copy-done.1, bf16[1024,256]{1,0:T(8,128)(2,1)S(1)} %copy-done), custom_call_target="tpu_custom_call" | custom-call | flops 1073741824 | bytes 16777216 | tf_op jit(solution)/shard_map/load/pallas_call | solution.py:77
  18.1 1.4 %project.15.refs_2_ = f32[1024,256]{1,0:T(8,128)S(1)} custom-call(s32[2]{0:T(128)S(1)} %pad_add_fusion.place, bf16[1024,8192]{1,0:T(8,128)(2,1)S(1)} %get-tuple-element.73.left, bf16[1024,256]{1,0:T(8,128)(2,1)S(1)} %collective-permute-done.5.refs_0_, f32[1024,256]{1,0:T(8,128)S(1)} %get-tuple-element.75.refs_1_), custom_call_target="tpu_custom_call", output_to_operand_aliasing={{}: (3, {})} | custom-call | flops 536870912 | bytes 4718592 | tf_op jit(solution)/shard_map/project/pallas_call | solution.py:132
  19.5 1.4 %project.14.refs_2_ = f32[1024,256]{1,0:T(8,128)S(1)} custom-call(s32[2]{0:T(128)S(1)} %pad_add_fusion.place, bf16[1024,8192]{1,0:T(8,128)(2,1)S(1)} %get-tuple-element.73.left, bf16[1024,256]{1,0:T(8,128)(2,1)S(1)} %collective-permute-done.4.refs_0_, f32[1024,256]{1,0:T(8,128)S(1)} %get-tuple-element.74.refs_1_), custom_call_target="tpu_custom_call", output_to_operand_aliasing={{}: (3, {})} | custom-call | flops 536870912 | bytes 4718592 | tf_op jit(solution)/shard_map/project/pallas_call | solution.py:132
  21.0 0.9 collective-permute-done.3.refs_1_
  21.9 0.5 collective-permute-start.7
  22.4 3.7 %collective-permute-start = (bf16[1152,256]{1,0:T(8,128)(2,1)S(1)}, bf16[1152,256]{1,0:T(8,128)(2,1)S(1)}, u32[]{:S(2)}, u32[]{:S(2)}) collective-permute-start(bf16[1152,256]{1,0:T(8,128)(2,1)S(1)} %constant_dynamic-update-slice_fusion), channel_id=1, source_target_pairs={{0,8},{8,16},{16,24},{1,9},{9,17},{17,25},{2,10},{10,18},{18,26},{... | collective-permute-start | bytes 1769480 | tf_op jit(solution)/shard_map/ppermute | solution.py:429
  26.0 1.3 collective-permute-start.1
  27.3 1.5 %project.16.refs_2_ = f32[1024,256]{1,0:T(8,128)S(1)} custom-call(s32[2]{0:T(128)S(1)} %pad_add_fusion.place, bf16[1024,8192]{1,0:T(8,128)(2,1)S(1)} %get-tuple-element.73.left, bf16[1024,256]{1,0:T(8,128)(2,1)S(1)} %collective-permute-done.2.refs_0_, bf16[1024,256]{1,0:T(8,128)(2,1)S(1)} %collective-permute-done.3.refs_1_, ...), custom_call_target="tpu_custom_call", output_to_operand_aliasing={{}: (4, {})} | custom-call | flops 1073741824 | bytes 7340032 | tf_op jit(solution)/shard_map/project/pallas_call | solution.py:132
  28.9 1.5 %project.17.refs_1_ = f32[1024,256]{1,0:T(8,128)S(1)} custom-call(s32[2]{0:T(128)S(1)} %pad_add_fusion.place, bf16[1024,8192]{1,0:T(8,128)(2,1)S(1)} %get-tuple-element.73.left, bf16[1024,256]{1,0:T(8,128)(2,1)S(1)} %collective-permute-done.6.refs_0_, bf16[1024,256]{1,0:T(8,128)(2,1)S(1)} %collective-permute-done.7.refs_1_, ...), custom_call_target="tpu_custom_call", output_to_operand_aliasing={{}: (4, {})} | custom-call | flops 1073741824 | bytes 7340032 | tf_op jit(solution)/shard_map/project/pallas_call | solution.py:132
  30.4 8.8 %collective-permute-done.refs_0_ = bf16[1152,256]{1,0:T(8,128)(2,1)S(1)} collective-permute-done((bf16[1152,256]{1,0:T(8,128)(2,1)S(1)}, bf16[1152,256]{1,0:T(8,128)(2,1)S(1)}, u32[]{:S(2)}, u32[]{:S(2)}) %collective-permute-start) | collective-permute-done | bytes 589856 | tf_op jit(solution)/shard_map/ppermute | solution.py:429
  39.2 4.1 %collective-permute-done.1.refs_1_ = bf16[1152,256]{1,0:T(8,128)(2,1)S(1)} collective-permute-done((bf16[1152,256]{1,0:T(8,128)(2,1)S(1)}, bf16[1152,256]{1,0:T(8,128)(2,1)S(1)}, u32[]{:S(2)}, u32[]{:S(2)}) %collective-permute-start.1) | collective-permute-done | bytes 589856 | tf_op jit(solution)/shard_map/ppermute | solution.py:430
  43.3 0.5 collective-permute-start.13
  43.8 0.7 collective-permute-start.10
  44.6 1.3 collective-permute-start.11
  46.0 0.7 collective-permute-start.8
  46.7 1.5 %project.18.refs_2_ = f32[1024,256]{1,0:T(8,128)S(1)} custom-call(s32[2]{0:T(128)S(1)} %pad_add_fusion.place, bf16[1024,8192]{1,0:T(8,128)(2,1)S(1)} %get-tuple-element.73.left, bf16[1152,256]{1,0:T(8,128)(2,1)S(1)} %collective-permute-done.refs_0_, bf16[1152,256]{1,0:T(8,128)(2,1)S(1)} %collective-permute-done.1.refs_1_, ...), custom_call_target="tpu_custom_call", output_to_operand_aliasing={{}: (4, {})} | custom-call | flops 1073741824 | bytes 7340032 | tf_op jit(solution)/shard_map/project/pallas_call | solution.py:132
  48.2 1.3 collective-permute-start.9
  49.6 1.5 %project.19.refs_1_ = f32[1024,256]{1,0:T(8,128)S(1)} custom-call(s32[2]{0:T(128)S(1)} %pad_add_fusion.place, bf16[1024,8192]{1,0:T(8,128)(2,1)S(1)} %get-tuple-element.73.left, bf16[1152,256]{1,0:T(8,128)(2,1)S(1)} %collective-permute-done.12.refs_0_, bf16[1152,256]{1,0:T(8,128)(2,1)S(1)} %collective-permute-done.13.refs_1_, ...), custom_call_target="tpu_custom_call", output_to_operand_aliasing={{}: (4, {})} | custom-call | flops 1073741824 | bytes 7340032 | tf_op jit(solution)/shard_map/project/pallas_call | solution.py:132
  51.1 12.5 %collective-permute-done.11 = bf16[1024,256]{1,0:T(8,128)(2,1)S(1)} collective-permute-done((bf16[1024,256]{1,0:T(8,128)(2,1)S(1)}, bf16[1024,256]{1,0:T(8,128)(2,1)S(1)}, u32[]{:S(2)}, u32[]{:S(2)}) %collective-permute-start.11) | collective-permute-done | bytes 524320 | tf_op jit(solution)/shard_map/ppermute | solution.py:430
  63.8 0.6 convert_reduce_fusion
  64.5 1.4 %project.20.refs_1_ = f32[1024,256]{1,0:T(8,128)S(1)} custom-call(s32[2]{0:T(128)S(1)} %pad_add_fusion.place, bf16[1024,8192]{1,0:T(8,128)(2,1)S(1)} %get-tuple-element.73.left, bf16[1024,256]{1,0:T(8,128)(2,1)S(1)} %add.90.refs_0_, f32[1024,256]{1,0:T(8,128)S(1)} %project.17.refs_1_), custom_call_target="tpu_custom_call", output_to_operand_aliasing={{}: (3, {})} | custom-call | flops 536870912 | bytes 4718592 | tf_op jit(solution)/shard_map/project/pallas_call | solution.py:132
  65.9 1.4 %project.21.refs_1_ = f32[1024,256]{1,0:T(8,128)S(1)} custom-call(s32[2]{0:T(128)S(1)} %pad_add_fusion.place, bf16[1024,8192]{1,0:T(8,128)(2,1)S(1)} %get-tuple-element.73.left, bf16[1024,256]{1,0:T(8,128)(2,1)S(1)} %collective-permute-done.14.refs_0_, f32[1024,256]{1,0:T(8,128)S(1)} %project.20.refs_1_), custom_call_target="tpu_custom_call", output_to_operand_aliasing={{}: (3, {})} | custom-call | flops 536870912 | bytes 4718592 | tf_op jit(solution)/shard_map/project/pallas_call | solution.py:132
  67.4 7.9 %collective-permute-done.9 = bf16[1152,256]{1,0:T(8,128)(2,1)S(1)} collective-permute-done((bf16[1152,256]{1,0:T(8,128)(2,1)S(1)}, bf16[1152,256]{1,0:T(8,128)(2,1)S(1)}, u32[]{:S(2)}, u32[]{:S(2)}) %collective-permute-start.9) | collective-permute-done | bytes 589856 | tf_op jit(solution)/shard_map/ppermute | solution.py:430
  75.5 0.7 collective-permute-start.17
  76.2 1.5 %collective-permute-start.18 = (bf16[1024,256]{1,0:T(8,128)(2,1)S(1)}, bf16[1024,256]{1,0:T(8,128)(2,1)S(1)}, u32[]{:S(2)}, u32[]{:S(2)}) collective-permute-start(bf16[1024,256]{1,0:T(8,128)(2,1)S(1)} %collective-permute-done.11), channel_id=1, source_target_pairs={{8,0},{9,1},{10,2},{11,3},{12,4},{13,5},{14,6},{15,7}} | collective-permute-start | bytes 1572872 | tf_op jit(solution)/shard_map/ppermute | solution.py:430
  77.7 0.2 fusion.2
  77.9 1.4 %project.22.refs_1_ = f32[1024,256]{1,0:T(8,128)S(1)} custom-call(s32[2]{0:T(128)S(1)} %pad_add_fusion.place, bf16[1024,8192]{1,0:T(8,128)(2,1)S(1)} %get-tuple-element.73.left, bf16[1152,256]{1,0:T(8,128)(2,1)S(1)} %add.91.refs_0_, f32[1024,256]{1,0:T(8,128)S(1)} %project.19.refs_1_), custom_call_target="tpu_custom_call", output_to_operand_aliasing={{}: (3, {})} | custom-call | flops 536870912 | bytes 4718592 | tf_op jit(solution)/shard_map/project/pallas_call | solution.py:132
  79.4 1.4 %project.23.refs_1_ = f32[1024,256]{1,0:T(8,128)S(1)} custom-call(s32[2]{0:T(128)S(1)} %pad_add_fusion.place, bf16[1024,8192]{1,0:T(8,128)(2,1)S(1)} %get-tuple-element.73.left, bf16[1152,256]{1,0:T(8,128)(2,1)S(1)} %collective-permute-done.19.refs_0_, f32[1024,256]{1,0:T(8,128)S(1)} %project.22.refs_1_), custom_call_target="tpu_custom_call", output_to_operand_aliasing={{}: (3, {})} | custom-call | flops 536870912 | bytes 4718592 | tf_op jit(solution)/shard_map/project/pallas_call | solution.py:132
  80.8 11.6 %collective-permute-done.18 = bf16[1024,256]{1,0:T(8,128)(2,1)S(1)} collective-permute-done((bf16[1024,256]{1,0:T(8,128)(2,1)S(1)}, bf16[1024,256]{1,0:T(8,128)(2,1)S(1)}, u32[]{:S(2)}, u32[]{:S(2)}) %collective-permute-start.18) | collective-permute-done | bytes 524320 | tf_op jit(solution)/shard_map/ppermute | solution.py:430
  92.6 0.2 fusion.1.count
  92.9 0.7 collective-permute-start.15
  93.6 1.3 collective-permute-start.16
  94.9 1.4 %project.24.refs_1_ = f32[1024,256]{1,0:T(8,128)S(1)} custom-call(s32[2]{0:T(128)S(1)} %pad_add_fusion.place, bf16[1024,8192]{1,0:T(8,128)(2,1)S(1)} %get-tuple-element.73.left, bf16[1024,256]{1,0:T(8,128)(2,1)S(1)} %add.92.refs_0_, f32[1024,256]{1,0:T(8,128)S(1)} %project.21.refs_1_), custom_call_target="tpu_custom_call", output_to_operand_aliasing={{}: (3, {})} | custom-call | flops 536870912 | bytes 4718592 | tf_op jit(solution)/shard_map/project/pallas_call | solution.py:132
  96.3 1.4 %project.25 = f32[1024,256]{1,0:T(8,128)S(1)} custom-call(s32[2]{0:T(128)S(1)} %pad_add_fusion.place, bf16[1024,8192]{1,0:T(8,128)(2,1)S(1)} %get-tuple-element.73.left, bf16[1024,256]{1,0:T(8,128)(2,1)S(1)} %collective-permute-done.20.refs_0_, f32[1024,256]{1,0:T(8,128)S(1)} %project.24.refs_1_), custom_call_target="tpu_custom_call", output_to_operand_aliasing={{}: (3, {})} | custom-call | flops 536870912 | bytes 4718592 | tf_op jit(solution)/shard_map/project/pallas_call | solution.py:132
  97.9 0.6 collective-permute-start.21
  98.4 0.8 collective-permute-done.21
  99.2 1.1 collective-permute-start.22
  100.4 2.7 %collective-permute-start.24 = (f32[1,256]{1,0:T(1,128)S(1)}, f32[1,256]{1,0:T(1,128)S(1)}, u32[]{:S(2)}, u32[]{:S(2)}) collective-permute-start(f32[1,256]{1,0:T(1,128)S(1)} %max.36), channel_id=1, source_target_pairs={{0,24},{8,0},{16,8},{24,16},{1,25},{9,1},{17,9},{25,17},{2,26},{10... | collective-permute-start | bytes 3080 | tf_op jit(solution)/shard_map/ppermute | solution.py:23
  103.1 1.5 %collective-permute-done.22 = f32[1,256]{1,0:T(1,128)S(1)} collective-permute-done((f32[1,256]{1,0:T(1,128)S(1)}, f32[1,256]{1,0:T(1,128)S(1)}, u32[]{:S(2)}, u32[]{:S(2)}) %collective-permute-start.22) | collective-permute-done | bytes 1056 | tf_op jit(solution)/shard_map/ppermute | solution.py:23
  104.6 0.2 collective-permute-done.23
  104.8 6.5 %collective-permute-done.24 = f32[1,256]{1,0:T(1,128)S(1)} collective-permute-done((f32[1,256]{1,0:T(1,128)S(1)}, f32[1,256]{1,0:T(1,128)S(1)}, u32[]{:S(2)}, u32[]{:S(2)}) %collective-permute-start.24) | collective-permute-done | bytes 1056 | tf_op jit(solution)/shard_map/ppermute | solution.py:23
  111.8 0.6 collective-permute-start.25
  112.4 1.4 %project.26.refs_1_ = f32[1024,256]{1,0:T(8,128)S(1)} custom-call(s32[2]{0:T(128)S(1)} %pad_add_fusion.place, bf16[1024,8192]{1,0:T(8,128)(2,1)S(1)} %get-tuple-element.73.left, bf16[1152,256]{1,0:T(8,128)(2,1)S(1)} %add.105.refs_0_, f32[1024,256]{1,0:T(8,128)S(1)} %project.23.refs_1_), custom_call_target="tpu_custom_call", output_to_operand_aliasing={{}: (3, {})} | custom-call | flops 536870912 | bytes 4718592 | tf_op jit(solution)/shard_map/project/pallas_call | solution.py:132
  113.9 1.4 %project.27 = f32[1024,256]{1,0:T(8,128)S(1)} custom-call(s32[2]{0:T(128)S(1)} %pad_add_fusion.place, bf16[1024,8192]{1,0:T(8,128)(2,1)S(1)} %get-tuple-element.73.left, bf16[1152,256]{1,0:T(8,128)(2,1)S(1)} %collective-permute-done.26.refs_0_, f32[1024,256]{1,0:T(8,128)S(1)} %project.26.refs_1_), custom_call_target="tpu_custom_call", output_to_operand_aliasing={{}: (3, {})} | custom-call | flops 536870912 | bytes 4718592 | tf_op jit(solution)/shard_map/project/pallas_call | solution.py:132
  115.6 4.7 %score.1 = (bf16[4,256,2048]{2,1,0:T(8,128)(2,1)S(1)}, f32[2,256]{1,0:T(2,128)S(1)}, f32[2,256]{1,0:T(2,128)S(1)}, f32[2,256]{1,0:T(2,128)S(1)}, f32[2,256]{1,0:T(2,128)S(1)}) custom-call(s32[4]{0:T(128)S(1)} %and_select_fusion.2.group, bf16[4,128,256]{2,1,0:T(8,128)(2,1)S(1)} %pad_maximum_fusion.1.query, f32[1,128]{1,0:T(1,128)S(1)} %broadcast_select_fusion.6.smooth, ...), custom_call_target="tpu_custom_call" | custom-call | flops 536870912 | bytes 4194304 | tf_op jit(solution)/shard_map/score/pallas_call | solution.py:203
  120.3 1.8 %weigh.1 = (bf16[272,128]{1,0:T(8,128)(2,1)S(1)}, bf16[272,128]{1,0:T(8,128)(2,1)S(1)}, bf16[272,128]{1,0:T(8,128)(2,1)S(1)}, bf16[272,128]{1,0:T(8,128)(2,1)S(1)}) custom-call(bf16[4,256,2048]{2,1,0:T(8,128)(2,1)S(1)} %get-tuple-element.105.probs, bf16[1024,128]{1,0:T(8,128)(2,1)S(1)} %get-tuple-element.138.refs_0_, ...), custom_call_target="tpu_custom_call" | custom-call | flops 536870912 | bytes 4194304 | tf_op jit(solution)/shard_map/weigh/pallas_call | solution.py:278
  122.2 0.8 copy.35
  123.0 0.8 copy.36
  124.0 1.9 %collective-permute-start.30 = (bf16[272,128]{1,0:T(8,128)(2,1)S(1)}, bf16[272,128]{1,0:T(8,128)(2,1)S(1)}, u32[]{:S(2)}, u32[]{:S(2)}) collective-permute-start(bf16[272,128]{1,0:T(8,128)(2,1)S(1)} %get-tuple-element.119), channel_id=1, source_target_pairs={{0,8},{8,16},{16,24},{24,0},{1,9},{9,17},{17,25},{25,1},{2,10},{10... | collective-permute-start | bytes 208904 | tf_op jit(solution)/shard_map/ppermute | solution.py:23
  125.9 3.2 %pad_maximum_fusion = bf16[1024,2,256]{2,1,0:T(2,128)(2,1)} fusion(bf16[1024,1,256]{2,1,0:T(2,128)(2,1)S(1)} %copy.36, bf16[1024,1,256]{2,1,0:T(2,128)(2,1)S(1)} %copy.35), kind=kLoop, calls=%fused_computation.3 | loop fusion | flops 2097152 | bytes 2097152 | tf_op jit(solution)/shard_map/stack | solution.py:555
  129.1 0.2 fresh.1
  129.3 0.3 collective-permute-done.28.refs_1_
  129.6 2.9 %collective-permute-done.29.refs_2_ = bf16[272,128]{1,0:T(8,128)(2,1)S(1)} collective-permute-done((bf16[272,128]{1,0:T(8,128)(2,1)S(1)}, bf16[272,128]{1,0:T(8,128)(2,1)S(1)}, u32[]{:S(2)}, u32[]{:S(2)}) %collective-permute-start.29) | collective-permute-done | bytes 69664 | tf_op jit(solution)/shard_map/ppermute | solution.py:23
  132.4 0.4 finish.1
  133.0 1.2 collective-permute-done.31
  134.2 0.7 maximum_bitcast_fusion
  (75 shorter events, 2.1 us)
Async XLA Ops:
  0.6 18.9 %collective-permute-start.4 = (bf16[1024,256]{1,0:T(8,128)(2,1)}, bf16[1024,256]{1,0:T(8,128)(2,1)S(1)}, u32[]{:S(2)}, u32[]{:S(2)}) collective-permute-start(bf16[1024,256]{1,0:T(8,128)(2,1)} %refs_0_), channel_id=1, source_target_pairs={{0,1},{1,0},{2,3},{3,2},{4,5},{5,4},{6,7},{7,6},{8,9},{9,8},{10,11... | collective-permute-start | bytes 1572872 | tf_op jit(solution)/shard_map/ppermute | solution.py:23
  1.2 19.8 %collective-permute-start.2 = (bf16[1024,256]{1,0:T(8,128)(2,1)}, bf16[1024,256]{1,0:T(8,128)(2,1)S(1)}, u32[]{:S(2)}, u32[]{:S(2)}) collective-permute-start(bf16[1024,256]{1,0:T(8,128)(2,1)} %refs_0_), channel_id=1, source_target_pairs={{0,8},{8,16},{16,24},{1,9},{9,17},{17,25},{2,10},{10,18},{18,26},{... | collective-permute-start | bytes 1572872 | tf_op jit(solution)/shard_map/ppermute | solution.py:429
  5.7 16.1 %collective-permute-start.3 = (bf16[1024,256]{1,0:T(8,128)(2,1)}, bf16[1024,256]{1,0:T(8,128)(2,1)S(1)}, u32[]{:S(2)}, u32[]{:S(2)}) collective-permute-start(bf16[1024,256]{1,0:T(8,128)(2,1)} %refs_0_), channel_id=1, source_target_pairs={{8,0},{16,8},{24,16},{9,1},{17,9},{25,17},{10,2},{18,10},{26,18},{... | collective-permute-start | bytes 1572872 | tf_op jit(solution)/shard_map/ppermute | solution.py:430
  7.0 11.0 %collective-permute-start.5 = (bf16[1024,256]{1,0:T(8,128)(2,1)}, bf16[1024,256]{1,0:T(8,128)(2,1)S(1)}, u32[]{:S(2)}, u32[]{:S(2)}) collective-permute-start(bf16[1024,256]{1,0:T(8,128)(2,1)} %refs_1_), channel_id=1, source_target_pairs={{0,1},{1,0},{2,3},{3,2},{4,5},{5,4},{6,7},{7,6},{8,9},{9,8},{10,11... | collective-permute-start | bytes 1572872 | tf_op jit(solution)/shard_map/ppermute | solution.py:23
  9.4 1.0 copy-start
  10.4 1.0 copy-start.1
  21.8 7.0 %collective-permute-start.6 = (bf16[1024,256]{1,0:T(8,128)(2,1)S(1)}, bf16[1024,256]{1,0:T(8,128)(2,1)S(1)}, u32[]{:S(2)}, u32[]{:S(2)}) collective-permute-start(bf16[1024,256]{1,0:T(8,128)(2,1)S(1)} %collective-permute-done.2.refs_0_), channel_id=1, source_target_pairs={{0,1},{1,0},{2,3},{3,2},{4,5},{5,4},{6,7},{7,6},{8,9},{9,8},{10,11... | collective-permute-start | bytes 1572872 | tf_op jit(solution)/shard_map/ppermute | solution.py:23
  21.9 7.0 %collective-permute-start.7 = (bf16[1024,256]{1,0:T(8,128)(2,1)S(1)}, bf16[1024,256]{1,0:T(8,128)(2,1)S(1)}, u32[]{:S(2)}, u32[]{:S(2)}) collective-permute-start(bf16[1024,256]{1,0:T(8,128)(2,1)S(1)} %collective-permute-done.3.refs_1_), channel_id=1, source_target_pairs={{0,1},{1,0},{2,3},{3,2},{4,5},{5,4},{6,7},{7,6},{8,9},{9,8},{10,11... | collective-permute-start | bytes 1572872 | tf_op jit(solution)/shard_map/ppermute | solution.py:23
  22.4 16.8 %collective-permute-start = (bf16[1152,256]{1,0:T(8,128)(2,1)S(1)}, bf16[1152,256]{1,0:T(8,128)(2,1)S(1)}, u32[]{:S(2)}, u32[]{:S(2)}) collective-permute-start(bf16[1152,256]{1,0:T(8,128)(2,1)S(1)} %constant_dynamic-update-slice_fusion), channel_id=1, source_target_pairs={{0,8},{8,16},{16,24},{1,9},{9,17},{17,25},{2,10},{10,18},{18,26},{... | collective-permute-start | bytes 1769480 | tf_op jit(solution)/shard_map/ppermute | solution.py:429
  26.0 17.3 %collective-permute-start.1 = (bf16[1152,256]{1,0:T(8,128)(2,1)S(1)}, bf16[1152,256]{1,0:T(8,128)(2,1)S(1)}, u32[]{:S(2)}, u32[]{:S(2)}) collective-permute-start(bf16[1152,256]{1,0:T(8,128)(2,1)S(1)} %constant_dynamic-update-slice_fusion), channel_id=1, source_target_pairs={{8,0},{16,8},{24,16},{9,1},{17,9},{25,17},{10,2},{18,10},{26,18},{... | collective-permute-start | bytes 1769480 | tf_op jit(solution)/shard_map/ppermute | solution.py:430
  28.8 15.0 %copy-start.6 = (s32[32]{0:T(128)S(1)}, s32[32]{0:T(128)}, u32[]{:S(2)}) copy-start(s32[32]{0:T(128)} %param.15) | copy-start | bytes 388
  43.3 4.9 %collective-permute-start.12 = (bf16[1152,256]{1,0:T(8,128)(2,1)S(1)}, bf16[1152,256]{1,0:T(8,128)(2,1)S(1)}, u32[]{:S(2)}, u32[]{:S(2)}) collective-permute-start(bf16[1152,256]{1,0:T(8,128)(2,1)S(1)} %collective-permute-done.refs_0_), channel_id=1, source_target_pairs={{0,1},{1,0},{2,3},{3,2},{4,5},{5,4},{6,7},{7,6},{8,9},{9,8},{10,11... | collective-permute-start | bytes 1769480 | tf_op jit(solution)/shard_map/ppermute | solution.py:23
  43.3 6.2 %collective-permute-start.13 = (bf16[1152,256]{1,0:T(8,128)(2,1)S(1)}, bf16[1152,256]{1,0:T(8,128)(2,1)S(1)}, u32[]{:S(2)}, u32[]{:S(2)}) collective-permute-start(bf16[1152,256]{1,0:T(8,128)(2,1)S(1)} %collective-permute-done.1.refs_1_), channel_id=1, source_target_pairs={{0,1},{1,0},{2,3},{3,2},{4,5},{5,4},{6,7},{7,6},{8,9},{9,8},{10,11... | collective-permute-start | bytes 1769480 | tf_op jit(solution)/shard_map/ppermute | solution.py:23
  43.8 7.2 %collective-permute-start.10 = (bf16[1024,256]{1,0:T(8,128)(2,1)S(1)}, bf16[1024,256]{1,0:T(8,128)(2,1)S(1)}, u32[]{:S(2)}, u32[]{:S(2)}) collective-permute-start(bf16[1024,256]{1,0:T(8,128)(2,1)S(1)} %collective-permute-done.2.refs_0_), channel_id=1, source_target_pairs={{8,16},{16,24},{9,17},{17,25},{10,18},{18,26},{11,19},{19,27},{12,... | collective-permute-start | bytes 1572872 | tf_op jit(solution)/shard_map/ppermute | solution.py:429
  44.6 19.0 %collective-permute-start.11 = (bf16[1024,256]{1,0:T(8,128)(2,1)S(1)}, bf16[1024,256]{1,0:T(8,128)(2,1)S(1)}, u32[]{:S(2)}, u32[]{:S(2)}) collective-permute-start(bf16[1024,256]{1,0:T(8,128)(2,1)S(1)} %collective-permute-done.3.refs_1_), channel_id=1, source_target_pairs={{8,0},{16,8},{9,1},{17,9},{10,2},{18,10},{11,3},{19,11},{12,4},{20... | collective-permute-start | bytes 1572872 | tf_op jit(solution)/shard_map/ppermute | solution.py:430
  46.0 21.4 %collective-permute-start.8 = (bf16[1152,256]{1,0:T(8,128)(2,1)S(1)}, bf16[1152,256]{1,0:T(8,128)(2,1)S(1)}, u32[]{:S(2)}, u32[]{:S(2)}) collective-permute-start(bf16[1152,256]{1,0:T(8,128)(2,1)S(1)} %collective-permute-done.refs_0_), channel_id=1, source_target_pairs={{8,16},{16,24},{9,17},{17,25},{10,18},{18,26},{11,19},{19,27},{12,... | collective-permute-start | bytes 1769480 | tf_op jit(solution)/shard_map/ppermute | solution.py:429
  48.2 15.6 %copy-start.3 = (s32[32,32]{1,0:T(8,128)S(1)}, s32[32,32]{1,0:T(8,128)}, u32[]{:S(2)}) copy-start(s32[32,32]{1,0:T(8,128)} %param.14) | copy-start | bytes 12292
  48.2 16.2 %copy-start.5 = (f32[2,256]{1,0:T(2,128)S(1)}, f32[2,256]{1,0:T(2,128)}, u32[]{:S(2)}) copy-start(f32[2,256]{1,0:T(2,128)} %param.11) | copy-start | bytes 6148
  48.2 16.2 %copy-start.2 = (bf16[4,8,2,256]{3,2,1,0:T(2,128)(2,1)S(1)}, bf16[4,8,2,256]{3,2,1,0:T(2,128)(2,1)}, u32[]{:S(2)}) copy-start(bf16[4,8,2,256]{3,2,1,0:T(2,128)(2,1)} %param.12) | copy-start | bytes 98308
  48.2 27.0 %collective-permute-start.9 = (bf16[1152,256]{1,0:T(8,128)(2,1)S(1)}, bf16[1152,256]{1,0:T(8,128)(2,1)S(1)}, u32[]{:S(2)}, u32[]{:S(2)}) collective-permute-start(bf16[1152,256]{1,0:T(8,128)(2,1)S(1)} %collective-permute-done.1.refs_1_), channel_id=1, source_target_pairs={{8,0},{16,8},{9,1},{17,9},{10,2},{18,10},{11,3},{19,11},{12,4},{20... | collective-permute-start | bytes 1769480 | tf_op jit(solution)/shard_map/ppermute | solution.py:430
  63.7 2.2 %collective-permute-start.14 = (bf16[1024,256]{1,0:T(8,128)(2,1)S(1)}, bf16[1024,256]{1,0:T(8,128)(2,1)S(1)}, u32[]{:S(2)}, u32[]{:S(2)}) collective-permute-start(bf16[1024,256]{1,0:T(8,128)(2,1)S(1)} %add.90.refs_0_), channel_id=1, source_target_pairs={{0,1},{1,0},{2,3},{3,2},{4,5},{5,4},{6,7},{7,6},{8,9},{9,8},{10,11... | collective-permute-start | bytes 1572872 | tf_op jit(solution)/shard_map/ppermute | solution.py:23
  75.4 4.0 %collective-permute-start.19 = (bf16[1152,256]{1,0:T(8,128)(2,1)S(1)}, bf16[1152,256]{1,0:T(8,128)(2,1)S(1)}, u32[]{:S(2)}, u32[]{:S(2)}) collective-permute-start(bf16[1152,256]{1,0:T(8,128)(2,1)S(1)} %add.91.refs_0_), channel_id=1, source_target_pairs={{0,1},{1,0},{2,3},{3,2},{4,5},{5,4},{6,7},{7,6},{8,9},{9,8},{10,11... | collective-permute-start | bytes 1769480 | tf_op jit(solution)/shard_map/ppermute | solution.py:23
  75.5 5.3 %collective-permute-start.17 = (bf16[1024,256]{1,0:T(8,128)(2,1)S(1)}, bf16[1024,256]{1,0:T(8,128)(2,1)S(1)}, u32[]{:S(2)}, u32[]{:S(2)}) collective-permute-start(bf16[1024,256]{1,0:T(8,128)(2,1)S(1)} %collective-permute-done.10), channel_id=1, source_target_pairs={{16,24},{17,25},{18,26},{19,27},{20,28},{21,29},{22,30},{23,31}} | collective-permute-start | bytes 1572872 | tf_op jit(solution)/shard_map/ppermute | solution.py:429
  76.2 16.2 %collective-permute-start.18 = (bf16[1024,256]{1,0:T(8,128)(2,1)S(1)}, bf16[1024,256]{1,0:T(8,128)(2,1)S(1)}, u32[]{:S(2)}, u32[]{:S(2)}) collective-permute-start(bf16[1024,256]{1,0:T(8,128)(2,1)S(1)} %collective-permute-done.11), channel_id=1, source_target_pairs={{8,0},{9,1},{10,2},{11,3},{12,4},{13,5},{14,6},{15,7}} | collective-permute-start | bytes 1572872 | tf_op jit(solution)/shard_map/ppermute | solution.py:430
  92.5 3.8 %collective-permute-start.20 = (bf16[1024,256]{1,0:T(8,128)(2,1)S(1)}, bf16[1024,256]{1,0:T(8,128)(2,1)S(1)}, u32[]{:S(2)}, u32[]{:S(2)}) collective-permute-start(bf16[1024,256]{1,0:T(8,128)(2,1)S(1)} %add.92.refs_0_), channel_id=1, source_target_pairs={{0,1},{1,0},{2,3},{3,2},{4,5},{5,4},{6,7},{7,6},{8,9},{9,8},{10,11... | collective-permute-start | bytes 1572872 | tf_op jit(solution)/shard_map/ppermute | solution.py:23
  92.9 18.5 %collective-permute-start.15 = (bf16[1152,256]{1,0:T(8,128)(2,1)S(1)}, bf16[1152,256]{1,0:T(8,128)(2,1)S(1)}, u32[]{:S(2)}, u32[]{:S(2)}) collective-permute-start(bf16[1152,256]{1,0:T(8,128)(2,1)S(1)} %collective-permute-done.8), channel_id=1, source_target_pairs={{16,24},{17,25},{18,26},{19,27},{20,28},{21,29},{22,30},{23,31}} | collective-permute-start | bytes 1769480 | tf_op jit(solution)/shard_map/ppermute | solution.py:429
  93.6 17.8 %collective-permute-start.16 = (bf16[1152,256]{1,0:T(8,128)(2,1)S(1)}, bf16[1152,256]{1,0:T(8,128)(2,1)S(1)}, u32[]{:S(2)}, u32[]{:S(2)}) collective-permute-start(bf16[1152,256]{1,0:T(8,128)(2,1)S(1)} %collective-permute-done.9), channel_id=1, source_target_pairs={{8,0},{9,1},{10,2},{11,3},{12,4},{13,5},{14,6},{15,7}} | collective-permute-start | bytes 1769480 | tf_op jit(solution)/shard_map/ppermute | solution.py:430
  97.9 1.4 %collective-permute-start.21 = (f32[1,256]{1,0:T(1,128)S(1)}, f32[1,256]{1,0:T(1,128)S(1)}, u32[]{:S(2)}, u32[]{:S(2)}) collective-permute-start(f32[1,256]{1,0:T(1,128)S(1)} %bitcast.32), channel_id=1, source_target_pairs={{0,1},{1,0},{2,3},{3,2},{4,5},{5,4},{6,7},{7,6},{8,9},{9,8},{10,11... | collective-permute-start | bytes 3080 | tf_op jit(solution)/shard_map/ppermute | solution.py:23
  99.2 5.4 %collective-permute-start.22 = (f32[1,256]{1,0:T(1,128)S(1)}, f32[1,256]{1,0:T(1,128)S(1)}, u32[]{:S(2)}, u32[]{:S(2)}) collective-permute-start(f32[1,256]{1,0:T(1,128)S(1)} %max.36), channel_id=1, source_target_pairs={{0,8},{8,16},{16,24},{24,0},{1,9},{9,17},{17,25},{25,1},{2,10},{10... | collective-permute-start | bytes 3080 | tf_op jit(solution)/shard_map/ppermute | solution.py:23
  100.4 4.5 %collective-permute-start.23 = (f32[1,256]{1,0:T(1,128)S(1)}, f32[1,256]{1,0:T(1,128)S(1)}, u32[]{:S(2)}, u32[]{:S(2)}) collective-permute-start(f32[1,256]{1,0:T(1,128)S(1)} %max.36), channel_id=1, source_target_pairs={{0,16},{8,24},{16,0},{24,8},{1,17},{9,25},{17,1},{25,9},{2,18},{10... | collective-permute-start | bytes 3080 | tf_op jit(solution)/shard_map/ppermute | solution.py:23
  100.4 11.0 %collective-permute-start.24 = (f32[1,256]{1,0:T(1,128)S(1)}, f32[1,256]{1,0:T(1,128)S(1)}, u32[]{:S(2)}, u32[]{:S(2)}) collective-permute-start(f32[1,256]{1,0:T(1,128)S(1)} %max.36), channel_id=1, source_target_pairs={{0,24},{8,0},{16,8},{24,16},{1,25},{9,1},{17,9},{25,17},{2,26},{10... | collective-permute-start | bytes 3080 | tf_op jit(solution)/shard_map/ppermute | solution.py:23
  111.3 4.3 %copy-start.4 = (f32[1,256]{1,0:T(1,128)}, f32[1,256]{1,0:T(1,128)S(1)}, u32[]{:S(2)}) copy-start(f32[1,256]{1,0:T(1,128)S(1)} %add_sqrt_fusion) | copy-start | bytes 3076
  111.5 2.4 %collective-permute-start.26 = (bf16[1152,256]{1,0:T(8,128)(2,1)S(1)}, bf16[1152,256]{1,0:T(8,128)(2,1)S(1)}, u32[]{:S(2)}, u32[]{:S(2)}) collective-permute-start(bf16[1152,256]{1,0:T(8,128)(2,1)S(1)} %add.105.refs_0_), channel_id=1, source_target_pairs={{0,1},{1,0},{2,3},{3,2},{4,5},{5,4},{6,7},{7,6},{8,9},{9,8},{10,11... | collective-permute-start | bytes 1769480 | tf_op jit(solution)/shard_map/ppermute | solution.py:23
  111.8 3.5 %collective-permute-start.25 = (bf16[1024,128]{1,0:T(8,128)(2,1)S(1)}, bf16[1024,128]{1,0:T(8,128)(2,1)S(1)}, u32[]{:S(2)}, u32[]{:S(2)}) collective-permute-start(bf16[1024,128]{1,0:T(8,128)(2,1)S(1)} %get-tuple-element.139), channel_id=1, source_target_pairs={{0,1},{1,0},{2,3},{3,2},{4,5},{5,4},{6,7},{7,6},{8,9},{9,8},{10,11... | collective-permute-start | bytes 786440 | tf_op jit(solution)/shard_map/ppermute | solution.py:23
  115.5 4.8 %collective-permute-start.27 = (bf16[1024,128]{1,0:T(8,128)(2,1)S(1)}, bf16[1024,128]{1,0:T(8,128)(2,1)S(1)}, u32[]{:S(2)}, u32[]{:S(2)}) collective-permute-start(bf16[1024,128]{1,0:T(8,128)(2,1)S(1)} %get-tuple-element.137), channel_id=1, source_target_pairs={{0,1},{1,0},{2,3},{3,2},{4,5},{5,4},{6,7},{7,6},{8,9},{9,8},{10,11... | collective-permute-start | bytes 786440 | tf_op jit(solution)/shard_map/ppermute | solution.py:23
  123.8 5.8 %collective-permute-start.28 = (bf16[272,128]{1,0:T(8,128)(2,1)S(1)}, bf16[272,128]{1,0:T(8,128)(2,1)S(1)}, u32[]{:S(2)}, u32[]{:S(2)}) collective-permute-start(bf16[272,128]{1,0:T(8,128)(2,1)S(1)} %get-tuple-element.117), channel_id=1, source_target_pairs={{0,24},{8,0},{16,8},{24,16},{1,25},{9,1},{17,9},{25,17},{2,26},{10... | collective-permute-start | bytes 208904 | tf_op jit(solution)/shard_map/ppermute | solution.py:23
  123.9 8.6 %collective-permute-start.29 = (bf16[272,128]{1,0:T(8,128)(2,1)S(1)}, bf16[272,128]{1,0:T(8,128)(2,1)S(1)}, u32[]{:S(2)}, u32[]{:S(2)}) collective-permute-start(bf16[272,128]{1,0:T(8,128)(2,1)S(1)} %get-tuple-element.118), channel_id=1, source_target_pairs={{0,16},{8,24},{16,0},{24,8},{1,17},{9,25},{17,1},{25,9},{2,18},{10... | collective-permute-start | bytes 208904 | tf_op jit(solution)/shard_map/ppermute | solution.py:23
  124.0 8.5 %collective-permute-start.30 = (bf16[272,128]{1,0:T(8,128)(2,1)S(1)}, bf16[272,128]{1,0:T(8,128)(2,1)S(1)}, u32[]{:S(2)}, u32[]{:S(2)}) collective-permute-start(bf16[272,128]{1,0:T(8,128)(2,1)S(1)} %get-tuple-element.119), channel_id=1, source_target_pairs={{0,8},{8,16},{16,24},{24,0},{1,9},{9,17},{17,25},{25,1},{2,10},{10... | collective-permute-start | bytes 208904 | tf_op jit(solution)/shard_map/ppermute | solution.py:23
  132.9 1.3 collective-permute-start.31

commit v6 on v5

--- a/solution.py
+++ b/solution.py
@@ -15,7 +15,7 @@
 
 EPSILON = 1e-05
 NEGATIVE = -1e30
-SHORT = 8
+LINE = 4
 
 
 def shifted(x, axis, k):
@@ -23,21 +23,58 @@
     return lax.ppermute(x, axis, [(i, (i + k) % n) for i in range(n)])
 
 
-def from_all(x, axis):
+def partner(me, k, n):
+    return me ^ k if n == LINE else (k - me) % n
+
+
+def swapped(x, axis, k):
     n = lax.axis_size(axis)
-    if n > SHORT:
-        order = (lax.axis_index(axis) - jnp.arange(n)) % n
-        return list(lax.all_gather(x, axis)[order])
-    return [x] + [shifted(x, axis, k) for k in range(1, n)]
+    return lax.ppermute(x, axis, [(i, partner(i, k, n)) for i in range(n)])
+
+
+def from_owners(x):
+    return [x] + [shifted(x, "rep", k) for k in range(1, lax.axis_size("rep"))]
+
+
+def from_groups(x):
+    n = lax.axis_size("seq")
+    if n != LINE:
+        return list(lax.all_gather(x, "seq")[partner(lax.axis_index("seq"), jnp.arange(n), n)])
+    return [x] + [swapped(x, "seq", k) for k in range(1, n)]
 
 
 def to_groups(x):
     n = lax.axis_size("seq")
-    if n > SHORT:
-        me, k = lax.axis_index("seq"), jnp.arange(n)
-        back = lax.all_to_all(jnp.stack(x)[(me - k) % n], "seq", split_axis=0, concat_axis=0)
-        return list(back[(me + k) % n])
-    return [x[0]] + [shifted(x[k], "seq", -k) for k in range(1, n)]
+    if n != LINE:
+        order = partner(lax.axis_index("seq"), jnp.arange(n), n)
+        back = lax.all_to_all(jnp.stack(x)[order], "seq", split_axis=0, concat_axis=0)
+        return list(back[order])
+    return [x[0]] + [swapped(x[k], "seq", k) for k in range(1, n)]
+
+
+def pack_kernel(weight, query, out, sem):
+    depth, columns = weight.shape
+    copy = pltpu.make_async_copy(weight, out.at[pl.ds(0, depth)], sem)
+    copy.start()
+    lines = query.shape[0]
+    for k in range(query.shape[1] // columns):
+        at = pl.ds(depth + k * lines, lines)
+        out[at, :] = query[:, k * columns : (k + 1) * columns]
+    copy.wait()
+
+
+def pack(weight, query):
+    depth, columns = weight.shape
+    whole = pl.BlockSpec(memory_space=pltpu.VMEM)
+    return pl.pallas_call(
+        pack_kernel,
+        out_shape=jax.ShapeDtypeStruct((depth + query.size // columns, columns), weight.dtype),
+        in_specs=[pl.BlockSpec(memory_space=pl.ANY), whole],
+        out_specs=whole,
+        scratch_shapes=[pltpu.SemaphoreType.DMA],
+        compiler_params=pltpu.CompilerParams(vmem_limit_bytes=8 * 2**20),
+        name="pack",
+    )(weight, query)
 
 
 def load_kernel(owners, place, hidden, *refs):
@@ -114,9 +151,10 @@
     owner = lax.rem(place[1] + owners - back, owners)
     for j, copy in enumerate(copies):
         copy.wait()
-        group = place[0] + hops[j][0]
-        for hop in hops[j][1:]:
-            group = jnp.where((group >= 0) & (group < groups), group, place[0] + hop)
+        group = jnp.int32(-1)
+        for parity, hop in hops[j]:
+            there = place[0] + jnp.where(lax.rem(place[0], 2) == parity, hop, -hop)
+            group = jnp.where((there >= 0) & (there < groups), there, group)
 
         @pl.when((group >= 0) & (group < groups))
         def _(j=j, group=group):
@@ -414,70 +452,90 @@
 
 def smooth_of(raw_keys):
     top = jnp.max(jnp.abs(raw_keys), axis=0, keepdims=True)
-    top = functools.reduce(jnp.maximum, from_all(top, "rep"))
-    top = functools.reduce(jnp.maximum, from_all(top, "seq"))
+    top = functools.reduce(jnp.maximum, from_owners(top))
+    top = functools.reduce(jnp.maximum, from_groups(top))
     return jnp.sqrt(top + EPSILON)
 
 
-def line_project(hidden, key_weight, value_weight, raw_query, early):
+def line_pairs(hop, parity, groups):
+    pairs = []
+    for i in range(parity, groups - 1, 2):
+        if i >= hop - 1:
+            pairs.append((i, i + 1))
+        if i + hop < groups:
+            pairs.append((i + 1, i))
+    return pairs
+
+
+def line_project(hidden, key_weight, value_weight, own_query, early):
     groups, owners = lax.axis_size("seq"), lax.axis_size("rep")
-    names = ("k", "v")
-    moving, arrived, totals = {}, {}, {}
-
-    def send(name, hop):
-        left, right = moving[name]
-        left = lax.ppermute(left, "seq", [(i, i + 1) for i in range(hop - 1, groups - 1)])
-        right = lax.ppermute(right, "seq", [(i, i - 1) for i in range(1, groups - hop + 1)])
-        arrived[name] = (left, right)
-
-    def absorb(name, hop):
-        left, right = moving[name]
-        if hop == 0:
-            here = [((0,), left)]
-        elif 2 * hop >= groups:
-            here = [((-hop, hop), left + right)]
-        else:
-            here = [((-hop,), left), ((hop,), right)]
-        blocks = [block for _, block in here]
+    depth = key_weight.shape[0]
+    barrier = lax.optimization_barrier
+
+    def send(x, hop, parity):
+        return lax.ppermute(x, "seq", line_pairs(hop, parity, groups))
+
+    def absorb(name, blocks, hops, first=0):
         passed = [[shifted(block, "rep", k) for block in blocks] for k in range(1, owners)]
         for k, ready in enumerate([blocks] + passed):
-            if hop == 0 and k == 0:
+            if k < first:
                 continue
             totals[name] = project(
-                hidden,
-                totals[name],
-                ready,
-                depth,
-                early[0],
-                tuple(hops for hops, _ in here),
-                k,
-                groups,
-                owners,
+                hidden, totals[name], ready, depth, early[0], hops, k, groups, owners
             )
 
-    depth = key_weight.shape[0]
-    moving["k"], moving["v"] = (key_weight,) * 2, (jnp.concatenate([value_weight, raw_query]),) * 2
-    lefts, rights = [None] * groups, [None] * groups
-    for name in names:
-        send(name, 1)
-    early, first = lax.optimization_barrier((early, (key_weight, value_weight)))
+    totals = {}
+    ka1 = send(key_weight, 1, 0)
+    kb1 = send(key_weight, 1, 1)
+    value_block = pack(value_weight, own_query)
+    va1 = send(value_block, 1, 0)
+    early, first = barrier((early, (key_weight, value_weight)))
     hidden, totals["k"], totals["v"] = load(hidden, *first, early[0], owners)
-    moving["v"] = (value_weight,) * 2
-    for name in names:
-        absorb(name, 0)
-    for hop in range(1, groups):
-        for name in names:
-            if name == names[-1] and hop == groups - 1:
-                smooth = smooth_of(totals["k"])
-                moving[name], smooth = lax.optimization_barrier((arrived[name], smooth))
-            else:
-                moving[name], totals = lax.optimization_barrier((arrived[name], totals))
-            if hop < groups - 1:
-                send(name, hop + 1)
-            absorb(name, hop)
-        lefts[hop], rights[groups - hop] = (block[depth:] for block in moving["v"])
-    queries = [raw_query] + [lefts[k] + rights[k] for k in range(1, groups)]
-    return totals["k"], totals["v"], smooth, queries, early
+    for name, weight in (("k", key_weight), ("v", value_weight)):
+        absorb(name, [weight], (((0, 0),),), 1)
+
+    ka1, kb1, value_block, totals = barrier((ka1, kb1, value_block, totals))
+    kb2 = send(ka1, 2, 1)
+    ka2 = send(kb1, 2, 0)
+    vb1 = send(value_block, 1, 1)
+    absorb("k", [ka1, kb1], (((0, 1),), ((1, 1),)))
+
+    kb2, va1, totals = barrier((kb2, va1, totals))
+    ka3 = send(kb2, 3, 0)
+    vb2 = send(va1, 2, 1)
+    absorb("v", [va1], (((0, 1),),))
+
+    ka2, totals = barrier((ka2, totals))
+    absorb("k", [ka2 + kb2], (((0, 2), (1, 2)),))
+
+    vb1, totals = barrier((vb1, totals))
+    va2 = send(vb1, 2, 0)
+    absorb("v", [vb1], (((1, 1),),))
+
+    ka3, totals = barrier((ka3, totals))
+    absorb("k", [ka3], (((0, 3),),))
+    raw_keys = totals["k"]
+    vb2, raw_keys = barrier((vb2, raw_keys))
+    far_query = lax.ppermute(vb2[depth:], "seq", line_pairs(3, 0, groups))
+    va3 = send(vb2, 3, 0)
+    smooth = smooth_of(raw_keys)
+    va2, vb2, smooth = barrier((va2, vb2, smooth))
+    absorb("v", [va2 + vb2], (((0, 2), (1, 2)),))
+    queries = [
+        value_block[depth:],
+        va1[depth:],
+        va2[depth:] + vb2[depth:],
+        vb1[depth:] + far_query,
+    ]
+
+    def finish_values(scored, *args):
+        args, totals["v"] = barrier((args, totals["v"]))
+        probs, stats = scored(*args)
+        block, stats = barrier((va3, stats))
+        absorb("v", [block], (((0, 3),),))
+        return probs, stats, totals["v"]
+
+    return raw_keys, smooth, queries, early, finish_values
 
 
 def on_device(
@@ -493,7 +551,6 @@
 
     owner_is = [my_owner == owner for owner in range(owners)]
     own_query = my_part(decode_query, 2, owner_is).reshape(step_count * per_group, -1)
-    raw_query = jnp.concatenate(jnp.split(own_query, own_query.shape[1] // columns, axis=1))
 
     first_pages = [
         (my_group * owners + (my_owner - k) % owners) * pages_dev for k in range(owners)
@@ -502,10 +559,14 @@
         jnp.stack([my_group, my_owner]),
         owner_is,
         first_pages,
-        (my_group - jnp.arange(groups, dtype=jnp.int32)) % groups,
+        partner(my_group, jnp.arange(groups, dtype=jnp.int32), groups),
         own_query,
     )
-    if groups > SHORT:
+    if groups == LINE:
+        raw_keys, smooth, queries, early, finish_values = line_project(
+            hidden, key_weight, value_weight, own_query, early
+        )
+    else:
         raw_keys, raw_values = (
             jnp.dot(
                 hidden,
@@ -514,12 +575,10 @@
             )
             for weight in (key_weight, value_weight)
         )
-        queries = from_all(raw_query, "seq")
+        queries = from_groups(
+            jnp.concatenate(jnp.split(own_query, own_query.shape[1] // columns, axis=1))
+        )
         smooth = smooth_of(raw_keys)
-    else:
-        raw_keys, raw_values, smooth, queries, early = line_project(
-            hidden, key_weight, value_weight, raw_query, early
-        )
     _, owner_is, first_pages, group_at, own_query = early
     counts = token_counts(page_table, lengths, first_pages, pages_dev)
     counts = counts.reshape(groups, per_group, -1)
@@ -534,18 +593,14 @@
     smoothing = smooth.reshape(-1)
     my_smooth = my_part(smooth, 1, owner_is)
     keys = clip_keys(raw_keys, smooth, group_scale)
-    head_keys, raw_values = lax.optimization_barrier((by_head(keys), raw_values))
+    score_scale = HD ** (-0.5)
+    scored = functools.partial(score, steps=step_count, scale=score_scale)
+    args = (group_at, jnp.stack(queries), my_smooth, counts, by_head(keys))
+    if groups == LINE:
+        probs, stats, raw_values = finish_values(scored, *args)
+    else:
+        probs, stats = scored(*args)
     values = clip_values(raw_values, group_scale)
-    score_scale = HD ** (-0.5)
-    probs, stats = score(
-        group_at,
-        jnp.stack(queries),
-        my_smooth,
-        counts,
-        head_keys,
-        step_count,
-        score_scale,
-    )
     messages = weigh(probs, by_head(values), stats)
 
     messages, keys, values, late = lax.optimization_barrier(
@@ -556,7 +611,7 @@
     own = fresh(late[0], late[1], *my_new, score_scale)
     messages, kv_cache, own = lax.optimization_barrier((messages, kv_cache, own))
     attention = finish(messages, own, step_count * per_group)
-    by_owner = from_all(attention, "rep")
+    by_owner = from_owners(attention)
     attention = jnp.concatenate(
         [
             functools.reduce(

time: 135 us -> 133 us (0.985)
  waiting for transfers between devices: 59.2 us -> 55.1 us
  Pallas kernels: 34.2 us -> 35.7 us
    ppermute x20 -> x14, waiting for transfers between devices: 13.5 us -> 4.33 us  [shifted(): return lax.ppermute(x, axis, [(i, (i + k) % n) for i in range(n)])]
    ppermute x12 -> x17, starting transfers between devices: 18.9 us -> 25.1 us  [the longest x10 15 us: send(): return lax.ppermute(x, 'seq', line_pairs(hop, parity, groups))]
    ppermute x20 -> x14, starting transfers between devices: 9.3 us -> 3.17 us  [shifted(): return lax.ppermute(x, axis, [(i, (i + k) % n) for i in range(n)])]
    ppermute x12 -> x17, waiting for transfers between devices: 45.8 us -> 50.8 us  [the longest x10 33.3 us: send(): return lax.ppermute(x, 'seq', line_pairs(hop, parity, groups))]
    pallas_call x14 -> x16, Pallas kernels: 20.4 us -> 21.8 us  [project(): pl.pallas_call(functools.partial(project_kernel, hops, back, groups, owne...]
    unnamed x17 -> x16, local copies, waits for them, and re-layouts: 3.2 us -> 3.15 us
  transfers between devices with their start and end apart: 32 -> 31, of which waited for: 13 -> 11; matrix products, arithmetic and copies ran while one was open for 5% -> 5% of each run, Pallas kernels for 24% -> 24%
where the time goes in v6:
time: 133 us; the launch traced here: 132 us
  waiting for transfers between devices  55.1 us (41%)
  Pallas kernels  35.7 us (27%)
  starting transfers between devices  28.3 us (21%)
  other arithmetic  6.38 us (5%)
  local copies, waits for them, and re-layouts  4.82 us (4%)
  between operations  1.34 us (1%)
    ppermute x10, waiting for transfers between devices, send(): return lax.ppermute(x, 'seq', line_pairs(hop, parity, groups))  33.3 us
    pallas_call x16, Pallas kernels, project(): pl.pallas_call(functools.partial(project_kernel, hops, back, groups, owne...  21.8 us
    ppermute x10, starting transfers between devices, send(): return lax.ppermute(x, 'seq', line_pairs(hop, parity, groups))  15 us
    ppermute x1, waiting for transfers between devices, line_project(): far_query = lax.ppermute(vb2[depth:], 'seq', line_pairs(3, 0, groups))  9.69 us
    ppermute x6, starting transfers between devices, swapped(): return lax.ppermute(x, axis, [(i, partner(i, k, n)) for i in range(n)])  8.83 us
    ppermute x6, waiting for transfers between devices, swapped(): return lax.ppermute(x, axis, [(i, partner(i, k, n)) for i in range(n)])  7.77 us
    pallas_call x1, Pallas kernels, load(): pl.pallas_call(functools.partial(load_kernel, owners), out_shape=(jax.Sha...  6.57 us
    pallas_call x1, Pallas kernels, score(): pl.pallas_call(functools.partial(score_kernel, slots, parts, steps, scale...  4.73 us
  transfers between devices with their start and end apart: 31, of which 11 were waited for; matrix products, arithmetic and copies ran while one was open for 5% of the time, Pallas kernels for 24%

profile of v6, /device:TPU:0, one launch (start us, length us, event | category | flops | bytes accessed | tf_op | source)
XLA Modules:
  0.0 132.0 jit_solution(1760040465845466738)
XLA Ops:
  0.6 0.6 collective-permute-start.2
  1.2 2.6 %collective-permute-start = (bf16[1024,256]{1,0:T(8,128)(2,1)}, bf16[1024,256]{1,0:T(8,128)(2,1)S(1)}, u32[]{:S(2)}, u32[]{:S(2)}) collective-permute-start(bf16[1024,256]{1,0:T(8,128)(2,1)} %refs_0_), channel_id=1, source_target_pairs={{0,8},{8,0},{16,24},{24,16},{1,9},{9,1},{17,25},{25,17},{2,10},{10... | collective-permute-start | bytes 1572872 | tf_op jit(solution)/shard_map/ppermute | solution.py:476
  3.8 0.7 collective-permute-start.1
  4.5 0.2 collective-permute-start.3
  4.7 0.9 select_bitcast_fusion.query
  5.7 1.0 copy-done
  6.9 1.0 copy-done.1
  7.9 1.0 copy-done.2
  8.9 6.6 %load.1 = (bf16[1024,8192]{1,0:T(8,128)(2,1)S(1)}, f32[1024,256]{1,0:T(8,128)S(1)}, f32[1024,256]{1,0:T(8,128)S(1)}) custom-call(s32[2]{0:T(128)S(1)} %pad_add_fusion.place, bf16[1024,8192]{1,0:T(8,128)(2,1)} %hidden.1, bf16[1024,256]{1,0:T(8,128)(2,1)S(1)} %copy-done.2, bf16[1024,256]{1,0:T(8,128)(2,1)S(1)} %copy-done.1), custom_call_target="tpu_custom_call" | custom-call | flops 1073741824 | bytes 16777216 | tf_op jit(solution)/shard_map/load/pallas_call | solution.py:114
  15.5 1.4 %project.17.refs_1_ = f32[1024,256]{1,0:T(8,128)S(1)} custom-call(s32[2]{0:T(128)S(1)} %pad_add_fusion.place, bf16[1024,8192]{1,0:T(8,128)(2,1)S(1)} %get-tuple-element.82.left, bf16[1024,256]{1,0:T(8,128)(2,1)S(1)} %collective-permute-done.3.refs_0_, f32[1024,256]{1,0:T(8,128)S(1)} %get-tuple-element.84.refs_1_), custom_call_target="tpu_custom_call", output_to_operand_aliasing={{}: (3, {})} | custom-call | flops 536870912 | bytes 4718592 | tf_op jit(solution)/shard_map/project/pallas_call | solution.py:170
  17.0 1.4 %project.16.refs_2_ = f32[1024,256]{1,0:T(8,128)S(1)} custom-call(s32[2]{0:T(128)S(1)} %pad_add_fusion.place, bf16[1024,8192]{1,0:T(8,128)(2,1)S(1)} %get-tuple-element.82.left, bf16[1024,256]{1,0:T(8,128)(2,1)S(1)} %collective-permute-done.2.refs_0_, f32[1024,256]{1,0:T(8,128)S(1)} %get-tuple-element.83.refs_1_), custom_call_target="tpu_custom_call", output_to_operand_aliasing={{}: (3, {})} | custom-call | flops 536870912 | bytes 4718592 | tf_op jit(solution)/shard_map/project/pallas_call | solution.py:170
  18.5 0.4 collective-permute-start.6
  19.0 4.3 %collective-permute-start.5 = (bf16[1152,256]{1,0:T(8,128)(2,1)S(1)}, bf16[1152,256]{1,0:T(8,128)(2,1)S(1)}, u32[]{:S(2)}, u32[]{:S(2)}) collective-permute-start(bf16[1152,256]{1,0:T(8,128)(2,1)S(1)} %pack.1), channel_id=1, source_target_pairs={{0,8},{8,0},{16,24},{24,16},{1,9},{9,1},{17,25},{25,17},{2,10},{10... | collective-permute-start | bytes 1769480 | tf_op jit(solution)/shard_map/ppermute | solution.py:476
  23.3 0.7 collective-permute-start.4
  24.0 1.5 %project.18.refs_2_ = f32[1024,256]{1,0:T(8,128)S(1)} custom-call(s32[2]{0:T(128)S(1)} %pad_add_fusion.place, bf16[1024,8192]{1,0:T(8,128)(2,1)S(1)} %get-tuple-element.82.left, bf16[1024,256]{1,0:T(8,128)(2,1)S(1)} %collective-permute-done.refs_0_, bf16[1024,256]{1,0:T(8,128)(2,1)S(1)} %collective-permute-done.1.refs_1_, ...), custom_call_target="tpu_custom_call", output_to_operand_aliasing={{}: (4, {})} | custom-call | flops 1073741824 | bytes 7340032 | tf_op jit(solution)/shard_map/project/pallas_call | solution.py:170
  25.6 1.5 %project.19.refs_1_ = f32[1024,256]{1,0:T(8,128)S(1)} custom-call(s32[2]{0:T(128)S(1)} %pad_add_fusion.place, bf16[1024,8192]{1,0:T(8,128)(2,1)S(1)} %get-tuple-element.82.left, bf16[1024,256]{1,0:T(8,128)(2,1)S(1)} %collective-permute-done.6.refs_0_, bf16[1024,256]{1,0:T(8,128)(2,1)S(1)} %collective-permute-done.7.refs_1_, ...), custom_call_target="tpu_custom_call", output_to_operand_aliasing={{}: (4, {})} | custom-call | flops 1073741824 | bytes 7340032 | tf_op jit(solution)/shard_map/project/pallas_call | solution.py:170
  27.1 10.2 %collective-permute-done.5.refs_0_ = bf16[1152,256]{1,0:T(8,128)(2,1)S(1)} collective-permute-done((bf16[1152,256]{1,0:T(8,128)(2,1)S(1)}, bf16[1152,256]{1,0:T(8,128)(2,1)S(1)}, u32[]{:S(2)}, u32[]{:S(2)}) %collective-permute-start.5) | collective-permute-done | bytes 589856 | tf_op jit(solution)/shard_map/ppermute | solution.py:476
  37.3 1.3 collective-permute-start.9
  38.5 0.7 collective-permute-start.8
  39.3 1.4 %project.20.refs_1_ = f32[1024,256]{1,0:T(8,128)S(1)} custom-call(s32[2]{0:T(128)S(1)} %pad_add_fusion.place, bf16[1024,8192]{1,0:T(8,128)(2,1)S(1)} %get-tuple-element.82.left, bf16[1152,256]{1,0:T(8,128)(2,1)S(1)} %collective-permute-done.5.refs_0_, f32[1024,256]{1,0:T(8,128)S(1)} %project.17.refs_1_), custom_call_target="tpu_custom_call", output_to_operand_aliasing={{}: (3, {})} | custom-call | flops 536870912 | bytes 4718592 | tf_op jit(solution)/shard_map/project/pallas_call | solution.py:170
  40.7 1.4 %project.21.refs_1_ = f32[1024,256]{1,0:T(8,128)S(1)} custom-call(s32[2]{0:T(128)S(1)} %pad_add_fusion.place, bf16[1024,8192]{1,0:T(8,128)(2,1)S(1)} %get-tuple-element.82.left, bf16[1152,256]{1,0:T(8,128)(2,1)S(1)} %collective-permute-done.10.refs_0_, f32[1024,256]{1,0:T(8,128)S(1)} %project.20.refs_1_), custom_call_target="tpu_custom_call", output_to_operand_aliasing={{}: (3, {})} | custom-call | flops 536870912 | bytes 4718592 | tf_op jit(solution)/shard_map/project/pallas_call | solution.py:170
  42.2 11.3 %collective-permute-done.9 = bf16[1024,256]{1,0:T(8,128)(2,1)S(1)} collective-permute-done((bf16[1024,256]{1,0:T(8,128)(2,1)S(1)}, bf16[1024,256]{1,0:T(8,128)(2,1)S(1)}, u32[]{:S(2)}, u32[]{:S(2)}) %collective-permute-start.9) | collective-permute-done | bytes 524320 | tf_op jit(solution)/shard_map/ppermute | solution.py:476
  53.7 1.4 %project.22.refs_1_ = f32[1024,256]{1,0:T(8,128)S(1)} custom-call(s32[2]{0:T(128)S(1)} %pad_add_fusion.place, bf16[1024,8192]{1,0:T(8,128)(2,1)S(1)} %get-tuple-element.82.left, bf16[1024,256]{1,0:T(8,128)(2,1)S(1)} %add.74.refs_0_, f32[1024,256]{1,0:T(8,128)S(1)} %project.19.refs_1_), custom_call_target="tpu_custom_call", output_to_operand_aliasing={{}: (3, {})} | custom-call | flops 536870912 | bytes 4718592 | tf_op jit(solution)/shard_map/project/pallas_call | solution.py:170
  55.2 0.4 collective-permute-done.11.refs_0_
  55.6 1.4 %project.23.refs_1_ = f32[1024,256]{1,0:T(8,128)S(1)} custom-call(s32[2]{0:T(128)S(1)} %pad_add_fusion.place, bf16[1024,8192]{1,0:T(8,128)(2,1)S(1)} %get-tuple-element.82.left, bf16[1024,256]{1,0:T(8,128)(2,1)S(1)} %collective-permute-done.11.refs_0_, f32[1024,256]{1,0:T(8,128)S(1)} %project.22.refs_1_), custom_call_target="tpu_custom_call", output_to_operand_aliasing={{}: (3, {})} | custom-call | flops 536870912 | bytes 4718592 | tf_op jit(solution)/shard_map/project/pallas_call | solution.py:170
  57.3 1.3 collective-permute-start.14
  58.7 0.6 convert_reduce_fusion
  59.3 0.7 collective-permute-start.13
  60.0 0.7 project.24.refs_1_
  60.8 0.7 project.25.refs_1_
  61.5 11.8 %collective-permute-done.14.refs_0_ = bf16[1024,256]{1,0:T(8,128)(2,1)S(1)} collective-permute-done((bf16[1024,256]{1,0:T(8,128)(2,1)S(1)}, bf16[1024,256]{1,0:T(8,128)(2,1)S(1)}, u32[]{:S(2)}, u32[]{:S(2)}) %collective-permute-start.14) | collective-permute-done | bytes 524320 | tf_op jit(solution)/shard_map/ppermute | solution.py:476
  73.4 0.2 fusion.2
  73.6 0.2 fusion.1.count
  73.8 1.5 %collective-permute-start.12 = (bf16[1152,256]{1,0:T(8,128)(2,1)S(1)}, bf16[1152,256]{1,0:T(8,128)(2,1)S(1)}, u32[]{:S(2)}, u32[]{:S(2)}) collective-permute-start(bf16[1152,256]{1,0:T(8,128)(2,1)S(1)} %collective-permute-done.8.refs_0_), channel_id=1, source_target_pairs={{8,0},{16,24},{9,1},{17,25},{10,2},{18,26},{11,3},{19,27},{12,4},{... | collective-permute-start | bytes 1769480 | tf_op jit(solution)/shard_map/ppermute | solution.py:476
  75.3 1.4 %project.26.refs_1_ = f32[1024,256]{1,0:T(8,128)S(1)} custom-call(s32[2]{0:T(128)S(1)} %pad_add_fusion.place, bf16[1024,8192]{1,0:T(8,128)(2,1)S(1)} %get-tuple-element.82.left, bf16[1024,256]{1,0:T(8,128)(2,1)S(1)} %collective-permute-done.14.refs_0_, f32[1024,256]{1,0:T(8,128)S(1)} %project.23.refs_1_), custom_call_target="tpu_custom_call", output_to_operand_aliasing={{}: (3, {})} | custom-call | flops 536870912 | bytes 4718592 | tf_op jit(solution)/shard_map/project/pallas_call | solution.py:170
  76.8 1.4 %project.27 = f32[1024,256]{1,0:T(8,128)S(1)} custom-call(s32[2]{0:T(128)S(1)} %pad_add_fusion.place, bf16[1024,8192]{1,0:T(8,128)(2,1)S(1)} %get-tuple-element.82.left, bf16[1024,256]{1,0:T(8,128)(2,1)S(1)} %collective-permute-done.16.refs_0_, f32[1024,256]{1,0:T(8,128)S(1)} %project.26.refs_1_), custom_call_target="tpu_custom_call", output_to_operand_aliasing={{}: (3, {})} | custom-call | flops 536870912 | bytes 4718592 | tf_op jit(solution)/shard_map/project/pallas_call | solution.py:170
  78.3 0.6 collective-permute-start.17
  78.9 0.8 collective-permute-done.17
  79.7 1.1 collective-permute-start.18
  80.8 0.5 collective-permute-start.19
  81.3 2.8 %collective-permute-start.20 = (f32[1,256]{1,0:T(1,128)S(1)}, f32[1,256]{1,0:T(1,128)S(1)}, u32[]{:S(2)}, u32[]{:S(2)}) collective-permute-start(f32[1,256]{1,0:T(1,128)S(1)} %max.36), channel_id=1, source_target_pairs={{0,24},{8,16},{16,8},{24,0},{1,25},{9,17},{17,9},{25,1},{2,26},{10... | collective-permute-start | bytes 3080 | tf_op jit(solution)/shard_map/ppermute | solution.py:32
  84.1 1.3 collective-permute-start.24
  85.4 6.6 %collective-permute-done.18 = f32[1,256]{1,0:T(1,128)S(1)} collective-permute-done((f32[1,256]{1,0:T(1,128)S(1)}, f32[1,256]{1,0:T(1,128)S(1)}, u32[]{:S(2)}, u32[]{:S(2)}) %collective-permute-start.18) | collective-permute-done | bytes 1056 | tf_op jit(solution)/shard_map/ppermute | solution.py:32
  92.0 1.3 collective-permute-start.21
  93.8 0.6 collective-permute-start.22
  94.4 1.4 %project.28.refs_1_ = f32[1024,256]{1,0:T(8,128)S(1)} custom-call(s32[2]{0:T(128)S(1)} %pad_add_fusion.place, bf16[1024,8192]{1,0:T(8,128)(2,1)S(1)} %get-tuple-element.82.left, bf16[1152,256]{1,0:T(8,128)(2,1)S(1)} %add.86.refs_0_, f32[1024,256]{1,0:T(8,128)S(1)} %project.25.refs_1_), custom_call_target="tpu_custom_call", output_to_operand_aliasing={{}: (3, {})} | custom-call | flops 536870912 | bytes 4718592 | tf_op jit(solution)/shard_map/project/pallas_call | solution.py:170
  95.9 9.7 %collective-permute-done.21 = bf16[128,256]{1,0:T(8,128)(2,1)S(1)} collective-permute-done((bf16[128,256]{1,0:T(8,128)(2,1)S(1)}, bf16[128,256]{1,0:T(8,128)(2,1)S(1)}, u32[]{:S(2)}, u32[]{:S(2)}) %collective-permute-start.21) | collective-permute-done | bytes 65568 | tf_op jit(solution)/shard_map/ppermute | solution.py:519
  105.6 1.4 %project.29.refs_1_ = f32[1024,256]{1,0:T(8,128)S(1)} custom-call(s32[2]{0:T(128)S(1)} %pad_add_fusion.place, bf16[1024,8192]{1,0:T(8,128)(2,1)S(1)} %get-tuple-element.82.left, bf16[1152,256]{1,0:T(8,128)(2,1)S(1)} %collective-permute-done.23.refs_0_, f32[1024,256]{1,0:T(8,128)S(1)} %project.28.refs_1_), custom_call_target="tpu_custom_call", output_to_operand_aliasing={{}: (3, {})} | custom-call | flops 536870912 | bytes 4718592 | tf_op jit(solution)/shard_map/project/pallas_call | solution.py:170
  107.1 4.7 %score.1 = (bf16[4,256,2048]{2,1,0:T(8,128)(2,1)S(1)}, f32[2,256]{1,0:T(2,128)S(1)}, f32[2,256]{1,0:T(2,128)S(1)}, f32[2,256]{1,0:T(2,128)S(1)}, f32[2,256]{1,0:T(2,128)S(1)}) custom-call(s32[4]{0:T(128)S(1)} %iota_xor_fusion.group, bf16[4,128,256]{2,1,0:T(8,128)(2,1)S(1)} %pad_maximum_fusion.1.query, f32[1,128]{1,0:T(1,128)S(1)} %broadcast_select_fusion.6.smooth, ...), custom_call_target="tpu_custom_call" | custom-call | flops 536870912 | bytes 4194304 | tf_op jit(solution)/shard_map/score/pallas_call | solution.py:241
  112.0 1.4 %project.30.refs_1_ = f32[1024,256]{1,0:T(8,128)S(1)} custom-call(s32[2]{0:T(128)S(1)} %pad_add_fusion.place, bf16[1024,8192]{1,0:T(8,128)(2,1)S(1)} %get-tuple-element.82.left, bf16[1152,256]{1,0:T(8,128)(2,1)S(1)} %collective-permute-done.24.refs_0_, f32[1024,256]{1,0:T(8,128)S(1)} %project.29.refs_1_), custom_call_target="tpu_custom_call", output_to_operand_aliasing={{}: (3, {})} | custom-call | flops 536870912 | bytes 4718592 | tf_op jit(solution)/shard_map/project/pallas_call | solution.py:170
  113.4 0.5 collective-permute-done.25.refs_0_
  113.9 1.4 %project.31 = f32[1024,256]{1,0:T(8,128)S(1)} custom-call(s32[2]{0:T(128)S(1)} %pad_add_fusion.place, bf16[1024,8192]{1,0:T(8,128)(2,1)S(1)} %get-tuple-element.82.left, bf16[1152,256]{1,0:T(8,128)(2,1)S(1)} %collective-permute-done.25.refs_0_, f32[1024,256]{1,0:T(8,128)S(1)} %project.30.refs_1_), custom_call_target="tpu_custom_call", output_to_operand_aliasing={{}: (3, {})} | custom-call | flops 536870912 | bytes 4718592 | tf_op jit(solution)/shard_map/project/pallas_call | solution.py:170
  115.7 1.4 %collective-permute-done.26.refs_1_ = bf16[1024,128]{1,0:T(8,128)(2,1)S(1)} collective-permute-done((bf16[1024,128]{1,0:T(8,128)(2,1)S(1)}, bf16[1024,128]{1,0:T(8,128)(2,1)S(1)}, u32[]{:S(2)}, u32[]{:S(2)}) %collective-permute-start.26) | collective-permute-done | bytes 262176 | tf_op jit(solution)/shard_map/ppermute | solution.py:23
  117.1 1.8 %weigh.1 = (bf16[272,128]{1,0:T(8,128)(2,1)S(1)}, bf16[272,128]{1,0:T(8,128)(2,1)S(1)}, bf16[272,128]{1,0:T(8,128)(2,1)S(1)}, bf16[272,128]{1,0:T(8,128)(2,1)S(1)}) custom-call(bf16[4,256,2048]{2,1,0:T(8,128)(2,1)S(1)} %get-tuple-element.118.probs, bf16[1024,128]{1,0:T(8,128)(2,1)S(1)} %get-tuple-element.156.refs_0_, ...), custom_call_target="tpu_custom_call" | custom-call | flops 536870912 | bytes 4194304 | tf_op jit(solution)/shard_map/weigh/pallas_call | solution.py:316
  119.0 0.8 copy.37
  119.8 0.8 copy.38
  120.7 1.6 %collective-permute-start.28 = (bf16[272,128]{1,0:T(8,128)(2,1)S(1)}, bf16[272,128]{1,0:T(8,128)(2,1)S(1)}, u32[]{:S(2)}, u32[]{:S(2)}) collective-permute-start(bf16[272,128]{1,0:T(8,128)(2,1)S(1)} %get-tuple-element.136), channel_id=1, source_target_pairs={{0,16},{8,24},{16,0},{24,8},{1,17},{9,25},{17,1},{25,9},{2,18},{10... | collective-permute-start | bytes 208904 | tf_op jit(solution)/shard_map/ppermute | solution.py:32
  122.3 2.8 %collective-permute-start.29 = (bf16[272,128]{1,0:T(8,128)(2,1)S(1)}, bf16[272,128]{1,0:T(8,128)(2,1)S(1)}, u32[]{:S(2)}, u32[]{:S(2)}) collective-permute-start(bf16[272,128]{1,0:T(8,128)(2,1)S(1)} %get-tuple-element.137), channel_id=1, source_target_pairs={{0,24},{8,16},{16,8},{24,0},{1,25},{9,17},{17,9},{25,1},{2,26},{10... | collective-permute-start | bytes 208904 | tf_op jit(solution)/shard_map/ppermute | solution.py:32
  125.0 3.2 %pad_maximum_fusion = bf16[1024,2,256]{2,1,0:T(2,128)(2,1)} fusion(bf16[1024,1,256]{2,1,0:T(2,128)(2,1)S(1)} %copy.38, bf16[1024,1,256]{2,1,0:T(2,128)(2,1)S(1)} %copy.37), kind=kLoop, calls=%fused_computation.3 | loop fusion | flops 2097152 | bytes 2097152 | tf_op jit(solution)/shard_map/stack | solution.py:610
  128.2 0.2 fresh.1
  128.5 1.1 collective-permute-done.28.refs_2_
  129.6 0.4 finish.1
  130.1 1.2 collective-permute-done.30
  131.4 0.7 maximum_bitcast_fusion
  (73 shorter events, 2.2 us)
Async XLA Ops:
  0.6 16.3 %collective-permute-start.2 = (bf16[1024,256]{1,0:T(8,128)(2,1)}, bf16[1024,256]{1,0:T(8,128)(2,1)S(1)}, u32[]{:S(2)}, u32[]{:S(2)}) collective-permute-start(bf16[1024,256]{1,0:T(8,128)(2,1)} %refs_0_), channel_id=1, source_target_pairs={{0,1},{1,0},{2,3},{3,2},{4,5},{5,4},{6,7},{7,6},{8,9},{9,8},{10,11... | collective-permute-start | bytes 1572872 | tf_op jit(solution)/shard_map/ppermute | solution.py:23
  1.2 17.2 %collective-permute-start = (bf16[1024,256]{1,0:T(8,128)(2,1)}, bf16[1024,256]{1,0:T(8,128)(2,1)S(1)}, u32[]{:S(2)}, u32[]{:S(2)}) collective-permute-start(bf16[1024,256]{1,0:T(8,128)(2,1)} %refs_0_), channel_id=1, source_target_pairs={{0,8},{8,0},{16,24},{24,16},{1,9},{9,1},{17,25},{25,17},{2,10},{10... | collective-permute-start | bytes 1572872 | tf_op jit(solution)/shard_map/ppermute | solution.py:476
  3.8 14.6 %collective-permute-start.1 = (bf16[1024,256]{1,0:T(8,128)(2,1)}, bf16[1024,256]{1,0:T(8,128)(2,1)S(1)}, u32[]{:S(2)}, u32[]{:S(2)}) collective-permute-start(bf16[1024,256]{1,0:T(8,128)(2,1)} %refs_0_), channel_id=1, source_target_pairs={{8,16},{16,8},{9,17},{17,9},{10,18},{18,10},{11,19},{19,11},{12,20... | collective-permute-start | bytes 1572872 | tf_op jit(solution)/shard_map/ppermute | solution.py:476
  4.5 11.0 %collective-permute-start.3 = (bf16[1024,256]{1,0:T(8,128)(2,1)}, bf16[1024,256]{1,0:T(8,128)(2,1)S(1)}, u32[]{:S(2)}, u32[]{:S(2)}) collective-permute-start(bf16[1024,256]{1,0:T(8,128)(2,1)} %refs_1_), channel_id=1, source_target_pairs={{0,1},{1,0},{2,3},{3,2},{4,5},{5,4},{6,7},{7,6},{8,9},{9,8},{10,11... | collective-permute-start | bytes 1572872 | tf_op jit(solution)/shard_map/ppermute | solution.py:23
  5.7 1.0 copy-start
  6.8 1.0 copy-start.1
  7.9 1.0 copy-start.2
  18.5 7.1 %collective-permute-start.6 = (bf16[1024,256]{1,0:T(8,128)(2,1)S(1)}, bf16[1024,256]{1,0:T(8,128)(2,1)S(1)}, u32[]{:S(2)}, u32[]{:S(2)}) collective-permute-start(bf16[1024,256]{1,0:T(8,128)(2,1)S(1)} %collective-permute-done.refs_0_), channel_id=1, source_target_pairs={{0,1},{1,0},{2,3},{3,2},{4,5},{5,4},{6,7},{7,6},{8,9},{9,8},{10,11... | collective-permute-start | bytes 1572872 | tf_op jit(solution)/shard_map/ppermute | solution.py:23
  18.9 6.7 %collective-permute-start.7 = (bf16[1024,256]{1,0:T(8,128)(2,1)S(1)}, bf16[1024,256]{1,0:T(8,128)(2,1)S(1)}, u32[]{:S(2)}, u32[]{:S(2)}) collective-permute-start(bf16[1024,256]{1,0:T(8,128)(2,1)S(1)} %collective-permute-done.1.refs_1_), channel_id=1, source_target_pairs={{0,1},{1,0},{2,3},{3,2},{4,5},{5,4},{6,7},{7,6},{8,9},{9,8},{10,11... | collective-permute-start | bytes 1572872 | tf_op jit(solution)/shard_map/ppermute | solution.py:23
  19.0 18.2 %collective-permute-start.5 = (bf16[1152,256]{1,0:T(8,128)(2,1)S(1)}, bf16[1152,256]{1,0:T(8,128)(2,1)S(1)}, u32[]{:S(2)}, u32[]{:S(2)}) collective-permute-start(bf16[1152,256]{1,0:T(8,128)(2,1)S(1)} %pack.1), channel_id=1, source_target_pairs={{0,8},{8,0},{16,24},{24,16},{1,9},{9,1},{17,25},{25,17},{2,10},{10... | collective-permute-start | bytes 1769480 | tf_op jit(solution)/shard_map/ppermute | solution.py:476
  23.3 13.9 %collective-permute-start.4 = (bf16[1024,256]{1,0:T(8,128)(2,1)S(1)}, bf16[1024,256]{1,0:T(8,128)(2,1)S(1)}, u32[]{:S(2)}, u32[]{:S(2)}) collective-permute-start(bf16[1024,256]{1,0:T(8,128)(2,1)S(1)} %collective-permute-done.refs_0_), channel_id=1, source_target_pairs={{8,16},{16,8},{9,17},{17,9},{10,18},{18,10},{11,19},{19,11},{12,20... | collective-permute-start | bytes 1572872 | tf_op jit(solution)/shard_map/ppermute | solution.py:476
  37.3 3.5 %collective-permute-start.10 = (bf16[1152,256]{1,0:T(8,128)(2,1)S(1)}, bf16[1152,256]{1,0:T(8,128)(2,1)S(1)}, u32[]{:S(2)}, u32[]{:S(2)}) collective-permute-start(bf16[1152,256]{1,0:T(8,128)(2,1)S(1)} %collective-permute-done.5.refs_0_), channel_id=1, source_target_pairs={{0,1},{1,0},{2,3},{3,2},{4,5},{5,4},{6,7},{7,6},{8,9},{9,8},{10,11... | collective-permute-start | bytes 1769480 | tf_op jit(solution)/shard_map/ppermute | solution.py:23
  37.3 16.2 %collective-permute-start.9 = (bf16[1024,256]{1,0:T(8,128)(2,1)S(1)}, bf16[1024,256]{1,0:T(8,128)(2,1)S(1)}, u32[]{:S(2)}, u32[]{:S(2)}) collective-permute-start(bf16[1024,256]{1,0:T(8,128)(2,1)S(1)} %collective-permute-done.1.refs_1_), channel_id=1, source_target_pairs={{8,0},{16,24},{9,1},{17,25},{10,2},{18,26},{11,3},{19,27},{12,4},{... | collective-permute-start | bytes 1572872 | tf_op jit(solution)/shard_map/ppermute | solution.py:476
  38.5 18.5 %collective-permute-start.8 = (bf16[1152,256]{1,0:T(8,128)(2,1)S(1)}, bf16[1152,256]{1,0:T(8,128)(2,1)S(1)}, u32[]{:S(2)}, u32[]{:S(2)}) collective-permute-start(bf16[1152,256]{1,0:T(8,128)(2,1)S(1)} %pack.1), channel_id=1, source_target_pairs={{8,16},{16,8},{9,17},{17,9},{10,18},{18,10},{11,19},{19,11},{12,20... | collective-permute-start | bytes 1769480 | tf_op jit(solution)/shard_map/ppermute | solution.py:476
  40.7 13.0 %copy-start.7 = (s32[32]{0:T(128)S(1)}, s32[32]{0:T(128)}, u32[]{:S(2)}) copy-start(s32[32]{0:T(128)} %param.15) | copy-start | bytes 388
  53.6 2.0 %collective-permute-start.11 = (bf16[1024,256]{1,0:T(8,128)(2,1)S(1)}, bf16[1024,256]{1,0:T(8,128)(2,1)S(1)}, u32[]{:S(2)}, u32[]{:S(2)}) collective-permute-start(bf16[1024,256]{1,0:T(8,128)(2,1)S(1)} %add.74.refs_0_), channel_id=1, source_target_pairs={{0,1},{1,0},{2,3},{3,2},{4,5},{5,4},{6,7},{7,6},{8,9},{9,8},{10,11... | collective-permute-start | bytes 1572872 | tf_op jit(solution)/shard_map/ppermute | solution.py:23
  55.2 3.5 %copy-start.4 = (s32[32,32]{1,0:T(8,128)S(1)}, s32[32,32]{1,0:T(8,128)}, u32[]{:S(2)}) copy-start(s32[32,32]{1,0:T(8,128)} %param.14) | copy-start | bytes 12292
  57.1 3.7 %collective-permute-start.15 = (bf16[1152,256]{1,0:T(8,128)(2,1)S(1)}, bf16[1152,256]{1,0:T(8,128)(2,1)S(1)}, u32[]{:S(2)}, u32[]{:S(2)}) collective-permute-start(bf16[1152,256]{1,0:T(8,128)(2,1)S(1)} %collective-permute-done.8.refs_0_), channel_id=1, source_target_pairs={{0,1},{1,0},{2,3},{3,2},{4,5},{5,4},{6,7},{7,6},{8,9},{9,8},{10,11... | collective-permute-start | bytes 1769480 | tf_op jit(solution)/shard_map/ppermute | solution.py:23
  57.3 16.1 %collective-permute-start.14 = (bf16[1024,256]{1,0:T(8,128)(2,1)S(1)}, bf16[1024,256]{1,0:T(8,128)(2,1)S(1)}, u32[]{:S(2)}, u32[]{:S(2)}) collective-permute-start(bf16[1024,256]{1,0:T(8,128)(2,1)S(1)} %collective-permute-done.4), channel_id=1, source_target_pairs={{8,0},{16,24},{9,1},{17,25},{10,2},{18,26},{11,3},{19,27},{12,4},{... | collective-permute-start | bytes 1572872 | tf_op jit(solution)/shard_map/ppermute | solution.py:476
  59.3 18.9 %collective-permute-start.13 = (bf16[1152,256]{1,0:T(8,128)(2,1)S(1)}, bf16[1152,256]{1,0:T(8,128)(2,1)S(1)}, u32[]{:S(2)}, u32[]{:S(2)}) collective-permute-start(bf16[1152,256]{1,0:T(8,128)(2,1)S(1)} %collective-permute-done.5.refs_0_), channel_id=1, source_target_pairs={{8,16},{16,8},{9,17},{17,9},{10,18},{18,10},{11,19},{19,11},{12,20... | collective-permute-start | bytes 1769480 | tf_op jit(solution)/shard_map/ppermute | solution.py:476
  60.8 13.0 %copy-start.6 = (f32[2,256]{1,0:T(2,128)S(1)}, f32[2,256]{1,0:T(2,128)}, u32[]{:S(2)}) copy-start(f32[2,256]{1,0:T(2,128)} %param.11) | copy-start | bytes 6148
  73.4 3.4 %collective-permute-start.16 = (bf16[1024,256]{1,0:T(8,128)(2,1)S(1)}, bf16[1024,256]{1,0:T(8,128)(2,1)S(1)}, u32[]{:S(2)}, u32[]{:S(2)}) collective-permute-start(bf16[1024,256]{1,0:T(8,128)(2,1)S(1)} %collective-permute-done.14.refs_0_), channel_id=1, source_target_pairs={{0,1},{1,0},{2,3},{3,2},{4,5},{5,4},{6,7},{7,6},{8,9},{9,8},{10,11... | collective-permute-start | bytes 1572872 | tf_op jit(solution)/shard_map/ppermute | solution.py:23
  73.8 19.5 %collective-permute-start.12 = (bf16[1152,256]{1,0:T(8,128)(2,1)S(1)}, bf16[1152,256]{1,0:T(8,128)(2,1)S(1)}, u32[]{:S(2)}, u32[]{:S(2)}) collective-permute-start(bf16[1152,256]{1,0:T(8,128)(2,1)S(1)} %collective-permute-done.8.refs_0_), channel_id=1, source_target_pairs={{8,0},{16,24},{9,1},{17,25},{10,2},{18,26},{11,3},{19,27},{12,4},{... | collective-permute-start | bytes 1769480 | tf_op jit(solution)/shard_map/ppermute | solution.py:476
  78.3 1.4 %collective-permute-start.17 = (f32[1,256]{1,0:T(1,128)S(1)}, f32[1,256]{1,0:T(1,128)S(1)}, u32[]{:S(2)}, u32[]{:S(2)}) collective-permute-start(f32[1,256]{1,0:T(1,128)S(1)} %bitcast.32), channel_id=1, source_target_pairs={{0,1},{1,0},{2,3},{3,2},{4,5},{5,4},{6,7},{7,6},{8,9},{9,8},{10,11... | collective-permute-start | bytes 3080 | tf_op jit(solution)/shard_map/ppermute | solution.py:23
  79.7 12.3 %collective-permute-start.18 = (f32[1,256]{1,0:T(1,128)S(1)}, f32[1,256]{1,0:T(1,128)S(1)}, u32[]{:S(2)}, u32[]{:S(2)}) collective-permute-start(f32[1,256]{1,0:T(1,128)S(1)} %max.36), channel_id=1, source_target_pairs={{0,8},{8,0},{16,24},{24,16},{1,9},{9,1},{17,25},{25,17},{2,10},{10... | collective-permute-start | bytes 3080 | tf_op jit(solution)/shard_map/ppermute | solution.py:32
  80.8 12.5 %collective-permute-start.19 = (f32[1,256]{1,0:T(1,128)S(1)}, f32[1,256]{1,0:T(1,128)S(1)}, u32[]{:S(2)}, u32[]{:S(2)}) collective-permute-start(f32[1,256]{1,0:T(1,128)S(1)} %max.36), channel_id=1, source_target_pairs={{0,16},{8,24},{16,0},{24,8},{1,17},{9,25},{17,1},{25,9},{2,18},{10... | collective-permute-start | bytes 3080 | tf_op jit(solution)/shard_map/ppermute | solution.py:32
  81.3 12.0 %collective-permute-start.20 = (f32[1,256]{1,0:T(1,128)S(1)}, f32[1,256]{1,0:T(1,128)S(1)}, u32[]{:S(2)}, u32[]{:S(2)}) collective-permute-start(f32[1,256]{1,0:T(1,128)S(1)} %max.36), channel_id=1, source_target_pairs={{0,24},{8,16},{16,8},{24,0},{1,25},{9,17},{17,9},{25,1},{2,26},{10... | collective-permute-start | bytes 3080 | tf_op jit(solution)/shard_map/ppermute | solution.py:32
  84.1 27.7 %collective-permute-start.24 = (bf16[1152,256]{1,0:T(8,128)(2,1)S(1)}, bf16[1152,256]{1,0:T(8,128)(2,1)S(1)}, u32[]{:S(2)}, u32[]{:S(2)}) collective-permute-start(bf16[1152,256]{1,0:T(8,128)(2,1)S(1)} %collective-permute-done.13), channel_id=1, source_target_pairs={{8,0},{16,24},{9,1},{17,25},{10,2},{18,26},{11,3},{19,27},{12,4},{... | collective-permute-start | bytes 1769480 | tf_op jit(solution)/shard_map/ppermute | solution.py:476
  92.0 13.5 %collective-permute-start.21 = (bf16[128,256]{1,0:T(8,128)(2,1)S(1)}, bf16[128,256]{1,0:T(8,128)(2,1)S(1)}, u32[]{:S(2)}, u32[]{:S(2)}) collective-permute-start(bf16[128,256]{1,0:T(8,128)(2,1)S(1)} %slice.79), channel_id=1, source_target_pairs={{8,0},{16,24},{9,1},{17,25},{10,2},{18,26},{11,3},{19,27},{12,4},{... | collective-permute-start | bytes 196616 | tf_op jit(solution)/shard_map/ppermute | solution.py:519
  93.3 2.5 %copy-start.5 = (f32[1,256]{1,0:T(1,128)}, f32[1,256]{1,0:T(1,128)S(1)}, u32[]{:S(2)}) copy-start(f32[1,256]{1,0:T(1,128)S(1)} %add_sqrt_fusion) | copy-start | bytes 3076
  93.5 12.1 %collective-permute-start.23 = (bf16[1152,256]{1,0:T(8,128)(2,1)S(1)}, bf16[1152,256]{1,0:T(8,128)(2,1)S(1)}, u32[]{:S(2)}, u32[]{:S(2)}) collective-permute-start(bf16[1152,256]{1,0:T(8,128)(2,1)S(1)} %add.86.refs_0_), channel_id=1, source_target_pairs={{0,1},{1,0},{2,3},{3,2},{4,5},{5,4},{6,7},{7,6},{8,9},{9,8},{10,11... | collective-permute-start | bytes 1769480 | tf_op jit(solution)/shard_map/ppermute | solution.py:23
  93.8 13.3 %collective-permute-start.22 = (bf16[1024,128]{1,0:T(8,128)(2,1)S(1)}, bf16[1024,128]{1,0:T(8,128)(2,1)S(1)}, u32[]{:S(2)}, u32[]{:S(2)}) collective-permute-start(bf16[1024,128]{1,0:T(8,128)(2,1)S(1)} %get-tuple-element.157), channel_id=1, source_target_pairs={{0,1},{1,0},{2,3},{3,2},{4,5},{5,4},{6,7},{7,6},{8,9},{9,8},{10,11... | collective-permute-start | bytes 786440 | tf_op jit(solution)/shard_map/ppermute | solution.py:23
  105.6 6.3 %copy-start.3 = (bf16[4,8,2,256]{3,2,1,0:T(2,128)(2,1)S(1)}, bf16[4,8,2,256]{3,2,1,0:T(2,128)(2,1)}, u32[]{:S(2)}) copy-start(bf16[4,8,2,256]{3,2,1,0:T(2,128)(2,1)} %param.12) | copy-start | bytes 98308
  111.8 2.1 %collective-permute-start.25 = (bf16[1152,256]{1,0:T(8,128)(2,1)S(1)}, bf16[1152,256]{1,0:T(8,128)(2,1)S(1)}, u32[]{:S(2)}, u32[]{:S(2)}) collective-permute-start(bf16[1152,256]{1,0:T(8,128)(2,1)S(1)} %collective-permute-done.24.refs_0_), channel_id=1, source_target_pairs={{0,1},{1,0},{2,3},{3,2},{4,5},{5,4},{6,7},{7,6},{8,9},{9,8},{10,11... | collective-permute-start | bytes 1769480 | tf_op jit(solution)/shard_map/ppermute | solution.py:23
  115.5 1.6 %collective-permute-start.26 = (bf16[1024,128]{1,0:T(8,128)(2,1)S(1)}, bf16[1024,128]{1,0:T(8,128)(2,1)S(1)}, u32[]{:S(2)}, u32[]{:S(2)}) collective-permute-start(bf16[1024,128]{1,0:T(8,128)(2,1)S(1)} %get-tuple-element.155), channel_id=1, source_target_pairs={{0,1},{1,0},{2,3},{3,2},{4,5},{5,4},{6,7},{7,6},{8,9},{9,8},{10,11... | collective-permute-start | bytes 786440 | tf_op jit(solution)/shard_map/ppermute | solution.py:23
  120.6 7.9 %collective-permute-start.27 = (bf16[272,128]{1,0:T(8,128)(2,1)S(1)}, bf16[272,128]{1,0:T(8,128)(2,1)S(1)}, u32[]{:S(2)}, u32[]{:S(2)}) collective-permute-start(bf16[272,128]{1,0:T(8,128)(2,1)S(1)} %get-tuple-element.135), channel_id=1, source_target_pairs={{0,8},{8,0},{16,24},{24,16},{1,9},{9,1},{17,25},{25,17},{2,10},{10... | collective-permute-start | bytes 208904 | tf_op jit(solution)/shard_map/ppermute | solution.py:32
  120.7 8.9 %collective-permute-start.28 = (bf16[272,128]{1,0:T(8,128)(2,1)S(1)}, bf16[272,128]{1,0:T(8,128)(2,1)S(1)}, u32[]{:S(2)}, u32[]{:S(2)}) collective-permute-start(bf16[272,128]{1,0:T(8,128)(2,1)S(1)} %get-tuple-element.136), channel_id=1, source_target_pairs={{0,16},{8,24},{16,0},{24,8},{1,17},{9,25},{17,1},{25,9},{2,18},{10... | collective-permute-start | bytes 208904 | tf_op jit(solution)/shard_map/ppermute | solution.py:32
  122.3 7.3 %collective-permute-start.29 = (bf16[272,128]{1,0:T(8,128)(2,1)S(1)}, bf16[272,128]{1,0:T(8,128)(2,1)S(1)}, u32[]{:S(2)}, u32[]{:S(2)}) collective-permute-start(bf16[272,128]{1,0:T(8,128)(2,1)S(1)} %get-tuple-element.137), channel_id=1, source_target_pairs={{0,24},{8,16},{16,8},{24,0},{1,25},{9,17},{17,9},{25,1},{2,26},{10... | collective-permute-start | bytes 208904 | tf_op jit(solution)/shard_map/ppermute | solution.py:32
  130.0 1.3 collective-permute-start.30

commit v7 on v6

--- a/solution.py
+++ b/solution.py
@@ -450,9 +450,12 @@
     return out
 
 
-def smooth_of(raw_keys):
+def chip_top(raw_keys):
     top = jnp.max(jnp.abs(raw_keys), axis=0, keepdims=True)
-    top = functools.reduce(jnp.maximum, from_owners(top))
+    return functools.reduce(jnp.maximum, from_owners(top))
+
+
+def smooth_of(top):
     top = functools.reduce(jnp.maximum, from_groups(top))
     return jnp.sqrt(top + EPSILON)
 
@@ -515,10 +518,11 @@
     ka3, totals = barrier((ka3, totals))
     absorb("k", [ka3], (((0, 3),),))
     raw_keys = totals["k"]
-    vb2, raw_keys = barrier((vb2, raw_keys))
+    top = chip_top(raw_keys)
+    smooth = smooth_of(top)
+    vb2, top = barrier((vb2, top))
     far_query = lax.ppermute(vb2[depth:], "seq", line_pairs(3, 0, groups))
     va3 = send(vb2, 3, 0)
-    smooth = smooth_of(raw_keys)
     va2, vb2, smooth = barrier((va2, vb2, smooth))
     absorb("v", [va2 + vb2], (((0, 2), (1, 2)),))
     queries = [
@@ -578,7 +582,7 @@
         queries = from_groups(
             jnp.concatenate(jnp.split(own_query, own_query.shape[1] // columns, axis=1))
         )
-        smooth = smooth_of(raw_keys)
+        smooth = smooth_of(chip_top(raw_keys))
     _, owner_is, first_pages, group_at, own_query = early
     counts = token_counts(page_table, lengths, first_pages, pages_dev)
     counts = counts.reshape(groups, per_group, -1)
@@ -607,7 +611,9 @@
         (messages, keys, values, (own_query, my_smooth))
     )
     messages = to_groups(messages)
-    kv_cache = with_layout_constraint(jnp.stack([keys, values], axis=1), Layout((0, 1, 2)))
+    is_key = lax.broadcasted_iota(jnp.int32, (1, 2, 1), 1) == 0
+    kv_cache = jnp.where(is_key, keys[:, None, :], values[:, None, :])
+    kv_cache = with_layout_constraint(kv_cache, Layout((0, 1, 2)))
     own = fresh(late[0], late[1], *my_new, score_scale)
     messages, kv_cache, own = lax.optimization_barrier((messages, kv_cache, own))
     attention = finish(messages, own, step_count * per_group)

time: 133 us -> 132 us (level)
  waiting for transfers between devices: 55.1 us -> 57.3 us
  local copies, waits for them, and re-layouts: 4.82 us -> 3.2 us
    another operation x1 -> x0, other arithmetic: 3.19 us -> none  [on_device(): jnp.stack([keys, values], axis=1)]
    select_n x0 -> x1, other arithmetic: none -> 2.32 us  [on_device(): kv_cache = jnp.where(is_key, keys[:, None, :], values[:, None, :])]
    another operation x2 -> x0, local copies, waits for them, and re-layouts: 1.62 us -> none  [on_device(): jnp.stack([keys, values], axis=1)]
  transfers between devices with their start and end apart: 31 -> 31, of which waited for: 11 -> 11; matrix products, arithmetic and copies ran while one was open for 5% -> 4% of each run, Pallas kernels for 24% -> 24%
where the time goes in v7:
time: 132 us
  waiting for transfers between devices  57.3 us (43%)
  Pallas kernels  35.7 us (27%)
  starting transfers between devices  28.3 us (21%)
  other arithmetic  5.51 us (4%)
  local copies, waits for them, and re-layouts  3.2 us (2%)
  between operations  1.33 us (1%)
    ppermute x10, waiting for transfers between devices, send(): return lax.ppermute(x, 'seq', line_pairs(hop, parity, groups))  34 us
    pallas_call x16, Pallas kernels, project(): pl.pallas_call(functools.partial(project_kernel, hops, back, groups, owne...  21.8 us
    ppermute x10, starting transfers between devices, send(): return lax.ppermute(x, 'seq', line_pairs(hop, parity, groups))  15 us
    ppermute x1, waiting for transfers between devices, line_project(): far_query = lax.ppermute(vb2[depth:], 'seq', line_pairs(3, 0, groups))  10.7 us
    ppermute x6, starting transfers between devices, swapped(): return lax.ppermute(x, axis, [(i, partner(i, k, n)) for i in range(n)])  8.83 us
    ppermute x6, waiting for transfers between devices, swapped(): return lax.ppermute(x, axis, [(i, partner(i, k, n)) for i in range(n)])  8.17 us
    pallas_call x1, Pallas kernels, load(): pl.pallas_call(functools.partial(load_kernel, owners), out_shape=(jax.Sha...  6.57 us
    pallas_call x1, Pallas kernels, score(): pl.pallas_call(functools.partial(score_kernel, slots, parts, steps, scale...  4.73 us
  transfers between devices with their start and end apart: 31, of which 11 were waited for; matrix products, arithmetic and copies ran while one was open for 4% of the time, Pallas kernels for 24%

profile of v7, /device:TPU:0, one launch (start us, length us, event | category | flops | bytes accessed | tf_op | source)
XLA Modules:
  0.0 131.7 jit_solution(14456390492657145723)
XLA Ops:
  0.6 0.6 collective-permute-start.2
  1.2 2.6 %collective-permute-start = (bf16[1024,256]{1,0:T(8,128)(2,1)}, bf16[1024,256]{1,0:T(8,128)(2,1)S(1)}, u32[]{:S(2)}, u32[]{:S(2)}) collective-permute-start(bf16[1024,256]{1,0:T(8,128)(2,1)} %refs_0_), channel_id=1, source_target_pairs={{0,8},{8,0},{16,24},{24,16},{1,9},{9,1},{17,25},{25,17},{2,10},{10... | collective-permute-start | bytes 1572872 | tf_op jit(solution)/shard_map/ppermute | solution.py:479
  3.8 0.7 collective-permute-start.1
  4.5 0.2 collective-permute-start.3
  4.7 0.9 select_bitcast_fusion.query
  5.7 1.0 copy-done
  6.9 1.0 copy-done.1
  7.9 1.0 copy-done.2
  8.9 6.6 %load.1 = (bf16[1024,8192]{1,0:T(8,128)(2,1)S(1)}, f32[1024,256]{1,0:T(8,128)S(1)}, f32[1024,256]{1,0:T(8,128)S(1)}) custom-call(s32[2]{0:T(128)S(1)} %pad_add_fusion.place, bf16[1024,8192]{1,0:T(8,128)(2,1)} %hidden.1, bf16[1024,256]{1,0:T(8,128)(2,1)S(1)} %copy-done.2, bf16[1024,256]{1,0:T(8,128)(2,1)S(1)} %copy-done.1), custom_call_target="tpu_custom_call" | custom-call | flops 1073741824 | bytes 16777216 | tf_op jit(solution)/shard_map/load/pallas_call | solution.py:114
  15.5 1.4 %project.17.refs_1_ = f32[1024,256]{1,0:T(8,128)S(1)} custom-call(s32[2]{0:T(128)S(1)} %pad_add_fusion.place, bf16[1024,8192]{1,0:T(8,128)(2,1)S(1)} %get-tuple-element.81.left, bf16[1024,256]{1,0:T(8,128)(2,1)S(1)} %collective-permute-done.3.refs_0_, f32[1024,256]{1,0:T(8,128)S(1)} %get-tuple-element.83.refs_1_), custom_call_target="tpu_custom_call", output_to_operand_aliasing={{}: (3, {})} | custom-call | flops 536870912 | bytes 4718592 | tf_op jit(solution)/shard_map/project/pallas_call | solution.py:170
  17.0 1.4 %project.16.refs_2_ = f32[1024,256]{1,0:T(8,128)S(1)} custom-call(s32[2]{0:T(128)S(1)} %pad_add_fusion.place, bf16[1024,8192]{1,0:T(8,128)(2,1)S(1)} %get-tuple-element.81.left, bf16[1024,256]{1,0:T(8,128)(2,1)S(1)} %collective-permute-done.2.refs_0_, f32[1024,256]{1,0:T(8,128)S(1)} %get-tuple-element.82.refs_1_), custom_call_target="tpu_custom_call", output_to_operand_aliasing={{}: (3, {})} | custom-call | flops 536870912 | bytes 4718592 | tf_op jit(solution)/shard_map/project/pallas_call | solution.py:170
  18.5 0.4 collective-permute-start.6
  19.0 4.3 %collective-permute-start.5 = (bf16[1152,256]{1,0:T(8,128)(2,1)S(1)}, bf16[1152,256]{1,0:T(8,128)(2,1)S(1)}, u32[]{:S(2)}, u32[]{:S(2)}) collective-permute-start(bf16[1152,256]{1,0:T(8,128)(2,1)S(1)} %pack.1), channel_id=1, source_target_pairs={{0,8},{8,0},{16,24},{24,16},{1,9},{9,1},{17,25},{25,17},{2,10},{10... | collective-permute-start | bytes 1769480 | tf_op jit(solution)/shard_map/ppermute | solution.py:479
  23.3 0.7 collective-permute-start.4
  24.0 1.5 %project.18.refs_2_ = f32[1024,256]{1,0:T(8,128)S(1)} custom-call(s32[2]{0:T(128)S(1)} %pad_add_fusion.place, bf16[1024,8192]{1,0:T(8,128)(2,1)S(1)} %get-tuple-element.81.left, bf16[1024,256]{1,0:T(8,128)(2,1)S(1)} %collective-permute-done.refs_0_, bf16[1024,256]{1,0:T(8,128)(2,1)S(1)} %collective-permute-done.1.refs_1_, ...), custom_call_target="tpu_custom_call", output_to_operand_aliasing={{}: (4, {})} | custom-call | flops 1073741824 | bytes 7340032 | tf_op jit(solution)/shard_map/project/pallas_call | solution.py:170
  25.6 1.5 %project.19.refs_1_ = f32[1024,256]{1,0:T(8,128)S(1)} custom-call(s32[2]{0:T(128)S(1)} %pad_add_fusion.place, bf16[1024,8192]{1,0:T(8,128)(2,1)S(1)} %get-tuple-element.81.left, bf16[1024,256]{1,0:T(8,128)(2,1)S(1)} %collective-permute-done.6.refs_0_, bf16[1024,256]{1,0:T(8,128)(2,1)S(1)} %collective-permute-done.7.refs_1_, ...), custom_call_target="tpu_custom_call", output_to_operand_aliasing={{}: (4, {})} | custom-call | flops 1073741824 | bytes 7340032 | tf_op jit(solution)/shard_map/project/pallas_call | solution.py:170
  27.1 10.2 %collective-permute-done.5.refs_0_ = bf16[1152,256]{1,0:T(8,128)(2,1)S(1)} collective-permute-done((bf16[1152,256]{1,0:T(8,128)(2,1)S(1)}, bf16[1152,256]{1,0:T(8,128)(2,1)S(1)}, u32[]{:S(2)}, u32[]{:S(2)}) %collective-permute-start.5) | collective-permute-done | bytes 589856 | tf_op jit(solution)/shard_map/ppermute | solution.py:479
  37.3 1.3 collective-permute-start.9
  38.5 0.7 collective-permute-start.8
  39.3 1.4 %project.20.refs_1_ = f32[1024,256]{1,0:T(8,128)S(1)} custom-call(s32[2]{0:T(128)S(1)} %pad_add_fusion.place, bf16[1024,8192]{1,0:T(8,128)(2,1)S(1)} %get-tuple-element.81.left, bf16[1152,256]{1,0:T(8,128)(2,1)S(1)} %collective-permute-done.5.refs_0_, f32[1024,256]{1,0:T(8,128)S(1)} %project.17.refs_1_), custom_call_target="tpu_custom_call", output_to_operand_aliasing={{}: (3, {})} | custom-call | flops 536870912 | bytes 4718592 | tf_op jit(solution)/shard_map/project/pallas_call | solution.py:170
  40.7 1.4 %project.21.refs_1_ = f32[1024,256]{1,0:T(8,128)S(1)} custom-call(s32[2]{0:T(128)S(1)} %pad_add_fusion.place, bf16[1024,8192]{1,0:T(8,128)(2,1)S(1)} %get-tuple-element.81.left, bf16[1152,256]{1,0:T(8,128)(2,1)S(1)} %collective-permute-done.10.refs_0_, f32[1024,256]{1,0:T(8,128)S(1)} %project.20.refs_1_), custom_call_target="tpu_custom_call", output_to_operand_aliasing={{}: (3, {})} | custom-call | flops 536870912 | bytes 4718592 | tf_op jit(solution)/shard_map/project/pallas_call | solution.py:170
  42.2 11.3 %collective-permute-done.9 = bf16[1024,256]{1,0:T(8,128)(2,1)S(1)} collective-permute-done((bf16[1024,256]{1,0:T(8,128)(2,1)S(1)}, bf16[1024,256]{1,0:T(8,128)(2,1)S(1)}, u32[]{:S(2)}, u32[]{:S(2)}) %collective-permute-start.9) | collective-permute-done | bytes 524320 | tf_op jit(solution)/shard_map/ppermute | solution.py:479
  53.7 1.4 %project.22.refs_1_ = f32[1024,256]{1,0:T(8,128)S(1)} custom-call(s32[2]{0:T(128)S(1)} %pad_add_fusion.place, bf16[1024,8192]{1,0:T(8,128)(2,1)S(1)} %get-tuple-element.81.left, bf16[1024,256]{1,0:T(8,128)(2,1)S(1)} %add.74.refs_0_, f32[1024,256]{1,0:T(8,128)S(1)} %project.19.refs_1_), custom_call_target="tpu_custom_call", output_to_operand_aliasing={{}: (3, {})} | custom-call | flops 536870912 | bytes 4718592 | tf_op jit(solution)/shard_map/project/pallas_call | solution.py:170
  55.2 0.4 collective-permute-done.11.refs_0_
  55.6 1.4 %project.23.refs_1_ = f32[1024,256]{1,0:T(8,128)S(1)} custom-call(s32[2]{0:T(128)S(1)} %pad_add_fusion.place, bf16[1024,8192]{1,0:T(8,128)(2,1)S(1)} %get-tuple-element.81.left, bf16[1024,256]{1,0:T(8,128)(2,1)S(1)} %collective-permute-done.11.refs_0_, f32[1024,256]{1,0:T(8,128)S(1)} %project.22.refs_1_), custom_call_target="tpu_custom_call", output_to_operand_aliasing={{}: (3, {})} | custom-call | flops 536870912 | bytes 4718592 | tf_op jit(solution)/shard_map/project/pallas_call | solution.py:170
  57.1 0.2 collective-permute-start.15
  57.3 1.3 collective-permute-start.14
  58.7 0.6 convert_reduce_fusion
  59.3 0.7 project.24.refs_1_
  60.1 0.7 project.25.refs_1_
  60.8 12.5 %collective-permute-done.14.refs_0_ = bf16[1024,256]{1,0:T(8,128)(2,1)S(1)} collective-permute-done((bf16[1024,256]{1,0:T(8,128)(2,1)S(1)}, bf16[1024,256]{1,0:T(8,128)(2,1)S(1)}, u32[]{:S(2)}, u32[]{:S(2)}) %collective-permute-start.14) | collective-permute-done | bytes 524320 | tf_op jit(solution)/shard_map/ppermute | solution.py:479
  73.3 0.2 fusion.2
  73.6 0.2 fusion.1.count
  73.8 0.7 collective-permute-start.13
  74.5 1.5 %collective-permute-start.12 = (bf16[1152,256]{1,0:T(8,128)(2,1)S(1)}, bf16[1152,256]{1,0:T(8,128)(2,1)S(1)}, u32[]{:S(2)}, u32[]{:S(2)}) collective-permute-start(bf16[1152,256]{1,0:T(8,128)(2,1)S(1)} %collective-permute-done.8.refs_0_), channel_id=1, source_target_pairs={{8,0},{16,24},{9,1},{17,25},{10,2},{18,26},{11,3},{19,27},{12,4},{... | collective-permute-start | bytes 1769480 | tf_op jit(solution)/shard_map/ppermute | solution.py:479
  76.0 1.4 %project.26.refs_1_ = f32[1024,256]{1,0:T(8,128)S(1)} custom-call(s32[2]{0:T(128)S(1)} %pad_add_fusion.place, bf16[1024,8192]{1,0:T(8,128)(2,1)S(1)} %get-tuple-element.81.left, bf16[1024,256]{1,0:T(8,128)(2,1)S(1)} %collective-permute-done.14.refs_0_, f32[1024,256]{1,0:T(8,128)S(1)} %project.23.refs_1_), custom_call_target="tpu_custom_call", output_to_operand_aliasing={{}: (3, {})} | custom-call | flops 536870912 | bytes 4718592 | tf_op jit(solution)/shard_map/project/pallas_call | solution.py:170
  77.5 1.4 %project.27 = f32[1024,256]{1,0:T(8,128)S(1)} custom-call(s32[2]{0:T(128)S(1)} %pad_add_fusion.place, bf16[1024,8192]{1,0:T(8,128)(2,1)S(1)} %get-tuple-element.81.left, bf16[1024,256]{1,0:T(8,128)(2,1)S(1)} %collective-permute-done.16.refs_0_, f32[1024,256]{1,0:T(8,128)S(1)} %project.26.refs_1_), custom_call_target="tpu_custom_call", output_to_operand_aliasing={{}: (3, {})} | custom-call | flops 536870912 | bytes 4718592 | tf_op jit(solution)/shard_map/project/pallas_call | solution.py:170
  79.0 0.6 collective-permute-start.17
  79.6 0.8 collective-permute-done.17
  80.4 1.1 collective-permute-start.18
  81.5 0.5 collective-permute-start.19
  82.0 2.8 %collective-permute-start.20 = (f32[1,256]{1,0:T(1,128)S(1)}, f32[1,256]{1,0:T(1,128)S(1)}, u32[]{:S(2)}, u32[]{:S(2)}) collective-permute-start(f32[1,256]{1,0:T(1,128)S(1)} %max.36), channel_id=1, source_target_pairs={{0,24},{8,16},{16,8},{24,0},{1,25},{9,17},{17,9},{25,1},{2,26},{10... | collective-permute-start | bytes 3080 | tf_op jit(solution)/shard_map/ppermute | solution.py:32
  84.8 1.3 collective-permute-start.24
  86.1 6.2 %collective-permute-done.18 = f32[1,256]{1,0:T(1,128)S(1)} collective-permute-done((f32[1,256]{1,0:T(1,128)S(1)}, f32[1,256]{1,0:T(1,128)S(1)}, u32[]{:S(2)}, u32[]{:S(2)}) %collective-permute-start.18) | collective-permute-done | bytes 1056 | tf_op jit(solution)/shard_map/ppermute | solution.py:32
  92.2 1.3 collective-permute-start.21
  94.1 0.6 collective-permute-start.22
  94.6 1.4 %project.28.refs_1_ = f32[1024,256]{1,0:T(8,128)S(1)} custom-call(s32[2]{0:T(128)S(1)} %pad_add_fusion.place, bf16[1024,8192]{1,0:T(8,128)(2,1)S(1)} %get-tuple-element.81.left, bf16[1152,256]{1,0:T(8,128)(2,1)S(1)} %add.86.refs_0_, f32[1024,256]{1,0:T(8,128)S(1)} %project.25.refs_1_), custom_call_target="tpu_custom_call", output_to_operand_aliasing={{}: (3, {})} | custom-call | flops 536870912 | bytes 4718592 | tf_op jit(solution)/shard_map/project/pallas_call | solution.py:170
  96.1 10.7 %collective-permute-done.21 = bf16[128,256]{1,0:T(8,128)(2,1)S(1)} collective-permute-done((bf16[128,256]{1,0:T(8,128)(2,1)S(1)}, bf16[128,256]{1,0:T(8,128)(2,1)S(1)}, u32[]{:S(2)}, u32[]{:S(2)}) %collective-permute-start.21) | collective-permute-done | bytes 65568 | tf_op jit(solution)/shard_map/ppermute | solution.py:524
  106.9 1.4 %project.29.refs_1_ = f32[1024,256]{1,0:T(8,128)S(1)} custom-call(s32[2]{0:T(128)S(1)} %pad_add_fusion.place, bf16[1024,8192]{1,0:T(8,128)(2,1)S(1)} %get-tuple-element.81.left, bf16[1152,256]{1,0:T(8,128)(2,1)S(1)} %collective-permute-done.23.refs_0_, f32[1024,256]{1,0:T(8,128)S(1)} %project.28.refs_1_), custom_call_target="tpu_custom_call", output_to_operand_aliasing={{}: (3, {})} | custom-call | flops 536870912 | bytes 4718592 | tf_op jit(solution)/shard_map/project/pallas_call | solution.py:170
  108.4 4.7 %score.1 = (bf16[4,256,2048]{2,1,0:T(8,128)(2,1)S(1)}, f32[2,256]{1,0:T(2,128)S(1)}, f32[2,256]{1,0:T(2,128)S(1)}, f32[2,256]{1,0:T(2,128)S(1)}, f32[2,256]{1,0:T(2,128)S(1)}) custom-call(s32[4]{0:T(128)S(1)} %iota_xor_fusion.group, bf16[4,128,256]{2,1,0:T(8,128)(2,1)S(1)} %pad_maximum_fusion.query, f32[1,128]{1,0:T(1,128)S(1)} %broadcast_select_fusion.7.smooth, ...), custom_call_target="tpu_custom_call" | custom-call | flops 536870912 | bytes 4194304 | tf_op jit(solution)/shard_map/score/pallas_call | solution.py:241
  113.3 1.4 %project.30.refs_1_ = f32[1024,256]{1,0:T(8,128)S(1)} custom-call(s32[2]{0:T(128)S(1)} %pad_add_fusion.place, bf16[1024,8192]{1,0:T(8,128)(2,1)S(1)} %get-tuple-element.81.left, bf16[1152,256]{1,0:T(8,128)(2,1)S(1)} %collective-permute-done.24.refs_0_, f32[1024,256]{1,0:T(8,128)S(1)} %project.29.refs_1_), custom_call_target="tpu_custom_call", output_to_operand_aliasing={{}: (3, {})} | custom-call | flops 536870912 | bytes 4718592 | tf_op jit(solution)/shard_map/project/pallas_call | solution.py:170
  114.7 0.5 collective-permute-done.25.refs_0_
  115.2 1.4 %project.31 = f32[1024,256]{1,0:T(8,128)S(1)} custom-call(s32[2]{0:T(128)S(1)} %pad_add_fusion.place, bf16[1024,8192]{1,0:T(8,128)(2,1)S(1)} %get-tuple-element.81.left, bf16[1152,256]{1,0:T(8,128)(2,1)S(1)} %collective-permute-done.25.refs_0_, f32[1024,256]{1,0:T(8,128)S(1)} %project.30.refs_1_), custom_call_target="tpu_custom_call", output_to_operand_aliasing={{}: (3, {})} | custom-call | flops 536870912 | bytes 4718592 | tf_op jit(solution)/shard_map/project/pallas_call | solution.py:170
  116.8 0.2 collective-permute-start.26
  117.0 1.4 %collective-permute-done.26.refs_1_ = bf16[1024,128]{1,0:T(8,128)(2,1)S(1)} collective-permute-done((bf16[1024,128]{1,0:T(8,128)(2,1)S(1)}, bf16[1024,128]{1,0:T(8,128)(2,1)S(1)}, u32[]{:S(2)}, u32[]{:S(2)}) %collective-permute-start.26) | collective-permute-done | bytes 262176 | tf_op jit(solution)/shard_map/ppermute | solution.py:23
  118.4 1.8 %weigh.1 = (bf16[272,128]{1,0:T(8,128)(2,1)S(1)}, bf16[272,128]{1,0:T(8,128)(2,1)S(1)}, bf16[272,128]{1,0:T(8,128)(2,1)S(1)}, bf16[272,128]{1,0:T(8,128)(2,1)S(1)}) custom-call(bf16[4,256,2048]{2,1,0:T(8,128)(2,1)S(1)} %get-tuple-element.116.probs, bf16[1024,128]{1,0:T(8,128)(2,1)S(1)} %get-tuple-element.154.refs_0_, ...), custom_call_target="tpu_custom_call" | custom-call | flops 536870912 | bytes 4194304 | tf_op jit(solution)/shard_map/weigh/pallas_call | solution.py:316
  120.3 1.9 %collective-permute-start.28 = (bf16[272,128]{1,0:T(8,128)(2,1)S(1)}, bf16[272,128]{1,0:T(8,128)(2,1)S(1)}, u32[]{:S(2)}, u32[]{:S(2)}) collective-permute-start(bf16[272,128]{1,0:T(8,128)(2,1)S(1)} %get-tuple-element.134), channel_id=1, source_target_pairs={{0,16},{8,24},{16,0},{24,8},{1,17},{9,25},{17,1},{25,9},{2,18},{10... | collective-permute-start | bytes 208904 | tf_op jit(solution)/shard_map/ppermute | solution.py:32
  122.2 2.5 %collective-permute-start.29 = (bf16[272,128]{1,0:T(8,128)(2,1)S(1)}, bf16[272,128]{1,0:T(8,128)(2,1)S(1)}, u32[]{:S(2)}, u32[]{:S(2)}) collective-permute-start(bf16[272,128]{1,0:T(8,128)(2,1)S(1)} %get-tuple-element.135), channel_id=1, source_target_pairs={{0,24},{8,16},{16,8},{24,0},{1,25},{9,17},{17,9},{25,1},{2,26},{10... | collective-permute-start | bytes 208904 | tf_op jit(solution)/shard_map/ppermute | solution.py:32
  124.7 2.3 %broadcast_select_fusion = bf16[1024,2,256]{2,1,0:T(2,128)(2,1)} fusion(pred[2]{0:T(512)(128)(4,1)S(1)} %iota_compare_fusion.5, bf16[1024,256]{1,0:T(8,128)(2,1)S(1)} %minimum_convert_fusion, bf16[1024,256]{1,0:T(8,128)(2,1)S(1)} %minimum_convert_fusion.1), kind=kLoop, calls=%fused_computation.3 | loop fusion | flops 524288 | bytes 2097154 | tf_op jit(solution)/shard_map/jit(_where)/select_n | solution.py:615
  127.0 0.2 fresh.1
  127.2 2.0 %collective-permute-done.28.refs_2_ = bf16[272,128]{1,0:T(8,128)(2,1)S(1)} collective-permute-done((bf16[272,128]{1,0:T(8,128)(2,1)S(1)}, bf16[272,128]{1,0:T(8,128)(2,1)S(1)}, u32[]{:S(2)}, u32[]{:S(2)}) %collective-permute-start.28) | collective-permute-done | bytes 69664 | tf_op jit(solution)/shard_map/ppermute | solution.py:32
  129.2 0.4 finish.1
  129.8 1.2 collective-permute-done.30
  131.0 0.7 maximum_bitcast_fusion
  (72 shorter events, 1.8 us)
Async XLA Ops:
  0.6 16.3 %collective-permute-start.2 = (bf16[1024,256]{1,0:T(8,128)(2,1)}, bf16[1024,256]{1,0:T(8,128)(2,1)S(1)}, u32[]{:S(2)}, u32[]{:S(2)}) collective-permute-start(bf16[1024,256]{1,0:T(8,128)(2,1)} %refs_0_), channel_id=1, source_target_pairs={{0,1},{1,0},{2,3},{3,2},{4,5},{5,4},{6,7},{7,6},{8,9},{9,8},{10,11... | collective-permute-start | bytes 1572872 | tf_op jit(solution)/shard_map/ppermute | solution.py:23
  1.2 17.2 %collective-permute-start = (bf16[1024,256]{1,0:T(8,128)(2,1)}, bf16[1024,256]{1,0:T(8,128)(2,1)S(1)}, u32[]{:S(2)}, u32[]{:S(2)}) collective-permute-start(bf16[1024,256]{1,0:T(8,128)(2,1)} %refs_0_), channel_id=1, source_target_pairs={{0,8},{8,0},{16,24},{24,16},{1,9},{9,1},{17,25},{25,17},{2,10},{10... | collective-permute-start | bytes 1572872 | tf_op jit(solution)/shard_map/ppermute | solution.py:479
  3.8 14.6 %collective-permute-start.1 = (bf16[1024,256]{1,0:T(8,128)(2,1)}, bf16[1024,256]{1,0:T(8,128)(2,1)S(1)}, u32[]{:S(2)}, u32[]{:S(2)}) collective-permute-start(bf16[1024,256]{1,0:T(8,128)(2,1)} %refs_0_), channel_id=1, source_target_pairs={{8,16},{16,8},{9,17},{17,9},{10,18},{18,10},{11,19},{19,11},{12,20... | collective-permute-start | bytes 1572872 | tf_op jit(solution)/shard_map/ppermute | solution.py:479
  4.5 11.0 %collective-permute-start.3 = (bf16[1024,256]{1,0:T(8,128)(2,1)}, bf16[1024,256]{1,0:T(8,128)(2,1)S(1)}, u32[]{:S(2)}, u32[]{:S(2)}) collective-permute-start(bf16[1024,256]{1,0:T(8,128)(2,1)} %refs_1_), channel_id=1, source_target_pairs={{0,1},{1,0},{2,3},{3,2},{4,5},{5,4},{6,7},{7,6},{8,9},{9,8},{10,11... | collective-permute-start | bytes 1572872 | tf_op jit(solution)/shard_map/ppermute | solution.py:23
  5.7 1.0 copy-start
  6.8 1.0 copy-start.1
  7.9 1.0 copy-start.2
  18.5 7.1 %collective-permute-start.6 = (bf16[1024,256]{1,0:T(8,128)(2,1)S(1)}, bf16[1024,256]{1,0:T(8,128)(2,1)S(1)}, u32[]{:S(2)}, u32[]{:S(2)}) collective-permute-start(bf16[1024,256]{1,0:T(8,128)(2,1)S(1)} %collective-permute-done.refs_0_), channel_id=1, source_target_pairs={{0,1},{1,0},{2,3},{3,2},{4,5},{5,4},{6,7},{7,6},{8,9},{9,8},{10,11... | collective-permute-start | bytes 1572872 | tf_op jit(solution)/shard_map/ppermute | solution.py:23
  18.9 6.7 %collective-permute-start.7 = (bf16[1024,256]{1,0:T(8,128)(2,1)S(1)}, bf16[1024,256]{1,0:T(8,128)(2,1)S(1)}, u32[]{:S(2)}, u32[]{:S(2)}) collective-permute-start(bf16[1024,256]{1,0:T(8,128)(2,1)S(1)} %collective-permute-done.1.refs_1_), channel_id=1, source_target_pairs={{0,1},{1,0},{2,3},{3,2},{4,5},{5,4},{6,7},{7,6},{8,9},{9,8},{10,11... | collective-permute-start | bytes 1572872 | tf_op jit(solution)/shard_map/ppermute | solution.py:23
  19.0 18.2 %collective-permute-start.5 = (bf16[1152,256]{1,0:T(8,128)(2,1)S(1)}, bf16[1152,256]{1,0:T(8,128)(2,1)S(1)}, u32[]{:S(2)}, u32[]{:S(2)}) collective-permute-start(bf16[1152,256]{1,0:T(8,128)(2,1)S(1)} %pack.1), channel_id=1, source_target_pairs={{0,8},{8,0},{16,24},{24,16},{1,9},{9,1},{17,25},{25,17},{2,10},{10... | collective-permute-start | bytes 1769480 | tf_op jit(solution)/shard_map/ppermute | solution.py:479
  23.3 13.9 %collective-permute-start.4 = (bf16[1024,256]{1,0:T(8,128)(2,1)S(1)}, bf16[1024,256]{1,0:T(8,128)(2,1)S(1)}, u32[]{:S(2)}, u32[]{:S(2)}) collective-permute-start(bf16[1024,256]{1,0:T(8,128)(2,1)S(1)} %collective-permute-done.refs_0_), channel_id=1, source_target_pairs={{8,16},{16,8},{9,17},{17,9},{10,18},{18,10},{11,19},{19,11},{12,20... | collective-permute-start | bytes 1572872 | tf_op jit(solution)/shard_map/ppermute | solution.py:479
  27.1 26.6 %copy-start.7 = (s32[32]{0:T(128)S(1)}, s32[32]{0:T(128)}, u32[]{:S(2)}) copy-start(s32[32]{0:T(128)} %param.15) | copy-start | bytes 388
  37.3 3.5 %collective-permute-start.10 = (bf16[1152,256]{1,0:T(8,128)(2,1)S(1)}, bf16[1152,256]{1,0:T(8,128)(2,1)S(1)}, u32[]{:S(2)}, u32[]{:S(2)}) collective-permute-start(bf16[1152,256]{1,0:T(8,128)(2,1)S(1)} %collective-permute-done.5.refs_0_), channel_id=1, source_target_pairs={{0,1},{1,0},{2,3},{3,2},{4,5},{5,4},{6,7},{7,6},{8,9},{9,8},{10,11... | collective-permute-start | bytes 1769480 | tf_op jit(solution)/shard_map/ppermute | solution.py:23
  37.3 16.2 %collective-permute-start.9 = (bf16[1024,256]{1,0:T(8,128)(2,1)S(1)}, bf16[1024,256]{1,0:T(8,128)(2,1)S(1)}, u32[]{:S(2)}, u32[]{:S(2)}) collective-permute-start(bf16[1024,256]{1,0:T(8,128)(2,1)S(1)} %collective-permute-done.1.refs_1_), channel_id=1, source_target_pairs={{8,0},{16,24},{9,1},{17,25},{10,2},{18,26},{11,3},{19,27},{12,4},{... | collective-permute-start | bytes 1572872 | tf_op jit(solution)/shard_map/ppermute | solution.py:479
  38.5 18.5 %collective-permute-start.8 = (bf16[1152,256]{1,0:T(8,128)(2,1)S(1)}, bf16[1152,256]{1,0:T(8,128)(2,1)S(1)}, u32[]{:S(2)}, u32[]{:S(2)}) collective-permute-start(bf16[1152,256]{1,0:T(8,128)(2,1)S(1)} %pack.1), channel_id=1, source_target_pairs={{8,16},{16,8},{9,17},{17,9},{10,18},{18,10},{11,19},{19,11},{12,20... | collective-permute-start | bytes 1769480 | tf_op jit(solution)/shard_map/ppermute | solution.py:479
  53.6 2.0 %collective-permute-start.11 = (bf16[1024,256]{1,0:T(8,128)(2,1)S(1)}, bf16[1024,256]{1,0:T(8,128)(2,1)S(1)}, u32[]{:S(2)}, u32[]{:S(2)}) collective-permute-start(bf16[1024,256]{1,0:T(8,128)(2,1)S(1)} %add.74.refs_0_), channel_id=1, source_target_pairs={{0,1},{1,0},{2,3},{3,2},{4,5},{5,4},{6,7},{7,6},{8,9},{9,8},{10,11... | collective-permute-start | bytes 1572872 | tf_op jit(solution)/shard_map/ppermute | solution.py:23
  53.7 5.0 %copy-start.4 = (s32[32,32]{1,0:T(8,128)S(1)}, s32[32,32]{1,0:T(8,128)}, u32[]{:S(2)}) copy-start(s32[32,32]{1,0:T(8,128)} %param.14) | copy-start | bytes 12292
  57.1 3.0 %collective-permute-start.15 = (bf16[1152,256]{1,0:T(8,128)(2,1)S(1)}, bf16[1152,256]{1,0:T(8,128)(2,1)S(1)}, u32[]{:S(2)}, u32[]{:S(2)}) collective-permute-start(bf16[1152,256]{1,0:T(8,128)(2,1)S(1)} %collective-permute-done.8.refs_0_), channel_id=1, source_target_pairs={{0,1},{1,0},{2,3},{3,2},{4,5},{5,4},{6,7},{7,6},{8,9},{9,8},{10,11... | collective-permute-start | bytes 1769480 | tf_op jit(solution)/shard_map/ppermute | solution.py:23
  57.3 16.1 %collective-permute-start.14 = (bf16[1024,256]{1,0:T(8,128)(2,1)S(1)}, bf16[1024,256]{1,0:T(8,128)(2,1)S(1)}, u32[]{:S(2)}, u32[]{:S(2)}) collective-permute-start(bf16[1024,256]{1,0:T(8,128)(2,1)S(1)} %collective-permute-done.4), channel_id=1, source_target_pairs={{8,0},{16,24},{9,1},{17,25},{10,2},{18,26},{11,3},{19,27},{12,4},{... | collective-permute-start | bytes 1572872 | tf_op jit(solution)/shard_map/ppermute | solution.py:479
  59.3 14.5 %copy-start.6 = (f32[2,256]{1,0:T(2,128)S(1)}, f32[2,256]{1,0:T(2,128)}, u32[]{:S(2)}) copy-start(f32[2,256]{1,0:T(2,128)} %param.11) | copy-start | bytes 6148
  73.3 4.1 %collective-permute-start.16 = (bf16[1024,256]{1,0:T(8,128)(2,1)S(1)}, bf16[1024,256]{1,0:T(8,128)(2,1)S(1)}, u32[]{:S(2)}, u32[]{:S(2)}) collective-permute-start(bf16[1024,256]{1,0:T(8,128)(2,1)S(1)} %collective-permute-done.14.refs_0_), channel_id=1, source_target_pairs={{0,1},{1,0},{2,3},{3,2},{4,5},{5,4},{6,7},{7,6},{8,9},{9,8},{10,11... | collective-permute-start | bytes 1572872 | tf_op jit(solution)/shard_map/ppermute | solution.py:23
  73.8 11.0 %collective-permute-start.13 = (bf16[1152,256]{1,0:T(8,128)(2,1)S(1)}, bf16[1152,256]{1,0:T(8,128)(2,1)S(1)}, u32[]{:S(2)}, u32[]{:S(2)}) collective-permute-start(bf16[1152,256]{1,0:T(8,128)(2,1)S(1)} %collective-permute-done.5.refs_0_), channel_id=1, source_target_pairs={{8,16},{16,8},{9,17},{17,9},{10,18},{18,10},{11,19},{19,11},{12,20... | collective-permute-start | bytes 1769480 | tf_op jit(solution)/shard_map/ppermute | solution.py:479
  74.5 19.1 %collective-permute-start.12 = (bf16[1152,256]{1,0:T(8,128)(2,1)S(1)}, bf16[1152,256]{1,0:T(8,128)(2,1)S(1)}, u32[]{:S(2)}, u32[]{:S(2)}) collective-permute-start(bf16[1152,256]{1,0:T(8,128)(2,1)S(1)} %collective-permute-done.8.refs_0_), channel_id=1, source_target_pairs={{8,0},{16,24},{9,1},{17,25},{10,2},{18,26},{11,3},{19,27},{12,4},{... | collective-permute-start | bytes 1769480 | tf_op jit(solution)/shard_map/ppermute | solution.py:479
  79.0 1.4 %collective-permute-start.17 = (f32[1,256]{1,0:T(1,128)S(1)}, f32[1,256]{1,0:T(1,128)S(1)}, u32[]{:S(2)}, u32[]{:S(2)}) collective-permute-start(f32[1,256]{1,0:T(1,128)S(1)} %bitcast.28), channel_id=1, source_target_pairs={{0,1},{1,0},{2,3},{3,2},{4,5},{5,4},{6,7},{7,6},{8,9},{9,8},{10,11... | collective-permute-start | bytes 3080 | tf_op jit(solution)/shard_map/ppermute | solution.py:23
  80.4 11.9 %collective-permute-start.18 = (f32[1,256]{1,0:T(1,128)S(1)}, f32[1,256]{1,0:T(1,128)S(1)}, u32[]{:S(2)}, u32[]{:S(2)}) collective-permute-start(f32[1,256]{1,0:T(1,128)S(1)} %max.36), channel_id=1, source_target_pairs={{0,8},{8,0},{16,24},{24,16},{1,9},{9,1},{17,25},{25,17},{2,10},{10... | collective-permute-start | bytes 3080 | tf_op jit(solution)/shard_map/ppermute | solution.py:32
  81.5 12.1 %collective-permute-start.19 = (f32[1,256]{1,0:T(1,128)S(1)}, f32[1,256]{1,0:T(1,128)S(1)}, u32[]{:S(2)}, u32[]{:S(2)}) collective-permute-start(f32[1,256]{1,0:T(1,128)S(1)} %max.36), channel_id=1, source_target_pairs={{0,16},{8,24},{16,0},{24,8},{1,17},{9,25},{17,1},{25,9},{2,18},{10... | collective-permute-start | bytes 3080 | tf_op jit(solution)/shard_map/ppermute | solution.py:32
  82.0 11.6 %collective-permute-start.20 = (f32[1,256]{1,0:T(1,128)S(1)}, f32[1,256]{1,0:T(1,128)S(1)}, u32[]{:S(2)}, u32[]{:S(2)}) collective-permute-start(f32[1,256]{1,0:T(1,128)S(1)} %max.36), channel_id=1, source_target_pairs={{0,24},{8,16},{16,8},{24,0},{1,25},{9,17},{17,9},{25,1},{2,26},{10... | collective-permute-start | bytes 3080 | tf_op jit(solution)/shard_map/ppermute | solution.py:32
  84.8 28.3 %collective-permute-start.24 = (bf16[1152,256]{1,0:T(8,128)(2,1)S(1)}, bf16[1152,256]{1,0:T(8,128)(2,1)S(1)}, u32[]{:S(2)}, u32[]{:S(2)}) collective-permute-start(bf16[1152,256]{1,0:T(8,128)(2,1)S(1)} %collective-permute-done.13), channel_id=1, source_target_pairs={{8,0},{16,24},{9,1},{17,25},{10,2},{18,26},{11,3},{19,27},{12,4},{... | collective-permute-start | bytes 1769480 | tf_op jit(solution)/shard_map/ppermute | solution.py:479
  92.2 14.6 %collective-permute-start.21 = (bf16[128,256]{1,0:T(8,128)(2,1)S(1)}, bf16[128,256]{1,0:T(8,128)(2,1)S(1)}, u32[]{:S(2)}, u32[]{:S(2)}) collective-permute-start(bf16[128,256]{1,0:T(8,128)(2,1)S(1)} %slice.79), channel_id=1, source_target_pairs={{8,0},{16,24},{9,1},{17,25},{10,2},{18,26},{11,3},{19,27},{12,4},{... | collective-permute-start | bytes 196616 | tf_op jit(solution)/shard_map/ppermute | solution.py:524
  93.6 14.8 %copy-start.5 = (f32[1,256]{1,0:T(1,128)}, f32[1,256]{1,0:T(1,128)S(1)}, u32[]{:S(2)}) copy-start(f32[1,256]{1,0:T(1,128)S(1)} %add_sqrt_fusion) | copy-start | bytes 3076
  93.8 13.1 %collective-permute-start.23 = (bf16[1152,256]{1,0:T(8,128)(2,1)S(1)}, bf16[1152,256]{1,0:T(8,128)(2,1)S(1)}, u32[]{:S(2)}, u32[]{:S(2)}) collective-permute-start(bf16[1152,256]{1,0:T(8,128)(2,1)S(1)} %add.86.refs_0_), channel_id=1, source_target_pairs={{0,1},{1,0},{2,3},{3,2},{4,5},{5,4},{6,7},{7,6},{8,9},{9,8},{10,11... | collective-permute-start | bytes 1769480 | tf_op jit(solution)/shard_map/ppermute | solution.py:23
  94.1 14.3 %collective-permute-start.22 = (bf16[1024,128]{1,0:T(8,128)(2,1)S(1)}, bf16[1024,128]{1,0:T(8,128)(2,1)S(1)}, u32[]{:S(2)}, u32[]{:S(2)}) collective-permute-start(bf16[1024,128]{1,0:T(8,128)(2,1)S(1)} %get-tuple-element.155), channel_id=1, source_target_pairs={{0,1},{1,0},{2,3},{3,2},{4,5},{5,4},{6,7},{7,6},{8,9},{9,8},{10,11... | collective-permute-start | bytes 786440 | tf_op jit(solution)/shard_map/ppermute | solution.py:23
  96.1 17.1 %copy-start.3 = (bf16[4,8,2,256]{3,2,1,0:T(2,128)(2,1)S(1)}, bf16[4,8,2,256]{3,2,1,0:T(2,128)(2,1)}, u32[]{:S(2)}) copy-start(bf16[4,8,2,256]{3,2,1,0:T(2,128)(2,1)} %param.12) | copy-start | bytes 98308
  113.1 2.1 %collective-permute-start.25 = (bf16[1152,256]{1,0:T(8,128)(2,1)S(1)}, bf16[1152,256]{1,0:T(8,128)(2,1)S(1)}, u32[]{:S(2)}, u32[]{:S(2)}) collective-permute-start(bf16[1152,256]{1,0:T(8,128)(2,1)S(1)} %collective-permute-done.24.refs_0_), channel_id=1, source_target_pairs={{0,1},{1,0},{2,3},{3,2},{4,5},{5,4},{6,7},{7,6},{8,9},{9,8},{10,11... | collective-permute-start | bytes 1769480 | tf_op jit(solution)/shard_map/ppermute | solution.py:23
  116.8 1.6 %collective-permute-start.26 = (bf16[1024,128]{1,0:T(8,128)(2,1)S(1)}, bf16[1024,128]{1,0:T(8,128)(2,1)S(1)}, u32[]{:S(2)}, u32[]{:S(2)}) collective-permute-start(bf16[1024,128]{1,0:T(8,128)(2,1)S(1)} %get-tuple-element.153), channel_id=1, source_target_pairs={{0,1},{1,0},{2,3},{3,2},{4,5},{5,4},{6,7},{7,6},{8,9},{9,8},{10,11... | collective-permute-start | bytes 786440 | tf_op jit(solution)/shard_map/ppermute | solution.py:23
  120.2 7.0 %collective-permute-start.27 = (bf16[272,128]{1,0:T(8,128)(2,1)S(1)}, bf16[272,128]{1,0:T(8,128)(2,1)S(1)}, u32[]{:S(2)}, u32[]{:S(2)}) collective-permute-start(bf16[272,128]{1,0:T(8,128)(2,1)S(1)} %get-tuple-element.133), channel_id=1, source_target_pairs={{0,8},{8,0},{16,24},{24,16},{1,9},{9,1},{17,25},{25,17},{2,10},{10... | collective-permute-start | bytes 208904 | tf_op jit(solution)/shard_map/ppermute | solution.py:32
  120.3 8.9 %collective-permute-start.28 = (bf16[272,128]{1,0:T(8,128)(2,1)S(1)}, bf16[272,128]{1,0:T(8,128)(2,1)S(1)}, u32[]{:S(2)}, u32[]{:S(2)}) collective-permute-start(bf16[272,128]{1,0:T(8,128)(2,1)S(1)} %get-tuple-element.134), channel_id=1, source_target_pairs={{0,16},{8,24},{16,0},{24,8},{1,17},{9,25},{17,1},{25,9},{2,18},{10... | collective-permute-start | bytes 208904 | tf_op jit(solution)/shard_map/ppermute | solution.py:32
  122.2 7.0 %collective-permute-start.29 = (bf16[272,128]{1,0:T(8,128)(2,1)S(1)}, bf16[272,128]{1,0:T(8,128)(2,1)S(1)}, u32[]{:S(2)}, u32[]{:S(2)}) collective-permute-start(bf16[272,128]{1,0:T(8,128)(2,1)S(1)} %get-tuple-element.135), channel_id=1, source_target_pairs={{0,24},{8,16},{16,8},{24,0},{1,25},{9,17},{17,9},{25,1},{2,26},{10... | collective-permute-start | bytes 208904 | tf_op jit(solution)/shard_map/ppermute | solution.py:32
  129.7 1.3 %collective-permute-start.30 = (bf16[32,1024]{1,0:T(8,128)(2,1)S(1)}, bf16[32,1024]{1,0:T(8,128)(2,1)S(1)}, u32[]{:S(2)}, u32[]{:S(2)}) collective-permute-start(bf16[32,1024]{1,0:T(8,128)(2,1)S(1)} %finish.1), channel_id=1, source_target_pairs={{0,1},{1,0},{2,3},{3,2},{4,5},{5,4},{6,7},{7,6},{8,9},{9,8},{10,11... | collective-permute-start | bytes 196616 | tf_op jit(solution)/shard_map/ppermute | solution.py:23

commit v8 on v7

--- a/solution.py
+++ b/solution.py
@@ -492,28 +492,27 @@
     kb1 = send(key_weight, 1, 1)
     value_block = pack(value_weight, own_query)
     va1 = send(value_block, 1, 0)
+    vb1 = send(value_block, 1, 1)
     early, first = barrier((early, (key_weight, value_weight)))
     hidden, totals["k"], totals["v"] = load(hidden, *first, early[0], owners)
     for name, weight in (("k", key_weight), ("v", value_weight)):
         absorb(name, [weight], (((0, 0),),), 1)
 
-    ka1, kb1, value_block, totals = barrier((ka1, kb1, value_block, totals))
+    ka1, kb1, totals = barrier((ka1, kb1, totals))
     kb2 = send(ka1, 2, 1)
     ka2 = send(kb1, 2, 0)
-    vb1 = send(value_block, 1, 1)
     absorb("k", [ka1, kb1], (((0, 1),), ((1, 1),)))
 
-    kb2, va1, totals = barrier((kb2, va1, totals))
+    va1, vb1, totals = barrier((va1, vb1, totals))
+    vb2 = send(va1, 2, 1)
+    absorb("v", [va1, vb1], (((0, 1),), ((1, 1),)))
+
+    kb2, vb1, totals = barrier((kb2, vb1, totals))
     ka3 = send(kb2, 3, 0)
-    vb2 = send(va1, 2, 1)
-    absorb("v", [va1], (((0, 1),),))
+    va2 = send(vb1, 2, 0)
 
     ka2, totals = barrier((ka2, totals))
     absorb("k", [ka2 + kb2], (((0, 2), (1, 2)),))
-
-    vb1, totals = barrier((vb1, totals))
-    va2 = send(vb1, 2, 0)
-    absorb("v", [vb1], (((1, 1),),))
 
     ka3, totals = barrier((ka3, totals))
     absorb("k", [ka3], (((0, 3),),))

time: 132 us -> 131 us (level)
    ppermute x10, waiting for transfers between devices: 34 us -> 35.9 us  [send(): return lax.ppermute(x, 'seq', line_pairs(hop, parity, groups))]
    pallas_call x16 -> x14, Pallas kernels: 21.8 us -> 20.7 us  [project(): pl.pallas_call(functools.partial(project_kernel, hops, back, groups, owne...]
    unnamed x16 -> x14, local copies, waits for them, and re-layouts: 3.15 us -> 2.1 us
  transfers between devices with their start and end apart: 31 -> 31, of which waited for: 11 -> 10; matrix products, arithmetic and copies ran while one was open for 4% -> 4% of each run, Pallas kernels for 24% -> 24%
where the time goes in v8:
time: 131 us
  waiting for transfers between devices  58.6 us (45%)
  Pallas kernels  34.5 us (26%)
  starting transfers between devices  28.5 us (22%)
  other arithmetic  5.5 us (4%)
  local copies, waits for them, and re-layouts  2.15 us (2%)
    ppermute x10, waiting for transfers between devices, send(): return lax.ppermute(x, 'seq', line_pairs(hop, parity, groups))  35.9 us
    pallas_call x14, Pallas kernels, project(): pl.pallas_call(functools.partial(project_kernel, hops, back, groups, owne...  20.7 us
    ppermute x10, starting transfers between devices, send(): return lax.ppermute(x, 'seq', line_pairs(hop, parity, groups))  14.9 us
    ppermute x1, waiting for transfers between devices, line_project(): far_query = lax.ppermute(vb2[depth:], 'seq', line_pairs(3, 0, groups))  10.7 us
    ppermute x6, starting transfers between devices, swapped(): return lax.ppermute(x, axis, [(i, partner(i, k, n)) for i in range(n)])  8.83 us
    ppermute x6, waiting for transfers between devices, swapped(): return lax.ppermute(x, axis, [(i, partner(i, k, n)) for i in range(n)])  8.21 us
    pallas_call x1, Pallas kernels, load(): pl.pallas_call(functools.partial(load_kernel, owners), out_shape=(jax.Sha...  6.57 us
    pallas_call x1, Pallas kernels, score(): pl.pallas_call(functools.partial(score_kernel, slots, parts, steps, scale...  4.73 us
  transfers between devices with their start and end apart: 31, of which 10 were waited for; matrix products, arithmetic and copies ran while one was open for 4% of the time, Pallas kernels for 24%

profile of v8, /device:TPU:0, one launch (start us, length us, event | category | flops | bytes accessed | tf_op | source)
XLA Modules:
  0.0 130.9 jit_solution(1494521274990531178)
XLA Ops:
  0.6 0.6 collective-permute-start.4
  1.2 2.6 %collective-permute-start.2 = (bf16[1024,256]{1,0:T(8,128)(2,1)}, bf16[1024,256]{1,0:T(8,128)(2,1)S(1)}, u32[]{:S(2)}, u32[]{:S(2)}) collective-permute-start(bf16[1024,256]{1,0:T(8,128)(2,1)} %refs_0_), channel_id=1, source_target_pairs={{0,8},{8,0},{16,24},{24,16},{1,9},{9,1},{17,25},{25,17},{2,10},{10... | collective-permute-start | bytes 1572872 | tf_op jit(solution)/shard_map/ppermute | solution.py:479
  3.8 0.7 collective-permute-start.3
  4.5 0.2 collective-permute-start.5
  4.8 0.9 select_bitcast_fusion.query
  5.7 1.0 copy-done
  6.7 1.0 copy-done.1
  7.8 6.6 %load.1 = (bf16[1024,8192]{1,0:T(8,128)(2,1)S(1)}, f32[1024,256]{1,0:T(8,128)S(1)}, f32[1024,256]{1,0:T(8,128)S(1)}) custom-call(s32[2]{0:T(128)S(1)} %pad_add_fusion.place, bf16[1024,8192]{1,0:T(8,128)(2,1)} %hidden.1, bf16[1024,256]{1,0:T(8,128)(2,1)S(1)} %copy-done.1, bf16[1024,256]{1,0:T(8,128)(2,1)S(1)} %copy-done), custom_call_target="tpu_custom_call" | custom-call | flops 1073741824 | bytes 16777216 | tf_op jit(solution)/shard_map/load/pallas_call | solution.py:114
  14.4 1.4 %project.15.refs_2_ = f32[1024,256]{1,0:T(8,128)S(1)} custom-call(s32[2]{0:T(128)S(1)} %pad_add_fusion.place, bf16[1024,8192]{1,0:T(8,128)(2,1)S(1)} %get-tuple-element.81.left, bf16[1024,256]{1,0:T(8,128)(2,1)S(1)} %collective-permute-done.5.refs_0_, f32[1024,256]{1,0:T(8,128)S(1)} %get-tuple-element.83.refs_1_), custom_call_target="tpu_custom_call", output_to_operand_aliasing={{}: (3, {})} | custom-call | flops 536870912 | bytes 4718592 | tf_op jit(solution)/shard_map/project/pallas_call | solution.py:170
  15.8 1.4 %project.14.refs_2_ = f32[1024,256]{1,0:T(8,128)S(1)} custom-call(s32[2]{0:T(128)S(1)} %pad_add_fusion.place, bf16[1024,8192]{1,0:T(8,128)(2,1)S(1)} %get-tuple-element.81.left, bf16[1024,256]{1,0:T(8,128)(2,1)S(1)} %collective-permute-done.4.refs_0_, f32[1024,256]{1,0:T(8,128)S(1)} %get-tuple-element.82.refs_1_), custom_call_target="tpu_custom_call", output_to_operand_aliasing={{}: (3, {})} | custom-call | flops 536870912 | bytes 4718592 | tf_op jit(solution)/shard_map/project/pallas_call | solution.py:170
  17.3 0.4 collective-permute-start.6
  17.7 0.1 collective-permute-start.7
  17.9 4.4 %collective-permute-start = (bf16[1152,256]{1,0:T(8,128)(2,1)S(1)}, bf16[1152,256]{1,0:T(8,128)(2,1)S(1)}, u32[]{:S(2)}, u32[]{:S(2)}) collective-permute-start(bf16[1152,256]{1,0:T(8,128)(2,1)S(1)} %pack.1), channel_id=1, source_target_pairs={{0,8},{8,0},{16,24},{24,16},{1,9},{9,1},{17,25},{25,17},{2,10},{10... | collective-permute-start | bytes 1769480 | tf_op jit(solution)/shard_map/ppermute | solution.py:479
  22.3 0.7 collective-permute-start.1
  23.0 1.5 %project.16.refs_2_ = f32[1024,256]{1,0:T(8,128)S(1)} custom-call(s32[2]{0:T(128)S(1)} %pad_add_fusion.place, bf16[1024,8192]{1,0:T(8,128)(2,1)S(1)} %get-tuple-element.81.left, bf16[1024,256]{1,0:T(8,128)(2,1)S(1)} %collective-permute-done.2.refs_0_, bf16[1024,256]{1,0:T(8,128)(2,1)S(1)} %collective-permute-done.3.refs_1_, ...), custom_call_target="tpu_custom_call", output_to_operand_aliasing={{}: (4, {})} | custom-call | flops 1073741824 | bytes 7340032 | tf_op jit(solution)/shard_map/project/pallas_call | solution.py:170
  24.5 1.5 %project.17.refs_1_ = f32[1024,256]{1,0:T(8,128)S(1)} custom-call(s32[2]{0:T(128)S(1)} %pad_add_fusion.place, bf16[1024,8192]{1,0:T(8,128)(2,1)S(1)} %get-tuple-element.81.left, bf16[1024,256]{1,0:T(8,128)(2,1)S(1)} %collective-permute-done.6.refs_0_, bf16[1024,256]{1,0:T(8,128)(2,1)S(1)} %collective-permute-done.7.refs_1_, ...), custom_call_target="tpu_custom_call", output_to_operand_aliasing={{}: (4, {})} | custom-call | flops 1073741824 | bytes 7340032 | tf_op jit(solution)/shard_map/project/pallas_call | solution.py:170
  26.1 10.2 %collective-permute-done.refs_0_ = bf16[1152,256]{1,0:T(8,128)(2,1)S(1)} collective-permute-done((bf16[1152,256]{1,0:T(8,128)(2,1)S(1)}, bf16[1152,256]{1,0:T(8,128)(2,1)S(1)}, u32[]{:S(2)}, u32[]{:S(2)}) %collective-permute-start) | collective-permute-done | bytes 589856 | tf_op jit(solution)/shard_map/ppermute | solution.py:479
  36.2 0.5 collective-permute-start.9
  36.8 0.7 collective-permute-start.8
  37.4 1.3 collective-permute-start.14
  38.9 1.5 %project.18.refs_2_ = f32[1024,256]{1,0:T(8,128)S(1)} custom-call(s32[2]{0:T(128)S(1)} %pad_add_fusion.place, bf16[1024,8192]{1,0:T(8,128)(2,1)S(1)} %get-tuple-element.81.left, bf16[1152,256]{1,0:T(8,128)(2,1)S(1)} %collective-permute-done.refs_0_, bf16[1152,256]{1,0:T(8,128)(2,1)S(1)} %collective-permute-done.1.refs_1_, ...), custom_call_target="tpu_custom_call", output_to_operand_aliasing={{}: (4, {})} | custom-call | flops 1073741824 | bytes 7340032 | tf_op jit(solution)/shard_map/project/pallas_call | solution.py:170
  40.4 1.5 %project.19.refs_1_ = f32[1024,256]{1,0:T(8,128)S(1)} custom-call(s32[2]{0:T(128)S(1)} %pad_add_fusion.place, bf16[1024,8192]{1,0:T(8,128)(2,1)S(1)} %get-tuple-element.81.left, bf16[1152,256]{1,0:T(8,128)(2,1)S(1)} %collective-permute-done.9.refs_0_, bf16[1152,256]{1,0:T(8,128)(2,1)S(1)} %collective-permute-done.10.refs_1_, ...), custom_call_target="tpu_custom_call", output_to_operand_aliasing={{}: (4, {})} | custom-call | flops 1073741824 | bytes 7340032 | tf_op jit(solution)/shard_map/project/pallas_call | solution.py:170
  41.9 14.4 %collective-permute-done.14 = bf16[1024,256]{1,0:T(8,128)(2,1)S(1)} collective-permute-done((bf16[1024,256]{1,0:T(8,128)(2,1)S(1)}, bf16[1024,256]{1,0:T(8,128)(2,1)S(1)}, u32[]{:S(2)}, u32[]{:S(2)}) %collective-permute-start.14) | collective-permute-done | bytes 524320 | tf_op jit(solution)/shard_map/ppermute | solution.py:479
  56.3 0.1 add.74.refs_0_
  56.6 1.3 collective-permute-start.13
  58.0 0.6 convert_reduce_fusion
  58.6 1.4 %project.20.refs_1_ = f32[1024,256]{1,0:T(8,128)S(1)} custom-call(s32[2]{0:T(128)S(1)} %pad_add_fusion.place, bf16[1024,8192]{1,0:T(8,128)(2,1)S(1)} %get-tuple-element.81.left, bf16[1024,256]{1,0:T(8,128)(2,1)S(1)} %add.74.refs_0_, f32[1024,256]{1,0:T(8,128)S(1)} %project.17.refs_1_), custom_call_target="tpu_custom_call", output_to_operand_aliasing={{}: (3, {})} | custom-call | flops 536870912 | bytes 4718592 | tf_op jit(solution)/shard_map/project/pallas_call | solution.py:170
  60.0 1.4 %project.21.refs_1_ = f32[1024,256]{1,0:T(8,128)S(1)} custom-call(s32[2]{0:T(128)S(1)} %pad_add_fusion.place, bf16[1024,8192]{1,0:T(8,128)(2,1)S(1)} %get-tuple-element.81.left, bf16[1024,256]{1,0:T(8,128)(2,1)S(1)} %collective-permute-done.15.refs_0_, f32[1024,256]{1,0:T(8,128)S(1)} %project.20.refs_1_), custom_call_target="tpu_custom_call", output_to_operand_aliasing={{}: (3, {})} | custom-call | flops 536870912 | bytes 4718592 | tf_op jit(solution)/shard_map/project/pallas_call | solution.py:170
  61.5 11.3 %collective-permute-done.13.refs_0_ = bf16[1024,256]{1,0:T(8,128)(2,1)S(1)} collective-permute-done((bf16[1024,256]{1,0:T(8,128)(2,1)S(1)}, bf16[1024,256]{1,0:T(8,128)(2,1)S(1)}, u32[]{:S(2)}, u32[]{:S(2)}) %collective-permute-start.13) | collective-permute-done | bytes 524320 | tf_op jit(solution)/shard_map/ppermute | solution.py:479
  72.8 0.2 fusion.2
  73.0 0.7 collective-permute-start.12
  73.7 1.3 collective-permute-start.11
  75.0 1.6 %project.22.refs_1_ = f32[1024,256]{1,0:T(8,128)S(1)} custom-call(s32[2]{0:T(128)S(1)} %pad_add_fusion.place, bf16[1024,8192]{1,0:T(8,128)(2,1)S(1)} %get-tuple-element.81.left, bf16[1024,256]{1,0:T(8,128)(2,1)S(1)} %collective-permute-done.13.refs_0_, f32[1024,256]{1,0:T(8,128)S(1)} %project.21.refs_1_), custom_call_target="tpu_custom_call", output_to_operand_aliasing={{}: (3, {})} | custom-call | flops 536870912 | bytes 4718592 | tf_op jit(solution)/shard_map/project/pallas_call | solution.py:170
  76.6 1.4 %project.23 = f32[1024,256]{1,0:T(8,128)S(1)} custom-call(s32[2]{0:T(128)S(1)} %pad_add_fusion.place, bf16[1024,8192]{1,0:T(8,128)(2,1)S(1)} %get-tuple-element.81.left, bf16[1024,256]{1,0:T(8,128)(2,1)S(1)} %collective-permute-done.16.refs_0_, f32[1024,256]{1,0:T(8,128)S(1)} %project.22.refs_1_), custom_call_target="tpu_custom_call", output_to_operand_aliasing={{}: (3, {})} | custom-call | flops 536870912 | bytes 4718592 | tf_op jit(solution)/shard_map/project/pallas_call | solution.py:170
  78.2 0.6 collective-permute-start.17
  78.7 0.2 fusion.1.count
  78.9 0.6 collective-permute-done.17
  79.6 1.1 collective-permute-start.18
  80.7 1.4 %collective-permute-start.19 = (f32[1,256]{1,0:T(1,128)S(1)}, f32[1,256]{1,0:T(1,128)S(1)}, u32[]{:S(2)}, u32[]{:S(2)}) collective-permute-start(f32[1,256]{1,0:T(1,128)S(1)} %max.36), channel_id=1, source_target_pairs={{0,16},{8,24},{16,0},{24,8},{1,17},{9,25},{17,1},{25,9},{2,18},{10... | collective-permute-start | bytes 3080 | tf_op jit(solution)/shard_map/ppermute | solution.py:32
  82.1 1.9 %collective-permute-start.20 = (f32[1,256]{1,0:T(1,128)S(1)}, f32[1,256]{1,0:T(1,128)S(1)}, u32[]{:S(2)}, u32[]{:S(2)}) collective-permute-start(f32[1,256]{1,0:T(1,128)S(1)} %max.36), channel_id=1, source_target_pairs={{0,24},{8,16},{16,8},{24,0},{1,25},{9,17},{17,9},{25,1},{2,26},{10... | collective-permute-start | bytes 3080 | tf_op jit(solution)/shard_map/ppermute | solution.py:32
  84.0 1.3 collective-permute-start.24
  85.3 6.2 %collective-permute-done.18 = f32[1,256]{1,0:T(1,128)S(1)} collective-permute-done((f32[1,256]{1,0:T(1,128)S(1)}, f32[1,256]{1,0:T(1,128)S(1)}, u32[]{:S(2)}, u32[]{:S(2)}) %collective-permute-start.18) | collective-permute-done | bytes 1056 | tf_op jit(solution)/shard_map/ppermute | solution.py:32
  91.4 1.3 collective-permute-start.21
  92.8 0.2 add.86.refs_0_
  93.1 0.1 minimum_convert_fusion.1
  93.3 0.6 collective-permute-start.22
  93.8 1.4 %project.24.refs_1_ = f32[1024,256]{1,0:T(8,128)S(1)} custom-call(s32[2]{0:T(128)S(1)} %pad_add_fusion.place, bf16[1024,8192]{1,0:T(8,128)(2,1)S(1)} %get-tuple-element.81.left, bf16[1152,256]{1,0:T(8,128)(2,1)S(1)} %add.86.refs_0_, f32[1024,256]{1,0:T(8,128)S(1)} %project.19.refs_1_), custom_call_target="tpu_custom_call", output_to_operand_aliasing={{}: (3, {})} | custom-call | flops 536870912 | bytes 4718592 | tf_op jit(solution)/shard_map/project/pallas_call | solution.py:170
  95.3 10.7 %collective-permute-done.21 = bf16[128,256]{1,0:T(8,128)(2,1)S(1)} collective-permute-done((bf16[128,256]{1,0:T(8,128)(2,1)S(1)}, bf16[128,256]{1,0:T(8,128)(2,1)S(1)}, u32[]{:S(2)}, u32[]{:S(2)}) %collective-permute-start.21) | collective-permute-done | bytes 65568 | tf_op jit(solution)/shard_map/ppermute | solution.py:523
  106.1 1.4 %project.25.refs_1_ = f32[1024,256]{1,0:T(8,128)S(1)} custom-call(s32[2]{0:T(128)S(1)} %pad_add_fusion.place, bf16[1024,8192]{1,0:T(8,128)(2,1)S(1)} %get-tuple-element.81.left, bf16[1152,256]{1,0:T(8,128)(2,1)S(1)} %collective-permute-done.23.refs_0_, f32[1024,256]{1,0:T(8,128)S(1)} %project.24.refs_1_), custom_call_target="tpu_custom_call", output_to_operand_aliasing={{}: (3, {})} | custom-call | flops 536870912 | bytes 4718592 | tf_op jit(solution)/shard_map/project/pallas_call | solution.py:170
  107.6 4.7 %score.1 = (bf16[4,256,2048]{2,1,0:T(8,128)(2,1)S(1)}, f32[2,256]{1,0:T(2,128)S(1)}, f32[2,256]{1,0:T(2,128)S(1)}, f32[2,256]{1,0:T(2,128)S(1)}, f32[2,256]{1,0:T(2,128)S(1)}) custom-call(s32[4]{0:T(128)S(1)} %iota_xor_fusion.group, bf16[4,128,256]{2,1,0:T(8,128)(2,1)S(1)} %pad_maximum_fusion.query, f32[1,128]{1,0:T(1,128)S(1)} %broadcast_select_fusion.7.smooth, ...), custom_call_target="tpu_custom_call" | custom-call | flops 536870912 | bytes 4194304 | tf_op jit(solution)/shard_map/score/pallas_call | solution.py:241
  112.5 1.4 %project.26.refs_1_ = f32[1024,256]{1,0:T(8,128)S(1)} custom-call(s32[2]{0:T(128)S(1)} %pad_add_fusion.place, bf16[1024,8192]{1,0:T(8,128)(2,1)S(1)} %get-tuple-element.81.left, bf16[1152,256]{1,0:T(8,128)(2,1)S(1)} %collective-permute-done.24.refs_0_, f32[1024,256]{1,0:T(8,128)S(1)} %project.25.refs_1_), custom_call_target="tpu_custom_call", output_to_operand_aliasing={{}: (3, {})} | custom-call | flops 536870912 | bytes 4718592 | tf_op jit(solution)/shard_map/project/pallas_call | solution.py:170
  113.9 0.5 collective-permute-done.25.refs_0_
  114.4 1.4 %project.27 = f32[1024,256]{1,0:T(8,128)S(1)} custom-call(s32[2]{0:T(128)S(1)} %pad_add_fusion.place, bf16[1024,8192]{1,0:T(8,128)(2,1)S(1)} %get-tuple-element.81.left, bf16[1152,256]{1,0:T(8,128)(2,1)S(1)} %collective-permute-done.25.refs_0_, f32[1024,256]{1,0:T(8,128)S(1)} %project.26.refs_1_), custom_call_target="tpu_custom_call", output_to_operand_aliasing={{}: (3, {})} | custom-call | flops 536870912 | bytes 4718592 | tf_op jit(solution)/shard_map/project/pallas_call | solution.py:170
  116.0 0.2 collective-permute-start.26
  116.2 1.4 %collective-permute-done.26.refs_1_ = bf16[1024,128]{1,0:T(8,128)(2,1)S(1)} collective-permute-done((bf16[1024,128]{1,0:T(8,128)(2,1)S(1)}, bf16[1024,128]{1,0:T(8,128)(2,1)S(1)}, u32[]{:S(2)}, u32[]{:S(2)}) %collective-permute-start.26) | collective-permute-done | bytes 262176 | tf_op jit(solution)/shard_map/ppermute | solution.py:23
  117.6 1.8 %weigh.1 = (bf16[272,128]{1,0:T(8,128)(2,1)S(1)}, bf16[272,128]{1,0:T(8,128)(2,1)S(1)}, bf16[272,128]{1,0:T(8,128)(2,1)S(1)}, bf16[272,128]{1,0:T(8,128)(2,1)S(1)}) custom-call(bf16[4,256,2048]{2,1,0:T(8,128)(2,1)S(1)} %get-tuple-element.116.probs, bf16[1024,128]{1,0:T(8,128)(2,1)S(1)} %get-tuple-element.154.refs_0_, ...), custom_call_target="tpu_custom_call" | custom-call | flops 536870912 | bytes 4194304 | tf_op jit(solution)/shard_map/weigh/pallas_call | solution.py:316
  119.5 2.5 %collective-permute-start.28 = (bf16[272,128]{1,0:T(8,128)(2,1)S(1)}, bf16[272,128]{1,0:T(8,128)(2,1)S(1)}, u32[]{:S(2)}, u32[]{:S(2)}) collective-permute-start(bf16[272,128]{1,0:T(8,128)(2,1)S(1)} %get-tuple-element.134), channel_id=1, source_target_pairs={{0,16},{8,24},{16,0},{24,8},{1,17},{9,25},{17,1},{25,9},{2,18},{10... | collective-permute-start | bytes 208904 | tf_op jit(solution)/shard_map/ppermute | solution.py:32
  122.0 1.9 %collective-permute-start.29 = (bf16[272,128]{1,0:T(8,128)(2,1)S(1)}, bf16[272,128]{1,0:T(8,128)(2,1)S(1)}, u32[]{:S(2)}, u32[]{:S(2)}) collective-permute-start(bf16[272,128]{1,0:T(8,128)(2,1)S(1)} %get-tuple-element.135), channel_id=1, source_target_pairs={{0,24},{8,16},{16,8},{24,0},{1,25},{9,17},{17,9},{25,1},{2,26},{10... | collective-permute-start | bytes 208904 | tf_op jit(solution)/shard_map/ppermute | solution.py:32
  123.9 2.3 %broadcast_select_fusion = bf16[1024,2,256]{2,1,0:T(2,128)(2,1)} fusion(pred[2]{0:T(512)(128)(4,1)S(1)} %iota_compare_fusion.5, bf16[1024,256]{1,0:T(8,128)(2,1)S(1)} %minimum_convert_fusion, bf16[1024,256]{1,0:T(8,128)(2,1)S(1)} %minimum_convert_fusion.1), kind=kLoop, calls=%fused_computation.3 | loop fusion | flops 524288 | bytes 2097154 | tf_op jit(solution)/shard_map/jit(_where)/select_n | solution.py:614
  126.2 0.2 fresh.1
  126.4 2.0 %collective-permute-done.28.refs_2_ = bf16[272,128]{1,0:T(8,128)(2,1)S(1)} collective-permute-done((bf16[272,128]{1,0:T(8,128)(2,1)S(1)}, bf16[272,128]{1,0:T(8,128)(2,1)S(1)}, u32[]{:S(2)}, u32[]{:S(2)}) %collective-permute-start.28) | collective-permute-done | bytes 69664 | tf_op jit(solution)/shard_map/ppermute | solution.py:32
  128.5 0.4 finish.1
  129.0 1.2 collective-permute-done.30
  130.3 0.7 maximum_bitcast_fusion
  (68 shorter events, 1.2 us)
Async XLA Ops:
  0.6 15.2 %collective-permute-start.4 = (bf16[1024,256]{1,0:T(8,128)(2,1)}, bf16[1024,256]{1,0:T(8,128)(2,1)S(1)}, u32[]{:S(2)}, u32[]{:S(2)}) collective-permute-start(bf16[1024,256]{1,0:T(8,128)(2,1)} %refs_0_), channel_id=1, source_target_pairs={{0,1},{1,0},{2,3},{3,2},{4,5},{5,4},{6,7},{7,6},{8,9},{9,8},{10,11... | collective-permute-start | bytes 1572872 | tf_op jit(solution)/shard_map/ppermute | solution.py:23
  1.2 16.1 %collective-permute-start.2 = (bf16[1024,256]{1,0:T(8,128)(2,1)}, bf16[1024,256]{1,0:T(8,128)(2,1)S(1)}, u32[]{:S(2)}, u32[]{:S(2)}) collective-permute-start(bf16[1024,256]{1,0:T(8,128)(2,1)} %refs_0_), channel_id=1, source_target_pairs={{0,8},{8,0},{16,24},{24,16},{1,9},{9,1},{17,25},{25,17},{2,10},{10... | collective-permute-start | bytes 1572872 | tf_op jit(solution)/shard_map/ppermute | solution.py:479
  3.8 13.5 %collective-permute-start.3 = (bf16[1024,256]{1,0:T(8,128)(2,1)}, bf16[1024,256]{1,0:T(8,128)(2,1)S(1)}, u32[]{:S(2)}, u32[]{:S(2)}) collective-permute-start(bf16[1024,256]{1,0:T(8,128)(2,1)} %refs_0_), channel_id=1, source_target_pairs={{8,16},{16,8},{9,17},{17,9},{10,18},{18,10},{11,19},{19,11},{12,20... | collective-permute-start | bytes 1572872 | tf_op jit(solution)/shard_map/ppermute | solution.py:479
  4.5 9.8 %collective-permute-start.5 = (bf16[1024,256]{1,0:T(8,128)(2,1)}, bf16[1024,256]{1,0:T(8,128)(2,1)S(1)}, u32[]{:S(2)}, u32[]{:S(2)}) collective-permute-start(bf16[1024,256]{1,0:T(8,128)(2,1)} %refs_1_), channel_id=1, source_target_pairs={{0,1},{1,0},{2,3},{3,2},{4,5},{5,4},{6,7},{7,6},{8,9},{9,8},{10,11... | collective-permute-start | bytes 1572872 | tf_op jit(solution)/shard_map/ppermute | solution.py:23
  5.7 1.0 copy-start
  6.7 1.0 copy-start.1
  17.3 7.2 %collective-permute-start.6 = (bf16[1024,256]{1,0:T(8,128)(2,1)S(1)}, bf16[1024,256]{1,0:T(8,128)(2,1)S(1)}, u32[]{:S(2)}, u32[]{:S(2)}) collective-permute-start(bf16[1024,256]{1,0:T(8,128)(2,1)S(1)} %collective-permute-done.2.refs_0_), channel_id=1, source_target_pairs={{0,1},{1,0},{2,3},{3,2},{4,5},{5,4},{6,7},{7,6},{8,9},{9,8},{10,11... | collective-permute-start | bytes 1572872 | tf_op jit(solution)/shard_map/ppermute | solution.py:23
  17.7 6.8 %collective-permute-start.7 = (bf16[1024,256]{1,0:T(8,128)(2,1)S(1)}, bf16[1024,256]{1,0:T(8,128)(2,1)S(1)}, u32[]{:S(2)}, u32[]{:S(2)}) collective-permute-start(bf16[1024,256]{1,0:T(8,128)(2,1)S(1)} %collective-permute-done.3.refs_1_), channel_id=1, source_target_pairs={{0,1},{1,0},{2,3},{3,2},{4,5},{5,4},{6,7},{7,6},{8,9},{9,8},{10,11... | collective-permute-start | bytes 1572872 | tf_op jit(solution)/shard_map/ppermute | solution.py:23
  17.9 20.8 %copy-start.6 = (s32[32]{0:T(128)S(1)}, s32[32]{0:T(128)}, u32[]{:S(2)}) copy-start(s32[32]{0:T(128)} %param.15) | copy-start | bytes 388
  17.9 18.3 %collective-permute-start = (bf16[1152,256]{1,0:T(8,128)(2,1)S(1)}, bf16[1152,256]{1,0:T(8,128)(2,1)S(1)}, u32[]{:S(2)}, u32[]{:S(2)}) collective-permute-start(bf16[1152,256]{1,0:T(8,128)(2,1)S(1)} %pack.1), channel_id=1, source_target_pairs={{0,8},{8,0},{16,24},{24,16},{1,9},{9,1},{17,25},{25,17},{2,10},{10... | collective-permute-start | bytes 1769480 | tf_op jit(solution)/shard_map/ppermute | solution.py:479
  22.3 13.9 %collective-permute-start.1 = (bf16[1152,256]{1,0:T(8,128)(2,1)S(1)}, bf16[1152,256]{1,0:T(8,128)(2,1)S(1)}, u32[]{:S(2)}, u32[]{:S(2)}) collective-permute-start(bf16[1152,256]{1,0:T(8,128)(2,1)S(1)} %pack.1), channel_id=1, source_target_pairs={{8,16},{16,8},{9,17},{17,9},{10,18},{18,10},{11,19},{19,11},{12,20... | collective-permute-start | bytes 1769480 | tf_op jit(solution)/shard_map/ppermute | solution.py:479
  36.2 4.1 %collective-permute-start.10 = (bf16[1152,256]{1,0:T(8,128)(2,1)S(1)}, bf16[1152,256]{1,0:T(8,128)(2,1)S(1)}, u32[]{:S(2)}, u32[]{:S(2)}) collective-permute-start(bf16[1152,256]{1,0:T(8,128)(2,1)S(1)} %collective-permute-done.1.refs_1_), channel_id=1, source_target_pairs={{0,1},{1,0},{2,3},{3,2},{4,5},{5,4},{6,7},{7,6},{8,9},{9,8},{10,11... | collective-permute-start | bytes 1769480 | tf_op jit(solution)/shard_map/ppermute | solution.py:23
  36.2 4.1 %collective-permute-start.9 = (bf16[1152,256]{1,0:T(8,128)(2,1)S(1)}, bf16[1152,256]{1,0:T(8,128)(2,1)S(1)}, u32[]{:S(2)}, u32[]{:S(2)}) collective-permute-start(bf16[1152,256]{1,0:T(8,128)(2,1)S(1)} %collective-permute-done.refs_0_), channel_id=1, source_target_pairs={{0,1},{1,0},{2,3},{3,2},{4,5},{5,4},{6,7},{7,6},{8,9},{9,8},{10,11... | collective-permute-start | bytes 1769480 | tf_op jit(solution)/shard_map/ppermute | solution.py:23
  36.8 5.2 %collective-permute-start.8 = (bf16[1024,256]{1,0:T(8,128)(2,1)S(1)}, bf16[1024,256]{1,0:T(8,128)(2,1)S(1)}, u32[]{:S(2)}, u32[]{:S(2)}) collective-permute-start(bf16[1024,256]{1,0:T(8,128)(2,1)S(1)} %collective-permute-done.2.refs_0_), channel_id=1, source_target_pairs={{8,16},{16,8},{9,17},{17,9},{10,18},{18,10},{11,19},{19,11},{12,20... | collective-permute-start | bytes 1572872 | tf_op jit(solution)/shard_map/ppermute | solution.py:479
  37.4 18.9 %collective-permute-start.14 = (bf16[1024,256]{1,0:T(8,128)(2,1)S(1)}, bf16[1024,256]{1,0:T(8,128)(2,1)S(1)}, u32[]{:S(2)}, u32[]{:S(2)}) collective-permute-start(bf16[1024,256]{1,0:T(8,128)(2,1)S(1)} %collective-permute-done.3.refs_1_), channel_id=1, source_target_pairs={{8,0},{16,24},{9,1},{17,25},{10,2},{18,26},{11,3},{19,27},{12,4},{... | collective-permute-start | bytes 1572872 | tf_op jit(solution)/shard_map/ppermute | solution.py:479
  38.8 19.1 %copy-start.3 = (s32[32,32]{1,0:T(8,128)S(1)}, s32[32,32]{1,0:T(8,128)}, u32[]{:S(2)}) copy-start(s32[32,32]{1,0:T(8,128)} %param.14) | copy-start | bytes 12292
  38.8 19.7 %copy-start.5 = (f32[2,256]{1,0:T(2,128)S(1)}, f32[2,256]{1,0:T(2,128)}, u32[]{:S(2)}) copy-start(f32[2,256]{1,0:T(2,128)} %param.11) | copy-start | bytes 6148
  56.5 3.5 %collective-permute-start.15 = (bf16[1024,256]{1,0:T(8,128)(2,1)S(1)}, bf16[1024,256]{1,0:T(8,128)(2,1)S(1)}, u32[]{:S(2)}, u32[]{:S(2)}) collective-permute-start(bf16[1024,256]{1,0:T(8,128)(2,1)S(1)} %add.74.refs_0_), channel_id=1, source_target_pairs={{0,1},{1,0},{2,3},{3,2},{4,5},{5,4},{6,7},{7,6},{8,9},{9,8},{10,11... | collective-permute-start | bytes 1572872 | tf_op jit(solution)/shard_map/ppermute | solution.py:23
  56.6 16.2 %collective-permute-start.13 = (bf16[1024,256]{1,0:T(8,128)(2,1)S(1)}, bf16[1024,256]{1,0:T(8,128)(2,1)S(1)}, u32[]{:S(2)}, u32[]{:S(2)}) collective-permute-start(bf16[1024,256]{1,0:T(8,128)(2,1)S(1)} %collective-permute-done.8), channel_id=1, source_target_pairs={{8,0},{16,24},{9,1},{17,25},{10,2},{18,26},{11,3},{19,27},{12,4},{... | collective-permute-start | bytes 1572872 | tf_op jit(solution)/shard_map/ppermute | solution.py:479
  72.8 3.9 %collective-permute-start.16 = (bf16[1024,256]{1,0:T(8,128)(2,1)S(1)}, bf16[1024,256]{1,0:T(8,128)(2,1)S(1)}, u32[]{:S(2)}, u32[]{:S(2)}) collective-permute-start(bf16[1024,256]{1,0:T(8,128)(2,1)S(1)} %collective-permute-done.13.refs_0_), channel_id=1, source_target_pairs={{0,1},{1,0},{2,3},{3,2},{4,5},{5,4},{6,7},{7,6},{8,9},{9,8},{10,11... | collective-permute-start | bytes 1572872 | tf_op jit(solution)/shard_map/ppermute | solution.py:23
  73.0 11.0 %collective-permute-start.12 = (bf16[1152,256]{1,0:T(8,128)(2,1)S(1)}, bf16[1152,256]{1,0:T(8,128)(2,1)S(1)}, u32[]{:S(2)}, u32[]{:S(2)}) collective-permute-start(bf16[1152,256]{1,0:T(8,128)(2,1)S(1)} %collective-permute-done.refs_0_), channel_id=1, source_target_pairs={{8,16},{16,8},{9,17},{17,9},{10,18},{18,10},{11,19},{19,11},{12,20... | collective-permute-start | bytes 1769480 | tf_op jit(solution)/shard_map/ppermute | solution.py:479
  73.7 19.1 %collective-permute-start.11 = (bf16[1152,256]{1,0:T(8,128)(2,1)S(1)}, bf16[1152,256]{1,0:T(8,128)(2,1)S(1)}, u32[]{:S(2)}, u32[]{:S(2)}) collective-permute-start(bf16[1152,256]{1,0:T(8,128)(2,1)S(1)} %collective-permute-done.1.refs_1_), channel_id=1, source_target_pairs={{8,0},{16,24},{9,1},{17,25},{10,2},{18,26},{11,3},{19,27},{12,4},{... | collective-permute-start | bytes 1769480 | tf_op jit(solution)/shard_map/ppermute | solution.py:479
  78.2 1.4 %collective-permute-start.17 = (f32[1,256]{1,0:T(1,128)S(1)}, f32[1,256]{1,0:T(1,128)S(1)}, u32[]{:S(2)}, u32[]{:S(2)}) collective-permute-start(f32[1,256]{1,0:T(1,128)S(1)} %bitcast.28), channel_id=1, source_target_pairs={{0,1},{1,0},{2,3},{3,2},{4,5},{5,4},{6,7},{7,6},{8,9},{9,8},{10,11... | collective-permute-start | bytes 3080 | tf_op jit(solution)/shard_map/ppermute | solution.py:23
  79.6 11.9 %collective-permute-start.18 = (f32[1,256]{1,0:T(1,128)S(1)}, f32[1,256]{1,0:T(1,128)S(1)}, u32[]{:S(2)}, u32[]{:S(2)}) collective-permute-start(f32[1,256]{1,0:T(1,128)S(1)} %max.36), channel_id=1, source_target_pairs={{0,8},{8,0},{16,24},{24,16},{1,9},{9,1},{17,25},{25,17},{2,10},{10... | collective-permute-start | bytes 3080 | tf_op jit(solution)/shard_map/ppermute | solution.py:32
  80.7 12.1 %collective-permute-start.19 = (f32[1,256]{1,0:T(1,128)S(1)}, f32[1,256]{1,0:T(1,128)S(1)}, u32[]{:S(2)}, u32[]{:S(2)}) collective-permute-start(f32[1,256]{1,0:T(1,128)S(1)} %max.36), channel_id=1, source_target_pairs={{0,16},{8,24},{16,0},{24,8},{1,17},{9,25},{17,1},{25,9},{2,18},{10... | collective-permute-start | bytes 3080 | tf_op jit(solution)/shard_map/ppermute | solution.py:32
  82.1 10.7 %collective-permute-start.20 = (f32[1,256]{1,0:T(1,128)S(1)}, f32[1,256]{1,0:T(1,128)S(1)}, u32[]{:S(2)}, u32[]{:S(2)}) collective-permute-start(f32[1,256]{1,0:T(1,128)S(1)} %max.36), channel_id=1, source_target_pairs={{0,24},{8,16},{16,8},{24,0},{1,25},{9,17},{17,9},{25,1},{2,26},{10... | collective-permute-start | bytes 3080 | tf_op jit(solution)/shard_map/ppermute | solution.py:32
  84.0 28.3 %collective-permute-start.24 = (bf16[1152,256]{1,0:T(8,128)(2,1)S(1)}, bf16[1152,256]{1,0:T(8,128)(2,1)S(1)}, u32[]{:S(2)}, u32[]{:S(2)}) collective-permute-start(bf16[1152,256]{1,0:T(8,128)(2,1)S(1)} %collective-permute-done.12), channel_id=1, source_target_pairs={{8,0},{16,24},{9,1},{17,25},{10,2},{18,26},{11,3},{19,27},{12,4},{... | collective-permute-start | bytes 1769480 | tf_op jit(solution)/shard_map/ppermute | solution.py:479
  91.4 14.6 %collective-permute-start.21 = (bf16[128,256]{1,0:T(8,128)(2,1)S(1)}, bf16[128,256]{1,0:T(8,128)(2,1)S(1)}, u32[]{:S(2)}, u32[]{:S(2)}) collective-permute-start(bf16[128,256]{1,0:T(8,128)(2,1)S(1)} %slice.79), channel_id=1, source_target_pairs={{8,0},{16,24},{9,1},{17,25},{10,2},{18,26},{11,3},{19,27},{12,4},{... | collective-permute-start | bytes 196616 | tf_op jit(solution)/shard_map/ppermute | solution.py:523
  92.8 14.8 %copy-start.4 = (f32[1,256]{1,0:T(1,128)}, f32[1,256]{1,0:T(1,128)S(1)}, u32[]{:S(2)}) copy-start(f32[1,256]{1,0:T(1,128)S(1)} %add_sqrt_fusion) | copy-start | bytes 3076
  93.0 13.1 %collective-permute-start.23 = (bf16[1152,256]{1,0:T(8,128)(2,1)S(1)}, bf16[1152,256]{1,0:T(8,128)(2,1)S(1)}, u32[]{:S(2)}, u32[]{:S(2)}) collective-permute-start(bf16[1152,256]{1,0:T(8,128)(2,1)S(1)} %add.86.refs_0_), channel_id=1, source_target_pairs={{0,1},{1,0},{2,3},{3,2},{4,5},{5,4},{6,7},{7,6},{8,9},{9,8},{10,11... | collective-permute-start | bytes 1769480 | tf_op jit(solution)/shard_map/ppermute | solution.py:23
  93.3 14.3 %collective-permute-start.22 = (bf16[1024,128]{1,0:T(8,128)(2,1)S(1)}, bf16[1024,128]{1,0:T(8,128)(2,1)S(1)}, u32[]{:S(2)}, u32[]{:S(2)}) collective-permute-start(bf16[1024,128]{1,0:T(8,128)(2,1)S(1)} %get-tuple-element.155), channel_id=1, source_target_pairs={{0,1},{1,0},{2,3},{3,2},{4,5},{5,4},{6,7},{7,6},{8,9},{9,8},{10,11... | collective-permute-start | bytes 786440 | tf_op jit(solution)/shard_map/ppermute | solution.py:23
  95.3 17.1 %copy-start.2 = (bf16[4,8,2,256]{3,2,1,0:T(2,128)(2,1)S(1)}, bf16[4,8,2,256]{3,2,1,0:T(2,128)(2,1)}, u32[]{:S(2)}) copy-start(bf16[4,8,2,256]{3,2,1,0:T(2,128)(2,1)} %param.12) | copy-start | bytes 98308
  112.3 2.1 %collective-permute-start.25 = (bf16[1152,256]{1,0:T(8,128)(2,1)S(1)}, bf16[1152,256]{1,0:T(8,128)(2,1)S(1)}, u32[]{:S(2)}, u32[]{:S(2)}) collective-permute-start(bf16[1152,256]{1,0:T(8,128)(2,1)S(1)} %collective-permute-done.24.refs_0_), channel_id=1, source_target_pairs={{0,1},{1,0},{2,3},{3,2},{4,5},{5,4},{6,7},{7,6},{8,9},{9,8},{10,11... | collective-permute-start | bytes 1769480 | tf_op jit(solution)/shard_map/ppermute | solution.py:23
  116.0 1.6 %collective-permute-start.26 = (bf16[1024,128]{1,0:T(8,128)(2,1)S(1)}, bf16[1024,128]{1,0:T(8,128)(2,1)S(1)}, u32[]{:S(2)}, u32[]{:S(2)}) collective-permute-start(bf16[1024,128]{1,0:T(8,128)(2,1)S(1)} %get-tuple-element.153), channel_id=1, source_target_pairs={{0,1},{1,0},{2,3},{3,2},{4,5},{5,4},{6,7},{7,6},{8,9},{9,8},{10,11... | collective-permute-start | bytes 786440 | tf_op jit(solution)/shard_map/ppermute | solution.py:23
  119.4 7.0 %collective-permute-start.27 = (bf16[272,128]{1,0:T(8,128)(2,1)S(1)}, bf16[272,128]{1,0:T(8,128)(2,1)S(1)}, u32[]{:S(2)}, u32[]{:S(2)}) collective-permute-start(bf16[272,128]{1,0:T(8,128)(2,1)S(1)} %get-tuple-element.133), channel_id=1, source_target_pairs={{0,8},{8,0},{16,24},{24,16},{1,9},{9,1},{17,25},{25,17},{2,10},{10... | collective-permute-start | bytes 208904 | tf_op jit(solution)/shard_map/ppermute | solution.py:32
  119.5 9.0 %collective-permute-start.28 = (bf16[272,128]{1,0:T(8,128)(2,1)S(1)}, bf16[272,128]{1,0:T(8,128)(2,1)S(1)}, u32[]{:S(2)}, u32[]{:S(2)}) collective-permute-start(bf16[272,128]{1,0:T(8,128)(2,1)S(1)} %get-tuple-element.134), channel_id=1, source_target_pairs={{0,16},{8,24},{16,0},{24,8},{1,17},{9,25},{17,1},{25,9},{2,18},{10... | collective-permute-start | bytes 208904 | tf_op jit(solution)/shard_map/ppermute | solution.py:32
  122.0 6.4 %collective-permute-start.29 = (bf16[272,128]{1,0:T(8,128)(2,1)S(1)}, bf16[272,128]{1,0:T(8,128)(2,1)S(1)}, u32[]{:S(2)}, u32[]{:S(2)}) collective-permute-start(bf16[272,128]{1,0:T(8,128)(2,1)S(1)} %get-tuple-element.135), channel_id=1, source_target_pairs={{0,24},{8,16},{16,8},{24,0},{1,25},{9,17},{17,9},{25,1},{2,26},{10... | collective-permute-start | bytes 208904 | tf_op jit(solution)/shard_map/ppermute | solution.py:32
  128.9 1.3 %collective-permute-start.30 = (bf16[32,1024]{1,0:T(8,128)(2,1)S(1)}, bf16[32,1024]{1,0:T(8,128)(2,1)S(1)}, u32[]{:S(2)}, u32[]{:S(2)}) collective-permute-start(bf16[32,1024]{1,0:T(8,128)(2,1)S(1)} %finish.1), channel_id=1, source_target_pairs={{0,1},{1,0},{2,3},{3,2},{4,5},{5,4},{6,7},{7,6},{8,9},{9,8},{10,11... | collective-permute-start | bytes 196616 | tf_op jit(solution)/shard_map/ppermute | solution.py:23

commit v9 on v7

--- a/solution.py
+++ b/solution.py
@@ -82,7 +82,7 @@
     depth = taken.shape[1]
     blocks = held.shape[1] // depth
     takes = [
-        pltpu.make_async_copy(weight, taken.at[j], taken_arrived.at[j])
+        pltpu.make_async_copy(weight.at[pl.ds(0, depth)], taken.at[j], taken_arrived.at[j])
         for j, weight in enumerate(weights)
     ]
 
@@ -492,18 +492,20 @@
     kb1 = send(key_weight, 1, 1)
     value_block = pack(value_weight, own_query)
     va1 = send(value_block, 1, 0)
-    early, first = barrier((early, (key_weight, value_weight)))
+    early, first = barrier((early, (key_weight, value_block)))
     hidden, totals["k"], totals["v"] = load(hidden, *first, early[0], owners)
-    for name, weight in (("k", key_weight), ("v", value_weight)):
-        absorb(name, [weight], (((0, 0),),), 1)
 
     ka1, kb1, value_block, totals = barrier((ka1, kb1, value_block, totals))
     kb2 = send(ka1, 2, 1)
     ka2 = send(kb1, 2, 0)
     vb1 = send(value_block, 1, 1)
+    for name, weight in (("k", key_weight), ("v", value_weight)):
+        absorb(name, [weight], (((0, 0),),), 1)
     absorb("k", [ka1, kb1], (((0, 1),), ((1, 1),)))
 
-    kb2, va1, totals = barrier((kb2, va1, totals))
+    kb2, va1, own_block, totals = barrier((kb2, va1, value_block, totals))
+    ends = [(0, groups - 1), (groups - 1, 0)]
+    far_query = lax.ppermute(own_block[depth:], "seq", ends)
     ka3 = send(kb2, 3, 0)
     vb2 = send(va1, 2, 1)
     absorb("v", [va1], (((0, 1),),))
@@ -521,7 +523,6 @@
     top = chip_top(raw_keys)
     smooth = smooth_of(top)
     vb2, top = barrier((vb2, top))
-    far_query = lax.ppermute(vb2[depth:], "seq", line_pairs(3, 0, groups))
     va3 = send(vb2, 3, 0)
     va2, vb2, smooth = barrier((va2, vb2, smooth))
     absorb("v", [va2 + vb2], (((0, 2), (1, 2)),))

time: 132 us -> 125 us (0.947)
  waiting for transfers between devices: 57.3 us -> 48 us
  starting transfers between devices: 28.3 us -> 31.9 us
    ppermute x1, waiting for transfers between devices: 10.7 us -> 0.01 us  [line_project(): far_query = lax.ppermute(own_block[depth:], 'seq', ends)]
    ppermute x1, starting transfers between devices: 1.28 us -> 4.54 us  [line_project(): far_query = lax.ppermute(own_block[depth:], 'seq', ends)]
    unnamed x16 -> x14, local copies, waits for them, and re-layouts: 3.15 us -> 2.11 us
  transfers between devices with their start and end apart: 31 -> 31, of which waited for: 11 -> 12; matrix products, arithmetic and copies ran while one was open for 4% -> 4% of each run, Pallas kernels for 24% -> 26%
where the time goes in v9:
time: 125 us
  waiting for transfers between devices  48 us (38%)
  Pallas kernels  35.7 us (29%)
  starting transfers between devices  31.9 us (26%)
  other arithmetic  5.49 us (4%)
  local copies, waits for them, and re-layouts  2.15 us (2%)
    ppermute x10, waiting for transfers between devices, send(): return lax.ppermute(x, 'seq', line_pairs(hop, parity, groups))  34.8 us
    pallas_call x16, Pallas kernels, project(): pl.pallas_call(functools.partial(project_kernel, hops, back, groups, owne...  21.8 us
    ppermute x10, starting transfers between devices, send(): return lax.ppermute(x, 'seq', line_pairs(hop, parity, groups))  16 us
    ppermute x6, starting transfers between devices, swapped(): return lax.ppermute(x, axis, [(i, partner(i, k, n)) for i in range(n)])  8.83 us
    ppermute x6, waiting for transfers between devices, swapped(): return lax.ppermute(x, axis, [(i, partner(i, k, n)) for i in range(n)])  8.79 us
    pallas_call x1, Pallas kernels, load(): pl.pallas_call(functools.partial(load_kernel, owners), out_shape=(jax.Sha...  6.57 us
    pallas_call x1, Pallas kernels, score(): pl.pallas_call(functools.partial(score_kernel, slots, parts, steps, scale...  4.73 us
    ppermute x1, starting transfers between devices, line_project(): far_query = lax.ppermute(own_block[depth:], 'seq', ends)  4.54 us
  transfers between devices with their start and end apart: 31, of which 12 were waited for; matrix products, arithmetic and copies ran while one was open for 4% of the time, Pallas kernels for 26%

profile of v9, /device:TPU:0, one launch (start us, length us, event | category | flops | bytes accessed | tf_op | source)
XLA Modules:
  0.0 124.8 jit_solution(932996193056861238)
XLA Ops:
  0.6 3.1 %collective-permute-start = (bf16[1024,256]{1,0:T(8,128)(2,1)}, bf16[1024,256]{1,0:T(8,128)(2,1)S(1)}, u32[]{:S(2)}, u32[]{:S(2)}) collective-permute-start(bf16[1024,256]{1,0:T(8,128)(2,1)} %refs_0_), channel_id=1, source_target_pairs={{0,8},{8,0},{16,24},{24,16},{1,9},{9,1},{17,25},{25,17},{2,10},{10... | collective-permute-start | bytes 1572872 | tf_op jit(solution)/shard_map/ppermute | solution.py:479
  3.7 0.7 collective-permute-start.1
  4.5 0.5 collective-permute-start.7
  5.0 0.9 select_bitcast_fusion.query
  6.0 1.0 copy-done
  7.1 1.0 copy-done.1
  8.1 6.6 %load.1 = (bf16[1024,8192]{1,0:T(8,128)(2,1)S(1)}, f32[1024,256]{1,0:T(8,128)S(1)}, f32[1024,256]{1,0:T(8,128)S(1)}) custom-call(s32[2]{0:T(128)S(1)} %pad_add_fusion.place, bf16[1024,8192]{1,0:T(8,128)(2,1)} %hidden.1, bf16[1024,256]{1,0:T(8,128)(2,1)S(1)} %copy-done.1, bf16[1152,256]{1,0:T(8,128)(2,1)S(1)} %pack.1.refs_1_), custom_call_target="tpu_custom_call" | custom-call | flops 1073741824 | bytes 16777216 | tf_op jit(solution)/shard_map/load/pallas_call | solution.py:114
  14.7 1.2 collective-permute-done.refs_0_
  15.9 0.5 collective-permute-start.5
  16.4 4.8 %collective-permute-start.3 = (bf16[1152,256]{1,0:T(8,128)(2,1)S(1)}, bf16[1152,256]{1,0:T(8,128)(2,1)S(1)}, u32[]{:S(2)}, u32[]{:S(2)}) collective-permute-start(bf16[1152,256]{1,0:T(8,128)(2,1)S(1)} %pack.1.refs_1_), channel_id=1, source_target_pairs={{0,8},{8,0},{16,24},{24,16},{1,9},{9,1},{17,25},{25,17},{2,10},{10... | collective-permute-start | bytes 1769480 | tf_op jit(solution)/shard_map/ppermute | solution.py:479
  21.2 0.7 collective-permute-start.2
  21.9 1.4 %project.19.refs_1_ = f32[1024,256]{1,0:T(8,128)S(1)} custom-call(s32[2]{0:T(128)S(1)} %pad_add_fusion.place, bf16[1024,8192]{1,0:T(8,128)(2,1)S(1)} %get-tuple-element.86.left, bf16[1024,256]{1,0:T(8,128)(2,1)S(1)} %collective-permute-done.7.refs_0_, f32[1024,256]{1,0:T(8,128)S(1)} %get-tuple-element.89.refs_1_), custom_call_target="tpu_custom_call", output_to_operand_aliasing={{}: (3, {})} | custom-call | flops 536870912 | bytes 4718592 | tf_op jit(solution)/shard_map/project/pallas_call | solution.py:170
  23.3 1.4 %project.16.refs_2_ = f32[1024,256]{1,0:T(8,128)S(1)} custom-call(s32[2]{0:T(128)S(1)} %pad_add_fusion.place, bf16[1024,8192]{1,0:T(8,128)(2,1)S(1)} %get-tuple-element.86.left, bf16[1024,256]{1,0:T(8,128)(2,1)S(1)} %collective-permute-done.6.refs_0_, f32[1024,256]{1,0:T(8,128)S(1)} %get-tuple-element.88.refs_1_), custom_call_target="tpu_custom_call", output_to_operand_aliasing={{}: (3, {})} | custom-call | flops 536870912 | bytes 4718592 | tf_op jit(solution)/shard_map/project/pallas_call | solution.py:170
  24.8 1.5 %project.17.refs_2_ = f32[1024,256]{1,0:T(8,128)S(1)} custom-call(s32[2]{0:T(128)S(1)} %pad_add_fusion.place, bf16[1024,8192]{1,0:T(8,128)(2,1)S(1)} %get-tuple-element.86.left, bf16[1024,256]{1,0:T(8,128)(2,1)S(1)} %collective-permute-done.refs_0_, bf16[1024,256]{1,0:T(8,128)(2,1)S(1)} %collective-permute-done.1.refs_1_, ...), custom_call_target="tpu_custom_call", output_to_operand_aliasing={{}: (4, {})} | custom-call | flops 1073741824 | bytes 7340032 | tf_op jit(solution)/shard_map/project/pallas_call | solution.py:170
  26.3 1.5 %project.18.refs_1_ = f32[1024,256]{1,0:T(8,128)S(1)} custom-call(s32[2]{0:T(128)S(1)} %pad_add_fusion.place, bf16[1024,8192]{1,0:T(8,128)(2,1)S(1)} %get-tuple-element.86.left, bf16[1024,256]{1,0:T(8,128)(2,1)S(1)} %collective-permute-done.4.refs_0_, bf16[1024,256]{1,0:T(8,128)(2,1)S(1)} %collective-permute-done.5.refs_1_, ...), custom_call_target="tpu_custom_call", output_to_operand_aliasing={{}: (4, {})} | custom-call | flops 1073741824 | bytes 7340032 | tf_op jit(solution)/shard_map/project/pallas_call | solution.py:170
  27.8 6.8 %collective-permute-done.3.refs_0_ = bf16[1152,256]{1,0:T(8,128)(2,1)S(1)} collective-permute-done((bf16[1152,256]{1,0:T(8,128)(2,1)S(1)}, bf16[1152,256]{1,0:T(8,128)(2,1)S(1)}, u32[]{:S(2)}, u32[]{:S(2)}) %collective-permute-start.3) | collective-permute-done | bytes 589856 | tf_op jit(solution)/shard_map/ppermute | solution.py:479
  34.7 1.3 %collective-permute-start.9 = (bf16[1024,256]{1,0:T(8,128)(2,1)S(1)}, bf16[1024,256]{1,0:T(8,128)(2,1)S(1)}, u32[]{:S(2)}, u32[]{:S(2)}) collective-permute-start(bf16[1024,256]{1,0:T(8,128)(2,1)S(1)} %collective-permute-done.1.refs_1_), channel_id=1, source_target_pairs={{8,0},{16,24},{9,1},{17,25},{10,2},{18,26},{11,3},{19,27},{12,4},{... | collective-permute-start | bytes 1572872 | tf_op jit(solution)/shard_map/ppermute | solution.py:479
  35.9 0.7 collective-permute-start.8
  36.7 1.4 %project.20.refs_1_ = f32[1024,256]{1,0:T(8,128)S(1)} custom-call(s32[2]{0:T(128)S(1)} %pad_add_fusion.place, bf16[1024,8192]{1,0:T(8,128)(2,1)S(1)} %get-tuple-element.86.left, bf16[1152,256]{1,0:T(8,128)(2,1)S(1)} %collective-permute-done.3.refs_0_, f32[1024,256]{1,0:T(8,128)S(1)} %project.19.refs_1_), custom_call_target="tpu_custom_call", output_to_operand_aliasing={{}: (3, {})} | custom-call | flops 536870912 | bytes 4718592 | tf_op jit(solution)/shard_map/project/pallas_call | solution.py:170
  38.1 1.4 %project.21.refs_1_ = f32[1024,256]{1,0:T(8,128)S(1)} custom-call(s32[2]{0:T(128)S(1)} %pad_add_fusion.place, bf16[1024,8192]{1,0:T(8,128)(2,1)S(1)} %get-tuple-element.86.left, bf16[1152,256]{1,0:T(8,128)(2,1)S(1)} %collective-permute-done.10.refs_0_, f32[1024,256]{1,0:T(8,128)S(1)} %project.20.refs_1_), custom_call_target="tpu_custom_call", output_to_operand_aliasing={{}: (3, {})} | custom-call | flops 536870912 | bytes 4718592 | tf_op jit(solution)/shard_map/project/pallas_call | solution.py:170
  39.6 11.3 %collective-permute-done.9 = bf16[1024,256]{1,0:T(8,128)(2,1)S(1)} collective-permute-done((bf16[1024,256]{1,0:T(8,128)(2,1)S(1)}, bf16[1024,256]{1,0:T(8,128)(2,1)S(1)}, u32[]{:S(2)}, u32[]{:S(2)}) %collective-permute-start.9) | collective-permute-done | bytes 524320 | tf_op jit(solution)/shard_map/ppermute | solution.py:479
  51.2 1.4 %project.22.refs_1_ = f32[1024,256]{1,0:T(8,128)S(1)} custom-call(s32[2]{0:T(128)S(1)} %pad_add_fusion.place, bf16[1024,8192]{1,0:T(8,128)(2,1)S(1)} %get-tuple-element.86.left, bf16[1024,256]{1,0:T(8,128)(2,1)S(1)} %add.74.refs_0_, f32[1024,256]{1,0:T(8,128)S(1)} %project.18.refs_1_), custom_call_target="tpu_custom_call", output_to_operand_aliasing={{}: (3, {})} | custom-call | flops 536870912 | bytes 4718592 | tf_op jit(solution)/shard_map/project/pallas_call | solution.py:170
  52.7 0.3 collective-permute-done.11.refs_0_
  53.0 1.4 %project.23.refs_1_ = f32[1024,256]{1,0:T(8,128)S(1)} custom-call(s32[2]{0:T(128)S(1)} %pad_add_fusion.place, bf16[1024,8192]{1,0:T(8,128)(2,1)S(1)} %get-tuple-element.86.left, bf16[1024,256]{1,0:T(8,128)(2,1)S(1)} %collective-permute-done.11.refs_0_, f32[1024,256]{1,0:T(8,128)S(1)} %project.22.refs_1_), custom_call_target="tpu_custom_call", output_to_operand_aliasing={{}: (3, {})} | custom-call | flops 536870912 | bytes 4718592 | tf_op jit(solution)/shard_map/project/pallas_call | solution.py:170
  54.5 0.2 collective-permute-start.15
  54.7 1.3 %collective-permute-start.14 = (bf16[1024,256]{1,0:T(8,128)(2,1)S(1)}, bf16[1024,256]{1,0:T(8,128)(2,1)S(1)}, u32[]{:S(2)}, u32[]{:S(2)}) collective-permute-start(bf16[1024,256]{1,0:T(8,128)(2,1)S(1)} %collective-permute-done.2), channel_id=1, source_target_pairs={{8,0},{16,24},{9,1},{17,25},{10,2},{18,26},{11,3},{19,27},{12,4},{... | collective-permute-start | bytes 1572872 | tf_op jit(solution)/shard_map/ppermute | solution.py:479
  56.1 0.6 convert_reduce_fusion
  56.6 0.2 fusion.2
  56.9 0.7 project.24.refs_1_
  57.6 0.7 project.25.refs_1_
  58.4 12.4 %collective-permute-done.14.refs_0_ = bf16[1024,256]{1,0:T(8,128)(2,1)S(1)} collective-permute-done((bf16[1024,256]{1,0:T(8,128)(2,1)S(1)}, bf16[1024,256]{1,0:T(8,128)(2,1)S(1)}, u32[]{:S(2)}, u32[]{:S(2)}) %collective-permute-start.14) | collective-permute-done | bytes 524320 | tf_op jit(solution)/shard_map/ppermute | solution.py:479
  70.8 0.2 fusion.1.count
  71.0 0.7 collective-permute-start.13
  71.7 4.5 %collective-permute-start.21 = (bf16[128,256]{1,0:T(8,128)(2,1)S(1)}, bf16[128,256]{1,0:T(8,128)(2,1)S(1)}, u32[]{:S(2)}, u32[]{:S(2)}) collective-permute-start(bf16[128,256]{1,0:T(8,128)(2,1)S(1)} %slice.79), channel_id=1, source_target_pairs={{0,24},{24,0},{1,25},{25,1},{2,26},{26,2},{3,27},{27,3},{4,28},{28... | collective-permute-start | bytes 196616 | tf_op jit(solution)/shard_map/ppermute | solution.py:508
  76.3 1.5 %collective-permute-start.12 = (bf16[1152,256]{1,0:T(8,128)(2,1)S(1)}, bf16[1152,256]{1,0:T(8,128)(2,1)S(1)}, u32[]{:S(2)}, u32[]{:S(2)}) collective-permute-start(bf16[1152,256]{1,0:T(8,128)(2,1)S(1)} %collective-permute-done.8.refs_0_), channel_id=1, source_target_pairs={{8,0},{16,24},{9,1},{17,25},{10,2},{18,26},{11,3},{19,27},{12,4},{... | collective-permute-start | bytes 1769480 | tf_op jit(solution)/shard_map/ppermute | solution.py:479
  77.8 1.4 %project.26.refs_1_ = f32[1024,256]{1,0:T(8,128)S(1)} custom-call(s32[2]{0:T(128)S(1)} %pad_add_fusion.place, bf16[1024,8192]{1,0:T(8,128)(2,1)S(1)} %get-tuple-element.86.left, bf16[1024,256]{1,0:T(8,128)(2,1)S(1)} %collective-permute-done.14.refs_0_, f32[1024,256]{1,0:T(8,128)S(1)} %project.23.refs_1_), custom_call_target="tpu_custom_call", output_to_operand_aliasing={{}: (3, {})} | custom-call | flops 536870912 | bytes 4718592 | tf_op jit(solution)/shard_map/project/pallas_call | solution.py:170
  79.2 1.4 %project.27 = f32[1024,256]{1,0:T(8,128)S(1)} custom-call(s32[2]{0:T(128)S(1)} %pad_add_fusion.place, bf16[1024,8192]{1,0:T(8,128)(2,1)S(1)} %get-tuple-element.86.left, bf16[1024,256]{1,0:T(8,128)(2,1)S(1)} %collective-permute-done.16.refs_0_, f32[1024,256]{1,0:T(8,128)S(1)} %project.26.refs_1_), custom_call_target="tpu_custom_call", output_to_operand_aliasing={{}: (3, {})} | custom-call | flops 536870912 | bytes 4718592 | tf_op jit(solution)/shard_map/project/pallas_call | solution.py:170
  80.7 0.3 collective-permute-start.17
  81.0 0.9 collective-permute-done.17
  82.0 1.1 collective-permute-start.18
  83.1 0.7 collective-permute-start.19
  83.7 2.6 %collective-permute-start.20 = (f32[1,256]{1,0:T(1,128)S(1)}, f32[1,256]{1,0:T(1,128)S(1)}, u32[]{:S(2)}, u32[]{:S(2)}) collective-permute-start(f32[1,256]{1,0:T(1,128)S(1)} %max.36), channel_id=1, source_target_pairs={{0,24},{8,16},{16,8},{24,0},{1,25},{9,17},{17,9},{25,1},{2,26},{10... | collective-permute-start | bytes 3080 | tf_op jit(solution)/shard_map/ppermute | solution.py:32
  86.4 1.3 %collective-permute-start.24 = (bf16[1152,256]{1,0:T(8,128)(2,1)S(1)}, bf16[1152,256]{1,0:T(8,128)(2,1)S(1)}, u32[]{:S(2)}, u32[]{:S(2)}) collective-permute-start(bf16[1152,256]{1,0:T(8,128)(2,1)S(1)} %collective-permute-done.13), channel_id=1, source_target_pairs={{8,0},{16,24},{9,1},{17,25},{10,2},{18,26},{11,3},{19,27},{12,4},{... | collective-permute-start | bytes 1769480 | tf_op jit(solution)/shard_map/ppermute | solution.py:479
  87.7 6.8 %collective-permute-done.18 = f32[1,256]{1,0:T(1,128)S(1)} collective-permute-done((f32[1,256]{1,0:T(1,128)S(1)}, f32[1,256]{1,0:T(1,128)S(1)}, u32[]{:S(2)}, u32[]{:S(2)}) %collective-permute-start.18) | collective-permute-done | bytes 1056 | tf_op jit(solution)/shard_map/ppermute | solution.py:32
  94.8 0.1 minimum_convert_fusion.1
  95.0 1.4 %project.28.refs_1_ = f32[1024,256]{1,0:T(8,128)S(1)} custom-call(s32[2]{0:T(128)S(1)} %pad_add_fusion.place, bf16[1024,8192]{1,0:T(8,128)(2,1)S(1)} %get-tuple-element.86.left, bf16[1152,256]{1,0:T(8,128)(2,1)S(1)} %add.86.refs_0_, f32[1024,256]{1,0:T(8,128)S(1)} %project.25.refs_1_), custom_call_target="tpu_custom_call", output_to_operand_aliasing={{}: (3, {})} | custom-call | flops 536870912 | bytes 4718592 | tf_op jit(solution)/shard_map/project/pallas_call | solution.py:170
  96.4 0.6 collective-permute-start.22
  97.1 1.4 %project.29.refs_1_ = f32[1024,256]{1,0:T(8,128)S(1)} custom-call(s32[2]{0:T(128)S(1)} %pad_add_fusion.place, bf16[1024,8192]{1,0:T(8,128)(2,1)S(1)} %get-tuple-element.86.left, bf16[1152,256]{1,0:T(8,128)(2,1)S(1)} %collective-permute-done.23.refs_0_, f32[1024,256]{1,0:T(8,128)S(1)} %project.28.refs_1_), custom_call_target="tpu_custom_call", output_to_operand_aliasing={{}: (3, {})} | custom-call | flops 536870912 | bytes 4718592 | tf_op jit(solution)/shard_map/project/pallas_call | solution.py:170
  98.5 4.7 %score.1 = (bf16[4,256,2048]{2,1,0:T(8,128)(2,1)S(1)}, f32[2,256]{1,0:T(2,128)S(1)}, f32[2,256]{1,0:T(2,128)S(1)}, f32[2,256]{1,0:T(2,128)S(1)}, f32[2,256]{1,0:T(2,128)S(1)}) custom-call(s32[4]{0:T(128)S(1)} %iota_xor_fusion.group, bf16[4,128,256]{2,1,0:T(8,128)(2,1)S(1)} %pad_maximum_fusion.query, f32[1,128]{1,0:T(1,128)S(1)} %broadcast_select_fusion.7.smooth, ...), custom_call_target="tpu_custom_call" | custom-call | flops 536870912 | bytes 4194304 | tf_op jit(solution)/shard_map/score/pallas_call | solution.py:241
  103.3 3.1 %collective-permute-done.24.refs_0_ = bf16[1152,256]{1,0:T(8,128)(2,1)S(1)} collective-permute-done((bf16[1152,256]{1,0:T(8,128)(2,1)S(1)}, bf16[1152,256]{1,0:T(8,128)(2,1)S(1)}, u32[]{:S(2)}, u32[]{:S(2)}) %collective-permute-start.24) | collective-permute-done | bytes 589856 | tf_op jit(solution)/shard_map/ppermute | solution.py:479
  106.4 1.4 %project.30.refs_1_ = f32[1024,256]{1,0:T(8,128)S(1)} custom-call(s32[2]{0:T(128)S(1)} %pad_add_fusion.place, bf16[1024,8192]{1,0:T(8,128)(2,1)S(1)} %get-tuple-element.86.left, bf16[1152,256]{1,0:T(8,128)(2,1)S(1)} %collective-permute-done.24.refs_0_, f32[1024,256]{1,0:T(8,128)S(1)} %project.29.refs_1_), custom_call_target="tpu_custom_call", output_to_operand_aliasing={{}: (3, {})} | custom-call | flops 536870912 | bytes 4718592 | tf_op jit(solution)/shard_map/project/pallas_call | solution.py:170
  107.9 0.5 collective-permute-done.25.refs_0_
  108.3 1.4 %project.31 = f32[1024,256]{1,0:T(8,128)S(1)} custom-call(s32[2]{0:T(128)S(1)} %pad_add_fusion.place, bf16[1024,8192]{1,0:T(8,128)(2,1)S(1)} %get-tuple-element.86.left, bf16[1152,256]{1,0:T(8,128)(2,1)S(1)} %collective-permute-done.25.refs_0_, f32[1024,256]{1,0:T(8,128)S(1)} %project.30.refs_1_), custom_call_target="tpu_custom_call", output_to_operand_aliasing={{}: (3, {})} | custom-call | flops 536870912 | bytes 4718592 | tf_op jit(solution)/shard_map/project/pallas_call | solution.py:170
  110.0 0.2 collective-permute-start.26
  110.2 1.4 %collective-permute-done.26.refs_1_ = bf16[1024,128]{1,0:T(8,128)(2,1)S(1)} collective-permute-done((bf16[1024,128]{1,0:T(8,128)(2,1)S(1)}, bf16[1024,128]{1,0:T(8,128)(2,1)S(1)}, u32[]{:S(2)}, u32[]{:S(2)}) %collective-permute-start.26) | collective-permute-done | bytes 262176 | tf_op jit(solution)/shard_map/ppermute | solution.py:23
  111.6 1.8 %weigh.1 = (bf16[272,128]{1,0:T(8,128)(2,1)S(1)}, bf16[272,128]{1,0:T(8,128)(2,1)S(1)}, bf16[272,128]{1,0:T(8,128)(2,1)S(1)}, bf16[272,128]{1,0:T(8,128)(2,1)S(1)}) custom-call(bf16[4,256,2048]{2,1,0:T(8,128)(2,1)S(1)} %get-tuple-element.118.probs, bf16[1024,128]{1,0:T(8,128)(2,1)S(1)} %get-tuple-element.156.refs_0_, ...), custom_call_target="tpu_custom_call" | custom-call | flops 536870912 | bytes 4194304 | tf_op jit(solution)/shard_map/weigh/pallas_call | solution.py:316
  113.5 2.2 %collective-permute-start.28 = (bf16[272,128]{1,0:T(8,128)(2,1)S(1)}, bf16[272,128]{1,0:T(8,128)(2,1)S(1)}, u32[]{:S(2)}, u32[]{:S(2)}) collective-permute-start(bf16[272,128]{1,0:T(8,128)(2,1)S(1)} %get-tuple-element.136), channel_id=1, source_target_pairs={{0,16},{8,24},{16,0},{24,8},{1,17},{9,25},{17,1},{25,9},{2,18},{10... | collective-permute-start | bytes 208904 | tf_op jit(solution)/shard_map/ppermute | solution.py:32
  115.7 2.2 %collective-permute-start.29 = (bf16[272,128]{1,0:T(8,128)(2,1)S(1)}, bf16[272,128]{1,0:T(8,128)(2,1)S(1)}, u32[]{:S(2)}, u32[]{:S(2)}) collective-permute-start(bf16[272,128]{1,0:T(8,128)(2,1)S(1)} %get-tuple-element.137), channel_id=1, source_target_pairs={{0,24},{8,16},{16,8},{24,0},{1,25},{9,17},{17,9},{25,1},{2,26},{10... | collective-permute-start | bytes 208904 | tf_op jit(solution)/shard_map/ppermute | solution.py:32
  117.8 2.3 %broadcast_select_fusion = bf16[1024,2,256]{2,1,0:T(2,128)(2,1)} fusion(pred[2]{0:T(512)(128)(4,1)S(1)} %iota_compare_fusion.5, bf16[1024,256]{1,0:T(8,128)(2,1)S(1)} %minimum_convert_fusion, bf16[1024,256]{1,0:T(8,128)(2,1)S(1)} %minimum_convert_fusion.1), kind=kLoop, calls=%fused_computation.3 | loop fusion | flops 524288 | bytes 2097154 | tf_op jit(solution)/shard_map/jit(_where)/select_n | solution.py:616
  120.2 0.2 fresh.1
  120.4 2.0 %collective-permute-done.28.refs_2_ = bf16[272,128]{1,0:T(8,128)(2,1)S(1)} collective-permute-done((bf16[272,128]{1,0:T(8,128)(2,1)S(1)}, bf16[272,128]{1,0:T(8,128)(2,1)S(1)}, u32[]{:S(2)}, u32[]{:S(2)}) %collective-permute-start.28) | collective-permute-done | bytes 69664 | tf_op jit(solution)/shard_map/ppermute | solution.py:32
  122.4 0.4 finish.1
  122.9 1.2 collective-permute-done.30
  124.2 0.7 maximum_bitcast_fusion
  (70 shorter events, 1.5 us)
Async XLA Ops:
  0.6 15.3 %collective-permute-start = (bf16[1024,256]{1,0:T(8,128)(2,1)}, bf16[1024,256]{1,0:T(8,128)(2,1)S(1)}, u32[]{:S(2)}, u32[]{:S(2)}) collective-permute-start(bf16[1024,256]{1,0:T(8,128)(2,1)} %refs_0_), channel_id=1, source_target_pairs={{0,8},{8,0},{16,24},{24,16},{1,9},{9,1},{17,25},{25,17},{2,10},{10... | collective-permute-start | bytes 1572872 | tf_op jit(solution)/shard_map/ppermute | solution.py:479
  3.7 12.1 %collective-permute-start.1 = (bf16[1024,256]{1,0:T(8,128)(2,1)}, bf16[1024,256]{1,0:T(8,128)(2,1)S(1)}, u32[]{:S(2)}, u32[]{:S(2)}) collective-permute-start(bf16[1024,256]{1,0:T(8,128)(2,1)} %refs_0_), channel_id=1, source_target_pairs={{8,16},{16,8},{9,17},{17,9},{10,18},{18,10},{11,19},{19,11},{12,20... | collective-permute-start | bytes 1572872 | tf_op jit(solution)/shard_map/ppermute | solution.py:479
  4.4 18.9 %collective-permute-start.6 = (bf16[1024,256]{1,0:T(8,128)(2,1)}, bf16[1024,256]{1,0:T(8,128)(2,1)S(1)}, u32[]{:S(2)}, u32[]{:S(2)}) collective-permute-start(bf16[1024,256]{1,0:T(8,128)(2,1)} %refs_0_), channel_id=1, source_target_pairs={{0,1},{1,0},{2,3},{3,2},{4,5},{5,4},{6,7},{7,6},{8,9},{9,8},{10,11... | collective-permute-start | bytes 1572872 | tf_op jit(solution)/shard_map/ppermute | solution.py:23
  4.5 16.6 %collective-permute-start.7 = (bf16[1024,256]{1,0:T(8,128)(2,1)}, bf16[1024,256]{1,0:T(8,128)(2,1)S(1)}, u32[]{:S(2)}, u32[]{:S(2)}) collective-permute-start(bf16[1024,256]{1,0:T(8,128)(2,1)} %weight.1), channel_id=1, source_target_pairs={{0,1},{1,0},{2,3},{3,2},{4,5},{5,4},{6,7},{7,6},{8,9},{9,8},{10,11... | collective-permute-start | bytes 1572872 | tf_op jit(solution)/shard_map/ppermute | solution.py:23
  6.0 1.0 copy-start
  7.1 1.0 copy-start.1
  15.9 10.4 %collective-permute-start.4 = (bf16[1024,256]{1,0:T(8,128)(2,1)S(1)}, bf16[1024,256]{1,0:T(8,128)(2,1)S(1)}, u32[]{:S(2)}, u32[]{:S(2)}) collective-permute-start(bf16[1024,256]{1,0:T(8,128)(2,1)S(1)} %collective-permute-done.refs_0_), channel_id=1, source_target_pairs={{0,1},{1,0},{2,3},{3,2},{4,5},{5,4},{6,7},{7,6},{8,9},{9,8},{10,11... | collective-permute-start | bytes 1572872 | tf_op jit(solution)/shard_map/ppermute | solution.py:23
  15.9 10.4 %collective-permute-start.5 = (bf16[1024,256]{1,0:T(8,128)(2,1)S(1)}, bf16[1024,256]{1,0:T(8,128)(2,1)S(1)}, u32[]{:S(2)}, u32[]{:S(2)}) collective-permute-start(bf16[1024,256]{1,0:T(8,128)(2,1)S(1)} %collective-permute-done.1.refs_1_), channel_id=1, source_target_pairs={{0,1},{1,0},{2,3},{3,2},{4,5},{5,4},{6,7},{7,6},{8,9},{9,8},{10,11... | collective-permute-start | bytes 1572872 | tf_op jit(solution)/shard_map/ppermute | solution.py:23
  16.4 18.2 %collective-permute-start.3 = (bf16[1152,256]{1,0:T(8,128)(2,1)S(1)}, bf16[1152,256]{1,0:T(8,128)(2,1)S(1)}, u32[]{:S(2)}, u32[]{:S(2)}) collective-permute-start(bf16[1152,256]{1,0:T(8,128)(2,1)S(1)} %pack.1.refs_1_), channel_id=1, source_target_pairs={{0,8},{8,0},{16,24},{24,16},{1,9},{9,1},{17,25},{25,17},{2,10},{10... | collective-permute-start | bytes 1769480 | tf_op jit(solution)/shard_map/ppermute | solution.py:479
  21.2 13.5 %collective-permute-start.2 = (bf16[1024,256]{1,0:T(8,128)(2,1)S(1)}, bf16[1024,256]{1,0:T(8,128)(2,1)S(1)}, u32[]{:S(2)}, u32[]{:S(2)}) collective-permute-start(bf16[1024,256]{1,0:T(8,128)(2,1)S(1)} %collective-permute-done.refs_0_), channel_id=1, source_target_pairs={{8,16},{16,8},{9,17},{17,9},{10,18},{18,10},{11,19},{19,11},{12,20... | collective-permute-start | bytes 1572872 | tf_op jit(solution)/shard_map/ppermute | solution.py:479
  27.8 23.3 %copy-start.6 = (s32[32]{0:T(128)S(1)}, s32[32]{0:T(128)}, u32[]{:S(2)}) copy-start(s32[32]{0:T(128)} %param.15) | copy-start | bytes 388
  34.7 3.5 %collective-permute-start.10 = (bf16[1152,256]{1,0:T(8,128)(2,1)S(1)}, bf16[1152,256]{1,0:T(8,128)(2,1)S(1)}, u32[]{:S(2)}, u32[]{:S(2)}) collective-permute-start(bf16[1152,256]{1,0:T(8,128)(2,1)S(1)} %collective-permute-done.3.refs_0_), channel_id=1, source_target_pairs={{0,1},{1,0},{2,3},{3,2},{4,5},{5,4},{6,7},{7,6},{8,9},{9,8},{10,11... | collective-permute-start | bytes 1769480 | tf_op jit(solution)/shard_map/ppermute | solution.py:23
  34.7 16.2 %collective-permute-start.9 = (bf16[1024,256]{1,0:T(8,128)(2,1)S(1)}, bf16[1024,256]{1,0:T(8,128)(2,1)S(1)}, u32[]{:S(2)}, u32[]{:S(2)}) collective-permute-start(bf16[1024,256]{1,0:T(8,128)(2,1)S(1)} %collective-permute-done.1.refs_1_), channel_id=1, source_target_pairs={{8,0},{16,24},{9,1},{17,25},{10,2},{18,26},{11,3},{19,27},{12,4},{... | collective-permute-start | bytes 1572872 | tf_op jit(solution)/shard_map/ppermute | solution.py:479
  35.9 18.5 %collective-permute-start.8 = (bf16[1152,256]{1,0:T(8,128)(2,1)S(1)}, bf16[1152,256]{1,0:T(8,128)(2,1)S(1)}, u32[]{:S(2)}, u32[]{:S(2)}) collective-permute-start(bf16[1152,256]{1,0:T(8,128)(2,1)S(1)} %pack.1.refs_1_), channel_id=1, source_target_pairs={{8,16},{16,8},{9,17},{17,9},{10,18},{18,10},{11,19},{19,11},{12,20... | collective-permute-start | bytes 1769480 | tf_op jit(solution)/shard_map/ppermute | solution.py:479
  51.0 2.0 %collective-permute-start.11 = (bf16[1024,256]{1,0:T(8,128)(2,1)S(1)}, bf16[1024,256]{1,0:T(8,128)(2,1)S(1)}, u32[]{:S(2)}, u32[]{:S(2)}) collective-permute-start(bf16[1024,256]{1,0:T(8,128)(2,1)S(1)} %add.74.refs_0_), channel_id=1, source_target_pairs={{0,1},{1,0},{2,3},{3,2},{4,5},{5,4},{6,7},{7,6},{8,9},{9,8},{10,11... | collective-permute-start | bytes 1572872 | tf_op jit(solution)/shard_map/ppermute | solution.py:23
  51.2 4.9 %copy-start.3 = (s32[32,32]{1,0:T(8,128)S(1)}, s32[32,32]{1,0:T(8,128)}, u32[]{:S(2)}) copy-start(s32[32,32]{1,0:T(8,128)} %param.14) | copy-start | bytes 12292
  54.5 3.1 %collective-permute-start.15 = (bf16[1152,256]{1,0:T(8,128)(2,1)S(1)}, bf16[1152,256]{1,0:T(8,128)(2,1)S(1)}, u32[]{:S(2)}, u32[]{:S(2)}) collective-permute-start(bf16[1152,256]{1,0:T(8,128)(2,1)S(1)} %collective-permute-done.8.refs_0_), channel_id=1, source_target_pairs={{0,1},{1,0},{2,3},{3,2},{4,5},{5,4},{6,7},{7,6},{8,9},{9,8},{10,11... | collective-permute-start | bytes 1769480 | tf_op jit(solution)/shard_map/ppermute | solution.py:23
  54.7 16.1 %collective-permute-start.14 = (bf16[1024,256]{1,0:T(8,128)(2,1)S(1)}, bf16[1024,256]{1,0:T(8,128)(2,1)S(1)}, u32[]{:S(2)}, u32[]{:S(2)}) collective-permute-start(bf16[1024,256]{1,0:T(8,128)(2,1)S(1)} %collective-permute-done.2), channel_id=1, source_target_pairs={{8,0},{16,24},{9,1},{17,25},{10,2},{18,26},{11,3},{19,27},{12,4},{... | collective-permute-start | bytes 1572872 | tf_op jit(solution)/shard_map/ppermute | solution.py:479
  56.8 14.1 %copy-start.5 = (f32[2,256]{1,0:T(2,128)S(1)}, f32[2,256]{1,0:T(2,128)}, u32[]{:S(2)}) copy-start(f32[2,256]{1,0:T(2,128)} %param.11) | copy-start | bytes 6148
  70.7 8.5 %collective-permute-start.16 = (bf16[1024,256]{1,0:T(8,128)(2,1)S(1)}, bf16[1024,256]{1,0:T(8,128)(2,1)S(1)}, u32[]{:S(2)}, u32[]{:S(2)}) collective-permute-start(bf16[1024,256]{1,0:T(8,128)(2,1)S(1)} %collective-permute-done.14.refs_0_), channel_id=1, source_target_pairs={{0,1},{1,0},{2,3},{3,2},{4,5},{5,4},{6,7},{7,6},{8,9},{9,8},{10,11... | collective-permute-start | bytes 1572872 | tf_op jit(solution)/shard_map/ppermute | solution.py:23
  71.0 15.4 %collective-permute-start.13 = (bf16[1152,256]{1,0:T(8,128)(2,1)S(1)}, bf16[1152,256]{1,0:T(8,128)(2,1)S(1)}, u32[]{:S(2)}, u32[]{:S(2)}) collective-permute-start(bf16[1152,256]{1,0:T(8,128)(2,1)S(1)} %collective-permute-done.3.refs_0_), channel_id=1, source_target_pairs={{8,16},{16,8},{9,17},{17,9},{10,18},{18,10},{11,19},{19,11},{12,20... | collective-permute-start | bytes 1769480 | tf_op jit(solution)/shard_map/ppermute | solution.py:479
  71.7 12.0 %collective-permute-start.21 = (bf16[128,256]{1,0:T(8,128)(2,1)S(1)}, bf16[128,256]{1,0:T(8,128)(2,1)S(1)}, u32[]{:S(2)}, u32[]{:S(2)}) collective-permute-start(bf16[128,256]{1,0:T(8,128)(2,1)S(1)} %slice.79), channel_id=1, source_target_pairs={{0,24},{24,0},{1,25},{25,1},{2,26},{26,2},{3,27},{27,3},{4,28},{28... | collective-permute-start | bytes 196616 | tf_op jit(solution)/shard_map/ppermute | solution.py:508
  76.3 18.2 %collective-permute-start.12 = (bf16[1152,256]{1,0:T(8,128)(2,1)S(1)}, bf16[1152,256]{1,0:T(8,128)(2,1)S(1)}, u32[]{:S(2)}, u32[]{:S(2)}) collective-permute-start(bf16[1152,256]{1,0:T(8,128)(2,1)S(1)} %collective-permute-done.8.refs_0_), channel_id=1, source_target_pairs={{8,0},{16,24},{9,1},{17,25},{10,2},{18,26},{11,3},{19,27},{12,4},{... | collective-permute-start | bytes 1769480 | tf_op jit(solution)/shard_map/ppermute | solution.py:479
  80.7 1.2 collective-permute-start.17
  82.0 12.5 %collective-permute-start.18 = (f32[1,256]{1,0:T(1,128)S(1)}, f32[1,256]{1,0:T(1,128)S(1)}, u32[]{:S(2)}, u32[]{:S(2)}) collective-permute-start(f32[1,256]{1,0:T(1,128)S(1)} %max.36), channel_id=1, source_target_pairs={{0,8},{8,0},{16,24},{24,16},{1,9},{9,1},{17,25},{25,17},{2,10},{10... | collective-permute-start | bytes 3080 | tf_op jit(solution)/shard_map/ppermute | solution.py:32
  83.1 11.4 %collective-permute-start.19 = (f32[1,256]{1,0:T(1,128)S(1)}, f32[1,256]{1,0:T(1,128)S(1)}, u32[]{:S(2)}, u32[]{:S(2)}) collective-permute-start(f32[1,256]{1,0:T(1,128)S(1)} %max.36), channel_id=1, source_target_pairs={{0,16},{8,24},{16,0},{24,8},{1,17},{9,25},{17,1},{25,9},{2,18},{10... | collective-permute-start | bytes 3080 | tf_op jit(solution)/shard_map/ppermute | solution.py:32
  83.7 10.7 %collective-permute-start.20 = (f32[1,256]{1,0:T(1,128)S(1)}, f32[1,256]{1,0:T(1,128)S(1)}, u32[]{:S(2)}, u32[]{:S(2)}) collective-permute-start(f32[1,256]{1,0:T(1,128)S(1)} %max.36), channel_id=1, source_target_pairs={{0,24},{8,16},{16,8},{24,0},{1,25},{9,17},{17,9},{25,1},{2,26},{10... | collective-permute-start | bytes 3080 | tf_op jit(solution)/shard_map/ppermute | solution.py:32
  86.4 19.9 %collective-permute-start.24 = (bf16[1152,256]{1,0:T(8,128)(2,1)S(1)}, bf16[1152,256]{1,0:T(8,128)(2,1)S(1)}, u32[]{:S(2)}, u32[]{:S(2)}) collective-permute-start(bf16[1152,256]{1,0:T(8,128)(2,1)S(1)} %collective-permute-done.13), channel_id=1, source_target_pairs={{8,0},{16,24},{9,1},{17,25},{10,2},{18,26},{11,3},{19,27},{12,4},{... | collective-permute-start | bytes 1769480 | tf_op jit(solution)/shard_map/ppermute | solution.py:479
  94.5 4.0 %copy-start.4 = (f32[1,256]{1,0:T(1,128)}, f32[1,256]{1,0:T(1,128)S(1)}, u32[]{:S(2)}) copy-start(f32[1,256]{1,0:T(1,128)S(1)} %add_sqrt_fusion) | copy-start | bytes 3076
  94.7 2.4 %collective-permute-start.23 = (bf16[1152,256]{1,0:T(8,128)(2,1)S(1)}, bf16[1152,256]{1,0:T(8,128)(2,1)S(1)}, u32[]{:S(2)}, u32[]{:S(2)}) collective-permute-start(bf16[1152,256]{1,0:T(8,128)(2,1)S(1)} %add.86.refs_0_), channel_id=1, source_target_pairs={{0,1},{1,0},{2,3},{3,2},{4,5},{5,4},{6,7},{7,6},{8,9},{9,8},{10,11... | collective-permute-start | bytes 1769480 | tf_op jit(solution)/shard_map/ppermute | solution.py:23
  96.4 9.9 %copy-start.2 = (bf16[4,8,2,256]{3,2,1,0:T(2,128)(2,1)S(1)}, bf16[4,8,2,256]{3,2,1,0:T(2,128)(2,1)}, u32[]{:S(2)}) copy-start(bf16[4,8,2,256]{3,2,1,0:T(2,128)(2,1)} %param.12) | copy-start | bytes 98308
  96.4 2.1 %collective-permute-start.22 = (bf16[1024,128]{1,0:T(8,128)(2,1)S(1)}, bf16[1024,128]{1,0:T(8,128)(2,1)S(1)}, u32[]{:S(2)}, u32[]{:S(2)}) collective-permute-start(bf16[1024,128]{1,0:T(8,128)(2,1)S(1)} %get-tuple-element.157), channel_id=1, source_target_pairs={{0,1},{1,0},{2,3},{3,2},{4,5},{5,4},{6,7},{7,6},{8,9},{9,8},{10,11... | collective-permute-start | bytes 786440 | tf_op jit(solution)/shard_map/ppermute | solution.py:23
  106.3 2.0 %collective-permute-start.25 = (bf16[1152,256]{1,0:T(8,128)(2,1)S(1)}, bf16[1152,256]{1,0:T(8,128)(2,1)S(1)}, u32[]{:S(2)}, u32[]{:S(2)}) collective-permute-start(bf16[1152,256]{1,0:T(8,128)(2,1)S(1)} %collective-permute-done.24.refs_0_), channel_id=1, source_target_pairs={{0,1},{1,0},{2,3},{3,2},{4,5},{5,4},{6,7},{7,6},{8,9},{9,8},{10,11... | collective-permute-start | bytes 1769480 | tf_op jit(solution)/shard_map/ppermute | solution.py:23
  110.0 1.6 %collective-permute-start.26 = (bf16[1024,128]{1,0:T(8,128)(2,1)S(1)}, bf16[1024,128]{1,0:T(8,128)(2,1)S(1)}, u32[]{:S(2)}, u32[]{:S(2)}) collective-permute-start(bf16[1024,128]{1,0:T(8,128)(2,1)S(1)} %get-tuple-element.155), channel_id=1, source_target_pairs={{0,1},{1,0},{2,3},{3,2},{4,5},{5,4},{6,7},{7,6},{8,9},{9,8},{10,11... | collective-permute-start | bytes 786440 | tf_op jit(solution)/shard_map/ppermute | solution.py:23
  113.4 7.0 %collective-permute-start.27 = (bf16[272,128]{1,0:T(8,128)(2,1)S(1)}, bf16[272,128]{1,0:T(8,128)(2,1)S(1)}, u32[]{:S(2)}, u32[]{:S(2)}) collective-permute-start(bf16[272,128]{1,0:T(8,128)(2,1)S(1)} %get-tuple-element.135), channel_id=1, source_target_pairs={{0,8},{8,0},{16,24},{24,16},{1,9},{9,1},{17,25},{25,17},{2,10},{10... | collective-permute-start | bytes 208904 | tf_op jit(solution)/shard_map/ppermute | solution.py:32
  113.5 8.9 %collective-permute-start.28 = (bf16[272,128]{1,0:T(8,128)(2,1)S(1)}, bf16[272,128]{1,0:T(8,128)(2,1)S(1)}, u32[]{:S(2)}, u32[]{:S(2)}) collective-permute-start(bf16[272,128]{1,0:T(8,128)(2,1)S(1)} %get-tuple-element.136), channel_id=1, source_target_pairs={{0,16},{8,24},{16,0},{24,8},{1,17},{9,25},{17,1},{25,9},{2,18},{10... | collective-permute-start | bytes 208904 | tf_op jit(solution)/shard_map/ppermute | solution.py:32
  115.7 6.7 %collective-permute-start.29 = (bf16[272,128]{1,0:T(8,128)(2,1)S(1)}, bf16[272,128]{1,0:T(8,128)(2,1)S(1)}, u32[]{:S(2)}, u32[]{:S(2)}) collective-permute-start(bf16[272,128]{1,0:T(8,128)(2,1)S(1)} %get-tuple-element.137), channel_id=1, source_target_pairs={{0,24},{8,16},{16,8},{24,0},{1,25},{9,17},{17,9},{25,1},{2,26},{10... | collective-permute-start | bytes 208904 | tf_op jit(solution)/shard_map/ppermute | solution.py:32
  122.8 1.3 %collective-permute-start.30 = (bf16[32,1024]{1,0:T(8,128)(2,1)S(1)}, bf16[32,1024]{1,0:T(8,128)(2,1)S(1)}, u32[]{:S(2)}, u32[]{:S(2)}) collective-permute-start(bf16[32,1024]{1,0:T(8,128)(2,1)S(1)} %finish.1), channel_id=1, source_target_pairs={{0,1},{1,0},{2,3},{3,2},{4,5},{5,4},{6,7},{7,6},{8,9},{9,8},{10,11... | collective-permute-start | bytes 196616 | tf_op jit(solution)/shard_map/ppermute | solution.py:23

commit v10 on v9

--- a/solution.py
+++ b/solution.py
@@ -278,23 +278,22 @@
     return out
 
 
-def weigh_kernel(slots, parts, probs, *refs):
-    values, stats, outs = refs[:parts], refs[parts : parts + slots], refs[parts + slots :]
-    tokens, width = values[0].shape
-    rows = probs.shape[1]
-    summed = sum(
-        jnp.dot(
-            probs[0, :, p * tokens : (p + 1) * tokens],
-            values[p][...],
-            preferred_element_type=jnp.float32,
-        )
-        for p in range(parts)
-    ).astype(jnp.bfloat16)
+def weigh_own_kernel(probs, values, out):
+    out[0] = jnp.dot(probs[0], values[...], preferred_element_type=jnp.float32)
+
+
+def weigh_kernel(slots, parts, own, *refs):
+    probs, values = refs[:parts], refs[parts : 2 * parts]
+    stats, outs = refs[2 * parts : 2 * parts + slots], refs[2 * parts + slots :]
+    rows, width = own.shape[1:]
+    summed = own[0]
+    for p in range(parts):
+        summed += jnp.dot(probs[p][0], values[p][...], preferred_element_type=jnp.float32)
     for slot in range(slots):
 
         @pl.when(pl.program_id(0) == slot)
         def _(slot=slot):
-            outs[slot][0:rows, :] = summed
+            outs[slot][0:rows, :] = summed.astype(jnp.bfloat16)
             lines = []
             for third in thirds(stats[slot][...]):
                 third = third.astype(jnp.float32)
@@ -311,24 +310,44 @@
 def weigh(probs, values, stats):
     slots, rows, _ = probs.shape
     tokens, width = values[0].shape
-    parts = len(values)
+    parts = len(values) - 1
     total_rows = packed_rows(rows, width)
+    flops = 2 * slots * rows * width * tokens
+
+    def probs_spec(p):
+        return pl.BlockSpec((1, rows, tokens), lambda k, p=p: (k, 0, p))
+
+    values_spec = pl.BlockSpec((tokens, width), lambda k: (0, 0))
+    own_spec = pl.BlockSpec((1, rows, width), lambda k: (k, 0, 0))
+    own = pl.pallas_call(
+        weigh_own_kernel,
+        out_shape=jax.ShapeDtypeStruct((slots, rows, width), jnp.float32),
+        grid=(slots,),
+        in_specs=[probs_spec(0), values_spec],
+        out_specs=own_spec,
+        compiler_params=pltpu.CompilerParams(vmem_limit_bytes=16 * 2**20),
+        cost_estimate=pl.CostEstimate(
+            flops=flops, bytes_accessed=2 * slots * rows * tokens, transcendentals=0
+        ),
+        name="weigh_own",
+    )(probs, values[0])
     return pl.pallas_call(
         functools.partial(weigh_kernel, slots, parts),
         out_shape=[jax.ShapeDtypeStruct((total_rows, width), jnp.bfloat16)] * slots,
         grid=(slots,),
-        in_specs=[pl.BlockSpec((1, rows, parts * tokens), lambda k: (k, 0, 0))]
-        + [pl.BlockSpec((tokens, width), lambda k: (0, 0))] * parts
+        in_specs=[own_spec]
+        + [probs_spec(p + 1) for p in range(parts)]
+        + [values_spec] * parts
         + [pl.BlockSpec((2, rows), lambda k: (0, 0))] * slots,
         out_specs=[pl.BlockSpec((total_rows, width), lambda k: (0, 0))] * slots,
         compiler_params=pltpu.CompilerParams(vmem_limit_bytes=16 * 2**20),
         cost_estimate=pl.CostEstimate(
-            flops=2 * slots * rows * width * parts * tokens,
-            bytes_accessed=2 * slots * rows * parts * tokens,
+            flops=flops * parts,
+            bytes_accessed=2 * slots * rows * tokens * parts,
             transcendentals=0,
         ),
         name="weigh",
-    )(probs, *values, *stats)
+    )(own, *([probs] * parts), *values[1:], *stats)
 
 
 def fresh_kernel(scale, query, smooth, new_keys, new_values, group_scale, summed, highest, total):
@@ -456,7 +475,19 @@
 
 
 def smooth_of(top):
-    top = functools.reduce(jnp.maximum, from_groups(top))
+    groups, owners = lax.axis_size("seq"), lax.axis_size("rep")
+    if groups != LINE:
+        return jnp.sqrt(lax.pmax(top, "seq") + EPSILON)
+    partners = list(range(1, groups))
+    found = [top]
+    for first in range(0, len(partners), owners):
+        pairs = [
+            (group * owners + owner, partner(group, k, groups) * owners + owner)
+            for owner, k in enumerate(partners[first : first + owners])
+            for group in range(groups)
+        ]
+        found.append(lax.ppermute(top, ("seq", "rep"), pairs))
+    top = functools.reduce(jnp.maximum, from_owners(functools.reduce(jnp.maximum, found)))
     return jnp.sqrt(top + EPSILON)
 
 

time: 125 us -> 131 us (1.048)
  starting transfers between devices: 31.9 us -> 36.7 us
    ppermute x10, waiting for transfers between devices: 34.8 us -> 42.8 us  [send(): return lax.ppermute(x, 'seq', line_pairs(hop, parity, groups))]
    ppermute x6 -> x3, waiting for transfers between devices: 8.79 us -> 2.08 us  [swapped(): return lax.ppermute(x, axis, [(i, partner(i, k, n)) for i in range(n)])]
    ppermute x14 -> x15, starting transfers between devices: 2.58 us -> 7.72 us  [shifted(): return lax.ppermute(x, axis, [(i, (i + k) % n) for i in range(n)])]
    ppermute x0 -> x2, starting transfers between devices: none -> 4.53 us  [smooth_of(): found.append(lax.ppermute(top, ('seq', 'rep'), pairs))]
    ppermute x6 -> x3, starting transfers between devices: 8.83 us -> 4.44 us  [swapped(): return lax.ppermute(x, axis, [(i, partner(i, k, n)) for i in range(n)])]
    ppermute x14 -> x15, waiting for transfers between devices: 4.4 us -> 2.3 us  [shifted(): return lax.ppermute(x, axis, [(i, (i + k) % n) for i in range(n)])]
    pallas_call x0 -> x1, Pallas kernels: none -> 1.34 us  [weigh(): pl.pallas_call(weigh_own_kernel, out_shape=jax.ShapeDtypeStruct((slots, r...]
  transfers between devices with their start and end apart: 31 -> 31, of which waited for: 12 -> 11; matrix products, arithmetic and copies ran while one was open for 4% -> 4% of each run, Pallas kernels for 26% -> 25%
where the time goes in v10:
time: 131 us; the launch traced here: 130 us
  waiting for transfers between devices  47.2 us (36%)
  Pallas kernels  36.8 us (28%)
  starting transfers between devices  36.7 us (28%)
  other arithmetic  5.51 us (4%)
  local copies, waits for them, and re-layouts  2.16 us (2%)
    ppermute x10, waiting for transfers between devices, send(): return lax.ppermute(x, 'seq', line_pairs(hop, parity, groups))  42.8 us
    pallas_call x16, Pallas kernels, project(): pl.pallas_call(functools.partial(project_kernel, hops, back, groups, owne...  22 us
    ppermute x10, starting transfers between devices, send(): return lax.ppermute(x, 'seq', line_pairs(hop, parity, groups))  15.8 us
    ppermute x15, starting transfers between devices, shifted(): return lax.ppermute(x, axis, [(i, (i + k) % n) for i in range(n)])  7.72 us
    pallas_call x1, Pallas kernels, load(): pl.pallas_call(functools.partial(load_kernel, owners), out_shape=(jax.Sha...  6.57 us
    pallas_call x1, Pallas kernels, score(): pl.pallas_call(functools.partial(score_kernel, slots, parts, steps, scale...  4.73 us
    ppermute x2, starting transfers between devices, smooth_of(): found.append(lax.ppermute(top, ('seq', 'rep'), pairs))  4.53 us
    ppermute x3, starting transfers between devices, swapped(): return lax.ppermute(x, axis, [(i, partner(i, k, n)) for i in range(n)])  4.44 us
  transfers between devices with their start and end apart: 31, of which 11 were waited for; matrix products, arithmetic and copies ran while one was open for 4% of the time, Pallas kernels for 25%

profile of v10, /device:TPU:0, one launch (start us, length us, event | category | flops | bytes accessed | tf_op | source)
XLA Modules:
  0.0 130.1 jit_solution(10788385260944201372)
XLA Ops:
  0.6 3.1 %collective-permute-start = (bf16[1024,256]{1,0:T(8,128)(2,1)}, bf16[1024,256]{1,0:T(8,128)(2,1)S(1)}, u32[]{:S(2)}, u32[]{:S(2)}) collective-permute-start(bf16[1024,256]{1,0:T(8,128)(2,1)} %refs_0_), channel_id=1, source_target_pairs={{0,8},{8,0},{16,24},{24,16},{1,9},{9,1},{17,25},{25,17},{2,10},{10... | collective-permute-start | bytes 1572872 | tf_op jit(solution)/shard_map/ppermute | solution.py:510
  3.7 0.7 collective-permute-start.1
  4.5 0.5 collective-permute-start.7
  5.0 0.9 select_bitcast_fusion.query
  6.0 1.0 copy-done
  7.1 1.0 copy-done.1
  8.1 6.6 %load.1 = (bf16[1024,8192]{1,0:T(8,128)(2,1)S(1)}, f32[1024,256]{1,0:T(8,128)S(1)}, f32[1024,256]{1,0:T(8,128)S(1)}) custom-call(s32[2]{0:T(128)S(1)} %pad_add_fusion.place, bf16[1024,8192]{1,0:T(8,128)(2,1)} %hidden.1, bf16[1024,256]{1,0:T(8,128)(2,1)S(1)} %copy-done.1, bf16[1152,256]{1,0:T(8,128)(2,1)S(1)} %pack.1.refs_1_), custom_call_target="tpu_custom_call" | custom-call | flops 1073741824 | bytes 16777216 | tf_op jit(solution)/shard_map/load/pallas_call | solution.py:114
  14.7 1.2 collective-permute-done.refs_0_
  15.9 0.5 collective-permute-start.5
  16.4 4.8 %collective-permute-start.3 = (bf16[1152,256]{1,0:T(8,128)(2,1)S(1)}, bf16[1152,256]{1,0:T(8,128)(2,1)S(1)}, u32[]{:S(2)}, u32[]{:S(2)}) collective-permute-start(bf16[1152,256]{1,0:T(8,128)(2,1)S(1)} %pack.1.refs_1_), channel_id=1, source_target_pairs={{0,8},{8,0},{16,24},{24,16},{1,9},{9,1},{17,25},{25,17},{2,10},{10... | collective-permute-start | bytes 1769480 | tf_op jit(solution)/shard_map/ppermute | solution.py:510
  21.2 0.7 collective-permute-start.2
  21.9 1.4 %project.19.refs_1_ = f32[1024,256]{1,0:T(8,128)S(1)} custom-call(s32[2]{0:T(128)S(1)} %pad_add_fusion.place, bf16[1024,8192]{1,0:T(8,128)(2,1)S(1)} %get-tuple-element.86.left, bf16[1024,256]{1,0:T(8,128)(2,1)S(1)} %collective-permute-done.7.refs_0_, f32[1024,256]{1,0:T(8,128)S(1)} %get-tuple-element.89.refs_1_), custom_call_target="tpu_custom_call", output_to_operand_aliasing={{}: (3, {})} | custom-call | flops 536870912 | bytes 4718592 | tf_op jit(solution)/shard_map/project/pallas_call | solution.py:170
  23.3 1.4 %project.16.refs_2_ = f32[1024,256]{1,0:T(8,128)S(1)} custom-call(s32[2]{0:T(128)S(1)} %pad_add_fusion.place, bf16[1024,8192]{1,0:T(8,128)(2,1)S(1)} %get-tuple-element.86.left, bf16[1024,256]{1,0:T(8,128)(2,1)S(1)} %collective-permute-done.6.refs_0_, f32[1024,256]{1,0:T(8,128)S(1)} %get-tuple-element.88.refs_1_), custom_call_target="tpu_custom_call", output_to_operand_aliasing={{}: (3, {})} | custom-call | flops 536870912 | bytes 4718592 | tf_op jit(solution)/shard_map/project/pallas_call | solution.py:170
  24.8 1.5 %project.17.refs_2_ = f32[1024,256]{1,0:T(8,128)S(1)} custom-call(s32[2]{0:T(128)S(1)} %pad_add_fusion.place, bf16[1024,8192]{1,0:T(8,128)(2,1)S(1)} %get-tuple-element.86.left, bf16[1024,256]{1,0:T(8,128)(2,1)S(1)} %collective-permute-done.refs_0_, bf16[1024,256]{1,0:T(8,128)(2,1)S(1)} %collective-permute-done.1.refs_1_, ...), custom_call_target="tpu_custom_call", output_to_operand_aliasing={{}: (4, {})} | custom-call | flops 1073741824 | bytes 7340032 | tf_op jit(solution)/shard_map/project/pallas_call | solution.py:170
  26.3 1.5 %project.18.refs_1_ = f32[1024,256]{1,0:T(8,128)S(1)} custom-call(s32[2]{0:T(128)S(1)} %pad_add_fusion.place, bf16[1024,8192]{1,0:T(8,128)(2,1)S(1)} %get-tuple-element.86.left, bf16[1024,256]{1,0:T(8,128)(2,1)S(1)} %collective-permute-done.4.refs_0_, bf16[1024,256]{1,0:T(8,128)(2,1)S(1)} %collective-permute-done.5.refs_1_, ...), custom_call_target="tpu_custom_call", output_to_operand_aliasing={{}: (4, {})} | custom-call | flops 1073741824 | bytes 7340032 | tf_op jit(solution)/shard_map/project/pallas_call | solution.py:170
  27.8 6.8 %collective-permute-done.3.refs_0_ = bf16[1152,256]{1,0:T(8,128)(2,1)S(1)} collective-permute-done((bf16[1152,256]{1,0:T(8,128)(2,1)S(1)}, bf16[1152,256]{1,0:T(8,128)(2,1)S(1)}, u32[]{:S(2)}, u32[]{:S(2)}) %collective-permute-start.3) | collective-permute-done | bytes 589856 | tf_op jit(solution)/shard_map/ppermute | solution.py:510
  34.7 1.3 collective-permute-start.9
  35.9 0.7 collective-permute-start.8
  36.7 1.4 %project.20.refs_1_ = f32[1024,256]{1,0:T(8,128)S(1)} custom-call(s32[2]{0:T(128)S(1)} %pad_add_fusion.place, bf16[1024,8192]{1,0:T(8,128)(2,1)S(1)} %get-tuple-element.86.left, bf16[1152,256]{1,0:T(8,128)(2,1)S(1)} %collective-permute-done.3.refs_0_, f32[1024,256]{1,0:T(8,128)S(1)} %project.19.refs_1_), custom_call_target="tpu_custom_call", output_to_operand_aliasing={{}: (3, {})} | custom-call | flops 536870912 | bytes 4718592 | tf_op jit(solution)/shard_map/project/pallas_call | solution.py:170
  38.1 1.4 %project.21.refs_1_ = f32[1024,256]{1,0:T(8,128)S(1)} custom-call(s32[2]{0:T(128)S(1)} %pad_add_fusion.place, bf16[1024,8192]{1,0:T(8,128)(2,1)S(1)} %get-tuple-element.86.left, bf16[1152,256]{1,0:T(8,128)(2,1)S(1)} %collective-permute-done.10.refs_0_, f32[1024,256]{1,0:T(8,128)S(1)} %project.20.refs_1_), custom_call_target="tpu_custom_call", output_to_operand_aliasing={{}: (3, {})} | custom-call | flops 536870912 | bytes 4718592 | tf_op jit(solution)/shard_map/project/pallas_call | solution.py:170
  39.6 11.3 %collective-permute-done.9 = bf16[1024,256]{1,0:T(8,128)(2,1)S(1)} collective-permute-done((bf16[1024,256]{1,0:T(8,128)(2,1)S(1)}, bf16[1024,256]{1,0:T(8,128)(2,1)S(1)}, u32[]{:S(2)}, u32[]{:S(2)}) %collective-permute-start.9) | collective-permute-done | bytes 524320 | tf_op jit(solution)/shard_map/ppermute | solution.py:510
  51.1 1.4 %project.22.refs_1_ = f32[1024,256]{1,0:T(8,128)S(1)} custom-call(s32[2]{0:T(128)S(1)} %pad_add_fusion.place, bf16[1024,8192]{1,0:T(8,128)(2,1)S(1)} %get-tuple-element.86.left, bf16[1024,256]{1,0:T(8,128)(2,1)S(1)} %add.74.refs_0_, f32[1024,256]{1,0:T(8,128)S(1)} %project.18.refs_1_), custom_call_target="tpu_custom_call", output_to_operand_aliasing={{}: (3, {})} | custom-call | flops 536870912 | bytes 4718592 | tf_op jit(solution)/shard_map/project/pallas_call | solution.py:170
  52.6 0.4 collective-permute-done.11.refs_0_
  53.0 1.4 %project.23.refs_1_ = f32[1024,256]{1,0:T(8,128)S(1)} custom-call(s32[2]{0:T(128)S(1)} %pad_add_fusion.place, bf16[1024,8192]{1,0:T(8,128)(2,1)S(1)} %get-tuple-element.86.left, bf16[1024,256]{1,0:T(8,128)(2,1)S(1)} %collective-permute-done.11.refs_0_, f32[1024,256]{1,0:T(8,128)S(1)} %project.22.refs_1_), custom_call_target="tpu_custom_call", output_to_operand_aliasing={{}: (3, {})} | custom-call | flops 536870912 | bytes 4718592 | tf_op jit(solution)/shard_map/project/pallas_call | solution.py:170
  54.5 0.2 collective-permute-start.15
  54.7 1.3 collective-permute-start.14
  56.1 0.6 convert_reduce_fusion
  56.7 0.7 project.24.refs_1_
  57.5 0.7 project.25.refs_1_
  58.2 12.5 %collective-permute-done.14.refs_0_ = bf16[1024,256]{1,0:T(8,128)(2,1)S(1)} collective-permute-done((bf16[1024,256]{1,0:T(8,128)(2,1)S(1)}, bf16[1024,256]{1,0:T(8,128)(2,1)S(1)}, u32[]{:S(2)}, u32[]{:S(2)}) %collective-permute-start.14) | collective-permute-done | bytes 524320 | tf_op jit(solution)/shard_map/ppermute | solution.py:510
  70.8 0.2 fusion.2
  71.0 0.2 fusion.1.count
  71.2 1.6 %project.26.refs_1_ = f32[1024,256]{1,0:T(8,128)S(1)} custom-call(s32[2]{0:T(128)S(1)} %pad_add_fusion.place, bf16[1024,8192]{1,0:T(8,128)(2,1)S(1)} %get-tuple-element.86.left, bf16[1024,256]{1,0:T(8,128)(2,1)S(1)} %collective-permute-done.14.refs_0_, f32[1024,256]{1,0:T(8,128)S(1)} %project.23.refs_1_), custom_call_target="tpu_custom_call", output_to_operand_aliasing={{}: (3, {})} | custom-call | flops 536870912 | bytes 4718592 | tf_op jit(solution)/shard_map/project/pallas_call | solution.py:170
  72.9 1.4 %project.27 = f32[1024,256]{1,0:T(8,128)S(1)} custom-call(s32[2]{0:T(128)S(1)} %pad_add_fusion.place, bf16[1024,8192]{1,0:T(8,128)(2,1)S(1)} %get-tuple-element.86.left, bf16[1024,256]{1,0:T(8,128)(2,1)S(1)} %collective-permute-done.16.refs_0_, f32[1024,256]{1,0:T(8,128)S(1)} %project.26.refs_1_), custom_call_target="tpu_custom_call", output_to_operand_aliasing={{}: (3, {})} | custom-call | flops 536870912 | bytes 4718592 | tf_op jit(solution)/shard_map/project/pallas_call | solution.py:170
  74.4 0.6 collective-permute-start.17
  75.0 0.7 collective-permute-start.13
  75.8 1.2 collective-permute-start.18
  77.0 3.3 %collective-permute-start.19 = (f32[1,256]{1,0:T(1,128)S(1)}, f32[1,256]{1,0:T(1,128)S(1)}, u32[]{:S(2)}, u32[]{:S(2)}) collective-permute-start(f32[1,256]{1,0:T(1,128)S(1)} %max.36), channel_id=1, source_target_pairs={{0,24},{8,16},{16,8},{24,0},{2,26},{10,18},{18,10},{26,2},{4,28},{... | collective-permute-start | bytes 3080 | tf_op jit(solution)/shard_map/ppermute | solution.py:489
  80.3 4.3 %collective-permute-start.21 = (bf16[128,256]{1,0:T(8,128)(2,1)S(1)}, bf16[128,256]{1,0:T(8,128)(2,1)S(1)}, u32[]{:S(2)}, u32[]{:S(2)}) collective-permute-start(bf16[128,256]{1,0:T(8,128)(2,1)S(1)} %slice.79), channel_id=1, source_target_pairs={{0,24},{24,0},{1,25},{25,1},{2,26},{26,2},{3,27},{27,3},{4,28},{28... | collective-permute-start | bytes 196616 | tf_op jit(solution)/shard_map/ppermute | solution.py:539
  84.6 1.3 collective-permute-start.12
  86.0 4.9 %collective-permute-start.20 = (f32[1,256]{1,0:T(1,128)S(1)}, f32[1,256]{1,0:T(1,128)S(1)}, u32[]{:S(2)}, u32[]{:S(2)}) collective-permute-start(f32[1,256]{1,0:T(1,128)S(1)} %maximum_maximum_fusion), channel_id=1, source_target_pairs={{0,1},{1,0},{2,3},{3,2},{4,5},{5,4},{6,7},{7,6},{8,9},{9,8},{10,11... | collective-permute-start | bytes 3080 | tf_op jit(solution)/shard_map/ppermute | solution.py:23
  90.9 1.3 collective-permute-start.24
  92.2 10.5 %collective-permute-done.12 = bf16[1152,256]{1,0:T(8,128)(2,1)S(1)} collective-permute-done((bf16[1152,256]{1,0:T(8,128)(2,1)S(1)}, bf16[1152,256]{1,0:T(8,128)(2,1)S(1)}, u32[]{:S(2)}, u32[]{:S(2)}) %collective-permute-start.12) | collective-permute-done | bytes 589856 | tf_op jit(solution)/shard_map/ppermute | solution.py:510
  102.7 0.1 add.86.refs_0_
  103.0 0.1 minimum_convert_fusion.1
  103.2 1.4 %project.28.refs_1_ = f32[1024,256]{1,0:T(8,128)S(1)} custom-call(s32[2]{0:T(128)S(1)} %pad_add_fusion.place, bf16[1024,8192]{1,0:T(8,128)(2,1)S(1)} %get-tuple-element.86.left, bf16[1152,256]{1,0:T(8,128)(2,1)S(1)} %add.86.refs_0_, f32[1024,256]{1,0:T(8,128)S(1)} %project.25.refs_1_), custom_call_target="tpu_custom_call", output_to_operand_aliasing={{}: (3, {})} | custom-call | flops 536870912 | bytes 4718592 | tf_op jit(solution)/shard_map/project/pallas_call | solution.py:170
  104.6 0.6 collective-permute-start.22
  105.3 1.5 %project.29.refs_1_ = f32[1024,256]{1,0:T(8,128)S(1)} custom-call(s32[2]{0:T(128)S(1)} %pad_add_fusion.place, bf16[1024,8192]{1,0:T(8,128)(2,1)S(1)} %get-tuple-element.86.left, bf16[1152,256]{1,0:T(8,128)(2,1)S(1)} %collective-permute-done.23.refs_0_, f32[1024,256]{1,0:T(8,128)S(1)} %project.28.refs_1_), custom_call_target="tpu_custom_call", output_to_operand_aliasing={{}: (3, {})} | custom-call | flops 536870912 | bytes 4718592 | tf_op jit(solution)/shard_map/project/pallas_call | solution.py:170
  106.7 4.7 %score.1 = (bf16[4,256,2048]{2,1,0:T(8,128)(2,1)S(1)}, f32[2,256]{1,0:T(2,128)S(1)}, f32[2,256]{1,0:T(2,128)S(1)}, f32[2,256]{1,0:T(2,128)S(1)}, f32[2,256]{1,0:T(2,128)S(1)}) custom-call(s32[4]{0:T(128)S(1)} %iota_xor_fusion.group, bf16[4,128,256]{2,1,0:T(8,128)(2,1)S(1)} %pad_maximum_fusion.query, f32[1,128]{1,0:T(1,128)S(1)} %broadcast_select_fusion.7.smooth, ...), custom_call_target="tpu_custom_call" | custom-call | flops 536870912 | bytes 4194304 | tf_op jit(solution)/shard_map/score/pallas_call | solution.py:241
  111.5 0.5 collective-permute-done.24.refs_0_
  112.0 1.4 %project.30.refs_1_ = f32[1024,256]{1,0:T(8,128)S(1)} custom-call(s32[2]{0:T(128)S(1)} %pad_add_fusion.place, bf16[1024,8192]{1,0:T(8,128)(2,1)S(1)} %get-tuple-element.86.left, bf16[1152,256]{1,0:T(8,128)(2,1)S(1)} %collective-permute-done.24.refs_0_, f32[1024,256]{1,0:T(8,128)S(1)} %project.29.refs_1_), custom_call_target="tpu_custom_call", output_to_operand_aliasing={{}: (3, {})} | custom-call | flops 536870912 | bytes 4718592 | tf_op jit(solution)/shard_map/project/pallas_call | solution.py:170
  113.4 0.5 collective-permute-done.25.refs_0_
  113.9 1.4 %project.31 = f32[1024,256]{1,0:T(8,128)S(1)} custom-call(s32[2]{0:T(128)S(1)} %pad_add_fusion.place, bf16[1024,8192]{1,0:T(8,128)(2,1)S(1)} %get-tuple-element.86.left, bf16[1152,256]{1,0:T(8,128)(2,1)S(1)} %collective-permute-done.25.refs_0_, f32[1024,256]{1,0:T(8,128)S(1)} %project.30.refs_1_), custom_call_target="tpu_custom_call", output_to_operand_aliasing={{}: (3, {})} | custom-call | flops 536870912 | bytes 4718592 | tf_op jit(solution)/shard_map/project/pallas_call | solution.py:170
  115.5 0.2 collective-permute-start.26
  115.8 1.3 %weigh_own.1.own = f32[4,256,128]{2,1,0:T(8,128)S(1)} custom-call(bf16[4,256,2048]{2,1,0:T(8,128)(2,1)S(1)} %get-tuple-element.118.probs.refs_0_, bf16[1024,128]{1,0:T(8,128)(2,1)S(1)} %get-tuple-element.156.values), custom_call_target="tpu_custom_call" | custom-call | flops 268435456 | bytes 2097152 | tf_op jit(solution)/shard_map/weigh_own/pallas_call | solution.py:322
  117.1 1.4 %weigh.1 = (bf16[272,128]{1,0:T(8,128)(2,1)S(1)}, bf16[272,128]{1,0:T(8,128)(2,1)S(1)}, bf16[272,128]{1,0:T(8,128)(2,1)S(1)}, bf16[272,128]{1,0:T(8,128)(2,1)S(1)}) custom-call(f32[4,256,128]{2,1,0:T(8,128)S(1)} %weigh_own.1.own, bf16[4,256,2048]{2,1,0:T(8,128)(2,1)S(1)} %get-tuple-element.118.probs.refs_0_, ...), custom_call_target="tpu_custom_call" | custom-call | flops 268435456 | bytes 2097152 | tf_op jit(solution)/shard_map/weigh/pallas_call | solution.py:334
  118.7 1.7 %collective-permute-start.28 = (bf16[272,128]{1,0:T(8,128)(2,1)S(1)}, bf16[272,128]{1,0:T(8,128)(2,1)S(1)}, u32[]{:S(2)}, u32[]{:S(2)}) collective-permute-start(bf16[272,128]{1,0:T(8,128)(2,1)S(1)} %get-tuple-element.136), channel_id=1, source_target_pairs={{0,16},{8,24},{16,0},{24,8},{1,17},{9,25},{17,1},{25,9},{2,18},{10... | collective-permute-start | bytes 208904 | tf_op jit(solution)/shard_map/ppermute | solution.py:32
  120.4 2.6 %collective-permute-start.29 = (bf16[272,128]{1,0:T(8,128)(2,1)S(1)}, bf16[272,128]{1,0:T(8,128)(2,1)S(1)}, u32[]{:S(2)}, u32[]{:S(2)}) collective-permute-start(bf16[272,128]{1,0:T(8,128)(2,1)S(1)} %get-tuple-element.137), channel_id=1, source_target_pairs={{0,24},{8,16},{16,8},{24,0},{1,25},{9,17},{17,9},{25,1},{2,26},{10... | collective-permute-start | bytes 208904 | tf_op jit(solution)/shard_map/ppermute | solution.py:32
  123.1 2.3 %broadcast_select_fusion = bf16[1024,2,256]{2,1,0:T(2,128)(2,1)} fusion(pred[2]{0:T(512)(128)(4,1)S(1)} %iota_compare_fusion.5, bf16[1024,256]{1,0:T(8,128)(2,1)S(1)} %minimum_convert_fusion, bf16[1024,256]{1,0:T(8,128)(2,1)S(1)} %minimum_convert_fusion.1), kind=kLoop, calls=%fused_computation.3 | loop fusion | flops 524288 | bytes 2097154 | tf_op jit(solution)/shard_map/jit(_where)/select_n | solution.py:647
  125.4 0.2 fresh.1
  125.6 2.1 %collective-permute-done.28.refs_2_ = bf16[272,128]{1,0:T(8,128)(2,1)S(1)} collective-permute-done((bf16[272,128]{1,0:T(8,128)(2,1)S(1)}, bf16[272,128]{1,0:T(8,128)(2,1)S(1)}, u32[]{:S(2)}, u32[]{:S(2)}) %collective-permute-start.28) | collective-permute-done | bytes 69664 | tf_op jit(solution)/shard_map/ppermute | solution.py:32
  127.7 0.4 finish.1
  128.2 1.2 collective-permute-done.30
  129.5 0.7 maximum_bitcast_fusion
  (72 shorter events, 1.5 us)
Async XLA Ops:
  0.6 15.3 %collective-permute-start = (bf16[1024,256]{1,0:T(8,128)(2,1)}, bf16[1024,256]{1,0:T(8,128)(2,1)S(1)}, u32[]{:S(2)}, u32[]{:S(2)}) collective-permute-start(bf16[1024,256]{1,0:T(8,128)(2,1)} %refs_0_), channel_id=1, source_target_pairs={{0,8},{8,0},{16,24},{24,16},{1,9},{9,1},{17,25},{25,17},{2,10},{10... | collective-permute-start | bytes 1572872 | tf_op jit(solution)/shard_map/ppermute | solution.py:510
  3.7 12.1 %collective-permute-start.1 = (bf16[1024,256]{1,0:T(8,128)(2,1)}, bf16[1024,256]{1,0:T(8,128)(2,1)S(1)}, u32[]{:S(2)}, u32[]{:S(2)}) collective-permute-start(bf16[1024,256]{1,0:T(8,128)(2,1)} %refs_0_), channel_id=1, source_target_pairs={{8,16},{16,8},{9,17},{17,9},{10,18},{18,10},{11,19},{19,11},{12,20... | collective-permute-start | bytes 1572872 | tf_op jit(solution)/shard_map/ppermute | solution.py:510
  4.4 18.9 %collective-permute-start.6 = (bf16[1024,256]{1,0:T(8,128)(2,1)}, bf16[1024,256]{1,0:T(8,128)(2,1)S(1)}, u32[]{:S(2)}, u32[]{:S(2)}) collective-permute-start(bf16[1024,256]{1,0:T(8,128)(2,1)} %refs_0_), channel_id=1, source_target_pairs={{0,1},{1,0},{2,3},{3,2},{4,5},{5,4},{6,7},{7,6},{8,9},{9,8},{10,11... | collective-permute-start | bytes 1572872 | tf_op jit(solution)/shard_map/ppermute | solution.py:23
  4.5 16.6 %collective-permute-start.7 = (bf16[1024,256]{1,0:T(8,128)(2,1)}, bf16[1024,256]{1,0:T(8,128)(2,1)S(1)}, u32[]{:S(2)}, u32[]{:S(2)}) collective-permute-start(bf16[1024,256]{1,0:T(8,128)(2,1)} %weight.1), channel_id=1, source_target_pairs={{0,1},{1,0},{2,3},{3,2},{4,5},{5,4},{6,7},{7,6},{8,9},{9,8},{10,11... | collective-permute-start | bytes 1572872 | tf_op jit(solution)/shard_map/ppermute | solution.py:23
  6.0 1.0 copy-start
  7.1 1.0 copy-start.1
  15.9 10.4 %collective-permute-start.4 = (bf16[1024,256]{1,0:T(8,128)(2,1)S(1)}, bf16[1024,256]{1,0:T(8,128)(2,1)S(1)}, u32[]{:S(2)}, u32[]{:S(2)}) collective-permute-start(bf16[1024,256]{1,0:T(8,128)(2,1)S(1)} %collective-permute-done.refs_0_), channel_id=1, source_target_pairs={{0,1},{1,0},{2,3},{3,2},{4,5},{5,4},{6,7},{7,6},{8,9},{9,8},{10,11... | collective-permute-start | bytes 1572872 | tf_op jit(solution)/shard_map/ppermute | solution.py:23
  15.9 10.4 %collective-permute-start.5 = (bf16[1024,256]{1,0:T(8,128)(2,1)S(1)}, bf16[1024,256]{1,0:T(8,128)(2,1)S(1)}, u32[]{:S(2)}, u32[]{:S(2)}) collective-permute-start(bf16[1024,256]{1,0:T(8,128)(2,1)S(1)} %collective-permute-done.1.refs_1_), channel_id=1, source_target_pairs={{0,1},{1,0},{2,3},{3,2},{4,5},{5,4},{6,7},{7,6},{8,9},{9,8},{10,11... | collective-permute-start | bytes 1572872 | tf_op jit(solution)/shard_map/ppermute | solution.py:23
  16.4 18.2 %collective-permute-start.3 = (bf16[1152,256]{1,0:T(8,128)(2,1)S(1)}, bf16[1152,256]{1,0:T(8,128)(2,1)S(1)}, u32[]{:S(2)}, u32[]{:S(2)}) collective-permute-start(bf16[1152,256]{1,0:T(8,128)(2,1)S(1)} %pack.1.refs_1_), channel_id=1, source_target_pairs={{0,8},{8,0},{16,24},{24,16},{1,9},{9,1},{17,25},{25,17},{2,10},{10... | collective-permute-start | bytes 1769480 | tf_op jit(solution)/shard_map/ppermute | solution.py:510
  21.2 13.5 %collective-permute-start.2 = (bf16[1024,256]{1,0:T(8,128)(2,1)S(1)}, bf16[1024,256]{1,0:T(8,128)(2,1)S(1)}, u32[]{:S(2)}, u32[]{:S(2)}) collective-permute-start(bf16[1024,256]{1,0:T(8,128)(2,1)S(1)} %collective-permute-done.refs_0_), channel_id=1, source_target_pairs={{8,16},{16,8},{9,17},{17,9},{10,18},{18,10},{11,19},{19,11},{12,20... | collective-permute-start | bytes 1572872 | tf_op jit(solution)/shard_map/ppermute | solution.py:510
  27.8 23.3 %copy-start.6 = (s32[32]{0:T(128)S(1)}, s32[32]{0:T(128)}, u32[]{:S(2)}) copy-start(s32[32]{0:T(128)} %param.15) | copy-start | bytes 388
  34.7 3.5 %collective-permute-start.10 = (bf16[1152,256]{1,0:T(8,128)(2,1)S(1)}, bf16[1152,256]{1,0:T(8,128)(2,1)S(1)}, u32[]{:S(2)}, u32[]{:S(2)}) collective-permute-start(bf16[1152,256]{1,0:T(8,128)(2,1)S(1)} %collective-permute-done.3.refs_0_), channel_id=1, source_target_pairs={{0,1},{1,0},{2,3},{3,2},{4,5},{5,4},{6,7},{7,6},{8,9},{9,8},{10,11... | collective-permute-start | bytes 1769480 | tf_op jit(solution)/shard_map/ppermute | solution.py:23
  34.7 16.2 %collective-permute-start.9 = (bf16[1024,256]{1,0:T(8,128)(2,1)S(1)}, bf16[1024,256]{1,0:T(8,128)(2,1)S(1)}, u32[]{:S(2)}, u32[]{:S(2)}) collective-permute-start(bf16[1024,256]{1,0:T(8,128)(2,1)S(1)} %collective-permute-done.1.refs_1_), channel_id=1, source_target_pairs={{8,0},{16,24},{9,1},{17,25},{10,2},{18,26},{11,3},{19,27},{12,4},{... | collective-permute-start | bytes 1572872 | tf_op jit(solution)/shard_map/ppermute | solution.py:510
  35.9 18.5 %collective-permute-start.8 = (bf16[1152,256]{1,0:T(8,128)(2,1)S(1)}, bf16[1152,256]{1,0:T(8,128)(2,1)S(1)}, u32[]{:S(2)}, u32[]{:S(2)}) collective-permute-start(bf16[1152,256]{1,0:T(8,128)(2,1)S(1)} %pack.1.refs_1_), channel_id=1, source_target_pairs={{8,16},{16,8},{9,17},{17,9},{10,18},{18,10},{11,19},{19,11},{12,20... | collective-permute-start | bytes 1769480 | tf_op jit(solution)/shard_map/ppermute | solution.py:510
  51.0 2.0 %collective-permute-start.11 = (bf16[1024,256]{1,0:T(8,128)(2,1)S(1)}, bf16[1024,256]{1,0:T(8,128)(2,1)S(1)}, u32[]{:S(2)}, u32[]{:S(2)}) collective-permute-start(bf16[1024,256]{1,0:T(8,128)(2,1)S(1)} %add.74.refs_0_), channel_id=1, source_target_pairs={{0,1},{1,0},{2,3},{3,2},{4,5},{5,4},{6,7},{7,6},{8,9},{9,8},{10,11... | collective-permute-start | bytes 1572872 | tf_op jit(solution)/shard_map/ppermute | solution.py:23
  51.1 5.0 %copy-start.3 = (s32[32,32]{1,0:T(8,128)S(1)}, s32[32,32]{1,0:T(8,128)}, u32[]{:S(2)}) copy-start(s32[32,32]{1,0:T(8,128)} %param.14) | copy-start | bytes 12292
  54.5 3.0 %collective-permute-start.15 = (bf16[1152,256]{1,0:T(8,128)(2,1)S(1)}, bf16[1152,256]{1,0:T(8,128)(2,1)S(1)}, u32[]{:S(2)}, u32[]{:S(2)}) collective-permute-start(bf16[1152,256]{1,0:T(8,128)(2,1)S(1)} %collective-permute-done.8.refs_0_), channel_id=1, source_target_pairs={{0,1},{1,0},{2,3},{3,2},{4,5},{5,4},{6,7},{7,6},{8,9},{9,8},{10,11... | collective-permute-start | bytes 1769480 | tf_op jit(solution)/shard_map/ppermute | solution.py:23
  54.7 16.1 %collective-permute-start.14 = (bf16[1024,256]{1,0:T(8,128)(2,1)S(1)}, bf16[1024,256]{1,0:T(8,128)(2,1)S(1)}, u32[]{:S(2)}, u32[]{:S(2)}) collective-permute-start(bf16[1024,256]{1,0:T(8,128)(2,1)S(1)} %collective-permute-done.2), channel_id=1, source_target_pairs={{8,0},{16,24},{9,1},{17,25},{10,2},{18,26},{11,3},{19,27},{12,4},{... | collective-permute-start | bytes 1572872 | tf_op jit(solution)/shard_map/ppermute | solution.py:510
  56.7 14.5 %copy-start.5 = (f32[2,256]{1,0:T(2,128)S(1)}, f32[2,256]{1,0:T(2,128)}, u32[]{:S(2)}) copy-start(f32[2,256]{1,0:T(2,128)} %param.11) | copy-start | bytes 6148
  70.7 2.1 %collective-permute-start.16 = (bf16[1024,256]{1,0:T(8,128)(2,1)S(1)}, bf16[1024,256]{1,0:T(8,128)(2,1)S(1)}, u32[]{:S(2)}, u32[]{:S(2)}) collective-permute-start(bf16[1024,256]{1,0:T(8,128)(2,1)S(1)} %collective-permute-done.14.refs_0_), channel_id=1, source_target_pairs={{0,1},{1,0},{2,3},{3,2},{4,5},{5,4},{6,7},{7,6},{8,9},{9,8},{10,11... | collective-permute-start | bytes 1572872 | tf_op jit(solution)/shard_map/ppermute | solution.py:23
  74.4 1.4 %collective-permute-start.17 = (f32[1,256]{1,0:T(1,128)S(1)}, f32[1,256]{1,0:T(1,128)S(1)}, u32[]{:S(2)}, u32[]{:S(2)}) collective-permute-start(f32[1,256]{1,0:T(1,128)S(1)} %bitcast.28), channel_id=1, source_target_pairs={{0,1},{1,0},{2,3},{3,2},{4,5},{5,4},{6,7},{7,6},{8,9},{9,8},{10,11... | collective-permute-start | bytes 3080 | tf_op jit(solution)/shard_map/ppermute | solution.py:23
  75.0 15.9 %collective-permute-start.13 = (bf16[1152,256]{1,0:T(8,128)(2,1)S(1)}, bf16[1152,256]{1,0:T(8,128)(2,1)S(1)}, u32[]{:S(2)}, u32[]{:S(2)}) collective-permute-start(bf16[1152,256]{1,0:T(8,128)(2,1)S(1)} %collective-permute-done.3.refs_0_), channel_id=1, source_target_pairs={{8,16},{16,8},{9,17},{17,9},{10,18},{18,10},{11,19},{19,11},{12,20... | collective-permute-start | bytes 1769480 | tf_op jit(solution)/shard_map/ppermute | solution.py:510
  75.8 10.2 %collective-permute-start.18 = (f32[1,256]{1,0:T(1,128)S(1)}, f32[1,256]{1,0:T(1,128)S(1)}, u32[]{:S(2)}, u32[]{:S(2)}) collective-permute-start(f32[1,256]{1,0:T(1,128)S(1)} %max.36), channel_id=1, source_target_pairs={{0,8},{8,0},{16,24},{24,16},{1,17},{9,25},{17,1},{25,9},{2,10},{10... | collective-permute-start | bytes 3080 | tf_op jit(solution)/shard_map/ppermute | solution.py:489
  77.0 9.0 %collective-permute-start.19 = (f32[1,256]{1,0:T(1,128)S(1)}, f32[1,256]{1,0:T(1,128)S(1)}, u32[]{:S(2)}, u32[]{:S(2)}) collective-permute-start(f32[1,256]{1,0:T(1,128)S(1)} %max.36), channel_id=1, source_target_pairs={{0,24},{8,16},{16,8},{24,0},{2,26},{10,18},{18,10},{26,2},{4,28},{... | collective-permute-start | bytes 3080 | tf_op jit(solution)/shard_map/ppermute | solution.py:489
  80.3 10.5 %collective-permute-start.21 = (bf16[128,256]{1,0:T(8,128)(2,1)S(1)}, bf16[128,256]{1,0:T(8,128)(2,1)S(1)}, u32[]{:S(2)}, u32[]{:S(2)}) collective-permute-start(bf16[128,256]{1,0:T(8,128)(2,1)S(1)} %slice.79), channel_id=1, source_target_pairs={{0,24},{24,0},{1,25},{25,1},{2,26},{26,2},{3,27},{27,3},{4,28},{28... | collective-permute-start | bytes 196616 | tf_op jit(solution)/shard_map/ppermute | solution.py:539
  84.6 18.1 %collective-permute-start.12 = (bf16[1152,256]{1,0:T(8,128)(2,1)S(1)}, bf16[1152,256]{1,0:T(8,128)(2,1)S(1)}, u32[]{:S(2)}, u32[]{:S(2)}) collective-permute-start(bf16[1152,256]{1,0:T(8,128)(2,1)S(1)} %collective-permute-done.8.refs_0_), channel_id=1, source_target_pairs={{8,0},{16,24},{9,1},{17,25},{10,2},{18,26},{11,3},{19,27},{12,4},{... | collective-permute-start | bytes 1769480 | tf_op jit(solution)/shard_map/ppermute | solution.py:510
  86.0 6.2 %collective-permute-start.20 = (f32[1,256]{1,0:T(1,128)S(1)}, f32[1,256]{1,0:T(1,128)S(1)}, u32[]{:S(2)}, u32[]{:S(2)}) collective-permute-start(f32[1,256]{1,0:T(1,128)S(1)} %maximum_maximum_fusion), channel_id=1, source_target_pairs={{0,1},{1,0},{2,3},{3,2},{4,5},{5,4},{6,7},{7,6},{8,9},{9,8},{10,11... | collective-permute-start | bytes 3080 | tf_op jit(solution)/shard_map/ppermute | solution.py:23
  90.9 21.1 %collective-permute-start.24 = (bf16[1152,256]{1,0:T(8,128)(2,1)S(1)}, bf16[1152,256]{1,0:T(8,128)(2,1)S(1)}, u32[]{:S(2)}, u32[]{:S(2)}) collective-permute-start(bf16[1152,256]{1,0:T(8,128)(2,1)S(1)} %collective-permute-done.13), channel_id=1, source_target_pairs={{8,0},{16,24},{9,1},{17,25},{10,2},{18,26},{11,3},{19,27},{12,4},{... | collective-permute-start | bytes 1769480 | tf_op jit(solution)/shard_map/ppermute | solution.py:510
  92.2 14.5 %copy-start.4 = (f32[1,256]{1,0:T(1,128)}, f32[1,256]{1,0:T(1,128)S(1)}, u32[]{:S(2)}) copy-start(f32[1,256]{1,0:T(1,128)S(1)} %add_sqrt_fusion) | copy-start | bytes 3076
  102.9 2.4 %collective-permute-start.23 = (bf16[1152,256]{1,0:T(8,128)(2,1)S(1)}, bf16[1152,256]{1,0:T(8,128)(2,1)S(1)}, u32[]{:S(2)}, u32[]{:S(2)}) collective-permute-start(bf16[1152,256]{1,0:T(8,128)(2,1)S(1)} %add.86.refs_0_), channel_id=1, source_target_pairs={{0,1},{1,0},{2,3},{3,2},{4,5},{5,4},{6,7},{7,6},{8,9},{9,8},{10,11... | collective-permute-start | bytes 1769480 | tf_op jit(solution)/shard_map/ppermute | solution.py:23
  104.6 7.3 %copy-start.2 = (bf16[4,8,2,256]{3,2,1,0:T(2,128)(2,1)S(1)}, bf16[4,8,2,256]{3,2,1,0:T(2,128)(2,1)}, u32[]{:S(2)}) copy-start(bf16[4,8,2,256]{3,2,1,0:T(2,128)(2,1)} %param.12) | copy-start | bytes 98308
  104.6 2.1 %collective-permute-start.22 = (bf16[1024,128]{1,0:T(8,128)(2,1)S(1)}, bf16[1024,128]{1,0:T(8,128)(2,1)S(1)}, u32[]{:S(2)}, u32[]{:S(2)}) collective-permute-start(bf16[1024,128]{1,0:T(8,128)(2,1)S(1)} %get-tuple-element.157), channel_id=1, source_target_pairs={{0,1},{1,0},{2,3},{3,2},{4,5},{5,4},{6,7},{7,6},{8,9},{9,8},{10,11... | collective-permute-start | bytes 786440 | tf_op jit(solution)/shard_map/ppermute | solution.py:23
  111.9 2.0 %collective-permute-start.25 = (bf16[1152,256]{1,0:T(8,128)(2,1)S(1)}, bf16[1152,256]{1,0:T(8,128)(2,1)S(1)}, u32[]{:S(2)}, u32[]{:S(2)}) collective-permute-start(bf16[1152,256]{1,0:T(8,128)(2,1)S(1)} %collective-permute-done.24.refs_0_), channel_id=1, source_target_pairs={{0,1},{1,0},{2,3},{3,2},{4,5},{5,4},{6,7},{7,6},{8,9},{9,8},{10,11... | collective-permute-start | bytes 1769480 | tf_op jit(solution)/shard_map/ppermute | solution.py:23
  115.5 1.6 %collective-permute-start.26 = (bf16[1024,128]{1,0:T(8,128)(2,1)S(1)}, bf16[1024,128]{1,0:T(8,128)(2,1)S(1)}, u32[]{:S(2)}, u32[]{:S(2)}) collective-permute-start(bf16[1024,128]{1,0:T(8,128)(2,1)S(1)} %get-tuple-element.155), channel_id=1, source_target_pairs={{0,1},{1,0},{2,3},{3,2},{4,5},{5,4},{6,7},{7,6},{8,9},{9,8},{10,11... | collective-permute-start | bytes 786440 | tf_op jit(solution)/shard_map/ppermute | solution.py:23
  118.6 7.0 %collective-permute-start.27 = (bf16[272,128]{1,0:T(8,128)(2,1)S(1)}, bf16[272,128]{1,0:T(8,128)(2,1)S(1)}, u32[]{:S(2)}, u32[]{:S(2)}) collective-permute-start(bf16[272,128]{1,0:T(8,128)(2,1)S(1)} %get-tuple-element.135), channel_id=1, source_target_pairs={{0,8},{8,0},{16,24},{24,16},{1,9},{9,1},{17,25},{25,17},{2,10},{10... | collective-permute-start | bytes 208904 | tf_op jit(solution)/shard_map/ppermute | solution.py:32
  118.7 9.0 %collective-permute-start.28 = (bf16[272,128]{1,0:T(8,128)(2,1)S(1)}, bf16[272,128]{1,0:T(8,128)(2,1)S(1)}, u32[]{:S(2)}, u32[]{:S(2)}) collective-permute-start(bf16[272,128]{1,0:T(8,128)(2,1)S(1)} %get-tuple-element.136), channel_id=1, source_target_pairs={{0,16},{8,24},{16,0},{24,8},{1,17},{9,25},{17,1},{25,9},{2,18},{10... | collective-permute-start | bytes 208904 | tf_op jit(solution)/shard_map/ppermute | solution.py:32
  120.4 7.3 %collective-permute-start.29 = (bf16[272,128]{1,0:T(8,128)(2,1)S(1)}, bf16[272,128]{1,0:T(8,128)(2,1)S(1)}, u32[]{:S(2)}, u32[]{:S(2)}) collective-permute-start(bf16[272,128]{1,0:T(8,128)(2,1)S(1)} %get-tuple-element.137), channel_id=1, source_target_pairs={{0,24},{8,16},{16,8},{24,0},{1,25},{9,17},{17,9},{25,1},{2,26},{10... | collective-permute-start | bytes 208904 | tf_op jit(solution)/shard_map/ppermute | solution.py:32
  128.1 1.3 %collective-permute-start.30 = (bf16[32,1024]{1,0:T(8,128)(2,1)S(1)}, bf16[32,1024]{1,0:T(8,128)(2,1)S(1)}, u32[]{:S(2)}, u32[]{:S(2)}) collective-permute-start(bf16[32,1024]{1,0:T(8,128)(2,1)S(1)} %finish.1), channel_id=1, source_target_pairs={{0,1},{1,0},{2,3},{3,2},{4,5},{5,4},{6,7},{7,6},{8,9},{9,8},{10,11... | collective-permute-start | bytes 196616 | tf_op jit(solution)/shard_map/ppermute | solution.py:23

commit v11 on v10

--- a/solution.py
+++ b/solution.py
@@ -475,19 +475,7 @@
 
 
 def smooth_of(top):
-    groups, owners = lax.axis_size("seq"), lax.axis_size("rep")
-    if groups != LINE:
-        return jnp.sqrt(lax.pmax(top, "seq") + EPSILON)
-    partners = list(range(1, groups))
-    found = [top]
-    for first in range(0, len(partners), owners):
-        pairs = [
-            (group * owners + owner, partner(group, k, groups) * owners + owner)
-            for owner, k in enumerate(partners[first : first + owners])
-            for group in range(groups)
-        ]
-        found.append(lax.ppermute(top, ("seq", "rep"), pairs))
-    top = functools.reduce(jnp.maximum, from_owners(functools.reduce(jnp.maximum, found)))
+    top = functools.reduce(jnp.maximum, from_groups(top))
     return jnp.sqrt(top + EPSILON)
 
 
@@ -544,17 +532,16 @@
     ka2, totals = barrier((ka2, totals))
     absorb("k", [ka2 + kb2], (((0, 2), (1, 2)),))
 
-    vb1, totals = barrier((vb1, totals))
     va2 = send(vb1, 2, 0)
-    absorb("v", [vb1], (((1, 1),),))
 
     ka3, totals = barrier((ka3, totals))
     absorb("k", [ka3], (((0, 3),),))
     raw_keys = totals["k"]
     top = chip_top(raw_keys)
     smooth = smooth_of(top)
-    vb2, top = barrier((vb2, top))
+    vb1, vb2, top = barrier((vb1, vb2, top))
     va3 = send(vb2, 3, 0)
+    absorb("v", [vb1], (((1, 1),),))
     va2, vb2, smooth = barrier((va2, vb2, smooth))
     absorb("v", [va2 + vb2], (((0, 2), (1, 2)),))
     queries = [

time: 131 us -> 121 us (0.924)
  starting transfers between devices: 36.7 us -> 31.8 us
  waiting for transfers between devices: 47.2 us -> 42.6 us
    ppermute x10, waiting for transfers between devices: 42.8 us -> 31.2 us  [send(): return lax.ppermute(x, 'seq', line_pairs(hop, parity, groups))]
    ppermute x3 -> x6, waiting for transfers between devices: 2.08 us -> 8.69 us  [swapped(): return lax.ppermute(x, axis, [(i, partner(i, k, n)) for i in range(n)])]
    ppermute x15 -> x14, starting transfers between devices: 7.72 us -> 2.36 us  [shifted(): return lax.ppermute(x, axis, [(i, (i + k) % n) for i in range(n)])]
    ppermute x2 -> x0, starting transfers between devices: 4.53 us -> none  [smooth_of(): found.append(lax.ppermute(top, ('seq', 'rep'), pairs))]
    ppermute x3 -> x6, starting transfers between devices: 4.44 us -> 8.83 us  [swapped(): return lax.ppermute(x, axis, [(i, partner(i, k, n)) for i in range(n)])]
    ppermute x15 -> x14, waiting for transfers between devices: 2.3 us -> 2.73 us  [shifted(): return lax.ppermute(x, axis, [(i, (i + k) % n) for i in range(n)])]
  transfers between devices with their start and end apart: 31 -> 31, of which waited for: 11 -> 11; matrix products, arithmetic and copies ran while one was open for 4% -> 4% of each run, Pallas kernels for 25% -> 28%
where the time goes in v11:
time: 121 us
  waiting for transfers between devices  42.6 us (35%)
  Pallas kernels  36.8 us (30%)
  starting transfers between devices  31.8 us (26%)
  other arithmetic  5.49 us (5%)
  local copies, waits for them, and re-layouts  2.15 us (2%)
  between operations  1.25 us (1%)
    ppermute x10, waiting for transfers between devices, send(): return lax.ppermute(x, 'seq', line_pairs(hop, parity, groups))  31.2 us
    pallas_call x16, Pallas kernels, project(): pl.pallas_call(functools.partial(project_kernel, hops, back, groups, owne...  22 us
    ppermute x10, starting transfers between devices, send(): return lax.ppermute(x, 'seq', line_pairs(hop, parity, groups))  16.1 us
    ppermute x6, starting transfers between devices, swapped(): return lax.ppermute(x, axis, [(i, partner(i, k, n)) for i in range(n)])  8.83 us
    ppermute x6, waiting for transfers between devices, swapped(): return lax.ppermute(x, axis, [(i, partner(i, k, n)) for i in range(n)])  8.69 us
    pallas_call x1, Pallas kernels, load(): pl.pallas_call(functools.partial(load_kernel, owners), out_shape=(jax.Sha...  6.57 us
    pallas_call x1, Pallas kernels, score(): pl.pallas_call(functools.partial(score_kernel, slots, parts, steps, scale...  4.73 us
    ppermute x1, starting transfers between devices, line_project(): far_query = lax.ppermute(own_block[depth:], 'seq', ends)  4.54 us
  transfers between devices with their start and end apart: 31, of which 11 were waited for; matrix products, arithmetic and copies ran while one was open for 4% of the time, Pallas kernels for 28%

profile of v11, /device:TPU:0, one launch (start us, length us, event | category | flops | bytes accessed | tf_op | source)
XLA Modules:
  0.0 120.5 jit_solution(11632715231380881411)
XLA Ops:
  0.6 3.1 %collective-permute-start = (bf16[1024,256]{1,0:T(8,128)(2,1)}, bf16[1024,256]{1,0:T(8,128)(2,1)S(1)}, u32[]{:S(2)}, u32[]{:S(2)}) collective-permute-start(bf16[1024,256]{1,0:T(8,128)(2,1)} %refs_0_), channel_id=1, source_target_pairs={{0,8},{8,0},{16,24},{24,16},{1,9},{9,1},{17,25},{25,17},{2,10},{10... | collective-permute-start | bytes 1572872 | tf_op jit(solution)/shard_map/ppermute | solution.py:498
  3.7 0.7 collective-permute-start.1
  4.5 0.5 collective-permute-start.7
  5.0 0.9 select_bitcast_fusion.query
  6.0 1.0 copy-done
  7.1 1.0 copy-done.1
  8.1 6.6 %load.1 = (bf16[1024,8192]{1,0:T(8,128)(2,1)S(1)}, f32[1024,256]{1,0:T(8,128)S(1)}, f32[1024,256]{1,0:T(8,128)S(1)}) custom-call(s32[2]{0:T(128)S(1)} %pad_add_fusion.place, bf16[1024,8192]{1,0:T(8,128)(2,1)} %hidden.1, bf16[1024,256]{1,0:T(8,128)(2,1)S(1)} %copy-done.1, bf16[1152,256]{1,0:T(8,128)(2,1)S(1)} %pack.1.refs_1_), custom_call_target="tpu_custom_call" | custom-call | flops 1073741824 | bytes 16777216 | tf_op jit(solution)/shard_map/load/pallas_call | solution.py:114
  14.7 1.2 collective-permute-done.refs_0_
  15.9 0.5 collective-permute-start.5
  16.4 4.8 %collective-permute-start.3 = (bf16[1152,256]{1,0:T(8,128)(2,1)S(1)}, bf16[1152,256]{1,0:T(8,128)(2,1)S(1)}, u32[]{:S(2)}, u32[]{:S(2)}) collective-permute-start(bf16[1152,256]{1,0:T(8,128)(2,1)S(1)} %pack.1.refs_1_), channel_id=1, source_target_pairs={{0,8},{8,0},{16,24},{24,16},{1,9},{9,1},{17,25},{25,17},{2,10},{10... | collective-permute-start | bytes 1769480 | tf_op jit(solution)/shard_map/ppermute | solution.py:498
  21.2 0.7 collective-permute-start.2
  21.9 1.4 %project.19.refs_1_ = f32[1024,256]{1,0:T(8,128)S(1)} custom-call(s32[2]{0:T(128)S(1)} %pad_add_fusion.place, bf16[1024,8192]{1,0:T(8,128)(2,1)S(1)} %get-tuple-element.84.left, bf16[1024,256]{1,0:T(8,128)(2,1)S(1)} %collective-permute-done.7.refs_0_, f32[1024,256]{1,0:T(8,128)S(1)} %get-tuple-element.87.refs_1_), custom_call_target="tpu_custom_call", output_to_operand_aliasing={{}: (3, {})} | custom-call | flops 536870912 | bytes 4718592 | tf_op jit(solution)/shard_map/project/pallas_call | solution.py:170
  23.3 1.4 %project.16.refs_2_ = f32[1024,256]{1,0:T(8,128)S(1)} custom-call(s32[2]{0:T(128)S(1)} %pad_add_fusion.place, bf16[1024,8192]{1,0:T(8,128)(2,1)S(1)} %get-tuple-element.84.left, bf16[1024,256]{1,0:T(8,128)(2,1)S(1)} %collective-permute-done.6.refs_0_, f32[1024,256]{1,0:T(8,128)S(1)} %get-tuple-element.86.refs_1_), custom_call_target="tpu_custom_call", output_to_operand_aliasing={{}: (3, {})} | custom-call | flops 536870912 | bytes 4718592 | tf_op jit(solution)/shard_map/project/pallas_call | solution.py:170
  24.8 1.5 %project.17.refs_2_ = f32[1024,256]{1,0:T(8,128)S(1)} custom-call(s32[2]{0:T(128)S(1)} %pad_add_fusion.place, bf16[1024,8192]{1,0:T(8,128)(2,1)S(1)} %get-tuple-element.84.left, bf16[1024,256]{1,0:T(8,128)(2,1)S(1)} %collective-permute-done.refs_0_, bf16[1024,256]{1,0:T(8,128)(2,1)S(1)} %collective-permute-done.1.refs_1_, ...), custom_call_target="tpu_custom_call", output_to_operand_aliasing={{}: (4, {})} | custom-call | flops 1073741824 | bytes 7340032 | tf_op jit(solution)/shard_map/project/pallas_call | solution.py:170
  26.3 1.5 %project.18.refs_1_ = f32[1024,256]{1,0:T(8,128)S(1)} custom-call(s32[2]{0:T(128)S(1)} %pad_add_fusion.place, bf16[1024,8192]{1,0:T(8,128)(2,1)S(1)} %get-tuple-element.84.left, bf16[1024,256]{1,0:T(8,128)(2,1)S(1)} %collective-permute-done.4.refs_0_, bf16[1024,256]{1,0:T(8,128)(2,1)S(1)} %collective-permute-done.5.refs_1_, ...), custom_call_target="tpu_custom_call", output_to_operand_aliasing={{}: (4, {})} | custom-call | flops 1073741824 | bytes 7340032 | tf_op jit(solution)/shard_map/project/pallas_call | solution.py:170
  27.8 6.8 %collective-permute-done.3.refs_0_ = bf16[1152,256]{1,0:T(8,128)(2,1)S(1)} collective-permute-done((bf16[1152,256]{1,0:T(8,128)(2,1)S(1)}, bf16[1152,256]{1,0:T(8,128)(2,1)S(1)}, u32[]{:S(2)}, u32[]{:S(2)}) %collective-permute-start.3) | collective-permute-done | bytes 589856 | tf_op jit(solution)/shard_map/ppermute | solution.py:498
  34.7 1.3 %collective-permute-start.12 = (bf16[1024,256]{1,0:T(8,128)(2,1)S(1)}, bf16[1024,256]{1,0:T(8,128)(2,1)S(1)}, u32[]{:S(2)}, u32[]{:S(2)}) collective-permute-start(bf16[1024,256]{1,0:T(8,128)(2,1)S(1)} %collective-permute-done.1.refs_1_), channel_id=1, source_target_pairs={{8,0},{16,24},{9,1},{17,25},{10,2},{18,26},{11,3},{19,27},{12,4},{... | collective-permute-start | bytes 1572872 | tf_op jit(solution)/shard_map/ppermute | solution.py:498
  36.1 1.4 %collective-permute-start.11 = (bf16[1024,256]{1,0:T(8,128)(2,1)S(1)}, bf16[1024,256]{1,0:T(8,128)(2,1)S(1)}, u32[]{:S(2)}, u32[]{:S(2)}) collective-permute-start(bf16[1024,256]{1,0:T(8,128)(2,1)S(1)} %collective-permute-done.2), channel_id=1, source_target_pairs={{8,0},{16,24},{9,1},{17,25},{10,2},{18,26},{11,3},{19,27},{12,4},{... | collective-permute-start | bytes 1572872 | tf_op jit(solution)/shard_map/ppermute | solution.py:498
  37.5 1.4 %project.20.refs_1_ = f32[1024,256]{1,0:T(8,128)S(1)} custom-call(s32[2]{0:T(128)S(1)} %pad_add_fusion.place, bf16[1024,8192]{1,0:T(8,128)(2,1)S(1)} %get-tuple-element.84.left, bf16[1152,256]{1,0:T(8,128)(2,1)S(1)} %collective-permute-done.3.refs_0_, f32[1024,256]{1,0:T(8,128)S(1)} %project.19.refs_1_), custom_call_target="tpu_custom_call", output_to_operand_aliasing={{}: (3, {})} | custom-call | flops 536870912 | bytes 4718592 | tf_op jit(solution)/shard_map/project/pallas_call | solution.py:170
  39.0 1.4 %project.21.refs_1_ = f32[1024,256]{1,0:T(8,128)S(1)} custom-call(s32[2]{0:T(128)S(1)} %pad_add_fusion.place, bf16[1024,8192]{1,0:T(8,128)(2,1)S(1)} %get-tuple-element.84.left, bf16[1152,256]{1,0:T(8,128)(2,1)S(1)} %collective-permute-done.13.refs_0_, f32[1024,256]{1,0:T(8,128)S(1)} %project.20.refs_1_), custom_call_target="tpu_custom_call", output_to_operand_aliasing={{}: (3, {})} | custom-call | flops 536870912 | bytes 4718592 | tf_op jit(solution)/shard_map/project/pallas_call | solution.py:170
  40.4 10.9 %collective-permute-done.12 = bf16[1024,256]{1,0:T(8,128)(2,1)S(1)} collective-permute-done((bf16[1024,256]{1,0:T(8,128)(2,1)S(1)}, bf16[1024,256]{1,0:T(8,128)(2,1)S(1)}, u32[]{:S(2)}, u32[]{:S(2)}) %collective-permute-start.12) | collective-permute-done | bytes 524320 | tf_op jit(solution)/shard_map/ppermute | solution.py:498
  51.4 0.1 add.74.refs_0_
  51.6 0.6 convert_reduce_fusion
  52.2 0.2 fusion.2
  52.4 0.8 collective-permute-start.8
  53.3 1.4 %project.22.refs_1_ = f32[1024,256]{1,0:T(8,128)S(1)} custom-call(s32[2]{0:T(128)S(1)} %pad_add_fusion.place, bf16[1024,8192]{1,0:T(8,128)(2,1)S(1)} %get-tuple-element.84.left, bf16[1024,256]{1,0:T(8,128)(2,1)S(1)} %add.74.refs_0_, f32[1024,256]{1,0:T(8,128)S(1)} %project.18.refs_1_), custom_call_target="tpu_custom_call", output_to_operand_aliasing={{}: (3, {})} | custom-call | flops 536870912 | bytes 4718592 | tf_op jit(solution)/shard_map/project/pallas_call | solution.py:170
  54.8 1.5 %project.23.refs_1_ = f32[1024,256]{1,0:T(8,128)S(1)} custom-call(s32[2]{0:T(128)S(1)} %pad_add_fusion.place, bf16[1024,8192]{1,0:T(8,128)(2,1)S(1)} %get-tuple-element.84.left, bf16[1024,256]{1,0:T(8,128)(2,1)S(1)} %collective-permute-done.14.refs_0_, f32[1024,256]{1,0:T(8,128)S(1)} %project.22.refs_1_), custom_call_target="tpu_custom_call", output_to_operand_aliasing={{}: (3, {})} | custom-call | flops 536870912 | bytes 4718592 | tf_op jit(solution)/shard_map/project/pallas_call | solution.py:170
  56.2 5.9 %collective-permute-done.11.refs_0_ = bf16[1024,256]{1,0:T(8,128)(2,1)S(1)} collective-permute-done((bf16[1024,256]{1,0:T(8,128)(2,1)S(1)}, bf16[1024,256]{1,0:T(8,128)(2,1)S(1)}, u32[]{:S(2)}, u32[]{:S(2)}) %collective-permute-start.11) | collective-permute-done | bytes 524320 | tf_op jit(solution)/shard_map/ppermute | solution.py:498
  62.1 0.2 fusion.1.count
  62.4 0.7 collective-permute-start.10
  63.1 4.5 %collective-permute-start.20 = (bf16[128,256]{1,0:T(8,128)(2,1)S(1)}, bf16[128,256]{1,0:T(8,128)(2,1)S(1)}, u32[]{:S(2)}, u32[]{:S(2)}) collective-permute-start(bf16[128,256]{1,0:T(8,128)(2,1)S(1)} %slice.79), channel_id=1, source_target_pairs={{0,24},{24,0},{1,25},{25,1},{2,26},{26,2},{3,27},{27,3},{4,28},{28... | collective-permute-start | bytes 196616 | tf_op jit(solution)/shard_map/ppermute | solution.py:527
  67.6 1.3 %collective-permute-start.9 = (bf16[1152,256]{1,0:T(8,128)(2,1)S(1)}, bf16[1152,256]{1,0:T(8,128)(2,1)S(1)}, u32[]{:S(2)}, u32[]{:S(2)}) collective-permute-start(bf16[1152,256]{1,0:T(8,128)(2,1)S(1)} %collective-permute-done.8.refs_0_), channel_id=1, source_target_pairs={{8,0},{16,24},{9,1},{17,25},{10,2},{18,26},{11,3},{19,27},{12,4},{... | collective-permute-start | bytes 1769480 | tf_op jit(solution)/shard_map/ppermute | solution.py:498
  68.9 1.4 %project.24.refs_1_ = f32[1024,256]{1,0:T(8,128)S(1)} custom-call(s32[2]{0:T(128)S(1)} %pad_add_fusion.place, bf16[1024,8192]{1,0:T(8,128)(2,1)S(1)} %get-tuple-element.84.left, bf16[1024,256]{1,0:T(8,128)(2,1)S(1)} %collective-permute-done.11.refs_0_, f32[1024,256]{1,0:T(8,128)S(1)} %project.23.refs_1_), custom_call_target="tpu_custom_call", output_to_operand_aliasing={{}: (3, {})} | custom-call | flops 536870912 | bytes 4718592 | tf_op jit(solution)/shard_map/project/pallas_call | solution.py:170
  70.4 1.6 %project.25 = f32[1024,256]{1,0:T(8,128)S(1)} custom-call(s32[2]{0:T(128)S(1)} %pad_add_fusion.place, bf16[1024,8192]{1,0:T(8,128)(2,1)S(1)} %get-tuple-element.84.left, bf16[1024,256]{1,0:T(8,128)(2,1)S(1)} %collective-permute-done.15.refs_0_, f32[1024,256]{1,0:T(8,128)S(1)} %project.24.refs_1_), custom_call_target="tpu_custom_call", output_to_operand_aliasing={{}: (3, {})} | custom-call | flops 536870912 | bytes 4718592 | tf_op jit(solution)/shard_map/project/pallas_call | solution.py:170
  72.1 0.3 collective-permute-start.16
  72.4 0.9 collective-permute-done.16
  73.3 1.3 %collective-permute-start.17 = (f32[1,256]{1,0:T(1,128)S(1)}, f32[1,256]{1,0:T(1,128)S(1)}, u32[]{:S(2)}, u32[]{:S(2)}) collective-permute-start(f32[1,256]{1,0:T(1,128)S(1)} %max.36), channel_id=1, source_target_pairs={{0,8},{8,0},{16,24},{24,16},{1,9},{9,1},{17,25},{25,17},{2,10},{10... | collective-permute-start | bytes 3080 | tf_op jit(solution)/shard_map/ppermute | solution.py:32
  74.6 1.1 collective-permute-start.18
  75.7 2.0 %collective-permute-start.19 = (f32[1,256]{1,0:T(1,128)S(1)}, f32[1,256]{1,0:T(1,128)S(1)}, u32[]{:S(2)}, u32[]{:S(2)}) collective-permute-start(f32[1,256]{1,0:T(1,128)S(1)} %max.36), channel_id=1, source_target_pairs={{0,24},{8,16},{16,8},{24,0},{1,25},{9,17},{17,9},{25,1},{2,26},{10... | collective-permute-start | bytes 3080 | tf_op jit(solution)/shard_map/ppermute | solution.py:32
  77.8 0.7 project.26.refs_1_
  78.5 6.6 %collective-permute-done.17 = f32[1,256]{1,0:T(1,128)S(1)} collective-permute-done((f32[1,256]{1,0:T(1,128)S(1)}, f32[1,256]{1,0:T(1,128)S(1)}, u32[]{:S(2)}, u32[]{:S(2)}) %collective-permute-start.17) | collective-permute-done | bytes 1056 | tf_op jit(solution)/shard_map/ppermute | solution.py:32
  85.1 1.3 %collective-permute-start.24 = (bf16[1152,256]{1,0:T(8,128)(2,1)S(1)}, bf16[1152,256]{1,0:T(8,128)(2,1)S(1)}, u32[]{:S(2)}, u32[]{:S(2)}) collective-permute-start(bf16[1152,256]{1,0:T(8,128)(2,1)S(1)} %collective-permute-done.10), channel_id=1, source_target_pairs={{8,0},{16,24},{9,1},{17,25},{10,2},{18,26},{11,3},{19,27},{12,4},{... | collective-permute-start | bytes 1769480 | tf_op jit(solution)/shard_map/ppermute | solution.py:498
  86.5 0.1 add.86.refs_0_
  86.7 0.1 minimum_convert_fusion.1
  86.9 0.6 collective-permute-start.21
  87.5 0.7 project.27.refs_1_
  88.3 1.4 %project.28.refs_1_ = f32[1024,256]{1,0:T(8,128)S(1)} custom-call(s32[2]{0:T(128)S(1)} %pad_add_fusion.place, bf16[1024,8192]{1,0:T(8,128)(2,1)S(1)} %get-tuple-element.84.left, bf16[1152,256]{1,0:T(8,128)(2,1)S(1)} %add.86.refs_0_, f32[1024,256]{1,0:T(8,128)S(1)} %project.27.refs_1_), custom_call_target="tpu_custom_call", output_to_operand_aliasing={{}: (3, {})} | custom-call | flops 536870912 | bytes 4718592 | tf_op jit(solution)/shard_map/project/pallas_call | solution.py:170
  89.8 1.4 %project.29.refs_1_ = f32[1024,256]{1,0:T(8,128)S(1)} custom-call(s32[2]{0:T(128)S(1)} %pad_add_fusion.place, bf16[1024,8192]{1,0:T(8,128)(2,1)S(1)} %get-tuple-element.84.left, bf16[1152,256]{1,0:T(8,128)(2,1)S(1)} %collective-permute-done.22.refs_0_, f32[1024,256]{1,0:T(8,128)S(1)} %project.28.refs_1_), custom_call_target="tpu_custom_call", output_to_operand_aliasing={{}: (3, {})} | custom-call | flops 536870912 | bytes 4718592 | tf_op jit(solution)/shard_map/project/pallas_call | solution.py:170
  91.2 4.7 %score.1 = (bf16[4,256,2048]{2,1,0:T(8,128)(2,1)S(1)}, f32[2,256]{1,0:T(2,128)S(1)}, f32[2,256]{1,0:T(2,128)S(1)}, f32[2,256]{1,0:T(2,128)S(1)}, f32[2,256]{1,0:T(2,128)S(1)}) custom-call(s32[4]{0:T(128)S(1)} %iota_xor_fusion.group, bf16[4,128,256]{2,1,0:T(8,128)(2,1)S(1)} %pad_maximum_fusion.query, f32[1,128]{1,0:T(1,128)S(1)} %broadcast_select_fusion.7.smooth, ...), custom_call_target="tpu_custom_call" | custom-call | flops 536870912 | bytes 4194304 | tf_op jit(solution)/shard_map/score/pallas_call | solution.py:241
  96.0 6.4 %collective-permute-done.24.refs_0_ = bf16[1152,256]{1,0:T(8,128)(2,1)S(1)} collective-permute-done((bf16[1152,256]{1,0:T(8,128)(2,1)S(1)}, bf16[1152,256]{1,0:T(8,128)(2,1)S(1)}, u32[]{:S(2)}, u32[]{:S(2)}) %collective-permute-start.24) | collective-permute-done | bytes 589856 | tf_op jit(solution)/shard_map/ppermute | solution.py:498
  102.4 1.4 %project.30.refs_1_ = f32[1024,256]{1,0:T(8,128)S(1)} custom-call(s32[2]{0:T(128)S(1)} %pad_add_fusion.place, bf16[1024,8192]{1,0:T(8,128)(2,1)S(1)} %get-tuple-element.84.left, bf16[1152,256]{1,0:T(8,128)(2,1)S(1)} %collective-permute-done.24.refs_0_, f32[1024,256]{1,0:T(8,128)S(1)} %project.29.refs_1_), custom_call_target="tpu_custom_call", output_to_operand_aliasing={{}: (3, {})} | custom-call | flops 536870912 | bytes 4718592 | tf_op jit(solution)/shard_map/project/pallas_call | solution.py:170
  103.9 0.5 collective-permute-done.25.refs_0_
  104.3 1.4 %project.31 = f32[1024,256]{1,0:T(8,128)S(1)} custom-call(s32[2]{0:T(128)S(1)} %pad_add_fusion.place, bf16[1024,8192]{1,0:T(8,128)(2,1)S(1)} %get-tuple-element.84.left, bf16[1152,256]{1,0:T(8,128)(2,1)S(1)} %collective-permute-done.25.refs_0_, f32[1024,256]{1,0:T(8,128)S(1)} %project.30.refs_1_), custom_call_target="tpu_custom_call", output_to_operand_aliasing={{}: (3, {})} | custom-call | flops 536870912 | bytes 4718592 | tf_op jit(solution)/shard_map/project/pallas_call | solution.py:170
  106.0 0.2 collective-permute-start.26
  106.2 1.3 %weigh_own.1.own = f32[4,256,128]{2,1,0:T(8,128)S(1)} custom-call(bf16[4,256,2048]{2,1,0:T(8,128)(2,1)S(1)} %get-tuple-element.114.probs.refs_0_, bf16[1024,128]{1,0:T(8,128)(2,1)S(1)} %get-tuple-element.152.values), custom_call_target="tpu_custom_call" | custom-call | flops 268435456 | bytes 2097152 | tf_op jit(solution)/shard_map/weigh_own/pallas_call | solution.py:322
  107.6 1.4 %weigh.1 = (bf16[272,128]{1,0:T(8,128)(2,1)S(1)}, bf16[272,128]{1,0:T(8,128)(2,1)S(1)}, bf16[272,128]{1,0:T(8,128)(2,1)S(1)}, bf16[272,128]{1,0:T(8,128)(2,1)S(1)}) custom-call(f32[4,256,128]{2,1,0:T(8,128)S(1)} %weigh_own.1.own, bf16[4,256,2048]{2,1,0:T(8,128)(2,1)S(1)} %get-tuple-element.114.probs.refs_0_, ...), custom_call_target="tpu_custom_call" | custom-call | flops 268435456 | bytes 2097152 | tf_op jit(solution)/shard_map/weigh/pallas_call | solution.py:334
  109.1 1.7 %collective-permute-start.28 = (bf16[272,128]{1,0:T(8,128)(2,1)S(1)}, bf16[272,128]{1,0:T(8,128)(2,1)S(1)}, u32[]{:S(2)}, u32[]{:S(2)}) collective-permute-start(bf16[272,128]{1,0:T(8,128)(2,1)S(1)} %get-tuple-element.132), channel_id=1, source_target_pairs={{0,16},{8,24},{16,0},{24,8},{1,17},{9,25},{17,1},{25,9},{2,18},{10... | collective-permute-start | bytes 208904 | tf_op jit(solution)/shard_map/ppermute | solution.py:32
  110.8 2.6 %collective-permute-start.29 = (bf16[272,128]{1,0:T(8,128)(2,1)S(1)}, bf16[272,128]{1,0:T(8,128)(2,1)S(1)}, u32[]{:S(2)}, u32[]{:S(2)}) collective-permute-start(bf16[272,128]{1,0:T(8,128)(2,1)S(1)} %get-tuple-element.133), channel_id=1, source_target_pairs={{0,24},{8,16},{16,8},{24,0},{1,25},{9,17},{17,9},{25,1},{2,26},{10... | collective-permute-start | bytes 208904 | tf_op jit(solution)/shard_map/ppermute | solution.py:32
  113.5 2.3 %broadcast_select_fusion = bf16[1024,2,256]{2,1,0:T(2,128)(2,1)} fusion(pred[2]{0:T(512)(128)(4,1)S(1)} %iota_compare_fusion.5, bf16[1024,256]{1,0:T(8,128)(2,1)S(1)} %minimum_convert_fusion, bf16[1024,256]{1,0:T(8,128)(2,1)S(1)} %minimum_convert_fusion.1), kind=kLoop, calls=%fused_computation.3 | loop fusion | flops 524288 | bytes 2097154 | tf_op jit(solution)/shard_map/jit(_where)/select_n | solution.py:634
  115.8 0.2 fresh.1
  116.0 2.1 %collective-permute-done.28.refs_2_ = bf16[272,128]{1,0:T(8,128)(2,1)S(1)} collective-permute-done((bf16[272,128]{1,0:T(8,128)(2,1)S(1)}, bf16[272,128]{1,0:T(8,128)(2,1)S(1)}, u32[]{:S(2)}, u32[]{:S(2)}) %collective-permute-start.28) | collective-permute-done | bytes 69664 | tf_op jit(solution)/shard_map/ppermute | solution.py:32
  118.1 0.4 finish.1
  118.6 1.2 %collective-permute-done.30 = bf16[32,1024]{1,0:T(8,128)(2,1)S(1)} collective-permute-done((bf16[32,1024]{1,0:T(8,128)(2,1)S(1)}, bf16[32,1024]{1,0:T(8,128)(2,1)S(1)}, u32[]{:S(2)}, u32[]{:S(2)}) %collective-permute-start.30) | collective-permute-done | bytes 65568 | tf_op jit(solution)/shard_map/ppermute | solution.py:23
  119.9 0.7 maximum_bitcast_fusion
  (71 shorter events, 1.2 us)
Async XLA Ops:
  0.6 15.3 %collective-permute-start = (bf16[1024,256]{1,0:T(8,128)(2,1)}, bf16[1024,256]{1,0:T(8,128)(2,1)S(1)}, u32[]{:S(2)}, u32[]{:S(2)}) collective-permute-start(bf16[1024,256]{1,0:T(8,128)(2,1)} %refs_0_), channel_id=1, source_target_pairs={{0,8},{8,0},{16,24},{24,16},{1,9},{9,1},{17,25},{25,17},{2,10},{10... | collective-permute-start | bytes 1572872 | tf_op jit(solution)/shard_map/ppermute | solution.py:498
  3.7 12.1 %collective-permute-start.1 = (bf16[1024,256]{1,0:T(8,128)(2,1)}, bf16[1024,256]{1,0:T(8,128)(2,1)S(1)}, u32[]{:S(2)}, u32[]{:S(2)}) collective-permute-start(bf16[1024,256]{1,0:T(8,128)(2,1)} %refs_0_), channel_id=1, source_target_pairs={{8,16},{16,8},{9,17},{17,9},{10,18},{18,10},{11,19},{19,11},{12,20... | collective-permute-start | bytes 1572872 | tf_op jit(solution)/shard_map/ppermute | solution.py:498
  4.4 18.9 %collective-permute-start.6 = (bf16[1024,256]{1,0:T(8,128)(2,1)}, bf16[1024,256]{1,0:T(8,128)(2,1)S(1)}, u32[]{:S(2)}, u32[]{:S(2)}) collective-permute-start(bf16[1024,256]{1,0:T(8,128)(2,1)} %refs_0_), channel_id=1, source_target_pairs={{0,1},{1,0},{2,3},{3,2},{4,5},{5,4},{6,7},{7,6},{8,9},{9,8},{10,11... | collective-permute-start | bytes 1572872 | tf_op jit(solution)/shard_map/ppermute | solution.py:23
  4.5 16.6 %collective-permute-start.7 = (bf16[1024,256]{1,0:T(8,128)(2,1)}, bf16[1024,256]{1,0:T(8,128)(2,1)S(1)}, u32[]{:S(2)}, u32[]{:S(2)}) collective-permute-start(bf16[1024,256]{1,0:T(8,128)(2,1)} %weight.1), channel_id=1, source_target_pairs={{0,1},{1,0},{2,3},{3,2},{4,5},{5,4},{6,7},{7,6},{8,9},{9,8},{10,11... | collective-permute-start | bytes 1572872 | tf_op jit(solution)/shard_map/ppermute | solution.py:23
  6.0 1.0 copy-start
  7.1 1.0 copy-start.1
  15.9 10.4 %collective-permute-start.4 = (bf16[1024,256]{1,0:T(8,128)(2,1)S(1)}, bf16[1024,256]{1,0:T(8,128)(2,1)S(1)}, u32[]{:S(2)}, u32[]{:S(2)}) collective-permute-start(bf16[1024,256]{1,0:T(8,128)(2,1)S(1)} %collective-permute-done.refs_0_), channel_id=1, source_target_pairs={{0,1},{1,0},{2,3},{3,2},{4,5},{5,4},{6,7},{7,6},{8,9},{9,8},{10,11... | collective-permute-start | bytes 1572872 | tf_op jit(solution)/shard_map/ppermute | solution.py:23
  15.9 10.4 %collective-permute-start.5 = (bf16[1024,256]{1,0:T(8,128)(2,1)S(1)}, bf16[1024,256]{1,0:T(8,128)(2,1)S(1)}, u32[]{:S(2)}, u32[]{:S(2)}) collective-permute-start(bf16[1024,256]{1,0:T(8,128)(2,1)S(1)} %collective-permute-done.1.refs_1_), channel_id=1, source_target_pairs={{0,1},{1,0},{2,3},{3,2},{4,5},{5,4},{6,7},{7,6},{8,9},{9,8},{10,11... | collective-permute-start | bytes 1572872 | tf_op jit(solution)/shard_map/ppermute | solution.py:23
  16.4 18.2 %collective-permute-start.3 = (bf16[1152,256]{1,0:T(8,128)(2,1)S(1)}, bf16[1152,256]{1,0:T(8,128)(2,1)S(1)}, u32[]{:S(2)}, u32[]{:S(2)}) collective-permute-start(bf16[1152,256]{1,0:T(8,128)(2,1)S(1)} %pack.1.refs_1_), channel_id=1, source_target_pairs={{0,8},{8,0},{16,24},{24,16},{1,9},{9,1},{17,25},{25,17},{2,10},{10... | collective-permute-start | bytes 1769480 | tf_op jit(solution)/shard_map/ppermute | solution.py:498
  21.2 13.5 %collective-permute-start.2 = (bf16[1024,256]{1,0:T(8,128)(2,1)S(1)}, bf16[1024,256]{1,0:T(8,128)(2,1)S(1)}, u32[]{:S(2)}, u32[]{:S(2)}) collective-permute-start(bf16[1024,256]{1,0:T(8,128)(2,1)S(1)} %collective-permute-done.refs_0_), channel_id=1, source_target_pairs={{8,16},{16,8},{9,17},{17,9},{10,18},{18,10},{11,19},{19,11},{12,20... | collective-permute-start | bytes 1572872 | tf_op jit(solution)/shard_map/ppermute | solution.py:498
  24.8 11.2 %copy-start.6 = (s32[32]{0:T(128)S(1)}, s32[32]{0:T(128)}, u32[]{:S(2)}) copy-start(s32[32]{0:T(128)} %param.15) | copy-start | bytes 388
  34.7 4.3 %collective-permute-start.13 = (bf16[1152,256]{1,0:T(8,128)(2,1)S(1)}, bf16[1152,256]{1,0:T(8,128)(2,1)S(1)}, u32[]{:S(2)}, u32[]{:S(2)}) collective-permute-start(bf16[1152,256]{1,0:T(8,128)(2,1)S(1)} %collective-permute-done.3.refs_0_), channel_id=1, source_target_pairs={{0,1},{1,0},{2,3},{3,2},{4,5},{5,4},{6,7},{7,6},{8,9},{9,8},{10,11... | collective-permute-start | bytes 1769480 | tf_op jit(solution)/shard_map/ppermute | solution.py:23
  34.7 16.7 %collective-permute-start.12 = (bf16[1024,256]{1,0:T(8,128)(2,1)S(1)}, bf16[1024,256]{1,0:T(8,128)(2,1)S(1)}, u32[]{:S(2)}, u32[]{:S(2)}) collective-permute-start(bf16[1024,256]{1,0:T(8,128)(2,1)S(1)} %collective-permute-done.1.refs_1_), channel_id=1, source_target_pairs={{8,0},{16,24},{9,1},{17,25},{10,2},{18,26},{11,3},{19,27},{12,4},{... | collective-permute-start | bytes 1572872 | tf_op jit(solution)/shard_map/ppermute | solution.py:498
  36.1 15.6 %copy-start.3 = (s32[32,32]{1,0:T(8,128)S(1)}, s32[32,32]{1,0:T(8,128)}, u32[]{:S(2)}) copy-start(s32[32,32]{1,0:T(8,128)} %param.14) | copy-start | bytes 12292
  36.1 26.0 %collective-permute-start.11 = (bf16[1024,256]{1,0:T(8,128)(2,1)S(1)}, bf16[1024,256]{1,0:T(8,128)(2,1)S(1)}, u32[]{:S(2)}, u32[]{:S(2)}) collective-permute-start(bf16[1024,256]{1,0:T(8,128)(2,1)S(1)} %collective-permute-done.2), channel_id=1, source_target_pairs={{8,0},{16,24},{9,1},{17,25},{10,2},{18,26},{11,3},{19,27},{12,4},{... | collective-permute-start | bytes 1572872 | tf_op jit(solution)/shard_map/ppermute | solution.py:498
  51.5 3.2 %collective-permute-start.14 = (bf16[1024,256]{1,0:T(8,128)(2,1)S(1)}, bf16[1024,256]{1,0:T(8,128)(2,1)S(1)}, u32[]{:S(2)}, u32[]{:S(2)}) collective-permute-start(bf16[1024,256]{1,0:T(8,128)(2,1)S(1)} %add.74.refs_0_), channel_id=1, source_target_pairs={{0,1},{1,0},{2,3},{3,2},{4,5},{5,4},{6,7},{7,6},{8,9},{9,8},{10,11... | collective-permute-start | bytes 1572872 | tf_op jit(solution)/shard_map/ppermute | solution.py:23
  52.4 9.9 %copy-start.5 = (f32[2,256]{1,0:T(2,128)S(1)}, f32[2,256]{1,0:T(2,128)}, u32[]{:S(2)}) copy-start(f32[2,256]{1,0:T(2,128)} %param.11) | copy-start | bytes 6148
  52.4 15.2 %collective-permute-start.8 = (bf16[1152,256]{1,0:T(8,128)(2,1)S(1)}, bf16[1152,256]{1,0:T(8,128)(2,1)S(1)}, u32[]{:S(2)}, u32[]{:S(2)}) collective-permute-start(bf16[1152,256]{1,0:T(8,128)(2,1)S(1)} %pack.1.refs_1_), channel_id=1, source_target_pairs={{8,16},{16,8},{9,17},{17,9},{10,18},{18,10},{11,19},{19,11},{12,20... | collective-permute-start | bytes 1769480 | tf_op jit(solution)/shard_map/ppermute | solution.py:498
  62.1 8.3 %collective-permute-start.15 = (bf16[1024,256]{1,0:T(8,128)(2,1)S(1)}, bf16[1024,256]{1,0:T(8,128)(2,1)S(1)}, u32[]{:S(2)}, u32[]{:S(2)}) collective-permute-start(bf16[1024,256]{1,0:T(8,128)(2,1)S(1)} %collective-permute-done.11.refs_0_), channel_id=1, source_target_pairs={{0,1},{1,0},{2,3},{3,2},{4,5},{5,4},{6,7},{7,6},{8,9},{9,8},{10,11... | collective-permute-start | bytes 1572872 | tf_op jit(solution)/shard_map/ppermute | solution.py:23
  62.4 13.3 %collective-permute-start.10 = (bf16[1152,256]{1,0:T(8,128)(2,1)S(1)}, bf16[1152,256]{1,0:T(8,128)(2,1)S(1)}, u32[]{:S(2)}, u32[]{:S(2)}) collective-permute-start(bf16[1152,256]{1,0:T(8,128)(2,1)S(1)} %collective-permute-done.3.refs_0_), channel_id=1, source_target_pairs={{8,16},{16,8},{9,17},{17,9},{10,18},{18,10},{11,19},{19,11},{12,20... | collective-permute-start | bytes 1769480 | tf_op jit(solution)/shard_map/ppermute | solution.py:498
  63.1 14.7 %collective-permute-start.20 = (bf16[128,256]{1,0:T(8,128)(2,1)S(1)}, bf16[128,256]{1,0:T(8,128)(2,1)S(1)}, u32[]{:S(2)}, u32[]{:S(2)}) collective-permute-start(bf16[128,256]{1,0:T(8,128)(2,1)S(1)} %slice.79), channel_id=1, source_target_pairs={{0,24},{24,0},{1,25},{25,1},{2,26},{26,2},{3,27},{27,3},{4,28},{28... | collective-permute-start | bytes 196616 | tf_op jit(solution)/shard_map/ppermute | solution.py:527
  67.6 18.8 %collective-permute-start.9 = (bf16[1152,256]{1,0:T(8,128)(2,1)S(1)}, bf16[1152,256]{1,0:T(8,128)(2,1)S(1)}, u32[]{:S(2)}, u32[]{:S(2)}) collective-permute-start(bf16[1152,256]{1,0:T(8,128)(2,1)S(1)} %collective-permute-done.8.refs_0_), channel_id=1, source_target_pairs={{8,0},{16,24},{9,1},{17,25},{10,2},{18,26},{11,3},{19,27},{12,4},{... | collective-permute-start | bytes 1769480 | tf_op jit(solution)/shard_map/ppermute | solution.py:498
  72.1 1.2 %collective-permute-start.16 = (f32[1,256]{1,0:T(1,128)S(1)}, f32[1,256]{1,0:T(1,128)S(1)}, u32[]{:S(2)}, u32[]{:S(2)}) collective-permute-start(f32[1,256]{1,0:T(1,128)S(1)} %bitcast.28), channel_id=1, source_target_pairs={{0,1},{1,0},{2,3},{3,2},{4,5},{5,4},{6,7},{7,6},{8,9},{9,8},{10,11... | collective-permute-start | bytes 3080 | tf_op jit(solution)/shard_map/ppermute | solution.py:23
  73.3 11.8 %collective-permute-start.17 = (f32[1,256]{1,0:T(1,128)S(1)}, f32[1,256]{1,0:T(1,128)S(1)}, u32[]{:S(2)}, u32[]{:S(2)}) collective-permute-start(f32[1,256]{1,0:T(1,128)S(1)} %max.36), channel_id=1, source_target_pairs={{0,8},{8,0},{16,24},{24,16},{1,9},{9,1},{17,25},{25,17},{2,10},{10... | collective-permute-start | bytes 3080 | tf_op jit(solution)/shard_map/ppermute | solution.py:32
  74.6 11.8 %collective-permute-start.18 = (f32[1,256]{1,0:T(1,128)S(1)}, f32[1,256]{1,0:T(1,128)S(1)}, u32[]{:S(2)}, u32[]{:S(2)}) collective-permute-start(f32[1,256]{1,0:T(1,128)S(1)} %max.36), channel_id=1, source_target_pairs={{0,16},{8,24},{16,0},{24,8},{1,17},{9,25},{17,1},{25,9},{2,18},{10... | collective-permute-start | bytes 3080 | tf_op jit(solution)/shard_map/ppermute | solution.py:32
  75.7 10.7 %collective-permute-start.19 = (f32[1,256]{1,0:T(1,128)S(1)}, f32[1,256]{1,0:T(1,128)S(1)}, u32[]{:S(2)}, u32[]{:S(2)}) collective-permute-start(f32[1,256]{1,0:T(1,128)S(1)} %max.36), channel_id=1, source_target_pairs={{0,24},{8,16},{16,8},{24,0},{1,25},{9,17},{17,9},{25,1},{2,26},{10... | collective-permute-start | bytes 3080 | tf_op jit(solution)/shard_map/ppermute | solution.py:32
  77.7 9.8 %collective-permute-start.23 = (bf16[1152,256]{1,0:T(8,128)(2,1)S(1)}, bf16[1152,256]{1,0:T(8,128)(2,1)S(1)}, u32[]{:S(2)}, u32[]{:S(2)}) collective-permute-start(bf16[1152,256]{1,0:T(8,128)(2,1)S(1)} %collective-permute-done.8.refs_0_), channel_id=1, source_target_pairs={{0,1},{1,0},{2,3},{3,2},{4,5},{5,4},{6,7},{7,6},{8,9},{9,8},{10,11... | collective-permute-start | bytes 1769480 | tf_op jit(solution)/shard_map/ppermute | solution.py:23
  85.1 17.2 %collective-permute-start.24 = (bf16[1152,256]{1,0:T(8,128)(2,1)S(1)}, bf16[1152,256]{1,0:T(8,128)(2,1)S(1)}, u32[]{:S(2)}, u32[]{:S(2)}) collective-permute-start(bf16[1152,256]{1,0:T(8,128)(2,1)S(1)} %collective-permute-done.10), channel_id=1, source_target_pairs={{8,0},{16,24},{9,1},{17,25},{10,2},{18,26},{11,3},{19,27},{12,4},{... | collective-permute-start | bytes 1769480 | tf_op jit(solution)/shard_map/ppermute | solution.py:498
  86.4 3.3 %copy-start.4 = (f32[1,256]{1,0:T(1,128)}, f32[1,256]{1,0:T(1,128)S(1)}, u32[]{:S(2)}) copy-start(f32[1,256]{1,0:T(1,128)S(1)} %add_sqrt_fusion) | copy-start | bytes 3076
  86.6 3.2 %collective-permute-start.22 = (bf16[1152,256]{1,0:T(8,128)(2,1)S(1)}, bf16[1152,256]{1,0:T(8,128)(2,1)S(1)}, u32[]{:S(2)}, u32[]{:S(2)}) collective-permute-start(bf16[1152,256]{1,0:T(8,128)(2,1)S(1)} %add.86.refs_0_), channel_id=1, source_target_pairs={{0,1},{1,0},{2,3},{3,2},{4,5},{5,4},{6,7},{7,6},{8,9},{9,8},{10,11... | collective-permute-start | bytes 1769480 | tf_op jit(solution)/shard_map/ppermute | solution.py:23
  86.9 4.3 %collective-permute-start.21 = (bf16[1024,128]{1,0:T(8,128)(2,1)S(1)}, bf16[1024,128]{1,0:T(8,128)(2,1)S(1)}, u32[]{:S(2)}, u32[]{:S(2)}) collective-permute-start(bf16[1024,128]{1,0:T(8,128)(2,1)S(1)} %get-tuple-element.153), channel_id=1, source_target_pairs={{0,1},{1,0},{2,3},{3,2},{4,5},{5,4},{6,7},{7,6},{8,9},{9,8},{10,11... | collective-permute-start | bytes 786440 | tf_op jit(solution)/shard_map/ppermute | solution.py:23
  88.3 14.1 %copy-start.2 = (bf16[4,8,2,256]{3,2,1,0:T(2,128)(2,1)S(1)}, bf16[4,8,2,256]{3,2,1,0:T(2,128)(2,1)}, u32[]{:S(2)}) copy-start(bf16[4,8,2,256]{3,2,1,0:T(2,128)(2,1)} %param.12) | copy-start | bytes 98308
  102.3 2.0 %collective-permute-start.25 = (bf16[1152,256]{1,0:T(8,128)(2,1)S(1)}, bf16[1152,256]{1,0:T(8,128)(2,1)S(1)}, u32[]{:S(2)}, u32[]{:S(2)}) collective-permute-start(bf16[1152,256]{1,0:T(8,128)(2,1)S(1)} %collective-permute-done.24.refs_0_), channel_id=1, source_target_pairs={{0,1},{1,0},{2,3},{3,2},{4,5},{5,4},{6,7},{7,6},{8,9},{9,8},{10,11... | collective-permute-start | bytes 1769480 | tf_op jit(solution)/shard_map/ppermute | solution.py:23
  106.0 1.6 %collective-permute-start.26 = (bf16[1024,128]{1,0:T(8,128)(2,1)S(1)}, bf16[1024,128]{1,0:T(8,128)(2,1)S(1)}, u32[]{:S(2)}, u32[]{:S(2)}) collective-permute-start(bf16[1024,128]{1,0:T(8,128)(2,1)S(1)} %get-tuple-element.151), channel_id=1, source_target_pairs={{0,1},{1,0},{2,3},{3,2},{4,5},{5,4},{6,7},{7,6},{8,9},{9,8},{10,11... | collective-permute-start | bytes 786440 | tf_op jit(solution)/shard_map/ppermute | solution.py:23
  109.0 7.0 %collective-permute-start.27 = (bf16[272,128]{1,0:T(8,128)(2,1)S(1)}, bf16[272,128]{1,0:T(8,128)(2,1)S(1)}, u32[]{:S(2)}, u32[]{:S(2)}) collective-permute-start(bf16[272,128]{1,0:T(8,128)(2,1)S(1)} %get-tuple-element.131), channel_id=1, source_target_pairs={{0,8},{8,0},{16,24},{24,16},{1,9},{9,1},{17,25},{25,17},{2,10},{10... | collective-permute-start | bytes 208904 | tf_op jit(solution)/shard_map/ppermute | solution.py:32
  109.1 9.0 %collective-permute-start.28 = (bf16[272,128]{1,0:T(8,128)(2,1)S(1)}, bf16[272,128]{1,0:T(8,128)(2,1)S(1)}, u32[]{:S(2)}, u32[]{:S(2)}) collective-permute-start(bf16[272,128]{1,0:T(8,128)(2,1)S(1)} %get-tuple-element.132), channel_id=1, source_target_pairs={{0,16},{8,24},{16,0},{24,8},{1,17},{9,25},{17,1},{25,9},{2,18},{10... | collective-permute-start | bytes 208904 | tf_op jit(solution)/shard_map/ppermute | solution.py:32
  110.8 7.3 %collective-permute-start.29 = (bf16[272,128]{1,0:T(8,128)(2,1)S(1)}, bf16[272,128]{1,0:T(8,128)(2,1)S(1)}, u32[]{:S(2)}, u32[]{:S(2)}) collective-permute-start(bf16[272,128]{1,0:T(8,128)(2,1)S(1)} %get-tuple-element.133), channel_id=1, source_target_pairs={{0,24},{8,16},{16,8},{24,0},{1,25},{9,17},{17,9},{25,1},{2,26},{10... | collective-permute-start | bytes 208904 | tf_op jit(solution)/shard_map/ppermute | solution.py:32
  118.5 1.3 %collective-permute-start.30 = (bf16[32,1024]{1,0:T(8,128)(2,1)S(1)}, bf16[32,1024]{1,0:T(8,128)(2,1)S(1)}, u32[]{:S(2)}, u32[]{:S(2)}) collective-permute-start(bf16[32,1024]{1,0:T(8,128)(2,1)S(1)} %finish.1), channel_id=1, source_target_pairs={{0,1},{1,0},{2,3},{3,2},{4,5},{5,4},{6,7},{7,6},{8,9},{9,8},{10,11... | collective-permute-start | bytes 196616 | tf_op jit(solution)/shard_map/ppermute | solution.py:23

commit v12 on v11

--- a/solution.py
+++ b/solution.py
@@ -49,7 +49,10 @@
         order = partner(lax.axis_index("seq"), jnp.arange(n), n)
         back = lax.all_to_all(jnp.stack(x)[order], "seq", split_axis=0, concat_axis=0)
         return list(back[order])
-    return [x[0]] + [swapped(x[k], "seq", k) for k in range(1, n)]
+    out = [x[0]]
+    for k in range(1, n):
+        out.append(swapped(x[k], "seq", k))
+    return out
 
 
 def pack_kernel(weight, query, out, sem):

time: 121 us -> 121 us (level)
  no operation moved by 1% of the time
where the time goes in v12:
time: 121 us
  waiting for transfers between devices  42.6 us (35%)
  Pallas kernels  36.8 us (30%)
  starting transfers between devices  31.8 us (26%)
  other arithmetic  5.49 us (5%)
  local copies, waits for them, and re-layouts  2.15 us (2%)
  between operations  1.25 us (1%)
    ppermute x10, waiting for transfers between devices, send(): return lax.ppermute(x, 'seq', line_pairs(hop, parity, groups))  31.2 us
    pallas_call x16, Pallas kernels, project(): pl.pallas_call(functools.partial(project_kernel, hops, back, groups, owne...  22 us
    ppermute x10, starting transfers between devices, send(): return lax.ppermute(x, 'seq', line_pairs(hop, parity, groups))  16.1 us
    ppermute x6, starting transfers between devices, swapped(): return lax.ppermute(x, axis, [(i, partner(i, k, n)) for i in range(n)])  8.83 us
    ppermute x6, waiting for transfers between devices, swapped(): return lax.ppermute(x, axis, [(i, partner(i, k, n)) for i in range(n)])  8.69 us
    pallas_call x1, Pallas kernels, load(): pl.pallas_call(functools.partial(load_kernel, owners), out_shape=(jax.Sha...  6.57 us
    pallas_call x1, Pallas kernels, score(): pl.pallas_call(functools.partial(score_kernel, slots, parts, steps, scale...  4.73 us
    ppermute x1, starting transfers between devices, line_project(): far_query = lax.ppermute(own_block[depth:], 'seq', ends)  4.54 us
  transfers between devices with their start and end apart: 31, of which 11 were waited for; matrix products, arithmetic and copies ran while one was open for 4% of the time, Pallas kernels for 28%

profile of v12, /device:TPU:0, one launch (start us, length us, event | category | flops | bytes accessed | tf_op | source)
XLA Modules:
  0.0 120.5 jit_solution(11632715231380881411)
XLA Ops:
  0.6 3.1 %collective-permute-start = (bf16[1024,256]{1,0:T(8,128)(2,1)}, bf16[1024,256]{1,0:T(8,128)(2,1)S(1)}, u32[]{:S(2)}, u32[]{:S(2)}) collective-permute-start(bf16[1024,256]{1,0:T(8,128)(2,1)} %refs_0_), channel_id=1, source_target_pairs={{0,8},{8,0},{16,24},{24,16},{1,9},{9,1},{17,25},{25,17},{2,10},{10... | collective-permute-start | bytes 1572872 | tf_op jit(solution)/shard_map/ppermute | solution.py:501
  3.7 0.7 collective-permute-start.1
  4.5 0.5 collective-permute-start.7
  5.0 0.9 select_bitcast_fusion.query
  6.0 1.0 copy-done
  7.1 1.0 copy-done.1
  8.1 6.6 %load.1 = (bf16[1024,8192]{1,0:T(8,128)(2,1)S(1)}, f32[1024,256]{1,0:T(8,128)S(1)}, f32[1024,256]{1,0:T(8,128)S(1)}) custom-call(s32[2]{0:T(128)S(1)} %pad_add_fusion.place, bf16[1024,8192]{1,0:T(8,128)(2,1)} %hidden.1, bf16[1024,256]{1,0:T(8,128)(2,1)S(1)} %copy-done.1, bf16[1152,256]{1,0:T(8,128)(2,1)S(1)} %pack.1.refs_1_), custom_call_target="tpu_custom_call" | custom-call | flops 1073741824 | bytes 16777216 | tf_op jit(solution)/shard_map/load/pallas_call | solution.py:117
  14.7 1.2 collective-permute-done.refs_0_
  15.9 0.5 collective-permute-start.5
  16.4 4.8 %collective-permute-start.3 = (bf16[1152,256]{1,0:T(8,128)(2,1)S(1)}, bf16[1152,256]{1,0:T(8,128)(2,1)S(1)}, u32[]{:S(2)}, u32[]{:S(2)}) collective-permute-start(bf16[1152,256]{1,0:T(8,128)(2,1)S(1)} %pack.1.refs_1_), channel_id=1, source_target_pairs={{0,8},{8,0},{16,24},{24,16},{1,9},{9,1},{17,25},{25,17},{2,10},{10... | collective-permute-start | bytes 1769480 | tf_op jit(solution)/shard_map/ppermute | solution.py:501
  21.2 0.7 collective-permute-start.2
  21.9 1.4 %project.19.refs_1_ = f32[1024,256]{1,0:T(8,128)S(1)} custom-call(s32[2]{0:T(128)S(1)} %pad_add_fusion.place, bf16[1024,8192]{1,0:T(8,128)(2,1)S(1)} %get-tuple-element.84.left, bf16[1024,256]{1,0:T(8,128)(2,1)S(1)} %collective-permute-done.7.refs_0_, f32[1024,256]{1,0:T(8,128)S(1)} %get-tuple-element.87.refs_1_), custom_call_target="tpu_custom_call", output_to_operand_aliasing={{}: (3, {})} | custom-call | flops 536870912 | bytes 4718592 | tf_op jit(solution)/shard_map/project/pallas_call | solution.py:173
  23.3 1.4 %project.16.refs_2_ = f32[1024,256]{1,0:T(8,128)S(1)} custom-call(s32[2]{0:T(128)S(1)} %pad_add_fusion.place, bf16[1024,8192]{1,0:T(8,128)(2,1)S(1)} %get-tuple-element.84.left, bf16[1024,256]{1,0:T(8,128)(2,1)S(1)} %collective-permute-done.6.refs_0_, f32[1024,256]{1,0:T(8,128)S(1)} %get-tuple-element.86.refs_1_), custom_call_target="tpu_custom_call", output_to_operand_aliasing={{}: (3, {})} | custom-call | flops 536870912 | bytes 4718592 | tf_op jit(solution)/shard_map/project/pallas_call | solution.py:173
  24.8 1.5 %project.17.refs_2_ = f32[1024,256]{1,0:T(8,128)S(1)} custom-call(s32[2]{0:T(128)S(1)} %pad_add_fusion.place, bf16[1024,8192]{1,0:T(8,128)(2,1)S(1)} %get-tuple-element.84.left, bf16[1024,256]{1,0:T(8,128)(2,1)S(1)} %collective-permute-done.refs_0_, bf16[1024,256]{1,0:T(8,128)(2,1)S(1)} %collective-permute-done.1.refs_1_, ...), custom_call_target="tpu_custom_call", output_to_operand_aliasing={{}: (4, {})} | custom-call | flops 1073741824 | bytes 7340032 | tf_op jit(solution)/shard_map/project/pallas_call | solution.py:173
  26.3 1.5 %project.18.refs_1_ = f32[1024,256]{1,0:T(8,128)S(1)} custom-call(s32[2]{0:T(128)S(1)} %pad_add_fusion.place, bf16[1024,8192]{1,0:T(8,128)(2,1)S(1)} %get-tuple-element.84.left, bf16[1024,256]{1,0:T(8,128)(2,1)S(1)} %collective-permute-done.4.refs_0_, bf16[1024,256]{1,0:T(8,128)(2,1)S(1)} %collective-permute-done.5.refs_1_, ...), custom_call_target="tpu_custom_call", output_to_operand_aliasing={{}: (4, {})} | custom-call | flops 1073741824 | bytes 7340032 | tf_op jit(solution)/shard_map/project/pallas_call | solution.py:173
  27.8 6.8 %collective-permute-done.3.refs_0_ = bf16[1152,256]{1,0:T(8,128)(2,1)S(1)} collective-permute-done((bf16[1152,256]{1,0:T(8,128)(2,1)S(1)}, bf16[1152,256]{1,0:T(8,128)(2,1)S(1)}, u32[]{:S(2)}, u32[]{:S(2)}) %collective-permute-start.3) | collective-permute-done | bytes 589856 | tf_op jit(solution)/shard_map/ppermute | solution.py:501
  34.7 1.3 %collective-permute-start.12 = (bf16[1024,256]{1,0:T(8,128)(2,1)S(1)}, bf16[1024,256]{1,0:T(8,128)(2,1)S(1)}, u32[]{:S(2)}, u32[]{:S(2)}) collective-permute-start(bf16[1024,256]{1,0:T(8,128)(2,1)S(1)} %collective-permute-done.1.refs_1_), channel_id=1, source_target_pairs={{8,0},{16,24},{9,1},{17,25},{10,2},{18,26},{11,3},{19,27},{12,4},{... | collective-permute-start | bytes 1572872 | tf_op jit(solution)/shard_map/ppermute | solution.py:501
  36.1 1.4 %collective-permute-start.11 = (bf16[1024,256]{1,0:T(8,128)(2,1)S(1)}, bf16[1024,256]{1,0:T(8,128)(2,1)S(1)}, u32[]{:S(2)}, u32[]{:S(2)}) collective-permute-start(bf16[1024,256]{1,0:T(8,128)(2,1)S(1)} %collective-permute-done.2), channel_id=1, source_target_pairs={{8,0},{16,24},{9,1},{17,25},{10,2},{18,26},{11,3},{19,27},{12,4},{... | collective-permute-start | bytes 1572872 | tf_op jit(solution)/shard_map/ppermute | solution.py:501
  37.5 1.4 %project.20.refs_1_ = f32[1024,256]{1,0:T(8,128)S(1)} custom-call(s32[2]{0:T(128)S(1)} %pad_add_fusion.place, bf16[1024,8192]{1,0:T(8,128)(2,1)S(1)} %get-tuple-element.84.left, bf16[1152,256]{1,0:T(8,128)(2,1)S(1)} %collective-permute-done.3.refs_0_, f32[1024,256]{1,0:T(8,128)S(1)} %project.19.refs_1_), custom_call_target="tpu_custom_call", output_to_operand_aliasing={{}: (3, {})} | custom-call | flops 536870912 | bytes 4718592 | tf_op jit(solution)/shard_map/project/pallas_call | solution.py:173
  39.0 1.4 %project.21.refs_1_ = f32[1024,256]{1,0:T(8,128)S(1)} custom-call(s32[2]{0:T(128)S(1)} %pad_add_fusion.place, bf16[1024,8192]{1,0:T(8,128)(2,1)S(1)} %get-tuple-element.84.left, bf16[1152,256]{1,0:T(8,128)(2,1)S(1)} %collective-permute-done.13.refs_0_, f32[1024,256]{1,0:T(8,128)S(1)} %project.20.refs_1_), custom_call_target="tpu_custom_call", output_to_operand_aliasing={{}: (3, {})} | custom-call | flops 536870912 | bytes 4718592 | tf_op jit(solution)/shard_map/project/pallas_call | solution.py:173
  40.4 10.9 %collective-permute-done.12 = bf16[1024,256]{1,0:T(8,128)(2,1)S(1)} collective-permute-done((bf16[1024,256]{1,0:T(8,128)(2,1)S(1)}, bf16[1024,256]{1,0:T(8,128)(2,1)S(1)}, u32[]{:S(2)}, u32[]{:S(2)}) %collective-permute-start.12) | collective-permute-done | bytes 524320 | tf_op jit(solution)/shard_map/ppermute | solution.py:501
  51.4 0.1 add.74.refs_0_
  51.6 0.6 convert_reduce_fusion
  52.2 0.2 fusion.2
  52.4 0.8 collective-permute-start.8
  53.3 1.4 %project.22.refs_1_ = f32[1024,256]{1,0:T(8,128)S(1)} custom-call(s32[2]{0:T(128)S(1)} %pad_add_fusion.place, bf16[1024,8192]{1,0:T(8,128)(2,1)S(1)} %get-tuple-element.84.left, bf16[1024,256]{1,0:T(8,128)(2,1)S(1)} %add.74.refs_0_, f32[1024,256]{1,0:T(8,128)S(1)} %project.18.refs_1_), custom_call_target="tpu_custom_call", output_to_operand_aliasing={{}: (3, {})} | custom-call | flops 536870912 | bytes 4718592 | tf_op jit(solution)/shard_map/project/pallas_call | solution.py:173
  54.8 1.5 %project.23.refs_1_ = f32[1024,256]{1,0:T(8,128)S(1)} custom-call(s32[2]{0:T(128)S(1)} %pad_add_fusion.place, bf16[1024,8192]{1,0:T(8,128)(2,1)S(1)} %get-tuple-element.84.left, bf16[1024,256]{1,0:T(8,128)(2,1)S(1)} %collective-permute-done.14.refs_0_, f32[1024,256]{1,0:T(8,128)S(1)} %project.22.refs_1_), custom_call_target="tpu_custom_call", output_to_operand_aliasing={{}: (3, {})} | custom-call | flops 536870912 | bytes 4718592 | tf_op jit(solution)/shard_map/project/pallas_call | solution.py:173
  56.2 5.9 %collective-permute-done.11.refs_0_ = bf16[1024,256]{1,0:T(8,128)(2,1)S(1)} collective-permute-done((bf16[1024,256]{1,0:T(8,128)(2,1)S(1)}, bf16[1024,256]{1,0:T(8,128)(2,1)S(1)}, u32[]{:S(2)}, u32[]{:S(2)}) %collective-permute-start.11) | collective-permute-done | bytes 524320 | tf_op jit(solution)/shard_map/ppermute | solution.py:501
  62.1 0.2 fusion.1.count
  62.4 0.7 collective-permute-start.10
  63.1 4.5 %collective-permute-start.20 = (bf16[128,256]{1,0:T(8,128)(2,1)S(1)}, bf16[128,256]{1,0:T(8,128)(2,1)S(1)}, u32[]{:S(2)}, u32[]{:S(2)}) collective-permute-start(bf16[128,256]{1,0:T(8,128)(2,1)S(1)} %slice.79), channel_id=1, source_target_pairs={{0,24},{24,0},{1,25},{25,1},{2,26},{26,2},{3,27},{27,3},{4,28},{28... | collective-permute-start | bytes 196616 | tf_op jit(solution)/shard_map/ppermute | solution.py:530
  67.6 1.3 %collective-permute-start.9 = (bf16[1152,256]{1,0:T(8,128)(2,1)S(1)}, bf16[1152,256]{1,0:T(8,128)(2,1)S(1)}, u32[]{:S(2)}, u32[]{:S(2)}) collective-permute-start(bf16[1152,256]{1,0:T(8,128)(2,1)S(1)} %collective-permute-done.8.refs_0_), channel_id=1, source_target_pairs={{8,0},{16,24},{9,1},{17,25},{10,2},{18,26},{11,3},{19,27},{12,4},{... | collective-permute-start | bytes 1769480 | tf_op jit(solution)/shard_map/ppermute | solution.py:501
  68.9 1.4 %project.24.refs_1_ = f32[1024,256]{1,0:T(8,128)S(1)} custom-call(s32[2]{0:T(128)S(1)} %pad_add_fusion.place, bf16[1024,8192]{1,0:T(8,128)(2,1)S(1)} %get-tuple-element.84.left, bf16[1024,256]{1,0:T(8,128)(2,1)S(1)} %collective-permute-done.11.refs_0_, f32[1024,256]{1,0:T(8,128)S(1)} %project.23.refs_1_), custom_call_target="tpu_custom_call", output_to_operand_aliasing={{}: (3, {})} | custom-call | flops 536870912 | bytes 4718592 | tf_op jit(solution)/shard_map/project/pallas_call | solution.py:173
  70.4 1.6 %project.25 = f32[1024,256]{1,0:T(8,128)S(1)} custom-call(s32[2]{0:T(128)S(1)} %pad_add_fusion.place, bf16[1024,8192]{1,0:T(8,128)(2,1)S(1)} %get-tuple-element.84.left, bf16[1024,256]{1,0:T(8,128)(2,1)S(1)} %collective-permute-done.15.refs_0_, f32[1024,256]{1,0:T(8,128)S(1)} %project.24.refs_1_), custom_call_target="tpu_custom_call", output_to_operand_aliasing={{}: (3, {})} | custom-call | flops 536870912 | bytes 4718592 | tf_op jit(solution)/shard_map/project/pallas_call | solution.py:173
  72.1 0.3 collective-permute-start.16
  72.4 0.9 collective-permute-done.16
  73.3 1.3 %collective-permute-start.17 = (f32[1,256]{1,0:T(1,128)S(1)}, f32[1,256]{1,0:T(1,128)S(1)}, u32[]{:S(2)}, u32[]{:S(2)}) collective-permute-start(f32[1,256]{1,0:T(1,128)S(1)} %max.36), channel_id=1, source_target_pairs={{0,8},{8,0},{16,24},{24,16},{1,9},{9,1},{17,25},{25,17},{2,10},{10... | collective-permute-start | bytes 3080 | tf_op jit(solution)/shard_map/ppermute | solution.py:32
  74.6 1.1 collective-permute-start.18
  75.7 2.0 %collective-permute-start.19 = (f32[1,256]{1,0:T(1,128)S(1)}, f32[1,256]{1,0:T(1,128)S(1)}, u32[]{:S(2)}, u32[]{:S(2)}) collective-permute-start(f32[1,256]{1,0:T(1,128)S(1)} %max.36), channel_id=1, source_target_pairs={{0,24},{8,16},{16,8},{24,0},{1,25},{9,17},{17,9},{25,1},{2,26},{10... | collective-permute-start | bytes 3080 | tf_op jit(solution)/shard_map/ppermute | solution.py:32
  77.8 0.7 project.26.refs_1_
  78.5 6.6 %collective-permute-done.17 = f32[1,256]{1,0:T(1,128)S(1)} collective-permute-done((f32[1,256]{1,0:T(1,128)S(1)}, f32[1,256]{1,0:T(1,128)S(1)}, u32[]{:S(2)}, u32[]{:S(2)}) %collective-permute-start.17) | collective-permute-done | bytes 1056 | tf_op jit(solution)/shard_map/ppermute | solution.py:32
  85.1 1.3 %collective-permute-start.24 = (bf16[1152,256]{1,0:T(8,128)(2,1)S(1)}, bf16[1152,256]{1,0:T(8,128)(2,1)S(1)}, u32[]{:S(2)}, u32[]{:S(2)}) collective-permute-start(bf16[1152,256]{1,0:T(8,128)(2,1)S(1)} %collective-permute-done.10), channel_id=1, source_target_pairs={{8,0},{16,24},{9,1},{17,25},{10,2},{18,26},{11,3},{19,27},{12,4},{... | collective-permute-start | bytes 1769480 | tf_op jit(solution)/shard_map/ppermute | solution.py:501
  86.5 0.1 add.86.refs_0_
  86.7 0.1 minimum_convert_fusion.1
  86.9 0.6 collective-permute-start.21
  87.5 0.7 project.27.refs_1_
  88.3 1.4 %project.28.refs_1_ = f32[1024,256]{1,0:T(8,128)S(1)} custom-call(s32[2]{0:T(128)S(1)} %pad_add_fusion.place, bf16[1024,8192]{1,0:T(8,128)(2,1)S(1)} %get-tuple-element.84.left, bf16[1152,256]{1,0:T(8,128)(2,1)S(1)} %add.86.refs_0_, f32[1024,256]{1,0:T(8,128)S(1)} %project.27.refs_1_), custom_call_target="tpu_custom_call", output_to_operand_aliasing={{}: (3, {})} | custom-call | flops 536870912 | bytes 4718592 | tf_op jit(solution)/shard_map/project/pallas_call | solution.py:173
  89.8 1.4 %project.29.refs_1_ = f32[1024,256]{1,0:T(8,128)S(1)} custom-call(s32[2]{0:T(128)S(1)} %pad_add_fusion.place, bf16[1024,8192]{1,0:T(8,128)(2,1)S(1)} %get-tuple-element.84.left, bf16[1152,256]{1,0:T(8,128)(2,1)S(1)} %collective-permute-done.22.refs_0_, f32[1024,256]{1,0:T(8,128)S(1)} %project.28.refs_1_), custom_call_target="tpu_custom_call", output_to_operand_aliasing={{}: (3, {})} | custom-call | flops 536870912 | bytes 4718592 | tf_op jit(solution)/shard_map/project/pallas_call | solution.py:173
  91.2 4.7 %score.1 = (bf16[4,256,2048]{2,1,0:T(8,128)(2,1)S(1)}, f32[2,256]{1,0:T(2,128)S(1)}, f32[2,256]{1,0:T(2,128)S(1)}, f32[2,256]{1,0:T(2,128)S(1)}, f32[2,256]{1,0:T(2,128)S(1)}) custom-call(s32[4]{0:T(128)S(1)} %iota_xor_fusion.group, bf16[4,128,256]{2,1,0:T(8,128)(2,1)S(1)} %pad_maximum_fusion.query, f32[1,128]{1,0:T(1,128)S(1)} %broadcast_select_fusion.7.smooth, ...), custom_call_target="tpu_custom_call" | custom-call | flops 536870912 | bytes 4194304 | tf_op jit(solution)/shard_map/score/pallas_call | solution.py:244
  96.0 6.4 %collective-permute-done.24.refs_0_ = bf16[1152,256]{1,0:T(8,128)(2,1)S(1)} collective-permute-done((bf16[1152,256]{1,0:T(8,128)(2,1)S(1)}, bf16[1152,256]{1,0:T(8,128)(2,1)S(1)}, u32[]{:S(2)}, u32[]{:S(2)}) %collective-permute-start.24) | collective-permute-done | bytes 589856 | tf_op jit(solution)/shard_map/ppermute | solution.py:501
  102.4 1.4 %project.30.refs_1_ = f32[1024,256]{1,0:T(8,128)S(1)} custom-call(s32[2]{0:T(128)S(1)} %pad_add_fusion.place, bf16[1024,8192]{1,0:T(8,128)(2,1)S(1)} %get-tuple-element.84.left, bf16[1152,256]{1,0:T(8,128)(2,1)S(1)} %collective-permute-done.24.refs_0_, f32[1024,256]{1,0:T(8,128)S(1)} %project.29.refs_1_), custom_call_target="tpu_custom_call", output_to_operand_aliasing={{}: (3, {})} | custom-call | flops 536870912 | bytes 4718592 | tf_op jit(solution)/shard_map/project/pallas_call | solution.py:173
  103.9 0.5 collective-permute-done.25.refs_0_
  104.3 1.4 %project.31 = f32[1024,256]{1,0:T(8,128)S(1)} custom-call(s32[2]{0:T(128)S(1)} %pad_add_fusion.place, bf16[1024,8192]{1,0:T(8,128)(2,1)S(1)} %get-tuple-element.84.left, bf16[1152,256]{1,0:T(8,128)(2,1)S(1)} %collective-permute-done.25.refs_0_, f32[1024,256]{1,0:T(8,128)S(1)} %project.30.refs_1_), custom_call_target="tpu_custom_call", output_to_operand_aliasing={{}: (3, {})} | custom-call | flops 536870912 | bytes 4718592 | tf_op jit(solution)/shard_map/project/pallas_call | solution.py:173
  106.0 0.2 collective-permute-start.26
  106.2 1.3 %weigh_own.1.own = f32[4,256,128]{2,1,0:T(8,128)S(1)} custom-call(bf16[4,256,2048]{2,1,0:T(8,128)(2,1)S(1)} %get-tuple-element.114.probs.refs_0_, bf16[1024,128]{1,0:T(8,128)(2,1)S(1)} %get-tuple-element.152.values), custom_call_target="tpu_custom_call" | custom-call | flops 268435456 | bytes 2097152 | tf_op jit(solution)/shard_map/weigh_own/pallas_call | solution.py:325
  107.6 1.4 %weigh.1 = (bf16[272,128]{1,0:T(8,128)(2,1)S(1)}, bf16[272,128]{1,0:T(8,128)(2,1)S(1)}, bf16[272,128]{1,0:T(8,128)(2,1)S(1)}, bf16[272,128]{1,0:T(8,128)(2,1)S(1)}) custom-call(f32[4,256,128]{2,1,0:T(8,128)S(1)} %weigh_own.1.own, bf16[4,256,2048]{2,1,0:T(8,128)(2,1)S(1)} %get-tuple-element.114.probs.refs_0_, ...), custom_call_target="tpu_custom_call" | custom-call | flops 268435456 | bytes 2097152 | tf_op jit(solution)/shard_map/weigh/pallas_call | solution.py:337
  109.1 1.7 %collective-permute-start.28 = (bf16[272,128]{1,0:T(8,128)(2,1)S(1)}, bf16[272,128]{1,0:T(8,128)(2,1)S(1)}, u32[]{:S(2)}, u32[]{:S(2)}) collective-permute-start(bf16[272,128]{1,0:T(8,128)(2,1)S(1)} %get-tuple-element.132), channel_id=1, source_target_pairs={{0,16},{8,24},{16,0},{24,8},{1,17},{9,25},{17,1},{25,9},{2,18},{10... | collective-permute-start | bytes 208904 | tf_op jit(solution)/shard_map/ppermute | solution.py:32
  110.8 2.6 %collective-permute-start.29 = (bf16[272,128]{1,0:T(8,128)(2,1)S(1)}, bf16[272,128]{1,0:T(8,128)(2,1)S(1)}, u32[]{:S(2)}, u32[]{:S(2)}) collective-permute-start(bf16[272,128]{1,0:T(8,128)(2,1)S(1)} %get-tuple-element.133), channel_id=1, source_target_pairs={{0,24},{8,16},{16,8},{24,0},{1,25},{9,17},{17,9},{25,1},{2,26},{10... | collective-permute-start | bytes 208904 | tf_op jit(solution)/shard_map/ppermute | solution.py:32
  113.5 2.3 %broadcast_select_fusion = bf16[1024,2,256]{2,1,0:T(2,128)(2,1)} fusion(pred[2]{0:T(512)(128)(4,1)S(1)} %iota_compare_fusion.5, bf16[1024,256]{1,0:T(8,128)(2,1)S(1)} %minimum_convert_fusion, bf16[1024,256]{1,0:T(8,128)(2,1)S(1)} %minimum_convert_fusion.1), kind=kLoop, calls=%fused_computation.3 | loop fusion | flops 524288 | bytes 2097154 | tf_op jit(solution)/shard_map/jit(_where)/select_n | solution.py:637
  115.8 0.2 fresh.1
  116.0 2.1 %collective-permute-done.28.refs_2_ = bf16[272,128]{1,0:T(8,128)(2,1)S(1)} collective-permute-done((bf16[272,128]{1,0:T(8,128)(2,1)S(1)}, bf16[272,128]{1,0:T(8,128)(2,1)S(1)}, u32[]{:S(2)}, u32[]{:S(2)}) %collective-permute-start.28) | collective-permute-done | bytes 69664 | tf_op jit(solution)/shard_map/ppermute | solution.py:32
  118.1 0.4 finish.1
  118.6 1.2 %collective-permute-done.30 = bf16[32,1024]{1,0:T(8,128)(2,1)S(1)} collective-permute-done((bf16[32,1024]{1,0:T(8,128)(2,1)S(1)}, bf16[32,1024]{1,0:T(8,128)(2,1)S(1)}, u32[]{:S(2)}, u32[]{:S(2)}) %collective-permute-start.30) | collective-permute-done | bytes 65568 | tf_op jit(solution)/shard_map/ppermute | solution.py:23
  119.9 0.7 maximum_bitcast_fusion
  (71 shorter events, 1.2 us)
Async XLA Ops:
  0.6 15.3 %collective-permute-start = (bf16[1024,256]{1,0:T(8,128)(2,1)}, bf16[1024,256]{1,0:T(8,128)(2,1)S(1)}, u32[]{:S(2)}, u32[]{:S(2)}) collective-permute-start(bf16[1024,256]{1,0:T(8,128)(2,1)} %refs_0_), channel_id=1, source_target_pairs={{0,8},{8,0},{16,24},{24,16},{1,9},{9,1},{17,25},{25,17},{2,10},{10... | collective-permute-start | bytes 1572872 | tf_op jit(solution)/shard_map/ppermute | solution.py:501
  3.7 12.1 %collective-permute-start.1 = (bf16[1024,256]{1,0:T(8,128)(2,1)}, bf16[1024,256]{1,0:T(8,128)(2,1)S(1)}, u32[]{:S(2)}, u32[]{:S(2)}) collective-permute-start(bf16[1024,256]{1,0:T(8,128)(2,1)} %refs_0_), channel_id=1, source_target_pairs={{8,16},{16,8},{9,17},{17,9},{10,18},{18,10},{11,19},{19,11},{12,20... | collective-permute-start | bytes 1572872 | tf_op jit(solution)/shard_map/ppermute | solution.py:501
  4.4 18.9 %collective-permute-start.6 = (bf16[1024,256]{1,0:T(8,128)(2,1)}, bf16[1024,256]{1,0:T(8,128)(2,1)S(1)}, u32[]{:S(2)}, u32[]{:S(2)}) collective-permute-start(bf16[1024,256]{1,0:T(8,128)(2,1)} %refs_0_), channel_id=1, source_target_pairs={{0,1},{1,0},{2,3},{3,2},{4,5},{5,4},{6,7},{7,6},{8,9},{9,8},{10,11... | collective-permute-start | bytes 1572872 | tf_op jit(solution)/shard_map/ppermute | solution.py:23
  4.5 16.6 %collective-permute-start.7 = (bf16[1024,256]{1,0:T(8,128)(2,1)}, bf16[1024,256]{1,0:T(8,128)(2,1)S(1)}, u32[]{:S(2)}, u32[]{:S(2)}) collective-permute-start(bf16[1024,256]{1,0:T(8,128)(2,1)} %weight.1), channel_id=1, source_target_pairs={{0,1},{1,0},{2,3},{3,2},{4,5},{5,4},{6,7},{7,6},{8,9},{9,8},{10,11... | collective-permute-start | bytes 1572872 | tf_op jit(solution)/shard_map/ppermute | solution.py:23
  6.0 1.0 copy-start
  7.1 1.0 copy-start.1
  15.9 10.4 %collective-permute-start.4 = (bf16[1024,256]{1,0:T(8,128)(2,1)S(1)}, bf16[1024,256]{1,0:T(8,128)(2,1)S(1)}, u32[]{:S(2)}, u32[]{:S(2)}) collective-permute-start(bf16[1024,256]{1,0:T(8,128)(2,1)S(1)} %collective-permute-done.refs_0_), channel_id=1, source_target_pairs={{0,1},{1,0},{2,3},{3,2},{4,5},{5,4},{6,7},{7,6},{8,9},{9,8},{10,11... | collective-permute-start | bytes 1572872 | tf_op jit(solution)/shard_map/ppermute | solution.py:23
  15.9 10.4 %collective-permute-start.5 = (bf16[1024,256]{1,0:T(8,128)(2,1)S(1)}, bf16[1024,256]{1,0:T(8,128)(2,1)S(1)}, u32[]{:S(2)}, u32[]{:S(2)}) collective-permute-start(bf16[1024,256]{1,0:T(8,128)(2,1)S(1)} %collective-permute-done.1.refs_1_), channel_id=1, source_target_pairs={{0,1},{1,0},{2,3},{3,2},{4,5},{5,4},{6,7},{7,6},{8,9},{9,8},{10,11... | collective-permute-start | bytes 1572872 | tf_op jit(solution)/shard_map/ppermute | solution.py:23
  16.4 18.2 %collective-permute-start.3 = (bf16[1152,256]{1,0:T(8,128)(2,1)S(1)}, bf16[1152,256]{1,0:T(8,128)(2,1)S(1)}, u32[]{:S(2)}, u32[]{:S(2)}) collective-permute-start(bf16[1152,256]{1,0:T(8,128)(2,1)S(1)} %pack.1.refs_1_), channel_id=1, source_target_pairs={{0,8},{8,0},{16,24},{24,16},{1,9},{9,1},{17,25},{25,17},{2,10},{10... | collective-permute-start | bytes 1769480 | tf_op jit(solution)/shard_map/ppermute | solution.py:501
  21.2 13.5 %collective-permute-start.2 = (bf16[1024,256]{1,0:T(8,128)(2,1)S(1)}, bf16[1024,256]{1,0:T(8,128)(2,1)S(1)}, u32[]{:S(2)}, u32[]{:S(2)}) collective-permute-start(bf16[1024,256]{1,0:T(8,128)(2,1)S(1)} %collective-permute-done.refs_0_), channel_id=1, source_target_pairs={{8,16},{16,8},{9,17},{17,9},{10,18},{18,10},{11,19},{19,11},{12,20... | collective-permute-start | bytes 1572872 | tf_op jit(solution)/shard_map/ppermute | solution.py:501
  24.8 11.2 %copy-start.6 = (s32[32]{0:T(128)S(1)}, s32[32]{0:T(128)}, u32[]{:S(2)}) copy-start(s32[32]{0:T(128)} %param.15) | copy-start | bytes 388
  34.7 4.3 %collective-permute-start.13 = (bf16[1152,256]{1,0:T(8,128)(2,1)S(1)}, bf16[1152,256]{1,0:T(8,128)(2,1)S(1)}, u32[]{:S(2)}, u32[]{:S(2)}) collective-permute-start(bf16[1152,256]{1,0:T(8,128)(2,1)S(1)} %collective-permute-done.3.refs_0_), channel_id=1, source_target_pairs={{0,1},{1,0},{2,3},{3,2},{4,5},{5,4},{6,7},{7,6},{8,9},{9,8},{10,11... | collective-permute-start | bytes 1769480 | tf_op jit(solution)/shard_map/ppermute | solution.py:23
  34.7 16.7 %collective-permute-start.12 = (bf16[1024,256]{1,0:T(8,128)(2,1)S(1)}, bf16[1024,256]{1,0:T(8,128)(2,1)S(1)}, u32[]{:S(2)}, u32[]{:S(2)}) collective-permute-start(bf16[1024,256]{1,0:T(8,128)(2,1)S(1)} %collective-permute-done.1.refs_1_), channel_id=1, source_target_pairs={{8,0},{16,24},{9,1},{17,25},{10,2},{18,26},{11,3},{19,27},{12,4},{... | collective-permute-start | bytes 1572872 | tf_op jit(solution)/shard_map/ppermute | solution.py:501
  36.1 15.6 %copy-start.3 = (s32[32,32]{1,0:T(8,128)S(1)}, s32[32,32]{1,0:T(8,128)}, u32[]{:S(2)}) copy-start(s32[32,32]{1,0:T(8,128)} %param.14) | copy-start | bytes 12292
  36.1 26.0 %collective-permute-start.11 = (bf16[1024,256]{1,0:T(8,128)(2,1)S(1)}, bf16[1024,256]{1,0:T(8,128)(2,1)S(1)}, u32[]{:S(2)}, u32[]{:S(2)}) collective-permute-start(bf16[1024,256]{1,0:T(8,128)(2,1)S(1)} %collective-permute-done.2), channel_id=1, source_target_pairs={{8,0},{16,24},{9,1},{17,25},{10,2},{18,26},{11,3},{19,27},{12,4},{... | collective-permute-start | bytes 1572872 | tf_op jit(solution)/shard_map/ppermute | solution.py:501
  51.5 3.2 %collective-permute-start.14 = (bf16[1024,256]{1,0:T(8,128)(2,1)S(1)}, bf16[1024,256]{1,0:T(8,128)(2,1)S(1)}, u32[]{:S(2)}, u32[]{:S(2)}) collective-permute-start(bf16[1024,256]{1,0:T(8,128)(2,1)S(1)} %add.74.refs_0_), channel_id=1, source_target_pairs={{0,1},{1,0},{2,3},{3,2},{4,5},{5,4},{6,7},{7,6},{8,9},{9,8},{10,11... | collective-permute-start | bytes 1572872 | tf_op jit(solution)/shard_map/ppermute | solution.py:23
  52.4 9.9 %copy-start.5 = (f32[2,256]{1,0:T(2,128)S(1)}, f32[2,256]{1,0:T(2,128)}, u32[]{:S(2)}) copy-start(f32[2,256]{1,0:T(2,128)} %param.11) | copy-start | bytes 6148
  52.4 15.2 %collective-permute-start.8 = (bf16[1152,256]{1,0:T(8,128)(2,1)S(1)}, bf16[1152,256]{1,0:T(8,128)(2,1)S(1)}, u32[]{:S(2)}, u32[]{:S(2)}) collective-permute-start(bf16[1152,256]{1,0:T(8,128)(2,1)S(1)} %pack.1.refs_1_), channel_id=1, source_target_pairs={{8,16},{16,8},{9,17},{17,9},{10,18},{18,10},{11,19},{19,11},{12,20... | collective-permute-start | bytes 1769480 | tf_op jit(solution)/shard_map/ppermute | solution.py:501
  62.1 8.3 %collective-permute-start.15 = (bf16[1024,256]{1,0:T(8,128)(2,1)S(1)}, bf16[1024,256]{1,0:T(8,128)(2,1)S(1)}, u32[]{:S(2)}, u32[]{:S(2)}) collective-permute-start(bf16[1024,256]{1,0:T(8,128)(2,1)S(1)} %collective-permute-done.11.refs_0_), channel_id=1, source_target_pairs={{0,1},{1,0},{2,3},{3,2},{4,5},{5,4},{6,7},{7,6},{8,9},{9,8},{10,11... | collective-permute-start | bytes 1572872 | tf_op jit(solution)/shard_map/ppermute | solution.py:23
  62.4 13.3 %collective-permute-start.10 = (bf16[1152,256]{1,0:T(8,128)(2,1)S(1)}, bf16[1152,256]{1,0:T(8,128)(2,1)S(1)}, u32[]{:S(2)}, u32[]{:S(2)}) collective-permute-start(bf16[1152,256]{1,0:T(8,128)(2,1)S(1)} %collective-permute-done.3.refs_0_), channel_id=1, source_target_pairs={{8,16},{16,8},{9,17},{17,9},{10,18},{18,10},{11,19},{19,11},{12,20... | collective-permute-start | bytes 1769480 | tf_op jit(solution)/shard_map/ppermute | solution.py:501
  63.1 14.7 %collective-permute-start.20 = (bf16[128,256]{1,0:T(8,128)(2,1)S(1)}, bf16[128,256]{1,0:T(8,128)(2,1)S(1)}, u32[]{:S(2)}, u32[]{:S(2)}) collective-permute-start(bf16[128,256]{1,0:T(8,128)(2,1)S(1)} %slice.79), channel_id=1, source_target_pairs={{0,24},{24,0},{1,25},{25,1},{2,26},{26,2},{3,27},{27,3},{4,28},{28... | collective-permute-start | bytes 196616 | tf_op jit(solution)/shard_map/ppermute | solution.py:530
  67.6 18.8 %collective-permute-start.9 = (bf16[1152,256]{1,0:T(8,128)(2,1)S(1)}, bf16[1152,256]{1,0:T(8,128)(2,1)S(1)}, u32[]{:S(2)}, u32[]{:S(2)}) collective-permute-start(bf16[1152,256]{1,0:T(8,128)(2,1)S(1)} %collective-permute-done.8.refs_0_), channel_id=1, source_target_pairs={{8,0},{16,24},{9,1},{17,25},{10,2},{18,26},{11,3},{19,27},{12,4},{... | collective-permute-start | bytes 1769480 | tf_op jit(solution)/shard_map/ppermute | solution.py:501
  72.1 1.2 %collective-permute-start.16 = (f32[1,256]{1,0:T(1,128)S(1)}, f32[1,256]{1,0:T(1,128)S(1)}, u32[]{:S(2)}, u32[]{:S(2)}) collective-permute-start(f32[1,256]{1,0:T(1,128)S(1)} %bitcast.28), channel_id=1, source_target_pairs={{0,1},{1,0},{2,3},{3,2},{4,5},{5,4},{6,7},{7,6},{8,9},{9,8},{10,11... | collective-permute-start | bytes 3080 | tf_op jit(solution)/shard_map/ppermute | solution.py:23
  73.3 11.8 %collective-permute-start.17 = (f32[1,256]{1,0:T(1,128)S(1)}, f32[1,256]{1,0:T(1,128)S(1)}, u32[]{:S(2)}, u32[]{:S(2)}) collective-permute-start(f32[1,256]{1,0:T(1,128)S(1)} %max.36), channel_id=1, source_target_pairs={{0,8},{8,0},{16,24},{24,16},{1,9},{9,1},{17,25},{25,17},{2,10},{10... | collective-permute-start | bytes 3080 | tf_op jit(solution)/shard_map/ppermute | solution.py:32
  74.6 11.8 %collective-permute-start.18 = (f32[1,256]{1,0:T(1,128)S(1)}, f32[1,256]{1,0:T(1,128)S(1)}, u32[]{:S(2)}, u32[]{:S(2)}) collective-permute-start(f32[1,256]{1,0:T(1,128)S(1)} %max.36), channel_id=1, source_target_pairs={{0,16},{8,24},{16,0},{24,8},{1,17},{9,25},{17,1},{25,9},{2,18},{10... | collective-permute-start | bytes 3080 | tf_op jit(solution)/shard_map/ppermute | solution.py:32
  75.7 10.7 %collective-permute-start.19 = (f32[1,256]{1,0:T(1,128)S(1)}, f32[1,256]{1,0:T(1,128)S(1)}, u32[]{:S(2)}, u32[]{:S(2)}) collective-permute-start(f32[1,256]{1,0:T(1,128)S(1)} %max.36), channel_id=1, source_target_pairs={{0,24},{8,16},{16,8},{24,0},{1,25},{9,17},{17,9},{25,1},{2,26},{10... | collective-permute-start | bytes 3080 | tf_op jit(solution)/shard_map/ppermute | solution.py:32
  77.7 9.8 %collective-permute-start.23 = (bf16[1152,256]{1,0:T(8,128)(2,1)S(1)}, bf16[1152,256]{1,0:T(8,128)(2,1)S(1)}, u32[]{:S(2)}, u32[]{:S(2)}) collective-permute-start(bf16[1152,256]{1,0:T(8,128)(2,1)S(1)} %collective-permute-done.8.refs_0_), channel_id=1, source_target_pairs={{0,1},{1,0},{2,3},{3,2},{4,5},{5,4},{6,7},{7,6},{8,9},{9,8},{10,11... | collective-permute-start | bytes 1769480 | tf_op jit(solution)/shard_map/ppermute | solution.py:23
  85.1 17.2 %collective-permute-start.24 = (bf16[1152,256]{1,0:T(8,128)(2,1)S(1)}, bf16[1152,256]{1,0:T(8,128)(2,1)S(1)}, u32[]{:S(2)}, u32[]{:S(2)}) collective-permute-start(bf16[1152,256]{1,0:T(8,128)(2,1)S(1)} %collective-permute-done.10), channel_id=1, source_target_pairs={{8,0},{16,24},{9,1},{17,25},{10,2},{18,26},{11,3},{19,27},{12,4},{... | collective-permute-start | bytes 1769480 | tf_op jit(solution)/shard_map/ppermute | solution.py:501
  86.4 3.3 %copy-start.4 = (f32[1,256]{1,0:T(1,128)}, f32[1,256]{1,0:T(1,128)S(1)}, u32[]{:S(2)}) copy-start(f32[1,256]{1,0:T(1,128)S(1)} %add_sqrt_fusion) | copy-start | bytes 3076
  86.6 3.2 %collective-permute-start.22 = (bf16[1152,256]{1,0:T(8,128)(2,1)S(1)}, bf16[1152,256]{1,0:T(8,128)(2,1)S(1)}, u32[]{:S(2)}, u32[]{:S(2)}) collective-permute-start(bf16[1152,256]{1,0:T(8,128)(2,1)S(1)} %add.86.refs_0_), channel_id=1, source_target_pairs={{0,1},{1,0},{2,3},{3,2},{4,5},{5,4},{6,7},{7,6},{8,9},{9,8},{10,11... | collective-permute-start | bytes 1769480 | tf_op jit(solution)/shard_map/ppermute | solution.py:23
  86.9 4.3 %collective-permute-start.21 = (bf16[1024,128]{1,0:T(8,128)(2,1)S(1)}, bf16[1024,128]{1,0:T(8,128)(2,1)S(1)}, u32[]{:S(2)}, u32[]{:S(2)}) collective-permute-start(bf16[1024,128]{1,0:T(8,128)(2,1)S(1)} %get-tuple-element.153), channel_id=1, source_target_pairs={{0,1},{1,0},{2,3},{3,2},{4,5},{5,4},{6,7},{7,6},{8,9},{9,8},{10,11... | collective-permute-start | bytes 786440 | tf_op jit(solution)/shard_map/ppermute | solution.py:23
  88.3 14.1 %copy-start.2 = (bf16[4,8,2,256]{3,2,1,0:T(2,128)(2,1)S(1)}, bf16[4,8,2,256]{3,2,1,0:T(2,128)(2,1)}, u32[]{:S(2)}) copy-start(bf16[4,8,2,256]{3,2,1,0:T(2,128)(2,1)} %param.12) | copy-start | bytes 98308
  102.3 2.0 %collective-permute-start.25 = (bf16[1152,256]{1,0:T(8,128)(2,1)S(1)}, bf16[1152,256]{1,0:T(8,128)(2,1)S(1)}, u32[]{:S(2)}, u32[]{:S(2)}) collective-permute-start(bf16[1152,256]{1,0:T(8,128)(2,1)S(1)} %collective-permute-done.24.refs_0_), channel_id=1, source_target_pairs={{0,1},{1,0},{2,3},{3,2},{4,5},{5,4},{6,7},{7,6},{8,9},{9,8},{10,11... | collective-permute-start | bytes 1769480 | tf_op jit(solution)/shard_map/ppermute | solution.py:23
  106.0 1.6 %collective-permute-start.26 = (bf16[1024,128]{1,0:T(8,128)(2,1)S(1)}, bf16[1024,128]{1,0:T(8,128)(2,1)S(1)}, u32[]{:S(2)}, u32[]{:S(2)}) collective-permute-start(bf16[1024,128]{1,0:T(8,128)(2,1)S(1)} %get-tuple-element.151), channel_id=1, source_target_pairs={{0,1},{1,0},{2,3},{3,2},{4,5},{5,4},{6,7},{7,6},{8,9},{9,8},{10,11... | collective-permute-start | bytes 786440 | tf_op jit(solution)/shard_map/ppermute | solution.py:23
  109.0 7.0 %collective-permute-start.27 = (bf16[272,128]{1,0:T(8,128)(2,1)S(1)}, bf16[272,128]{1,0:T(8,128)(2,1)S(1)}, u32[]{:S(2)}, u32[]{:S(2)}) collective-permute-start(bf16[272,128]{1,0:T(8,128)(2,1)S(1)} %get-tuple-element.131), channel_id=1, source_target_pairs={{0,8},{8,0},{16,24},{24,16},{1,9},{9,1},{17,25},{25,17},{2,10},{10... | collective-permute-start | bytes 208904 | tf_op jit(solution)/shard_map/ppermute | solution.py:32
  109.1 9.0 %collective-permute-start.28 = (bf16[272,128]{1,0:T(8,128)(2,1)S(1)}, bf16[272,128]{1,0:T(8,128)(2,1)S(1)}, u32[]{:S(2)}, u32[]{:S(2)}) collective-permute-start(bf16[272,128]{1,0:T(8,128)(2,1)S(1)} %get-tuple-element.132), channel_id=1, source_target_pairs={{0,16},{8,24},{16,0},{24,8},{1,17},{9,25},{17,1},{25,9},{2,18},{10... | collective-permute-start | bytes 208904 | tf_op jit(solution)/shard_map/ppermute | solution.py:32
  110.8 7.3 %collective-permute-start.29 = (bf16[272,128]{1,0:T(8,128)(2,1)S(1)}, bf16[272,128]{1,0:T(8,128)(2,1)S(1)}, u32[]{:S(2)}, u32[]{:S(2)}) collective-permute-start(bf16[272,128]{1,0:T(8,128)(2,1)S(1)} %get-tuple-element.133), channel_id=1, source_target_pairs={{0,24},{8,16},{16,8},{24,0},{1,25},{9,17},{17,9},{25,1},{2,26},{10... | collective-permute-start | bytes 208904 | tf_op jit(solution)/shard_map/ppermute | solution.py:32
  118.5 1.3 %collective-permute-start.30 = (bf16[32,1024]{1,0:T(8,128)(2,1)S(1)}, bf16[32,1024]{1,0:T(8,128)(2,1)S(1)}, u32[]{:S(2)}, u32[]{:S(2)}) collective-permute-start(bf16[32,1024]{1,0:T(8,128)(2,1)S(1)} %finish.1), channel_id=1, source_target_pairs={{0,1},{1,0},{2,3},{3,2},{4,5},{5,4},{6,7},{7,6},{8,9},{9,8},{10,11... | collective-permute-start | bytes 196616 | tf_op jit(solution)/shard_map/ppermute | solution.py:23

commit v13 on v12

--- a/solution.py
+++ b/solution.py
@@ -1,4 +1,5 @@
 import functools
+import math
 
 import jax
 import jax.numpy as jnp
@@ -139,18 +140,17 @@
     )(place, hidden, key_weight, value_weight)
 
 
-def project_kernel(hops, back, groups, owners, place, left, *refs):
+def project_kernel(depth, start, hops, back, groups, owners, place, left, *refs):
     count = len(hops)
-    weights, total = refs[:count], refs[count]
+    weights = refs[:count]
     out, held, arrived = refs[-3:]
-    depth = held.shape[1]
+    size = held.shape[1]
     copies = [
-        pltpu.make_async_copy(weights[j].at[pl.ds(0, depth)], held.at[j], arrived.at[j])
+        pltpu.make_async_copy(weights[j].at[pl.ds(0, size)], held.at[j], arrived.at[j])
         for j in range(count)
     ]
     for copy in copies:
         copy.start()
-    out[...] = total[...]
     owner = lax.rem(place[1] + owners - back, owners)
     for j, copy in enumerate(copies):
         copy.wait()
@@ -161,30 +161,32 @@
 
         @pl.when((group >= 0) & (group < groups))
         def _(j=j, group=group):
-            block = pl.ds(pl.multiple_of((group * owners + owner) * depth, depth), depth)
+            first = (group * owners + owner) * depth + start
+            block = pl.ds(pl.multiple_of(first, math.gcd(depth, start)), size)
             out[...] += jnp.dot(left[:, block], held[j], preferred_element_type=jnp.float32)
 
 
-def project(hidden, total, weights, depth, place, hops, back, groups, owners):
+def project(hidden, total, weights, depth, part, place, hops, back, groups, owners):
     tokens = hidden.shape[0]
     columns = weights[0].shape[1]
     count = len(weights)
+    size = part[1] - part[0]
     whole = pl.BlockSpec(memory_space=pltpu.VMEM)
     return pl.pallas_call(
-        functools.partial(project_kernel, hops, back, groups, owners),
+        functools.partial(project_kernel, depth, part[0], hops, back, groups, owners),
         out_shape=jax.ShapeDtypeStruct((tokens, columns), jnp.float32),
         in_specs=[pl.BlockSpec(memory_space=pltpu.SMEM), whole]
         + [pl.BlockSpec(memory_space=pl.ANY)] * count
         + [whole],
         out_specs=whole,
         scratch_shapes=[
-            pltpu.VMEM((count, depth, columns), weights[0].dtype),
+            pltpu.VMEM((count, size, columns), weights[0].dtype),
             pltpu.SemaphoreType.DMA((count,)),
         ],
         compiler_params=pltpu.CompilerParams(vmem_limit_bytes=12 * 2**20),
         cost_estimate=pl.CostEstimate(
-            flops=2 * tokens * depth * columns * count,
-            bytes_accessed=2 * count * depth * (tokens + columns) + 8 * tokens * columns,
+            flops=2 * tokens * size * columns * count,
+            bytes_accessed=2 * count * size * (tokens + columns) + 8 * tokens * columns,
             transcendentals=0,
         ),
         input_output_aliases={2 + count: 0},
@@ -500,13 +502,14 @@
     def send(x, hop, parity):
         return lax.ppermute(x, "seq", line_pairs(hop, parity, groups))
 
-    def absorb(name, blocks, hops, first=0):
+    def absorb(name, blocks, hops, first=0, part=None):
+        part = part or (0, depth)
         passed = [[shifted(block, "rep", k) for block in blocks] for k in range(1, owners)]
         for k, ready in enumerate([blocks] + passed):
             if k < first:
                 continue
             totals[name] = project(
-                hidden, totals[name], ready, depth, early[0], hops, k, groups, owners
+                hidden, totals[name], ready, depth, part, early[0], hops, k, groups, owners
             )
 
     totals = {}
@@ -543,7 +546,9 @@
     top = chip_top(raw_keys)
     smooth = smooth_of(top)
     vb1, vb2, top = barrier((vb1, vb2, top))
-    va3 = send(vb2, 3, 0)
+    cut = depth * 3 // 4
+    va3 = send(vb2[:cut], 3, 0)
+    va3_rest = lax.ppermute(vb2[cut:depth], "seq", line_pairs(3, 0, groups))
     absorb("v", [vb1], (((1, 1),),))
     va2, vb2, smooth = barrier((va2, vb2, smooth))
     absorb("v", [va2 + vb2], (((0, 2), (1, 2)),))
@@ -558,7 +563,9 @@
         args, totals["v"] = barrier((args, totals["v"]))
         probs, stats = scored(*args)
         block, stats = barrier((va3, stats))
-        absorb("v", [block], (((0, 3),),))
+        absorb("v", [block], (((0, 3),),), part=(0, cut))
+        rest, totals["v"] = barrier((va3_rest, totals["v"]))
+        absorb("v", [rest], (((0, 3),),), part=(cut, depth))
         return probs, stats, totals["v"]
 
     return raw_keys, smooth, queries, early, finish_values

time: 121 us -> 124 us (1.025)
  starting transfers between devices: 31.8 us -> 39.9 us
  waiting for transfers between devices: 42.6 us -> 37.3 us
    ppermute x6, starting transfers between devices: 8.83 us -> 15.4 us  [swapped(): return lax.ppermute(x, axis, [(i, partner(i, k, n)) for i in range(n)])]
    ppermute x6, waiting for transfers between devices: 8.69 us -> 2.38 us  [swapped(): return lax.ppermute(x, axis, [(i, partner(i, k, n)) for i in range(n)])]
    ppermute x0 -> x1, waiting for transfers between devices: none -> 3.77 us  [line_project(): va3_rest = lax.ppermute(vb2[cut:depth], 'seq', line_pairs(3, 0, groups))]
    ppermute x10, waiting for transfers between devices: 31.2 us -> 28.7 us  [send(): return lax.ppermute(x, 'seq', line_pairs(hop, parity, groups))]
    ppermute x0 -> x1, starting transfers between devices: none -> 1.29 us  [line_project(): va3_rest = lax.ppermute(vb2[cut:depth], 'seq', line_pairs(3, 0, groups))]
    ppermute x14 -> x15, waiting for transfers between devices: 2.73 us -> 2.5 us  [shifted(): return lax.ppermute(x, axis, [(i, (i + k) % n) for i in range(n)])]
    pallas_call x16 -> x18, Pallas kernels: 22 us -> 21.9 us  [project(): pl.pallas_call(functools.partial(project_kernel, depth, part[0], hops, ba...]
  transfers between devices with their start and end apart: 31 -> 33, of which waited for: 11 -> 11; matrix products, arithmetic and copies ran while one was open for 4% -> 4% of each run, Pallas kernels for 28% -> 27%
where the time goes in v13:
time: 124 us; the launch traced here: 123 us
  starting transfers between devices  39.9 us (32%)
  waiting for transfers between devices  37.3 us (30%)
  Pallas kernels  36.7 us (30%)
  other arithmetic  5.49 us (4%)
  local copies, waits for them, and re-layouts  2.19 us (2%)
  between operations  1.31 us (1%)
    ppermute x10, waiting for transfers between devices, send(): return lax.ppermute(x, 'seq', line_pairs(hop, parity, groups))  28.7 us
    pallas_call x18, Pallas kernels, project(): pl.pallas_call(functools.partial(project_kernel, depth, part[0], hops, ba...  21.9 us
    ppermute x10, starting transfers between devices, send(): return lax.ppermute(x, 'seq', line_pairs(hop, parity, groups))  16.2 us
    ppermute x6, starting transfers between devices, swapped(): return lax.ppermute(x, axis, [(i, partner(i, k, n)) for i in range(n)])  15.4 us
    pallas_call x1, Pallas kernels, load(): pl.pallas_call(functools.partial(load_kernel, owners), out_shape=(jax.Sha...  6.57 us
    pallas_call x1, Pallas kernels, score(): pl.pallas_call(functools.partial(score_kernel, slots, parts, steps, scale...  4.73 us
    ppermute x1, starting transfers between devices, line_project(): far_query = lax.ppermute(own_block[depth:], 'seq', ends)  4.54 us
    ppermute x1, waiting for transfers between devices, line_project(): va3_rest = lax.ppermute(vb2[cut:depth], 'seq', line_pairs(3, 0, groups))  3.77 us
  transfers between devices with their start and end apart: 33, of which 11 were waited for; matrix products, arithmetic and copies ran while one was open for 4% of the time, Pallas kernels for 27%

profile of v13, /device:TPU:0, one launch (start us, length us, event | category | flops | bytes accessed | tf_op | source)
XLA Modules:
  0.0 123.3 jit_solution(731023325722809254)
XLA Ops:
  0.6 3.1 %collective-permute-start = (bf16[1024,256]{1,0:T(8,128)(2,1)}, bf16[1024,256]{1,0:T(8,128)(2,1)S(1)}, u32[]{:S(2)}, u32[]{:S(2)}) collective-permute-start(bf16[1024,256]{1,0:T(8,128)(2,1)} %refs_0_), channel_id=1, source_target_pairs={{0,8},{8,0},{16,24},{24,16},{1,9},{9,1},{17,25},{25,17},{2,10},{10... | collective-permute-start | bytes 1572872 | tf_op jit(solution)/shard_map/ppermute | solution.py:503
  3.7 0.7 collective-permute-start.1
  4.5 0.5 collective-permute-start.7
  5.0 0.9 select_bitcast_fusion.query
  6.0 1.0 copy-done
  7.1 1.0 copy-done.1
  8.1 6.6 %load.1 = (bf16[1024,8192]{1,0:T(8,128)(2,1)S(1)}, f32[1024,256]{1,0:T(8,128)S(1)}, f32[1024,256]{1,0:T(8,128)S(1)}) custom-call(s32[2]{0:T(128)S(1)} %pad_add_fusion.place, bf16[1024,8192]{1,0:T(8,128)(2,1)} %hidden.1, bf16[1024,256]{1,0:T(8,128)(2,1)S(1)} %copy-done.1, bf16[1152,256]{1,0:T(8,128)(2,1)S(1)} %pack.1.refs_1_), custom_call_target="tpu_custom_call" | custom-call | flops 1073741824 | bytes 16777216 | tf_op jit(solution)/shard_map/load/pallas_call | solution.py:118
  14.7 1.2 collective-permute-done.refs_0_
  15.9 0.5 collective-permute-start.5
  16.4 4.8 %collective-permute-start.3 = (bf16[1152,256]{1,0:T(8,128)(2,1)S(1)}, bf16[1152,256]{1,0:T(8,128)(2,1)S(1)}, u32[]{:S(2)}, u32[]{:S(2)}) collective-permute-start(bf16[1152,256]{1,0:T(8,128)(2,1)S(1)} %pack.1.refs_1_), channel_id=1, source_target_pairs={{0,8},{8,0},{16,24},{24,16},{1,9},{9,1},{17,25},{25,17},{2,10},{10... | collective-permute-start | bytes 1769480 | tf_op jit(solution)/shard_map/ppermute | solution.py:503
  21.2 0.7 collective-permute-start.2
  21.9 1.3 %project.18.refs_2_ = f32[1024,256]{1,0:T(8,128)S(1)} custom-call(s32[2]{0:T(128)S(1)} %pad_add_fusion.place, bf16[1024,8192]{1,0:T(8,128)(2,1)S(1)} %get-tuple-element.86.left, bf16[1024,256]{1,0:T(8,128)(2,1)S(1)} %collective-permute-done.6.refs_0_, f32[1024,256]{1,0:T(8,128)S(1)} %get-tuple-element.88.refs_1_), custom_call_target="tpu_custom_call", output_to_operand_aliasing={{}: (3, {})} | custom-call | flops 536870912 | bytes 4718592 | tf_op jit(solution)/shard_map/project/pallas_call | solution.py:175
  23.2 1.3 %project.21.refs_1_ = f32[1024,256]{1,0:T(8,128)S(1)} custom-call(s32[2]{0:T(128)S(1)} %pad_add_fusion.place, bf16[1024,8192]{1,0:T(8,128)(2,1)S(1)} %get-tuple-element.86.left, bf16[1024,256]{1,0:T(8,128)(2,1)S(1)} %collective-permute-done.7.refs_0_, f32[1024,256]{1,0:T(8,128)S(1)} %get-tuple-element.89.refs_1_), custom_call_target="tpu_custom_call", output_to_operand_aliasing={{}: (3, {})} | custom-call | flops 536870912 | bytes 4718592 | tf_op jit(solution)/shard_map/project/pallas_call | solution.py:175
  24.5 1.4 %project.19.refs_2_ = f32[1024,256]{1,0:T(8,128)S(1)} custom-call(s32[2]{0:T(128)S(1)} %pad_add_fusion.place, bf16[1024,8192]{1,0:T(8,128)(2,1)S(1)} %get-tuple-element.86.left, bf16[1024,256]{1,0:T(8,128)(2,1)S(1)} %collective-permute-done.refs_0_, bf16[1024,256]{1,0:T(8,128)(2,1)S(1)} %collective-permute-done.1.refs_1_, ...), custom_call_target="tpu_custom_call", output_to_operand_aliasing={{}: (4, {})} | custom-call | flops 1073741824 | bytes 7340032 | tf_op jit(solution)/shard_map/project/pallas_call | solution.py:175
  25.9 1.4 %project.20.refs_1_ = f32[1024,256]{1,0:T(8,128)S(1)} custom-call(s32[2]{0:T(128)S(1)} %pad_add_fusion.place, bf16[1024,8192]{1,0:T(8,128)(2,1)S(1)} %get-tuple-element.86.left, bf16[1024,256]{1,0:T(8,128)(2,1)S(1)} %collective-permute-done.4.refs_0_, bf16[1024,256]{1,0:T(8,128)(2,1)S(1)} %collective-permute-done.5.refs_1_, ...), custom_call_target="tpu_custom_call", output_to_operand_aliasing={{}: (4, {})} | custom-call | flops 1073741824 | bytes 7340032 | tf_op jit(solution)/shard_map/project/pallas_call | solution.py:175
  27.3 7.4 %collective-permute-done.3.refs_0_ = bf16[1152,256]{1,0:T(8,128)(2,1)S(1)} collective-permute-done((bf16[1152,256]{1,0:T(8,128)(2,1)S(1)}, bf16[1152,256]{1,0:T(8,128)(2,1)S(1)}, u32[]{:S(2)}, u32[]{:S(2)}) %collective-permute-start.3) | collective-permute-done | bytes 589856 | tf_op jit(solution)/shard_map/ppermute | solution.py:503
  34.7 1.3 %collective-permute-start.12 = (bf16[1024,256]{1,0:T(8,128)(2,1)S(1)}, bf16[1024,256]{1,0:T(8,128)(2,1)S(1)}, u32[]{:S(2)}, u32[]{:S(2)}) collective-permute-start(bf16[1024,256]{1,0:T(8,128)(2,1)S(1)} %collective-permute-done.1.refs_1_), channel_id=1, source_target_pairs={{8,0},{16,24},{9,1},{17,25},{10,2},{18,26},{11,3},{19,27},{12,4},{... | collective-permute-start | bytes 1572872 | tf_op jit(solution)/shard_map/ppermute | solution.py:503
  36.1 1.4 %collective-permute-start.11 = (bf16[1024,256]{1,0:T(8,128)(2,1)S(1)}, bf16[1024,256]{1,0:T(8,128)(2,1)S(1)}, u32[]{:S(2)}, u32[]{:S(2)}) collective-permute-start(bf16[1024,256]{1,0:T(8,128)(2,1)S(1)} %collective-permute-done.2), channel_id=1, source_target_pairs={{8,0},{16,24},{9,1},{17,25},{10,2},{18,26},{11,3},{19,27},{12,4},{... | collective-permute-start | bytes 1572872 | tf_op jit(solution)/shard_map/ppermute | solution.py:503
  37.5 1.3 %project.22.refs_1_ = f32[1024,256]{1,0:T(8,128)S(1)} custom-call(s32[2]{0:T(128)S(1)} %pad_add_fusion.place, bf16[1024,8192]{1,0:T(8,128)(2,1)S(1)} %get-tuple-element.86.left, bf16[1152,256]{1,0:T(8,128)(2,1)S(1)} %collective-permute-done.3.refs_0_, f32[1024,256]{1,0:T(8,128)S(1)} %project.21.refs_1_), custom_call_target="tpu_custom_call", output_to_operand_aliasing={{}: (3, {})} | custom-call | flops 536870912 | bytes 4718592 | tf_op jit(solution)/shard_map/project/pallas_call | solution.py:175
  38.8 1.3 %project.23.refs_1_ = f32[1024,256]{1,0:T(8,128)S(1)} custom-call(s32[2]{0:T(128)S(1)} %pad_add_fusion.place, bf16[1024,8192]{1,0:T(8,128)(2,1)S(1)} %get-tuple-element.86.left, bf16[1152,256]{1,0:T(8,128)(2,1)S(1)} %collective-permute-done.13.refs_0_, f32[1024,256]{1,0:T(8,128)S(1)} %project.22.refs_1_), custom_call_target="tpu_custom_call", output_to_operand_aliasing={{}: (3, {})} | custom-call | flops 536870912 | bytes 4718592 | tf_op jit(solution)/shard_map/project/pallas_call | solution.py:175
  40.2 11.2 %collective-permute-done.12 = bf16[1024,256]{1,0:T(8,128)(2,1)S(1)} collective-permute-done((bf16[1024,256]{1,0:T(8,128)(2,1)S(1)}, bf16[1024,256]{1,0:T(8,128)(2,1)S(1)}, u32[]{:S(2)}, u32[]{:S(2)}) %collective-permute-start.12) | collective-permute-done | bytes 524320 | tf_op jit(solution)/shard_map/ppermute | solution.py:503
  51.6 0.6 convert_reduce_fusion
  52.4 0.8 collective-permute-start.8
  53.3 1.3 %project.24.refs_1_ = f32[1024,256]{1,0:T(8,128)S(1)} custom-call(s32[2]{0:T(128)S(1)} %pad_add_fusion.place, bf16[1024,8192]{1,0:T(8,128)(2,1)S(1)} %get-tuple-element.86.left, bf16[1024,256]{1,0:T(8,128)(2,1)S(1)} %add.74.refs_0_, f32[1024,256]{1,0:T(8,128)S(1)} %project.20.refs_1_), custom_call_target="tpu_custom_call", output_to_operand_aliasing={{}: (3, {})} | custom-call | flops 536870912 | bytes 4718592 | tf_op jit(solution)/shard_map/project/pallas_call | solution.py:175
  54.6 1.3 %project.25.refs_1_ = f32[1024,256]{1,0:T(8,128)S(1)} custom-call(s32[2]{0:T(128)S(1)} %pad_add_fusion.place, bf16[1024,8192]{1,0:T(8,128)(2,1)S(1)} %get-tuple-element.86.left, bf16[1024,256]{1,0:T(8,128)(2,1)S(1)} %collective-permute-done.14.refs_0_, f32[1024,256]{1,0:T(8,128)S(1)} %project.24.refs_1_), custom_call_target="tpu_custom_call", output_to_operand_aliasing={{}: (3, {})} | custom-call | flops 536870912 | bytes 4718592 | tf_op jit(solution)/shard_map/project/pallas_call | solution.py:175
  55.9 6.2 %collective-permute-done.11.refs_0_ = bf16[1024,256]{1,0:T(8,128)(2,1)S(1)} collective-permute-done((bf16[1024,256]{1,0:T(8,128)(2,1)S(1)}, bf16[1024,256]{1,0:T(8,128)(2,1)S(1)}, u32[]{:S(2)}, u32[]{:S(2)}) %collective-permute-start.11) | collective-permute-done | bytes 524320 | tf_op jit(solution)/shard_map/ppermute | solution.py:503
  62.1 0.2 fusion.1.count
  62.4 0.7 collective-permute-start.10
  63.1 4.5 %collective-permute-start.20 = (bf16[128,256]{1,0:T(8,128)(2,1)S(1)}, bf16[128,256]{1,0:T(8,128)(2,1)S(1)}, u32[]{:S(2)}, u32[]{:S(2)}) collective-permute-start(bf16[128,256]{1,0:T(8,128)(2,1)S(1)} %slice.85), channel_id=1, source_target_pairs={{0,24},{24,0},{1,25},{25,1},{2,26},{26,2},{3,27},{27,3},{4,28},{28... | collective-permute-start | bytes 196616 | tf_op jit(solution)/shard_map/ppermute | solution.py:533
  67.6 1.3 %collective-permute-start.9 = (bf16[1152,256]{1,0:T(8,128)(2,1)S(1)}, bf16[1152,256]{1,0:T(8,128)(2,1)S(1)}, u32[]{:S(2)}, u32[]{:S(2)}) collective-permute-start(bf16[1152,256]{1,0:T(8,128)(2,1)S(1)} %collective-permute-done.8.refs_0_), channel_id=1, source_target_pairs={{8,0},{16,24},{9,1},{17,25},{10,2},{18,26},{11,3},{19,27},{12,4},{... | collective-permute-start | bytes 1769480 | tf_op jit(solution)/shard_map/ppermute | solution.py:503
  68.9 1.3 %project.26.refs_1_ = f32[1024,256]{1,0:T(8,128)S(1)} custom-call(s32[2]{0:T(128)S(1)} %pad_add_fusion.place, bf16[1024,8192]{1,0:T(8,128)(2,1)S(1)} %get-tuple-element.86.left, bf16[1024,256]{1,0:T(8,128)(2,1)S(1)} %collective-permute-done.11.refs_0_, f32[1024,256]{1,0:T(8,128)S(1)} %project.25.refs_1_), custom_call_target="tpu_custom_call", output_to_operand_aliasing={{}: (3, {})} | custom-call | flops 536870912 | bytes 4718592 | tf_op jit(solution)/shard_map/project/pallas_call | solution.py:175
  70.3 1.3 %project.27 = f32[1024,256]{1,0:T(8,128)S(1)} custom-call(s32[2]{0:T(128)S(1)} %pad_add_fusion.place, bf16[1024,8192]{1,0:T(8,128)(2,1)S(1)} %get-tuple-element.86.left, bf16[1024,256]{1,0:T(8,128)(2,1)S(1)} %collective-permute-done.15.refs_0_, f32[1024,256]{1,0:T(8,128)S(1)} %project.26.refs_1_), custom_call_target="tpu_custom_call", output_to_operand_aliasing={{}: (3, {})} | custom-call | flops 536870912 | bytes 4718592 | tf_op jit(solution)/shard_map/project/pallas_call | solution.py:175
  71.7 0.3 collective-permute-start.16
  72.0 0.9 collective-permute-done.16
  72.9 1.2 collective-permute-start.19
  74.1 1.5 %collective-permute-start.18 = (f32[1,256]{1,0:T(1,128)S(1)}, f32[1,256]{1,0:T(1,128)S(1)}, u32[]{:S(2)}, u32[]{:S(2)}) collective-permute-start(f32[1,256]{1,0:T(1,128)S(1)} %max.36), channel_id=1, source_target_pairs={{0,16},{8,24},{16,0},{24,8},{1,17},{9,25},{17,1},{25,9},{2,18},{10... | collective-permute-start | bytes 3080 | tf_op jit(solution)/shard_map/ppermute | solution.py:33
  75.6 8.2 %collective-permute-start.17 = (f32[1,256]{1,0:T(1,128)S(1)}, f32[1,256]{1,0:T(1,128)S(1)}, u32[]{:S(2)}, u32[]{:S(2)}) collective-permute-start(f32[1,256]{1,0:T(1,128)S(1)} %max.36), channel_id=1, source_target_pairs={{0,8},{8,0},{16,24},{24,16},{1,9},{9,1},{17,25},{25,17},{2,10},{10... | collective-permute-start | bytes 3080 | tf_op jit(solution)/shard_map/ppermute | solution.py:33
  83.9 0.6 project.28.refs_1_
  84.5 1.5 %collective-permute-start.25 = (bf16[768,256]{1,0:T(8,128)(2,1)S(1)}, bf16[768,256]{1,0:T(8,128)(2,1)S(1)}, u32[]{:S(2)}, u32[]{:S(2)}) collective-permute-start(bf16[768,256]{1,0:T(8,128)(2,1)S(1)} %slice.93), channel_id=1, source_target_pairs={{8,0},{16,24},{9,1},{17,25},{10,2},{18,26},{11,3},{19,27},{12,4},{... | collective-permute-start | bytes 1179656 | tf_op jit(solution)/shard_map/ppermute | solution.py:503
  86.2 0.6 collective-permute-start.22
  87.2 0.6 project.29.refs_1_
  87.8 1.3 %project.30.refs_1_ = f32[1024,256]{1,0:T(8,128)S(1)} custom-call(s32[2]{0:T(128)S(1)} %pad_add_fusion.place, bf16[1024,8192]{1,0:T(8,128)(2,1)S(1)} %get-tuple-element.86.left, bf16[1152,256]{1,0:T(8,128)(2,1)S(1)} %add.86.refs_0_, f32[1024,256]{1,0:T(8,128)S(1)} %project.29.refs_1_), custom_call_target="tpu_custom_call", output_to_operand_aliasing={{}: (3, {})} | custom-call | flops 536870912 | bytes 4718592 | tf_op jit(solution)/shard_map/project/pallas_call | solution.py:175
  89.1 1.3 %project.31.refs_1_ = f32[1024,256]{1,0:T(8,128)S(1)} custom-call(s32[2]{0:T(128)S(1)} %pad_add_fusion.place, bf16[1024,8192]{1,0:T(8,128)(2,1)S(1)} %get-tuple-element.86.left, bf16[1152,256]{1,0:T(8,128)(2,1)S(1)} %collective-permute-done.22.refs_0_, f32[1024,256]{1,0:T(8,128)S(1)} %project.30.refs_1_), custom_call_target="tpu_custom_call", output_to_operand_aliasing={{}: (3, {})} | custom-call | flops 536870912 | bytes 4718592 | tf_op jit(solution)/shard_map/project/pallas_call | solution.py:175
  90.5 4.7 %score.1 = (bf16[4,256,2048]{2,1,0:T(8,128)(2,1)S(1)}, f32[2,256]{1,0:T(2,128)S(1)}, f32[2,256]{1,0:T(2,128)S(1)}, f32[2,256]{1,0:T(2,128)S(1)}, f32[2,256]{1,0:T(2,128)S(1)}) custom-call(s32[4]{0:T(128)S(1)} %iota_xor_fusion.group, bf16[4,128,256]{2,1,0:T(8,128)(2,1)S(1)} %pad_maximum_fusion.query, f32[1,128]{1,0:T(1,128)S(1)} %broadcast_select_fusion.7.smooth, ...), custom_call_target="tpu_custom_call" | custom-call | flops 536870912 | bytes 4194304 | tf_op jit(solution)/shard_map/score/pallas_call | solution.py:246
  95.2 2.7 %collective-permute-done.25.refs_0_ = bf16[768,256]{1,0:T(8,128)(2,1)S(1)} collective-permute-done((bf16[768,256]{1,0:T(8,128)(2,1)S(1)}, bf16[768,256]{1,0:T(8,128)(2,1)S(1)}, u32[]{:S(2)}, u32[]{:S(2)}) %collective-permute-start.25) | collective-permute-done | bytes 393248 | tf_op jit(solution)/shard_map/ppermute | solution.py:503
  98.0 1.3 %collective-permute-start.24 = (bf16[256,256]{1,0:T(8,128)(2,1)S(1)}, bf16[256,256]{1,0:T(8,128)(2,1)S(1)}, u32[]{:S(2)}, u32[]{:S(2)}) collective-permute-start(bf16[256,256]{1,0:T(8,128)(2,1)S(1)} %slice.92), channel_id=1, source_target_pairs={{8,0},{16,24},{9,1},{17,25},{10,2},{18,26},{11,3},{19,27},{12,4},{... | collective-permute-start | bytes 393224 | tf_op jit(solution)/shard_map/ppermute | solution.py:551
  99.3 1.3 %project.32.refs_1_ = f32[1024,256]{1,0:T(8,128)S(1)} custom-call(s32[2]{0:T(128)S(1)} %pad_add_fusion.place, bf16[1024,8192]{1,0:T(8,128)(2,1)S(1)} %get-tuple-element.86.left, bf16[768,256]{1,0:T(8,128)(2,1)S(1)} %collective-permute-done.25.refs_0_, f32[1024,256]{1,0:T(8,128)S(1)} %project.31.refs_1_), custom_call_target="tpu_custom_call", output_to_operand_aliasing={{}: (3, {})} | custom-call | flops 402653184 | bytes 4063232 | tf_op jit(solution)/shard_map/project/pallas_call | solution.py:175
  100.7 1.3 %project.33.refs_1_ = f32[1024,256]{1,0:T(8,128)S(1)} custom-call(s32[2]{0:T(128)S(1)} %pad_add_fusion.place, bf16[1024,8192]{1,0:T(8,128)(2,1)S(1)} %get-tuple-element.86.left, bf16[768,256]{1,0:T(8,128)(2,1)S(1)} %collective-permute-done.26.refs_0_, f32[1024,256]{1,0:T(8,128)S(1)} %project.32.refs_1_), custom_call_target="tpu_custom_call", output_to_operand_aliasing={{}: (3, {})} | custom-call | flops 402653184 | bytes 4063232 | tf_op jit(solution)/shard_map/project/pallas_call | solution.py:175
  102.0 3.8 %collective-permute-done.24.refs_0_ = bf16[256,256]{1,0:T(8,128)(2,1)S(1)} collective-permute-done((bf16[256,256]{1,0:T(8,128)(2,1)S(1)}, bf16[256,256]{1,0:T(8,128)(2,1)S(1)}, u32[]{:S(2)}, u32[]{:S(2)}) %collective-permute-start.24) | collective-permute-done | bytes 131104 | tf_op jit(solution)/shard_map/ppermute | solution.py:551
  105.8 1.0 project.34.refs_1_
  106.9 0.3 collective-permute-done.27.refs_0_
  107.2 1.0 project.35
  108.4 0.3 collective-permute-start.28
  108.7 1.3 %weigh_own.1.own = f32[4,256,128]{2,1,0:T(8,128)S(1)} custom-call(bf16[4,256,2048]{2,1,0:T(8,128)(2,1)S(1)} %get-tuple-element.116.probs.refs_0_, bf16[1024,128]{1,0:T(8,128)(2,1)S(1)} %get-tuple-element.156.values), custom_call_target="tpu_custom_call" | custom-call | flops 268435456 | bytes 2097152 | tf_op jit(solution)/shard_map/weigh_own/pallas_call | solution.py:327
  110.0 1.5 %weigh.1 = (bf16[272,128]{1,0:T(8,128)(2,1)S(1)}, bf16[272,128]{1,0:T(8,128)(2,1)S(1)}, bf16[272,128]{1,0:T(8,128)(2,1)S(1)}, bf16[272,128]{1,0:T(8,128)(2,1)S(1)}) custom-call(f32[4,256,128]{2,1,0:T(8,128)S(1)} %weigh_own.1.own, bf16[4,256,2048]{2,1,0:T(8,128)(2,1)S(1)} %get-tuple-element.116.probs.refs_0_, ...), custom_call_target="tpu_custom_call" | custom-call | flops 268435456 | bytes 2097152 | tf_op jit(solution)/shard_map/weigh/pallas_call | solution.py:339
  111.6 3.2 %collective-permute-start.30 = (bf16[272,128]{1,0:T(8,128)(2,1)S(1)}, bf16[272,128]{1,0:T(8,128)(2,1)S(1)}, u32[]{:S(2)}, u32[]{:S(2)}) collective-permute-start(bf16[272,128]{1,0:T(8,128)(2,1)S(1)} %get-tuple-element.136), channel_id=1, source_target_pairs={{0,16},{8,24},{16,0},{24,8},{1,17},{9,25},{17,1},{25,9},{2,18},{10... | collective-permute-start | bytes 208904 | tf_op jit(solution)/shard_map/ppermute | solution.py:33
  114.7 1.2 collective-permute-start.31
  115.9 2.3 %broadcast_select_fusion = bf16[1024,2,256]{2,1,0:T(2,128)(2,1)} fusion(pred[2]{0:T(512)(128)(4,1)S(1)} %iota_compare_fusion.5, bf16[1024,256]{1,0:T(8,128)(2,1)S(1)} %minimum_convert_fusion, bf16[1024,256]{1,0:T(8,128)(2,1)S(1)} %minimum_convert_fusion.1), kind=kLoop, calls=%fused_computation.3 | loop fusion | flops 524288 | bytes 2097154 | tf_op jit(solution)/shard_map/jit(_where)/select_n | solution.py:644
  118.3 0.2 fresh.1
  118.5 1.3 %collective-permute-done.30.refs_2_ = bf16[272,128]{1,0:T(8,128)(2,1)S(1)} collective-permute-done((bf16[272,128]{1,0:T(8,128)(2,1)S(1)}, bf16[272,128]{1,0:T(8,128)(2,1)S(1)}, u32[]{:S(2)}, u32[]{:S(2)}) %collective-permute-start.30) | collective-permute-done | bytes 69664 | tf_op jit(solution)/shard_map/ppermute | solution.py:33
  119.7 1.1 collective-permute-done.31.refs_3_
  120.9 0.4 finish.1
  121.4 1.2 %collective-permute-done.32 = bf16[32,1024]{1,0:T(8,128)(2,1)S(1)} collective-permute-done((bf16[32,1024]{1,0:T(8,128)(2,1)S(1)}, bf16[32,1024]{1,0:T(8,128)(2,1)S(1)}, u32[]{:S(2)}, u32[]{:S(2)}) %collective-permute-start.32) | collective-permute-done | bytes 65568 | tf_op jit(solution)/shard_map/ppermute | solution.py:24
  122.6 0.7 maximum_bitcast_fusion
  (79 shorter events, 1.9 us)
Async XLA Ops:
  0.6 15.3 %collective-permute-start = (bf16[1024,256]{1,0:T(8,128)(2,1)}, bf16[1024,256]{1,0:T(8,128)(2,1)S(1)}, u32[]{:S(2)}, u32[]{:S(2)}) collective-permute-start(bf16[1024,256]{1,0:T(8,128)(2,1)} %refs_0_), channel_id=1, source_target_pairs={{0,8},{8,0},{16,24},{24,16},{1,9},{9,1},{17,25},{25,17},{2,10},{10... | collective-permute-start | bytes 1572872 | tf_op jit(solution)/shard_map/ppermute | solution.py:503
  3.7 12.1 %collective-permute-start.1 = (bf16[1024,256]{1,0:T(8,128)(2,1)}, bf16[1024,256]{1,0:T(8,128)(2,1)S(1)}, u32[]{:S(2)}, u32[]{:S(2)}) collective-permute-start(bf16[1024,256]{1,0:T(8,128)(2,1)} %refs_0_), channel_id=1, source_target_pairs={{8,16},{16,8},{9,17},{17,9},{10,18},{18,10},{11,19},{19,11},{12,20... | collective-permute-start | bytes 1572872 | tf_op jit(solution)/shard_map/ppermute | solution.py:503
  4.4 16.7 %collective-permute-start.6 = (bf16[1024,256]{1,0:T(8,128)(2,1)}, bf16[1024,256]{1,0:T(8,128)(2,1)S(1)}, u32[]{:S(2)}, u32[]{:S(2)}) collective-permute-start(bf16[1024,256]{1,0:T(8,128)(2,1)} %refs_0_), channel_id=1, source_target_pairs={{0,1},{1,0},{2,3},{3,2},{4,5},{5,4},{6,7},{7,6},{8,9},{9,8},{10,11... | collective-permute-start | bytes 1572872 | tf_op jit(solution)/shard_map/ppermute | solution.py:24
  4.5 18.7 %collective-permute-start.7 = (bf16[1024,256]{1,0:T(8,128)(2,1)}, bf16[1024,256]{1,0:T(8,128)(2,1)S(1)}, u32[]{:S(2)}, u32[]{:S(2)}) collective-permute-start(bf16[1024,256]{1,0:T(8,128)(2,1)} %weight.1), channel_id=1, source_target_pairs={{0,1},{1,0},{2,3},{3,2},{4,5},{5,4},{6,7},{7,6},{8,9},{9,8},{10,11... | collective-permute-start | bytes 1572872 | tf_op jit(solution)/shard_map/ppermute | solution.py:24
  6.0 1.0 copy-start
  7.1 1.0 copy-start.1
  15.9 10.0 %collective-permute-start.4 = (bf16[1024,256]{1,0:T(8,128)(2,1)S(1)}, bf16[1024,256]{1,0:T(8,128)(2,1)S(1)}, u32[]{:S(2)}, u32[]{:S(2)}) collective-permute-start(bf16[1024,256]{1,0:T(8,128)(2,1)S(1)} %collective-permute-done.refs_0_), channel_id=1, source_target_pairs={{0,1},{1,0},{2,3},{3,2},{4,5},{5,4},{6,7},{7,6},{8,9},{9,8},{10,11... | collective-permute-start | bytes 1572872 | tf_op jit(solution)/shard_map/ppermute | solution.py:24
  15.9 10.0 %collective-permute-start.5 = (bf16[1024,256]{1,0:T(8,128)(2,1)S(1)}, bf16[1024,256]{1,0:T(8,128)(2,1)S(1)}, u32[]{:S(2)}, u32[]{:S(2)}) collective-permute-start(bf16[1024,256]{1,0:T(8,128)(2,1)S(1)} %collective-permute-done.1.refs_1_), channel_id=1, source_target_pairs={{0,1},{1,0},{2,3},{3,2},{4,5},{5,4},{6,7},{7,6},{8,9},{9,8},{10,11... | collective-permute-start | bytes 1572872 | tf_op jit(solution)/shard_map/ppermute | solution.py:24
  16.4 18.2 %collective-permute-start.3 = (bf16[1152,256]{1,0:T(8,128)(2,1)S(1)}, bf16[1152,256]{1,0:T(8,128)(2,1)S(1)}, u32[]{:S(2)}, u32[]{:S(2)}) collective-permute-start(bf16[1152,256]{1,0:T(8,128)(2,1)S(1)} %pack.1.refs_1_), channel_id=1, source_target_pairs={{0,8},{8,0},{16,24},{24,16},{1,9},{9,1},{17,25},{25,17},{2,10},{10... | collective-permute-start | bytes 1769480 | tf_op jit(solution)/shard_map/ppermute | solution.py:503
  21.2 13.5 %collective-permute-start.2 = (bf16[1024,256]{1,0:T(8,128)(2,1)S(1)}, bf16[1024,256]{1,0:T(8,128)(2,1)S(1)}, u32[]{:S(2)}, u32[]{:S(2)}) collective-permute-start(bf16[1024,256]{1,0:T(8,128)(2,1)S(1)} %collective-permute-done.refs_0_), channel_id=1, source_target_pairs={{8,16},{16,8},{9,17},{17,9},{10,18},{18,10},{11,19},{19,11},{12,20... | collective-permute-start | bytes 1572872 | tf_op jit(solution)/shard_map/ppermute | solution.py:503
  24.5 11.5 %copy-start.6 = (s32[32]{0:T(128)S(1)}, s32[32]{0:T(128)}, u32[]{:S(2)}) copy-start(s32[32]{0:T(128)} %param.15) | copy-start | bytes 388
  34.7 4.2 %collective-permute-start.13 = (bf16[1152,256]{1,0:T(8,128)(2,1)S(1)}, bf16[1152,256]{1,0:T(8,128)(2,1)S(1)}, u32[]{:S(2)}, u32[]{:S(2)}) collective-permute-start(bf16[1152,256]{1,0:T(8,128)(2,1)S(1)} %collective-permute-done.3.refs_0_), channel_id=1, source_target_pairs={{0,1},{1,0},{2,3},{3,2},{4,5},{5,4},{6,7},{7,6},{8,9},{9,8},{10,11... | collective-permute-start | bytes 1769480 | tf_op jit(solution)/shard_map/ppermute | solution.py:24
  34.7 16.7 %collective-permute-start.12 = (bf16[1024,256]{1,0:T(8,128)(2,1)S(1)}, bf16[1024,256]{1,0:T(8,128)(2,1)S(1)}, u32[]{:S(2)}, u32[]{:S(2)}) collective-permute-start(bf16[1024,256]{1,0:T(8,128)(2,1)S(1)} %collective-permute-done.1.refs_1_), channel_id=1, source_target_pairs={{8,0},{16,24},{9,1},{17,25},{10,2},{18,26},{11,3},{19,27},{12,4},{... | collective-permute-start | bytes 1572872 | tf_op jit(solution)/shard_map/ppermute | solution.py:503
  36.1 15.6 %copy-start.3 = (s32[32,32]{1,0:T(8,128)S(1)}, s32[32,32]{1,0:T(8,128)}, u32[]{:S(2)}) copy-start(s32[32,32]{1,0:T(8,128)} %param.14) | copy-start | bytes 12292
  36.1 26.0 %collective-permute-start.11 = (bf16[1024,256]{1,0:T(8,128)(2,1)S(1)}, bf16[1024,256]{1,0:T(8,128)(2,1)S(1)}, u32[]{:S(2)}, u32[]{:S(2)}) collective-permute-start(bf16[1024,256]{1,0:T(8,128)(2,1)S(1)} %collective-permute-done.2), channel_id=1, source_target_pairs={{8,0},{16,24},{9,1},{17,25},{10,2},{18,26},{11,3},{19,27},{12,4},{... | collective-permute-start | bytes 1572872 | tf_op jit(solution)/shard_map/ppermute | solution.py:503
  51.5 3.1 %collective-permute-start.14 = (bf16[1024,256]{1,0:T(8,128)(2,1)S(1)}, bf16[1024,256]{1,0:T(8,128)(2,1)S(1)}, u32[]{:S(2)}, u32[]{:S(2)}) collective-permute-start(bf16[1024,256]{1,0:T(8,128)(2,1)S(1)} %add.74.refs_0_), channel_id=1, source_target_pairs={{0,1},{1,0},{2,3},{3,2},{4,5},{5,4},{6,7},{7,6},{8,9},{9,8},{10,11... | collective-permute-start | bytes 1572872 | tf_op jit(solution)/shard_map/ppermute | solution.py:24
  52.4 9.9 %copy-start.5 = (f32[2,256]{1,0:T(2,128)S(1)}, f32[2,256]{1,0:T(2,128)}, u32[]{:S(2)}) copy-start(f32[2,256]{1,0:T(2,128)} %param.11) | copy-start | bytes 6148
  52.4 15.2 %collective-permute-start.8 = (bf16[1152,256]{1,0:T(8,128)(2,1)S(1)}, bf16[1152,256]{1,0:T(8,128)(2,1)S(1)}, u32[]{:S(2)}, u32[]{:S(2)}) collective-permute-start(bf16[1152,256]{1,0:T(8,128)(2,1)S(1)} %pack.1.refs_1_), channel_id=1, source_target_pairs={{8,16},{16,8},{9,17},{17,9},{10,18},{18,10},{11,19},{19,11},{12,20... | collective-permute-start | bytes 1769480 | tf_op jit(solution)/shard_map/ppermute | solution.py:503
  62.1 8.2 %collective-permute-start.15 = (bf16[1024,256]{1,0:T(8,128)(2,1)S(1)}, bf16[1024,256]{1,0:T(8,128)(2,1)S(1)}, u32[]{:S(2)}, u32[]{:S(2)}) collective-permute-start(bf16[1024,256]{1,0:T(8,128)(2,1)S(1)} %collective-permute-done.11.refs_0_), channel_id=1, source_target_pairs={{0,1},{1,0},{2,3},{3,2},{4,5},{5,4},{6,7},{7,6},{8,9},{9,8},{10,11... | collective-permute-start | bytes 1572872 | tf_op jit(solution)/shard_map/ppermute | solution.py:24
  62.4 13.3 %collective-permute-start.10 = (bf16[1152,256]{1,0:T(8,128)(2,1)S(1)}, bf16[1152,256]{1,0:T(8,128)(2,1)S(1)}, u32[]{:S(2)}, u32[]{:S(2)}) collective-permute-start(bf16[1152,256]{1,0:T(8,128)(2,1)S(1)} %collective-permute-done.3.refs_0_), channel_id=1, source_target_pairs={{8,16},{16,8},{9,17},{17,9},{10,18},{18,10},{11,19},{19,11},{12,20... | collective-permute-start | bytes 1769480 | tf_op jit(solution)/shard_map/ppermute | solution.py:503
  63.1 20.8 %collective-permute-start.20 = (bf16[128,256]{1,0:T(8,128)(2,1)S(1)}, bf16[128,256]{1,0:T(8,128)(2,1)S(1)}, u32[]{:S(2)}, u32[]{:S(2)}) collective-permute-start(bf16[128,256]{1,0:T(8,128)(2,1)S(1)} %slice.85), channel_id=1, source_target_pairs={{0,24},{24,0},{1,25},{25,1},{2,26},{26,2},{3,27},{27,3},{4,28},{28... | collective-permute-start | bytes 196616 | tf_op jit(solution)/shard_map/ppermute | solution.py:533
  67.6 18.4 %collective-permute-start.9 = (bf16[1152,256]{1,0:T(8,128)(2,1)S(1)}, bf16[1152,256]{1,0:T(8,128)(2,1)S(1)}, u32[]{:S(2)}, u32[]{:S(2)}) collective-permute-start(bf16[1152,256]{1,0:T(8,128)(2,1)S(1)} %collective-permute-done.8.refs_0_), channel_id=1, source_target_pairs={{8,0},{16,24},{9,1},{17,25},{10,2},{18,26},{11,3},{19,27},{12,4},{... | collective-permute-start | bytes 1769480 | tf_op jit(solution)/shard_map/ppermute | solution.py:503
  71.7 1.2 collective-permute-start.16
  72.9 11.6 %collective-permute-start.19 = (f32[1,256]{1,0:T(1,128)S(1)}, f32[1,256]{1,0:T(1,128)S(1)}, u32[]{:S(2)}, u32[]{:S(2)}) collective-permute-start(f32[1,256]{1,0:T(1,128)S(1)} %max.36), channel_id=1, source_target_pairs={{0,24},{8,16},{16,8},{24,0},{1,25},{9,17},{17,9},{25,1},{2,26},{10... | collective-permute-start | bytes 3080 | tf_op jit(solution)/shard_map/ppermute | solution.py:33
  74.1 11.9 %collective-permute-start.18 = (f32[1,256]{1,0:T(1,128)S(1)}, f32[1,256]{1,0:T(1,128)S(1)}, u32[]{:S(2)}, u32[]{:S(2)}) collective-permute-start(f32[1,256]{1,0:T(1,128)S(1)} %max.36), channel_id=1, source_target_pairs={{0,16},{8,24},{16,0},{24,8},{1,17},{9,25},{17,1},{25,9},{2,18},{10... | collective-permute-start | bytes 3080 | tf_op jit(solution)/shard_map/ppermute | solution.py:33
  75.6 10.4 %collective-permute-start.17 = (f32[1,256]{1,0:T(1,128)S(1)}, f32[1,256]{1,0:T(1,128)S(1)}, u32[]{:S(2)}, u32[]{:S(2)}) collective-permute-start(f32[1,256]{1,0:T(1,128)S(1)} %max.36), channel_id=1, source_target_pairs={{0,8},{8,0},{16,24},{24,16},{1,9},{9,1},{17,25},{25,17},{2,10},{10... | collective-permute-start | bytes 3080 | tf_op jit(solution)/shard_map/ppermute | solution.py:33
  83.9 3.3 %collective-permute-start.23 = (bf16[1152,256]{1,0:T(8,128)(2,1)S(1)}, bf16[1152,256]{1,0:T(8,128)(2,1)S(1)}, u32[]{:S(2)}, u32[]{:S(2)}) collective-permute-start(bf16[1152,256]{1,0:T(8,128)(2,1)S(1)} %collective-permute-done.8.refs_0_), channel_id=1, source_target_pairs={{0,1},{1,0},{2,3},{3,2},{4,5},{5,4},{6,7},{7,6},{8,9},{9,8},{10,11... | collective-permute-start | bytes 1769480 | tf_op jit(solution)/shard_map/ppermute | solution.py:24
  84.5 13.4 %collective-permute-start.25 = (bf16[768,256]{1,0:T(8,128)(2,1)S(1)}, bf16[768,256]{1,0:T(8,128)(2,1)S(1)}, u32[]{:S(2)}, u32[]{:S(2)}) collective-permute-start(bf16[768,256]{1,0:T(8,128)(2,1)S(1)} %slice.93), channel_id=1, source_target_pairs={{8,0},{16,24},{9,1},{17,25},{10,2},{18,26},{11,3},{19,27},{12,4},{... | collective-permute-start | bytes 1179656 | tf_op jit(solution)/shard_map/ppermute | solution.py:503
  86.1 3.1 %copy-start.4 = (f32[1,256]{1,0:T(1,128)}, f32[1,256]{1,0:T(1,128)S(1)}, u32[]{:S(2)}) copy-start(f32[1,256]{1,0:T(1,128)S(1)} %add_sqrt_fusion) | copy-start | bytes 3076
  86.2 2.9 %collective-permute-start.22 = (bf16[1152,256]{1,0:T(8,128)(2,1)S(1)}, bf16[1152,256]{1,0:T(8,128)(2,1)S(1)}, u32[]{:S(2)}, u32[]{:S(2)}) collective-permute-start(bf16[1152,256]{1,0:T(8,128)(2,1)S(1)} %add.86.refs_0_), channel_id=1, source_target_pairs={{0,1},{1,0},{2,3},{3,2},{4,5},{5,4},{6,7},{7,6},{8,9},{9,8},{10,11... | collective-permute-start | bytes 1769480 | tf_op jit(solution)/shard_map/ppermute | solution.py:24
  87.0 3.4 %collective-permute-start.21 = (bf16[1024,128]{1,0:T(8,128)(2,1)S(1)}, bf16[1024,128]{1,0:T(8,128)(2,1)S(1)}, u32[]{:S(2)}, u32[]{:S(2)}) collective-permute-start(bf16[1024,128]{1,0:T(8,128)(2,1)S(1)} %get-tuple-element.157), channel_id=1, source_target_pairs={{0,1},{1,0},{2,3},{3,2},{4,5},{5,4},{6,7},{7,6},{8,9},{9,8},{10,11... | collective-permute-start | bytes 786440 | tf_op jit(solution)/shard_map/ppermute | solution.py:24
  87.8 10.2 %copy-start.2 = (bf16[4,8,2,256]{3,2,1,0:T(2,128)(2,1)S(1)}, bf16[4,8,2,256]{3,2,1,0:T(2,128)(2,1)}, u32[]{:S(2)}) copy-start(bf16[4,8,2,256]{3,2,1,0:T(2,128)(2,1)} %param.12) | copy-start | bytes 98308
  98.0 2.7 %collective-permute-start.26 = (bf16[768,256]{1,0:T(8,128)(2,1)S(1)}, bf16[768,256]{1,0:T(8,128)(2,1)S(1)}, u32[]{:S(2)}, u32[]{:S(2)}) collective-permute-start(bf16[768,256]{1,0:T(8,128)(2,1)S(1)} %collective-permute-done.25.refs_0_), channel_id=1, source_target_pairs={{0,1},{1,0},{2,3},{3,2},{4,5},{5,4},{6,7},{7,6},{8,9},{9,8},{10,11... | collective-permute-start | bytes 1179656 | tf_op jit(solution)/shard_map/ppermute | solution.py:24
  98.0 7.8 %collective-permute-start.24 = (bf16[256,256]{1,0:T(8,128)(2,1)S(1)}, bf16[256,256]{1,0:T(8,128)(2,1)S(1)}, u32[]{:S(2)}, u32[]{:S(2)}) collective-permute-start(bf16[256,256]{1,0:T(8,128)(2,1)S(1)} %slice.92), channel_id=1, source_target_pairs={{8,0},{16,24},{9,1},{17,25},{10,2},{18,26},{11,3},{19,27},{12,4},{... | collective-permute-start | bytes 393224 | tf_op jit(solution)/shard_map/ppermute | solution.py:551
  105.8 1.3 %collective-permute-start.27 = (bf16[256,256]{1,0:T(8,128)(2,1)S(1)}, bf16[256,256]{1,0:T(8,128)(2,1)S(1)}, u32[]{:S(2)}, u32[]{:S(2)}) collective-permute-start(bf16[256,256]{1,0:T(8,128)(2,1)S(1)} %collective-permute-done.24.refs_0_), channel_id=1, source_target_pairs={{0,1},{1,0},{2,3},{3,2},{4,5},{5,4},{6,7},{7,6},{8,9},{9,8},{10,11... | collective-permute-start | bytes 393224 | tf_op jit(solution)/shard_map/ppermute | solution.py:24
  108.4 1.6 %collective-permute-start.28 = (bf16[1024,128]{1,0:T(8,128)(2,1)S(1)}, bf16[1024,128]{1,0:T(8,128)(2,1)S(1)}, u32[]{:S(2)}, u32[]{:S(2)}) collective-permute-start(bf16[1024,128]{1,0:T(8,128)(2,1)S(1)} %get-tuple-element.155), channel_id=1, source_target_pairs={{0,1},{1,0},{2,3},{3,2},{4,5},{5,4},{6,7},{7,6},{8,9},{9,8},{10,11... | collective-permute-start | bytes 786440 | tf_op jit(solution)/shard_map/ppermute | solution.py:24
  111.5 7.0 %collective-permute-start.29 = (bf16[272,128]{1,0:T(8,128)(2,1)S(1)}, bf16[272,128]{1,0:T(8,128)(2,1)S(1)}, u32[]{:S(2)}, u32[]{:S(2)}) collective-permute-start(bf16[272,128]{1,0:T(8,128)(2,1)S(1)} %get-tuple-element.135), channel_id=1, source_target_pairs={{0,8},{8,0},{16,24},{24,16},{1,9},{9,1},{17,25},{25,17},{2,10},{10... | collective-permute-start | bytes 208904 | tf_op jit(solution)/shard_map/ppermute | solution.py:33
  111.6 8.2 %collective-permute-start.30 = (bf16[272,128]{1,0:T(8,128)(2,1)S(1)}, bf16[272,128]{1,0:T(8,128)(2,1)S(1)}, u32[]{:S(2)}, u32[]{:S(2)}) collective-permute-start(bf16[272,128]{1,0:T(8,128)(2,1)S(1)} %get-tuple-element.136), channel_id=1, source_target_pairs={{0,16},{8,24},{16,0},{24,8},{1,17},{9,25},{17,1},{25,9},{2,18},{10... | collective-permute-start | bytes 208904 | tf_op jit(solution)/shard_map/ppermute | solution.py:33
  114.7 6.1 %collective-permute-start.31 = (bf16[272,128]{1,0:T(8,128)(2,1)S(1)}, bf16[272,128]{1,0:T(8,128)(2,1)S(1)}, u32[]{:S(2)}, u32[]{:S(2)}) collective-permute-start(bf16[272,128]{1,0:T(8,128)(2,1)S(1)} %get-tuple-element.137), channel_id=1, source_target_pairs={{0,24},{8,16},{16,8},{24,0},{1,25},{9,17},{17,9},{25,1},{2,26},{10... | collective-permute-start | bytes 208904 | tf_op jit(solution)/shard_map/ppermute | solution.py:33
  121.3 1.3 %collective-permute-start.32 = (bf16[32,1024]{1,0:T(8,128)(2,1)S(1)}, bf16[32,1024]{1,0:T(8,128)(2,1)S(1)}, u32[]{:S(2)}, u32[]{:S(2)}) collective-permute-start(bf16[32,1024]{1,0:T(8,128)(2,1)S(1)} %finish.1), channel_id=1, source_target_pairs={{0,1},{1,0},{2,3},{3,2},{4,5},{5,4},{6,7},{7,6},{8,9},{9,8},{10,11... | collective-permute-start | bytes 196616 | tf_op jit(solution)/shard_map/ppermute | solution.py:24

commit v14 on v13

--- a/solution.py
+++ b/solution.py
@@ -149,18 +149,24 @@
         pltpu.make_async_copy(weights[j].at[pl.ds(0, size)], held.at[j], arrived.at[j])
         for j in range(count)
     ]
-    for copy in copies:
-        copy.start()
     owner = lax.rem(place[1] + owners - back, owners)
-    for j, copy in enumerate(copies):
-        copy.wait()
+    sources = []
+    for j in range(count):
         group = jnp.int32(-1)
         for parity, hop in hops[j]:
             there = place[0] + jnp.where(lax.rem(place[0], 2) == parity, hop, -hop)
             group = jnp.where((there >= 0) & (there < groups), there, group)
-
-        @pl.when((group >= 0) & (group < groups))
+        sources.append(group)
+
+        @pl.when(group >= 0)
+        def _(j=j):
+            copies[j].start()
+
+    for j, group in enumerate(sources):
+
+        @pl.when(group >= 0)
         def _(j=j, group=group):
+            copies[j].wait()
             first = (group * owners + owner) * depth + start
             block = pl.ds(pl.multiple_of(first, math.gcd(depth, start)), size)
             out[...] += jnp.dot(left[:, block], held[j], preferred_element_type=jnp.float32)

time: 124 us -> 124 us (level)
  no operation moved by 1% of the time
where the time goes in v14:
time: 124 us; the launch traced here: 123 us
  starting transfers between devices  39.9 us (32%)
  waiting for transfers between devices  37.4 us (30%)
  Pallas kernels  36.5 us (29%)
  other arithmetic  5.49 us (4%)
  local copies, waits for them, and re-layouts  2.19 us (2%)
  between operations  1.31 us (1%)
    ppermute x10, waiting for transfers between devices, send(): return lax.ppermute(x, 'seq', line_pairs(hop, parity, groups))  28.8 us
    pallas_call x18, Pallas kernels, project(): pl.pallas_call(functools.partial(project_kernel, depth, part[0], hops, ba...  21.7 us
    ppermute x10, starting transfers between devices, send(): return lax.ppermute(x, 'seq', line_pairs(hop, parity, groups))  16.2 us
    ppermute x6, starting transfers between devices, swapped(): return lax.ppermute(x, axis, [(i, partner(i, k, n)) for i in range(n)])  15.4 us
    pallas_call x1, Pallas kernels, load(): pl.pallas_call(functools.partial(load_kernel, owners), out_shape=(jax.Sha...  6.57 us
    pallas_call x1, Pallas kernels, score(): pl.pallas_call(functools.partial(score_kernel, slots, parts, steps, scale...  4.73 us
    ppermute x1, starting transfers between devices, line_project(): far_query = lax.ppermute(own_block[depth:], 'seq', ends)  4.54 us
    ppermute x1, waiting for transfers between devices, line_project(): va3_rest = lax.ppermute(vb2[cut:depth], 'seq', line_pairs(3, 0, groups))  3.78 us
  transfers between devices with their start and end apart: 33, of which 11 were waited for; matrix products, arithmetic and copies ran while one was open for 4% of the time, Pallas kernels for 27%

profile of v14, /device:TPU:0, one launch (start us, length us, event | category | flops | bytes accessed | tf_op | source)
XLA Modules:
  0.0 123.2 jit_solution(10063812361274145983)
XLA Ops:
  0.6 3.1 %collective-permute-start = (bf16[1024,256]{1,0:T(8,128)(2,1)}, bf16[1024,256]{1,0:T(8,128)(2,1)S(1)}, u32[]{:S(2)}, u32[]{:S(2)}) collective-permute-start(bf16[1024,256]{1,0:T(8,128)(2,1)} %refs_0_), channel_id=1, source_target_pairs={{0,8},{8,0},{16,24},{24,16},{1,9},{9,1},{17,25},{25,17},{2,10},{10... | collective-permute-start | bytes 1572872 | tf_op jit(solution)/shard_map/ppermute | solution.py:509
  3.7 0.7 collective-permute-start.1
  4.5 0.5 collective-permute-start.7
  5.0 0.9 select_bitcast_fusion.query
  6.0 1.0 copy-done
  7.1 1.0 copy-done.1
  8.1 6.6 %load.1 = (bf16[1024,8192]{1,0:T(8,128)(2,1)S(1)}, f32[1024,256]{1,0:T(8,128)S(1)}, f32[1024,256]{1,0:T(8,128)S(1)}) custom-call(s32[2]{0:T(128)S(1)} %pad_add_fusion.place, bf16[1024,8192]{1,0:T(8,128)(2,1)} %hidden.1, bf16[1024,256]{1,0:T(8,128)(2,1)S(1)} %copy-done.1, bf16[1152,256]{1,0:T(8,128)(2,1)S(1)} %pack.1.refs_1_), custom_call_target="tpu_custom_call" | custom-call | flops 1073741824 | bytes 16777216 | tf_op jit(solution)/shard_map/load/pallas_call | solution.py:118
  14.7 1.2 collective-permute-done.refs_0_
  15.9 0.5 collective-permute-start.5
  16.4 4.8 %collective-permute-start.3 = (bf16[1152,256]{1,0:T(8,128)(2,1)S(1)}, bf16[1152,256]{1,0:T(8,128)(2,1)S(1)}, u32[]{:S(2)}, u32[]{:S(2)}) collective-permute-start(bf16[1152,256]{1,0:T(8,128)(2,1)S(1)} %pack.1.refs_1_), channel_id=1, source_target_pairs={{0,8},{8,0},{16,24},{24,16},{1,9},{9,1},{17,25},{25,17},{2,10},{10... | collective-permute-start | bytes 1769480 | tf_op jit(solution)/shard_map/ppermute | solution.py:509
  21.2 0.7 collective-permute-start.2
  21.9 1.3 %project.18.refs_2_ = f32[1024,256]{1,0:T(8,128)S(1)} custom-call(s32[2]{0:T(128)S(1)} %pad_add_fusion.place, bf16[1024,8192]{1,0:T(8,128)(2,1)S(1)} %get-tuple-element.86.left, bf16[1024,256]{1,0:T(8,128)(2,1)S(1)} %collective-permute-done.6.refs_0_, f32[1024,256]{1,0:T(8,128)S(1)} %get-tuple-element.88.refs_1_), custom_call_target="tpu_custom_call", output_to_operand_aliasing={{}: (3, {})} | custom-call | flops 536870912 | bytes 4718592 | tf_op jit(solution)/shard_map/project/pallas_call | solution.py:181
  23.2 1.3 %project.21.refs_1_ = f32[1024,256]{1,0:T(8,128)S(1)} custom-call(s32[2]{0:T(128)S(1)} %pad_add_fusion.place, bf16[1024,8192]{1,0:T(8,128)(2,1)S(1)} %get-tuple-element.86.left, bf16[1024,256]{1,0:T(8,128)(2,1)S(1)} %collective-permute-done.7.refs_0_, f32[1024,256]{1,0:T(8,128)S(1)} %get-tuple-element.89.refs_1_), custom_call_target="tpu_custom_call", output_to_operand_aliasing={{}: (3, {})} | custom-call | flops 536870912 | bytes 4718592 | tf_op jit(solution)/shard_map/project/pallas_call | solution.py:181
  24.5 1.3 %project.19.refs_2_ = f32[1024,256]{1,0:T(8,128)S(1)} custom-call(s32[2]{0:T(128)S(1)} %pad_add_fusion.place, bf16[1024,8192]{1,0:T(8,128)(2,1)S(1)} %get-tuple-element.86.left, bf16[1024,256]{1,0:T(8,128)(2,1)S(1)} %collective-permute-done.refs_0_, bf16[1024,256]{1,0:T(8,128)(2,1)S(1)} %collective-permute-done.1.refs_1_, ...), custom_call_target="tpu_custom_call", output_to_operand_aliasing={{}: (4, {})} | custom-call | flops 1073741824 | bytes 7340032 | tf_op jit(solution)/shard_map/project/pallas_call | solution.py:181
  25.9 1.3 %project.20.refs_1_ = f32[1024,256]{1,0:T(8,128)S(1)} custom-call(s32[2]{0:T(128)S(1)} %pad_add_fusion.place, bf16[1024,8192]{1,0:T(8,128)(2,1)S(1)} %get-tuple-element.86.left, bf16[1024,256]{1,0:T(8,128)(2,1)S(1)} %collective-permute-done.4.refs_0_, bf16[1024,256]{1,0:T(8,128)(2,1)S(1)} %collective-permute-done.5.refs_1_, ...), custom_call_target="tpu_custom_call", output_to_operand_aliasing={{}: (4, {})} | custom-call | flops 1073741824 | bytes 7340032 | tf_op jit(solution)/shard_map/project/pallas_call | solution.py:181
  27.2 7.4 %collective-permute-done.3.refs_0_ = bf16[1152,256]{1,0:T(8,128)(2,1)S(1)} collective-permute-done((bf16[1152,256]{1,0:T(8,128)(2,1)S(1)}, bf16[1152,256]{1,0:T(8,128)(2,1)S(1)}, u32[]{:S(2)}, u32[]{:S(2)}) %collective-permute-start.3) | collective-permute-done | bytes 589856 | tf_op jit(solution)/shard_map/ppermute | solution.py:509
  34.7 1.3 %collective-permute-start.12 = (bf16[1024,256]{1,0:T(8,128)(2,1)S(1)}, bf16[1024,256]{1,0:T(8,128)(2,1)S(1)}, u32[]{:S(2)}, u32[]{:S(2)}) collective-permute-start(bf16[1024,256]{1,0:T(8,128)(2,1)S(1)} %collective-permute-done.1.refs_1_), channel_id=1, source_target_pairs={{8,0},{16,24},{9,1},{17,25},{10,2},{18,26},{11,3},{19,27},{12,4},{... | collective-permute-start | bytes 1572872 | tf_op jit(solution)/shard_map/ppermute | solution.py:509
  36.1 1.4 %collective-permute-start.11 = (bf16[1024,256]{1,0:T(8,128)(2,1)S(1)}, bf16[1024,256]{1,0:T(8,128)(2,1)S(1)}, u32[]{:S(2)}, u32[]{:S(2)}) collective-permute-start(bf16[1024,256]{1,0:T(8,128)(2,1)S(1)} %collective-permute-done.2), channel_id=1, source_target_pairs={{8,0},{16,24},{9,1},{17,25},{10,2},{18,26},{11,3},{19,27},{12,4},{... | collective-permute-start | bytes 1572872 | tf_op jit(solution)/shard_map/ppermute | solution.py:509
  37.5 1.3 %project.22.refs_1_ = f32[1024,256]{1,0:T(8,128)S(1)} custom-call(s32[2]{0:T(128)S(1)} %pad_add_fusion.place, bf16[1024,8192]{1,0:T(8,128)(2,1)S(1)} %get-tuple-element.86.left, bf16[1152,256]{1,0:T(8,128)(2,1)S(1)} %collective-permute-done.3.refs_0_, f32[1024,256]{1,0:T(8,128)S(1)} %project.21.refs_1_), custom_call_target="tpu_custom_call", output_to_operand_aliasing={{}: (3, {})} | custom-call | flops 536870912 | bytes 4718592 | tf_op jit(solution)/shard_map/project/pallas_call | solution.py:181
  38.8 1.3 %project.23.refs_1_ = f32[1024,256]{1,0:T(8,128)S(1)} custom-call(s32[2]{0:T(128)S(1)} %pad_add_fusion.place, bf16[1024,8192]{1,0:T(8,128)(2,1)S(1)} %get-tuple-element.86.left, bf16[1152,256]{1,0:T(8,128)(2,1)S(1)} %collective-permute-done.13.refs_0_, f32[1024,256]{1,0:T(8,128)S(1)} %project.22.refs_1_), custom_call_target="tpu_custom_call", output_to_operand_aliasing={{}: (3, {})} | custom-call | flops 536870912 | bytes 4718592 | tf_op jit(solution)/shard_map/project/pallas_call | solution.py:181
  40.1 11.2 %collective-permute-done.12 = bf16[1024,256]{1,0:T(8,128)(2,1)S(1)} collective-permute-done((bf16[1024,256]{1,0:T(8,128)(2,1)S(1)}, bf16[1024,256]{1,0:T(8,128)(2,1)S(1)}, u32[]{:S(2)}, u32[]{:S(2)}) %collective-permute-start.12) | collective-permute-done | bytes 524320 | tf_op jit(solution)/shard_map/ppermute | solution.py:509
  51.6 0.6 convert_reduce_fusion
  52.4 0.8 collective-permute-start.8
  53.3 1.3 %project.24.refs_1_ = f32[1024,256]{1,0:T(8,128)S(1)} custom-call(s32[2]{0:T(128)S(1)} %pad_add_fusion.place, bf16[1024,8192]{1,0:T(8,128)(2,1)S(1)} %get-tuple-element.86.left, bf16[1024,256]{1,0:T(8,128)(2,1)S(1)} %add.74.refs_0_, f32[1024,256]{1,0:T(8,128)S(1)} %project.20.refs_1_), custom_call_target="tpu_custom_call", output_to_operand_aliasing={{}: (3, {})} | custom-call | flops 536870912 | bytes 4718592 | tf_op jit(solution)/shard_map/project/pallas_call | solution.py:181
  54.6 1.3 %project.25.refs_1_ = f32[1024,256]{1,0:T(8,128)S(1)} custom-call(s32[2]{0:T(128)S(1)} %pad_add_fusion.place, bf16[1024,8192]{1,0:T(8,128)(2,1)S(1)} %get-tuple-element.86.left, bf16[1024,256]{1,0:T(8,128)(2,1)S(1)} %collective-permute-done.14.refs_0_, f32[1024,256]{1,0:T(8,128)S(1)} %project.24.refs_1_), custom_call_target="tpu_custom_call", output_to_operand_aliasing={{}: (3, {})} | custom-call | flops 536870912 | bytes 4718592 | tf_op jit(solution)/shard_map/project/pallas_call | solution.py:181
  55.9 6.2 %collective-permute-done.11.refs_0_ = bf16[1024,256]{1,0:T(8,128)(2,1)S(1)} collective-permute-done((bf16[1024,256]{1,0:T(8,128)(2,1)S(1)}, bf16[1024,256]{1,0:T(8,128)(2,1)S(1)}, u32[]{:S(2)}, u32[]{:S(2)}) %collective-permute-start.11) | collective-permute-done | bytes 524320 | tf_op jit(solution)/shard_map/ppermute | solution.py:509
  62.1 0.2 fusion.1.count
  62.4 0.7 collective-permute-start.10
  63.1 4.5 %collective-permute-start.20 = (bf16[128,256]{1,0:T(8,128)(2,1)S(1)}, bf16[128,256]{1,0:T(8,128)(2,1)S(1)}, u32[]{:S(2)}, u32[]{:S(2)}) collective-permute-start(bf16[128,256]{1,0:T(8,128)(2,1)S(1)} %slice.85), channel_id=1, source_target_pairs={{0,24},{24,0},{1,25},{25,1},{2,26},{26,2},{3,27},{27,3},{4,28},{28... | collective-permute-start | bytes 196616 | tf_op jit(solution)/shard_map/ppermute | solution.py:539
  67.6 1.3 %collective-permute-start.9 = (bf16[1152,256]{1,0:T(8,128)(2,1)S(1)}, bf16[1152,256]{1,0:T(8,128)(2,1)S(1)}, u32[]{:S(2)}, u32[]{:S(2)}) collective-permute-start(bf16[1152,256]{1,0:T(8,128)(2,1)S(1)} %collective-permute-done.8.refs_0_), channel_id=1, source_target_pairs={{8,0},{16,24},{9,1},{17,25},{10,2},{18,26},{11,3},{19,27},{12,4},{... | collective-permute-start | bytes 1769480 | tf_op jit(solution)/shard_map/ppermute | solution.py:509
  68.9 1.3 %project.26.refs_1_ = f32[1024,256]{1,0:T(8,128)S(1)} custom-call(s32[2]{0:T(128)S(1)} %pad_add_fusion.place, bf16[1024,8192]{1,0:T(8,128)(2,1)S(1)} %get-tuple-element.86.left, bf16[1024,256]{1,0:T(8,128)(2,1)S(1)} %collective-permute-done.11.refs_0_, f32[1024,256]{1,0:T(8,128)S(1)} %project.25.refs_1_), custom_call_target="tpu_custom_call", output_to_operand_aliasing={{}: (3, {})} | custom-call | flops 536870912 | bytes 4718592 | tf_op jit(solution)/shard_map/project/pallas_call | solution.py:181
  70.3 1.3 %project.27 = f32[1024,256]{1,0:T(8,128)S(1)} custom-call(s32[2]{0:T(128)S(1)} %pad_add_fusion.place, bf16[1024,8192]{1,0:T(8,128)(2,1)S(1)} %get-tuple-element.86.left, bf16[1024,256]{1,0:T(8,128)(2,1)S(1)} %collective-permute-done.15.refs_0_, f32[1024,256]{1,0:T(8,128)S(1)} %project.26.refs_1_), custom_call_target="tpu_custom_call", output_to_operand_aliasing={{}: (3, {})} | custom-call | flops 536870912 | bytes 4718592 | tf_op jit(solution)/shard_map/project/pallas_call | solution.py:181
  71.7 0.3 collective-permute-start.16
  72.0 0.9 collective-permute-done.16
  72.9 1.2 collective-permute-start.19
  74.1 1.5 %collective-permute-start.18 = (f32[1,256]{1,0:T(1,128)S(1)}, f32[1,256]{1,0:T(1,128)S(1)}, u32[]{:S(2)}, u32[]{:S(2)}) collective-permute-start(f32[1,256]{1,0:T(1,128)S(1)} %max.36), channel_id=1, source_target_pairs={{0,16},{8,24},{16,0},{24,8},{1,17},{9,25},{17,1},{25,9},{2,18},{10... | collective-permute-start | bytes 3080 | tf_op jit(solution)/shard_map/ppermute | solution.py:33
  75.5 8.3 %collective-permute-start.17 = (f32[1,256]{1,0:T(1,128)S(1)}, f32[1,256]{1,0:T(1,128)S(1)}, u32[]{:S(2)}, u32[]{:S(2)}) collective-permute-start(f32[1,256]{1,0:T(1,128)S(1)} %max.36), channel_id=1, source_target_pairs={{0,8},{8,0},{16,24},{24,16},{1,9},{9,1},{17,25},{25,17},{2,10},{10... | collective-permute-start | bytes 3080 | tf_op jit(solution)/shard_map/ppermute | solution.py:33
  83.9 0.6 project.28.refs_1_
  84.5 1.5 %collective-permute-start.25 = (bf16[768,256]{1,0:T(8,128)(2,1)S(1)}, bf16[768,256]{1,0:T(8,128)(2,1)S(1)}, u32[]{:S(2)}, u32[]{:S(2)}) collective-permute-start(bf16[768,256]{1,0:T(8,128)(2,1)S(1)} %slice.93), channel_id=1, source_target_pairs={{8,0},{16,24},{9,1},{17,25},{10,2},{18,26},{11,3},{19,27},{12,4},{... | collective-permute-start | bytes 1179656 | tf_op jit(solution)/shard_map/ppermute | solution.py:509
  86.2 0.6 collective-permute-start.22
  87.1 0.6 project.29.refs_1_
  87.7 1.3 %project.30.refs_1_ = f32[1024,256]{1,0:T(8,128)S(1)} custom-call(s32[2]{0:T(128)S(1)} %pad_add_fusion.place, bf16[1024,8192]{1,0:T(8,128)(2,1)S(1)} %get-tuple-element.86.left, bf16[1152,256]{1,0:T(8,128)(2,1)S(1)} %add.86.refs_0_, f32[1024,256]{1,0:T(8,128)S(1)} %project.29.refs_1_), custom_call_target="tpu_custom_call", output_to_operand_aliasing={{}: (3, {})} | custom-call | flops 536870912 | bytes 4718592 | tf_op jit(solution)/shard_map/project/pallas_call | solution.py:181
  89.1 1.3 %project.31.refs_1_ = f32[1024,256]{1,0:T(8,128)S(1)} custom-call(s32[2]{0:T(128)S(1)} %pad_add_fusion.place, bf16[1024,8192]{1,0:T(8,128)(2,1)S(1)} %get-tuple-element.86.left, bf16[1152,256]{1,0:T(8,128)(2,1)S(1)} %collective-permute-done.22.refs_0_, f32[1024,256]{1,0:T(8,128)S(1)} %project.30.refs_1_), custom_call_target="tpu_custom_call", output_to_operand_aliasing={{}: (3, {})} | custom-call | flops 536870912 | bytes 4718592 | tf_op jit(solution)/shard_map/project/pallas_call | solution.py:181
  90.4 4.7 %score.1 = (bf16[4,256,2048]{2,1,0:T(8,128)(2,1)S(1)}, f32[2,256]{1,0:T(2,128)S(1)}, f32[2,256]{1,0:T(2,128)S(1)}, f32[2,256]{1,0:T(2,128)S(1)}, f32[2,256]{1,0:T(2,128)S(1)}) custom-call(s32[4]{0:T(128)S(1)} %iota_xor_fusion.group, bf16[4,128,256]{2,1,0:T(8,128)(2,1)S(1)} %pad_maximum_fusion.query, f32[1,128]{1,0:T(1,128)S(1)} %broadcast_select_fusion.7.smooth, ...), custom_call_target="tpu_custom_call" | custom-call | flops 536870912 | bytes 4194304 | tf_op jit(solution)/shard_map/score/pallas_call | solution.py:252
  95.1 2.8 %collective-permute-done.25.refs_0_ = bf16[768,256]{1,0:T(8,128)(2,1)S(1)} collective-permute-done((bf16[768,256]{1,0:T(8,128)(2,1)S(1)}, bf16[768,256]{1,0:T(8,128)(2,1)S(1)}, u32[]{:S(2)}, u32[]{:S(2)}) %collective-permute-start.25) | collective-permute-done | bytes 393248 | tf_op jit(solution)/shard_map/ppermute | solution.py:509
  98.0 1.3 %collective-permute-start.24 = (bf16[256,256]{1,0:T(8,128)(2,1)S(1)}, bf16[256,256]{1,0:T(8,128)(2,1)S(1)}, u32[]{:S(2)}, u32[]{:S(2)}) collective-permute-start(bf16[256,256]{1,0:T(8,128)(2,1)S(1)} %slice.92), channel_id=1, source_target_pairs={{8,0},{16,24},{9,1},{17,25},{10,2},{18,26},{11,3},{19,27},{12,4},{... | collective-permute-start | bytes 393224 | tf_op jit(solution)/shard_map/ppermute | solution.py:557
  99.3 1.3 %project.32.refs_1_ = f32[1024,256]{1,0:T(8,128)S(1)} custom-call(s32[2]{0:T(128)S(1)} %pad_add_fusion.place, bf16[1024,8192]{1,0:T(8,128)(2,1)S(1)} %get-tuple-element.86.left, bf16[768,256]{1,0:T(8,128)(2,1)S(1)} %collective-permute-done.25.refs_0_, f32[1024,256]{1,0:T(8,128)S(1)} %project.31.refs_1_), custom_call_target="tpu_custom_call", output_to_operand_aliasing={{}: (3, {})} | custom-call | flops 402653184 | bytes 4063232 | tf_op jit(solution)/shard_map/project/pallas_call | solution.py:181
  100.6 1.3 %project.33.refs_1_ = f32[1024,256]{1,0:T(8,128)S(1)} custom-call(s32[2]{0:T(128)S(1)} %pad_add_fusion.place, bf16[1024,8192]{1,0:T(8,128)(2,1)S(1)} %get-tuple-element.86.left, bf16[768,256]{1,0:T(8,128)(2,1)S(1)} %collective-permute-done.26.refs_0_, f32[1024,256]{1,0:T(8,128)S(1)} %project.32.refs_1_), custom_call_target="tpu_custom_call", output_to_operand_aliasing={{}: (3, {})} | custom-call | flops 402653184 | bytes 4063232 | tf_op jit(solution)/shard_map/project/pallas_call | solution.py:181
  102.0 3.8 %collective-permute-done.24.refs_0_ = bf16[256,256]{1,0:T(8,128)(2,1)S(1)} collective-permute-done((bf16[256,256]{1,0:T(8,128)(2,1)S(1)}, bf16[256,256]{1,0:T(8,128)(2,1)S(1)}, u32[]{:S(2)}, u32[]{:S(2)}) %collective-permute-start.24) | collective-permute-done | bytes 131104 | tf_op jit(solution)/shard_map/ppermute | solution.py:557
  105.8 1.0 project.34.refs_1_
  106.8 0.3 collective-permute-done.27.refs_0_
  107.1 1.0 project.35
  108.3 0.3 collective-permute-start.28
  108.6 1.3 %weigh_own.1.own = f32[4,256,128]{2,1,0:T(8,128)S(1)} custom-call(bf16[4,256,2048]{2,1,0:T(8,128)(2,1)S(1)} %get-tuple-element.116.probs.refs_0_, bf16[1024,128]{1,0:T(8,128)(2,1)S(1)} %get-tuple-element.156.values), custom_call_target="tpu_custom_call" | custom-call | flops 268435456 | bytes 2097152 | tf_op jit(solution)/shard_map/weigh_own/pallas_call | solution.py:333
  110.0 1.5 %weigh.1 = (bf16[272,128]{1,0:T(8,128)(2,1)S(1)}, bf16[272,128]{1,0:T(8,128)(2,1)S(1)}, bf16[272,128]{1,0:T(8,128)(2,1)S(1)}, bf16[272,128]{1,0:T(8,128)(2,1)S(1)}) custom-call(f32[4,256,128]{2,1,0:T(8,128)S(1)} %weigh_own.1.own, bf16[4,256,2048]{2,1,0:T(8,128)(2,1)S(1)} %get-tuple-element.116.probs.refs_0_, ...), custom_call_target="tpu_custom_call" | custom-call | flops 268435456 | bytes 2097152 | tf_op jit(solution)/shard_map/weigh/pallas_call | solution.py:345
  111.5 3.2 %collective-permute-start.30 = (bf16[272,128]{1,0:T(8,128)(2,1)S(1)}, bf16[272,128]{1,0:T(8,128)(2,1)S(1)}, u32[]{:S(2)}, u32[]{:S(2)}) collective-permute-start(bf16[272,128]{1,0:T(8,128)(2,1)S(1)} %get-tuple-element.136), channel_id=1, source_target_pairs={{0,16},{8,24},{16,0},{24,8},{1,17},{9,25},{17,1},{25,9},{2,18},{10... | collective-permute-start | bytes 208904 | tf_op jit(solution)/shard_map/ppermute | solution.py:33
  114.7 1.2 collective-permute-start.31
  115.9 2.3 %broadcast_select_fusion = bf16[1024,2,256]{2,1,0:T(2,128)(2,1)} fusion(pred[2]{0:T(512)(128)(4,1)S(1)} %iota_compare_fusion.5, bf16[1024,256]{1,0:T(8,128)(2,1)S(1)} %minimum_convert_fusion, bf16[1024,256]{1,0:T(8,128)(2,1)S(1)} %minimum_convert_fusion.1), kind=kLoop, calls=%fused_computation.3 | loop fusion | flops 524288 | bytes 2097154 | tf_op jit(solution)/shard_map/jit(_where)/select_n | solution.py:650
  118.2 0.2 fresh.1
  118.4 1.3 %collective-permute-done.30.refs_2_ = bf16[272,128]{1,0:T(8,128)(2,1)S(1)} collective-permute-done((bf16[272,128]{1,0:T(8,128)(2,1)S(1)}, bf16[272,128]{1,0:T(8,128)(2,1)S(1)}, u32[]{:S(2)}, u32[]{:S(2)}) %collective-permute-start.30) | collective-permute-done | bytes 69664 | tf_op jit(solution)/shard_map/ppermute | solution.py:33
  119.7 1.1 collective-permute-done.31.refs_3_
  120.8 0.4 finish.1
  121.3 1.2 %collective-permute-done.32 = bf16[32,1024]{1,0:T(8,128)(2,1)S(1)} collective-permute-done((bf16[32,1024]{1,0:T(8,128)(2,1)S(1)}, bf16[32,1024]{1,0:T(8,128)(2,1)S(1)}, u32[]{:S(2)}, u32[]{:S(2)}) %collective-permute-start.32) | collective-permute-done | bytes 65568 | tf_op jit(solution)/shard_map/ppermute | solution.py:24
  122.6 0.7 maximum_bitcast_fusion
  (79 shorter events, 1.9 us)
Async XLA Ops:
  0.6 15.3 %collective-permute-start = (bf16[1024,256]{1,0:T(8,128)(2,1)}, bf16[1024,256]{1,0:T(8,128)(2,1)S(1)}, u32[]{:S(2)}, u32[]{:S(2)}) collective-permute-start(bf16[1024,256]{1,0:T(8,128)(2,1)} %refs_0_), channel_id=1, source_target_pairs={{0,8},{8,0},{16,24},{24,16},{1,9},{9,1},{17,25},{25,17},{2,10},{10... | collective-permute-start | bytes 1572872 | tf_op jit(solution)/shard_map/ppermute | solution.py:509
  3.7 12.1 %collective-permute-start.1 = (bf16[1024,256]{1,0:T(8,128)(2,1)}, bf16[1024,256]{1,0:T(8,128)(2,1)S(1)}, u32[]{:S(2)}, u32[]{:S(2)}) collective-permute-start(bf16[1024,256]{1,0:T(8,128)(2,1)} %refs_0_), channel_id=1, source_target_pairs={{8,16},{16,8},{9,17},{17,9},{10,18},{18,10},{11,19},{19,11},{12,20... | collective-permute-start | bytes 1572872 | tf_op jit(solution)/shard_map/ppermute | solution.py:509
  4.4 16.7 %collective-permute-start.6 = (bf16[1024,256]{1,0:T(8,128)(2,1)}, bf16[1024,256]{1,0:T(8,128)(2,1)S(1)}, u32[]{:S(2)}, u32[]{:S(2)}) collective-permute-start(bf16[1024,256]{1,0:T(8,128)(2,1)} %refs_0_), channel_id=1, source_target_pairs={{0,1},{1,0},{2,3},{3,2},{4,5},{5,4},{6,7},{7,6},{8,9},{9,8},{10,11... | collective-permute-start | bytes 1572872 | tf_op jit(solution)/shard_map/ppermute | solution.py:24
  4.5 18.7 %collective-permute-start.7 = (bf16[1024,256]{1,0:T(8,128)(2,1)}, bf16[1024,256]{1,0:T(8,128)(2,1)S(1)}, u32[]{:S(2)}, u32[]{:S(2)}) collective-permute-start(bf16[1024,256]{1,0:T(8,128)(2,1)} %weight.1), channel_id=1, source_target_pairs={{0,1},{1,0},{2,3},{3,2},{4,5},{5,4},{6,7},{7,6},{8,9},{9,8},{10,11... | collective-permute-start | bytes 1572872 | tf_op jit(solution)/shard_map/ppermute | solution.py:24
  6.0 1.0 copy-start
  7.1 1.0 copy-start.1
  15.9 10.0 %collective-permute-start.4 = (bf16[1024,256]{1,0:T(8,128)(2,1)S(1)}, bf16[1024,256]{1,0:T(8,128)(2,1)S(1)}, u32[]{:S(2)}, u32[]{:S(2)}) collective-permute-start(bf16[1024,256]{1,0:T(8,128)(2,1)S(1)} %collective-permute-done.refs_0_), channel_id=1, source_target_pairs={{0,1},{1,0},{2,3},{3,2},{4,5},{5,4},{6,7},{7,6},{8,9},{9,8},{10,11... | collective-permute-start | bytes 1572872 | tf_op jit(solution)/shard_map/ppermute | solution.py:24
  15.9 10.0 %collective-permute-start.5 = (bf16[1024,256]{1,0:T(8,128)(2,1)S(1)}, bf16[1024,256]{1,0:T(8,128)(2,1)S(1)}, u32[]{:S(2)}, u32[]{:S(2)}) collective-permute-start(bf16[1024,256]{1,0:T(8,128)(2,1)S(1)} %collective-permute-done.1.refs_1_), channel_id=1, source_target_pairs={{0,1},{1,0},{2,3},{3,2},{4,5},{5,4},{6,7},{7,6},{8,9},{9,8},{10,11... | collective-permute-start | bytes 1572872 | tf_op jit(solution)/shard_map/ppermute | solution.py:24
  16.4 18.2 %collective-permute-start.3 = (bf16[1152,256]{1,0:T(8,128)(2,1)S(1)}, bf16[1152,256]{1,0:T(8,128)(2,1)S(1)}, u32[]{:S(2)}, u32[]{:S(2)}) collective-permute-start(bf16[1152,256]{1,0:T(8,128)(2,1)S(1)} %pack.1.refs_1_), channel_id=1, source_target_pairs={{0,8},{8,0},{16,24},{24,16},{1,9},{9,1},{17,25},{25,17},{2,10},{10... | collective-permute-start | bytes 1769480 | tf_op jit(solution)/shard_map/ppermute | solution.py:509
  21.2 13.5 %collective-permute-start.2 = (bf16[1024,256]{1,0:T(8,128)(2,1)S(1)}, bf16[1024,256]{1,0:T(8,128)(2,1)S(1)}, u32[]{:S(2)}, u32[]{:S(2)}) collective-permute-start(bf16[1024,256]{1,0:T(8,128)(2,1)S(1)} %collective-permute-done.refs_0_), channel_id=1, source_target_pairs={{8,16},{16,8},{9,17},{17,9},{10,18},{18,10},{11,19},{19,11},{12,20... | collective-permute-start | bytes 1572872 | tf_op jit(solution)/shard_map/ppermute | solution.py:509
  24.5 11.5 %copy-start.6 = (s32[32]{0:T(128)S(1)}, s32[32]{0:T(128)}, u32[]{:S(2)}) copy-start(s32[32]{0:T(128)} %param.15) | copy-start | bytes 388
  34.7 4.2 %collective-permute-start.13 = (bf16[1152,256]{1,0:T(8,128)(2,1)S(1)}, bf16[1152,256]{1,0:T(8,128)(2,1)S(1)}, u32[]{:S(2)}, u32[]{:S(2)}) collective-permute-start(bf16[1152,256]{1,0:T(8,128)(2,1)S(1)} %collective-permute-done.3.refs_0_), channel_id=1, source_target_pairs={{0,1},{1,0},{2,3},{3,2},{4,5},{5,4},{6,7},{7,6},{8,9},{9,8},{10,11... | collective-permute-start | bytes 1769480 | tf_op jit(solution)/shard_map/ppermute | solution.py:24
  34.7 16.7 %collective-permute-start.12 = (bf16[1024,256]{1,0:T(8,128)(2,1)S(1)}, bf16[1024,256]{1,0:T(8,128)(2,1)S(1)}, u32[]{:S(2)}, u32[]{:S(2)}) collective-permute-start(bf16[1024,256]{1,0:T(8,128)(2,1)S(1)} %collective-permute-done.1.refs_1_), channel_id=1, source_target_pairs={{8,0},{16,24},{9,1},{17,25},{10,2},{18,26},{11,3},{19,27},{12,4},{... | collective-permute-start | bytes 1572872 | tf_op jit(solution)/shard_map/ppermute | solution.py:509
  36.1 15.6 %copy-start.3 = (s32[32,32]{1,0:T(8,128)S(1)}, s32[32,32]{1,0:T(8,128)}, u32[]{:S(2)}) copy-start(s32[32,32]{1,0:T(8,128)} %param.14) | copy-start | bytes 12292
  36.1 26.0 %collective-permute-start.11 = (bf16[1024,256]{1,0:T(8,128)(2,1)S(1)}, bf16[1024,256]{1,0:T(8,128)(2,1)S(1)}, u32[]{:S(2)}, u32[]{:S(2)}) collective-permute-start(bf16[1024,256]{1,0:T(8,128)(2,1)S(1)} %collective-permute-done.2), channel_id=1, source_target_pairs={{8,0},{16,24},{9,1},{17,25},{10,2},{18,26},{11,3},{19,27},{12,4},{... | collective-permute-start | bytes 1572872 | tf_op jit(solution)/shard_map/ppermute | solution.py:509
  51.5 3.1 %collective-permute-start.14 = (bf16[1024,256]{1,0:T(8,128)(2,1)S(1)}, bf16[1024,256]{1,0:T(8,128)(2,1)S(1)}, u32[]{:S(2)}, u32[]{:S(2)}) collective-permute-start(bf16[1024,256]{1,0:T(8,128)(2,1)S(1)} %add.74.refs_0_), channel_id=1, source_target_pairs={{0,1},{1,0},{2,3},{3,2},{4,5},{5,4},{6,7},{7,6},{8,9},{9,8},{10,11... | collective-permute-start | bytes 1572872 | tf_op jit(solution)/shard_map/ppermute | solution.py:24
  52.4 9.9 %copy-start.5 = (f32[2,256]{1,0:T(2,128)S(1)}, f32[2,256]{1,0:T(2,128)}, u32[]{:S(2)}) copy-start(f32[2,256]{1,0:T(2,128)} %param.11) | copy-start | bytes 6148
  52.4 15.2 %collective-permute-start.8 = (bf16[1152,256]{1,0:T(8,128)(2,1)S(1)}, bf16[1152,256]{1,0:T(8,128)(2,1)S(1)}, u32[]{:S(2)}, u32[]{:S(2)}) collective-permute-start(bf16[1152,256]{1,0:T(8,128)(2,1)S(1)} %pack.1.refs_1_), channel_id=1, source_target_pairs={{8,16},{16,8},{9,17},{17,9},{10,18},{18,10},{11,19},{19,11},{12,20... | collective-permute-start | bytes 1769480 | tf_op jit(solution)/shard_map/ppermute | solution.py:509
  62.1 8.2 %collective-permute-start.15 = (bf16[1024,256]{1,0:T(8,128)(2,1)S(1)}, bf16[1024,256]{1,0:T(8,128)(2,1)S(1)}, u32[]{:S(2)}, u32[]{:S(2)}) collective-permute-start(bf16[1024,256]{1,0:T(8,128)(2,1)S(1)} %collective-permute-done.11.refs_0_), channel_id=1, source_target_pairs={{0,1},{1,0},{2,3},{3,2},{4,5},{5,4},{6,7},{7,6},{8,9},{9,8},{10,11... | collective-permute-start | bytes 1572872 | tf_op jit(solution)/shard_map/ppermute | solution.py:24
  62.4 13.2 %collective-permute-start.10 = (bf16[1152,256]{1,0:T(8,128)(2,1)S(1)}, bf16[1152,256]{1,0:T(8,128)(2,1)S(1)}, u32[]{:S(2)}, u32[]{:S(2)}) collective-permute-start(bf16[1152,256]{1,0:T(8,128)(2,1)S(1)} %collective-permute-done.3.refs_0_), channel_id=1, source_target_pairs={{8,16},{16,8},{9,17},{17,9},{10,18},{18,10},{11,19},{19,11},{12,20... | collective-permute-start | bytes 1769480 | tf_op jit(solution)/shard_map/ppermute | solution.py:509
  63.1 20.8 %collective-permute-start.20 = (bf16[128,256]{1,0:T(8,128)(2,1)S(1)}, bf16[128,256]{1,0:T(8,128)(2,1)S(1)}, u32[]{:S(2)}, u32[]{:S(2)}) collective-permute-start(bf16[128,256]{1,0:T(8,128)(2,1)S(1)} %slice.85), channel_id=1, source_target_pairs={{0,24},{24,0},{1,25},{25,1},{2,26},{26,2},{3,27},{27,3},{4,28},{28... | collective-permute-start | bytes 196616 | tf_op jit(solution)/shard_map/ppermute | solution.py:539
  67.6 18.4 %collective-permute-start.9 = (bf16[1152,256]{1,0:T(8,128)(2,1)S(1)}, bf16[1152,256]{1,0:T(8,128)(2,1)S(1)}, u32[]{:S(2)}, u32[]{:S(2)}) collective-permute-start(bf16[1152,256]{1,0:T(8,128)(2,1)S(1)} %collective-permute-done.8.refs_0_), channel_id=1, source_target_pairs={{8,0},{16,24},{9,1},{17,25},{10,2},{18,26},{11,3},{19,27},{12,4},{... | collective-permute-start | bytes 1769480 | tf_op jit(solution)/shard_map/ppermute | solution.py:509
  71.7 1.2 collective-permute-start.16
  72.9 11.6 %collective-permute-start.19 = (f32[1,256]{1,0:T(1,128)S(1)}, f32[1,256]{1,0:T(1,128)S(1)}, u32[]{:S(2)}, u32[]{:S(2)}) collective-permute-start(f32[1,256]{1,0:T(1,128)S(1)} %max.36), channel_id=1, source_target_pairs={{0,24},{8,16},{16,8},{24,0},{1,25},{9,17},{17,9},{25,1},{2,26},{10... | collective-permute-start | bytes 3080 | tf_op jit(solution)/shard_map/ppermute | solution.py:33
  74.1 11.9 %collective-permute-start.18 = (f32[1,256]{1,0:T(1,128)S(1)}, f32[1,256]{1,0:T(1,128)S(1)}, u32[]{:S(2)}, u32[]{:S(2)}) collective-permute-start(f32[1,256]{1,0:T(1,128)S(1)} %max.36), channel_id=1, source_target_pairs={{0,16},{8,24},{16,0},{24,8},{1,17},{9,25},{17,1},{25,9},{2,18},{10... | collective-permute-start | bytes 3080 | tf_op jit(solution)/shard_map/ppermute | solution.py:33
  75.5 10.4 %collective-permute-start.17 = (f32[1,256]{1,0:T(1,128)S(1)}, f32[1,256]{1,0:T(1,128)S(1)}, u32[]{:S(2)}, u32[]{:S(2)}) collective-permute-start(f32[1,256]{1,0:T(1,128)S(1)} %max.36), channel_id=1, source_target_pairs={{0,8},{8,0},{16,24},{24,16},{1,9},{9,1},{17,25},{25,17},{2,10},{10... | collective-permute-start | bytes 3080 | tf_op jit(solution)/shard_map/ppermute | solution.py:33
  83.9 3.3 %collective-permute-start.23 = (bf16[1152,256]{1,0:T(8,128)(2,1)S(1)}, bf16[1152,256]{1,0:T(8,128)(2,1)S(1)}, u32[]{:S(2)}, u32[]{:S(2)}) collective-permute-start(bf16[1152,256]{1,0:T(8,128)(2,1)S(1)} %collective-permute-done.8.refs_0_), channel_id=1, source_target_pairs={{0,1},{1,0},{2,3},{3,2},{4,5},{5,4},{6,7},{7,6},{8,9},{9,8},{10,11... | collective-permute-start | bytes 1769480 | tf_op jit(solution)/shard_map/ppermute | solution.py:24
  84.5 13.4 %collective-permute-start.25 = (bf16[768,256]{1,0:T(8,128)(2,1)S(1)}, bf16[768,256]{1,0:T(8,128)(2,1)S(1)}, u32[]{:S(2)}, u32[]{:S(2)}) collective-permute-start(bf16[768,256]{1,0:T(8,128)(2,1)S(1)} %slice.93), channel_id=1, source_target_pairs={{8,0},{16,24},{9,1},{17,25},{10,2},{18,26},{11,3},{19,27},{12,4},{... | collective-permute-start | bytes 1179656 | tf_op jit(solution)/shard_map/ppermute | solution.py:509
  86.0 3.0 %copy-start.4 = (f32[1,256]{1,0:T(1,128)}, f32[1,256]{1,0:T(1,128)S(1)}, u32[]{:S(2)}) copy-start(f32[1,256]{1,0:T(1,128)S(1)} %add_sqrt_fusion) | copy-start | bytes 3076
  86.2 2.9 %collective-permute-start.22 = (bf16[1152,256]{1,0:T(8,128)(2,1)S(1)}, bf16[1152,256]{1,0:T(8,128)(2,1)S(1)}, u32[]{:S(2)}, u32[]{:S(2)}) collective-permute-start(bf16[1152,256]{1,0:T(8,128)(2,1)S(1)} %add.86.refs_0_), channel_id=1, source_target_pairs={{0,1},{1,0},{2,3},{3,2},{4,5},{5,4},{6,7},{7,6},{8,9},{9,8},{10,11... | collective-permute-start | bytes 1769480 | tf_op jit(solution)/shard_map/ppermute | solution.py:24
  87.0 3.4 %collective-permute-start.21 = (bf16[1024,128]{1,0:T(8,128)(2,1)S(1)}, bf16[1024,128]{1,0:T(8,128)(2,1)S(1)}, u32[]{:S(2)}, u32[]{:S(2)}) collective-permute-start(bf16[1024,128]{1,0:T(8,128)(2,1)S(1)} %get-tuple-element.157), channel_id=1, source_target_pairs={{0,1},{1,0},{2,3},{3,2},{4,5},{5,4},{6,7},{7,6},{8,9},{9,8},{10,11... | collective-permute-start | bytes 786440 | tf_op jit(solution)/shard_map/ppermute | solution.py:24
  87.7 10.2 %copy-start.2 = (bf16[4,8,2,256]{3,2,1,0:T(2,128)(2,1)S(1)}, bf16[4,8,2,256]{3,2,1,0:T(2,128)(2,1)}, u32[]{:S(2)}) copy-start(bf16[4,8,2,256]{3,2,1,0:T(2,128)(2,1)} %param.12) | copy-start | bytes 98308
  97.9 2.7 %collective-permute-start.26 = (bf16[768,256]{1,0:T(8,128)(2,1)S(1)}, bf16[768,256]{1,0:T(8,128)(2,1)S(1)}, u32[]{:S(2)}, u32[]{:S(2)}) collective-permute-start(bf16[768,256]{1,0:T(8,128)(2,1)S(1)} %collective-permute-done.25.refs_0_), channel_id=1, source_target_pairs={{0,1},{1,0},{2,3},{3,2},{4,5},{5,4},{6,7},{7,6},{8,9},{9,8},{10,11... | collective-permute-start | bytes 1179656 | tf_op jit(solution)/shard_map/ppermute | solution.py:24
  98.0 7.8 %collective-permute-start.24 = (bf16[256,256]{1,0:T(8,128)(2,1)S(1)}, bf16[256,256]{1,0:T(8,128)(2,1)S(1)}, u32[]{:S(2)}, u32[]{:S(2)}) collective-permute-start(bf16[256,256]{1,0:T(8,128)(2,1)S(1)} %slice.92), channel_id=1, source_target_pairs={{8,0},{16,24},{9,1},{17,25},{10,2},{18,26},{11,3},{19,27},{12,4},{... | collective-permute-start | bytes 393224 | tf_op jit(solution)/shard_map/ppermute | solution.py:557
  105.8 1.3 %collective-permute-start.27 = (bf16[256,256]{1,0:T(8,128)(2,1)S(1)}, bf16[256,256]{1,0:T(8,128)(2,1)S(1)}, u32[]{:S(2)}, u32[]{:S(2)}) collective-permute-start(bf16[256,256]{1,0:T(8,128)(2,1)S(1)} %collective-permute-done.24.refs_0_), channel_id=1, source_target_pairs={{0,1},{1,0},{2,3},{3,2},{4,5},{5,4},{6,7},{7,6},{8,9},{9,8},{10,11... | collective-permute-start | bytes 393224 | tf_op jit(solution)/shard_map/ppermute | solution.py:24
  108.3 1.6 %collective-permute-start.28 = (bf16[1024,128]{1,0:T(8,128)(2,1)S(1)}, bf16[1024,128]{1,0:T(8,128)(2,1)S(1)}, u32[]{:S(2)}, u32[]{:S(2)}) collective-permute-start(bf16[1024,128]{1,0:T(8,128)(2,1)S(1)} %get-tuple-element.155), channel_id=1, source_target_pairs={{0,1},{1,0},{2,3},{3,2},{4,5},{5,4},{6,7},{7,6},{8,9},{9,8},{10,11... | collective-permute-start | bytes 786440 | tf_op jit(solution)/shard_map/ppermute | solution.py:24
  111.4 7.0 %collective-permute-start.29 = (bf16[272,128]{1,0:T(8,128)(2,1)S(1)}, bf16[272,128]{1,0:T(8,128)(2,1)S(1)}, u32[]{:S(2)}, u32[]{:S(2)}) collective-permute-start(bf16[272,128]{1,0:T(8,128)(2,1)S(1)} %get-tuple-element.135), channel_id=1, source_target_pairs={{0,8},{8,0},{16,24},{24,16},{1,9},{9,1},{17,25},{25,17},{2,10},{10... | collective-permute-start | bytes 208904 | tf_op jit(solution)/shard_map/ppermute | solution.py:33
  111.5 8.2 %collective-permute-start.30 = (bf16[272,128]{1,0:T(8,128)(2,1)S(1)}, bf16[272,128]{1,0:T(8,128)(2,1)S(1)}, u32[]{:S(2)}, u32[]{:S(2)}) collective-permute-start(bf16[272,128]{1,0:T(8,128)(2,1)S(1)} %get-tuple-element.136), channel_id=1, source_target_pairs={{0,16},{8,24},{16,0},{24,8},{1,17},{9,25},{17,1},{25,9},{2,18},{10... | collective-permute-start | bytes 208904 | tf_op jit(solution)/shard_map/ppermute | solution.py:33
  114.7 6.1 %collective-permute-start.31 = (bf16[272,128]{1,0:T(8,128)(2,1)S(1)}, bf16[272,128]{1,0:T(8,128)(2,1)S(1)}, u32[]{:S(2)}, u32[]{:S(2)}) collective-permute-start(bf16[272,128]{1,0:T(8,128)(2,1)S(1)} %get-tuple-element.137), channel_id=1, source_target_pairs={{0,24},{8,16},{16,8},{24,0},{1,25},{9,17},{17,9},{25,1},{2,26},{10... | collective-permute-start | bytes 208904 | tf_op jit(solution)/shard_map/ppermute | solution.py:33
  121.2 1.3 %collective-permute-start.32 = (bf16[32,1024]{1,0:T(8,128)(2,1)S(1)}, bf16[32,1024]{1,0:T(8,128)(2,1)S(1)}, u32[]{:S(2)}, u32[]{:S(2)}) collective-permute-start(bf16[32,1024]{1,0:T(8,128)(2,1)S(1)} %finish.1), channel_id=1, source_target_pairs={{0,1},{1,0},{2,3},{3,2},{4,5},{5,4},{6,7},{7,6},{8,9},{9,8},{10,11... | collective-permute-start | bytes 196616 | tf_op jit(solution)/shard_map/ppermute | solution.py:24

commit v15 on v12

--- a/solution.py
+++ b/solution.py
@@ -141,26 +141,31 @@
 
 def project_kernel(hops, back, groups, owners, place, left, *refs):
     count = len(hops)
-    weights, total = refs[:count], refs[count]
+    weights = refs[:count]
     out, held, arrived = refs[-3:]
     depth = held.shape[1]
     copies = [
         pltpu.make_async_copy(weights[j].at[pl.ds(0, depth)], held.at[j], arrived.at[j])
         for j in range(count)
     ]
-    for copy in copies:
-        copy.start()
-    out[...] = total[...]
     owner = lax.rem(place[1] + owners - back, owners)
-    for j, copy in enumerate(copies):
-        copy.wait()
+    sources = []
+    for j in range(count):
         group = jnp.int32(-1)
         for parity, hop in hops[j]:
             there = place[0] + jnp.where(lax.rem(place[0], 2) == parity, hop, -hop)
             group = jnp.where((there >= 0) & (there < groups), there, group)
-
-        @pl.when((group >= 0) & (group < groups))
+        sources.append(group)
+
+        @pl.when(group >= 0)
+        def _(j=j):
+            copies[j].start()
+
+    for j, group in enumerate(sources):
+
+        @pl.when(group >= 0)
         def _(j=j, group=group):
+            copies[j].wait()
             block = pl.ds(pl.multiple_of((group * owners + owner) * depth, depth), depth)
             out[...] += jnp.dot(left[:, block], held[j], preferred_element_type=jnp.float32)
 

time: 121 us -> 121 us (level)
  Pallas kernels: 36.8 us -> 34.3 us
  waiting for transfers between devices: 42.6 us -> 44.7 us
    pallas_call x16, Pallas kernels: 22 us -> 19.6 us  [project(): pl.pallas_call(functools.partial(project_kernel, hops, back, groups, owne...]
    ppermute x10, waiting for transfers between devices: 31.2 us -> 32.5 us  [send(): return lax.ppermute(x, 'seq', line_pairs(hop, parity, groups))]
  transfers between devices with their start and end apart: 31 -> 31, of which waited for: 11 -> 11; matrix products, arithmetic and copies ran while one was open for 4% -> 4% of each run, Pallas kernels for 28% -> 26%
where the time goes in v15:
time: 121 us; the launch traced here: 120 us
  waiting for transfers between devices  44.7 us (37%)
  Pallas kernels  34.3 us (28%)
  starting transfers between devices  32 us (26%)
  other arithmetic  5.49 us (5%)
  local copies, waits for them, and re-layouts  2.15 us (2%)
  between operations  1.25 us (1%)
    ppermute x10, waiting for transfers between devices, send(): return lax.ppermute(x, 'seq', line_pairs(hop, parity, groups))  32.5 us
    pallas_call x16, Pallas kernels, project(): pl.pallas_call(functools.partial(project_kernel, hops, back, groups, owne...  19.6 us
    ppermute x10, starting transfers between devices, send(): return lax.ppermute(x, 'seq', line_pairs(hop, parity, groups))  16.2 us
    ppermute x6, waiting for transfers between devices, swapped(): return lax.ppermute(x, axis, [(i, partner(i, k, n)) for i in range(n)])  9.31 us
    ppermute x6, starting transfers between devices, swapped(): return lax.ppermute(x, axis, [(i, partner(i, k, n)) for i in range(n)])  8.83 us
    pallas_call x1, Pallas kernels, load(): pl.pallas_call(functools.partial(load_kernel, owners), out_shape=(jax.Sha...  6.57 us
    pallas_call x1, Pallas kernels, score(): pl.pallas_call(functools.partial(score_kernel, slots, parts, steps, scale...  4.73 us
    ppermute x1, starting transfers between devices, line_project(): far_query = lax.ppermute(own_block[depth:], 'seq', ends)  4.54 us
  transfers between devices with their start and end apart: 31, of which 11 were waited for; matrix products, arithmetic and copies ran while one was open for 4% of the time, Pallas kernels for 26%

profile of v15, /device:TPU:0, one launch (start us, length us, event | category | flops | bytes accessed | tf_op | source)
XLA Modules:
  0.0 120.3 jit_solution(18446340991833189570)
XLA Ops:
  0.6 3.1 %collective-permute-start = (bf16[1024,256]{1,0:T(8,128)(2,1)}, bf16[1024,256]{1,0:T(8,128)(2,1)S(1)}, u32[]{:S(2)}, u32[]{:S(2)}) collective-permute-start(bf16[1024,256]{1,0:T(8,128)(2,1)} %refs_0_), channel_id=1, source_target_pairs={{0,8},{8,0},{16,24},{24,16},{1,9},{9,1},{17,25},{25,17},{2,10},{10... | collective-permute-start | bytes 1572872 | tf_op jit(solution)/shard_map/ppermute | solution.py:506
  3.7 0.7 collective-permute-start.1
  4.5 0.5 collective-permute-start.7
  5.0 0.9 select_bitcast_fusion.query
  6.0 1.0 copy-done
  7.1 1.0 copy-done.1
  8.1 6.6 %load.1 = (bf16[1024,8192]{1,0:T(8,128)(2,1)S(1)}, f32[1024,256]{1,0:T(8,128)S(1)}, f32[1024,256]{1,0:T(8,128)S(1)}) custom-call(s32[2]{0:T(128)S(1)} %pad_add_fusion.place, bf16[1024,8192]{1,0:T(8,128)(2,1)} %hidden.1, bf16[1024,256]{1,0:T(8,128)(2,1)S(1)} %copy-done.1, bf16[1152,256]{1,0:T(8,128)(2,1)S(1)} %pack.1.refs_1_), custom_call_target="tpu_custom_call" | custom-call | flops 1073741824 | bytes 16777216 | tf_op jit(solution)/shard_map/load/pallas_call | solution.py:117
  14.7 1.2 collective-permute-done.refs_0_
  15.9 0.5 collective-permute-start.5
  16.4 4.8 %collective-permute-start.3 = (bf16[1152,256]{1,0:T(8,128)(2,1)S(1)}, bf16[1152,256]{1,0:T(8,128)(2,1)S(1)}, u32[]{:S(2)}, u32[]{:S(2)}) collective-permute-start(bf16[1152,256]{1,0:T(8,128)(2,1)S(1)} %pack.1.refs_1_), channel_id=1, source_target_pairs={{0,8},{8,0},{16,24},{24,16},{1,9},{9,1},{17,25},{25,17},{2,10},{10... | collective-permute-start | bytes 1769480 | tf_op jit(solution)/shard_map/ppermute | solution.py:506
  21.2 0.7 collective-permute-start.2
  21.9 1.3 %project.19.refs_1_ = f32[1024,256]{1,0:T(8,128)S(1)} custom-call(s32[2]{0:T(128)S(1)} %pad_add_fusion.place, bf16[1024,8192]{1,0:T(8,128)(2,1)S(1)} %get-tuple-element.84.left, bf16[1024,256]{1,0:T(8,128)(2,1)S(1)} %collective-permute-done.7.refs_0_, f32[1024,256]{1,0:T(8,128)S(1)} %get-tuple-element.87.refs_1_), custom_call_target="tpu_custom_call", output_to_operand_aliasing={{}: (3, {})} | custom-call | flops 536870912 | bytes 4718592 | tf_op jit(solution)/shard_map/project/pallas_call | solution.py:178
  23.2 1.3 %project.16.refs_2_ = f32[1024,256]{1,0:T(8,128)S(1)} custom-call(s32[2]{0:T(128)S(1)} %pad_add_fusion.place, bf16[1024,8192]{1,0:T(8,128)(2,1)S(1)} %get-tuple-element.84.left, bf16[1024,256]{1,0:T(8,128)(2,1)S(1)} %collective-permute-done.6.refs_0_, f32[1024,256]{1,0:T(8,128)S(1)} %get-tuple-element.86.refs_1_), custom_call_target="tpu_custom_call", output_to_operand_aliasing={{}: (3, {})} | custom-call | flops 536870912 | bytes 4718592 | tf_op jit(solution)/shard_map/project/pallas_call | solution.py:178
  24.5 1.3 %project.17.refs_2_ = f32[1024,256]{1,0:T(8,128)S(1)} custom-call(s32[2]{0:T(128)S(1)} %pad_add_fusion.place, bf16[1024,8192]{1,0:T(8,128)(2,1)S(1)} %get-tuple-element.84.left, bf16[1024,256]{1,0:T(8,128)(2,1)S(1)} %collective-permute-done.refs_0_, bf16[1024,256]{1,0:T(8,128)(2,1)S(1)} %collective-permute-done.1.refs_1_, ...), custom_call_target="tpu_custom_call", output_to_operand_aliasing={{}: (4, {})} | custom-call | flops 1073741824 | bytes 7340032 | tf_op jit(solution)/shard_map/project/pallas_call | solution.py:178
  25.9 1.3 %project.18.refs_1_ = f32[1024,256]{1,0:T(8,128)S(1)} custom-call(s32[2]{0:T(128)S(1)} %pad_add_fusion.place, bf16[1024,8192]{1,0:T(8,128)(2,1)S(1)} %get-tuple-element.84.left, bf16[1024,256]{1,0:T(8,128)(2,1)S(1)} %collective-permute-done.4.refs_0_, bf16[1024,256]{1,0:T(8,128)(2,1)S(1)} %collective-permute-done.5.refs_1_, ...), custom_call_target="tpu_custom_call", output_to_operand_aliasing={{}: (4, {})} | custom-call | flops 1073741824 | bytes 7340032 | tf_op jit(solution)/shard_map/project/pallas_call | solution.py:178
  27.2 7.4 %collective-permute-done.3.refs_0_ = bf16[1152,256]{1,0:T(8,128)(2,1)S(1)} collective-permute-done((bf16[1152,256]{1,0:T(8,128)(2,1)S(1)}, bf16[1152,256]{1,0:T(8,128)(2,1)S(1)}, u32[]{:S(2)}, u32[]{:S(2)}) %collective-permute-start.3) | collective-permute-done | bytes 589856 | tf_op jit(solution)/shard_map/ppermute | solution.py:506
  34.7 1.3 %collective-permute-start.12 = (bf16[1024,256]{1,0:T(8,128)(2,1)S(1)}, bf16[1024,256]{1,0:T(8,128)(2,1)S(1)}, u32[]{:S(2)}, u32[]{:S(2)}) collective-permute-start(bf16[1024,256]{1,0:T(8,128)(2,1)S(1)} %collective-permute-done.1.refs_1_), channel_id=1, source_target_pairs={{8,0},{16,24},{9,1},{17,25},{10,2},{18,26},{11,3},{19,27},{12,4},{... | collective-permute-start | bytes 1572872 | tf_op jit(solution)/shard_map/ppermute | solution.py:506
  36.1 1.4 %collective-permute-start.11 = (bf16[1024,256]{1,0:T(8,128)(2,1)S(1)}, bf16[1024,256]{1,0:T(8,128)(2,1)S(1)}, u32[]{:S(2)}, u32[]{:S(2)}) collective-permute-start(bf16[1024,256]{1,0:T(8,128)(2,1)S(1)} %collective-permute-done.2), channel_id=1, source_target_pairs={{8,0},{16,24},{9,1},{17,25},{10,2},{18,26},{11,3},{19,27},{12,4},{... | collective-permute-start | bytes 1572872 | tf_op jit(solution)/shard_map/ppermute | solution.py:506
  37.5 1.3 %project.20.refs_1_ = f32[1024,256]{1,0:T(8,128)S(1)} custom-call(s32[2]{0:T(128)S(1)} %pad_add_fusion.place, bf16[1024,8192]{1,0:T(8,128)(2,1)S(1)} %get-tuple-element.84.left, bf16[1152,256]{1,0:T(8,128)(2,1)S(1)} %collective-permute-done.3.refs_0_, f32[1024,256]{1,0:T(8,128)S(1)} %project.19.refs_1_), custom_call_target="tpu_custom_call", output_to_operand_aliasing={{}: (3, {})} | custom-call | flops 536870912 | bytes 4718592 | tf_op jit(solution)/shard_map/project/pallas_call | solution.py:178
  38.8 1.3 %project.21.refs_1_ = f32[1024,256]{1,0:T(8,128)S(1)} custom-call(s32[2]{0:T(128)S(1)} %pad_add_fusion.place, bf16[1024,8192]{1,0:T(8,128)(2,1)S(1)} %get-tuple-element.84.left, bf16[1152,256]{1,0:T(8,128)(2,1)S(1)} %collective-permute-done.13.refs_0_, f32[1024,256]{1,0:T(8,128)S(1)} %project.20.refs_1_), custom_call_target="tpu_custom_call", output_to_operand_aliasing={{}: (3, {})} | custom-call | flops 536870912 | bytes 4718592 | tf_op jit(solution)/shard_map/project/pallas_call | solution.py:178
  40.1 11.2 %collective-permute-done.12 = bf16[1024,256]{1,0:T(8,128)(2,1)S(1)} collective-permute-done((bf16[1024,256]{1,0:T(8,128)(2,1)S(1)}, bf16[1024,256]{1,0:T(8,128)(2,1)S(1)}, u32[]{:S(2)}, u32[]{:S(2)}) %collective-permute-start.12) | collective-permute-done | bytes 524320 | tf_op jit(solution)/shard_map/ppermute | solution.py:506
  51.4 0.1 add.74.refs_0_
  51.6 0.6 convert_reduce_fusion
  52.2 0.2 fusion.2
  52.4 0.8 collective-permute-start.8
  53.3 1.3 %project.22.refs_1_ = f32[1024,256]{1,0:T(8,128)S(1)} custom-call(s32[2]{0:T(128)S(1)} %pad_add_fusion.place, bf16[1024,8192]{1,0:T(8,128)(2,1)S(1)} %get-tuple-element.84.left, bf16[1024,256]{1,0:T(8,128)(2,1)S(1)} %add.74.refs_0_, f32[1024,256]{1,0:T(8,128)S(1)} %project.18.refs_1_), custom_call_target="tpu_custom_call", output_to_operand_aliasing={{}: (3, {})} | custom-call | flops 536870912 | bytes 4718592 | tf_op jit(solution)/shard_map/project/pallas_call | solution.py:178
  54.6 1.3 %project.23.refs_1_ = f32[1024,256]{1,0:T(8,128)S(1)} custom-call(s32[2]{0:T(128)S(1)} %pad_add_fusion.place, bf16[1024,8192]{1,0:T(8,128)(2,1)S(1)} %get-tuple-element.84.left, bf16[1024,256]{1,0:T(8,128)(2,1)S(1)} %collective-permute-done.14.refs_0_, f32[1024,256]{1,0:T(8,128)S(1)} %project.22.refs_1_), custom_call_target="tpu_custom_call", output_to_operand_aliasing={{}: (3, {})} | custom-call | flops 536870912 | bytes 4718592 | tf_op jit(solution)/shard_map/project/pallas_call | solution.py:178
  55.9 6.2 %collective-permute-done.11.refs_0_ = bf16[1024,256]{1,0:T(8,128)(2,1)S(1)} collective-permute-done((bf16[1024,256]{1,0:T(8,128)(2,1)S(1)}, bf16[1024,256]{1,0:T(8,128)(2,1)S(1)}, u32[]{:S(2)}, u32[]{:S(2)}) %collective-permute-start.11) | collective-permute-done | bytes 524320 | tf_op jit(solution)/shard_map/ppermute | solution.py:506
  62.1 0.2 fusion.1.count
  62.4 0.7 collective-permute-start.10
  63.1 4.5 %collective-permute-start.20 = (bf16[128,256]{1,0:T(8,128)(2,1)S(1)}, bf16[128,256]{1,0:T(8,128)(2,1)S(1)}, u32[]{:S(2)}, u32[]{:S(2)}) collective-permute-start(bf16[128,256]{1,0:T(8,128)(2,1)S(1)} %slice.79), channel_id=1, source_target_pairs={{0,24},{24,0},{1,25},{25,1},{2,26},{26,2},{3,27},{27,3},{4,28},{28... | collective-permute-start | bytes 196616 | tf_op jit(solution)/shard_map/ppermute | solution.py:535
  67.6 1.3 %collective-permute-start.9 = (bf16[1152,256]{1,0:T(8,128)(2,1)S(1)}, bf16[1152,256]{1,0:T(8,128)(2,1)S(1)}, u32[]{:S(2)}, u32[]{:S(2)}) collective-permute-start(bf16[1152,256]{1,0:T(8,128)(2,1)S(1)} %collective-permute-done.8.refs_0_), channel_id=1, source_target_pairs={{8,0},{16,24},{9,1},{17,25},{10,2},{18,26},{11,3},{19,27},{12,4},{... | collective-permute-start | bytes 1769480 | tf_op jit(solution)/shard_map/ppermute | solution.py:506
  68.9 1.3 %project.24.refs_1_ = f32[1024,256]{1,0:T(8,128)S(1)} custom-call(s32[2]{0:T(128)S(1)} %pad_add_fusion.place, bf16[1024,8192]{1,0:T(8,128)(2,1)S(1)} %get-tuple-element.84.left, bf16[1024,256]{1,0:T(8,128)(2,1)S(1)} %collective-permute-done.11.refs_0_, f32[1024,256]{1,0:T(8,128)S(1)} %project.23.refs_1_), custom_call_target="tpu_custom_call", output_to_operand_aliasing={{}: (3, {})} | custom-call | flops 536870912 | bytes 4718592 | tf_op jit(solution)/shard_map/project/pallas_call | solution.py:178
  70.3 1.3 %project.25 = f32[1024,256]{1,0:T(8,128)S(1)} custom-call(s32[2]{0:T(128)S(1)} %pad_add_fusion.place, bf16[1024,8192]{1,0:T(8,128)(2,1)S(1)} %get-tuple-element.84.left, bf16[1024,256]{1,0:T(8,128)(2,1)S(1)} %collective-permute-done.15.refs_0_, f32[1024,256]{1,0:T(8,128)S(1)} %project.24.refs_1_), custom_call_target="tpu_custom_call", output_to_operand_aliasing={{}: (3, {})} | custom-call | flops 536870912 | bytes 4718592 | tf_op jit(solution)/shard_map/project/pallas_call | solution.py:178
  71.7 0.3 collective-permute-start.16
  72.0 0.9 collective-permute-done.16
  72.9 1.2 collective-permute-start.17
  74.1 1.1 collective-permute-start.18
  75.2 2.1 %collective-permute-start.19 = (f32[1,256]{1,0:T(1,128)S(1)}, f32[1,256]{1,0:T(1,128)S(1)}, u32[]{:S(2)}, u32[]{:S(2)}) collective-permute-start(f32[1,256]{1,0:T(1,128)S(1)} %max.36), channel_id=1, source_target_pairs={{0,24},{8,16},{16,8},{24,0},{1,25},{9,17},{17,9},{25,1},{2,26},{10... | collective-permute-start | bytes 3080 | tf_op jit(solution)/shard_map/ppermute | solution.py:32
  77.3 0.6 project.26.refs_1_
  77.9 7.2 %collective-permute-done.17 = f32[1,256]{1,0:T(1,128)S(1)} collective-permute-done((f32[1,256]{1,0:T(1,128)S(1)}, f32[1,256]{1,0:T(1,128)S(1)}, u32[]{:S(2)}, u32[]{:S(2)}) %collective-permute-start.17) | collective-permute-done | bytes 1056 | tf_op jit(solution)/shard_map/ppermute | solution.py:32
  85.1 1.5 %collective-permute-start.24 = (bf16[1152,256]{1,0:T(8,128)(2,1)S(1)}, bf16[1152,256]{1,0:T(8,128)(2,1)S(1)}, u32[]{:S(2)}, u32[]{:S(2)}) collective-permute-start(bf16[1152,256]{1,0:T(8,128)(2,1)S(1)} %collective-permute-done.10), channel_id=1, source_target_pairs={{8,0},{16,24},{9,1},{17,25},{10,2},{18,26},{11,3},{19,27},{12,4},{... | collective-permute-start | bytes 1769480 | tf_op jit(solution)/shard_map/ppermute | solution.py:506
  86.6 0.1 add.86.refs_0_
  86.9 0.1 minimum_convert_fusion.1
  87.1 0.6 collective-permute-start.21
  87.7 0.6 project.27.refs_1_
  88.3 1.3 %project.28.refs_1_ = f32[1024,256]{1,0:T(8,128)S(1)} custom-call(s32[2]{0:T(128)S(1)} %pad_add_fusion.place, bf16[1024,8192]{1,0:T(8,128)(2,1)S(1)} %get-tuple-element.84.left, bf16[1152,256]{1,0:T(8,128)(2,1)S(1)} %add.86.refs_0_, f32[1024,256]{1,0:T(8,128)S(1)} %project.27.refs_1_), custom_call_target="tpu_custom_call", output_to_operand_aliasing={{}: (3, {})} | custom-call | flops 536870912 | bytes 4718592 | tf_op jit(solution)/shard_map/project/pallas_call | solution.py:178
  89.7 1.3 %project.29.refs_1_ = f32[1024,256]{1,0:T(8,128)S(1)} custom-call(s32[2]{0:T(128)S(1)} %pad_add_fusion.place, bf16[1024,8192]{1,0:T(8,128)(2,1)S(1)} %get-tuple-element.84.left, bf16[1152,256]{1,0:T(8,128)(2,1)S(1)} %collective-permute-done.22.refs_0_, f32[1024,256]{1,0:T(8,128)S(1)} %project.28.refs_1_), custom_call_target="tpu_custom_call", output_to_operand_aliasing={{}: (3, {})} | custom-call | flops 536870912 | bytes 4718592 | tf_op jit(solution)/shard_map/project/pallas_call | solution.py:178
  91.0 4.7 %score.1 = (bf16[4,256,2048]{2,1,0:T(8,128)(2,1)S(1)}, f32[2,256]{1,0:T(2,128)S(1)}, f32[2,256]{1,0:T(2,128)S(1)}, f32[2,256]{1,0:T(2,128)S(1)}, f32[2,256]{1,0:T(2,128)S(1)}) custom-call(s32[4]{0:T(128)S(1)} %iota_xor_fusion.group, bf16[4,128,256]{2,1,0:T(8,128)(2,1)S(1)} %pad_maximum_fusion.query, f32[1,128]{1,0:T(1,128)S(1)} %broadcast_select_fusion.7.smooth, ...), custom_call_target="tpu_custom_call" | custom-call | flops 536870912 | bytes 4194304 | tf_op jit(solution)/shard_map/score/pallas_call | solution.py:249
  95.7 6.5 %collective-permute-done.24.refs_0_ = bf16[1152,256]{1,0:T(8,128)(2,1)S(1)} collective-permute-done((bf16[1152,256]{1,0:T(8,128)(2,1)S(1)}, bf16[1152,256]{1,0:T(8,128)(2,1)S(1)}, u32[]{:S(2)}, u32[]{:S(2)}) %collective-permute-start.24) | collective-permute-done | bytes 589856 | tf_op jit(solution)/shard_map/ppermute | solution.py:506
  102.3 1.3 %project.30.refs_1_ = f32[1024,256]{1,0:T(8,128)S(1)} custom-call(s32[2]{0:T(128)S(1)} %pad_add_fusion.place, bf16[1024,8192]{1,0:T(8,128)(2,1)S(1)} %get-tuple-element.84.left, bf16[1152,256]{1,0:T(8,128)(2,1)S(1)} %collective-permute-done.24.refs_0_, f32[1024,256]{1,0:T(8,128)S(1)} %project.29.refs_1_), custom_call_target="tpu_custom_call", output_to_operand_aliasing={{}: (3, {})} | custom-call | flops 536870912 | bytes 4718592 | tf_op jit(solution)/shard_map/project/pallas_call | solution.py:178
  103.6 0.6 collective-permute-done.25.refs_0_
  104.2 1.3 %project.31 = f32[1024,256]{1,0:T(8,128)S(1)} custom-call(s32[2]{0:T(128)S(1)} %pad_add_fusion.place, bf16[1024,8192]{1,0:T(8,128)(2,1)S(1)} %get-tuple-element.84.left, bf16[1152,256]{1,0:T(8,128)(2,1)S(1)} %collective-permute-done.25.refs_0_, f32[1024,256]{1,0:T(8,128)S(1)} %project.30.refs_1_), custom_call_target="tpu_custom_call", output_to_operand_aliasing={{}: (3, {})} | custom-call | flops 536870912 | bytes 4718592 | tf_op jit(solution)/shard_map/project/pallas_call | solution.py:178
  105.7 0.2 collective-permute-start.26
  105.9 1.3 %weigh_own.1.own = f32[4,256,128]{2,1,0:T(8,128)S(1)} custom-call(bf16[4,256,2048]{2,1,0:T(8,128)(2,1)S(1)} %get-tuple-element.114.probs.refs_0_, bf16[1024,128]{1,0:T(8,128)(2,1)S(1)} %get-tuple-element.152.values), custom_call_target="tpu_custom_call" | custom-call | flops 268435456 | bytes 2097152 | tf_op jit(solution)/shard_map/weigh_own/pallas_call | solution.py:330
  107.3 1.4 %weigh.1 = (bf16[272,128]{1,0:T(8,128)(2,1)S(1)}, bf16[272,128]{1,0:T(8,128)(2,1)S(1)}, bf16[272,128]{1,0:T(8,128)(2,1)S(1)}, bf16[272,128]{1,0:T(8,128)(2,1)S(1)}) custom-call(f32[4,256,128]{2,1,0:T(8,128)S(1)} %weigh_own.1.own, bf16[4,256,2048]{2,1,0:T(8,128)(2,1)S(1)} %get-tuple-element.114.probs.refs_0_, ...), custom_call_target="tpu_custom_call" | custom-call | flops 268435456 | bytes 2097152 | tf_op jit(solution)/shard_map/weigh/pallas_call | solution.py:342
  108.8 1.7 %collective-permute-start.28 = (bf16[272,128]{1,0:T(8,128)(2,1)S(1)}, bf16[272,128]{1,0:T(8,128)(2,1)S(1)}, u32[]{:S(2)}, u32[]{:S(2)}) collective-permute-start(bf16[272,128]{1,0:T(8,128)(2,1)S(1)} %get-tuple-element.132), channel_id=1, source_target_pairs={{0,16},{8,24},{16,0},{24,8},{1,17},{9,25},{17,1},{25,9},{2,18},{10... | collective-permute-start | bytes 208904 | tf_op jit(solution)/shard_map/ppermute | solution.py:32
  110.6 2.6 %collective-permute-start.29 = (bf16[272,128]{1,0:T(8,128)(2,1)S(1)}, bf16[272,128]{1,0:T(8,128)(2,1)S(1)}, u32[]{:S(2)}, u32[]{:S(2)}) collective-permute-start(bf16[272,128]{1,0:T(8,128)(2,1)S(1)} %get-tuple-element.133), channel_id=1, source_target_pairs={{0,24},{8,16},{16,8},{24,0},{1,25},{9,17},{17,9},{25,1},{2,26},{10... | collective-permute-start | bytes 208904 | tf_op jit(solution)/shard_map/ppermute | solution.py:32
  113.2 2.3 %broadcast_select_fusion = bf16[1024,2,256]{2,1,0:T(2,128)(2,1)} fusion(pred[2]{0:T(512)(128)(4,1)S(1)} %iota_compare_fusion.5, bf16[1024,256]{1,0:T(8,128)(2,1)S(1)} %minimum_convert_fusion, bf16[1024,256]{1,0:T(8,128)(2,1)S(1)} %minimum_convert_fusion.1), kind=kLoop, calls=%fused_computation.3 | loop fusion | flops 524288 | bytes 2097154 | tf_op jit(solution)/shard_map/jit(_where)/select_n | solution.py:642
  115.5 0.2 fresh.1
  115.7 2.1 %collective-permute-done.28.refs_2_ = bf16[272,128]{1,0:T(8,128)(2,1)S(1)} collective-permute-done((bf16[272,128]{1,0:T(8,128)(2,1)S(1)}, bf16[272,128]{1,0:T(8,128)(2,1)S(1)}, u32[]{:S(2)}, u32[]{:S(2)}) %collective-permute-start.28) | collective-permute-done | bytes 69664 | tf_op jit(solution)/shard_map/ppermute | solution.py:32
  117.8 0.4 finish.1
  118.3 1.2 %collective-permute-done.30 = bf16[32,1024]{1,0:T(8,128)(2,1)S(1)} collective-permute-done((bf16[32,1024]{1,0:T(8,128)(2,1)S(1)}, bf16[32,1024]{1,0:T(8,128)(2,1)S(1)}, u32[]{:S(2)}, u32[]{:S(2)}) %collective-permute-start.30) | collective-permute-done | bytes 65568 | tf_op jit(solution)/shard_map/ppermute | solution.py:23
  119.6 0.7 maximum_bitcast_fusion
  (71 shorter events, 1.2 us)
Async XLA Ops:
  0.6 15.3 %collective-permute-start = (bf16[1024,256]{1,0:T(8,128)(2,1)}, bf16[1024,256]{1,0:T(8,128)(2,1)S(1)}, u32[]{:S(2)}, u32[]{:S(2)}) collective-permute-start(bf16[1024,256]{1,0:T(8,128)(2,1)} %refs_0_), channel_id=1, source_target_pairs={{0,8},{8,0},{16,24},{24,16},{1,9},{9,1},{17,25},{25,17},{2,10},{10... | collective-permute-start | bytes 1572872 | tf_op jit(solution)/shard_map/ppermute | solution.py:506
  3.7 12.1 %collective-permute-start.1 = (bf16[1024,256]{1,0:T(8,128)(2,1)}, bf16[1024,256]{1,0:T(8,128)(2,1)S(1)}, u32[]{:S(2)}, u32[]{:S(2)}) collective-permute-start(bf16[1024,256]{1,0:T(8,128)(2,1)} %refs_0_), channel_id=1, source_target_pairs={{8,16},{16,8},{9,17},{17,9},{10,18},{18,10},{11,19},{19,11},{12,20... | collective-permute-start | bytes 1572872 | tf_op jit(solution)/shard_map/ppermute | solution.py:506
  4.4 18.7 %collective-permute-start.6 = (bf16[1024,256]{1,0:T(8,128)(2,1)}, bf16[1024,256]{1,0:T(8,128)(2,1)S(1)}, u32[]{:S(2)}, u32[]{:S(2)}) collective-permute-start(bf16[1024,256]{1,0:T(8,128)(2,1)} %refs_0_), channel_id=1, source_target_pairs={{0,1},{1,0},{2,3},{3,2},{4,5},{5,4},{6,7},{7,6},{8,9},{9,8},{10,11... | collective-permute-start | bytes 1572872 | tf_op jit(solution)/shard_map/ppermute | solution.py:23
  4.5 16.6 %collective-permute-start.7 = (bf16[1024,256]{1,0:T(8,128)(2,1)}, bf16[1024,256]{1,0:T(8,128)(2,1)S(1)}, u32[]{:S(2)}, u32[]{:S(2)}) collective-permute-start(bf16[1024,256]{1,0:T(8,128)(2,1)} %weight.1), channel_id=1, source_target_pairs={{0,1},{1,0},{2,3},{3,2},{4,5},{5,4},{6,7},{7,6},{8,9},{9,8},{10,11... | collective-permute-start | bytes 1572872 | tf_op jit(solution)/shard_map/ppermute | solution.py:23
  6.0 1.0 copy-start
  7.1 1.0 copy-start.1
  15.9 10.0 %collective-permute-start.4 = (bf16[1024,256]{1,0:T(8,128)(2,1)S(1)}, bf16[1024,256]{1,0:T(8,128)(2,1)S(1)}, u32[]{:S(2)}, u32[]{:S(2)}) collective-permute-start(bf16[1024,256]{1,0:T(8,128)(2,1)S(1)} %collective-permute-done.refs_0_), channel_id=1, source_target_pairs={{0,1},{1,0},{2,3},{3,2},{4,5},{5,4},{6,7},{7,6},{8,9},{9,8},{10,11... | collective-permute-start | bytes 1572872 | tf_op jit(solution)/shard_map/ppermute | solution.py:23
  15.9 10.0 %collective-permute-start.5 = (bf16[1024,256]{1,0:T(8,128)(2,1)S(1)}, bf16[1024,256]{1,0:T(8,128)(2,1)S(1)}, u32[]{:S(2)}, u32[]{:S(2)}) collective-permute-start(bf16[1024,256]{1,0:T(8,128)(2,1)S(1)} %collective-permute-done.1.refs_1_), channel_id=1, source_target_pairs={{0,1},{1,0},{2,3},{3,2},{4,5},{5,4},{6,7},{7,6},{8,9},{9,8},{10,11... | collective-permute-start | bytes 1572872 | tf_op jit(solution)/shard_map/ppermute | solution.py:23
  16.4 18.2 %collective-permute-start.3 = (bf16[1152,256]{1,0:T(8,128)(2,1)S(1)}, bf16[1152,256]{1,0:T(8,128)(2,1)S(1)}, u32[]{:S(2)}, u32[]{:S(2)}) collective-permute-start(bf16[1152,256]{1,0:T(8,128)(2,1)S(1)} %pack.1.refs_1_), channel_id=1, source_target_pairs={{0,8},{8,0},{16,24},{24,16},{1,9},{9,1},{17,25},{25,17},{2,10},{10... | collective-permute-start | bytes 1769480 | tf_op jit(solution)/shard_map/ppermute | solution.py:506
  21.2 13.5 %collective-permute-start.2 = (bf16[1024,256]{1,0:T(8,128)(2,1)S(1)}, bf16[1024,256]{1,0:T(8,128)(2,1)S(1)}, u32[]{:S(2)}, u32[]{:S(2)}) collective-permute-start(bf16[1024,256]{1,0:T(8,128)(2,1)S(1)} %collective-permute-done.refs_0_), channel_id=1, source_target_pairs={{8,16},{16,8},{9,17},{17,9},{10,18},{18,10},{11,19},{19,11},{12,20... | collective-permute-start | bytes 1572872 | tf_op jit(solution)/shard_map/ppermute | solution.py:506
  24.5 11.5 %copy-start.6 = (s32[32]{0:T(128)S(1)}, s32[32]{0:T(128)}, u32[]{:S(2)}) copy-start(s32[32]{0:T(128)} %param.15) | copy-start | bytes 388
  34.7 4.2 %collective-permute-start.13 = (bf16[1152,256]{1,0:T(8,128)(2,1)S(1)}, bf16[1152,256]{1,0:T(8,128)(2,1)S(1)}, u32[]{:S(2)}, u32[]{:S(2)}) collective-permute-start(bf16[1152,256]{1,0:T(8,128)(2,1)S(1)} %collective-permute-done.3.refs_0_), channel_id=1, source_target_pairs={{0,1},{1,0},{2,3},{3,2},{4,5},{5,4},{6,7},{7,6},{8,9},{9,8},{10,11... | collective-permute-start | bytes 1769480 | tf_op jit(solution)/shard_map/ppermute | solution.py:23
  34.7 16.7 %collective-permute-start.12 = (bf16[1024,256]{1,0:T(8,128)(2,1)S(1)}, bf16[1024,256]{1,0:T(8,128)(2,1)S(1)}, u32[]{:S(2)}, u32[]{:S(2)}) collective-permute-start(bf16[1024,256]{1,0:T(8,128)(2,1)S(1)} %collective-permute-done.1.refs_1_), channel_id=1, source_target_pairs={{8,0},{16,24},{9,1},{17,25},{10,2},{18,26},{11,3},{19,27},{12,4},{... | collective-permute-start | bytes 1572872 | tf_op jit(solution)/shard_map/ppermute | solution.py:506
  36.1 15.6 %copy-start.3 = (s32[32,32]{1,0:T(8,128)S(1)}, s32[32,32]{1,0:T(8,128)}, u32[]{:S(2)}) copy-start(s32[32,32]{1,0:T(8,128)} %param.14) | copy-start | bytes 12292
  36.1 26.0 %collective-permute-start.11 = (bf16[1024,256]{1,0:T(8,128)(2,1)S(1)}, bf16[1024,256]{1,0:T(8,128)(2,1)S(1)}, u32[]{:S(2)}, u32[]{:S(2)}) collective-permute-start(bf16[1024,256]{1,0:T(8,128)(2,1)S(1)} %collective-permute-done.2), channel_id=1, source_target_pairs={{8,0},{16,24},{9,1},{17,25},{10,2},{18,26},{11,3},{19,27},{12,4},{... | collective-permute-start | bytes 1572872 | tf_op jit(solution)/shard_map/ppermute | solution.py:506
  51.5 3.1 %collective-permute-start.14 = (bf16[1024,256]{1,0:T(8,128)(2,1)S(1)}, bf16[1024,256]{1,0:T(8,128)(2,1)S(1)}, u32[]{:S(2)}, u32[]{:S(2)}) collective-permute-start(bf16[1024,256]{1,0:T(8,128)(2,1)S(1)} %add.74.refs_0_), channel_id=1, source_target_pairs={{0,1},{1,0},{2,3},{3,2},{4,5},{5,4},{6,7},{7,6},{8,9},{9,8},{10,11... | collective-permute-start | bytes 1572872 | tf_op jit(solution)/shard_map/ppermute | solution.py:23
  52.4 9.9 %copy-start.5 = (f32[2,256]{1,0:T(2,128)S(1)}, f32[2,256]{1,0:T(2,128)}, u32[]{:S(2)}) copy-start(f32[2,256]{1,0:T(2,128)} %param.11) | copy-start | bytes 6148
  52.4 15.2 %collective-permute-start.8 = (bf16[1152,256]{1,0:T(8,128)(2,1)S(1)}, bf16[1152,256]{1,0:T(8,128)(2,1)S(1)}, u32[]{:S(2)}, u32[]{:S(2)}) collective-permute-start(bf16[1152,256]{1,0:T(8,128)(2,1)S(1)} %pack.1.refs_1_), channel_id=1, source_target_pairs={{8,16},{16,8},{9,17},{17,9},{10,18},{18,10},{11,19},{19,11},{12,20... | collective-permute-start | bytes 1769480 | tf_op jit(solution)/shard_map/ppermute | solution.py:506
  62.1 8.2 %collective-permute-start.15 = (bf16[1024,256]{1,0:T(8,128)(2,1)S(1)}, bf16[1024,256]{1,0:T(8,128)(2,1)S(1)}, u32[]{:S(2)}, u32[]{:S(2)}) collective-permute-start(bf16[1024,256]{1,0:T(8,128)(2,1)S(1)} %collective-permute-done.11.refs_0_), channel_id=1, source_target_pairs={{0,1},{1,0},{2,3},{3,2},{4,5},{5,4},{6,7},{7,6},{8,9},{9,8},{10,11... | collective-permute-start | bytes 1572872 | tf_op jit(solution)/shard_map/ppermute | solution.py:23
  62.4 12.8 %collective-permute-start.10 = (bf16[1152,256]{1,0:T(8,128)(2,1)S(1)}, bf16[1152,256]{1,0:T(8,128)(2,1)S(1)}, u32[]{:S(2)}, u32[]{:S(2)}) collective-permute-start(bf16[1152,256]{1,0:T(8,128)(2,1)S(1)} %collective-permute-done.3.refs_0_), channel_id=1, source_target_pairs={{8,16},{16,8},{9,17},{17,9},{10,18},{18,10},{11,19},{19,11},{12,20... | collective-permute-start | bytes 1769480 | tf_op jit(solution)/shard_map/ppermute | solution.py:506
  63.1 14.2 %collective-permute-start.20 = (bf16[128,256]{1,0:T(8,128)(2,1)S(1)}, bf16[128,256]{1,0:T(8,128)(2,1)S(1)}, u32[]{:S(2)}, u32[]{:S(2)}) collective-permute-start(bf16[128,256]{1,0:T(8,128)(2,1)S(1)} %slice.79), channel_id=1, source_target_pairs={{0,24},{24,0},{1,25},{25,1},{2,26},{26,2},{3,27},{27,3},{4,28},{28... | collective-permute-start | bytes 196616 | tf_op jit(solution)/shard_map/ppermute | solution.py:535
  67.6 19.0 %collective-permute-start.9 = (bf16[1152,256]{1,0:T(8,128)(2,1)S(1)}, bf16[1152,256]{1,0:T(8,128)(2,1)S(1)}, u32[]{:S(2)}, u32[]{:S(2)}) collective-permute-start(bf16[1152,256]{1,0:T(8,128)(2,1)S(1)} %collective-permute-done.8.refs_0_), channel_id=1, source_target_pairs={{8,0},{16,24},{9,1},{17,25},{10,2},{18,26},{11,3},{19,27},{12,4},{... | collective-permute-start | bytes 1769480 | tf_op jit(solution)/shard_map/ppermute | solution.py:506
  71.7 1.2 %collective-permute-start.16 = (f32[1,256]{1,0:T(1,128)S(1)}, f32[1,256]{1,0:T(1,128)S(1)}, u32[]{:S(2)}, u32[]{:S(2)}) collective-permute-start(f32[1,256]{1,0:T(1,128)S(1)} %bitcast.28), channel_id=1, source_target_pairs={{0,1},{1,0},{2,3},{3,2},{4,5},{5,4},{6,7},{7,6},{8,9},{9,8},{10,11... | collective-permute-start | bytes 3080 | tf_op jit(solution)/shard_map/ppermute | solution.py:23
  72.9 12.2 %collective-permute-start.17 = (f32[1,256]{1,0:T(1,128)S(1)}, f32[1,256]{1,0:T(1,128)S(1)}, u32[]{:S(2)}, u32[]{:S(2)}) collective-permute-start(f32[1,256]{1,0:T(1,128)S(1)} %max.36), channel_id=1, source_target_pairs={{0,8},{8,0},{16,24},{24,16},{1,9},{9,1},{17,25},{25,17},{2,10},{10... | collective-permute-start | bytes 3080 | tf_op jit(solution)/shard_map/ppermute | solution.py:32
  74.1 12.5 %collective-permute-start.18 = (f32[1,256]{1,0:T(1,128)S(1)}, f32[1,256]{1,0:T(1,128)S(1)}, u32[]{:S(2)}, u32[]{:S(2)}) collective-permute-start(f32[1,256]{1,0:T(1,128)S(1)} %max.36), channel_id=1, source_target_pairs={{0,16},{8,24},{16,0},{24,8},{1,17},{9,25},{17,1},{25,9},{2,18},{10... | collective-permute-start | bytes 3080 | tf_op jit(solution)/shard_map/ppermute | solution.py:32
  75.2 11.4 %collective-permute-start.19 = (f32[1,256]{1,0:T(1,128)S(1)}, f32[1,256]{1,0:T(1,128)S(1)}, u32[]{:S(2)}, u32[]{:S(2)}) collective-permute-start(f32[1,256]{1,0:T(1,128)S(1)} %max.36), channel_id=1, source_target_pairs={{0,24},{8,16},{16,8},{24,0},{1,25},{9,17},{17,9},{25,1},{2,26},{10... | collective-permute-start | bytes 3080 | tf_op jit(solution)/shard_map/ppermute | solution.py:32
  77.3 10.4 %collective-permute-start.23 = (bf16[1152,256]{1,0:T(8,128)(2,1)S(1)}, bf16[1152,256]{1,0:T(8,128)(2,1)S(1)}, u32[]{:S(2)}, u32[]{:S(2)}) collective-permute-start(bf16[1152,256]{1,0:T(8,128)(2,1)S(1)} %collective-permute-done.8.refs_0_), channel_id=1, source_target_pairs={{0,1},{1,0},{2,3},{3,2},{4,5},{5,4},{6,7},{7,6},{8,9},{9,8},{10,11... | collective-permute-start | bytes 1769480 | tf_op jit(solution)/shard_map/ppermute | solution.py:23
  85.1 17.1 %collective-permute-start.24 = (bf16[1152,256]{1,0:T(8,128)(2,1)S(1)}, bf16[1152,256]{1,0:T(8,128)(2,1)S(1)}, u32[]{:S(2)}, u32[]{:S(2)}) collective-permute-start(bf16[1152,256]{1,0:T(8,128)(2,1)S(1)} %collective-permute-done.10), channel_id=1, source_target_pairs={{8,0},{16,24},{9,1},{17,25},{10,2},{18,26},{11,3},{19,27},{12,4},{... | collective-permute-start | bytes 1769480 | tf_op jit(solution)/shard_map/ppermute | solution.py:506
  86.6 3.0 %copy-start.4 = (f32[1,256]{1,0:T(1,128)}, f32[1,256]{1,0:T(1,128)S(1)}, u32[]{:S(2)}) copy-start(f32[1,256]{1,0:T(1,128)S(1)} %add_sqrt_fusion) | copy-start | bytes 3076
  86.8 2.8 %collective-permute-start.22 = (bf16[1152,256]{1,0:T(8,128)(2,1)S(1)}, bf16[1152,256]{1,0:T(8,128)(2,1)S(1)}, u32[]{:S(2)}, u32[]{:S(2)}) collective-permute-start(bf16[1152,256]{1,0:T(8,128)(2,1)S(1)} %add.86.refs_0_), channel_id=1, source_target_pairs={{0,1},{1,0},{2,3},{3,2},{4,5},{5,4},{6,7},{7,6},{8,9},{9,8},{10,11... | collective-permute-start | bytes 1769480 | tf_op jit(solution)/shard_map/ppermute | solution.py:23
  87.1 3.9 %collective-permute-start.21 = (bf16[1024,128]{1,0:T(8,128)(2,1)S(1)}, bf16[1024,128]{1,0:T(8,128)(2,1)S(1)}, u32[]{:S(2)}, u32[]{:S(2)}) collective-permute-start(bf16[1024,128]{1,0:T(8,128)(2,1)S(1)} %get-tuple-element.153), channel_id=1, source_target_pairs={{0,1},{1,0},{2,3},{3,2},{4,5},{5,4},{6,7},{7,6},{8,9},{9,8},{10,11... | collective-permute-start | bytes 786440 | tf_op jit(solution)/shard_map/ppermute | solution.py:23
  88.3 13.9 %copy-start.2 = (bf16[4,8,2,256]{3,2,1,0:T(2,128)(2,1)S(1)}, bf16[4,8,2,256]{3,2,1,0:T(2,128)(2,1)}, u32[]{:S(2)}) copy-start(bf16[4,8,2,256]{3,2,1,0:T(2,128)(2,1)} %param.12) | copy-start | bytes 98308
  102.2 2.0 %collective-permute-start.25 = (bf16[1152,256]{1,0:T(8,128)(2,1)S(1)}, bf16[1152,256]{1,0:T(8,128)(2,1)S(1)}, u32[]{:S(2)}, u32[]{:S(2)}) collective-permute-start(bf16[1152,256]{1,0:T(8,128)(2,1)S(1)} %collective-permute-done.24.refs_0_), channel_id=1, source_target_pairs={{0,1},{1,0},{2,3},{3,2},{4,5},{5,4},{6,7},{7,6},{8,9},{9,8},{10,11... | collective-permute-start | bytes 1769480 | tf_op jit(solution)/shard_map/ppermute | solution.py:23
  105.7 1.6 %collective-permute-start.26 = (bf16[1024,128]{1,0:T(8,128)(2,1)S(1)}, bf16[1024,128]{1,0:T(8,128)(2,1)S(1)}, u32[]{:S(2)}, u32[]{:S(2)}) collective-permute-start(bf16[1024,128]{1,0:T(8,128)(2,1)S(1)} %get-tuple-element.151), channel_id=1, source_target_pairs={{0,1},{1,0},{2,3},{3,2},{4,5},{5,4},{6,7},{7,6},{8,9},{9,8},{10,11... | collective-permute-start | bytes 786440 | tf_op jit(solution)/shard_map/ppermute | solution.py:23
  108.7 7.0 %collective-permute-start.27 = (bf16[272,128]{1,0:T(8,128)(2,1)S(1)}, bf16[272,128]{1,0:T(8,128)(2,1)S(1)}, u32[]{:S(2)}, u32[]{:S(2)}) collective-permute-start(bf16[272,128]{1,0:T(8,128)(2,1)S(1)} %get-tuple-element.131), channel_id=1, source_target_pairs={{0,8},{8,0},{16,24},{24,16},{1,9},{9,1},{17,25},{25,17},{2,10},{10... | collective-permute-start | bytes 208904 | tf_op jit(solution)/shard_map/ppermute | solution.py:32
  108.8 9.0 %collective-permute-start.28 = (bf16[272,128]{1,0:T(8,128)(2,1)S(1)}, bf16[272,128]{1,0:T(8,128)(2,1)S(1)}, u32[]{:S(2)}, u32[]{:S(2)}) collective-permute-start(bf16[272,128]{1,0:T(8,128)(2,1)S(1)} %get-tuple-element.132), channel_id=1, source_target_pairs={{0,16},{8,24},{16,0},{24,8},{1,17},{9,25},{17,1},{25,9},{2,18},{10... | collective-permute-start | bytes 208904 | tf_op jit(solution)/shard_map/ppermute | solution.py:32
  110.6 7.3 %collective-permute-start.29 = (bf16[272,128]{1,0:T(8,128)(2,1)S(1)}, bf16[272,128]{1,0:T(8,128)(2,1)S(1)}, u32[]{:S(2)}, u32[]{:S(2)}) collective-permute-start(bf16[272,128]{1,0:T(8,128)(2,1)S(1)} %get-tuple-element.133), channel_id=1, source_target_pairs={{0,24},{8,16},{16,8},{24,0},{1,25},{9,17},{17,9},{25,1},{2,26},{10... | collective-permute-start | bytes 208904 | tf_op jit(solution)/shard_map/ppermute | solution.py:32
  118.3 1.3 %collective-permute-start.30 = (bf16[32,1024]{1,0:T(8,128)(2,1)S(1)}, bf16[32,1024]{1,0:T(8,128)(2,1)S(1)}, u32[]{:S(2)}, u32[]{:S(2)}) collective-permute-start(bf16[32,1024]{1,0:T(8,128)(2,1)S(1)} %finish.1), channel_id=1, source_target_pairs={{0,1},{1,0},{2,3},{3,2},{4,5},{5,4},{6,7},{7,6},{8,9},{9,8},{10,11... | collective-permute-start | bytes 196616 | tf_op jit(solution)/shard_map/ppermute | solution.py:23
